TPU v7x, 32 devices: a whole 2x2x4 slice. The times are simulated.
32 devices in a mesh: blk: 8 (over y, x, core), mp: 4 (over z).
Axes of the slice: x: 2, y: 2, z: 4, core: 2. Of those that a mesh axis runs over, the one named last changes fastest.
Arguments:
- streams: bfloat16 [8192, 4, 2048], P('blk', None, 'mp'), may hold values from -36 to 36
- proj_master: float32 [2048, 4, 2048], P(('blk', 'mp')), may hold values from -3 to 3
- hc_proj: float32 [2048, 6], P('mp'), may hold values from -0.125 to 0.125
- hc_static: float32 [4, 6], replicated, may hold values from -2 to 2
- segment_ids: int32 [8192], P('blk'), may hold values from 0 to 31, as said below
- block_mask: int32 [16], P('blk'), may hold values from 0 to 1, as said below
Outputs:
- new_streams: bfloat16 [8192, 4, 2048], P('blk', None, 'mp')
Inputs may be any that keep to these rules, and one draw needn't show every extreme that they name: `segment_ids`: never falls along the tokens; every prompt has 1 to 511 tokens, one of them exactly 511; each block of 512 tokens holds the start of two prompts. `block_mask`: entry b is 1 exactly where the first token of block b belongs to the prompt of the last token of block b - 1; entry 0 is 0.
All inputs are finite; a program needn't handle non-finite values.
Results may differ from a plain program's by a relative error of at most 0.0023.
Values may be sent and summed in bfloat16 or wider, within the bound.
No kernel may reach another device: no remote copies, remote signals or barrier semaphores. Data moves between devices by JAX's collectives and lax.ppermute only.
A program may use at most 128 MiB of HBM per device.

v0:
```python
import jax
import jax.numpy as jnp
from jax import lax
from jax.sharding import PartitionSpec as P

D = 2048
HEAD_DIM = 128
BLOCK = 512


def passed_along(value, axis, steps):
    count = lax.axis_size(axis)
    first, last = (max(0, -steps), min(count, count - steps))
    return lax.ppermute(value, axis, [(source, source + steps) for source in range(first, last)])


def rotate(values, positions):
    half_dim = values.shape[-1] // 2
    inverse = 10000.0 ** (-(jnp.arange(half_dim, dtype=jnp.float32) * 2.0 / values.shape[-1]))
    angles = positions.astype(jnp.float32)[:, None] * inverse[None, :]
    cosine = jnp.cos(angles)[:, None, :]
    sine = jnp.sin(angles)[:, None, :]
    first_half = values[..., :half_dim]
    second_half = values[..., half_dim:]
    return jnp.concatenate(
        [first_half * cosine - second_half * sine, second_half * cosine + first_half * sine],
        axis=-1,
    )


def body(streams, proj_master, hc_proj, hc_static, segment_ids, block_mask):
    highest = lax.Precision.HIGHEST
    tokens_local, stream_count, local_width = streams.shape
    heads_local = local_width // HEAD_DIM
    stream_values = streams.astype(jnp.float32)
    sum_first = jnp.sum(stream_values, axis=-1)
    sum_second = jnp.sum(stream_values * stream_values, axis=-1)
    projected = jnp.einsum("tkc,cj->tkj", stream_values, hc_proj, precision=highest)
    column_sum = jnp.sum(hc_proj, axis=0)
    sum_first, sum_second, projected, column_sum = lax.psum(
        (sum_first, sum_second, projected, column_sum), "mp"
    )
    stream_mean = sum_first / D
    stream_spread = sum_second / D - stream_mean * stream_mean
    inverse_std = lax.rsqrt(stream_spread + 1e-05)
    dynamic = jnp.tanh(inverse_std[..., None] * (projected - stream_mean[..., None] * column_sum))
    coefficients = hc_static[None] + dynamic
    input_mix = coefficients[..., 0]
    mixed = jnp.einsum("tk,tkc->tc", input_mix, stream_values, precision=highest)
    mixed_first, mixed_second = lax.psum(
        (jnp.sum(mixed, axis=-1), jnp.sum(mixed * mixed, axis=-1)), "mp"
    )
    mixed_mean = mixed_first / D
    mixed_spread = mixed_second / D - mixed_mean * mixed_mean
    normed = ((mixed - mixed_mean[:, None]) * lax.rsqrt(mixed_spread + 1e-05)[:, None]).astype(
        jnp.bfloat16
    )
    whole_rows = lax.all_gather(normed, "mp", axis=1, tiled=True)
    local_master = proj_master.astype(jnp.bfloat16)
    master_count = local_master.shape[0]
    cycle_size = lax.axis_size("blk")
    group_size = lax.axis_size("mp")
    slot_count = 4
    collected = lax.all_gather(local_master, "blk", axis=0, tiled=True)
    divided = lax.all_to_all(collected, "mp", split_axis=2, concat_axis=0, tiled=True)
    server = divided.reshape(group_size, cycle_size, master_count, slot_count, local_width)
    server = jnp.transpose(server, (1, 0, 2, 3, 4)).reshape(D, slot_count, local_width)
    server_flat = server.reshape(D, slot_count * local_width)
    qkv = jnp.dot(whole_rows, server_flat[:, : 3 * local_width], preferred_element_type=jnp.float32)
    cycle_index = lax.axis_index("blk")
    local_slots = jnp.arange(tokens_local, dtype=jnp.int32)
    global_slots = cycle_index * tokens_local + local_slots
    opening = jnp.concatenate([block_mask[:1] == 0, segment_ids[1:] != segment_ids[:-1]])
    local_start = lax.cummax(jnp.where(opening, global_slots, -1))
    carried = passed_along(local_start[-1:], "blk", 1)
    doc_start = jnp.where(local_start < 0, carried[0], local_start)
    positions = global_slots - doc_start
    queries = rotate(
        qkv[:, :local_width].reshape(tokens_local, heads_local, HEAD_DIM), positions
    ).astype(jnp.bfloat16)
    keys_rot = rotate(
        qkv[:, local_width : 2 * local_width].reshape(tokens_local, heads_local, HEAD_DIM),
        positions,
    ).astype(jnp.bfloat16)
    values_v = (
        qkv[:, 2 * local_width :].reshape(tokens_local, heads_local, HEAD_DIM).astype(jnp.bfloat16)
    )
    prior_keys, prior_values, prior_segments = passed_along(
        (keys_rot[-BLOCK:], values_v[-BLOCK:], segment_ids[-BLOCK:]), "blk", 1
    )
    keys_ext = jnp.concatenate([prior_keys, keys_rot])
    values_ext = jnp.concatenate([prior_values, values_v])
    segments_ext = jnp.concatenate([prior_segments, segment_ids])
    scale = 1.0 / HEAD_DIM**0.5

    def attend(block):
        offset = block * BLOCK
        query_rows = lax.dynamic_slice_in_dim(queries, offset, BLOCK, 0)
        key_rows = lax.dynamic_slice_in_dim(keys_ext, offset, 2 * BLOCK, 0)
        value_rows = lax.dynamic_slice_in_dim(values_ext, offset, 2 * BLOCK, 0)
        query_segments = lax.dynamic_slice_in_dim(segment_ids, offset, BLOCK, 0)
        key_segments = lax.dynamic_slice_in_dim(segments_ext, offset, 2 * BLOCK, 0)
        scores = (
            jnp.einsum("qhc,khc->hqk", query_rows, key_rows, preferred_element_type=jnp.float32)
            * scale
        )
        key_slot = jnp.arange(2 * BLOCK, dtype=jnp.int32)[None, :]
        query_slot = jnp.arange(BLOCK, dtype=jnp.int32)[:, None]
        current = (key_slot >= BLOCK) & (key_slot - BLOCK <= query_slot)
        earlier = (key_slot < BLOCK) & (block_mask[block] == 1)
        allowed = (query_segments[:, None] == key_segments[None, :]) & (current | earlier)
        masked = jnp.where(allowed[None], scores, -1e30)
        row_max = jnp.max(masked, axis=-1, keepdims=True)
        weights_exp = jnp.where(allowed[None], jnp.exp(masked - row_max), 0.0)
        row_total = jnp.sum(weights_exp, axis=-1)
        result = jnp.einsum(
            "hqk,khc->qhc",
            weights_exp.astype(jnp.bfloat16),
            value_rows,
            preferred_element_type=jnp.float32,
        )
        result = result / jnp.transpose(row_total)[:, :, None]
        return result.astype(jnp.bfloat16).reshape(BLOCK, local_width)

    block_total = tokens_local // BLOCK
    attended = lax.map(attend, jnp.arange(block_total, dtype=jnp.int32)).reshape(
        tokens_local, local_width
    )
    update_part = lax.dot_general(
        attended,
        server_flat[:, 3 * local_width :],
        (((1,), (1,)), ((), ())),
        preferred_element_type=jnp.float32,
    )
    update = lax.psum_scatter(update_part, "mp", scatter_dimension=1, tiled=True)
    kept = jnp.einsum(
        "tkj,tkc->tjc", coefficients[..., 1 : 1 + stream_count], stream_values, precision=highest
    )
    added = coefficients[..., 1 + stream_count][..., None] * update[:, None, :]
    return (kept + added).astype(jnp.bfloat16)


def solution(mesh):
    in_specs = (
        P("blk", None, "mp"),
        P(("blk", "mp"), None, None),
        P("mp", None),
        P(),
        P("blk"),
        P("blk"),
    )
    out_specs = P("blk", None, "mp")
    return jax.shard_map(body, mesh=mesh, in_specs=in_specs, out_specs=out_specs, check_vma=False)
```

profile of v0, /device:TPU:0, one launch (start us, length us, event | category | flops | bytes accessed | tf_op | source)
XLA Modules:
  0.0 667.8 jit_solution(271150901729547387)
XLA Ops:
  7.4 3.0 convert_element_type.40
  10.4 57.2 %all-gather.5.cloned.1.call-done = bf16[512,4,2048]{2,1,0:T(4,128)(2,1)} async-done(((bf16[64,4,2048]{2,1,0:T(4,128)(2,1)}), bf16[512,4,2048]{2,1,0:T(4,128)(2,1)}) %all-gather.5.cloned.1.call-update) | async-done | bytes 8388624 | tf_op jit(solution)/shard_map/all_gather | solution.py:64
  67.7 19.1 %copy.87 = bf16[512,4,2048]{0,1,2:T(4,128)(2,1)} copy(bf16[512,4,2048]{2,1,0:T(4,128)(2,1)} %all-gather.5.cloned.1.call-done) | data formatting | bytes 16777216 | tf_op jit(solution)/shard_map/all_gather | solution.py:64
  86.8 5.6 all-to-all-start
  92.5 5.6 fusion.28
  98.2 0.2 copy.83
  98.6 6.5 fusion.31
  105.1 184.4 %all-reduce.1 = (f32[6]{0:T(128)S(1)}, f32[1024,4]{0,1:T(4,128)S(1)}, f32[1024,4]{0,1:T(4,128)S(1)}) all-reduce(f32[6]{0:T(128)S(1)} %reduce_sum.59, f32[1024,4]{0,1:T(4,128)S(1)} %copy.83, f32[1024,4]{0,1:T(4,128)S(1)} %copy.82), channel_id=1, replica_groups=mesh['blk'=8,'mp'=4] {'mp'}, use_global_device_ids=true, to_apply=%region_6.0 | all-reduce | flops 8198 | bytes 65584 | tf_op jit(solution)/shard_map/psum | solution.py:40
  289.7 1.0 tanh_add_fusion
  290.7 0.2 copy.101
  290.9 8.9 %fusion.47 = f32[1024,1,512]{2,1,0:T(1,128)S(1)} fusion(f32[1024,4,1]{1,2,0:T(1,128)S(1)} %bitcast.72, bf16[1024,4,512]{2,1,0:T(4,128)(2,1)} %param.8), kind=kOutput, calls=%fused_computation.77 | convolution fusion | flops 25165824 | bytes 6307840 | tf_op jit(solution)/shard_map/tk,tkc->tc/dot_general | solution.py:49
  299.8 0.4 bitcast_reduce_fusion
  300.2 11.0 %all-reduce = (f32[1024]{0:T(1024)S(1)}, f32[1024]{0:T(1024)S(1)}) all-reduce(f32[1024]{0:T(1024)S(1)} %get-tuple-element.122, f32[1024]{0:T(1024)S(1)} %get-tuple-element.121), channel_id=1, replica_groups=mesh['blk'=8,'mp'=4] {'mp'}, use_global_device_ids=true, to_apply=%region_10.0 | all-reduce | flops 2048 | bytes 16384 | tf_op jit(solution)/shard_map/psum | solution.py:50
  311.2 1.3 fusion.36
  312.8 0.3 reduce-window.9
  313.3 0.6 slice.84
  313.9 2.2 collective-permute-start.2
  316.2 0.7 fusion.40
  316.9 3.1 multiply_cosine_fusion
  320.0 8.3 %copy.88 = bf16[512,4,2048]{0,2,1:T(8,128)(2,1)} copy(bf16[512,4,2048]{0,1,2:T(4,128)(2,1)} %all-to-all-done) | data formatting | bytes 16777216 | tf_op jit(solution)/shard_map/all_to_all | solution.py:65
  328.3 13.3 %copy.89 = bf16[4,512,4,512]{3,1,2,0:T(8,128)(2,1)} copy(bf16[4,512,4,512]{1,3,0,2:T(8,128)(2,1)} %bitcast.64) | data formatting | bytes 16777216 | tf_op jit(solution)/shard_map/all_to_all | solution.py:65
  341.5 11.1 %copy.90 = bf16[8,4,64,4,512]{4,3,2,1,0:T(4,128)(2,1)} copy(bf16[8,4,64,4,512]{4,2,0,3,1:T(8,128)(2,1)} %bitcast.65) | data formatting | bytes 16777216 | tf_op jit(solution)/shard_map/transpose | solution.py:67
  352.6 10.3 %copy.110 = bf16[256,8,4,512]{3,1,2,0:T(8,128)(2,1)} copy(bf16[256,8,4,512]{3,2,1,0:T(4,128)(2,1)} %bitcast.66) | data formatting | bytes 16777216
  362.9 27.6 %all-gather.3.cloned.1.call-done = bf16[1024,2048]{1,0:T(8,128)(2,1)} async-done(((bf16[1024,512]{1,0:T(8,128)(2,1)}), bf16[1024,2048]{1,0:T(8,128)(2,1)}) %all-gather.3.cloned.1.call-update) | async-done | bytes 4194320 | tf_op jit(solution)/shard_map/all_gather | solution.py:58
  390.5 11.1 %fusion.46 = (bf16[1024,1536]{1,0:T(8,128)(2,1)}, f32[1024,1536]{1,0:T(8,128)S(1)}) fusion(bf16[1024,2048]{1,0:T(8,128)(2,1)} %all-gather.3.cloned.1.call-done, bf16[2048,2048]{1,0:T(8,128)(2,1)} %bitcast.68), kind=kOutput, calls=%fused_computation.76 | convolution fusion | flops 6444023808 | bytes 19922944 | tf_op jit(solution)/shard_map/dot_general | solution.py:69
  401.6 2.4 fusion.42
  404.0 1.9 reshape.214
  405.9 14.2 %reshape.216 = f32[1024,4,128]{2,1,0:T(4,128)} reshape(f32[1024,512]{1,0:T(8,128)} %get-tuple-element.150) | data formatting | bytes 4194304 | tf_op jit(solution)/shard_map/reshape | solution.py:82
  420.1 4.7 fusion.43
  424.9 2.1 subtract_convert_fusion
  426.9 1.0 copy-done
  428.0 1.1 pad_maximum_fusion.2
  429.1 2.5 collective-permute-start.3
  431.6 2.9 collective-permute-start.1
  434.5 1.1 slice.95
  435.6 1.0 copy.102
  436.6 2.7 collective-permute-start
  439.3 1.3 slice.96
  440.6 1.3 copy.103
  441.9 2.9 pad_maximum_fusion.1
  444.8 1.7 maximum_maximum_fusion
  446.5 2.3 pad_maximum_fusion
  448.8 47.4 %while.12 = (s32[]{:T(128)}, bf16[2,512,512]{2,1,0:T(8,128)(2,1)}, s32[2]{0:T(128)S(1)}, bf16[1536,4,128]{0,2,1:T(8,128)(2,1)}, s32[1024]{0:T(1024)S(1)}, /*inde...) while((s32[]{:T(128)}, bf16[2,512,512]{2,1,0:T(8,128)(2,1)}, ...), condition=%wide.region_16.17_spmd, body=%wide.region_13.16_spmd.sunk | while | flops 1093669888 | bytes 37796688 | solution.py:126
  448.8 0.6 dynamic_slice.59
  450.1 5.5 fusion.67
  457.6 0.6 dynamic_slice.62
  458.8 0.6 fusion.68
  459.5 10.4 %fusion.69 = (f32[4,512]{1,0:T(4,128)S(1)}, bf16[4,512,1024]{2,1,0:T(8,128)(2,1)S(1)}) fusion(f32[4,512,1024]{2,1,0:T(8,128)} %fusion.67, pred[512,1024]{1,0:T(8,128)(4,1)S(1)} %fusion.68), kind=kOutput, calls=%fused_computation.71.clone.1 | output fusion | flops 16778240 | bytes 13115392 | tf_op jit(solution)/shard_map/while/body/eval_jaxpr/sub | solution.py:114
  469.9 1.5 fusion.70
  471.4 0.2 copy.125
  471.7 0.8 constant_dynamic-update-slice_fusion.2
  472.5 0.6 dynamic_slice.59
  473.7 5.5 fusion.67
  481.2 0.6 dynamic_slice.62
  482.5 0.6 fusion.68
  483.1 10.4 %fusion.69 = (f32[4,512]{1,0:T(4,128)S(1)}, bf16[4,512,1024]{2,1,0:T(8,128)(2,1)S(1)}) fusion(f32[4,512,1024]{2,1,0:T(8,128)} %fusion.67, pred[512,1024]{1,0:T(8,128)(4,1)S(1)} %fusion.68), kind=kOutput, calls=%fused_computation.71.clone.1 | output fusion | flops 16778240 | bytes 13115392 | tf_op jit(solution)/shard_map/while/body/eval_jaxpr/sub | solution.py:114
  493.6 1.5 fusion.70
  495.1 0.2 copy.125
  495.3 0.9 constant_dynamic-update-slice_fusion.2
  496.2 7.5 %fusion.33 = f32[1024,2048]{1,0:T(8,128)} fusion(bf16[1024,512]{1,0:T(8,128)(2,1)} %bitcast.73, bf16[2048,2048]{1,0:T(8,128)(2,1)} %bitcast.69), kind=kOutput, calls=%fused_computation.37 | convolution fusion | flops 2147483648 | bytes 11534336 | tf_op jit(solution)/shard_map/dot_general | solution.py:129
  503.7 0.2 copy.100
  504.0 0.9 copy.85
  504.9 142.8 %reduce-scatter.2.cloned.1.call-done = f32[1024,512]{1,0:T(8,128)} async-done(((f32[1024,2048]{1,0:T(8,128)}), f32[1024,512]{1,0:T(8,128)}) %reduce-scatter.2.cloned.1.call-update) | async-done | bytes 2097168 | tf_op jit(solution)/shard_map/reduce_scatter | solution.py:135
  647.7 12.3 %add_convert_fusion = bf16[1024,4,512]{2,1,0:T(4,128)(2,1)} fusion(f32[1024,4,4]{1,2,0:T(4,128)S(1)} %copy.85, bf16[1024,4,512]{2,1,0:T(4,128)(2,1)} %param.8, f32[1024,512]{1,0:T(8,128)} %reduce-scatter.2.cloned.1.call-done, f32[1024,4]{1,0:T(8,128)S(1)} %bitcast.71), kind=kOutput, calls=%fused_computation.32 | convolution fusion | flops 106954752 | bytes 10567680 | tf_op jit(solution)/shard_map/tkj,tkc->tjc/dot_general | solution.py:136
  (60 shorter events, 1.6 us)
Async XLA Ops:
  7.4 60.3 %all-gather.5.cloned.1.call-start = ((), (), s32[]{:S(2)}) async-start(), calls=%async_computation.4 | async-start | bytes 9437184 | tf_op jit(solution)/shard_map/all_gather | solution.py:64
  86.8 233.2 %all-to-all-start = ((bf16[512,4,2048]{0,1,2:T(4,128)(2,1)}), bf16[512,4,2048]{0,1,2:T(4,128)(2,1)}, u32[]{:S(2)}, u32[]{:S(2)}) async-start(bf16[512,4,2048]{0,1,2:T(4,128)(2,1)} %copy.87), calls=%async_computation | async-start | bytes 16777216 | tf_op jit(solution)/shard_map/all_to_all | solution.py:65
  92.4 6.0 copy-start.7
  92.4 197.2 %all-reduce.4.cloned.1.call-start = ((), (), s32[]{:S(2)}) async-start(), calls=%async_computation.2 | async-start | bytes 262144 | tf_op jit(solution)/shard_map/psum | solution.py:40
  98.6 191.1 %copy-start.8 = (f32[4,6]{1,0:T(4,128)S(1)}, f32[4,6]{1,0:T(4,128)}, u32[]{:S(2)}) copy-start(f32[4,6]{1,0:T(4,128)} %param.11) | copy-start | bytes 292
  105.1 285.4 %all-gather.3.cloned.1.call-start = ((), (), s32[]{:S(2)}) async-start(), calls=%async_computation.3 | async-start | bytes 5242880 | tf_op jit(solution)/shard_map/all_gather | solution.py:58
  311.1 1.4 copy-start.9
  311.2 1.5 copy-start.6
  312.5 335.2 %reduce-scatter.2.cloned.1.call-start = ((), (), s32[]{:S(2)}) async-start(), calls=%async_computation.5 | async-start | bytes 10485760 | tf_op jit(solution)/shard_map/reduce_scatter | solution.py:135
  313.9 2.3 collective-permute-start.2
  420.1 4.7 copy-start.3
  420.1 4.7 copy-start.4
  426.9 1.0 copy-start
  429.1 15.7 %collective-permute-start.3 = (bf16[512,4,128]{2,0,1:T(8,128)(2,1)}, bf16[512,4,128]{2,0,1:T(8,128)(2,1)}, u32[]{:S(2)}, u32[]{:S(2)}) collective-permute-start(bf16[512,4,128]{2,0,1:T(8,128)(2,1)} %pad_maximum_fusion.2), channel_id=1, source_target_pairs={{0,4},{4,8},{8,12},{12,16},{16,20},{20,24},{24,28},{1,5},{5,9},{9,... | collective-permute-start | bytes 1572872 | tf_op jit(solution)/shard_map/ppermute | solution.py:14
  431.6 7.7 %collective-permute-start.1 = (s32[512]{0:T(512)S(1)}, s32[512]{0:T(512)S(1)}, u32[]{:S(2)}, u32[]{:S(2)}) collective-permute-start(s32[512]{0:T(512)S(1)} %slice.76), channel_id=1, source_target_pairs={{0,4},{4,8},{8,12},{12,16},{16,20},{20,24},{24,28},{1,5},{5,9},{9,... | collective-permute-start | bytes 6152 | tf_op jit(solution)/shard_map/ppermute | solution.py:14
  436.6 10.0 %collective-permute-start = (bf16[512,4,128]{0,2,1:T(8,128)(2,1)}, bf16[512,4,128]{0,2,1:T(8,128)(2,1)}, u32[]{:S(2)}, u32[]{:S(2)}) collective-permute-start(bf16[512,4,128]{0,2,1:T(8,128)(2,1)} %bitcast.13), channel_id=1, source_target_pairs={{0,4},{4,8},{8,12},{12,16},{16,20},{20,24},{24,28},{1,5},{5,9},{9,... | collective-permute-start | bytes 1572872 | tf_op jit(solution)/shard_map/ppermute | solution.py:14
  441.9 2.9 copy-start.1
  444.8 1.8 copy-start.2
  459.4 10.5 %copy-start.5 = (bf16[1536,4,128]{0,2,1:T(8,128)(2,1)S(1)}, bf16[1536,4,128]{0,2,1:T(8,128)(2,1)}, u32[]{:S(2)}) copy-start(bf16[1536,4,128]{0,2,1:T(8,128)(2,1)} %get-tuple-element.274) | copy-start | bytes 4718596 | tf_op jit(solution)/shard_map/while
  483.1 10.5 %copy-start.5 = (bf16[1536,4,128]{0,2,1:T(8,128)(2,1)S(1)}, bf16[1536,4,128]{0,2,1:T(8,128)(2,1)}, u32[]{:S(2)}) copy-start(bf16[1536,4,128]{0,2,1:T(8,128)(2,1)} %get-tuple-element.274) | copy-start | bytes 4718596 | tf_op jit(solution)/shard_map/while
Sparse Core Ops, SparseCore 0:
  10.5 57.0 all-gather.4
Sparse Core Ops, SparseCore 1:
  105.2 66.4 all-reduce.3
  312.6 77.8 all-gather.2
  503.8 143.8 reduce-scatter.1
where the time goes:
time: 670 us; the launch traced here: 668 us
  waiting for transfers between devices  228 us (34%)
  blocking collectives  195 us (29%)
  local copies, waits for them, and re-layouts  98.3 us (15%)
  matrix products  60.4 us (9%)
  other arithmetic  47.9 us (7%)
  starting transfers between devices  16 us (2%)
  between operations  15.6 us (2%)
    psum x1, blocking collectives, body(): lax.psum((sum_first, sum_second, projected, column_sum), 'mp')  184 us
    reduce_scatter x1, waiting for transfers between devices, body(): lax.psum_scatter(update_part, 'mp', scatter_dimension=1, tiled=True)  143 us
    all_gather x1, waiting for transfers between devices, body(): collected = lax.all_gather(local_master, 'blk', axis=0, tiled=True)  57.2 us
    all_gather x1, waiting for transfers between devices, body(): whole_rows = lax.all_gather(normed, 'mp', axis=1, tiled=True)  27.6 us
    all_to_all x2, local copies, waits for them, and re-layouts, body(): lax.all_to_all(collected, 'mp', split_axis=2, concat_axis=0, tiled=True)  21.6 us
    sub x2, other arithmetic, attend(): weights_exp = jnp.where(allowed[None], jnp.exp(masked - row_max), 0.0)  20.9 us
    all_gather x1, local copies, waits for them, and re-layouts, body(): collected = lax.all_gather(local_master, 'blk', axis=0, tiled=True)  19.1 us
    reshape x1, local copies, waits for them, and re-layouts, body(): qkv[:, local_width:2 * local_width]  14.2 us
  transfers between devices with their start and end apart: 9, of which 4 were waited for; matrix products, arithmetic and copies ran while one was open for 12% of the time, Pallas kernels for 0%

commit v1 on v0

v1 whole, which is shorter than its diff:
```python
import functools

import jax
import jax.numpy as jnp
from jax import lax
from jax.experimental import pallas as pl
from jax.experimental.pallas import tpu as pltpu
from jax.sharding import PartitionSpec as P

D = 2048
HEAD_DIM = 128
BLOCK = 512
CHUNK = 256
SUB = 64
STREAMS = 4
EPS = 1e-05
BF = jnp.bfloat16
F32 = jnp.float32


def passed_along(value, axis, steps):
    count = lax.axis_size(axis)
    first, last = (max(0, -steps), min(count, count - steps))
    return lax.ppermute(value, axis, [(source, source + steps) for source in range(first, last)])


def from_others(value, axis):
    count = lax.axis_size(axis)
    return [
        lax.ppermute(value, axis, [(source, (source + step) % count) for source in range(count)])
        for step in range(1, count)
    ]


def cost(flops, nbytes, transcendentals=0):
    return pl.CostEstimate(flops=flops, bytes_accessed=nbytes, transcendentals=transcendentals)


def params(limit=40):
    return pltpu.CompilerParams(vmem_limit_bytes=limit << 20)


def split(value, parts):
    out = []
    for _ in range(parts):
        part = value.astype(BF)
        out.append(part)
        value = value - part.astype(F32)
    return out


def contract(a, b, a_dim, b_dim):
    return lax.dot_general(a, b, (((a_dim,), (b_dim,)), ((), ())), preferred_element_type=F32)


def iotas(rows, cols):
    return (
        lax.broadcasted_iota(jnp.int32, (rows, cols), 0),
        lax.broadcasted_iota(jnp.int32, (rows, cols), 1),
    )


def regroup_kernel(master_ref, qkv_ref, out_ref):
    width = out_ref.shape[-1]
    for slot in range(4):
        part = master_ref[:, slot, :].astype(BF)
        if slot < 3:
            qkv_ref[0, :, slot * width : (slot + 1) * width] = part
        else:
            out_ref[0] = part


def regroup(master, servers):
    rows, _, total = master.shape
    width = total // servers
    return pl.pallas_call(
        regroup_kernel,
        grid=(servers,),
        in_specs=[pl.BlockSpec((rows, 4, width), lambda i: (0, 0, i))],
        out_specs=[
            pl.BlockSpec((1, rows, 3 * width), lambda i: (i, 0, 0)),
            pl.BlockSpec((1, rows, width), lambda i: (i, 0, 0)),
        ],
        out_shape=[
            jax.ShapeDtypeStruct((servers, rows, 3 * width), BF),
            jax.ShapeDtypeStruct((servers, rows, width), BF),
        ],
        cost_estimate=cost(0, rows * total * 24),
        name="regroup",
    )(master)


def stats_kernel(x_ref, proj_ref, first_ref, second_ref):
    tokens, _, width = x_ref.shape
    proj = proj_ref[...]
    pieces = jnp.concatenate(split(proj, 3), axis=0)
    column = jnp.sum(proj, axis=1, keepdims=True)
    row, col = iotas(4 * SUB, 4 * SUB)
    same = (row >> 2) == (col >> 2)
    ring = jnp.where(same, (row - col) & 3, -1)
    for at in range(tokens // SUB):
        lanes = slice(at * 4 * SUB, (at + 1) * 4 * SUB)
        v = x_ref[at * SUB : (at + 1) * SUB].reshape(4 * SUB, width)
        sums = contract(pieces, v, 1, 1)
        sums = sums[0:8] + sums[8:16] + sums[16:24]
        gram = contract(v, v, 1, 1)
        first_ref[0:1, lanes] = sums[0:1]
        first_ref[1:2, lanes] = sums[6:7]
        for shift in range(3):
            first_ref[2 + shift : 3 + shift, lanes] = jnp.sum(
                jnp.where(ring == shift, gram, 0.0), axis=0, keepdims=True
            )
        first_ref[5:6, lanes] = jnp.broadcast_to(column[0:1], (1, 4 * SUB))
        first_ref[6:8, lanes] = sums[1:3]
        second_ref[0:3, lanes] = sums[3:6]
        second_ref[3:8, lanes] = jnp.broadcast_to(column[1:6], (5, 4 * SUB))


def stats(x, proj, start, tokens, step=128):
    width = x.shape[-1]
    return pl.pallas_call(
        stats_kernel,
        grid=(tokens // step,),
        in_specs=[
            pl.BlockSpec((step, 4, width), lambda i: (start // step + i, 0, 0)),
            pl.BlockSpec((8, width), lambda i: (0, 0)),
        ],
        out_specs=[pl.BlockSpec((8, 4 * step), lambda i: (0, i))] * 2,
        out_shape=[jax.ShapeDtypeStruct((8, 4 * tokens), F32)] * 2,
        cost_estimate=cost(tokens * 4 * width * 600, tokens * 8 * width),
        compiler_params=params(),
        name="stats",
    )(x, proj)


def by_stream(static_ref, column, stream):
    value = jnp.full(stream.shape, static_ref[0, column], F32)
    for k in range(1, 4):
        value = jnp.where(stream == k, static_ref[k, column], value)
    return value


def centre(first):
    mean = first[1:2] * (1.0 / D)
    spread = first[2:3] * (1.0 / D) - mean * mean
    return mean, lax.rsqrt(spread + EPS)


def mix_kernel(static_ref, x_ref, own_ref, a_ref, b_ref, c_ref, sums_ref, normed_ref):
    tokens, _, width = x_ref.shape
    lanes_total = 4 * tokens
    first = (own_ref[...] + a_ref[...]) + (b_ref[...] + c_ref[...])
    sums_ref[...] = first
    mean, inverse = centre(first)
    stream = lax.broadcasted_iota(jnp.int32, (1, lanes_total), 1) & 3
    mix = by_stream(static_ref, 0, stream) + jnp.tanh(
        inverse * (first[0:1] - mean * first[5:6])
    )
    one = jnp.where(stream < 3, pltpu.roll(mix, lanes_total - 1, 1), pltpu.roll(mix, 3, 1))
    two = jnp.where(stream < 2, pltpu.roll(mix, lanes_total - 2, 1), pltpu.roll(mix, 2, 1))
    linear = mix * first[1:2]
    square = mix * (mix * first[2:3] + 2.0 * one * first[3:4] + two * first[4:5])
    row, col = iotas(SUB, 4 * SUB)
    mine = row == (col >> 2)
    for at in range(tokens // SUB):
        lanes = slice(at * 4 * SUB, (at + 1) * 4 * SUB)
        v = x_ref[at * SUB : (at + 1) * SUB].reshape(4 * SUB, width)
        matrix = jnp.where(mine, mix[:, lanes], 0.0)
        mixed = contract(jnp.concatenate(split(matrix, 3), axis=0), v, 1, 0)
        mixed = mixed[0:SUB] + mixed[SUB : 2 * SUB] + mixed[2 * SUB : 3 * SUB]
        average = jnp.sum(jnp.where(mine, linear[:, lanes], 0.0), axis=1, keepdims=True) * (1.0 / D)
        power = jnp.sum(jnp.where(mine, square[:, lanes], 0.0), axis=1, keepdims=True) * (1.0 / D)
        scale = lax.rsqrt(jnp.maximum(power - average * average, 0.0) + EPS)
        normed_ref[at * SUB : (at + 1) * SUB, :] = ((mixed - average) * scale).astype(BF)


def mix(static, x, parts, start, tokens, offset, step=128):
    width = x.shape[-1]
    lane_block = pl.BlockSpec((8, 4 * step), lambda i: (0, offset // step + i))
    return pl.pallas_call(
        mix_kernel,
        grid=(tokens // step,),
        in_specs=[
            pl.BlockSpec(memory_space=pltpu.SMEM),
            pl.BlockSpec((step, 4, width), lambda i: (start // step + i, 0, 0)),
        ]
        + [lane_block] * 4,
        out_specs=[
            pl.BlockSpec((8, 4 * step), lambda i: (0, i)),
            pl.BlockSpec((step, width), lambda i: (i, 0)),
        ],
        out_shape=[
            jax.ShapeDtypeStruct((8, 4 * tokens), F32),
            jax.ShapeDtypeStruct((tokens, width), BF),
        ],
        cost_estimate=cost(tokens * 4 * width * 400, tokens * 10 * width),
        compiler_params=params(),
        name="mix",
    )(static, x, *parts)


def qkv_kernel(rows_ref, weight_ref, cosine_ref, sine_ref, out_ref):
    servers, _, width = rows_ref.shape
    total = contract(rows_ref[0], weight_ref[0:width, :], 1, 0)
    for server in range(1, servers):
        total += contract(rows_ref[server], weight_ref[server * width : (server + 1) * width, :], 1, 0)
    slot = pl.program_id(0)

    @pl.when(slot < 2)
    def _():
        cosine, sine = cosine_ref[...], sine_ref[...]
        for head in range(total.shape[1] // HEAD_DIM):
            part = total[:, head * HEAD_DIM : (head + 1) * HEAD_DIM]
            turned = part * cosine + pltpu.roll(part, HEAD_DIM // 2, 1) * sine
            out_ref[0, :, head * HEAD_DIM : (head + 1) * HEAD_DIM] = turned.astype(BF)

    @pl.when(slot == 2)
    def _():
        out_ref[0] = total.astype(BF)


def qkv_columns(rows, weight, cosine, sine, start):
    servers, tokens, width = rows.shape
    table = pl.BlockSpec((tokens, HEAD_DIM), lambda j: (start // tokens, 0))
    return pl.pallas_call(
        qkv_kernel,
        grid=(3,),
        in_specs=[
            pl.BlockSpec((servers, tokens, width), lambda j: (0, 0, 0)),
            pl.BlockSpec((D, width), lambda j: (0, j)),
            table,
            table,
        ],
        out_specs=pl.BlockSpec((1, tokens, width), lambda j: (j, 0, 0)),
        out_shape=jax.ShapeDtypeStruct((3, tokens, width), BF),
        cost_estimate=cost(2 * tokens * D * 3 * width, D * 6 * width + tokens * D * 5),
        compiler_params=params(),
        name="qkv",
    )(rows, weight, cosine, sine)


def attend_kernel(
    place_ref, q_ref, k0, k1, k2, v0, v1, v2, qseg_ref, kseg_ref, out_ref, sent_ref, own_ref
):
    tokens, width = q_ref.shape[1:]
    window = kseg_ref.shape[-1]
    place = place_ref[0]
    row, col = iotas(tokens, window)
    allowed = (qseg_ref[...] == kseg_ref[0]) & (col - (window - tokens) <= row)
    bias = jnp.where(allowed, 0.0, -1e30)
    factor = 1.4426950408889634 / HEAD_DIM**0.5
    heads = []
    for head in range(width // HEAD_DIM):
        lanes = slice(head * HEAD_DIM, (head + 1) * HEAD_DIM)
        query = q_ref[0, :, lanes]
        scores = jnp.concatenate(
            [contract(query, k[0, :, lanes], 1, 1) for k in (k0, k1, k2)], axis=1
        )
        scores = scores + bias
        weights = jnp.exp2((scores - jnp.max(scores, axis=1, keepdims=True)) * factor)
        total = jnp.sum(weights, axis=1, keepdims=True)
        values = jnp.concatenate([v[0, :, lanes] for v in (v0, v1, v2)], axis=0)
        heads.append((contract(weights.astype(BF), values, 1, 0) / total).astype(BF))
    attended = jnp.concatenate(heads, axis=1)
    for server in range(sent_ref.shape[0]):
        part = contract(attended, out_ref[server * width : (server + 1) * width, :], 1, 1)
        sent_ref[server] = jnp.where(place == server, 0.0, part).astype(BF)

        @pl.when(place == server)
        def _():
            own_ref[...] = part


def attend(place, query, window, qseg, kseg, weight, chunk):
    source, at = query
    width = source.shape[-1]
    servers = D // width
    block = (1, CHUNK, width)
    keys = [pl.BlockSpec(block, lambda i, s=slot, r=where: (s, r, 0)) for _, slot, where in window]
    values = [
        pl.BlockSpec(block, lambda i, s=slot + 1, r=where: (s, r, 0)) for _, slot, where in window
    ]
    arrays = [array for array, _, _ in window]
    reach = kseg.shape[-1]
    return pl.pallas_call(
        attend_kernel,
        grid=(1,),
        in_specs=[pl.BlockSpec(memory_space=pltpu.SMEM), pl.BlockSpec(block, lambda i: (0, at, 0))]
        + keys
        + values
        + [
            pl.BlockSpec((CHUNK, 1), lambda i: (chunk, 0)),
            pl.BlockSpec((1, 1, reach), lambda i: (chunk, 0, 0)),
            pl.BlockSpec((D, width), lambda i: (0, 0)),
        ],
        out_specs=[
            pl.BlockSpec((servers, CHUNK, width), lambda i: (0, 0, 0)),
            pl.BlockSpec((CHUNK, width), lambda i: (0, 0)),
        ],
        out_shape=[
            jax.ShapeDtypeStruct((servers, CHUNK, width), BF),
            jax.ShapeDtypeStruct((CHUNK, width), F32),
        ],
        cost_estimate=cost(
            4 * CHUNK * reach * width + 2 * CHUNK * D * width,
            D * width * 2 + CHUNK * width * 24,
            CHUNK * reach * 4,
        ),
        compiler_params=params(),
        name="attend",
    )(place, source, *arrays, *arrays, qseg, kseg, weight)


def final_kernel(
    static_ref, x_ref, first_ref, own2_ref, a_ref, b_ref, c_ref, other_ref, own_ref, *rest
):
    new_ref = rest[-1]
    tokens, _, width = x_ref.shape
    first = first_ref[...]
    second = (own2_ref[...] + a_ref[...]) + (b_ref[...] + c_ref[...])
    mean, inverse = centre(first)
    stream = lax.broadcasted_iota(jnp.int32, (1, 4 * tokens), 1) & 3

    def coefficient(column, projected):
        dynamic = jnp.tanh(inverse * (projected - mean * second[2 + column : 3 + column]))
        return by_stream(static_ref, column, stream) + dynamic

    projected = [first[6:7], first[7:8], second[0:1], second[1:2], second[2:3]]
    columns = [coefficient(1 + j, projected[j]) for j in range(5)]
    residual = jnp.concatenate(columns[:4] + columns[:4], axis=0)
    row, col = iotas(4 * SUB, 4 * SUB)
    same = (row >> 2) == (col >> 2)
    row, col = iotas(SUB, 4 * SUB)
    mine = row == (col >> 2)
    for at in range(tokens // SUB):
        lanes = slice(at * 4 * SUB, (at + 1) * 4 * SUB)
        rows = slice(at * SUB, (at + 1) * SUB)
        v = x_ref[rows].reshape(4 * SUB, width)
        matrix = jnp.where(same, jnp.tile(residual[:, lanes], (SUB // 2, 1)), 0.0)
        high, low = split(matrix, 2)
        new = contract(high, v, 1, 0) + contract(low, v, 1, 0)
        update = other_ref[rows, :].astype(F32) + own_ref[rows, :]
        update_high, update_low = split(update, 2)
        spread_high, spread_low = split(jnp.where(mine, columns[4][:, lanes], 0.0), 2)
        new += contract(
            jnp.concatenate([spread_high, spread_high, spread_low], axis=0),
            jnp.concatenate([update_high, update_low, update_high], axis=0),
            0,
            0,
        )
        new_ref[rows] = new.astype(BF).reshape(SUB, 4, width)


def final(static, x, first, first_at, second, second_at, others, own, start, previous, step=128):
    tokens, width = own.shape
    lane_block = pl.BlockSpec((8, 4 * step), lambda i: (0, second_at // step + i))
    stream_block = pl.BlockSpec((step, 4, width), lambda i: (start // step + i, 0, 0))
    specs = [
        pl.BlockSpec(memory_space=pltpu.SMEM),
        stream_block,
        pl.BlockSpec((8, 4 * step), lambda i: (0, first_at // step + i)),
    ]
    specs += [lane_block] * 4
    specs += [pl.BlockSpec((step, width), lambda i: (i, 0))] * 2
    args = [static, x, first, *second, others, own]
    aliases = {}
    if previous is not None:
        specs.append(pl.BlockSpec(memory_space=pl.ANY))
        aliases = {len(args): 0}
        args.append(previous)
    return pl.pallas_call(
        final_kernel,
        grid=(tokens // step,),
        in_specs=specs,
        out_specs=stream_block,
        out_shape=jax.ShapeDtypeStruct(x.shape, BF),
        input_output_aliases=aliases,
        cost_estimate=cost(tokens * 4 * width * 1200, tokens * 22 * width),
        compiler_params=params(),
        name="final",
    )(*args)


def body(streams, proj_master, hc_proj, hc_static, segment_ids, block_mask):
    tokens_local, _, width = streams.shape
    group_size = lax.axis_size("mp")
    place = lax.axis_index("mp").astype(jnp.int32).reshape(1)

    proj_rows = jnp.concatenate(
        [hc_proj.T, jnp.ones((1, width), F32), jnp.zeros((1, width), F32)], axis=0
    )
    first_late, second_late = stats(streams, proj_rows, BLOCK, BLOCK)
    late = [first_late] + from_others(first_late, "mp")
    qkv_part, out_part = regroup(proj_master, group_size)
    first_early, second_early = stats(streams, proj_rows, 0, BLOCK)
    early = [first_early] + from_others(first_early, "mp")

    def served(part):
        exchanged = lax.all_to_all(part, "mp", split_axis=0, concat_axis=0, tiled=True)
        return lax.all_gather(exchanged.reshape(-1, part.shape[-1]), "blk", axis=0, tiled=True)

    qkv_weight = served(qkv_part)
    out_weight = served(out_part)

    def gathered(normed):
        rows = lax.all_gather(normed, "mp", axis=0, tiled=True)
        return rows.reshape(group_size, normed.shape[0], width)

    sums_late, normed_late = mix(hc_static, streams, late, BLOCK, BLOCK, 0)
    rows_late = gathered(normed_late)
    sums_0, normed_0 = mix(hc_static, streams, early, 0, CHUNK, 0)
    rows_0 = gathered(normed_0)
    sums_1, normed_1 = mix(hc_static, streams, early, CHUNK, CHUNK, CHUNK)
    rows_1 = gathered(normed_1)
    second_late = [second_late] + from_others(second_late, "mp")
    second_early = [second_early] + from_others(second_early, "mp")

    halo = passed_along(segment_ids[-BLOCK:], "blk", 1)
    halo = jnp.where(lax.axis_index("blk") == 0, -1, halo)
    extended = jnp.concatenate([halo, segment_ids])
    key_at = jnp.arange(tokens_local + BLOCK, dtype=jnp.int32)[None, :]
    query_at = jnp.arange(tokens_local, dtype=jnp.int32)[:, None] + BLOCK
    earlier = (extended[None, :] == segment_ids[:, None]) & (key_at < query_at)
    positions = jnp.sum(earlier.astype(jnp.int32), axis=1)
    half = HEAD_DIM // 2
    inverse = 10000.0 ** (-(jnp.arange(half, dtype=F32) * 2.0 / HEAD_DIM))
    angles = positions.astype(F32)[:, None] * inverse[None, :]
    cosine, sine = jnp.cos(angles), jnp.sin(angles)
    cosine = jnp.concatenate([cosine, cosine], axis=1)
    sine = jnp.concatenate([-sine, sine], axis=1)
    windows = []
    for block in range(tokens_local // BLOCK):
        before = extended[block * BLOCK : (block + 1) * BLOCK]
        before = jnp.where(block_mask[block] == 1, before, -1)
        seen = jnp.concatenate([before, segment_ids[block * BLOCK : (block + 1) * BLOCK]])
        for chunk in range(BLOCK // CHUNK):
            windows.append(seen[chunk * CHUNK : chunk * CHUNK + BLOCK + CHUNK])
    key_segments = jnp.stack(windows)[:, None, :]
    query_segments = segment_ids[:, None]

    qkv_late = qkv_columns(rows_late, qkv_weight, cosine, sine, BLOCK)
    halo_rows = passed_along(qkv_late[1:3], "blk", 1)
    qkv_0 = qkv_columns(rows_0, qkv_weight, cosine, sine, 0)
    qkv_1 = qkv_columns(rows_1, qkv_weight, cosine, sine, CHUNK)

    chunks = [(halo_rows, 0, 0), (halo_rows, 0, 1), (qkv_0, 1, 0), (qkv_1, 1, 0)]
    chunks += [(qkv_late, 1, 0), (qkv_late, 1, 1)]
    order = [
        (0, (sums_0, 0), (second_early, 0)),
        (1, (sums_1, 0), (second_early, CHUNK)),
        (2, (sums_late, 0), (second_late, 0)),
        (3, (sums_late, CHUNK), (second_late, CHUNK)),
    ]
    result = None
    for chunk, (first, first_at), (second, second_at) in order:
        source, _, at = chunks[chunk + 2]
        sent, own = attend(
            place,
            (source, at),
            chunks[chunk : chunk + 3],
            query_segments,
            key_segments,
            out_weight,
            chunk,
        )
        others = lax.psum_scatter(
            sent.reshape(group_size * CHUNK, width), "mp", scatter_dimension=0, tiled=True
        )
        result = final(
            hc_static,
            streams,
            first,
            first_at,
            second,
            second_at,
            others,
            own,
            chunk * CHUNK,
            result,
        )
    return result


def solution(mesh):
    in_specs = (
        P("blk", None, "mp"),
        P(("blk", "mp"), None, None),
        P("mp", None),
        P(),
        P("blk"),
        P("blk"),
    )
    out_specs = P("blk", None, "mp")
    return jax.shard_map(body, mesh=mesh, in_specs=in_specs, out_specs=out_specs, check_vma=False)
```

time: 670 us -> 359 us (0.54)
  blocking collectives: 195 us -> 59.2 us
  waiting for transfers between devices: 228 us -> 150 us
  matrix products: 60.4 us -> 0 us
  Pallas kernels: 0 us -> 48.6 us
  local copies, waits for them, and re-layouts: 98.3 us -> 54.9 us
  other arithmetic: 47.9 us -> 6.45 us
  starting transfers between devices: 16 us -> 23.3 us
    psum x2 -> x0, blocking collectives: 195 us -> none  [the longest x1 184 us: body(): lax.psum((sum_first, sum_second, projected, column_sum), 'mp')]
    reduce_scatter x1 -> x4, waiting for transfers between devices: 143 us -> 62.1 us  [body(): lax.psum_scatter(sent.reshape(group_size * CHUNK, width), 'mp', scatter_d...]
    dot_general x9 -> x0, matrix products: 60.4 us -> none  [the longest x1 12.3 us: body(): jnp.einsum('tkj,tkc->tjc', coefficients[..., 1:1 + stream_count], stream_...]
    all_to_all x0 -> x2, blocking collectives: none -> 59.2 us  [served(): lax.all_to_all(part, 'mp', split_axis=0, concat_axis=0, tiled=True)]
    pallas_call x0 -> x17, Pallas kernels: none -> 48.6 us  [the longest x4 12.1 us: attend(): pl.pallas_call(attend_kernel, grid=(1,), in_specs=[pl.BlockSpec(memory_sp...]
    unnamed x19 -> x110, local copies, waits for them, and re-layouts: 11.4 us -> 52.1 us
    all_to_all x2 -> x0, local copies, waits for them, and re-layouts: 21.6 us -> none  [body(): lax.all_to_all(collected, 'mp', split_axis=2, concat_axis=0, tiled=True)]
    sub x4 -> x0, other arithmetic: 20.9 us -> none  [the longest x2 20.9 us: attend(): weights_exp = jnp.where(allowed[None], jnp.exp(masked - row_max), 0.0)]
  transfers between devices with their start and end apart: 9 -> 23, of which waited for: 4 -> 14; matrix products, arithmetic and copies ran while one was open for 12% -> 2% of each run, Pallas kernels for 0% -> 12%
where the time goes in v1:
time: 359 us; the launch traced here: 357 us
  waiting for transfers between devices  150 us (42%)
  blocking collectives  59.2 us (16%)
  local copies, waits for them, and re-layouts  54.9 us (15%)
  Pallas kernels  48.6 us (14%)
  starting transfers between devices  23.3 us (6%)
  between operations  14.9 us (4%)
  other arithmetic  6.45 us (2%)
    reduce_scatter x4, waiting for transfers between devices, body(): lax.psum_scatter(sent.reshape(group_size * CHUNK, width), 'mp', scatter_d...  62.1 us
    all_to_all x2, blocking collectives, served(): lax.all_to_all(part, 'mp', split_axis=0, concat_axis=0, tiled=True)  59.2 us
    unnamed x110, local copies, waits for them, and re-layouts  52.1 us
    all_gather x2, waiting for transfers between devices, served(): lax.all_gather(exchanged.reshape(-1, part.shape[-1]), 'blk', axis=0, tile...  41 us
    all_gather x3, waiting for transfers between devices, gathered(): rows = lax.all_gather(normed, 'mp', axis=0, tiled=True)  36.4 us
    ppermute x12, starting transfers between devices, from_others(): lax.ppermute(value, axis, [(source, (source + step) % count) for source i...  19.3 us
    pallas_call x4, Pallas kernels, attend(): pl.pallas_call(attend_kernel, grid=(1,), in_specs=[pl.BlockSpec(memory_sp...  12.1 us
    pallas_call x3, Pallas kernels, qkv_columns(): pl.pallas_call(qkv_kernel, grid=(3,), in_specs=[pl.BlockSpec((servers, to...  11 us
  transfers between devices with their start and end apart: 23, of which 14 were waited for; matrix products, arithmetic and copies ran while one was open for 2% of the time, Pallas kernels for 12%

profile of v1, /device:TPU:0, one launch (start us, length us, event | category | flops | bytes accessed | tf_op | source)
XLA Modules:
  0.0 357.4 jit_solution(11056051841308049863)
XLA Ops:
  7.5 2.2 copy-done
  9.7 2.1 stats.2
  11.7 3.1 collective-permute-start
  14.8 2.6 collective-permute-start.1
  17.4 1.3 collective-permute-start.2
  19.4 2.5 collective-permute-done.1.b_ref
  22.1 2.8 mix.3
  24.9 4.4 %regroup.1 = (bf16[4,64,1536]{2,1,0:T(8,128)(2,1)}, bf16[4,64,512]{2,1,0:T(8,128)(2,1)}) custom-call(f32[64,4,2048]{2,1,0:T(4,128)} %master_ref.1), custom_call_target="tpu_custom_call" | custom-call | bytes 3145728 | tf_op jit(solution)/shard_map/regroup/pallas_call | solution.py:76
  29.4 45.6 %all_to_all.10 = bf16[4,64,1536]{2,1,0:T(8,128)(2,1)} all-to-all(bf16[4,64,1536]{2,1,0:T(8,128)(2,1)} %get-tuple-element.29), channel_id=1, replica_groups=mesh['blk'=8,'mp'=4] {'mp'}, dimensions={0} | all-to-all | bytes 1572864 | tf_op jit(solution)/shard_map/all_to_all | solution.py:399
  75.1 2.2 copy-done.1
  77.3 2.0 stats.3
  80.0 3.4 collective-permute-start.8
  83.8 4.1 %collective-permute-done.7.a_ref = f32[8,2048]{1,0:T(8,128)S(1)} collective-permute-done((f32[8,2048]{1,0:T(8,128)S(1)}, f32[8,2048]{1,0:T(8,128)S(1)}, u32[]{:S(2)}, u32[]{:S(2)}) %collective-permute-start.7) | collective-permute-done | bytes 65568 | tf_op jit(solution)/shard_map/ppermute | solution.py:30
  87.9 2.5 collective-permute-done.8.b_ref
  90.3 1.8 mix.5
  92.3 13.6 %all_to_all.11 = bf16[4,64,512]{2,1,0:T(8,128)(2,1)} all-to-all(bf16[4,64,512]{2,1,0:T(8,128)(2,1)S(1)} %copy-done.50), channel_id=1, replica_groups=mesh['blk'=8,'mp'=4] {'mp'}, dimensions={0} | all-to-all | bytes 524288 | tf_op jit(solution)/shard_map/all_to_all | solution.py:399
  107.8 1.3 collective-permute-start.6
  110.4 1.6 convert_reduce_fusion
  112.0 1.9 fusion.1
  113.9 2.2 copy-done.2
  116.1 1.8 mix.4
  118.4 20.9 %all-gather.8.cloned.1.call-done.weight_ref = bf16[2048,1536]{1,0:T(8,128)(2,1)} async-done(((bf16[256,1536]{1,0:T(8,128)(2,1)}), bf16[2048,1536]{1,0:T(8,128)(2,1)}) %all-gather.8.cloned.1.call-update) | async-done | bytes 6291472 | tf_op jit(solution)/shard_map/all_gather | solution.py:400
  139.3 2.8 copy-done.13
  142.1 1.6 copy-done.49
  143.7 4.9 %qkv.3.q_ref.k1.k2.v1.v2 = bf16[3,512,512]{2,1,0:T(8,128)(2,1)S(1)} custom-call(bf16[4,512,512]{2,1,0:T(8,128)(2,1)S(1)} %bitcast.22, bf16[2048,1536]{1,0:T(8,128)(2,1)S(1)} %copy-done.13, f32[1024,128]{1,0:T(8,128)S(1)} %get-tuple-element.59.cosine_ref, f32[1024,128]{1,0:T(8,128)S(1)} %get-tuple-element.60.sine_ref), custom_call_target="tpu_custom_call" | custom-call | flops 3221225472 | bytes 11534336 | tf_op jit(solution)/shard_map/qkv/pallas_call | solution.py:225
  149.7 2.2 collective-permute-start.13
  153.7 15.1 %all-gather.14.cloned.1.call-done = bf16[1024,512]{1,0:T(8,128)(2,1)} async-done(((bf16[256,512]{1,0:T(8,128)(2,1)}), bf16[1024,512]{1,0:T(8,128)(2,1)}) %all-gather.14.cloned.1.call-update) | async-done | bytes 1048592 | tf_op jit(solution)/shard_map/all_gather | solution.py:406
  168.8 2.8 copy-done.14
  171.6 1.0 copy-done.21
  172.7 1.0 copy-done.24
  173.7 1.2 copy-done.26
  174.9 3.0 qkv.5.k0.v0.k1.v1.q_ref.k2.v2
  178.0 20.1 %all-gather.12.cloned.1.call-done.out_ref = bf16[2048,512]{1,0:T(8,128)(2,1)} async-done(((bf16[256,512]{1,0:T(8,128)(2,1)}), bf16[2048,512]{1,0:T(8,128)(2,1)}) %all-gather.12.cloned.1.call-update) | async-done | bytes 2097168 | tf_op jit(solution)/shard_map/all_gather | solution.py:400
  198.0 2.0 copy-done.9
  200.0 1.0 copy-done.16
  201.0 3.0 attend.7
  206.1 21.3 %all-gather.10.cloned.1.call-done = bf16[1024,512]{1,0:T(8,128)(2,1)} async-done(((bf16[256,512]{1,0:T(8,128)(2,1)}), bf16[1024,512]{1,0:T(8,128)(2,1)}) %all-gather.10.cloned.1.call-update) | async-done | bytes 1048592 | tf_op jit(solution)/shard_map/all_gather | solution.py:406
  227.4 2.8 copy-done.15
  230.2 1.0 copy-done.22
  231.2 1.0 copy-done.25
  232.3 1.2 copy-done.27
  233.5 3.0 qkv.4.k0.v0.k1.v1.q_ref.k2.v2
  236.6 3.0 attend.6
  241.5 1.6 copy-done.11
  243.1 1.0 copy-done.18
  244.2 3.0 attend.5
  249.1 1.6 copy-done.12
  251.7 3.0 attend.4
  255.8 1.5 collective-permute-start.10
  258.3 2.4 collective-permute-start.12
  260.7 1.6 collective-permute-start.4
  262.6 2.0 collective-permute-start.5
  264.6 2.2 copy-done.3
  266.8 1.0 copy-done.37
  268.8 2.6 final.4.rest_0_
  271.4 16.9 %reduce-scatter.9.cloned.1.call-done.other_ref = bf16[256,512]{1,0:T(8,128)(2,1)} async-done(((bf16[1024,512]{1,0:T(8,128)(2,1)}), bf16[256,512]{1,0:T(8,128)(2,1)}) %reduce-scatter.9.cloned.1.call-update) | async-done | bytes 262160 | tf_op jit(solution)/shard_map/reduce_scatter | solution.py:466
  288.4 2.2 copy-done.4
  291.5 2.6 final.5.rest_0_
  294.2 22.7 %reduce-scatter.7.cloned.1.call-done.other_ref = bf16[256,512]{1,0:T(8,128)(2,1)} async-done(((bf16[1024,512]{1,0:T(8,128)(2,1)}), bf16[256,512]{1,0:T(8,128)(2,1)}) %reduce-scatter.7.cloned.1.call-update) | async-done | bytes 262160 | tf_op jit(solution)/shard_map/reduce_scatter | solution.py:466
  316.9 2.2 copy-done.5
  320.0 2.6 final.6.rest_0_
  322.7 22.4 %reduce-scatter.5.cloned.1.call-done.other_ref = bf16[256,512]{1,0:T(8,128)(2,1)} async-done(((bf16[1024,512]{1,0:T(8,128)(2,1)}), bf16[256,512]{1,0:T(8,128)(2,1)}) %reduce-scatter.5.cloned.1.call-update) | async-done | bytes 262160 | tf_op jit(solution)/shard_map/reduce_scatter | solution.py:466
  345.1 2.2 copy-done.6
  348.2 2.6 final.7
  (145 shorter events, 21.2 us)
Async XLA Ops:
  6.5 15.6 %copy-start.44 = (f32[4,6]{1,0:T(4,128)S(1)}, f32[4,6]{1,0:T(4,128)}, u32[]{:S(2)}) copy-start(f32[4,6]{1,0:T(4,128)} %static_ref.13) | copy-start | bytes 292
  6.5 111.8 %all-gather.6.cloned.1.call-start = ((), (), s32[]{:S(2)}) async-start(), calls=%async_computation.6 | async-start | bytes 2621440 | tf_op jit(solution)/shard_map/all_gather | solution.py:406
  7.5 2.2 copy-start
  11.7 7.6 %collective-permute-start = (f32[8,2048]{1,0:T(8,128)S(1)}, f32[8,2048]{1,0:T(8,128)S(1)}, u32[]{:S(2)}, u32[]{:S(2)}) collective-permute-start(f32[8,2048]{1,0:T(8,128)S(1)} %get-tuple-element.25.own_ref), channel_id=1, source_target_pairs={{0,1},{1,2},{2,3},{3,0},{4,5},{5,6},{6,7},{7,4},{8,9},{9,10},{10,1... | collective-permute-start | bytes 196616 | tf_op jit(solution)/shard_map/ppermute | solution.py:30
  14.8 7.1 %collective-permute-start.1 = (f32[8,2048]{1,0:T(8,128)S(1)}, f32[8,2048]{1,0:T(8,128)S(1)}, u32[]{:S(2)}, u32[]{:S(2)}) collective-permute-start(f32[8,2048]{1,0:T(8,128)S(1)} %get-tuple-element.25.own_ref), channel_id=1, source_target_pairs={{0,2},{1,3},{2,0},{3,1},{4,6},{5,7},{6,4},{7,5},{8,10},{9,11},{10,... | collective-permute-start | bytes 196616 | tf_op jit(solution)/shard_map/ppermute | solution.py:30
  17.4 4.7 %collective-permute-start.2 = (f32[8,2048]{1,0:T(8,128)S(1)}, f32[8,2048]{1,0:T(8,128)S(1)}, u32[]{:S(2)}, u32[]{:S(2)}) collective-permute-start(f32[8,2048]{1,0:T(8,128)S(1)} %get-tuple-element.25.own_ref), channel_id=1, source_target_pairs={{0,3},{1,0},{2,1},{3,2},{4,7},{5,4},{6,5},{7,6},{8,11},{9,8},{10,9... | collective-permute-start | bytes 196616 | tf_op jit(solution)/shard_map/ppermute | solution.py:30
  24.9 114.4 %all-gather.8.cloned.1.call-start = ((), (), s32[]{:S(2)}) async-start(), calls=%async_computation.7 | async-start | bytes 7077888 | tf_op jit(solution)/shard_map/all_gather | solution.py:400
  75.0 93.8 %all-gather.14.cloned.1.call-start = ((), (), s32[]{:S(2)}) async-start(), calls=%async_computation.11 | async-start | bytes 1310720 | tf_op jit(solution)/shard_map/all_gather | solution.py:406
  75.1 2.2 copy-start.1
  77.3 15.0 %copy-start.50 = (bf16[4,64,512]{2,1,0:T(8,128)(2,1)S(1)}, bf16[4,64,512]{2,1,0:T(8,128)(2,1)}, u32[]{:S(2)}) copy-start(bf16[4,64,512]{2,1,0:T(8,128)(2,1)} %get-tuple-element.32) | copy-start | bytes 786436
  77.3 28.6 %copy-start.54 = (s32[2]{0:T(128)S(1)}, s32[2]{0:T(128)}, u32[]{:S(2)}) copy-start(s32[2]{0:T(128)} %param.11) | copy-start | bytes 28
  77.3 29.9 %copy-start.51 = (s32[1024]{0:T(1024)S(1)}, s32[1024]{0:T(1024)}, u32[]{:S(2)}) copy-start(s32[1024]{0:T(1024)} %param.10) | copy-start | bytes 12292
  80.0 7.9 %collective-permute-start.7 = (f32[8,2048]{1,0:T(8,128)S(1)}, f32[8,2048]{1,0:T(8,128)S(1)}, u32[]{:S(2)}, u32[]{:S(2)}) collective-permute-start(f32[8,2048]{1,0:T(8,128)S(1)} %get-tuple-element.30.own_ref), channel_id=1, source_target_pairs={{0,1},{1,2},{2,3},{3,0},{4,5},{5,6},{6,7},{7,4},{8,9},{9,10},{10,1... | collective-permute-start | bytes 196616 | tf_op jit(solution)/shard_map/ppermute | solution.py:30
  80.0 10.4 %collective-permute-start.8 = (f32[8,2048]{1,0:T(8,128)S(1)}, f32[8,2048]{1,0:T(8,128)S(1)}, u32[]{:S(2)}, u32[]{:S(2)}) collective-permute-start(f32[8,2048]{1,0:T(8,128)S(1)} %get-tuple-element.30.own_ref), channel_id=1, source_target_pairs={{0,2},{1,3},{2,0},{3,1},{4,6},{5,7},{6,4},{7,5},{8,10},{9,11},{10,... | collective-permute-start | bytes 196616 | tf_op jit(solution)/shard_map/ppermute | solution.py:30
  83.4 7.0 %collective-permute-start.9 = (f32[8,2048]{1,0:T(8,128)S(1)}, f32[8,2048]{1,0:T(8,128)S(1)}, u32[]{:S(2)}, u32[]{:S(2)}) collective-permute-start(f32[8,2048]{1,0:T(8,128)S(1)} %get-tuple-element.30.own_ref), channel_id=1, source_target_pairs={{0,3},{1,0},{2,1},{3,2},{4,7},{5,4},{6,5},{7,6},{8,11},{9,8},{10,9... | collective-permute-start | bytes 196616 | tf_op jit(solution)/shard_map/ppermute | solution.py:30
  92.2 19.8 %copy-start.47 = (f32[8,1024]{1,0:T(8,128)}, f32[8,1024]{1,0:T(8,128)S(1)}, u32[]{:S(2)}) copy-start(f32[8,1024]{1,0:T(8,128)S(1)} %get-tuple-element.42.first_ref) | copy-start | bytes 98308
  92.2 105.8 %all-gather.12.cloned.1.call-start = ((), (), s32[]{:S(2)}) async-start(), calls=%async_computation.9 | async-start | bytes 2359296 | tf_op jit(solution)/shard_map/all_gather | solution.py:400
  105.9 121.5 %all-gather.10.cloned.1.call-start = ((), (), s32[]{:S(2)}) async-start(), calls=%async_computation.8 | async-start | bytes 1310720 | tf_op jit(solution)/shard_map/all_gather | solution.py:406
  107.8 2.1 copy-start.52
  107.8 2.1 collective-permute-start.6
  113.9 2.2 copy-start.2
  117.9 21.4 %copy-start.45 = (f32[8,1024]{1,0:T(8,128)}, f32[8,1024]{1,0:T(8,128)S(1)}, u32[]{:S(2)}) copy-start(f32[8,1024]{1,0:T(8,128)S(1)} %get-tuple-element.38.first_ref) | copy-start | bytes 98308
  117.9 146.7 %reduce-scatter.11.cloned.1.call-start = ((), (), s32[]{:S(2)}) async-start(), calls=%async_computation.14 | async-start | bytes 1310720 | tf_op jit(solution)/shard_map/reduce_scatter | solution.py:466
  118.3 30.3 %copy-start.20 = (f32[1024,128]{1,0:T(8,128)}, f32[1024,128]{1,0:T(8,128)S(1)}, u32[]{:S(2)}) copy-start(f32[1024,128]{1,0:T(8,128)S(1)} %get-tuple-element.59.cosine_ref) | copy-start | bytes 1572868
  118.3 30.3 %copy-start.23 = (f32[1024,128]{1,0:T(8,128)}, f32[1024,128]{1,0:T(8,128)S(1)}, u32[]{:S(2)}) copy-start(f32[1024,128]{1,0:T(8,128)S(1)} %get-tuple-element.60.sine_ref) | copy-start | bytes 1572868
  139.3 2.8 copy-start.13
  142.1 1.6 copy-start.49
  143.7 9.3 %copy-start.53 = (s32[512]{0:T(512)S(1)}, s32[512]{0:T(512)}, u32[]{:S(2)}) copy-start(s32[512]{0:T(512)} %copy-done.52) | copy-start | bytes 6148
  149.7 48.3 %collective-permute-start.13 = (bf16[2,512,512]{2,1,0:T(8,128)(2,1)}, bf16[2,512,512]{2,1,0:T(8,128)(2,1)S(1)}, u32[]{:S(2)}, u32[]{:S(2)}) collective-permute-start(bf16[2,512,512]{2,1,0:T(8,128)(2,1)} %slice.38), channel_id=1, source_target_pairs={{0,4},{4,8},{8,12},{12,16},{16,20},{20,24},{24,28},{1,5},{5,9},{9,... | collective-permute-start | bytes 3145736 | tf_op jit(solution)/shard_map/ppermute | solution.py:24
  168.8 2.8 copy-start.14
  171.6 1.0 copy-start.21
  172.7 1.0 copy-start.24
  173.7 1.2 copy-start.26
  198.0 6.1 %copy-start.7 = (bf16[2,512,512]{2,1,0:T(8,128)(2,1)}, bf16[2,512,512]{2,1,0:T(8,128)(2,1)S(1)}, u32[]{:S(2)}) copy-start(bf16[2,512,512]{2,1,0:T(8,128)(2,1)S(1)} %collective-permute-done.13.k0.v0.k1.v1) | copy-start | bytes 3145732
  198.0 2.0 copy-start.9
  200.0 1.0 copy-start.16
  205.9 82.5 %reduce-scatter.9.cloned.1.call-start = ((), (), s32[]{:S(2)}) async-start(), calls=%async_computation.13 | async-start | bytes 1310720 | tf_op jit(solution)/shard_map/reduce_scatter | solution.py:466
  227.4 2.8 copy-start.15
  230.2 1.0 copy-start.22
  231.2 1.0 copy-start.25
  232.3 1.2 copy-start.27
  233.5 3.0 copy-start.8
  233.5 3.0 copy-start.10
  233.5 3.1 copy-start.17
  241.4 75.4 %reduce-scatter.7.cloned.1.call-start = ((), (), s32[]{:S(2)}) async-start(), calls=%async_computation.12 | async-start | bytes 1310720 | tf_op jit(solution)/shard_map/reduce_scatter | solution.py:466
  241.5 1.6 copy-start.11
  243.1 1.0 copy-start.18
  249.0 96.1 %reduce-scatter.5.cloned.1.call-start = ((), (), s32[]{:S(2)}) async-start(), calls=%async_computation.10 | async-start | bytes 1310720 | tf_op jit(solution)/shard_map/reduce_scatter | solution.py:466
  249.1 1.6 copy-start.12
  251.7 4.1 %copy-start.43 = (f32[8,2048]{1,0:T(8,128)S(1)}, f32[8,2048]{1,0:T(8,128)}, u32[]{:S(2)}) copy-start(f32[8,2048]{1,0:T(8,128)} %copy-done.42) | copy-start | bytes 196612
  251.7 12.9 %copy-start.48 = (f32[8,1024]{1,0:T(8,128)S(1)}, f32[8,1024]{1,0:T(8,128)}, u32[]{:S(2)}) copy-start(f32[8,1024]{1,0:T(8,128)} %copy-done.47) | copy-start | bytes 98308
  255.8 6.8 %collective-permute-start.10 = (f32[8,2048]{1,0:T(8,128)S(1)}, f32[8,2048]{1,0:T(8,128)S(1)}, u32[]{:S(2)}, u32[]{:S(2)}) collective-permute-start(f32[8,2048]{1,0:T(8,128)S(1)} %copy-done.43), channel_id=1, source_target_pairs={{0,1},{1,2},{2,3},{3,0},{4,5},{5,6},{6,7},{7,4},{8,9},{9,10},{10,1... | collective-permute-start | bytes 196616 | tf_op jit(solution)/shard_map/ppermute | solution.py:30
  257.3 7.3 %collective-permute-start.11 = (f32[8,2048]{1,0:T(8,128)S(1)}, f32[8,2048]{1,0:T(8,128)S(1)}, u32[]{:S(2)}, u32[]{:S(2)}) collective-permute-start(f32[8,2048]{1,0:T(8,128)S(1)} %copy-done.43), channel_id=1, source_target_pairs={{0,2},{1,3},{2,0},{3,1},{4,6},{5,7},{6,4},{7,5},{8,10},{9,11},{10,... | collective-permute-start | bytes 196616 | tf_op jit(solution)/shard_map/ppermute | solution.py:30
  258.3 6.3 %collective-permute-start.12 = (f32[8,2048]{1,0:T(8,128)S(1)}, f32[8,2048]{1,0:T(8,128)S(1)}, u32[]{:S(2)}, u32[]{:S(2)}) collective-permute-start(f32[8,2048]{1,0:T(8,128)S(1)} %copy-done.43), channel_id=1, source_target_pairs={{0,3},{1,0},{2,1},{3,2},{4,7},{5,4},{6,5},{7,6},{8,11},{9,8},{10,9... | collective-permute-start | bytes 196616 | tf_op jit(solution)/shard_map/ppermute | solution.py:30
  260.7 33.5 %collective-permute-start.3 = (f32[8,2048]{1,0:T(8,128)S(1)}, f32[8,2048]{1,0:T(8,128)S(1)}, u32[]{:S(2)}, u32[]{:S(2)}) collective-permute-start(f32[8,2048]{1,0:T(8,128)S(1)} %get-tuple-element.27.own2_ref), channel_id=1, source_target_pairs={{0,1},{1,2},{2,3},{3,0},{4,5},{5,6},{6,7},{7,4},{8,9},{9,10},{10,1... | collective-permute-start | bytes 196616 | tf_op jit(solution)/shard_map/ppermute | solution.py:30
  260.7 33.5 %collective-permute-start.4 = (f32[8,2048]{1,0:T(8,128)S(1)}, f32[8,2048]{1,0:T(8,128)S(1)}, u32[]{:S(2)}, u32[]{:S(2)}) collective-permute-start(f32[8,2048]{1,0:T(8,128)S(1)} %get-tuple-element.27.own2_ref), channel_id=1, source_target_pairs={{0,2},{1,3},{2,0},{3,1},{4,6},{5,7},{6,4},{7,5},{8,10},{9,11},{10,... | collective-permute-start | bytes 196616 | tf_op jit(solution)/shard_map/ppermute | solution.py:30
  262.6 31.6 %collective-permute-start.5 = (f32[8,2048]{1,0:T(8,128)S(1)}, f32[8,2048]{1,0:T(8,128)S(1)}, u32[]{:S(2)}, u32[]{:S(2)}) collective-permute-start(f32[8,2048]{1,0:T(8,128)S(1)} %get-tuple-element.27.own2_ref), channel_id=1, source_target_pairs={{0,3},{1,0},{2,1},{3,2},{4,7},{5,4},{6,5},{7,6},{8,11},{9,8},{10,9... | collective-permute-start | bytes 196616 | tf_op jit(solution)/shard_map/ppermute | solution.py:30
  264.6 2.2 copy-start.3
  268.8 19.6 %copy-start.35 = (f32[256,512]{1,0:T(8,128)S(1)}, f32[256,512]{1,0:T(8,128)}, u32[]{:S(2)}) copy-start(f32[256,512]{1,0:T(8,128)} %copy-done.34) | copy-start | bytes 1572868
  268.8 19.6 %copy-start.46 = (f32[8,1024]{1,0:T(8,128)S(1)}, f32[8,1024]{1,0:T(8,128)}, u32[]{:S(2)}) copy-start(f32[8,1024]{1,0:T(8,128)} %copy-done.45) | copy-start | bytes 98308
  288.4 2.2 copy-start.4
  291.5 25.4 %copy-start.33 = (f32[256,512]{1,0:T(8,128)S(1)}, f32[256,512]{1,0:T(8,128)}, u32[]{:S(2)}) copy-start(f32[256,512]{1,0:T(8,128)} %copy-done.32) | copy-start | bytes 1572868
  316.9 2.2 copy-start.5
  345.1 2.2 copy-start.6
  (14 other events, 12.9 us)
Sparse Core Ops, SparseCore 0:
  25.0 68.3 all-gather.5
  95.3 43.9 all-gather.7
  140.9 27.9 all-gather.13
  170.6 27.3 all-gather.11
  199.4 27.9 all-gather.9
  229.5 26.6 reduce-scatter.10
  258.6 29.7 reduce-scatter.8
  290.7 26.1 reduce-scatter.6
  319.3 25.7 reduce-scatter.4

commit v2 on v1

--- a/solution.py
+++ b/solution.py
@@ -36,7 +36,7 @@
     return pl.CostEstimate(flops=flops, bytes_accessed=nbytes, transcendentals=transcendentals)
 
 
-def params(limit=40):
+def params(limit=60):
     return pltpu.CompilerParams(vmem_limit_bytes=limit << 20)
 
 
@@ -60,34 +60,70 @@
     )
 
 
-def regroup_kernel(master_ref, qkv_ref, out_ref):
-    width = out_ref.shape[-1]
-    for slot in range(4):
-        part = master_ref[:, slot, :].astype(BF)
-        if slot < 3:
-            qkv_ref[0, :, slot * width : (slot + 1) * width] = part
-        else:
-            out_ref[0] = part
-
-
-def regroup(master, servers):
+def regroup_kernel(place_ref, master_ref, *parts):
+    servers = len(parts)
+    width = master_ref.shape[-1] // servers
+    for step, part_ref in enumerate(parts):
+        server = (place_ref[0] + step) % servers
+        own = pl.ds(pl.multiple_of(server * width, width), width)
+        pair = pl.ds(pl.multiple_of((server // 2) * 2 * width, 2 * width), 2 * width)
+        for slot in range(3):
+            part_ref[:, slot * width : (slot + 1) * width] = master_ref[:, slot, own].astype(BF)
+        part_ref[:, 3 * width :] = master_ref[:, 3, pair].astype(BF)
+
+
+def regroup(place, master, servers):
     rows, _, total = master.shape
-    width = total // servers
+    columns = 5 * total // servers
     return pl.pallas_call(
         regroup_kernel,
-        grid=(servers,),
-        in_specs=[pl.BlockSpec((rows, 4, width), lambda i: (0, 0, i))],
-        out_specs=[
-            pl.BlockSpec((1, rows, 3 * width), lambda i: (i, 0, 0)),
-            pl.BlockSpec((1, rows, width), lambda i: (i, 0, 0)),
-        ],
-        out_shape=[
-            jax.ShapeDtypeStruct((servers, rows, 3 * width), BF),
-            jax.ShapeDtypeStruct((servers, rows, width), BF),
-        ],
-        cost_estimate=cost(0, rows * total * 24),
+        in_specs=[pl.BlockSpec(memory_space=pltpu.SMEM), pl.BlockSpec(memory_space=pltpu.VMEM)],
+        out_specs=[pl.BlockSpec(memory_space=pltpu.VMEM)] * servers,
+        out_shape=[jax.ShapeDtypeStruct((rows, columns), BF)] * servers,
+        cost_estimate=cost(0, rows * total * 26),
+        compiler_params=params(),
         name="regroup",
-    )(master)
+    )(place, master)
+
+
+def assemble_kernel(place_ref, *refs):
+    out_ref = refs[-1]
+    parts = refs[:-1]
+    rows = parts[0].shape[0]
+    for step, part_ref in enumerate(parts):
+        source = (place_ref[0] + len(parts) - step) % len(parts)
+        out_ref[pl.ds(pl.multiple_of(source * rows, rows), rows), :] = part_ref[...]
+
+
+def assemble(place, parts):
+    rows, columns = parts[0].shape
+    return pl.pallas_call(
+        assemble_kernel,
+        in_specs=[pl.BlockSpec(memory_space=pltpu.SMEM)]
+        + [pl.BlockSpec(memory_space=pltpu.VMEM)] * len(parts),
+        out_specs=pl.BlockSpec(memory_space=pltpu.VMEM),
+        out_shape=jax.ShapeDtypeStruct((rows * len(parts), columns), BF),
+        cost_estimate=cost(0, rows * columns * len(parts) * 4),
+        compiler_params=params(),
+        name="assemble",
+    )(place, *parts)
+
+
+def swapped(value, axis, mask):
+    count = lax.axis_size(axis)
+    return lax.ppermute(value, axis, [(source, source ^ mask) for source in range(count)])
+
+
+def weight_pieces(part):
+    count = lax.axis_size("blk")
+    if count & (count - 1) or part.shape[0] % HEAD_DIM or count > 8:
+        return [lax.all_gather(part, "blk", axis=0, tiled=True)]
+    pieces = {0: part}
+    for mask in range(2, count, 2):
+        pieces[mask] = swapped(part, "blk", mask)
+    for mask in range(0, count, 2):
+        pieces[mask + 1] = swapped(pieces[mask], "blk", 1)
+    return [pieces[mask] for mask in range(count)]
 
 
 def stats_kernel(x_ref, proj_ref, first_ref, second_ref):
@@ -199,11 +235,22 @@
     )(static, x, *parts)
 
 
-def qkv_kernel(rows_ref, weight_ref, cosine_ref, sine_ref, out_ref):
+def qkv_kernel(ring_ref, rows_ref, cosine_ref, sine_ref, *refs):
+    out_ref = refs[-1]
+    pieces = refs[:-1]
     servers, _, width = rows_ref.shape
-    total = contract(rows_ref[0], weight_ref[0:width, :], 1, 0)
-    for server in range(1, servers):
-        total += contract(rows_ref[server], weight_ref[server * width : (server + 1) * width, :], 1, 0)
+    depth = pieces[0].shape[0]
+    if len(pieces) == 1:
+        left = [rows_ref[server] for server in range(servers)]
+    else:
+        left = []
+        for piece in range(len(pieces)):
+            source = ring_ref[0] ^ piece
+            inside = pl.multiple_of((source % (width // depth)) * depth, depth)
+            left.append(rows_ref[source // (width // depth), :, pl.ds(inside, depth)])
+    left = jnp.concatenate(left, axis=1)
+    right = jnp.concatenate([piece[...] for piece in pieces], axis=0)
+    total = contract(left, right, 1, 0)
     slot = pl.program_id(0)
 
     @pl.when(slot < 2)
@@ -219,37 +266,34 @@
         out_ref[0] = total.astype(BF)
 
 
-def qkv_columns(rows, weight, cosine, sine, start):
+def qkv_columns(ring, rows, pieces, cosine, sine, start):
     servers, tokens, width = rows.shape
     table = pl.BlockSpec((tokens, HEAD_DIM), lambda j: (start // tokens, 0))
     return pl.pallas_call(
         qkv_kernel,
         grid=(3,),
         in_specs=[
+            pl.BlockSpec(memory_space=pltpu.SMEM),
             pl.BlockSpec((servers, tokens, width), lambda j: (0, 0, 0)),
-            pl.BlockSpec((D, width), lambda j: (0, j)),
             table,
             table,
-        ],
+        ]
+        + [pl.BlockSpec((pieces[0].shape[0], width), lambda j: (0, j))] * len(pieces),
         out_specs=pl.BlockSpec((1, tokens, width), lambda j: (j, 0, 0)),
         out_shape=jax.ShapeDtypeStruct((3, tokens, width), BF),
         cost_estimate=cost(2 * tokens * D * 3 * width, D * 6 * width + tokens * D * 5),
         compiler_params=params(),
         name="qkv",
-    )(rows, weight, cosine, sine)
-
-
-def attend_kernel(
-    place_ref, q_ref, k0, k1, k2, v0, v1, v2, qseg_ref, kseg_ref, out_ref, sent_ref, own_ref
-):
+    )(ring, rows, cosine, sine, *pieces)
+
+
+def attend_kernel(q_ref, k0, k1, k2, v0, v1, v2, qseg_ref, kseg_ref, attended_ref):
     tokens, width = q_ref.shape[1:]
     window = kseg_ref.shape[-1]
-    place = place_ref[0]
     row, col = iotas(tokens, window)
     allowed = (qseg_ref[...] == kseg_ref[0]) & (col - (window - tokens) <= row)
     bias = jnp.where(allowed, 0.0, -1e30)
     factor = 1.4426950408889634 / HEAD_DIM**0.5
-    heads = []
     for head in range(width // HEAD_DIM):
         lanes = slice(head * HEAD_DIM, (head + 1) * HEAD_DIM)
         query = q_ref[0, :, lanes]
@@ -260,21 +304,12 @@
         weights = jnp.exp2((scores - jnp.max(scores, axis=1, keepdims=True)) * factor)
         total = jnp.sum(weights, axis=1, keepdims=True)
         values = jnp.concatenate([v[0, :, lanes] for v in (v0, v1, v2)], axis=0)
-        heads.append((contract(weights.astype(BF), values, 1, 0) / total).astype(BF))
-    attended = jnp.concatenate(heads, axis=1)
-    for server in range(sent_ref.shape[0]):
-        part = contract(attended, out_ref[server * width : (server + 1) * width, :], 1, 1)
-        sent_ref[server] = jnp.where(place == server, 0.0, part).astype(BF)
-
-        @pl.when(place == server)
-        def _():
-            own_ref[...] = part
-
-
-def attend(place, query, window, qseg, kseg, weight, chunk):
+        attended_ref[:, lanes] = (contract(weights.astype(BF), values, 1, 0) / total).astype(BF)
+
+
+def attend(query, window, qseg, kseg, chunk):
     source, at = query
     width = source.shape[-1]
-    servers = D // width
     block = (1, CHUNK, width)
     keys = [pl.BlockSpec(block, lambda i, s=slot, r=where: (s, r, 0)) for _, slot, where in window]
     values = [
@@ -285,34 +320,72 @@
     return pl.pallas_call(
         attend_kernel,
         grid=(1,),
-        in_specs=[pl.BlockSpec(memory_space=pltpu.SMEM), pl.BlockSpec(block, lambda i: (0, at, 0))]
+        in_specs=[pl.BlockSpec(block, lambda i: (0, at, 0))]
         + keys
         + values
         + [
             pl.BlockSpec((CHUNK, 1), lambda i: (chunk, 0)),
             pl.BlockSpec((1, 1, reach), lambda i: (chunk, 0, 0)),
-            pl.BlockSpec((D, width), lambda i: (0, 0)),
         ],
-        out_specs=[
-            pl.BlockSpec((servers, CHUNK, width), lambda i: (0, 0, 0)),
-            pl.BlockSpec((CHUNK, width), lambda i: (0, 0)),
+        out_specs=pl.BlockSpec((CHUNK, width), lambda i: (0, 0)),
+        out_shape=jax.ShapeDtypeStruct((CHUNK, width), BF),
+        cost_estimate=cost(4 * CHUNK * reach * width, CHUNK * width * 16, CHUNK * reach * 4),
+        compiler_params=params(),
+        name="attend",
+    )(source, *arrays, *arrays, qseg, kseg)
+
+
+def project_kernel(place_ref, ring_ref, own_ref, other_ref, *refs):
+    pieces = refs[:-4]
+    kept_ref, inner_ref, outer_ref, sums = refs[-4:]
+    servers, _, width = sums.shape
+    place = place_ref[0]
+    even = place % 2 == 0
+    own, other = own_ref[...], other_ref[...]
+    both = jnp.concatenate([jnp.where(even, own, other), jnp.where(even, other, own)], axis=1)
+    depth = pieces[0].shape[0]
+    if len(pieces) == 1:
+        for server in range(servers):
+            rows = pieces[0][server * width : (server + 1) * width, :]
+            sums[server] = contract(both, rows, 1, 1)
+    else:
+        for piece in range(len(pieces)):
+            target = ring_ref[0] ^ piece
+            inside = pl.multiple_of((target % (width // depth)) * depth, depth)
+            sums[target // (width // depth), :, pl.ds(inside, depth)] = contract(
+                both, pieces[piece][...], 1, 1
+            )
+    kept_ref[...] = sums[place]
+    low = place < 2
+    inner_ref[...] = sums[jnp.where(low, 2, 1)].astype(BF)
+    outer_ref[...] = sums[jnp.where(low, 3, 0)].astype(BF)
+
+
+def project(place, ring, own, other, pieces, servers):
+    tokens, width = own.shape
+    rows, columns = pieces[0].shape
+    pair = 2 * width
+    tail = pl.BlockSpec((pl.Element(rows), pl.Element(pair)), lambda i: (0, columns - pair))
+    full = pl.BlockSpec((tokens, width), lambda i: (0, 0))
+    return pl.pallas_call(
+        project_kernel,
+        grid=(1,),
+        in_specs=[pl.BlockSpec(memory_space=pltpu.SMEM)] * 2 + [full] * 2 + [tail] * len(pieces),
+        out_specs=[full] * 3,
+        out_shape=[
+            jax.ShapeDtypeStruct((tokens, width), F32),
+            jax.ShapeDtypeStruct((tokens, width), BF),
+            jax.ShapeDtypeStruct((tokens, width), BF),
         ],
-        out_shape=[
-            jax.ShapeDtypeStruct((servers, CHUNK, width), BF),
-            jax.ShapeDtypeStruct((CHUNK, width), F32),
-        ],
-        cost_estimate=cost(
-            4 * CHUNK * reach * width + 2 * CHUNK * D * width,
-            D * width * 2 + CHUNK * width * 24,
-            CHUNK * reach * 4,
-        ),
-        compiler_params=params(),
-        name="attend",
-    )(place, source, *arrays, *arrays, qseg, kseg, weight)
+        scratch_shapes=[pltpu.VMEM((servers, tokens, width), F32)],
+        cost_estimate=cost(2 * tokens * D * pair, D * pair * 2 + tokens * width * 12),
+        compiler_params=params(),
+        name="project",
+    )(place, ring, own, other, *pieces)
 
 
 def final_kernel(
-    static_ref, x_ref, first_ref, own2_ref, a_ref, b_ref, c_ref, other_ref, own_ref, *rest
+    static_ref, x_ref, first_ref, own2_ref, a_ref, b_ref, c_ref, own_ref, inner_ref, outer_ref, *rest
 ):
     new_ref = rest[-1]
     tokens, _, width = x_ref.shape
@@ -339,7 +412,8 @@
         matrix = jnp.where(same, jnp.tile(residual[:, lanes], (SUB // 2, 1)), 0.0)
         high, low = split(matrix, 2)
         new = contract(high, v, 1, 0) + contract(low, v, 1, 0)
-        update = other_ref[rows, :].astype(F32) + own_ref[rows, :]
+        sent = inner_ref[rows, :].astype(F32) + outer_ref[rows, :].astype(F32)
+        update = own_ref[rows, :] + sent
         update_high, update_low = split(update, 2)
         spread_high, spread_low = split(jnp.where(mine, columns[4][:, lanes], 0.0), 2)
         new += contract(
@@ -351,8 +425,8 @@
         new_ref[rows] = new.astype(BF).reshape(SUB, 4, width)
 
 
-def final(static, x, first, first_at, second, second_at, others, own, start, previous, step=128):
-    tokens, width = own.shape
+def final(static, x, first, first_at, second, second_at, updates, start, previous, step=128):
+    tokens, width = updates[0].shape
     lane_block = pl.BlockSpec((8, 4 * step), lambda i: (0, second_at // step + i))
     stream_block = pl.BlockSpec((step, 4, width), lambda i: (start // step + i, 0, 0))
     specs = [
@@ -361,8 +435,8 @@
         pl.BlockSpec((8, 4 * step), lambda i: (0, first_at // step + i)),
     ]
     specs += [lane_block] * 4
-    specs += [pl.BlockSpec((step, width), lambda i: (i, 0))] * 2
-    args = [static, x, first, *second, others, own]
+    specs += [pl.BlockSpec((step, width), lambda i: (i, 0))] * 3
+    args = [static, x, first, *second, *updates]
     aliases = {}
     if previous is not None:
         specs.append(pl.BlockSpec(memory_space=pl.ANY))
@@ -385,22 +459,22 @@
     tokens_local, _, width = streams.shape
     group_size = lax.axis_size("mp")
     place = lax.axis_index("mp").astype(jnp.int32).reshape(1)
+    ring = lax.axis_index("blk").astype(jnp.int32).reshape(1)
 
     proj_rows = jnp.concatenate(
         [hc_proj.T, jnp.ones((1, width), F32), jnp.zeros((1, width), F32)], axis=0
     )
     first_late, second_late = stats(streams, proj_rows, BLOCK, BLOCK)
     late = [first_late] + from_others(first_late, "mp")
-    qkv_part, out_part = regroup(proj_master, group_size)
+    parts = list(regroup(place, proj_master, group_size))
     first_early, second_early = stats(streams, proj_rows, 0, BLOCK)
     early = [first_early] + from_others(first_early, "mp")
 
-    def served(part):
-        exchanged = lax.all_to_all(part, "mp", split_axis=0, concat_axis=0, tiled=True)
-        return lax.all_gather(exchanged.reshape(-1, part.shape[-1]), "blk", axis=0, tiled=True)
-
-    qkv_weight = served(qkv_part)
-    out_weight = served(out_part)
+    for step in range(1, group_size):
+        parts[step] = lax.ppermute(
+            parts[step], "mp", [(at, (at + step) % group_size) for at in range(group_size)]
+        )
+    pieces = weight_pieces(assemble(place, parts))
 
     def gathered(normed):
         rows = lax.all_gather(normed, "mp", axis=0, tiled=True)
@@ -408,10 +482,8 @@
 
     sums_late, normed_late = mix(hc_static, streams, late, BLOCK, BLOCK, 0)
     rows_late = gathered(normed_late)
-    sums_0, normed_0 = mix(hc_static, streams, early, 0, CHUNK, 0)
-    rows_0 = gathered(normed_0)
-    sums_1, normed_1 = mix(hc_static, streams, early, CHUNK, CHUNK, CHUNK)
-    rows_1 = gathered(normed_1)
+    sums_early, normed_early = mix(hc_static, streams, early, 0, BLOCK, 0)
+    rows_early = gathered(normed_early)
     second_late = [second_late] + from_others(second_late, "mp")
     second_early = [second_early] + from_others(second_early, "mp")
 
@@ -438,43 +510,34 @@
     key_segments = jnp.stack(windows)[:, None, :]
     query_segments = segment_ids[:, None]
 
-    qkv_late = qkv_columns(rows_late, qkv_weight, cosine, sine, BLOCK)
+    qkv_late = qkv_columns(ring, rows_late, pieces, cosine, sine, BLOCK)
     halo_rows = passed_along(qkv_late[1:3], "blk", 1)
-    qkv_0 = qkv_columns(rows_0, qkv_weight, cosine, sine, 0)
-    qkv_1 = qkv_columns(rows_1, qkv_weight, cosine, sine, CHUNK)
-
-    chunks = [(halo_rows, 0, 0), (halo_rows, 0, 1), (qkv_0, 1, 0), (qkv_1, 1, 0)]
+    qkv_early = qkv_columns(ring, rows_early, pieces, cosine, sine, 0)
+
+    chunks = [(halo_rows, 0, 0), (halo_rows, 0, 1), (qkv_early, 1, 0), (qkv_early, 1, 1)]
     chunks += [(qkv_late, 1, 0), (qkv_late, 1, 1)]
     order = [
-        (0, (sums_0, 0), (second_early, 0)),
-        (1, (sums_1, 0), (second_early, CHUNK)),
-        (2, (sums_late, 0), (second_late, 0)),
-        (3, (sums_late, CHUNK), (second_late, CHUNK)),
+        (2, sums_late, second_late, 0),
+        (3, sums_late, second_late, CHUNK),
+        (0, sums_early, second_early, 0),
+        (1, sums_early, second_early, CHUNK),
     ]
     result = None
-    for chunk, (first, first_at), (second, second_at) in order:
+    for chunk, first, second, lanes_at in order:
         source, _, at = chunks[chunk + 2]
-        sent, own = attend(
-            place,
-            (source, at),
-            chunks[chunk : chunk + 3],
-            query_segments,
-            key_segments,
-            out_weight,
-            chunk,
-        )
-        others = lax.psum_scatter(
-            sent.reshape(group_size * CHUNK, width), "mp", scatter_dimension=0, tiled=True
-        )
+        window = chunks[chunk : chunk + 3]
+        own = attend((source, at), window, query_segments, key_segments, chunk)
+        kept, inner, outer = project(place, ring, own, swapped(own, "mp", 1), pieces, group_size)
+        inner = lax.ppermute(inner, "mp", [(1, 2), (2, 1)])
+        outer = lax.ppermute(outer, "mp", [(1, 3), (2, 0)])
         result = final(
             hc_static,
             streams,
             first,
-            first_at,
+            lanes_at,
             second,
-            second_at,
-            others,
-            own,
+            lanes_at,
+            [kept, inner, outer],
             chunk * CHUNK,
             result,
         )

time: 359 us -> 280 us (0.78)
  waiting for transfers between devices: 150 us -> 82.2 us
  blocking collectives: 59.2 us -> 0 us
  starting transfers between devices: 23.3 us -> 75 us
  local copies, waits for them, and re-layouts: 54.9 us -> 10.1 us
  Pallas kernels: 48.6 us -> 88.9 us
    reduce_scatter x4 -> x0, waiting for transfers between devices: 62.1 us -> none  [body(): lax.psum_scatter(sent.reshape(group_size * CHUNK, width), 'mp', scatter_d...]
    all_to_all x2 -> x0, blocking collectives: 59.2 us -> none  [served(): lax.all_to_all(part, 'mp', split_axis=0, concat_axis=0, tiled=True)]
    ppermute x0 -> x22, waiting for transfers between devices: none -> 56.7 us  [the longest x3 37.2 us: body(): lax.ppermute(parts[step], 'mp', [(at, (at + step) % group_size) for at in...]
    unnamed x110 -> x72, local copies, waits for them, and re-layouts: 52.1 us -> 6.34 us
    all_gather x2 -> x0, waiting for transfers between devices: 41 us -> none  [served(): lax.all_gather(exchanged.reshape(-1, part.shape[-1]), 'blk', axis=0, tile...]
    pallas_call x8 -> x12, Pallas kernels: 27.6 us -> 58.3 us  [the longest x4 18.6 us: project(): pl.pallas_call(project_kernel, grid=(1,), in_specs=[pl.BlockSpec(memory_s...]
    ppermute x0 -> x22, starting transfers between devices: none -> 28 us  [the longest x11 15.6 us: swapped(): lax.ppermute(value, axis, [(source, source ^ mask) for source in range(co...]
    all_gather x3 -> x2, waiting for transfers between devices: 36.4 us -> 11.4 us  [gathered(): rows = lax.all_gather(normed, 'mp', axis=0, tiled=True)]
  transfers between devices with their start and end apart: 23 -> 38, of which waited for: 14 -> 13; matrix products, arithmetic and copies ran while one was open for 2% -> 3% of each run, Pallas kernels for 12% -> 28%
where the time goes in v2:
time: 280 us; the launch traced here: 278 us
  Pallas kernels  88.9 us (32%)
  waiting for transfers between devices  82.2 us (29%)
  starting transfers between devices  75 us (27%)
  between operations  15.1 us (5%)
  local copies, waits for them, and re-layouts  10.1 us (4%)
  other arithmetic  6.31 us (2%)
    ppermute x12, starting transfers between devices, from_others(): lax.ppermute(value, axis, [(source, (source + step) % count) for source i...  43.5 us
    ppermute x3, waiting for transfers between devices, body(): lax.ppermute(parts[step], 'mp', [(at, (at + step) % group_size) for at in...  37.2 us
    pallas_call x4, Pallas kernels, project(): pl.pallas_call(project_kernel, grid=(1,), in_specs=[pl.BlockSpec(memory_s...  18.6 us
    pallas_call x4, Pallas kernels, attend(): pl.pallas_call(attend_kernel, grid=(1,), in_specs=[pl.BlockSpec(block, la...  16.2 us
    pallas_call x2, Pallas kernels, qkv_columns(): pl.pallas_call(qkv_kernel, grid=(3,), in_specs=[pl.BlockSpec(memory_space...  16.1 us
    ppermute x11, starting transfers between devices, swapped(): lax.ppermute(value, axis, [(source, source ^ mask) for source in range(co...  15.6 us
    ppermute x12, waiting for transfers between devices, from_others(): lax.ppermute(value, axis, [(source, (source + step) % count) for source i...  14 us
    pallas_call x4, Pallas kernels, final(): pl.pallas_call(final_kernel, grid=(tokens // step,), in_specs=specs, out_...  13.7 us
  transfers between devices with their start and end apart: 38, of which 13 were waited for; matrix products, arithmetic and copies ran while one was open for 3% of the time, Pallas kernels for 28%

profile of v2, /device:TPU:0, one launch (start us, length us, event | category | flops | bytes accessed | tf_op | source)
XLA Modules:
  0.0 277.5 jit_solution(7783494742990947843)
XLA Ops:
  6.7 1.4 maximum_maximum_fusion.proj_ref
  8.1 4.3 %stats.3 = (f32[8,2048]{1,0:T(8,128)}, f32[8,2048]{1,0:T(8,128)}) custom-call(bf16[1024,4,512]{2,1,0:T(4,128)(2,1)} %x_ref.15, f32[8,512]{1,0:T(8,128)} %maximum_maximum_fusion.proj_ref), custom_call_target="tpu_custom_call" | custom-call | flops 629145600 | bytes 2097152 | tf_op jit(solution)/shard_map/stats/pallas_call | solution.py:157
  12.4 5.0 %collective-permute-start.19 = (f32[8,2048]{1,0:T(8,128)}, f32[8,2048]{1,0:T(8,128)S(1)}, u32[]{:S(2)}, u32[]{:S(2)}) collective-permute-start(f32[8,2048]{1,0:T(8,128)} %get-tuple-element.37.own_ref), channel_id=1, source_target_pairs={{0,3},{1,0},{2,1},{3,2},{4,7},{5,4},{6,5},{7,6},{8,11},{9,8},{10,9... | collective-permute-start | bytes 196616 | tf_op jit(solution)/shard_map/ppermute | solution.py:30
  17.5 1.0 collective-permute-start.17
  18.5 1.8 collective-permute-done.19.c_ref
  20.3 3.9 %collective-permute-done.18.b_ref = f32[8,2048]{1,0:T(8,128)S(1)} collective-permute-done((f32[8,2048]{1,0:T(8,128)}, f32[8,2048]{1,0:T(8,128)S(1)}, u32[]{:S(2)}, u32[]{:S(2)}) %collective-permute-start.18) | collective-permute-done | bytes 65568 | tf_op jit(solution)/shard_map/ppermute | solution.py:30
  25.4 4.1 %mix.3 = (f32[8,2048]{1,0:T(8,128)}, bf16[512,512]{1,0:T(8,128)(2,1)}) custom-call(f32[4,6]{1,0:T(4,128)} %static_ref.11, bf16[1024,4,512]{2,1,0:T(4,128)(2,1)} %x_ref.15, f32[8,2048]{1,0:T(8,128)} %get-tuple-element.37.own_ref, f32[8,2048]{1,0:T(8,128)} %copy-done.30, f32[8,2048]{1,0:T(8,128)} %copy-done.28, f32[8,2048]{1,0:T(8,128)} %copy-done.26), custom_call_target="tpu_custom_call" | custom-call | flops 419430400 | bytes 2621440 | tf_op jit(solution)/shard_map/mix/pallas_call | solution.py:216
  29.6 4.9 %regroup.1 = (bf16[64,2560]{1,0:T(8,128)(2,1)}, bf16[64,2560]{1,0:T(8,128)(2,1)}, bf16[64,2560]{1,0:T(8,128)(2,1)}, bf16[64,2560]{1,0:T(8,128)(2,1)}) custom-call(s32[1]{0:T(128)} %bitcast.1.place_ref, f32[64,4,2048]{2,1,0:T(4,128)} %master_ref.1), custom_call_target="tpu_custom_call" | custom-call | bytes 3407872 | tf_op jit(solution)/shard_map/regroup/pallas_call | solution.py:78
  34.5 2.5 collective-permute-start.8
  36.9 1.6 collective-permute-start.9
  38.6 14.0 %collective-permute-done.7.refs_1_ = bf16[64,2560]{1,0:T(8,128)(2,1)S(1)} collective-permute-done((bf16[64,2560]{1,0:T(8,128)(2,1)}, bf16[64,2560]{1,0:T(8,128)(2,1)S(1)}, u32[]{:S(2)}, u32[]{:S(2)}) %collective-permute-start.7) | collective-permute-done | bytes 327712 | tf_op jit(solution)/shard_map/ppermute | solution.py:474
  52.6 23.2 %collective-permute-done.8.refs_2_ = bf16[64,2560]{1,0:T(8,128)(2,1)S(1)} collective-permute-done((bf16[64,2560]{1,0:T(8,128)(2,1)}, bf16[64,2560]{1,0:T(8,128)(2,1)S(1)}, u32[]{:S(2)}, u32[]{:S(2)}) %collective-permute-start.8) | collective-permute-done | bytes 327712 | tf_op jit(solution)/shard_map/ppermute | solution.py:474
  75.8 0.7 copy-done.4
  76.6 2.5 assemble.1.refs_0_
  79.1 2.6 collective-permute-start.15
  82.6 4.3 %stats.2 = (f32[8,2048]{1,0:T(8,128)}, f32[8,2048]{1,0:T(8,128)}) custom-call(bf16[1024,4,512]{2,1,0:T(4,128)(2,1)} %x_ref.15, f32[8,512]{1,0:T(8,128)} %maximum_maximum_fusion.proj_ref), custom_call_target="tpu_custom_call" | custom-call | flops 629145600 | bytes 2097152 | tf_op jit(solution)/shard_map/stats/pallas_call | solution.py:157
  86.9 20.3 %collective-permute-start.2 = (f32[8,2048]{1,0:T(8,128)}, f32[8,2048]{1,0:T(8,128)S(1)}, u32[]{:S(2)}, u32[]{:S(2)}) collective-permute-start(f32[8,2048]{1,0:T(8,128)} %get-tuple-element.29.own_ref), channel_id=1, source_target_pairs={{0,3},{1,0},{2,1},{3,2},{4,7},{5,4},{6,5},{7,6},{8,11},{9,8},{10,9... | collective-permute-start | bytes 196616 | tf_op jit(solution)/shard_map/ppermute | solution.py:30
  107.2 2.9 %collective-permute-start.1 = (f32[8,2048]{1,0:T(8,128)}, f32[8,2048]{1,0:T(8,128)S(1)}, u32[]{:S(2)}, u32[]{:S(2)}) collective-permute-start(f32[8,2048]{1,0:T(8,128)} %get-tuple-element.29.own_ref), channel_id=1, source_target_pairs={{0,2},{1,3},{2,0},{3,1},{4,6},{5,7},{6,4},{7,5},{8,10},{9,11},{10,... | collective-permute-start | bytes 196616 | tf_op jit(solution)/shard_map/ppermute | solution.py:30
  110.1 1.4 collective-permute-done.2.c_ref
  111.5 1.6 collective-permute-start
  113.1 0.8 collective-permute-done.1.b_ref
  114.0 3.8 %collective-permute-done.a_ref = f32[8,2048]{1,0:T(8,128)S(1)} collective-permute-done((f32[8,2048]{1,0:T(8,128)}, f32[8,2048]{1,0:T(8,128)S(1)}, u32[]{:S(2)}, u32[]{:S(2)}) %collective-permute-start) | collective-permute-done | bytes 65568 | tf_op jit(solution)/shard_map/ppermute | solution.py:30
  118.4 4.1 %mix.2 = (f32[8,2048]{1,0:T(8,128)}, bf16[512,512]{1,0:T(8,128)(2,1)}) custom-call(f32[4,6]{1,0:T(4,128)} %static_ref.11, bf16[1024,4,512]{2,1,0:T(4,128)(2,1)} %x_ref.15, f32[8,2048]{1,0:T(8,128)} %get-tuple-element.29.own_ref, f32[8,2048]{1,0:T(8,128)} %copy-done.31, f32[8,2048]{1,0:T(8,128)} %copy-done.29, f32[8,2048]{1,0:T(8,128)} %copy-done.27), custom_call_target="tpu_custom_call" | custom-call | flops 419430400 | bytes 2621440 | tf_op jit(solution)/shard_map/mix/pallas_call | solution.py:216
  123.8 1.3 collective-permute-start.6
  125.1 2.3 collective-permute-start.10
  127.5 8.6 %collective-permute-done.13.refs_4_ = bf16[256,2560]{1,0:T(8,128)(2,1)} collective-permute-done((bf16[256,2560]{1,0:T(8,128)(2,1)}, bf16[256,2560]{1,0:T(8,128)(2,1)}, u32[]{:S(2)}, u32[]{:S(2)}) %collective-permute-start.13) | collective-permute-done | bytes 1310752 | tf_op jit(solution)/shard_map/ppermute | solution.py:114
  137.2 1.6 convert_reduce_fusion
  138.8 1.9 fusion.1
  140.7 1.4 pad_maximum_fusion
  142.1 8.1 %qkv.3.q_ref.k1.k2.v1.v2 = bf16[3,512,512]{2,1,0:T(8,128)(2,1)} custom-call(s32[1]{0:T(128)} %bitcast.2.ring_ref, bf16[4,512,512]{2,1,0:T(8,128)(2,1)} %bitcast.10, f32[1024,128]{1,0:T(8,128)} %get-tuple-element.67.cosine_ref, f32[1024,128]{1,0:T(8,128)} %get-tuple-element.68.sine_ref, bf16[256,2560]{1,0:T(8,128)(2,1)} %assemble.1.refs_0_, ...), custom_call_target="tpu_custom_call" | custom-call | flops 3221225472 | bytes 11534336 | tf_op jit(solution)/shard_map/qkv/pallas_call | solution.py:272
  150.2 1.3 slice.38
  151.5 2.2 collective-permute-start.20
  153.8 1.0 copy.14.qseg_ref
  155.4 11.4 %all-gather.3.cloned.1.call-done = bf16[2048,512]{1,0:T(8,128)(2,1)} async-done(((bf16[512,512]{1,0:T(8,128)(2,1)}), bf16[2048,512]{1,0:T(8,128)(2,1)}) %all-gather.3.cloned.1.call-update) | async-done | bytes 2097168 | tf_op jit(solution)/shard_map/all_gather | solution.py:480
  166.8 8.1 %qkv.2.q_ref.k1.k2.v1.v2.k0.v0 = bf16[3,512,512]{2,1,0:T(8,128)(2,1)} custom-call(s32[1]{0:T(128)} %bitcast.2.ring_ref, bf16[4,512,512]{2,1,0:T(8,128)(2,1)} %bitcast.11, f32[1024,128]{1,0:T(8,128)} %get-tuple-element.67.cosine_ref, f32[1024,128]{1,0:T(8,128)} %get-tuple-element.68.sine_ref, bf16[256,2560]{1,0:T(8,128)(2,1)} %assemble.1.refs_0_, ...), custom_call_target="tpu_custom_call" | custom-call | flops 3221225472 | bytes 11534336 | tf_op jit(solution)/shard_map/qkv/pallas_call | solution.py:272
  174.9 4.0 %attend.7.own_ref = bf16[256,512]{1,0:T(8,128)(2,1)} custom-call(bf16[3,512,512]{2,1,0:T(8,128)(2,1)} %qkv.3.q_ref.k1.k2.v1.v2, bf16[3,512,512]{2,1,0:T(8,128)(2,1)} %qkv.2.q_ref.k1.k2.v1.v2.k0.v0, bf16[3,512,512]{2,1,0:T(8,128)(2,1)} %qkv.2.q_ref.k1.k2.v1.v2.k0.v0, bf16[3,512,512]{2,1,0:T(8,128)(2,1)} %qkv.3.q_ref.k1.k2.v1.v2, ...), custom_call_target="tpu_custom_call" | custom-call | flops 402653184 | bytes 2097152 | tf_op jit(solution)/shard_map/attend/pallas_call | solution.py:320
  178.9 9.0 %collective-permute-start.33 = (bf16[256,512]{1,0:T(8,128)(2,1)}, bf16[256,512]{1,0:T(8,128)(2,1)S(1)}, u32[]{:S(2)}, u32[]{:S(2)}) collective-permute-start(bf16[256,512]{1,0:T(8,128)(2,1)} %attend.7.own_ref), channel_id=1, source_target_pairs={{0,1},{1,0},{2,3},{3,2},{4,5},{5,4},{6,7},{7,6},{8,9},{9,8},{10,11... | collective-permute-start | bytes 786440 | tf_op jit(solution)/shard_map/ppermute | solution.py:114
  188.0 4.0 %attend.6.own_ref = bf16[256,512]{1,0:T(8,128)(2,1)} custom-call(bf16[3,512,512]{2,1,0:T(8,128)(2,1)} %qkv.3.q_ref.k1.k2.v1.v2, bf16[3,512,512]{2,1,0:T(8,128)(2,1)} %qkv.2.q_ref.k1.k2.v1.v2.k0.v0, bf16[3,512,512]{2,1,0:T(8,128)(2,1)} %qkv.3.q_ref.k1.k2.v1.v2, bf16[3,512,512]{2,1,0:T(8,128)(2,1)} %qkv.3.q_ref.k1.k2.v1.v2, ...), custom_call_target="tpu_custom_call" | custom-call | flops 402653184 | bytes 2097152 | tf_op jit(solution)/shard_map/attend/pallas_call | solution.py:320
  192.5 3.0 %collective-permute-start.28 = (f32[8,2048]{1,0:T(8,128)S(1)}, f32[8,2048]{1,0:T(8,128)S(1)}, u32[]{:S(2)}, u32[]{:S(2)}) collective-permute-start(f32[8,2048]{1,0:T(8,128)S(1)} %copy-done.6), channel_id=1, source_target_pairs={{0,2},{1,3},{2,0},{3,1},{4,6},{5,7},{6,4},{7,5},{8,10},{9,11},{10,... | collective-permute-start | bytes 196616 | tf_op jit(solution)/shard_map/ppermute | solution.py:30
  195.5 0.9 copy-done.2
  196.4 4.0 %attend.5.own_ref = bf16[256,512]{1,0:T(8,128)(2,1)} custom-call(bf16[3,512,512]{2,1,0:T(8,128)(2,1)} %qkv.2.q_ref.k1.k2.v1.v2.k0.v0, bf16[2,512,512]{2,1,0:T(8,128)(2,1)} %copy-done.2, bf16[2,512,512]{2,1,0:T(8,128)(2,1)} %copy-done.2, bf16[3,512,512]{2,1,0:T(8,128)(2,1)} %qkv.2.q_ref.k1.k2.v1.v2.k0.v0, bf16[2,512,512]{2,1,0:T(8,128)(2,1)} %copy-done.2, ...), custom_call_target="tpu_custom_call" | custom-call | flops 402653184 | bytes 2097152 | tf_op jit(solution)/shard_map/attend/pallas_call | solution.py:320
  201.2 4.6 %project.7 = (f32[256,512]{1,0:T(8,128)}, bf16[256,512]{1,0:T(8,128)(2,1)}, bf16[256,512]{1,0:T(8,128)(2,1)}) custom-call(s32[1]{0:T(128)} %bitcast.1.place_ref, s32[1]{0:T(128)} %bitcast.2.ring_ref, bf16[256,512]{1,0:T(8,128)(2,1)} %attend.7.own_ref, bf16[256,512]{1,0:T(8,128)(2,1)} %copy-done.25, bf16[256,2560]{1,0:T(8,128)(2,1)} %assemble.1.refs_0_, ...), custom_call_target="tpu_custom_call" | custom-call | flops 1073741824 | bytes 5767168 | tf_op jit(solution)/shard_map/project/pallas_call | solution.py:370
  205.8 4.1 %attend.4.own_ref = bf16[256,512]{1,0:T(8,128)(2,1)} custom-call(bf16[3,512,512]{2,1,0:T(8,128)(2,1)} %qkv.2.q_ref.k1.k2.v1.v2.k0.v0, bf16[2,512,512]{2,1,0:T(8,128)(2,1)} %copy-done.2, bf16[3,512,512]{2,1,0:T(8,128)(2,1)} %qkv.2.q_ref.k1.k2.v1.v2.k0.v0, bf16[3,512,512]{2,1,0:T(8,128)(2,1)} %qkv.2.q_ref.k1.k2.v1.v2.k0.v0, bf16[2,512,512]{2,1,0:T(8,128)(2,1)} %copy-done.2, ...), custom_call_target="tpu_custom_call" | custom-call | flops 402653184 | bytes 2097152 | tf_op jit(solution)/shard_map/attend/pallas_call | solution.py:320
  209.9 2.9 %collective-permute-start.5 = (f32[8,2048]{1,0:T(8,128)S(1)}, f32[8,2048]{1,0:T(8,128)S(1)}, u32[]{:S(2)}, u32[]{:S(2)}) collective-permute-start(f32[8,2048]{1,0:T(8,128)S(1)} %copy-done.7), channel_id=1, source_target_pairs={{0,3},{1,0},{2,1},{3,2},{4,7},{5,4},{6,5},{7,6},{8,11},{9,8},{10,9... | collective-permute-start | bytes 196616 | tf_op jit(solution)/shard_map/ppermute | solution.py:30
  212.9 0.8 collective-permute-start.34
  213.7 1.9 collective-permute-start.4
  216.3 4.7 %project.6 = (f32[256,512]{1,0:T(8,128)}, bf16[256,512]{1,0:T(8,128)(2,1)}, bf16[256,512]{1,0:T(8,128)(2,1)}) custom-call(s32[1]{0:T(128)} %bitcast.1.place_ref, s32[1]{0:T(128)} %bitcast.2.ring_ref, bf16[256,512]{1,0:T(8,128)(2,1)} %attend.6.own_ref, bf16[256,512]{1,0:T(8,128)(2,1)} %copy-done.21, bf16[256,2560]{1,0:T(8,128)(2,1)} %assemble.1.refs_0_, ...), custom_call_target="tpu_custom_call" | custom-call | flops 1073741824 | bytes 5767168 | tf_op jit(solution)/shard_map/project/pallas_call | solution.py:370
  221.0 1.3 collective-permute-start.35
  222.3 2.3 collective-permute-done.4.b_ref
  225.3 1.5 collective-permute-start.32
  226.8 4.6 %project.5 = (f32[256,512]{1,0:T(8,128)}, bf16[256,512]{1,0:T(8,128)(2,1)}, bf16[256,512]{1,0:T(8,128)(2,1)}) custom-call(s32[1]{0:T(128)} %bitcast.1.place_ref, s32[1]{0:T(128)} %bitcast.2.ring_ref, bf16[256,512]{1,0:T(8,128)(2,1)} %attend.5.own_ref, bf16[256,512]{1,0:T(8,128)(2,1)} %copy-done.20, bf16[256,2560]{1,0:T(8,128)(2,1)} %assemble.1.refs_0_, ...), custom_call_target="tpu_custom_call" | custom-call | flops 1073741824 | bytes 5767168 | tf_op jit(solution)/shard_map/project/pallas_call | solution.py:370
  232.2 1.3 collective-permute-start.26
  233.5 4.7 %project.4 = (f32[256,512]{1,0:T(8,128)}, bf16[256,512]{1,0:T(8,128)(2,1)}, bf16[256,512]{1,0:T(8,128)(2,1)}) custom-call(s32[1]{0:T(128)} %bitcast.1.place_ref, s32[1]{0:T(128)} %bitcast.2.ring_ref, bf16[256,512]{1,0:T(8,128)(2,1)} %attend.4.own_ref, bf16[256,512]{1,0:T(8,128)(2,1)} %copy-done.23, bf16[256,2560]{1,0:T(8,128)(2,1)} %assemble.1.refs_0_, ...), custom_call_target="tpu_custom_call" | custom-call | flops 1073741824 | bytes 5767168 | tf_op jit(solution)/shard_map/project/pallas_call | solution.py:370
  238.9 1.3 collective-permute-start.23
  240.2 4.0 %collective-permute-done.32.outer_ref = bf16[256,512]{1,0:T(8,128)(2,1)S(1)} collective-permute-done((bf16[256,512]{1,0:T(8,128)(2,1)}, bf16[256,512]{1,0:T(8,128)(2,1)S(1)}, u32[]{:S(2)}, u32[]{:S(2)}) %collective-permute-start.32) | collective-permute-done | bytes 262176 | tf_op jit(solution)/shard_map/ppermute | solution.py:532
  244.3 4.3 %collective-permute-start.3 = (f32[8,2048]{1,0:T(8,128)S(1)}, f32[8,2048]{1,0:T(8,128)S(1)}, u32[]{:S(2)}, u32[]{:S(2)}) collective-permute-start(f32[8,2048]{1,0:T(8,128)S(1)} %copy-done.7), channel_id=1, source_target_pairs={{0,1},{1,2},{2,3},{3,0},{4,5},{5,6},{6,7},{7,4},{8,9},{9,10},{10,1... | collective-permute-start | bytes 196616 | tf_op jit(solution)/shard_map/ppermute | solution.py:30
  248.6 3.4 %final.4.rest_0_ = bf16[1024,4,512]{2,1,0:T(4,128)(2,1)} custom-call(f32[4,6]{1,0:T(4,128)} %static_ref.11, bf16[1024,4,512]{2,1,0:T(4,128)(2,1)} %x_ref.15, f32[8,2048]{1,0:T(8,128)} %get-tuple-element.45.first_ref, f32[8,2048]{1,0:T(8,128)} %get-tuple-element.46.own2_ref, f32[8,2048]{1,0:T(8,128)} %copy-done.11, f32[8,2048]{1,0:T(8,128)} %copy-done.10, ...), custom_call_target="tpu_custom_call" | custom-call | flops 629145600 | bytes 2883584 | tf_op jit(solution)/shard_map/final/pallas_call | solution.py:445
  252.1 3.5 %final.5.rest_0_ = bf16[1024,4,512]{2,1,0:T(4,128)(2,1)} custom-call(f32[4,6]{1,0:T(4,128)} %static_ref.11, bf16[1024,4,512]{2,1,0:T(4,128)(2,1)} %x_ref.15, f32[8,2048]{1,0:T(8,128)} %get-tuple-element.45.first_ref, f32[8,2048]{1,0:T(8,128)} %get-tuple-element.46.own2_ref, f32[8,2048]{1,0:T(8,128)} %copy-done.11, ...), custom_call_target="tpu_custom_call", output_to_operand_aliasing={{}: (10, {})} | custom-call | flops 629145600 | bytes 2883584 | tf_op jit(solution)/shard_map/final/pallas_call | solution.py:445
  255.6 1.4 collective-permute-done.26.outer_ref
  256.9 0.7 copy-done.19
  257.6 3.4 %final.6.rest_0_ = bf16[1024,4,512]{2,1,0:T(4,128)(2,1)} custom-call(f32[4,6]{1,0:T(4,128)} %static_ref.11, bf16[1024,4,512]{2,1,0:T(4,128)(2,1)} %x_ref.15, f32[8,2048]{1,0:T(8,128)} %get-tuple-element.30.first_ref, f32[8,2048]{1,0:T(8,128)} %get-tuple-element.31.own2_ref, f32[8,2048]{1,0:T(8,128)} %copy-done.13, ...), custom_call_target="tpu_custom_call", output_to_operand_aliasing={{}: (10, {})} | custom-call | flops 629145600 | bytes 2883584 | tf_op jit(solution)/shard_map/final/pallas_call | solution.py:445
  261.0 5.5 %collective-permute-done.23.outer_ref = bf16[256,512]{1,0:T(8,128)(2,1)S(1)} collective-permute-done((bf16[256,512]{1,0:T(8,128)(2,1)}, bf16[256,512]{1,0:T(8,128)(2,1)S(1)}, u32[]{:S(2)}, u32[]{:S(2)}) %collective-permute-start.23) | collective-permute-done | bytes 262176 | tf_op jit(solution)/shard_map/ppermute | solution.py:532
  266.6 0.7 copy-done.24
  267.3 3.4 %final.7 = bf16[1024,4,512]{2,1,0:T(4,128)(2,1)} custom-call(f32[4,6]{1,0:T(4,128)} %static_ref.11, bf16[1024,4,512]{2,1,0:T(4,128)(2,1)} %x_ref.15, f32[8,2048]{1,0:T(8,128)} %get-tuple-element.30.first_ref, f32[8,2048]{1,0:T(8,128)} %get-tuple-element.31.own2_ref, f32[8,2048]{1,0:T(8,128)} %copy-done.13, ...), custom_call_target="tpu_custom_call", output_to_operand_aliasing={{}: (10, {})} | custom-call | flops 629145600 | bytes 2883584 | tf_op jit(solution)/shard_map/final/pallas_call | solution.py:445
  (131 shorter events, 9.2 us)
Async XLA Ops:
  6.5 135.6 %all-gather.5.cloned.1.call-start = ((), (), s32[]{:S(2)}) async-start(), calls=%async_computation.1 | async-start | bytes 2621440 | tf_op jit(solution)/shard_map/all_gather | solution.py:480
  12.4 7.9 %collective-permute-start.19 = (f32[8,2048]{1,0:T(8,128)}, f32[8,2048]{1,0:T(8,128)S(1)}, u32[]{:S(2)}, u32[]{:S(2)}) collective-permute-start(f32[8,2048]{1,0:T(8,128)} %get-tuple-element.37.own_ref), channel_id=1, source_target_pairs={{0,3},{1,0},{2,1},{3,2},{4,7},{5,4},{6,5},{7,6},{8,11},{9,8},{10,9... | collective-permute-start | bytes 196616 | tf_op jit(solution)/shard_map/ppermute | solution.py:30
  17.5 6.7 %collective-permute-start.18 = (f32[8,2048]{1,0:T(8,128)}, f32[8,2048]{1,0:T(8,128)S(1)}, u32[]{:S(2)}, u32[]{:S(2)}) collective-permute-start(f32[8,2048]{1,0:T(8,128)} %get-tuple-element.37.own_ref), channel_id=1, source_target_pairs={{0,2},{1,3},{2,0},{3,1},{4,6},{5,7},{6,4},{7,5},{8,10},{9,11},{10,... | collective-permute-start | bytes 196616 | tf_op jit(solution)/shard_map/ppermute | solution.py:30
  17.5 6.7 %collective-permute-start.17 = (f32[8,2048]{1,0:T(8,128)}, f32[8,2048]{1,0:T(8,128)S(1)}, u32[]{:S(2)}, u32[]{:S(2)}) collective-permute-start(f32[8,2048]{1,0:T(8,128)} %get-tuple-element.37.own_ref), channel_id=1, source_target_pairs={{0,1},{1,2},{2,3},{3,0},{4,5},{5,6},{6,7},{7,4},{8,9},{9,10},{10,1... | collective-permute-start | bytes 196616 | tf_op jit(solution)/shard_map/ppermute | solution.py:30
  20.3 3.9 %copy-start.26 = (f32[8,2048]{1,0:T(8,128)}, f32[8,2048]{1,0:T(8,128)S(1)}, u32[]{:S(2)}) copy-start(f32[8,2048]{1,0:T(8,128)S(1)} %collective-permute-done.19.c_ref) | copy-start | bytes 196612
  29.5 137.3 %all-gather.3.cloned.1.call-start = ((), (), s32[]{:S(2)}) async-start(), calls=%async_computation | async-start | bytes 2621440 | tf_op jit(solution)/shard_map/all_gather | solution.py:480
  34.5 18.1 %collective-permute-start.7 = (bf16[64,2560]{1,0:T(8,128)(2,1)}, bf16[64,2560]{1,0:T(8,128)(2,1)S(1)}, u32[]{:S(2)}, u32[]{:S(2)}) collective-permute-start(bf16[64,2560]{1,0:T(8,128)(2,1)} %get-tuple-element.34), channel_id=1, source_target_pairs={{0,1},{1,2},{2,3},{3,0},{4,5},{5,6},{6,7},{7,4},{8,9},{9,10},{10,1... | collective-permute-start | bytes 983048 | tf_op jit(solution)/shard_map/ppermute | solution.py:474
  34.5 41.3 %collective-permute-start.8 = (bf16[64,2560]{1,0:T(8,128)(2,1)}, bf16[64,2560]{1,0:T(8,128)(2,1)S(1)}, u32[]{:S(2)}, u32[]{:S(2)}) collective-permute-start(bf16[64,2560]{1,0:T(8,128)(2,1)} %get-tuple-element.35), channel_id=1, source_target_pairs={{0,2},{1,3},{2,0},{3,1},{4,6},{5,7},{6,4},{7,5},{8,10},{9,11},{10,... | collective-permute-start | bytes 983048 | tf_op jit(solution)/shard_map/ppermute | solution.py:474
  36.9 38.8 %collective-permute-start.9 = (bf16[64,2560]{1,0:T(8,128)(2,1)}, bf16[64,2560]{1,0:T(8,128)(2,1)S(1)}, u32[]{:S(2)}, u32[]{:S(2)}) collective-permute-start(bf16[64,2560]{1,0:T(8,128)(2,1)} %get-tuple-element.36), channel_id=1, source_target_pairs={{0,3},{1,0},{2,1},{3,2},{4,7},{5,4},{6,5},{7,6},{8,11},{9,8},{10,9... | collective-permute-start | bytes 983048 | tf_op jit(solution)/shard_map/ppermute | solution.py:474
  52.6 23.2 %copy-start.3 = (bf16[64,2560]{1,0:T(8,128)(2,1)}, bf16[64,2560]{1,0:T(8,128)(2,1)S(1)}, u32[]{:S(2)}) copy-start(bf16[64,2560]{1,0:T(8,128)(2,1)S(1)} %collective-permute-done.7.refs_1_) | copy-start | bytes 983044
  79.1 48.3 %collective-permute-start.15 = (bf16[256,2560]{1,0:T(8,128)(2,1)}, bf16[256,2560]{1,0:T(8,128)(2,1)S(1)}, u32[]{:S(2)}, u32[]{:S(2)}) collective-permute-start(bf16[256,2560]{1,0:T(8,128)(2,1)} %assemble.1.refs_0_), channel_id=1, source_target_pairs={{0,24},{4,28},{8,16},{12,20},{16,8},{20,12},{24,0},{28,4},{1,25},{... | collective-permute-start | bytes 3932168 | tf_op jit(solution)/shard_map/ppermute | solution.py:114
  81.6 54.4 %collective-permute-start.13 = (bf16[256,2560]{1,0:T(8,128)(2,1)}, bf16[256,2560]{1,0:T(8,128)(2,1)}, u32[]{:S(2)}, u32[]{:S(2)}) collective-permute-start(bf16[256,2560]{1,0:T(8,128)(2,1)} %assemble.1.refs_0_), channel_id=1, source_target_pairs={{0,16},{4,20},{8,24},{12,28},{16,0},{20,4},{24,8},{28,12},{1,17},{... | collective-permute-start | bytes 3932168 | tf_op jit(solution)/shard_map/ppermute | solution.py:114
  82.0 54.0 %collective-permute-start.11 = (bf16[256,2560]{1,0:T(8,128)(2,1)}, bf16[256,2560]{1,0:T(8,128)(2,1)}, u32[]{:S(2)}, u32[]{:S(2)}) collective-permute-start(bf16[256,2560]{1,0:T(8,128)(2,1)} %assemble.1.refs_0_), channel_id=1, source_target_pairs={{0,8},{4,12},{8,0},{12,4},{16,24},{20,28},{24,16},{28,20},{1,9},{5... | collective-permute-start | bytes 3932168 | tf_op jit(solution)/shard_map/ppermute | solution.py:114
  86.9 35.6 %copy-start.33 = (s32[2]{0:T(128)S(1)}, s32[2]{0:T(128)}, u32[]{:S(2)}) copy-start(s32[2]{0:T(128)} %param.11) | copy-start | bytes 28
  86.9 36.9 %copy-start.32 = (s32[1024]{0:T(1024)S(1)}, s32[1024]{0:T(1024)}, u32[]{:S(2)}) copy-start(s32[1024]{0:T(1024)} %param.10) | copy-start | bytes 12292
  86.9 38.2 %copy-start = (bf16[256,2560]{1,0:T(8,128)(2,1)S(1)}, bf16[256,2560]{1,0:T(8,128)(2,1)}, u32[]{:S(2)}) copy-start(bf16[256,2560]{1,0:T(8,128)(2,1)} %assemble.1.refs_0_) | copy-start | bytes 3932164
  86.9 24.6 %collective-permute-start.2 = (f32[8,2048]{1,0:T(8,128)}, f32[8,2048]{1,0:T(8,128)S(1)}, u32[]{:S(2)}, u32[]{:S(2)}) collective-permute-start(f32[8,2048]{1,0:T(8,128)} %get-tuple-element.29.own_ref), channel_id=1, source_target_pairs={{0,3},{1,0},{2,1},{3,2},{4,7},{5,4},{6,5},{7,6},{8,11},{9,8},{10,9... | collective-permute-start | bytes 196616 | tf_op jit(solution)/shard_map/ppermute | solution.py:30
  107.2 6.8 %collective-permute-start.1 = (f32[8,2048]{1,0:T(8,128)}, f32[8,2048]{1,0:T(8,128)S(1)}, u32[]{:S(2)}, u32[]{:S(2)}) collective-permute-start(f32[8,2048]{1,0:T(8,128)} %get-tuple-element.29.own_ref), channel_id=1, source_target_pairs={{0,2},{1,3},{2,0},{3,1},{4,6},{5,7},{6,4},{7,5},{8,10},{9,11},{10,... | collective-permute-start | bytes 196616 | tf_op jit(solution)/shard_map/ppermute | solution.py:30
  111.5 6.3 %copy-start.27 = (f32[8,2048]{1,0:T(8,128)}, f32[8,2048]{1,0:T(8,128)S(1)}, u32[]{:S(2)}) copy-start(f32[8,2048]{1,0:T(8,128)S(1)} %collective-permute-done.2.c_ref) | copy-start | bytes 196612
  111.5 6.3 %collective-permute-start = (f32[8,2048]{1,0:T(8,128)}, f32[8,2048]{1,0:T(8,128)S(1)}, u32[]{:S(2)}, u32[]{:S(2)}) collective-permute-start(f32[8,2048]{1,0:T(8,128)} %get-tuple-element.29.own_ref), channel_id=1, source_target_pairs={{0,1},{1,2},{2,3},{3,0},{4,5},{5,6},{6,7},{7,4},{8,9},{9,10},{10,1... | collective-permute-start | bytes 196616 | tf_op jit(solution)/shard_map/ppermute | solution.py:30
  114.0 3.8 %copy-start.29 = (f32[8,2048]{1,0:T(8,128)}, f32[8,2048]{1,0:T(8,128)S(1)}, u32[]{:S(2)}) copy-start(f32[8,2048]{1,0:T(8,128)S(1)} %collective-permute-done.1.b_ref) | copy-start | bytes 196612
  123.8 13.4 %collective-permute-start.6 = (s32[512]{0:T(512)S(1)}, s32[512]{0:T(512)S(1)}, u32[]{:S(2)}, u32[]{:S(2)}) collective-permute-start(s32[512]{0:T(512)S(1)} %get-tuple-element.62), channel_id=1, source_target_pairs={{0,4},{4,8},{8,12},{12,16},{16,20},{20,24},{24,28},{1,5},{5,9},{9,... | collective-permute-start | bytes 6152 | tf_op jit(solution)/shard_map/ppermute | solution.py:24
  125.1 17.0 %collective-permute-start.10 = (bf16[256,2560]{1,0:T(8,128)(2,1)S(1)}, bf16[256,2560]{1,0:T(8,128)(2,1)}, u32[]{:S(2)}, u32[]{:S(2)}) collective-permute-start(bf16[256,2560]{1,0:T(8,128)(2,1)S(1)} %copy-done), channel_id=1, source_target_pairs={{0,4},{4,0},{8,12},{12,8},{16,20},{20,16},{24,28},{28,24},{1,5},{5... | collective-permute-start | bytes 3932168 | tf_op jit(solution)/shard_map/ppermute | solution.py:114
  127.4 14.7 %copy-start.1 = (bf16[256,2560]{1,0:T(8,128)(2,1)}, bf16[256,2560]{1,0:T(8,128)(2,1)S(1)}, u32[]{:S(2)}) copy-start(bf16[256,2560]{1,0:T(8,128)(2,1)S(1)} %collective-permute-done.15.refs_6_) | copy-start | bytes 3932164
  127.4 14.7 %collective-permute-start.16 = (bf16[256,2560]{1,0:T(8,128)(2,1)S(1)}, bf16[256,2560]{1,0:T(8,128)(2,1)}, u32[]{:S(2)}, u32[]{:S(2)}) collective-permute-start(bf16[256,2560]{1,0:T(8,128)(2,1)S(1)} %collective-permute-done.15.refs_6_), channel_id=1, source_target_pairs={{0,4},{4,0},{8,12},{12,8},{16,20},{20,16},{24,28},{28,24},{1,5},{5... | collective-permute-start | bytes 3932168 | tf_op jit(solution)/shard_map/ppermute | solution.py:114
  136.1 6.0 %collective-permute-start.14 = (bf16[256,2560]{1,0:T(8,128)(2,1)}, bf16[256,2560]{1,0:T(8,128)(2,1)}, u32[]{:S(2)}, u32[]{:S(2)}) collective-permute-start(bf16[256,2560]{1,0:T(8,128)(2,1)} %collective-permute-done.13.refs_4_), channel_id=1, source_target_pairs={{0,4},{4,0},{8,12},{12,8},{16,20},{20,16},{24,28},{28,24},{1,5},{5... | collective-permute-start | bytes 3932168 | tf_op jit(solution)/shard_map/ppermute | solution.py:114
  136.1 6.0 %collective-permute-start.12 = (bf16[256,2560]{1,0:T(8,128)(2,1)}, bf16[256,2560]{1,0:T(8,128)(2,1)}, u32[]{:S(2)}, u32[]{:S(2)}) collective-permute-start(bf16[256,2560]{1,0:T(8,128)(2,1)} %collective-permute-done.11.refs_2_), channel_id=1, source_target_pairs={{0,4},{4,0},{8,12},{12,8},{16,20},{20,16},{24,28},{28,24},{1,5},{5... | collective-permute-start | bytes 3932168 | tf_op jit(solution)/shard_map/ppermute | solution.py:114
  151.5 44.0 %collective-permute-start.20 = (bf16[2,512,512]{2,1,0:T(8,128)(2,1)S(1)}, bf16[2,512,512]{2,1,0:T(8,128)(2,1)S(1)}, u32[]{:S(2)}, u32[]{:S(2)}) collective-permute-start(bf16[2,512,512]{2,1,0:T(8,128)(2,1)S(1)} %slice.38), channel_id=1, source_target_pairs={{0,4},{4,8},{8,12},{12,16},{16,20},{20,24},{24,28},{1,5},{5,9},{9,... | collective-permute-start | bytes 3145736 | tf_op jit(solution)/shard_map/ppermute | solution.py:24
  178.9 13.1 %copy-start.6 = (f32[8,2048]{1,0:T(8,128)S(1)}, f32[8,2048]{1,0:T(8,128)}, u32[]{:S(2)}) copy-start(f32[8,2048]{1,0:T(8,128)} %get-tuple-element.46.own2_ref) | copy-start | bytes 196612
  178.9 21.6 %collective-permute-start.33 = (bf16[256,512]{1,0:T(8,128)(2,1)}, bf16[256,512]{1,0:T(8,128)(2,1)S(1)}, u32[]{:S(2)}, u32[]{:S(2)}) collective-permute-start(bf16[256,512]{1,0:T(8,128)(2,1)} %attend.7.own_ref), channel_id=1, source_target_pairs={{0,1},{1,0},{2,3},{3,2},{4,5},{5,4},{6,7},{7,6},{8,9},{9,8},{10,11... | collective-permute-start | bytes 786440 | tf_op jit(solution)/shard_map/ppermute | solution.py:114
  192.0 23.6 %collective-permute-start.30 = (bf16[256,512]{1,0:T(8,128)(2,1)}, bf16[256,512]{1,0:T(8,128)(2,1)S(1)}, u32[]{:S(2)}, u32[]{:S(2)}) collective-permute-start(bf16[256,512]{1,0:T(8,128)(2,1)} %attend.6.own_ref), channel_id=1, source_target_pairs={{0,1},{1,0},{2,3},{3,2},{4,5},{5,4},{6,7},{7,6},{8,9},{9,8},{10,11... | collective-permute-start | bytes 786440 | tf_op jit(solution)/shard_map/ppermute | solution.py:114
  192.0 17.9 %collective-permute-start.29 = (f32[8,2048]{1,0:T(8,128)S(1)}, f32[8,2048]{1,0:T(8,128)S(1)}, u32[]{:S(2)}, u32[]{:S(2)}) collective-permute-start(f32[8,2048]{1,0:T(8,128)S(1)} %copy-done.6), channel_id=1, source_target_pairs={{0,3},{1,0},{2,1},{3,2},{4,7},{5,4},{6,5},{7,6},{8,11},{9,8},{10,9... | collective-permute-start | bytes 196616 | tf_op jit(solution)/shard_map/ppermute | solution.py:30
  192.5 20.3 %collective-permute-start.28 = (f32[8,2048]{1,0:T(8,128)S(1)}, f32[8,2048]{1,0:T(8,128)S(1)}, u32[]{:S(2)}, u32[]{:S(2)}) collective-permute-start(f32[8,2048]{1,0:T(8,128)S(1)} %copy-done.6), channel_id=1, source_target_pairs={{0,2},{1,3},{2,0},{3,1},{4,6},{5,7},{6,4},{7,5},{8,10},{9,11},{10,... | collective-permute-start | bytes 196616 | tf_op jit(solution)/shard_map/ppermute | solution.py:30
  195.5 18.2 %collective-permute-start.27 = (f32[8,2048]{1,0:T(8,128)S(1)}, f32[8,2048]{1,0:T(8,128)S(1)}, u32[]{:S(2)}, u32[]{:S(2)}) collective-permute-start(f32[8,2048]{1,0:T(8,128)S(1)} %copy-done.6), channel_id=1, source_target_pairs={{0,1},{1,2},{2,3},{3,0},{4,5},{5,6},{6,7},{7,4},{8,9},{9,10},{10,1... | collective-permute-start | bytes 196616 | tf_op jit(solution)/shard_map/ppermute | solution.py:30
  200.5 24.8 %collective-permute-start.24 = (bf16[256,512]{1,0:T(8,128)(2,1)}, bf16[256,512]{1,0:T(8,128)(2,1)S(1)}, u32[]{:S(2)}, u32[]{:S(2)}) collective-permute-start(bf16[256,512]{1,0:T(8,128)(2,1)} %attend.5.own_ref), channel_id=1, source_target_pairs={{0,1},{1,0},{2,3},{3,2},{4,5},{5,4},{6,7},{7,6},{8,9},{9,8},{10,11... | collective-permute-start | bytes 786440 | tf_op jit(solution)/shard_map/ppermute | solution.py:114
  205.8 4.1 %copy-start.7 = (f32[8,2048]{1,0:T(8,128)S(1)}, f32[8,2048]{1,0:T(8,128)}, u32[]{:S(2)}) copy-start(f32[8,2048]{1,0:T(8,128)} %get-tuple-element.31.own2_ref) | copy-start | bytes 196612
  205.8 7.0 %copy-start.35 = (bf16[256,512]{1,0:T(8,128)(2,1)S(1)}, bf16[256,512]{1,0:T(8,128)(2,1)}, u32[]{:S(2)}) copy-start(bf16[256,512]{1,0:T(8,128)(2,1)} %get-tuple-element.51) | copy-start | bytes 786436
  209.9 11.1 %copy-start.8 = (f32[8,2048]{1,0:T(8,128)}, f32[8,2048]{1,0:T(8,128)S(1)}, u32[]{:S(2)}) copy-start(f32[8,2048]{1,0:T(8,128)S(1)} %collective-permute-done.29.c_ref) | copy-start | bytes 196612
  209.9 11.1 %collective-permute-start.5 = (f32[8,2048]{1,0:T(8,128)S(1)}, f32[8,2048]{1,0:T(8,128)S(1)}, u32[]{:S(2)}, u32[]{:S(2)}) collective-permute-start(f32[8,2048]{1,0:T(8,128)S(1)} %copy-done.7), channel_id=1, source_target_pairs={{0,3},{1,0},{2,1},{3,2},{4,7},{5,4},{6,5},{7,6},{8,11},{9,8},{10,9... | collective-permute-start | bytes 196616 | tf_op jit(solution)/shard_map/ppermute | solution.py:30
  212.9 8.1 %copy-start.10 = (f32[8,2048]{1,0:T(8,128)}, f32[8,2048]{1,0:T(8,128)S(1)}, u32[]{:S(2)}) copy-start(f32[8,2048]{1,0:T(8,128)S(1)} %collective-permute-done.28.b_ref) | copy-start | bytes 196612
  212.9 8.1 %copy-start.34 = (bf16[256,512]{1,0:T(8,128)(2,1)S(1)}, bf16[256,512]{1,0:T(8,128)(2,1)}, u32[]{:S(2)}) copy-start(bf16[256,512]{1,0:T(8,128)(2,1)} %get-tuple-element.52) | copy-start | bytes 786436
  212.9 18.6 %collective-permute-start.34 = (bf16[256,512]{1,0:T(8,128)(2,1)S(1)}, bf16[256,512]{1,0:T(8,128)(2,1)S(1)}, u32[]{:S(2)}, u32[]{:S(2)}) collective-permute-start(bf16[256,512]{1,0:T(8,128)(2,1)S(1)} %copy-done.35), channel_id=1, source_target_pairs={{1,2},{2,1},{5,6},{6,5},{9,10},{10,9},{13,14},{14,13},{17,18},{18,... | collective-permute-start | bytes 786440 | tf_op jit(solution)/shard_map/ppermute | solution.py:531
  213.7 7.3 %copy-start.11 = (f32[8,2048]{1,0:T(8,128)}, f32[8,2048]{1,0:T(8,128)S(1)}, u32[]{:S(2)}) copy-start(f32[8,2048]{1,0:T(8,128)S(1)} %collective-permute-done.27.a_ref) | copy-start | bytes 196612
  213.7 10.9 %collective-permute-start.4 = (f32[8,2048]{1,0:T(8,128)S(1)}, f32[8,2048]{1,0:T(8,128)S(1)}, u32[]{:S(2)}, u32[]{:S(2)}) collective-permute-start(f32[8,2048]{1,0:T(8,128)S(1)} %copy-done.7), channel_id=1, source_target_pairs={{0,2},{1,3},{2,0},{3,1},{4,6},{5,7},{6,4},{7,5},{8,10},{9,11},{10,... | collective-permute-start | bytes 196616 | tf_op jit(solution)/shard_map/ppermute | solution.py:30
  215.6 16.6 %collective-permute-start.21 = (bf16[256,512]{1,0:T(8,128)(2,1)}, bf16[256,512]{1,0:T(8,128)(2,1)S(1)}, u32[]{:S(2)}, u32[]{:S(2)}) collective-permute-start(bf16[256,512]{1,0:T(8,128)(2,1)} %attend.4.own_ref), channel_id=1, source_target_pairs={{0,1},{1,0},{2,3},{3,2},{4,5},{5,4},{6,7},{7,6},{8,9},{9,8},{10,11... | collective-permute-start | bytes 786440 | tf_op jit(solution)/shard_map/ppermute | solution.py:114
  221.0 10.5 %copy-start.9 = (f32[8,2048]{1,0:T(8,128)}, f32[8,2048]{1,0:T(8,128)S(1)}, u32[]{:S(2)}) copy-start(f32[8,2048]{1,0:T(8,128)S(1)} %collective-permute-done.5.c_ref) | copy-start | bytes 196612
  221.0 17.2 %collective-permute-start.35 = (bf16[256,512]{1,0:T(8,128)(2,1)S(1)}, bf16[256,512]{1,0:T(8,128)(2,1)S(1)}, u32[]{:S(2)}, u32[]{:S(2)}) collective-permute-start(bf16[256,512]{1,0:T(8,128)(2,1)S(1)} %copy-done.34), channel_id=1, source_target_pairs={{1,3},{2,0},{5,7},{6,4},{9,11},{10,8},{13,15},{14,12},{17,19},{18,... | collective-permute-start | bytes 786440 | tf_op jit(solution)/shard_map/ppermute | solution.py:532
  224.6 6.9 %copy-start.12 = (f32[8,2048]{1,0:T(8,128)}, f32[8,2048]{1,0:T(8,128)S(1)}, u32[]{:S(2)}) copy-start(f32[8,2048]{1,0:T(8,128)S(1)} %collective-permute-done.4.b_ref) | copy-start | bytes 196612
  224.6 14.3 %collective-permute-start.31 = (bf16[256,512]{1,0:T(8,128)(2,1)}, bf16[256,512]{1,0:T(8,128)(2,1)S(1)}, u32[]{:S(2)}, u32[]{:S(2)}) collective-permute-start(bf16[256,512]{1,0:T(8,128)(2,1)} %get-tuple-element.48), channel_id=1, source_target_pairs={{1,2},{2,1},{5,6},{6,5},{9,10},{10,9},{13,14},{14,13},{17,18},{18,... | collective-permute-start | bytes 786440 | tf_op jit(solution)/shard_map/ppermute | solution.py:531
  225.3 1.5 copy-start.20
  225.3 19.0 %collective-permute-start.32 = (bf16[256,512]{1,0:T(8,128)(2,1)}, bf16[256,512]{1,0:T(8,128)(2,1)S(1)}, u32[]{:S(2)}, u32[]{:S(2)}) collective-permute-start(bf16[256,512]{1,0:T(8,128)(2,1)} %get-tuple-element.49), channel_id=1, source_target_pairs={{1,3},{2,0},{5,7},{6,4},{9,11},{10,8},{13,15},{14,12},{17,19},{18,... | collective-permute-start | bytes 786440 | tf_op jit(solution)/shard_map/ppermute | solution.py:532
  231.5 6.7 %copy-start.14 = (bf16[256,512]{1,0:T(8,128)(2,1)}, bf16[256,512]{1,0:T(8,128)(2,1)S(1)}, u32[]{:S(2)}) copy-start(bf16[256,512]{1,0:T(8,128)(2,1)S(1)} %collective-permute-done.34.inner_ref) | copy-start | bytes 786436
  231.5 24.0 %collective-permute-start.25 = (bf16[256,512]{1,0:T(8,128)(2,1)}, bf16[256,512]{1,0:T(8,128)(2,1)S(1)}, u32[]{:S(2)}, u32[]{:S(2)}) collective-permute-start(bf16[256,512]{1,0:T(8,128)(2,1)} %get-tuple-element.43), channel_id=1, source_target_pairs={{1,2},{2,1},{5,6},{6,5},{9,10},{10,9},{13,14},{14,13},{17,18},{18,... | collective-permute-start | bytes 786440 | tf_op jit(solution)/shard_map/ppermute | solution.py:531
  232.2 1.3 copy-start.23
  232.2 24.7 %collective-permute-start.26 = (bf16[256,512]{1,0:T(8,128)(2,1)}, bf16[256,512]{1,0:T(8,128)(2,1)S(1)}, u32[]{:S(2)}, u32[]{:S(2)}) collective-permute-start(bf16[256,512]{1,0:T(8,128)(2,1)} %get-tuple-element.44), channel_id=1, source_target_pairs={{1,3},{2,0},{5,7},{6,4},{9,11},{10,8},{13,15},{14,12},{17,19},{18,... | collective-permute-start | bytes 786440 | tf_op jit(solution)/shard_map/ppermute | solution.py:532
  238.2 10.4 %copy-start.16 = (bf16[256,512]{1,0:T(8,128)(2,1)}, bf16[256,512]{1,0:T(8,128)(2,1)S(1)}, u32[]{:S(2)}) copy-start(bf16[256,512]{1,0:T(8,128)(2,1)S(1)} %collective-permute-done.35.outer_ref) | copy-start | bytes 786436
  238.2 22.8 %collective-permute-start.22 = (bf16[256,512]{1,0:T(8,128)(2,1)}, bf16[256,512]{1,0:T(8,128)(2,1)S(1)}, u32[]{:S(2)}, u32[]{:S(2)}) collective-permute-start(bf16[256,512]{1,0:T(8,128)(2,1)} %get-tuple-element.40), channel_id=1, source_target_pairs={{1,2},{2,1},{5,6},{6,5},{9,10},{10,9},{13,14},{14,13},{17,18},{18,... | collective-permute-start | bytes 786440 | tf_op jit(solution)/shard_map/ppermute | solution.py:531
  238.9 13.1 %copy-start.15 = (bf16[256,512]{1,0:T(8,128)(2,1)}, bf16[256,512]{1,0:T(8,128)(2,1)S(1)}, u32[]{:S(2)}) copy-start(bf16[256,512]{1,0:T(8,128)(2,1)S(1)} %collective-permute-done.31.inner_ref) | copy-start | bytes 786436
  238.9 27.6 %collective-permute-start.23 = (bf16[256,512]{1,0:T(8,128)(2,1)}, bf16[256,512]{1,0:T(8,128)(2,1)S(1)}, u32[]{:S(2)}, u32[]{:S(2)}) collective-permute-start(bf16[256,512]{1,0:T(8,128)(2,1)} %get-tuple-element.41), channel_id=1, source_target_pairs={{1,3},{2,0},{5,7},{6,4},{9,11},{10,8},{13,15},{14,12},{17,19},{18,... | collective-permute-start | bytes 786440 | tf_op jit(solution)/shard_map/ppermute | solution.py:532
  244.3 7.8 %copy-start.18 = (bf16[256,512]{1,0:T(8,128)(2,1)}, bf16[256,512]{1,0:T(8,128)(2,1)S(1)}, u32[]{:S(2)}) copy-start(bf16[256,512]{1,0:T(8,128)(2,1)S(1)} %collective-permute-done.32.outer_ref) | copy-start | bytes 786436
  244.3 11.2 %collective-permute-start.3 = (f32[8,2048]{1,0:T(8,128)S(1)}, f32[8,2048]{1,0:T(8,128)S(1)}, u32[]{:S(2)}, u32[]{:S(2)}) collective-permute-start(f32[8,2048]{1,0:T(8,128)S(1)} %copy-done.7), channel_id=1, source_target_pairs={{0,1},{1,2},{2,3},{3,0},{4,5},{5,6},{6,7},{7,4},{8,9},{9,10},{10,1... | collective-permute-start | bytes 196616 | tf_op jit(solution)/shard_map/ppermute | solution.py:30
  255.5 1.4 copy-start.13
  255.5 1.4 copy-start.17
  261.0 5.5 %copy-start.22 = (bf16[256,512]{1,0:T(8,128)(2,1)}, bf16[256,512]{1,0:T(8,128)(2,1)S(1)}, u32[]{:S(2)}) copy-start(bf16[256,512]{1,0:T(8,128)(2,1)S(1)} %collective-permute-done.22.inner_ref) | copy-start | bytes 786436
  (10 other events, 7.2 us)
Sparse Core Ops, SparseCore 0:
  29.6 70.5 all-gather.4
  122.6 44.1 all-gather.2

commit v3 on v2

--- a/solution.py
+++ b/solution.py
@@ -336,24 +336,32 @@
 
 
 def project_kernel(place_ref, ring_ref, own_ref, other_ref, *refs):
-    pieces = refs[:-4]
-    kept_ref, inner_ref, outer_ref, sums = refs[-4:]
+    pieces = refs[:-6]
+    kept_ref, inner_ref, outer_ref, sums, held, arrived = refs[-6:]
     servers, _, width = sums.shape
+    depth, pair = held.shape[1:]
+    copies = []
+    for at, piece in enumerate(pieces):
+        start = piece.shape[1] - pair
+        copies.append(
+            pltpu.make_async_copy(piece.at[:, start : start + pair], held.at[at], arrived.at[at])
+        )
+        copies[-1].start()
     place = place_ref[0]
     even = place % 2 == 0
     own, other = own_ref[...], other_ref[...]
     both = jnp.concatenate([jnp.where(even, own, other), jnp.where(even, other, own)], axis=1)
-    depth = pieces[0].shape[0]
-    if len(pieces) == 1:
-        for server in range(servers):
-            rows = pieces[0][server * width : (server + 1) * width, :]
-            sums[server] = contract(both, rows, 1, 1)
-    else:
-        for piece in range(len(pieces)):
-            target = ring_ref[0] ^ piece
+    for at, copy in enumerate(copies):
+        copy.wait()
+        if len(pieces) == 1:
+            for server in range(servers):
+                rows = held[0, server * width : (server + 1) * width, :]
+                sums[server] = contract(both, rows, 1, 1)
+        else:
+            target = ring_ref[0] ^ at
             inside = pl.multiple_of((target % (width // depth)) * depth, depth)
             sums[target // (width // depth), :, pl.ds(inside, depth)] = contract(
-                both, pieces[piece][...], 1, 1
+                both, held[at], 1, 1
             )
     kept_ref[...] = sums[place]
     low = place < 2
@@ -363,21 +371,25 @@
 
 def project(place, ring, own, other, pieces, servers):
     tokens, width = own.shape
-    rows, columns = pieces[0].shape
+    rows = pieces[0].shape[0]
     pair = 2 * width
-    tail = pl.BlockSpec((pl.Element(rows), pl.Element(pair)), lambda i: (0, columns - pair))
-    full = pl.BlockSpec((tokens, width), lambda i: (0, 0))
+    full = pl.BlockSpec(memory_space=pltpu.VMEM)
     return pl.pallas_call(
         project_kernel,
-        grid=(1,),
-        in_specs=[pl.BlockSpec(memory_space=pltpu.SMEM)] * 2 + [full] * 2 + [tail] * len(pieces),
+        in_specs=[pl.BlockSpec(memory_space=pltpu.SMEM)] * 2
+        + [full] * 2
+        + [pl.BlockSpec(memory_space=pl.ANY)] * len(pieces),
         out_specs=[full] * 3,
         out_shape=[
             jax.ShapeDtypeStruct((tokens, width), F32),
             jax.ShapeDtypeStruct((tokens, width), BF),
             jax.ShapeDtypeStruct((tokens, width), BF),
         ],
-        scratch_shapes=[pltpu.VMEM((servers, tokens, width), F32)],
+        scratch_shapes=[
+            pltpu.VMEM((servers, tokens, width), F32),
+            pltpu.VMEM((len(pieces), rows, pair), BF),
+            pltpu.SemaphoreType.DMA((len(pieces),)),
+        ],
         cost_estimate=cost(2 * tokens * D * pair, D * pair * 2 + tokens * width * 12),
         compiler_params=params(),
         name="project",
@@ -465,27 +477,32 @@
         [hc_proj.T, jnp.ones((1, width), F32), jnp.zeros((1, width), F32)], axis=0
     )
     first_late, second_late = stats(streams, proj_rows, BLOCK, BLOCK)
-    late = [first_late] + from_others(first_late, "mp")
+    late = from_others(first_late, "mp")
     parts = list(regroup(place, proj_master, group_size))
     first_early, second_early = stats(streams, proj_rows, 0, BLOCK)
-    early = [first_early] + from_others(first_early, "mp")
-
+    late, parts, first_early = lax.optimization_barrier((late, parts, first_early))
+    early = from_others(first_early, "mp")
     for step in range(1, group_size):
         parts[step] = lax.ppermute(
             parts[step], "mp", [(at, (at + step) % group_size) for at in range(group_size)]
         )
-    pieces = weight_pieces(assemble(place, parts))
 
     def gathered(normed):
         rows = lax.all_gather(normed, "mp", axis=0, tiled=True)
         return rows.reshape(group_size, normed.shape[0], width)
 
-    sums_late, normed_late = mix(hc_static, streams, late, BLOCK, BLOCK, 0)
+    sums_late, normed_late = mix(hc_static, streams, [first_late] + late, BLOCK, BLOCK, 0)
     rows_late = gathered(normed_late)
-    sums_early, normed_early = mix(hc_static, streams, early, 0, BLOCK, 0)
+    sums_early, normed_early = mix(hc_static, streams, [first_early] + early, 0, BLOCK, 0)
+
+    parts, normed_early = lax.optimization_barrier((parts, normed_early))
     rows_early = gathered(normed_early)
+    pieces = weight_pieces(assemble(place, parts))
     second_late = [second_late] + from_others(second_late, "mp")
     second_early = [second_early] + from_others(second_early, "mp")
+    rows_late, second_late, second_early = lax.optimization_barrier(
+        (rows_late, second_late, second_early)
+    )
 
     halo = passed_along(segment_ids[-BLOCK:], "blk", 1)
     halo = jnp.where(lax.axis_index("blk") == 0, -1, halo)

time: 280 us -> 322 us (1.15)
  waiting for transfers between devices: 82.2 us -> 126 us
  starting transfers between devices: 75 us -> 63.9 us
  Pallas kernels: 88.9 us -> 97.6 us
    ppermute x12, waiting for transfers between devices: 14 us -> 63.6 us  [from_others(): lax.ppermute(value, axis, [(source, (source + step) % count) for source i...]
    ppermute x11, waiting for transfers between devices: 8.59 us -> 51.6 us  [swapped(): lax.ppermute(value, axis, [(source, source ^ mask) for source in range(co...]
    ppermute x3, waiting for transfers between devices: 37.2 us -> 0.01 us  [body(): lax.ppermute(parts[step], 'mp', [(at, (at + step) % group_size) for at in...]
    all_gather x2, waiting for transfers between devices: 11.4 us -> 0.01 us  [gathered(): rows = lax.all_gather(normed, 'mp', axis=0, tiled=True)]
    pallas_call x4, Pallas kernels: 18.6 us -> 27.2 us  [project(): pl.pallas_call(project_kernel, in_specs=[pl.BlockSpec(memory_space=pltpu....]
    ppermute x12, starting transfers between devices: 43.5 us -> 36.4 us  [from_others(): lax.ppermute(value, axis, [(source, (source + step) % count) for source i...]
    ppermute x11, starting transfers between devices: 15.6 us -> 11.5 us  [swapped(): lax.ppermute(value, axis, [(source, source ^ mask) for source in range(co...]
    unnamed x72 -> x78, local copies, waits for them, and re-layouts: 6.34 us -> 7.41 us
  transfers between devices with their start and end apart: 38 -> 38, of which waited for: 13 -> 13; matrix products, arithmetic and copies ran while one was open for 3% -> 3% of each run, Pallas kernels for 28% -> 27%
where the time goes in v3:
time: 322 us; the launch traced here: 320 us
  waiting for transfers between devices  126 us (39%)
  Pallas kernels  97.6 us (30%)
  starting transfers between devices  63.9 us (20%)
  between operations  15.3 us (5%)
  local copies, waits for them, and re-layouts  11.1 us (3%)
  other arithmetic  6.3 us (2%)
    ppermute x12, waiting for transfers between devices, from_others(): lax.ppermute(value, axis, [(source, (source + step) % count) for source i...  63.6 us
    ppermute x11, waiting for transfers between devices, swapped(): lax.ppermute(value, axis, [(source, source ^ mask) for source in range(co...  51.6 us
    ppermute x12, starting transfers between devices, from_others(): lax.ppermute(value, axis, [(source, (source + step) % count) for source i...  36.4 us
    pallas_call x4, Pallas kernels, project(): pl.pallas_call(project_kernel, in_specs=[pl.BlockSpec(memory_space=pltpu....  27.2 us
    pallas_call x4, Pallas kernels, attend(): pl.pallas_call(attend_kernel, grid=(1,), in_specs=[pl.BlockSpec(block, la...  16.1 us
    pallas_call x2, Pallas kernels, qkv_columns(): pl.pallas_call(qkv_kernel, grid=(3,), in_specs=[pl.BlockSpec(memory_space...  16.1 us
    pallas_call x4, Pallas kernels, final(): pl.pallas_call(final_kernel, grid=(tokens // step,), in_specs=specs, out_...  13.7 us
    ppermute x11, starting transfers between devices, swapped(): lax.ppermute(value, axis, [(source, source ^ mask) for source in range(co...  11.5 us
  transfers between devices with their start and end apart: 38, of which 13 were waited for; matrix products, arithmetic and copies ran while one was open for 3% of the time, Pallas kernels for 27%

profile of v3, /device:TPU:0, one launch (start us, length us, event | category | flops | bytes accessed | tf_op | source)
XLA Modules:
  0.0 320.4 jit_solution(6345693208906232672)
XLA Ops:
  6.7 1.4 maximum_maximum_fusion.proj_ref
  8.1 4.3 %stats.2 = (f32[8,2048]{1,0:T(8,128)}, f32[8,2048]{1,0:T(8,128)}) custom-call(bf16[1024,4,512]{2,1,0:T(4,128)(2,1)} %x_ref.15, f32[8,512]{1,0:T(8,128)} %maximum_maximum_fusion.proj_ref), custom_call_target="tpu_custom_call" | custom-call | flops 629145600 | bytes 2097152 | tf_op jit(solution)/shard_map/stats/pallas_call | solution.py:157
  12.4 5.0 %collective-permute-start.2 = (f32[8,2048]{1,0:T(8,128)}, f32[8,2048]{1,0:T(8,128)S(1)}, u32[]{:S(2)}, u32[]{:S(2)}) collective-permute-start(f32[8,2048]{1,0:T(8,128)} %get-tuple-element.51.own_ref), channel_id=1, source_target_pairs={{0,3},{1,0},{2,1},{3,2},{4,7},{5,4},{6,5},{7,6},{8,11},{9,8},{10,9... | collective-permute-start | bytes 196616 | tf_op jit(solution)/shard_map/ppermute | solution.py:30
  17.5 1.0 collective-permute-start
  18.5 4.9 %regroup.1 = (bf16[64,2560]{1,0:T(8,128)(2,1)}, bf16[64,2560]{1,0:T(8,128)(2,1)}, bf16[64,2560]{1,0:T(8,128)(2,1)}, bf16[64,2560]{1,0:T(8,128)(2,1)}) custom-call(s32[1]{0:T(128)} %bitcast.1.place_ref, f32[64,4,2048]{2,1,0:T(4,128)} %master_ref.1), custom_call_target="tpu_custom_call" | custom-call | bytes 3407872 | tf_op jit(solution)/shard_map/regroup/pallas_call | solution.py:78
  23.4 4.3 %stats.3 = (f32[8,2048]{1,0:T(8,128)}, f32[8,2048]{1,0:T(8,128)}) custom-call(bf16[1024,4,512]{2,1,0:T(4,128)(2,1)} %x_ref.15, f32[8,512]{1,0:T(8,128)} %maximum_maximum_fusion.proj_ref), custom_call_target="tpu_custom_call" | custom-call | flops 629145600 | bytes 2097152 | tf_op jit(solution)/shard_map/stats/pallas_call | solution.py:157
  28.4 4.2 %mix.3 = (f32[8,2048]{1,0:T(8,128)}, bf16[512,512]{1,0:T(8,128)(2,1)}) custom-call(f32[4,6]{1,0:T(4,128)} %static_ref.11, bf16[1024,4,512]{2,1,0:T(4,128)(2,1)} %x_ref.15, f32[8,2048]{1,0:T(8,128)} %get-tuple-element.51.own_ref, f32[8,2048]{1,0:T(8,128)} %copy-done.29, f32[8,2048]{1,0:T(8,128)} %copy-done.28, f32[8,2048]{1,0:T(8,128)} %copy-done.27), custom_call_target="tpu_custom_call" | custom-call | flops 419430400 | bytes 2621440 | tf_op jit(solution)/shard_map/mix/pallas_call | solution.py:216
  32.7 2.5 collective-permute-start.12
  35.2 0.9 collective-permute-start.13
  36.1 1.6 collective-permute-start.14
  37.7 1.9 collective-permute-start.5
  39.6 35.1 %collective-permute-done.5.c_ref = f32[8,2048]{1,0:T(8,128)S(1)} collective-permute-done((f32[8,2048]{1,0:T(8,128)S(1)}, f32[8,2048]{1,0:T(8,128)S(1)}, u32[]{:S(2)}, u32[]{:S(2)}) %collective-permute-start.5) | collective-permute-done | bytes 65568 | tf_op jit(solution)/shard_map/ppermute | solution.py:30
  74.7 26.5 %collective-permute-start.3 = (f32[8,2048]{1,0:T(8,128)S(1)}, f32[8,2048]{1,0:T(8,128)S(1)}, u32[]{:S(2)}, u32[]{:S(2)}) collective-permute-start(f32[8,2048]{1,0:T(8,128)S(1)} %copy-done.26), channel_id=1, source_target_pairs={{0,1},{1,2},{2,3},{3,0},{4,5},{5,6},{6,7},{7,4},{8,9},{9,10},{10,1... | collective-permute-start | bytes 196616 | tf_op jit(solution)/shard_map/ppermute | solution.py:30
  101.3 2.3 collective-permute-done.4.b_ref
  104.8 4.1 %mix.2 = (f32[8,2048]{1,0:T(8,128)}, bf16[512,512]{1,0:T(8,128)(2,1)}) custom-call(f32[4,6]{1,0:T(4,128)} %static_ref.11, bf16[1024,4,512]{2,1,0:T(4,128)(2,1)} %x_ref.15, f32[8,2048]{1,0:T(8,128)} %get-tuple-element.57.own_ref, f32[8,2048]{1,0:T(8,128)} %copy-done.32, f32[8,2048]{1,0:T(8,128)} %copy-done.31, f32[8,2048]{1,0:T(8,128)} %copy-done.30), custom_call_target="tpu_custom_call" | custom-call | flops 419430400 | bytes 2621440 | tf_op jit(solution)/shard_map/mix/pallas_call | solution.py:216
  109.0 0.7 copy-done.3
  110.0 2.5 assemble.1.refs_0_
  112.4 2.5 collective-permute-start.21
  117.2 1.3 collective-permute-start.15
  118.5 2.3 collective-permute-start.16
  120.8 24.4 %collective-permute-done.21.refs_6_ = bf16[256,2560]{1,0:T(8,128)(2,1)S(1)} collective-permute-done((bf16[256,2560]{1,0:T(8,128)(2,1)}, bf16[256,2560]{1,0:T(8,128)(2,1)S(1)}, u32[]{:S(2)}, u32[]{:S(2)}) %collective-permute-start.21) | collective-permute-done | bytes 1310752 | tf_op jit(solution)/shard_map/ppermute | solution.py:114
  145.2 27.0 %collective-permute-done.19.refs_4_ = bf16[256,2560]{1,0:T(8,128)(2,1)S(1)} collective-permute-done((bf16[256,2560]{1,0:T(8,128)(2,1)}, bf16[256,2560]{1,0:T(8,128)(2,1)S(1)}, u32[]{:S(2)}, u32[]{:S(2)}) %collective-permute-start.19) | collective-permute-done | bytes 1310752 | tf_op jit(solution)/shard_map/ppermute | solution.py:114
  173.4 0.9 collective-permute-start.11
  174.4 3.4 %collective-permute-done.11.c_ref = f32[8,2048]{1,0:T(8,128)S(1)} collective-permute-done((f32[8,2048]{1,0:T(8,128)S(1)}, f32[8,2048]{1,0:T(8,128)S(1)}, u32[]{:S(2)}, u32[]{:S(2)}) %collective-permute-start.11) | collective-permute-done | bytes 65568 | tf_op jit(solution)/shard_map/ppermute | solution.py:30
  177.8 5.6 %collective-permute-done.10.b_ref = f32[8,2048]{1,0:T(8,128)S(1)} collective-permute-done((f32[8,2048]{1,0:T(8,128)S(1)}, f32[8,2048]{1,0:T(8,128)S(1)}, u32[]{:S(2)}, u32[]{:S(2)}) %collective-permute-start.10) | collective-permute-done | bytes 65568 | tf_op jit(solution)/shard_map/ppermute | solution.py:30
  183.5 6.2 %collective-permute-done.9.a_ref = f32[8,2048]{1,0:T(8,128)S(1)} collective-permute-done((f32[8,2048]{1,0:T(8,128)S(1)}, f32[8,2048]{1,0:T(8,128)S(1)}, u32[]{:S(2)}, u32[]{:S(2)}) %collective-permute-start.9) | collective-permute-done | bytes 65568 | tf_op jit(solution)/shard_map/ppermute | solution.py:30
  189.7 0.8 collective-permute-start.8
  190.5 1.6 convert_reduce_fusion
  192.1 2.5 collective-permute-done.8.c_ref
  194.7 1.9 fusion.1
  196.6 3.8 %collective-permute-done.7.b_ref = f32[8,2048]{1,0:T(8,128)S(1)} collective-permute-done((f32[8,2048]{1,0:T(8,128)S(1)}, f32[8,2048]{1,0:T(8,128)S(1)}, u32[]{:S(2)}, u32[]{:S(2)}) %collective-permute-start.7) | collective-permute-done | bytes 65568 | tf_op jit(solution)/shard_map/ppermute | solution.py:30
  200.4 1.4 pad_maximum_fusion
  201.8 4.6 %collective-permute-done.6.a_ref = f32[8,2048]{1,0:T(8,128)S(1)} collective-permute-done((f32[8,2048]{1,0:T(8,128)S(1)}, f32[8,2048]{1,0:T(8,128)S(1)}, u32[]{:S(2)}, u32[]{:S(2)}) %collective-permute-start.6) | collective-permute-done | bytes 65568 | tf_op jit(solution)/shard_map/ppermute | solution.py:30
  206.5 8.1 %qkv.3.q_ref.k1.k2.v1.v2 = bf16[3,512,512]{2,1,0:T(8,128)(2,1)} custom-call(s32[1]{0:T(128)} %bitcast.3.ring_ref, bf16[4,512,512]{2,1,0:T(8,128)(2,1)} %bitcast.10, f32[1024,128]{1,0:T(8,128)} %get-tuple-element.111.cosine_ref, f32[1024,128]{1,0:T(8,128)} %get-tuple-element.112.sine_ref, bf16[256,2560]{1,0:T(8,128)(2,1)} %assemble.1.refs_0_, ...), custom_call_target="tpu_custom_call" | custom-call | flops 3221225472 | bytes 11534336 | tf_op jit(solution)/shard_map/qkv/pallas_call | solution.py:272
  214.5 1.3 slice.38
  215.8 1.5 collective-permute-start.23
  217.4 1.0 copy.14.qseg_ref
  219.1 8.1 %qkv.2.q_ref.k1.k2.v1.v2.k0.v0 = bf16[3,512,512]{2,1,0:T(8,128)(2,1)} custom-call(s32[1]{0:T(128)} %bitcast.3.ring_ref, bf16[4,512,512]{2,1,0:T(8,128)(2,1)} %bitcast.11, f32[1024,128]{1,0:T(8,128)} %get-tuple-element.111.cosine_ref, f32[1024,128]{1,0:T(8,128)} %get-tuple-element.112.sine_ref, bf16[256,2560]{1,0:T(8,128)(2,1)} %assemble.1.refs_0_, ...), custom_call_target="tpu_custom_call" | custom-call | flops 3221225472 | bytes 11534336 | tf_op jit(solution)/shard_map/qkv/pallas_call | solution.py:272
  227.2 4.0 %attend.7.own_ref = bf16[256,512]{1,0:T(8,128)(2,1)} custom-call(bf16[3,512,512]{2,1,0:T(8,128)(2,1)} %qkv.3.q_ref.k1.k2.v1.v2, bf16[3,512,512]{2,1,0:T(8,128)(2,1)} %qkv.2.q_ref.k1.k2.v1.v2.k0.v0, bf16[3,512,512]{2,1,0:T(8,128)(2,1)} %qkv.2.q_ref.k1.k2.v1.v2.k0.v0, bf16[3,512,512]{2,1,0:T(8,128)(2,1)} %qkv.3.q_ref.k1.k2.v1.v2, ...), custom_call_target="tpu_custom_call" | custom-call | flops 402653184 | bytes 2097152 | tf_op jit(solution)/shard_map/attend/pallas_call | solution.py:320
  231.2 4.0 %attend.6.own_ref = bf16[256,512]{1,0:T(8,128)(2,1)} custom-call(bf16[3,512,512]{2,1,0:T(8,128)(2,1)} %qkv.3.q_ref.k1.k2.v1.v2, bf16[3,512,512]{2,1,0:T(8,128)(2,1)} %qkv.2.q_ref.k1.k2.v1.v2.k0.v0, bf16[3,512,512]{2,1,0:T(8,128)(2,1)} %qkv.3.q_ref.k1.k2.v1.v2, bf16[3,512,512]{2,1,0:T(8,128)(2,1)} %qkv.3.q_ref.k1.k2.v1.v2, ...), custom_call_target="tpu_custom_call" | custom-call | flops 402653184 | bytes 2097152 | tf_op jit(solution)/shard_map/attend/pallas_call | solution.py:320
  235.3 2.0 collective-permute-start.30
  237.3 1.0 copy-done.2
  238.3 4.0 %attend.5.own_ref = bf16[256,512]{1,0:T(8,128)(2,1)} custom-call(bf16[3,512,512]{2,1,0:T(8,128)(2,1)} %qkv.2.q_ref.k1.k2.v1.v2.k0.v0, bf16[2,512,512]{2,1,0:T(8,128)(2,1)} %copy-done.2, bf16[2,512,512]{2,1,0:T(8,128)(2,1)} %copy-done.2, bf16[3,512,512]{2,1,0:T(8,128)(2,1)} %qkv.2.q_ref.k1.k2.v1.v2.k0.v0, bf16[2,512,512]{2,1,0:T(8,128)(2,1)} %copy-done.2, ...), custom_call_target="tpu_custom_call" | custom-call | flops 402653184 | bytes 2097152 | tf_op jit(solution)/shard_map/attend/pallas_call | solution.py:320
  242.3 0.7 copy-done.25
  243.0 6.8 %project.7 = (f32[256,512]{1,0:T(8,128)}, bf16[256,512]{1,0:T(8,128)(2,1)}, bf16[256,512]{1,0:T(8,128)(2,1)}) custom-call(s32[1]{0:T(128)} %bitcast.1.place_ref, s32[1]{0:T(128)} %bitcast.3.ring_ref, bf16[256,512]{1,0:T(8,128)(2,1)} %attend.7.own_ref, bf16[256,512]{1,0:T(8,128)(2,1)} %copy-done.25, bf16[256,2560]{1,0:T(8,128)(2,1)} %assemble.1.refs_0_, ...), custom_call_target="tpu_custom_call" | custom-call | flops 1073741824 | bytes 5767168 | tf_op jit(solution)/shard_map/project/pallas_call | solution.py:377
  249.8 0.8 collective-permute-start.34
  250.6 4.1 %attend.4.own_ref = bf16[256,512]{1,0:T(8,128)(2,1)} custom-call(bf16[3,512,512]{2,1,0:T(8,128)(2,1)} %qkv.2.q_ref.k1.k2.v1.v2.k0.v0, bf16[2,512,512]{2,1,0:T(8,128)(2,1)} %copy-done.2, bf16[3,512,512]{2,1,0:T(8,128)(2,1)} %qkv.2.q_ref.k1.k2.v1.v2.k0.v0, bf16[3,512,512]{2,1,0:T(8,128)(2,1)} %qkv.2.q_ref.k1.k2.v1.v2.k0.v0, bf16[2,512,512]{2,1,0:T(8,128)(2,1)} %copy-done.2, ...), custom_call_target="tpu_custom_call" | custom-call | flops 402653184 | bytes 2097152 | tf_op jit(solution)/shard_map/attend/pallas_call | solution.py:320
  254.7 3.3 %collective-permute-start.24 = (bf16[256,512]{1,0:T(8,128)(2,1)}, bf16[256,512]{1,0:T(8,128)(2,1)S(1)}, u32[]{:S(2)}, u32[]{:S(2)}) collective-permute-start(bf16[256,512]{1,0:T(8,128)(2,1)} %attend.4.own_ref), channel_id=1, source_target_pairs={{0,1},{1,0},{2,3},{3,2},{4,5},{5,4},{6,7},{7,6},{8,9},{9,8},{10,11... | collective-permute-start | bytes 786440 | tf_op jit(solution)/shard_map/ppermute | solution.py:114
  258.0 1.5 collective-permute-start.35
  260.2 6.8 %project.6 = (f32[256,512]{1,0:T(8,128)}, bf16[256,512]{1,0:T(8,128)(2,1)}, bf16[256,512]{1,0:T(8,128)(2,1)}) custom-call(s32[1]{0:T(128)} %bitcast.1.place_ref, s32[1]{0:T(128)} %bitcast.3.ring_ref, bf16[256,512]{1,0:T(8,128)(2,1)} %attend.6.own_ref, bf16[256,512]{1,0:T(8,128)(2,1)} %copy-done.24, bf16[256,2560]{1,0:T(8,128)(2,1)} %assemble.1.refs_0_, ...), custom_call_target="tpu_custom_call" | custom-call | flops 1073741824 | bytes 5767168 | tf_op jit(solution)/shard_map/project/pallas_call | solution.py:377
  267.7 1.3 collective-permute-start.32
  269.0 6.8 %project.5 = (f32[256,512]{1,0:T(8,128)}, bf16[256,512]{1,0:T(8,128)(2,1)}, bf16[256,512]{1,0:T(8,128)(2,1)}) custom-call(s32[1]{0:T(128)} %bitcast.1.place_ref, s32[1]{0:T(128)} %bitcast.3.ring_ref, bf16[256,512]{1,0:T(8,128)(2,1)} %attend.5.own_ref, bf16[256,512]{1,0:T(8,128)(2,1)} %copy-done.23, bf16[256,2560]{1,0:T(8,128)(2,1)} %assemble.1.refs_0_, ...), custom_call_target="tpu_custom_call" | custom-call | flops 1073741824 | bytes 5767168 | tf_op jit(solution)/shard_map/project/pallas_call | solution.py:377
  276.6 1.3 collective-permute-start.29
  277.9 6.8 %project.4 = (f32[256,512]{1,0:T(8,128)}, bf16[256,512]{1,0:T(8,128)(2,1)}, bf16[256,512]{1,0:T(8,128)(2,1)}) custom-call(s32[1]{0:T(128)} %bitcast.1.place_ref, s32[1]{0:T(128)} %bitcast.3.ring_ref, bf16[256,512]{1,0:T(8,128)(2,1)} %attend.4.own_ref, bf16[256,512]{1,0:T(8,128)(2,1)} %copy-done.20, bf16[256,2560]{1,0:T(8,128)(2,1)} %assemble.1.refs_0_, ...), custom_call_target="tpu_custom_call" | custom-call | flops 1073741824 | bytes 5767168 | tf_op jit(solution)/shard_map/project/pallas_call | solution.py:377
  285.4 1.3 collective-permute-start.26
  286.7 3.4 %final.4.rest_0_ = bf16[1024,4,512]{2,1,0:T(4,128)(2,1)} custom-call(f32[4,6]{1,0:T(4,128)} %static_ref.11, bf16[1024,4,512]{2,1,0:T(4,128)(2,1)} %x_ref.15, f32[8,2048]{1,0:T(8,128)} %get-tuple-element.86.first_ref, f32[8,2048]{1,0:T(8,128)} %get-tuple-element.87.own2_ref, f32[8,2048]{1,0:T(8,128)} %copy-done.13, f32[8,2048]{1,0:T(8,128)} %copy-done.12, ...), custom_call_target="tpu_custom_call" | custom-call | flops 629145600 | bytes 2883584 | tf_op jit(solution)/shard_map/final/pallas_call | solution.py:457
  290.2 0.7 copy-done.17
  290.9 3.4 %final.5.rest_0_ = bf16[1024,4,512]{2,1,0:T(4,128)(2,1)} custom-call(f32[4,6]{1,0:T(4,128)} %static_ref.11, bf16[1024,4,512]{2,1,0:T(4,128)(2,1)} %x_ref.15, f32[8,2048]{1,0:T(8,128)} %get-tuple-element.86.first_ref, f32[8,2048]{1,0:T(8,128)} %get-tuple-element.87.own2_ref, f32[8,2048]{1,0:T(8,128)} %copy-done.13, ...), custom_call_target="tpu_custom_call", output_to_operand_aliasing={{}: (10, {})} | custom-call | flops 629145600 | bytes 2883584 | tf_op jit(solution)/shard_map/final/pallas_call | solution.py:457
  294.4 4.3 %collective-permute-done.29.outer_ref = bf16[256,512]{1,0:T(8,128)(2,1)S(1)} collective-permute-done((bf16[256,512]{1,0:T(8,128)(2,1)}, bf16[256,512]{1,0:T(8,128)(2,1)S(1)}, u32[]{:S(2)}, u32[]{:S(2)}) %collective-permute-start.29) | collective-permute-done | bytes 262176 | tf_op jit(solution)/shard_map/ppermute | solution.py:549
  298.6 0.7 copy-done.19
  299.3 3.4 %final.6.rest_0_ = bf16[1024,4,512]{2,1,0:T(4,128)(2,1)} custom-call(f32[4,6]{1,0:T(4,128)} %static_ref.11, bf16[1024,4,512]{2,1,0:T(4,128)(2,1)} %x_ref.15, f32[8,2048]{1,0:T(8,128)} %get-tuple-element.58.first_ref, f32[8,2048]{1,0:T(8,128)} %get-tuple-element.65.own2_ref, f32[8,2048]{1,0:T(8,128)} %copy-done.10, ...), custom_call_target="tpu_custom_call", output_to_operand_aliasing={{}: (10, {})} | custom-call | flops 629145600 | bytes 2883584 | tf_op jit(solution)/shard_map/final/pallas_call | solution.py:457
  302.8 6.7 %collective-permute-done.26.outer_ref = bf16[256,512]{1,0:T(8,128)(2,1)S(1)} collective-permute-done((bf16[256,512]{1,0:T(8,128)(2,1)}, bf16[256,512]{1,0:T(8,128)(2,1)S(1)}, u32[]{:S(2)}, u32[]{:S(2)}) %collective-permute-start.26) | collective-permute-done | bytes 262176 | tf_op jit(solution)/shard_map/ppermute | solution.py:549
  309.5 0.7 copy-done.22
  310.2 3.4 %final.7 = bf16[1024,4,512]{2,1,0:T(4,128)(2,1)} custom-call(f32[4,6]{1,0:T(4,128)} %static_ref.11, bf16[1024,4,512]{2,1,0:T(4,128)(2,1)} %x_ref.15, f32[8,2048]{1,0:T(8,128)} %get-tuple-element.58.first_ref, f32[8,2048]{1,0:T(8,128)} %get-tuple-element.65.own2_ref, f32[8,2048]{1,0:T(8,128)} %copy-done.10, ...), custom_call_target="tpu_custom_call", output_to_operand_aliasing={{}: (10, {})} | custom-call | flops 629145600 | bytes 2883584 | tf_op jit(solution)/shard_map/final/pallas_call | solution.py:457
  (137 shorter events, 8.2 us)
Async XLA Ops:
  6.5 199.9 %all-gather.3.cloned.1.call-start = ((), (), s32[]{:S(2)}) async-start(), calls=%async_computation | async-start | bytes 2621440 | tf_op jit(solution)/shard_map/all_gather | solution.py:491
  12.4 15.3 %collective-permute-start.2 = (f32[8,2048]{1,0:T(8,128)}, f32[8,2048]{1,0:T(8,128)S(1)}, u32[]{:S(2)}, u32[]{:S(2)}) collective-permute-start(f32[8,2048]{1,0:T(8,128)} %get-tuple-element.51.own_ref), channel_id=1, source_target_pairs={{0,3},{1,0},{2,1},{3,2},{4,7},{5,4},{6,5},{7,6},{8,11},{9,8},{10,9... | collective-permute-start | bytes 196616 | tf_op jit(solution)/shard_map/ppermute | solution.py:30
  17.5 10.2 %collective-permute-start.1 = (f32[8,2048]{1,0:T(8,128)}, f32[8,2048]{1,0:T(8,128)S(1)}, u32[]{:S(2)}, u32[]{:S(2)}) collective-permute-start(f32[8,2048]{1,0:T(8,128)} %get-tuple-element.51.own_ref), channel_id=1, source_target_pairs={{0,2},{1,3},{2,0},{3,1},{4,6},{5,7},{6,4},{7,5},{8,10},{9,11},{10,... | collective-permute-start | bytes 196616 | tf_op jit(solution)/shard_map/ppermute | solution.py:30
  17.5 10.3 %collective-permute-start = (f32[8,2048]{1,0:T(8,128)}, f32[8,2048]{1,0:T(8,128)S(1)}, u32[]{:S(2)}, u32[]{:S(2)}) collective-permute-start(f32[8,2048]{1,0:T(8,128)} %get-tuple-element.51.own_ref), channel_id=1, source_target_pairs={{0,1},{1,2},{2,3},{3,0},{4,5},{5,6},{6,7},{7,4},{8,9},{9,10},{10,1... | collective-permute-start | bytes 196616 | tf_op jit(solution)/shard_map/ppermute | solution.py:30
  28.4 4.3 %copy-start.37 = (bf16[64,2560]{1,0:T(8,128)(2,1)S(1)}, bf16[64,2560]{1,0:T(8,128)(2,1)}, u32[]{:S(2)}) copy-start(bf16[64,2560]{1,0:T(8,128)(2,1)} %get-tuple-element.70) | copy-start | bytes 983044
  28.4 6.9 %copy-start.36 = (bf16[64,2560]{1,0:T(8,128)(2,1)S(1)}, bf16[64,2560]{1,0:T(8,128)(2,1)}, u32[]{:S(2)}) copy-start(bf16[64,2560]{1,0:T(8,128)(2,1)} %get-tuple-element.71) | copy-start | bytes 983044
  28.4 7.8 %copy-start.35 = (bf16[64,2560]{1,0:T(8,128)(2,1)S(1)}, bf16[64,2560]{1,0:T(8,128)(2,1)}, u32[]{:S(2)}) copy-start(bf16[64,2560]{1,0:T(8,128)(2,1)} %get-tuple-element.72) | copy-start | bytes 983044
  28.4 9.3 %copy-start.26 = (f32[8,2048]{1,0:T(8,128)S(1)}, f32[8,2048]{1,0:T(8,128)}, u32[]{:S(2)}) copy-start(f32[8,2048]{1,0:T(8,128)} %get-tuple-element.57.own_ref) | copy-start | bytes 196612
  32.6 186.5 %all-gather.5.cloned.1.call-start = ((), (), s32[]{:S(2)}) async-start(), calls=%async_computation.1 | async-start | bytes 2621440 | tf_op jit(solution)/shard_map/all_gather | solution.py:491
  32.7 76.3 %collective-permute-start.12 = (bf16[64,2560]{1,0:T(8,128)(2,1)S(1)}, bf16[64,2560]{1,0:T(8,128)(2,1)S(1)}, u32[]{:S(2)}, u32[]{:S(2)}) collective-permute-start(bf16[64,2560]{1,0:T(8,128)(2,1)S(1)} %copy-done.37), channel_id=1, source_target_pairs={{0,1},{1,2},{2,3},{3,0},{4,5},{5,6},{6,7},{7,4},{8,9},{9,10},{10,1... | collective-permute-start | bytes 983048 | tf_op jit(solution)/shard_map/ppermute | solution.py:486
  35.2 73.7 %collective-permute-start.13 = (bf16[64,2560]{1,0:T(8,128)(2,1)S(1)}, bf16[64,2560]{1,0:T(8,128)(2,1)S(1)}, u32[]{:S(2)}, u32[]{:S(2)}) collective-permute-start(bf16[64,2560]{1,0:T(8,128)(2,1)S(1)} %copy-done.36), channel_id=1, source_target_pairs={{0,2},{1,3},{2,0},{3,1},{4,6},{5,7},{6,4},{7,5},{8,10},{9,11},{10,... | collective-permute-start | bytes 983048 | tf_op jit(solution)/shard_map/ppermute | solution.py:486
  36.1 72.9 %collective-permute-start.14 = (bf16[64,2560]{1,0:T(8,128)(2,1)S(1)}, bf16[64,2560]{1,0:T(8,128)(2,1)S(1)}, u32[]{:S(2)}, u32[]{:S(2)}) collective-permute-start(bf16[64,2560]{1,0:T(8,128)(2,1)S(1)} %copy-done.35), channel_id=1, source_target_pairs={{0,3},{1,0},{2,1},{3,2},{4,7},{5,4},{6,5},{7,6},{8,11},{9,8},{10,9... | collective-permute-start | bytes 983048 | tf_op jit(solution)/shard_map/ppermute | solution.py:486
  37.7 37.1 %collective-permute-start.5 = (f32[8,2048]{1,0:T(8,128)S(1)}, f32[8,2048]{1,0:T(8,128)S(1)}, u32[]{:S(2)}, u32[]{:S(2)}) collective-permute-start(f32[8,2048]{1,0:T(8,128)S(1)} %copy-done.26), channel_id=1, source_target_pairs={{0,3},{1,0},{2,1},{3,2},{4,7},{5,4},{6,5},{7,6},{8,11},{9,8},{10,9... | collective-permute-start | bytes 196616 | tf_op jit(solution)/shard_map/ppermute | solution.py:30
  39.6 63.9 %collective-permute-start.4 = (f32[8,2048]{1,0:T(8,128)S(1)}, f32[8,2048]{1,0:T(8,128)S(1)}, u32[]{:S(2)}, u32[]{:S(2)}) collective-permute-start(f32[8,2048]{1,0:T(8,128)S(1)} %copy-done.26), channel_id=1, source_target_pairs={{0,2},{1,3},{2,0},{3,1},{4,6},{5,7},{6,4},{7,5},{8,10},{9,11},{10,... | collective-permute-start | bytes 196616 | tf_op jit(solution)/shard_map/ppermute | solution.py:30
  74.7 28.8 %copy-start.30 = (f32[8,2048]{1,0:T(8,128)}, f32[8,2048]{1,0:T(8,128)S(1)}, u32[]{:S(2)}) copy-start(f32[8,2048]{1,0:T(8,128)S(1)} %collective-permute-done.5.c_ref) | copy-start | bytes 196612
  74.7 28.8 %collective-permute-start.3 = (f32[8,2048]{1,0:T(8,128)S(1)}, f32[8,2048]{1,0:T(8,128)S(1)}, u32[]{:S(2)}, u32[]{:S(2)}) collective-permute-start(f32[8,2048]{1,0:T(8,128)S(1)} %copy-done.26), channel_id=1, source_target_pairs={{0,1},{1,2},{2,3},{3,0},{4,5},{5,6},{6,7},{7,4},{8,9},{9,10},{10,1... | collective-permute-start | bytes 196616 | tf_op jit(solution)/shard_map/ppermute | solution.py:30
  108.9 7.0 %copy-start.34 = (s32[2]{0:T(128)S(1)}, s32[2]{0:T(128)}, u32[]{:S(2)}) copy-start(s32[2]{0:T(128)} %param.11) | copy-start | bytes 28
  108.9 8.3 %copy-start.33 = (s32[1024]{0:T(1024)S(1)}, s32[1024]{0:T(1024)}, u32[]{:S(2)}) copy-start(s32[1024]{0:T(1024)} %param.10) | copy-start | bytes 12292
  108.9 64.5 %copy-start.6 = (f32[8,2048]{1,0:T(8,128)S(1)}, f32[8,2048]{1,0:T(8,128)}, u32[]{:S(2)}) copy-start(f32[8,2048]{1,0:T(8,128)} %get-tuple-element.65.own2_ref) | copy-start | bytes 196612
  108.9 80.8 %copy-start.7 = (f32[8,2048]{1,0:T(8,128)S(1)}, f32[8,2048]{1,0:T(8,128)}, u32[]{:S(2)}) copy-start(f32[8,2048]{1,0:T(8,128)} %get-tuple-element.87.own2_ref) | copy-start | bytes 196612
  112.4 32.8 %collective-permute-start.21 = (bf16[256,2560]{1,0:T(8,128)(2,1)}, bf16[256,2560]{1,0:T(8,128)(2,1)S(1)}, u32[]{:S(2)}, u32[]{:S(2)}) collective-permute-start(bf16[256,2560]{1,0:T(8,128)(2,1)} %assemble.1.refs_0_), channel_id=1, source_target_pairs={{0,24},{4,28},{8,16},{12,20},{16,8},{20,12},{24,0},{28,4},{1,25},{... | collective-permute-start | bytes 3932168 | tf_op jit(solution)/shard_map/ppermute | solution.py:114
  114.9 57.4 %collective-permute-start.19 = (bf16[256,2560]{1,0:T(8,128)(2,1)}, bf16[256,2560]{1,0:T(8,128)(2,1)S(1)}, u32[]{:S(2)}, u32[]{:S(2)}) collective-permute-start(bf16[256,2560]{1,0:T(8,128)(2,1)} %assemble.1.refs_0_), channel_id=1, source_target_pairs={{0,16},{4,20},{8,24},{12,28},{16,0},{20,4},{24,8},{28,12},{1,17},{... | collective-permute-start | bytes 3932168 | tf_op jit(solution)/shard_map/ppermute | solution.py:114
  115.4 57.1 %collective-permute-start.17 = (bf16[256,2560]{1,0:T(8,128)(2,1)}, bf16[256,2560]{1,0:T(8,128)(2,1)}, u32[]{:S(2)}, u32[]{:S(2)}) collective-permute-start(bf16[256,2560]{1,0:T(8,128)(2,1)} %assemble.1.refs_0_), channel_id=1, source_target_pairs={{0,8},{4,12},{8,0},{12,4},{16,24},{20,28},{24,16},{28,20},{1,9},{5... | collective-permute-start | bytes 3932168 | tf_op jit(solution)/shard_map/ppermute | solution.py:114
  117.2 56.2 %collective-permute-start.15 = (s32[512]{0:T(512)S(1)}, s32[512]{0:T(512)S(1)}, u32[]{:S(2)}, u32[]{:S(2)}) collective-permute-start(s32[512]{0:T(512)S(1)} %get-tuple-element.106), channel_id=1, source_target_pairs={{0,4},{4,8},{8,12},{12,16},{16,20},{20,24},{24,28},{1,5},{5,9},{9,... | collective-permute-start | bytes 6152 | tf_op jit(solution)/shard_map/ppermute | solution.py:24
  118.5 87.9 %collective-permute-start.16 = (bf16[256,2560]{1,0:T(8,128)(2,1)}, bf16[256,2560]{1,0:T(8,128)(2,1)}, u32[]{:S(2)}, u32[]{:S(2)}) collective-permute-start(bf16[256,2560]{1,0:T(8,128)(2,1)} %assemble.1.refs_0_), channel_id=1, source_target_pairs={{0,4},{4,0},{8,12},{12,8},{16,20},{20,16},{24,28},{28,24},{1,5},{5... | collective-permute-start | bytes 3932168 | tf_op jit(solution)/shard_map/ppermute | solution.py:114
  145.2 56.5 %copy-start = (bf16[256,2560]{1,0:T(8,128)(2,1)}, bf16[256,2560]{1,0:T(8,128)(2,1)S(1)}, u32[]{:S(2)}) copy-start(bf16[256,2560]{1,0:T(8,128)(2,1)S(1)} %collective-permute-done.21.refs_6_) | copy-start | bytes 3932164
  145.2 61.2 %collective-permute-start.22 = (bf16[256,2560]{1,0:T(8,128)(2,1)S(1)}, bf16[256,2560]{1,0:T(8,128)(2,1)}, u32[]{:S(2)}, u32[]{:S(2)}) collective-permute-start(bf16[256,2560]{1,0:T(8,128)(2,1)S(1)} %collective-permute-done.21.refs_6_), channel_id=1, source_target_pairs={{0,4},{4,0},{8,12},{12,8},{16,20},{20,16},{24,28},{28,24},{1,5},{5... | collective-permute-start | bytes 3932168 | tf_op jit(solution)/shard_map/ppermute | solution.py:114
  172.3 29.5 %copy-start.1 = (bf16[256,2560]{1,0:T(8,128)(2,1)}, bf16[256,2560]{1,0:T(8,128)(2,1)S(1)}, u32[]{:S(2)}) copy-start(bf16[256,2560]{1,0:T(8,128)(2,1)S(1)} %collective-permute-done.19.refs_4_) | copy-start | bytes 3932164
  172.3 34.2 %collective-permute-start.20 = (bf16[256,2560]{1,0:T(8,128)(2,1)S(1)}, bf16[256,2560]{1,0:T(8,128)(2,1)}, u32[]{:S(2)}, u32[]{:S(2)}) collective-permute-start(bf16[256,2560]{1,0:T(8,128)(2,1)S(1)} %collective-permute-done.19.refs_4_), channel_id=1, source_target_pairs={{0,4},{4,0},{8,12},{12,8},{16,20},{20,16},{24,28},{28,24},{1,5},{5... | collective-permute-start | bytes 3932168 | tf_op jit(solution)/shard_map/ppermute | solution.py:114
  172.5 34.0 %collective-permute-start.18 = (bf16[256,2560]{1,0:T(8,128)(2,1)}, bf16[256,2560]{1,0:T(8,128)(2,1)}, u32[]{:S(2)}, u32[]{:S(2)}) collective-permute-start(bf16[256,2560]{1,0:T(8,128)(2,1)} %collective-permute-done.17.refs_2_), channel_id=1, source_target_pairs={{0,4},{4,0},{8,12},{12,8},{16,20},{20,16},{24,28},{28,24},{1,5},{5... | collective-permute-start | bytes 3932168 | tf_op jit(solution)/shard_map/ppermute | solution.py:114
  173.4 4.3 %collective-permute-start.11 = (f32[8,2048]{1,0:T(8,128)S(1)}, f32[8,2048]{1,0:T(8,128)S(1)}, u32[]{:S(2)}, u32[]{:S(2)}) collective-permute-start(f32[8,2048]{1,0:T(8,128)S(1)} %copy-done.6), channel_id=1, source_target_pairs={{0,3},{1,0},{2,1},{3,2},{4,7},{5,4},{6,5},{7,6},{8,11},{9,8},{10,9... | collective-permute-start | bytes 196616 | tf_op jit(solution)/shard_map/ppermute | solution.py:30
  177.8 24.0 %copy-start.8 = (f32[8,2048]{1,0:T(8,128)}, f32[8,2048]{1,0:T(8,128)S(1)}, u32[]{:S(2)}) copy-start(f32[8,2048]{1,0:T(8,128)S(1)} %collective-permute-done.11.c_ref) | copy-start | bytes 196612
  177.8 5.6 %collective-permute-start.10 = (f32[8,2048]{1,0:T(8,128)S(1)}, f32[8,2048]{1,0:T(8,128)S(1)}, u32[]{:S(2)}, u32[]{:S(2)}) collective-permute-start(f32[8,2048]{1,0:T(8,128)S(1)} %copy-done.6), channel_id=1, source_target_pairs={{0,2},{1,3},{2,0},{3,1},{4,6},{5,7},{6,4},{7,5},{8,10},{9,11},{10,... | collective-permute-start | bytes 196616 | tf_op jit(solution)/shard_map/ppermute | solution.py:30
  183.4 18.4 %copy-start.9 = (f32[8,2048]{1,0:T(8,128)}, f32[8,2048]{1,0:T(8,128)S(1)}, u32[]{:S(2)}) copy-start(f32[8,2048]{1,0:T(8,128)S(1)} %collective-permute-done.10.b_ref) | copy-start | bytes 196612
  183.4 6.3 %collective-permute-start.9 = (f32[8,2048]{1,0:T(8,128)S(1)}, f32[8,2048]{1,0:T(8,128)S(1)}, u32[]{:S(2)}, u32[]{:S(2)}) collective-permute-start(f32[8,2048]{1,0:T(8,128)S(1)} %copy-done.6), channel_id=1, source_target_pairs={{0,1},{1,2},{2,3},{3,0},{4,5},{5,6},{6,7},{7,4},{8,9},{9,10},{10,1... | collective-permute-start | bytes 196616 | tf_op jit(solution)/shard_map/ppermute | solution.py:30
  189.7 12.1 %copy-start.10 = (f32[8,2048]{1,0:T(8,128)}, f32[8,2048]{1,0:T(8,128)S(1)}, u32[]{:S(2)}) copy-start(f32[8,2048]{1,0:T(8,128)S(1)} %collective-permute-done.9.a_ref) | copy-start | bytes 196612
  189.7 5.0 %collective-permute-start.8 = (f32[8,2048]{1,0:T(8,128)S(1)}, f32[8,2048]{1,0:T(8,128)S(1)}, u32[]{:S(2)}, u32[]{:S(2)}) collective-permute-start(f32[8,2048]{1,0:T(8,128)S(1)} %copy-done.7), channel_id=1, source_target_pairs={{0,3},{1,0},{2,1},{3,2},{4,7},{5,4},{6,5},{7,6},{8,11},{9,8},{10,9... | collective-permute-start | bytes 196616 | tf_op jit(solution)/shard_map/ppermute | solution.py:30
  194.7 7.1 %copy-start.11 = (f32[8,2048]{1,0:T(8,128)}, f32[8,2048]{1,0:T(8,128)S(1)}, u32[]{:S(2)}) copy-start(f32[8,2048]{1,0:T(8,128)S(1)} %collective-permute-done.8.c_ref) | copy-start | bytes 196612
  194.7 5.7 %collective-permute-start.7 = (f32[8,2048]{1,0:T(8,128)S(1)}, f32[8,2048]{1,0:T(8,128)S(1)}, u32[]{:S(2)}, u32[]{:S(2)}) collective-permute-start(f32[8,2048]{1,0:T(8,128)S(1)} %copy-done.7), channel_id=1, source_target_pairs={{0,2},{1,3},{2,0},{3,1},{4,6},{5,7},{6,4},{7,5},{8,10},{9,11},{10,... | collective-permute-start | bytes 196616 | tf_op jit(solution)/shard_map/ppermute | solution.py:30
  200.4 14.2 %copy-start.12 = (f32[8,2048]{1,0:T(8,128)}, f32[8,2048]{1,0:T(8,128)S(1)}, u32[]{:S(2)}) copy-start(f32[8,2048]{1,0:T(8,128)S(1)} %collective-permute-done.7.b_ref) | copy-start | bytes 196612
  200.4 6.1 %collective-permute-start.6 = (f32[8,2048]{1,0:T(8,128)S(1)}, f32[8,2048]{1,0:T(8,128)S(1)}, u32[]{:S(2)}, u32[]{:S(2)}) collective-permute-start(f32[8,2048]{1,0:T(8,128)S(1)} %copy-done.7), channel_id=1, source_target_pairs={{0,1},{1,2},{2,3},{3,0},{4,5},{5,6},{6,7},{7,4},{8,9},{9,10},{10,1... | collective-permute-start | bytes 196616 | tf_op jit(solution)/shard_map/ppermute | solution.py:30
  206.4 8.1 %copy-start.13 = (f32[8,2048]{1,0:T(8,128)}, f32[8,2048]{1,0:T(8,128)S(1)}, u32[]{:S(2)}) copy-start(f32[8,2048]{1,0:T(8,128)S(1)} %collective-permute-done.6.a_ref) | copy-start | bytes 196612
  215.8 21.5 %collective-permute-start.23 = (bf16[2,512,512]{2,1,0:T(8,128)(2,1)S(1)}, bf16[2,512,512]{2,1,0:T(8,128)(2,1)S(1)}, u32[]{:S(2)}, u32[]{:S(2)}) collective-permute-start(bf16[2,512,512]{2,1,0:T(8,128)(2,1)S(1)} %slice.38), channel_id=1, source_target_pairs={{0,4},{4,8},{8,12},{12,16},{16,20},{20,24},{24,28},{1,5},{5,9},{9,... | collective-permute-start | bytes 3145736 | tf_op jit(solution)/shard_map/ppermute | solution.py:24
  231.2 11.1 %collective-permute-start.33 = (bf16[256,512]{1,0:T(8,128)(2,1)}, bf16[256,512]{1,0:T(8,128)(2,1)S(1)}, u32[]{:S(2)}, u32[]{:S(2)}) collective-permute-start(bf16[256,512]{1,0:T(8,128)(2,1)} %attend.7.own_ref), channel_id=1, source_target_pairs={{0,1},{1,0},{2,3},{3,2},{4,5},{5,4},{6,7},{7,6},{8,9},{9,8},{10,11... | collective-permute-start | bytes 786440 | tf_op jit(solution)/shard_map/ppermute | solution.py:114
  235.3 24.2 %collective-permute-start.30 = (bf16[256,512]{1,0:T(8,128)(2,1)}, bf16[256,512]{1,0:T(8,128)(2,1)S(1)}, u32[]{:S(2)}, u32[]{:S(2)}) collective-permute-start(bf16[256,512]{1,0:T(8,128)(2,1)} %attend.6.own_ref), channel_id=1, source_target_pairs={{0,1},{1,0},{2,3},{3,2},{4,5},{5,4},{6,7},{7,6},{8,9},{9,8},{10,11... | collective-permute-start | bytes 786440 | tf_op jit(solution)/shard_map/ppermute | solution.py:114
  237.3 1.0 copy-start.2
  242.3 25.4 %collective-permute-start.27 = (bf16[256,512]{1,0:T(8,128)(2,1)}, bf16[256,512]{1,0:T(8,128)(2,1)S(1)}, u32[]{:S(2)}, u32[]{:S(2)}) collective-permute-start(bf16[256,512]{1,0:T(8,128)(2,1)} %attend.5.own_ref), channel_id=1, source_target_pairs={{0,1},{1,0},{2,3},{3,2},{4,5},{5,4},{6,7},{7,6},{8,9},{9,8},{10,11... | collective-permute-start | bytes 786440 | tf_op jit(solution)/shard_map/ppermute | solution.py:114
  249.8 8.1 %copy-start.38 = (bf16[256,512]{1,0:T(8,128)(2,1)S(1)}, bf16[256,512]{1,0:T(8,128)(2,1)}, u32[]{:S(2)}) copy-start(bf16[256,512]{1,0:T(8,128)(2,1)} %get-tuple-element.96) | copy-start | bytes 786436
  249.8 26.0 %collective-permute-start.34 = (bf16[256,512]{1,0:T(8,128)(2,1)}, bf16[256,512]{1,0:T(8,128)(2,1)S(1)}, u32[]{:S(2)}, u32[]{:S(2)}) collective-permute-start(bf16[256,512]{1,0:T(8,128)(2,1)} %get-tuple-element.95), channel_id=1, source_target_pairs={{1,2},{2,1},{5,6},{6,5},{9,10},{10,9},{13,14},{14,13},{17,18},{18,... | collective-permute-start | bytes 786440 | tf_op jit(solution)/shard_map/ppermute | solution.py:548
  254.7 21.8 %collective-permute-start.24 = (bf16[256,512]{1,0:T(8,128)(2,1)}, bf16[256,512]{1,0:T(8,128)(2,1)S(1)}, u32[]{:S(2)}, u32[]{:S(2)}) collective-permute-start(bf16[256,512]{1,0:T(8,128)(2,1)} %attend.4.own_ref), channel_id=1, source_target_pairs={{0,1},{1,0},{2,3},{3,2},{4,5},{5,4},{6,7},{7,6},{8,9},{9,8},{10,11... | collective-permute-start | bytes 786440 | tf_op jit(solution)/shard_map/ppermute | solution.py:114
  258.0 26.8 %collective-permute-start.35 = (bf16[256,512]{1,0:T(8,128)(2,1)S(1)}, bf16[256,512]{1,0:T(8,128)(2,1)S(1)}, u32[]{:S(2)}, u32[]{:S(2)}) collective-permute-start(bf16[256,512]{1,0:T(8,128)(2,1)S(1)} %copy-done.38), channel_id=1, source_target_pairs={{1,3},{2,0},{5,7},{6,4},{9,11},{10,8},{13,15},{14,12},{17,19},{18,... | collective-permute-start | bytes 786440 | tf_op jit(solution)/shard_map/ppermute | solution.py:549
  267.0 18.4 %collective-permute-start.31 = (bf16[256,512]{1,0:T(8,128)(2,1)}, bf16[256,512]{1,0:T(8,128)(2,1)S(1)}, u32[]{:S(2)}, u32[]{:S(2)}) collective-permute-start(bf16[256,512]{1,0:T(8,128)(2,1)} %get-tuple-element.92), channel_id=1, source_target_pairs={{1,2},{2,1},{5,6},{6,5},{9,10},{10,9},{13,14},{14,13},{17,18},{18,... | collective-permute-start | bytes 786440 | tf_op jit(solution)/shard_map/ppermute | solution.py:548
  267.7 1.3 copy-start.23
  267.7 22.5 %collective-permute-start.32 = (bf16[256,512]{1,0:T(8,128)(2,1)}, bf16[256,512]{1,0:T(8,128)(2,1)S(1)}, u32[]{:S(2)}, u32[]{:S(2)}) collective-permute-start(bf16[256,512]{1,0:T(8,128)(2,1)} %get-tuple-element.93), channel_id=1, source_target_pairs={{1,3},{2,0},{5,7},{6,4},{9,11},{10,8},{13,15},{14,12},{17,19},{18,... | collective-permute-start | bytes 786440 | tf_op jit(solution)/shard_map/ppermute | solution.py:549
  275.8 8.9 %copy-start.14 = (bf16[256,512]{1,0:T(8,128)(2,1)}, bf16[256,512]{1,0:T(8,128)(2,1)S(1)}, u32[]{:S(2)}) copy-start(bf16[256,512]{1,0:T(8,128)(2,1)S(1)} %collective-permute-done.34.inner_ref) | copy-start | bytes 786436
  275.9 18.5 %collective-permute-start.28 = (bf16[256,512]{1,0:T(8,128)(2,1)}, bf16[256,512]{1,0:T(8,128)(2,1)S(1)}, u32[]{:S(2)}, u32[]{:S(2)}) collective-permute-start(bf16[256,512]{1,0:T(8,128)(2,1)} %get-tuple-element.84), channel_id=1, source_target_pairs={{1,2},{2,1},{5,6},{6,5},{9,10},{10,9},{13,14},{14,13},{17,18},{18,... | collective-permute-start | bytes 786440 | tf_op jit(solution)/shard_map/ppermute | solution.py:548
  276.6 1.3 copy-start.20
  276.6 22.1 %collective-permute-start.29 = (bf16[256,512]{1,0:T(8,128)(2,1)}, bf16[256,512]{1,0:T(8,128)(2,1)S(1)}, u32[]{:S(2)}, u32[]{:S(2)}) collective-permute-start(bf16[256,512]{1,0:T(8,128)(2,1)} %get-tuple-element.85), channel_id=1, source_target_pairs={{1,3},{2,0},{5,7},{6,4},{9,11},{10,8},{13,15},{14,12},{17,19},{18,... | collective-permute-start | bytes 786440 | tf_op jit(solution)/shard_map/ppermute | solution.py:549
  284.7 2.0 copy-start.15
  284.7 18.0 %collective-permute-start.25 = (bf16[256,512]{1,0:T(8,128)(2,1)}, bf16[256,512]{1,0:T(8,128)(2,1)S(1)}, u32[]{:S(2)}, u32[]{:S(2)}) collective-permute-start(bf16[256,512]{1,0:T(8,128)(2,1)} %get-tuple-element.81), channel_id=1, source_target_pairs={{1,2},{2,1},{5,6},{6,5},{9,10},{10,9},{13,14},{14,13},{17,18},{18,... | collective-permute-start | bytes 786440 | tf_op jit(solution)/shard_map/ppermute | solution.py:548
  285.4 4.8 %copy-start.16 = (bf16[256,512]{1,0:T(8,128)(2,1)}, bf16[256,512]{1,0:T(8,128)(2,1)S(1)}, u32[]{:S(2)}) copy-start(bf16[256,512]{1,0:T(8,128)(2,1)S(1)} %collective-permute-done.31.inner_ref) | copy-start | bytes 786436
  285.4 24.0 %collective-permute-start.26 = (bf16[256,512]{1,0:T(8,128)(2,1)}, bf16[256,512]{1,0:T(8,128)(2,1)S(1)}, u32[]{:S(2)}, u32[]{:S(2)}) collective-permute-start(bf16[256,512]{1,0:T(8,128)(2,1)} %get-tuple-element.82), channel_id=1, source_target_pairs={{1,3},{2,0},{5,7},{6,4},{9,11},{10,8},{13,15},{14,12},{17,19},{18,... | collective-permute-start | bytes 786440 | tf_op jit(solution)/shard_map/ppermute | solution.py:549
  294.4 4.3 %copy-start.18 = (bf16[256,512]{1,0:T(8,128)(2,1)}, bf16[256,512]{1,0:T(8,128)(2,1)S(1)}, u32[]{:S(2)}) copy-start(bf16[256,512]{1,0:T(8,128)(2,1)S(1)} %collective-permute-done.28.inner_ref) | copy-start | bytes 786436
  302.7 6.7 %copy-start.21 = (bf16[256,512]{1,0:T(8,128)(2,1)}, bf16[256,512]{1,0:T(8,128)(2,1)S(1)}, u32[]{:S(2)}) copy-start(bf16[256,512]{1,0:T(8,128)(2,1)S(1)} %collective-permute-done.25.inner_ref) | copy-start | bytes 786436
  (13 other events, 9.2 us)
Sparse Core Ops, SparseCore 0:
  32.8 71.1 all-gather.2
  116.1 44.9 all-gather.4

commit v4 on v2

--- a/solution.py
+++ b/solution.py
@@ -12,6 +12,7 @@
 BLOCK = 512
 CHUNK = 256
 SUB = 64
+STEP = 128
 STREAMS = 4
 EPS = 1e-05
 BF = jnp.bfloat16
@@ -61,29 +62,31 @@
 
 
 def regroup_kernel(place_ref, master_ref, *parts):
-    servers = len(parts)
+    servers = len(parts) // 2
     width = master_ref.shape[-1] // servers
-    for step, part_ref in enumerate(parts):
+    for step in range(servers):
         server = (place_ref[0] + step) % servers
         own = pl.ds(pl.multiple_of(server * width, width), width)
         pair = pl.ds(pl.multiple_of((server // 2) * 2 * width, 2 * width), 2 * width)
         for slot in range(3):
-            part_ref[:, slot * width : (slot + 1) * width] = master_ref[:, slot, own].astype(BF)
-        part_ref[:, 3 * width :] = master_ref[:, 3, pair].astype(BF)
+            parts[step][:, slot * width : (slot + 1) * width] = master_ref[:, slot, own].astype(BF)
+        parts[servers + step][...] = master_ref[:, 3, pair].astype(BF)
 
 
 def regroup(place, master, servers):
     rows, _, total = master.shape
-    columns = 5 * total // servers
-    return pl.pallas_call(
+    width = total // servers
+    parts = pl.pallas_call(
         regroup_kernel,
         in_specs=[pl.BlockSpec(memory_space=pltpu.SMEM), pl.BlockSpec(memory_space=pltpu.VMEM)],
-        out_specs=[pl.BlockSpec(memory_space=pltpu.VMEM)] * servers,
-        out_shape=[jax.ShapeDtypeStruct((rows, columns), BF)] * servers,
+        out_specs=[pl.BlockSpec(memory_space=pltpu.VMEM)] * (2 * servers),
+        out_shape=[jax.ShapeDtypeStruct((rows, 3 * width), BF)] * servers
+        + [jax.ShapeDtypeStruct((rows, 2 * width), BF)] * servers,
         cost_estimate=cost(0, rows * total * 26),
         compiler_params=params(),
         name="regroup",
     )(place, master)
+    return list(parts[:servers]), list(parts[servers:])
 
 
 def assemble_kernel(place_ref, *refs):
@@ -126,43 +129,56 @@
     return [pieces[mask] for mask in range(count)]
 
 
-def stats_kernel(x_ref, proj_ref, first_ref, second_ref):
-    tokens, _, width = x_ref.shape
+def stats_kernel(x_ref, proj_ref, out_ref):
+    block, _, width = x_ref.shape
+    tokens = block * pl.num_programs(0)
+    base = pl.program_id(0) * (block // STEP)
     proj = proj_ref[...]
     pieces = jnp.concatenate(split(proj, 3), axis=0)
-    column = jnp.sum(proj, axis=1, keepdims=True)
+    out_ref[:, out_ref.shape[1] - 128 :] = jnp.broadcast_to(jnp.sum(proj, axis=1, keepdims=True), (8, 128))
     row, col = iotas(4 * SUB, 4 * SUB)
     same = (row >> 2) == (col >> 2)
     ring = jnp.where(same, (row - col) & 3, -1)
-    for at in range(tokens // SUB):
-        lanes = slice(at * 4 * SUB, (at + 1) * 4 * SUB)
-        v = x_ref[at * SUB : (at + 1) * SUB].reshape(4 * SUB, width)
-        sums = contract(pieces, v, 1, 1)
-        sums = sums[0:8] + sums[8:16] + sums[16:24]
-        gram = contract(v, v, 1, 1)
-        first_ref[0:1, lanes] = sums[0:1]
-        first_ref[1:2, lanes] = sums[6:7]
-        for shift in range(3):
-            first_ref[2 + shift : 3 + shift, lanes] = jnp.sum(
-                jnp.where(ring == shift, gram, 0.0), axis=0, keepdims=True
-            )
-        first_ref[5:6, lanes] = jnp.broadcast_to(column[0:1], (1, 4 * SUB))
-        first_ref[6:8, lanes] = sums[1:3]
-        second_ref[0:3, lanes] = sums[3:6]
-        second_ref[3:8, lanes] = jnp.broadcast_to(column[1:6], (5, 4 * SUB))
-
-
-def stats(x, proj, start, tokens, step=128):
-    width = x.shape[-1]
+
+    @pl.loop(0, block // STEP)
+    def _(local):
+        step = base + local
+        folded = []
+        for half in range(STEP // SUB):
+            lanes = pl.ds(pl.multiple_of(step * 4 * STEP, 4 * STEP) + half * 4 * SUB, 4 * SUB)
+            v = x_ref[pl.ds(local * STEP + half * SUB, SUB)].reshape(4 * SUB, width)
+            sums = contract(pieces, v, 1, 1)
+            sums = sums[0:8] + sums[8:16] + sums[16:24]
+            gram = contract(v, v, 1, 1)
+            out_ref[0:1, lanes] = sums[0:1]
+            out_ref[1:2, lanes] = sums[6:7]
+            for shift in range(3):
+                out_ref[2 + shift : 3 + shift, lanes] = jnp.sum(
+                    jnp.where(ring == shift, gram, 0.0), axis=0, keepdims=True
+                )
+            out_ref[5:8, lanes] = sums[1:4]
+            folded.append(sums[4:6])
+        folded = jnp.concatenate(folded, axis=1)
+        lanes = pl.ds(pl.multiple_of(4 * tokens + step * STEP, STEP), STEP)
+        for part in range(4):
+            for which in range(2):
+                out_ref[4 * which + part : 4 * which + part + 1, lanes] = folded[
+                    which : which + 1, part * STEP : (part + 1) * STEP
+                ]
+
+
+def stats(x, proj):
+    tokens, _, width = x.shape
+    lanes = 5 * tokens + 128
     return pl.pallas_call(
         stats_kernel,
-        grid=(tokens // step,),
+        grid=(tokens // (2 * STEP),),
         in_specs=[
-            pl.BlockSpec((step, 4, width), lambda i: (start // step + i, 0, 0)),
+            pl.BlockSpec((2 * STEP, 4, width), lambda i: (i, 0, 0)),
             pl.BlockSpec((8, width), lambda i: (0, 0)),
         ],
-        out_specs=[pl.BlockSpec((8, 4 * step), lambda i: (0, i))] * 2,
-        out_shape=[jax.ShapeDtypeStruct((8, 4 * tokens), F32)] * 2,
+        out_specs=pl.BlockSpec((8, lanes), lambda i: (0, 0)),
+        out_shape=jax.ShapeDtypeStruct((8, lanes), F32),
         cost_estimate=cost(tokens * 4 * width * 600, tokens * 8 * width),
         compiler_params=params(),
         name="stats",
@@ -182,51 +198,55 @@
     return mean, lax.rsqrt(spread + EPS)
 
 
-def mix_kernel(static_ref, x_ref, own_ref, a_ref, b_ref, c_ref, sums_ref, normed_ref):
+def mix_kernel(offset, static_ref, x_ref, own_ref, a_ref, b_ref, c_ref, sums_ref, normed_ref):
     tokens, _, width = x_ref.shape
-    lanes_total = 4 * tokens
-    first = (own_ref[...] + a_ref[...]) + (b_ref[...] + c_ref[...])
-    sums_ref[...] = first
-    mean, inverse = centre(first)
-    stream = lax.broadcasted_iota(jnp.int32, (1, lanes_total), 1) & 3
-    mix = by_stream(static_ref, 0, stream) + jnp.tanh(
-        inverse * (first[0:1] - mean * first[5:6])
-    )
-    one = jnp.where(stream < 3, pltpu.roll(mix, lanes_total - 1, 1), pltpu.roll(mix, 3, 1))
-    two = jnp.where(stream < 2, pltpu.roll(mix, lanes_total - 2, 1), pltpu.roll(mix, 2, 1))
-    linear = mix * first[1:2]
-    square = mix * (mix * first[2:3] + 2.0 * one * first[3:4] + two * first[4:5])
+    sums_ref[...] = (own_ref[...] + a_ref[...]) + (b_ref[...] + c_ref[...])
+    last = sums_ref.shape[1] - 128
+    column = sums_ref[0:1, last : last + 1]
+    stream = lax.broadcasted_iota(jnp.int32, (1, 4 * STEP), 1) & 3
+    static = by_stream(static_ref, 0, stream)
     row, col = iotas(SUB, 4 * SUB)
     mine = row == (col >> 2)
-    for at in range(tokens // SUB):
-        lanes = slice(at * 4 * SUB, (at + 1) * 4 * SUB)
-        v = x_ref[at * SUB : (at + 1) * SUB].reshape(4 * SUB, width)
-        matrix = jnp.where(mine, mix[:, lanes], 0.0)
-        mixed = contract(jnp.concatenate(split(matrix, 3), axis=0), v, 1, 0)
-        mixed = mixed[0:SUB] + mixed[SUB : 2 * SUB] + mixed[2 * SUB : 3 * SUB]
-        average = jnp.sum(jnp.where(mine, linear[:, lanes], 0.0), axis=1, keepdims=True) * (1.0 / D)
-        power = jnp.sum(jnp.where(mine, square[:, lanes], 0.0), axis=1, keepdims=True) * (1.0 / D)
-        scale = lax.rsqrt(jnp.maximum(power - average * average, 0.0) + EPS)
-        normed_ref[at * SUB : (at + 1) * SUB, :] = ((mixed - average) * scale).astype(BF)
-
-
-def mix(static, x, parts, start, tokens, offset, step=128):
+
+    @pl.loop(0, tokens // STEP)
+    def _(step):
+        at = pl.multiple_of(4 * offset + step * 4 * STEP, 4 * STEP)
+        first = sums_ref[:, pl.ds(at, 4 * STEP)]
+        mean, inverse = centre(first)
+        mix = static + jnp.tanh(inverse * (first[0:1] - mean * column))
+        one = jnp.where(stream < 3, pltpu.roll(mix, 4 * STEP - 1, 1), pltpu.roll(mix, 3, 1))
+        two = jnp.where(stream < 2, pltpu.roll(mix, 4 * STEP - 2, 1), pltpu.roll(mix, 2, 1))
+        linear = mix * first[1:2]
+        square = mix * (mix * first[2:3] + 2.0 * one * first[3:4] + two * first[4:5])
+        for half in range(STEP // SUB):
+            lanes = slice(half * 4 * SUB, (half + 1) * 4 * SUB)
+            rows = pl.ds(step * STEP + half * SUB, SUB)
+            v = x_ref[rows].reshape(4 * SUB, width)
+            matrix = jnp.where(mine, mix[:, lanes], 0.0)
+            mixed = contract(jnp.concatenate(split(matrix, 3), axis=0), v, 1, 0)
+            mixed = mixed[0:SUB] + mixed[SUB : 2 * SUB] + mixed[2 * SUB : 3 * SUB]
+            average = jnp.sum(jnp.where(mine, linear[:, lanes], 0.0), axis=1, keepdims=True)
+            power = jnp.sum(jnp.where(mine, square[:, lanes], 0.0), axis=1, keepdims=True)
+            average, power = average * (1.0 / D), power * (1.0 / D)
+            scale = lax.rsqrt(jnp.maximum(power - average * average, 0.0) + EPS)
+            normed_ref[rows, :] = ((mixed - average) * scale).astype(BF)
+
+
+def mix(static, x, parts, start, tokens):
     width = x.shape[-1]
-    lane_block = pl.BlockSpec((8, 4 * step), lambda i: (0, offset // step + i))
-    return pl.pallas_call(
-        mix_kernel,
-        grid=(tokens // step,),
+    lanes = parts[0].shape[1]
+    whole = pl.BlockSpec((8, lanes), lambda i: (0, 0))
+    return pl.pallas_call(
+        functools.partial(mix_kernel, start),
+        grid=(1,),
         in_specs=[
             pl.BlockSpec(memory_space=pltpu.SMEM),
-            pl.BlockSpec((step, 4, width), lambda i: (start // step + i, 0, 0)),
+            pl.BlockSpec((tokens, 4, width), lambda i: (start // tokens, 0, 0)),
         ]
-        + [lane_block] * 4,
-        out_specs=[
-            pl.BlockSpec((8, 4 * step), lambda i: (0, i)),
-            pl.BlockSpec((step, width), lambda i: (i, 0)),
-        ],
+        + [whole] * 4,
+        out_specs=[whole, pl.BlockSpec((tokens, width), lambda i: (0, 0))],
         out_shape=[
-            jax.ShapeDtypeStruct((8, 4 * tokens), F32),
+            jax.ShapeDtypeStruct((8, lanes), F32),
             jax.ShapeDtypeStruct((tokens, width), BF),
         ],
         cost_estimate=cost(tokens * 4 * width * 400, tokens * 10 * width),
@@ -363,9 +383,8 @@
 
 def project(place, ring, own, other, pieces, servers):
     tokens, width = own.shape
-    rows, columns = pieces[0].shape
-    pair = 2 * width
-    tail = pl.BlockSpec((pl.Element(rows), pl.Element(pair)), lambda i: (0, columns - pair))
+    rows, pair = pieces[0].shape
+    tail = pl.BlockSpec((rows, pair), lambda i: (0, 0))
     full = pl.BlockSpec((tokens, width), lambda i: (0, 0))
     return pl.pallas_call(
         project_kernel,
@@ -385,20 +404,24 @@
 
 
 def final_kernel(
-    static_ref, x_ref, first_ref, own2_ref, a_ref, b_ref, c_ref, own_ref, inner_ref, outer_ref, *rest
+    static_ref, x_ref, first_ref, folded_ref, column_ref, own_ref, inner_ref, outer_ref, *rest
 ):
     new_ref = rest[-1]
     tokens, _, width = x_ref.shape
     first = first_ref[...]
-    second = (own2_ref[...] + a_ref[...]) + (b_ref[...] + c_ref[...])
     mean, inverse = centre(first)
     stream = lax.broadcasted_iota(jnp.int32, (1, 4 * tokens), 1) & 3
 
     def coefficient(column, projected):
-        dynamic = jnp.tanh(inverse * (projected - mean * second[2 + column : 3 + column]))
+        dynamic = jnp.tanh(inverse * (projected - mean * column_ref[column : column + 1, 0:1]))
         return by_stream(static_ref, column, stream) + dynamic
 
-    projected = [first[6:7], first[7:8], second[0:1], second[1:2], second[2:3]]
+    def unfolded(which):
+        return jnp.concatenate(
+            [folded_ref[4 * which + part : 4 * which + part + 1] for part in range(4)], axis=1
+        )
+
+    projected = [first[5:6], first[6:7], first[7:8], unfolded(0), unfolded(1)]
     columns = [coefficient(1 + j, projected[j]) for j in range(5)]
     residual = jnp.concatenate(columns[:4] + columns[:4], axis=0)
     row, col = iotas(4 * SUB, 4 * SUB)
@@ -413,8 +436,7 @@
         high, low = split(matrix, 2)
         new = contract(high, v, 1, 0) + contract(low, v, 1, 0)
         sent = inner_ref[rows, :].astype(F32) + outer_ref[rows, :].astype(F32)
-        update = own_ref[rows, :] + sent
-        update_high, update_low = split(update, 2)
+        update_high, update_low = split(own_ref[rows, :] + sent, 2)
         spread_high, spread_low = split(jnp.where(mine, columns[4][:, lanes], 0.0), 2)
         new += contract(
             jnp.concatenate([spread_high, spread_high, spread_low], axis=0),
@@ -425,18 +447,19 @@
         new_ref[rows] = new.astype(BF).reshape(SUB, 4, width)
 
 
-def final(static, x, first, first_at, second, second_at, updates, start, previous, step=128):
+def final(static, x, sums, updates, start, previous):
     tokens, width = updates[0].shape
-    lane_block = pl.BlockSpec((8, 4 * step), lambda i: (0, second_at // step + i))
-    stream_block = pl.BlockSpec((step, 4, width), lambda i: (start // step + i, 0, 0))
+    group = (sums.shape[1] - 128) // 5
+    stream_block = pl.BlockSpec((STEP, 4, width), lambda i: (start // STEP + i, 0, 0))
     specs = [
         pl.BlockSpec(memory_space=pltpu.SMEM),
         stream_block,
-        pl.BlockSpec((8, 4 * step), lambda i: (0, first_at // step + i)),
+        pl.BlockSpec((8, 4 * STEP), lambda i: (0, start // STEP + i)),
+        pl.BlockSpec((8, STEP), lambda i: (0, 4 * group // STEP + start // STEP + i)),
+        pl.BlockSpec((8, 128), lambda i: (0, 5 * group // 128)),
     ]
-    specs += [lane_block] * 4
-    specs += [pl.BlockSpec((step, width), lambda i: (i, 0))] * 3
-    args = [static, x, first, *second, *updates]
+    specs += [pl.BlockSpec((STEP, width), lambda i: (i, 0))] * 3
+    args = [static, x, sums, sums, sums, *updates]
     aliases = {}
     if previous is not None:
         specs.append(pl.BlockSpec(memory_space=pl.ANY))
@@ -444,7 +467,7 @@
         args.append(previous)
     return pl.pallas_call(
         final_kernel,
-        grid=(tokens // step,),
+        grid=(tokens // STEP,),
         in_specs=specs,
         out_specs=stream_block,
         out_shape=jax.ShapeDtypeStruct(x.shape, BF),
@@ -464,28 +487,30 @@
     proj_rows = jnp.concatenate(
         [hc_proj.T, jnp.ones((1, width), F32), jnp.zeros((1, width), F32)], axis=0
     )
-    first_late, second_late = stats(streams, proj_rows, BLOCK, BLOCK)
-    late = [first_late] + from_others(first_late, "mp")
-    parts = list(regroup(place, proj_master, group_size))
-    first_early, second_early = stats(streams, proj_rows, 0, BLOCK)
-    early = [first_early] + from_others(first_early, "mp")
-
-    for step in range(1, group_size):
-        parts[step] = lax.ppermute(
-            parts[step], "mp", [(at, (at + step) % group_size) for at in range(group_size)]
-        )
-    pieces = weight_pieces(assemble(place, parts))
+    own = stats(streams, proj_rows)
+    qkv_parts, out_parts = regroup(place, proj_master, group_size)
+    sums, qkv_parts = lax.optimization_barrier(([own] + from_others(own, "mp"), qkv_parts))
 
     def gathered(normed):
         rows = lax.all_gather(normed, "mp", axis=0, tiled=True)
         return rows.reshape(group_size, normed.shape[0], width)
 
-    sums_late, normed_late = mix(hc_static, streams, late, BLOCK, BLOCK, 0)
+    sums_late, normed_late = mix(hc_static, streams, sums, BLOCK, BLOCK)
     rows_late = gathered(normed_late)
-    sums_early, normed_early = mix(hc_static, streams, early, 0, BLOCK, 0)
+    _, normed_early = mix(hc_static, streams, sums, 0, BLOCK)
     rows_early = gathered(normed_early)
-    second_late = [second_late] + from_others(second_late, "mp")
-    second_early = [second_early] + from_others(second_early, "mp")
+
+    def served(parts):
+        for step in range(1, group_size):
+            parts[step] = lax.ppermute(
+                parts[step], "mp", [(at, (at + step) % group_size) for at in range(group_size)]
+            )
+        return assemble(place, parts)
+
+    qkv_part = served(qkv_parts)
+    qkv_part, out_parts, normed_early = lax.optimization_barrier((qkv_part, out_parts, normed_early))
+    qkv_pieces = weight_pieces(qkv_part)
+    out_pieces = weight_pieces(served(out_parts))
 
     halo = passed_along(segment_ids[-BLOCK:], "blk", 1)
     halo = jnp.where(lax.axis_index("blk") == 0, -1, halo)
@@ -510,37 +535,23 @@
     key_segments = jnp.stack(windows)[:, None, :]
     query_segments = segment_ids[:, None]
 
-    qkv_late = qkv_columns(ring, rows_late, pieces, cosine, sine, BLOCK)
+    qkv_late = qkv_columns(ring, rows_late, qkv_pieces, cosine, sine, BLOCK)
     halo_rows = passed_along(qkv_late[1:3], "blk", 1)
-    qkv_early = qkv_columns(ring, rows_early, pieces, cosine, sine, 0)
+    qkv_early = qkv_columns(ring, rows_early, qkv_pieces, cosine, sine, 0)
 
     chunks = [(halo_rows, 0, 0), (halo_rows, 0, 1), (qkv_early, 1, 0), (qkv_early, 1, 1)]
     chunks += [(qkv_late, 1, 0), (qkv_late, 1, 1)]
-    order = [
-        (2, sums_late, second_late, 0),
-        (3, sums_late, second_late, CHUNK),
-        (0, sums_early, second_early, 0),
-        (1, sums_early, second_early, CHUNK),
-    ]
     result = None
-    for chunk, first, second, lanes_at in order:
+    for chunk in (2, 3, 0, 1):
         source, _, at = chunks[chunk + 2]
         window = chunks[chunk : chunk + 3]
-        own = attend((source, at), window, query_segments, key_segments, chunk)
-        kept, inner, outer = project(place, ring, own, swapped(own, "mp", 1), pieces, group_size)
+        attended = attend((source, at), window, query_segments, key_segments, chunk)
+        other = swapped(attended, "mp", 1)
+        kept, inner, outer = project(place, ring, attended, other, out_pieces, group_size)
         inner = lax.ppermute(inner, "mp", [(1, 2), (2, 1)])
         outer = lax.ppermute(outer, "mp", [(1, 3), (2, 0)])
-        result = final(
-            hc_static,
-            streams,
-            first,
-            lanes_at,
-            second,
-            lanes_at,
-            [kept, inner, outer],
-            chunk * CHUNK,
-            result,
-        )
+        updates = [kept, inner, outer]
+        result = final(hc_static, streams, sums_late, updates, chunk * CHUNK, result)
     return result
 
 

time: 280 us -> 291 us (1.039)
  waiting for transfers between devices: 82.2 us -> 96.1 us
    ppermute x12 -> x3, starting transfers between devices: 43.5 us -> 6.96 us  [from_others(): lax.ppermute(value, axis, [(source, (source + step) % count) for source i...]
    ppermute x11 -> x18, waiting for transfers between devices: 8.59 us -> 34.8 us  [swapped(): lax.ppermute(value, axis, [(source, source ^ mask) for source in range(co...]
    ppermute x3 -> x6, starting transfers between devices: 4.1 us -> 27.9 us  [served(): lax.ppermute(parts[step], 'mp', [(at, (at + step) % group_size) for at in...]
    ppermute x11 -> x18, starting transfers between devices: 15.6 us -> 28 us  [swapped(): lax.ppermute(value, axis, [(source, source ^ mask) for source in range(co...]
    all_gather x2, waiting for transfers between devices: 11.4 us -> 0.01 us  [gathered(): rows = lax.all_gather(normed, 'mp', axis=0, tiled=True)]
    ppermute x12 -> x3, waiting for transfers between devices: 14 us -> 5.06 us  [from_others(): lax.ppermute(value, axis, [(source, (source + step) % count) for source i...]
    ppermute x3 -> x6, waiting for transfers between devices: 37.2 us -> 42.2 us  [served(): lax.ppermute(parts[step], 'mp', [(at, (at + step) % group_size) for at in...]
    ppermute x4, waiting for transfers between devices: 10.9 us -> 14 us  [body(): outer = lax.ppermute(outer, 'mp', [(1, 3), (2, 0)])]
  transfers between devices with their start and end apart: 38 -> 39, of which waited for: 13 -> 14; matrix products, arithmetic and copies ran while one was open for 3% -> 3% of each run, Pallas kernels for 28% -> 26%
where the time goes in v4:
time: 291 us; the launch traced here: 290 us
  waiting for transfers between devices  96.1 us (33%)
  Pallas kernels  87.8 us (30%)
  starting transfers between devices  73.7 us (25%)
  between operations  15 us (5%)
  local copies, waits for them, and re-layouts  11.1 us (4%)
  other arithmetic  6.29 us (2%)
    ppermute x6, waiting for transfers between devices, served(): lax.ppermute(parts[step], 'mp', [(at, (at + step) % group_size) for at in...  42.2 us
    ppermute x18, waiting for transfers between devices, swapped(): lax.ppermute(value, axis, [(source, source ^ mask) for source in range(co...  34.8 us
    ppermute x18, starting transfers between devices, swapped(): lax.ppermute(value, axis, [(source, source ^ mask) for source in range(co...  28 us
    ppermute x6, starting transfers between devices, served(): lax.ppermute(parts[step], 'mp', [(at, (at + step) % group_size) for at in...  27.9 us
    pallas_call x4, Pallas kernels, project(): pl.pallas_call(project_kernel, grid=(1,), in_specs=[pl.BlockSpec(memory_s...  18.6 us
    pallas_call x2, Pallas kernels, qkv_columns(): pl.pallas_call(qkv_kernel, grid=(3,), in_specs=[pl.BlockSpec(memory_space...  16.2 us
    pallas_call x4, Pallas kernels, attend(): pl.pallas_call(attend_kernel, grid=(1,), in_specs=[pl.BlockSpec(block, la...  16.1 us
    ppermute x4, waiting for transfers between devices, body(): outer = lax.ppermute(outer, 'mp', [(1, 3), (2, 0)])  14 us
  transfers between devices with their start and end apart: 39, of which 14 were waited for; matrix products, arithmetic and copies ran while one was open for 3% of the time, Pallas kernels for 26%

profile of v4, /device:TPU:0, one launch (start us, length us, event | category | flops | bytes accessed | tf_op | source)
XLA Modules:
  0.0 290.0 jit_solution(11972062471241393319)
XLA Ops:
  6.7 1.4 maximum_maximum_fusion.proj_ref
  8.1 6.4 %stats.1.own_ref = f32[8,5248]{1,0:T(8,128)} custom-call(bf16[1024,4,512]{2,1,0:T(4,128)(2,1)} %x_ref.13, f32[8,512]{1,0:T(8,128)} %maximum_maximum_fusion.proj_ref), custom_call_target="tpu_custom_call" | custom-call | flops 1258291200 | bytes 4194304 | tf_op jit(solution)/shard_map/stats/pallas_call | solution.py:173
  14.4 3.0 %collective-permute-start = (f32[8,5248]{1,0:T(8,128)}, f32[8,5248]{1,0:T(8,128)S(1)}, u32[]{:S(2)}, u32[]{:S(2)}) collective-permute-start(f32[8,5248]{1,0:T(8,128)} %stats.1.own_ref), channel_id=1, source_target_pairs={{0,1},{1,2},{2,3},{3,0},{4,5},{5,6},{6,7},{7,4},{8,9},{9,10},{10,1... | collective-permute-start | bytes 503816 | tf_op jit(solution)/shard_map/ppermute | solution.py:31
  17.5 2.6 collective-permute-start.1
  20.0 1.3 collective-permute-start.2
  21.4 4.8 %regroup.1 = (bf16[64,1536]{1,0:T(8,128)(2,1)}, bf16[64,1536]{1,0:T(8,128)(2,1)}, bf16[64,1536]{1,0:T(8,128)(2,1)}, bf16[64,1536]{1,0:T(8,128)(2,1)}, bf16[64,10...) custom-call(s32[1]{0:T(128)} %bitcast.1.place_ref, ...), custom_call_target="tpu_custom_call" | custom-call | bytes 3407872 | tf_op jit(solution)/shard_map/regroup/pallas_call | solution.py:79
  26.2 5.1 %collective-permute-done.1.b_ref = f32[8,5248]{1,0:T(8,128)S(1)} collective-permute-done((f32[8,5248]{1,0:T(8,128)}, f32[8,5248]{1,0:T(8,128)S(1)}, u32[]{:S(2)}, u32[]{:S(2)}) %collective-permute-start.1) | collective-permute-done | bytes 167968 | tf_op jit(solution)/shard_map/ppermute | solution.py:31
  32.0 4.0 %mix.2 = (f32[8,5248]{1,0:T(8,128)}, bf16[512,512]{1,0:T(8,128)(2,1)}) custom-call(f32[4,6]{1,0:T(4,128)} %static_ref.11, bf16[1024,4,512]{2,1,0:T(4,128)(2,1)} %x_ref.13, f32[8,5248]{1,0:T(8,128)} %stats.1.own_ref, f32[8,5248]{1,0:T(8,128)} %copy-done.5, f32[8,5248]{1,0:T(8,128)} %copy-done.6, f32[8,5248]{1,0:T(8,128)} %copy-done.7), custom_call_target="tpu_custom_call" | custom-call | flops 419430400 | bytes 2621440 | tf_op jit(solution)/shard_map/mix/pallas_call | solution.py:239
  36.1 4.0 %mix.3 = (f32[8,5248]{1,0:T(8,128)}, bf16[512,512]{1,0:T(8,128)(2,1)}) custom-call(f32[4,6]{1,0:T(4,128)} %static_ref.11, bf16[1024,4,512]{2,1,0:T(4,128)(2,1)} %x_ref.13, f32[8,5248]{1,0:T(8,128)} %stats.1.own_ref, f32[8,5248]{1,0:T(8,128)} %copy-done.5, f32[8,5248]{1,0:T(8,128)} %copy-done.6, f32[8,5248]{1,0:T(8,128)} %copy-done.7), custom_call_target="tpu_custom_call" | custom-call | flops 419430400 | bytes 2621440 | tf_op jit(solution)/shard_map/mix/pallas_call | solution.py:239
  40.2 4.1 %collective-permute-start.4 = (bf16[64,1536]{1,0:T(8,128)(2,1)S(1)}, bf16[64,1536]{1,0:T(8,128)(2,1)S(1)}, u32[]{:S(2)}, u32[]{:S(2)}) collective-permute-start(bf16[64,1536]{1,0:T(8,128)(2,1)S(1)} %copy-done.33), channel_id=1, source_target_pairs={{0,1},{1,2},{2,3},{3,0},{4,5},{5,6},{6,7},{7,4},{8,9},{9,10},{10,1... | collective-permute-start | bytes 589832 | tf_op jit(solution)/shard_map/ppermute | solution.py:505
  44.2 1.7 collective-permute-start.5
  46.7 5.0 %collective-permute-done.4.refs_1_ = bf16[64,1536]{1,0:T(8,128)(2,1)S(1)} collective-permute-done((bf16[64,1536]{1,0:T(8,128)(2,1)S(1)}, bf16[64,1536]{1,0:T(8,128)(2,1)S(1)}, u32[]{:S(2)}, u32[]{:S(2)}) %collective-permute-start.4) | collective-permute-done | bytes 196640 | tf_op jit(solution)/shard_map/ppermute | solution.py:505
  51.7 14.6 %collective-permute-done.5.refs_2_ = bf16[64,1536]{1,0:T(8,128)(2,1)S(1)} collective-permute-done((bf16[64,1536]{1,0:T(8,128)(2,1)S(1)}, bf16[64,1536]{1,0:T(8,128)(2,1)S(1)}, u32[]{:S(2)}, u32[]{:S(2)}) %collective-permute-start.5) | collective-permute-done | bytes 196640 | tf_op jit(solution)/shard_map/ppermute | solution.py:505
  66.3 1.3 collective-permute-done.6.refs_3_
  68.3 2.2 assemble.2.refs_0_
  70.5 1.3 collective-permute-start.8
  71.7 1.6 collective-permute-start.10
  75.1 1.3 collective-permute-start.3
  77.1 2.1 collective-permute-start.7
  79.1 12.0 %collective-permute-done.8.refs_2_ = bf16[256,1536]{1,0:T(8,128)(2,1)S(1)} collective-permute-done((bf16[256,1536]{1,0:T(8,128)(2,1)}, bf16[256,1536]{1,0:T(8,128)(2,1)S(1)}, u32[]{:S(2)}, u32[]{:S(2)}) %collective-permute-start.8) | collective-permute-done | bytes 786464 | tf_op jit(solution)/shard_map/ppermute | solution.py:117
  91.2 16.2 %collective-permute-done.10.refs_4_ = bf16[256,1536]{1,0:T(8,128)(2,1)S(1)} collective-permute-done((bf16[256,1536]{1,0:T(8,128)(2,1)}, bf16[256,1536]{1,0:T(8,128)(2,1)S(1)}, u32[]{:S(2)}, u32[]{:S(2)}) %collective-permute-start.10) | collective-permute-done | bytes 786464 | tf_op jit(solution)/shard_map/ppermute | solution.py:117
  107.9 15.4 %collective-permute-start.16 = (bf16[64,1024]{1,0:T(8,128)(2,1)S(1)}, bf16[64,1024]{1,0:T(8,128)(2,1)S(1)}, u32[]{:S(2)}, u32[]{:S(2)}) collective-permute-start(bf16[64,1024]{1,0:T(8,128)(2,1)S(1)} %copy-done.36), channel_id=1, source_target_pairs={{0,1},{1,2},{2,3},{3,0},{4,5},{5,6},{6,7},{7,4},{8,9},{9,10},{10,1... | collective-permute-start | bytes 393224 | tf_op jit(solution)/shard_map/ppermute | solution.py:505
  123.3 1.6 convert_reduce_fusion
  124.9 4.8 %collective-permute-done.16.refs_1_ = bf16[64,1024]{1,0:T(8,128)(2,1)S(1)} collective-permute-done((bf16[64,1024]{1,0:T(8,128)(2,1)S(1)}, bf16[64,1024]{1,0:T(8,128)(2,1)S(1)}, u32[]{:S(2)}, u32[]{:S(2)}) %collective-permute-start.16) | collective-permute-done | bytes 131104 | tf_op jit(solution)/shard_map/ppermute | solution.py:505
  129.7 4.8 %collective-permute-start.17 = (bf16[64,1024]{1,0:T(8,128)(2,1)S(1)}, bf16[64,1024]{1,0:T(8,128)(2,1)S(1)}, u32[]{:S(2)}, u32[]{:S(2)}) collective-permute-start(bf16[64,1024]{1,0:T(8,128)(2,1)S(1)} %copy-done.35), channel_id=1, source_target_pairs={{0,2},{1,3},{2,0},{3,1},{4,6},{5,7},{6,4},{7,5},{8,10},{9,11},{10,... | collective-permute-start | bytes 393224 | tf_op jit(solution)/shard_map/ppermute | solution.py:505
  134.5 1.9 fusion.1
  136.4 12.7 %collective-permute-done.17.refs_2_ = bf16[64,1024]{1,0:T(8,128)(2,1)S(1)} collective-permute-done((bf16[64,1024]{1,0:T(8,128)(2,1)S(1)}, bf16[64,1024]{1,0:T(8,128)(2,1)S(1)}, u32[]{:S(2)}, u32[]{:S(2)}) %collective-permute-start.17) | collective-permute-done | bytes 131104 | tf_op jit(solution)/shard_map/ppermute | solution.py:505
  149.1 1.2 collective-permute-start.18
  150.3 1.4 pad_maximum_fusion
  151.7 3.8 %collective-permute-done.18.refs_3_ = bf16[64,1024]{1,0:T(8,128)(2,1)S(1)} collective-permute-done((bf16[64,1024]{1,0:T(8,128)(2,1)S(1)}, bf16[64,1024]{1,0:T(8,128)(2,1)S(1)}, u32[]{:S(2)}, u32[]{:S(2)}) %collective-permute-start.18) | collective-permute-done | bytes 131104 | tf_op jit(solution)/shard_map/ppermute | solution.py:505
  156.1 1.9 assemble.3.refs_0_
  158.0 1.6 collective-permute-start.20
  160.3 1.2 collective-permute-start.24
  161.6 8.1 %qkv.3.q_ref.k1.k2.v1.v2 = bf16[3,512,512]{2,1,0:T(8,128)(2,1)} custom-call(s32[1]{0:T(128)} %bitcast.2.ring_ref, bf16[4,512,512]{2,1,0:T(8,128)(2,1)} %bitcast.13, f32[1024,128]{1,0:T(8,128)} %get-tuple-element.91.cosine_ref, f32[1024,128]{1,0:T(8,128)} %get-tuple-element.92.sine_ref, bf16[256,1536]{1,0:T(8,128)(2,1)} %assemble.2.refs_0_, ...), custom_call_target="tpu_custom_call" | custom-call | flops 3221225472 | bytes 11534336 | tf_op jit(solution)/shard_map/qkv/pallas_call | solution.py:292
  169.7 2.2 slice.38
  171.9 1.5 collective-permute-start.14
  173.4 1.0 copy.14.qseg_ref
  174.5 2.4 collective-permute-start.19
  177.6 6.5 %collective-permute-done.22.refs_4_ = bf16[256,1024]{1,0:T(8,128)(2,1)S(1)} collective-permute-done((bf16[256,1024]{1,0:T(8,128)(2,1)}, bf16[256,1024]{1,0:T(8,128)(2,1)S(1)}, u32[]{:S(2)}, u32[]{:S(2)}) %collective-permute-start.22) | collective-permute-done | bytes 524320 | tf_op jit(solution)/shard_map/ppermute | solution.py:117
  184.6 8.1 %qkv.2.q_ref.k1.k2.v1.v2.k0.v0 = bf16[3,512,512]{2,1,0:T(8,128)(2,1)} custom-call(s32[1]{0:T(128)} %bitcast.2.ring_ref, bf16[4,512,512]{2,1,0:T(8,128)(2,1)} %bitcast.12, f32[1024,128]{1,0:T(8,128)} %get-tuple-element.91.cosine_ref, f32[1024,128]{1,0:T(8,128)} %get-tuple-element.92.sine_ref, bf16[256,1536]{1,0:T(8,128)(2,1)} %assemble.2.refs_0_, ...), custom_call_target="tpu_custom_call" | custom-call | flops 3221225472 | bytes 11534336 | tf_op jit(solution)/shard_map/qkv/pallas_call | solution.py:292
  192.7 4.0 %attend.6.own_ref = bf16[256,512]{1,0:T(8,128)(2,1)} custom-call(bf16[3,512,512]{2,1,0:T(8,128)(2,1)} %qkv.3.q_ref.k1.k2.v1.v2, bf16[3,512,512]{2,1,0:T(8,128)(2,1)} %qkv.2.q_ref.k1.k2.v1.v2.k0.v0, bf16[3,512,512]{2,1,0:T(8,128)(2,1)} %qkv.3.q_ref.k1.k2.v1.v2, bf16[3,512,512]{2,1,0:T(8,128)(2,1)} %qkv.3.q_ref.k1.k2.v1.v2, ...), custom_call_target="tpu_custom_call" | custom-call | flops 402653184 | bytes 2097152 | tf_op jit(solution)/shard_map/attend/pallas_call | solution.py:340
  196.7 9.8 %collective-permute-start.31 = (bf16[256,512]{1,0:T(8,128)(2,1)}, bf16[256,512]{1,0:T(8,128)(2,1)S(1)}, u32[]{:S(2)}, u32[]{:S(2)}) collective-permute-start(bf16[256,512]{1,0:T(8,128)(2,1)} %attend.6.own_ref), channel_id=1, source_target_pairs={{0,1},{1,0},{2,3},{3,2},{4,5},{5,4},{6,7},{7,6},{8,9},{9,8},{10,11... | collective-permute-start | bytes 786440 | tf_op jit(solution)/shard_map/ppermute | solution.py:117
  206.6 4.0 %attend.7.own_ref = bf16[256,512]{1,0:T(8,128)(2,1)} custom-call(bf16[3,512,512]{2,1,0:T(8,128)(2,1)} %qkv.3.q_ref.k1.k2.v1.v2, bf16[3,512,512]{2,1,0:T(8,128)(2,1)} %qkv.2.q_ref.k1.k2.v1.v2.k0.v0, bf16[3,512,512]{2,1,0:T(8,128)(2,1)} %qkv.2.q_ref.k1.k2.v1.v2.k0.v0, bf16[3,512,512]{2,1,0:T(8,128)(2,1)} %qkv.3.q_ref.k1.k2.v1.v2, ...), custom_call_target="tpu_custom_call" | custom-call | flops 402653184 | bytes 2097152 | tf_op jit(solution)/shard_map/attend/pallas_call | solution.py:340
  210.7 0.9 copy-done
  211.5 4.0 %attend.5.own_ref = bf16[256,512]{1,0:T(8,128)(2,1)} custom-call(bf16[3,512,512]{2,1,0:T(8,128)(2,1)} %qkv.2.q_ref.k1.k2.v1.v2.k0.v0, bf16[2,512,512]{2,1,0:T(8,128)(2,1)} %copy-done, bf16[2,512,512]{2,1,0:T(8,128)(2,1)} %copy-done, bf16[3,512,512]{2,1,0:T(8,128)(2,1)} %qkv.2.q_ref.k1.k2.v1.v2.k0.v0, bf16[2,512,512]{2,1,0:T(8,128)(2,1)} %copy-done, ...), custom_call_target="tpu_custom_call" | custom-call | flops 402653184 | bytes 2097152 | tf_op jit(solution)/shard_map/attend/pallas_call | solution.py:340
  215.6 1.1 collective-permute-start.28
  217.4 4.7 %project.6 = (f32[256,512]{1,0:T(8,128)}, bf16[256,512]{1,0:T(8,128)(2,1)}, bf16[256,512]{1,0:T(8,128)(2,1)}) custom-call(s32[1]{0:T(128)} %bitcast.1.place_ref, s32[1]{0:T(128)} %bitcast.2.ring_ref, bf16[256,512]{1,0:T(8,128)(2,1)} %attend.6.own_ref, bf16[256,512]{1,0:T(8,128)(2,1)} %copy-done.13, bf16[256,1024]{1,0:T(8,128)(2,1)} %assemble.3.refs_0_, ...), custom_call_target="tpu_custom_call" | custom-call | flops 1073741824 | bytes 5767168 | tf_op jit(solution)/shard_map/project/pallas_call | solution.py:389
  222.8 4.0 %attend.4.own_ref = bf16[256,512]{1,0:T(8,128)(2,1)} custom-call(bf16[3,512,512]{2,1,0:T(8,128)(2,1)} %qkv.2.q_ref.k1.k2.v1.v2.k0.v0, bf16[2,512,512]{2,1,0:T(8,128)(2,1)} %copy-done, bf16[3,512,512]{2,1,0:T(8,128)(2,1)} %qkv.2.q_ref.k1.k2.v1.v2.k0.v0, bf16[3,512,512]{2,1,0:T(8,128)(2,1)} %qkv.2.q_ref.k1.k2.v1.v2.k0.v0, bf16[2,512,512]{2,1,0:T(8,128)(2,1)} %copy-done, ...), custom_call_target="tpu_custom_call" | custom-call | flops 402653184 | bytes 2097152 | tf_op jit(solution)/shard_map/attend/pallas_call | solution.py:340
  226.8 4.5 %collective-permute-start.15 = (bf16[256,512]{1,0:T(8,128)(2,1)}, bf16[256,512]{1,0:T(8,128)(2,1)S(1)}, u32[]{:S(2)}, u32[]{:S(2)}) collective-permute-start(bf16[256,512]{1,0:T(8,128)(2,1)} %attend.4.own_ref), channel_id=1, source_target_pairs={{0,1},{1,0},{2,3},{3,2},{4,5},{5,4},{6,7},{7,6},{8,9},{9,8},{10,11... | collective-permute-start | bytes 786440 | tf_op jit(solution)/shard_map/ppermute | solution.py:117
  232.0 4.6 %project.7 = (f32[256,512]{1,0:T(8,128)}, bf16[256,512]{1,0:T(8,128)(2,1)}, bf16[256,512]{1,0:T(8,128)(2,1)}) custom-call(s32[1]{0:T(128)} %bitcast.1.place_ref, s32[1]{0:T(128)} %bitcast.2.ring_ref, bf16[256,512]{1,0:T(8,128)(2,1)} %attend.7.own_ref, bf16[256,512]{1,0:T(8,128)(2,1)} %copy-done.12, bf16[256,1024]{1,0:T(8,128)(2,1)} %assemble.3.refs_0_, ...), custom_call_target="tpu_custom_call" | custom-call | flops 1073741824 | bytes 5767168 | tf_op jit(solution)/shard_map/project/pallas_call | solution.py:389
  237.3 1.3 collective-permute-start.36
  238.6 1.5 collective-permute-start.33
  240.1 4.7 %project.5 = (f32[256,512]{1,0:T(8,128)}, bf16[256,512]{1,0:T(8,128)(2,1)}, bf16[256,512]{1,0:T(8,128)(2,1)}) custom-call(s32[1]{0:T(128)} %bitcast.1.place_ref, s32[1]{0:T(128)} %bitcast.2.ring_ref, bf16[256,512]{1,0:T(8,128)(2,1)} %attend.5.own_ref, bf16[256,512]{1,0:T(8,128)(2,1)} %copy-done.11, bf16[256,1024]{1,0:T(8,128)(2,1)} %assemble.3.refs_0_, ...), custom_call_target="tpu_custom_call" | custom-call | flops 1073741824 | bytes 5767168 | tf_op jit(solution)/shard_map/project/pallas_call | solution.py:389
  245.5 1.3 collective-permute-start.30
  246.8 4.7 %project.4 = (f32[256,512]{1,0:T(8,128)}, bf16[256,512]{1,0:T(8,128)(2,1)}, bf16[256,512]{1,0:T(8,128)(2,1)}) custom-call(s32[1]{0:T(128)} %bitcast.1.place_ref, s32[1]{0:T(128)} %bitcast.2.ring_ref, bf16[256,512]{1,0:T(8,128)(2,1)} %attend.4.own_ref, bf16[256,512]{1,0:T(8,128)(2,1)} %copy-done.10, bf16[256,1024]{1,0:T(8,128)(2,1)} %assemble.3.refs_0_, ...), custom_call_target="tpu_custom_call" | custom-call | flops 1073741824 | bytes 5767168 | tf_op jit(solution)/shard_map/project/pallas_call | solution.py:389
  252.2 0.8 collective-permute-done.36.outer_ref
  253.0 1.3 collective-permute-start.27
  254.3 3.4 %final.4.rest_0_ = bf16[1024,4,512]{2,1,0:T(4,128)(2,1)} custom-call(f32[4,6]{1,0:T(4,128)} %static_ref.11, bf16[1024,4,512]{2,1,0:T(4,128)(2,1)} %x_ref.13, f32[8,5248]{1,0:T(8,128)} %get-tuple-element.49.first_ref.folded_ref.column_ref, f32[8,5248]{1,0:T(8,128)} %get-tuple-element.49.first_ref.folded_ref.column_ref, ...), custom_call_target="tpu_custom_call" | custom-call | flops 629145600 | bytes 2883584 | tf_op jit(solution)/shard_map/final/pallas_call | solution.py:468
  257.7 0.9 collective-permute-done.33.outer_ref
  259.3 3.4 %final.5.rest_0_ = bf16[1024,4,512]{2,1,0:T(4,128)(2,1)} custom-call(f32[4,6]{1,0:T(4,128)} %static_ref.11, bf16[1024,4,512]{2,1,0:T(4,128)(2,1)} %x_ref.13, f32[8,5248]{1,0:T(8,128)} %get-tuple-element.49.first_ref.folded_ref.column_ref, f32[8,5248]{1,0:T(8,128)} %get-tuple-element.49.first_ref.folded_ref.column_ref, ...), custom_call_target="tpu_custom_call", output_to_operand_aliasing={{}: (8, {})} | custom-call | flops 629145600 | bytes 2883584 | tf_op jit(solution)/shard_map/final/pallas_call | solution.py:468
  262.7 7.1 %collective-permute-done.30.outer_ref = bf16[256,512]{1,0:T(8,128)(2,1)S(1)} collective-permute-done((bf16[256,512]{1,0:T(8,128)(2,1)}, bf16[256,512]{1,0:T(8,128)(2,1)S(1)}, u32[]{:S(2)}, u32[]{:S(2)}) %collective-permute-start.30) | collective-permute-done | bytes 262176 | tf_op jit(solution)/shard_map/ppermute | solution.py:552
  270.6 3.4 %final.6.rest_0_ = bf16[1024,4,512]{2,1,0:T(4,128)(2,1)} custom-call(f32[4,6]{1,0:T(4,128)} %static_ref.11, bf16[1024,4,512]{2,1,0:T(4,128)(2,1)} %x_ref.13, f32[8,5248]{1,0:T(8,128)} %get-tuple-element.49.first_ref.folded_ref.column_ref, f32[8,5248]{1,0:T(8,128)} %get-tuple-element.49.first_ref.folded_ref.column_ref, ...), custom_call_target="tpu_custom_call", output_to_operand_aliasing={{}: (8, {})} | custom-call | flops 629145600 | bytes 2883584 | tf_op jit(solution)/shard_map/final/pallas_call | solution.py:468
  274.0 5.1 %collective-permute-done.27.outer_ref = bf16[256,512]{1,0:T(8,128)(2,1)S(1)} collective-permute-done((bf16[256,512]{1,0:T(8,128)(2,1)}, bf16[256,512]{1,0:T(8,128)(2,1)S(1)}, u32[]{:S(2)}, u32[]{:S(2)}) %collective-permute-start.27) | collective-permute-done | bytes 262176 | tf_op jit(solution)/shard_map/ppermute | solution.py:552
  279.8 3.4 %final.7 = bf16[1024,4,512]{2,1,0:T(4,128)(2,1)} custom-call(f32[4,6]{1,0:T(4,128)} %static_ref.11, bf16[1024,4,512]{2,1,0:T(4,128)(2,1)} %x_ref.13, f32[8,5248]{1,0:T(8,128)} %get-tuple-element.49.first_ref.folded_ref.column_ref, f32[8,5248]{1,0:T(8,128)} %get-tuple-element.49.first_ref.folded_ref.column_ref, ...), custom_call_target="tpu_custom_call", output_to_operand_aliasing={{}: (8, {})} | custom-call | flops 629145600 | bytes 2883584 | tf_op jit(solution)/shard_map/final/pallas_call | solution.py:468
  (135 shorter events, 13.0 us)
Async XLA Ops:
  6.5 155.0 %all-gather.5.cloned.1.call-start = ((), (), s32[]{:S(2)}) async-start(), calls=%async_computation.1 | async-start | bytes 2621440 | tf_op jit(solution)/shard_map/all_gather | solution.py:495
  14.4 11.8 %collective-permute-start = (f32[8,5248]{1,0:T(8,128)}, f32[8,5248]{1,0:T(8,128)S(1)}, u32[]{:S(2)}, u32[]{:S(2)}) collective-permute-start(f32[8,5248]{1,0:T(8,128)} %stats.1.own_ref), channel_id=1, source_target_pairs={{0,1},{1,2},{2,3},{3,0},{4,5},{5,6},{6,7},{7,4},{8,9},{9,10},{10,1... | collective-permute-start | bytes 503816 | tf_op jit(solution)/shard_map/ppermute | solution.py:31
  17.5 13.8 %collective-permute-start.1 = (f32[8,5248]{1,0:T(8,128)}, f32[8,5248]{1,0:T(8,128)S(1)}, u32[]{:S(2)}, u32[]{:S(2)}) collective-permute-start(f32[8,5248]{1,0:T(8,128)} %stats.1.own_ref), channel_id=1, source_target_pairs={{0,2},{1,3},{2,0},{3,1},{4,6},{5,7},{6,4},{7,5},{8,10},{9,11},{10,... | collective-permute-start | bytes 503816 | tf_op jit(solution)/shard_map/ppermute | solution.py:31
  20.0 11.2 %collective-permute-start.2 = (f32[8,5248]{1,0:T(8,128)}, f32[8,5248]{1,0:T(8,128)S(1)}, u32[]{:S(2)}, u32[]{:S(2)}) collective-permute-start(f32[8,5248]{1,0:T(8,128)} %stats.1.own_ref), channel_id=1, source_target_pairs={{0,3},{1,0},{2,1},{3,2},{4,7},{5,4},{6,5},{7,6},{8,11},{9,8},{10,9... | collective-permute-start | bytes 503816 | tf_op jit(solution)/shard_map/ppermute | solution.py:31
  26.2 5.1 %copy-start.5 = (f32[8,5248]{1,0:T(8,128)}, f32[8,5248]{1,0:T(8,128)S(1)}, u32[]{:S(2)}) copy-start(f32[8,5248]{1,0:T(8,128)S(1)} %collective-permute-done.a_ref) | copy-start | bytes 503812
  32.0 8.2 %copy-start.33 = (bf16[64,1536]{1,0:T(8,128)(2,1)S(1)}, bf16[64,1536]{1,0:T(8,128)(2,1)}, u32[]{:S(2)}) copy-start(bf16[64,1536]{1,0:T(8,128)(2,1)} %get-tuple-element.52) | copy-start | bytes 589828
  32.0 12.2 %copy-start.32 = (bf16[64,1536]{1,0:T(8,128)(2,1)S(1)}, bf16[64,1536]{1,0:T(8,128)(2,1)}, u32[]{:S(2)}) copy-start(bf16[64,1536]{1,0:T(8,128)(2,1)} %get-tuple-element.53) | copy-start | bytes 589828
  32.0 13.9 %copy-start.31 = (bf16[64,1536]{1,0:T(8,128)(2,1)S(1)}, bf16[64,1536]{1,0:T(8,128)(2,1)}, u32[]{:S(2)}) copy-start(bf16[64,1536]{1,0:T(8,128)(2,1)} %get-tuple-element.54) | copy-start | bytes 589828
  36.0 38.0 %copy-start.27 = (s32[2]{0:T(128)S(1)}, s32[2]{0:T(128)}, u32[]{:S(2)}) copy-start(s32[2]{0:T(128)} %param.11) | copy-start | bytes 28
  36.0 39.1 %copy-start.26 = (s32[1024]{0:T(1024)S(1)}, s32[1024]{0:T(1024)}, u32[]{:S(2)}) copy-start(s32[1024]{0:T(1024)} %param.10) | copy-start | bytes 12292
  36.0 71.9 %copy-start.36 = (bf16[64,1024]{1,0:T(8,128)(2,1)S(1)}, bf16[64,1024]{1,0:T(8,128)(2,1)}, u32[]{:S(2)}) copy-start(bf16[64,1024]{1,0:T(8,128)(2,1)} %get-tuple-element.62) | copy-start | bytes 393220
  36.0 93.7 %copy-start.35 = (bf16[64,1024]{1,0:T(8,128)(2,1)S(1)}, bf16[64,1024]{1,0:T(8,128)(2,1)}, u32[]{:S(2)}) copy-start(bf16[64,1024]{1,0:T(8,128)(2,1)} %get-tuple-element.63) | copy-start | bytes 393220
  36.0 113.1 %copy-start.34 = (bf16[64,1024]{1,0:T(8,128)(2,1)S(1)}, bf16[64,1024]{1,0:T(8,128)(2,1)}, u32[]{:S(2)}) copy-start(bf16[64,1024]{1,0:T(8,128)(2,1)} %get-tuple-element.64) | copy-start | bytes 393220
  36.0 148.6 %all-gather.3.cloned.1.call-start = ((), (), s32[]{:S(2)}) async-start(), calls=%async_computation | async-start | bytes 2621440 | tf_op jit(solution)/shard_map/all_gather | solution.py:495
  40.2 11.6 %collective-permute-start.4 = (bf16[64,1536]{1,0:T(8,128)(2,1)S(1)}, bf16[64,1536]{1,0:T(8,128)(2,1)S(1)}, u32[]{:S(2)}, u32[]{:S(2)}) collective-permute-start(bf16[64,1536]{1,0:T(8,128)(2,1)S(1)} %copy-done.33), channel_id=1, source_target_pairs={{0,1},{1,2},{2,3},{3,0},{4,5},{5,6},{6,7},{7,4},{8,9},{9,10},{10,1... | collective-permute-start | bytes 589832 | tf_op jit(solution)/shard_map/ppermute | solution.py:505
  44.2 22.1 %collective-permute-start.5 = (bf16[64,1536]{1,0:T(8,128)(2,1)S(1)}, bf16[64,1536]{1,0:T(8,128)(2,1)S(1)}, u32[]{:S(2)}, u32[]{:S(2)}) collective-permute-start(bf16[64,1536]{1,0:T(8,128)(2,1)S(1)} %copy-done.32), channel_id=1, source_target_pairs={{0,2},{1,3},{2,0},{3,1},{4,6},{5,7},{6,4},{7,5},{8,10},{9,11},{10,... | collective-permute-start | bytes 589832 | tf_op jit(solution)/shard_map/ppermute | solution.py:505
  45.9 21.7 %collective-permute-start.6 = (bf16[64,1536]{1,0:T(8,128)(2,1)S(1)}, bf16[64,1536]{1,0:T(8,128)(2,1)S(1)}, u32[]{:S(2)}, u32[]{:S(2)}) collective-permute-start(bf16[64,1536]{1,0:T(8,128)(2,1)S(1)} %copy-done.31), channel_id=1, source_target_pairs={{0,3},{1,0},{2,1},{3,2},{4,7},{5,4},{6,5},{7,6},{8,11},{9,8},{10,9... | collective-permute-start | bytes 589832 | tf_op jit(solution)/shard_map/ppermute | solution.py:505
  51.7 15.9 %copy-start.20 = (bf16[64,1536]{1,0:T(8,128)(2,1)}, bf16[64,1536]{1,0:T(8,128)(2,1)S(1)}, u32[]{:S(2)}) copy-start(bf16[64,1536]{1,0:T(8,128)(2,1)S(1)} %collective-permute-done.4.refs_1_) | copy-start | bytes 589828
  70.5 20.7 %collective-permute-start.8 = (bf16[256,1536]{1,0:T(8,128)(2,1)}, bf16[256,1536]{1,0:T(8,128)(2,1)S(1)}, u32[]{:S(2)}, u32[]{:S(2)}) collective-permute-start(bf16[256,1536]{1,0:T(8,128)(2,1)} %assemble.2.refs_0_), channel_id=1, source_target_pairs={{0,8},{4,12},{8,0},{12,4},{16,24},{20,28},{24,16},{28,20},{1,9},{5... | collective-permute-start | bytes 2359304 | tf_op jit(solution)/shard_map/ppermute | solution.py:117
  71.7 35.6 %collective-permute-start.10 = (bf16[256,1536]{1,0:T(8,128)(2,1)}, bf16[256,1536]{1,0:T(8,128)(2,1)S(1)}, u32[]{:S(2)}, u32[]{:S(2)}) collective-permute-start(bf16[256,1536]{1,0:T(8,128)(2,1)} %assemble.2.refs_0_), channel_id=1, source_target_pairs={{0,16},{4,20},{8,24},{12,28},{16,0},{20,4},{24,8},{28,12},{1,17},{... | collective-permute-start | bytes 2359304 | tf_op jit(solution)/shard_map/ppermute | solution.py:117
  73.3 34.1 %collective-permute-start.12 = (bf16[256,1536]{1,0:T(8,128)(2,1)}, bf16[256,1536]{1,0:T(8,128)(2,1)}, u32[]{:S(2)}, u32[]{:S(2)}) collective-permute-start(bf16[256,1536]{1,0:T(8,128)(2,1)} %assemble.2.refs_0_), channel_id=1, source_target_pairs={{0,24},{4,28},{8,16},{12,20},{16,8},{20,12},{24,0},{28,4},{1,25},{... | collective-permute-start | bytes 2359304 | tf_op jit(solution)/shard_map/ppermute | solution.py:117
  75.1 32.8 %collective-permute-start.3 = (s32[512]{0:T(512)S(1)}, s32[512]{0:T(512)S(1)}, u32[]{:S(2)}, u32[]{:S(2)}) collective-permute-start(s32[512]{0:T(512)S(1)} %get-tuple-element.86), channel_id=1, source_target_pairs={{0,4},{4,8},{8,12},{12,16},{16,20},{20,24},{24,28},{1,5},{5,9},{9,... | collective-permute-start | bytes 6152 | tf_op jit(solution)/shard_map/ppermute | solution.py:25
  77.1 82.6 %collective-permute-start.7 = (bf16[256,1536]{1,0:T(8,128)(2,1)}, bf16[256,1536]{1,0:T(8,128)(2,1)}, u32[]{:S(2)}, u32[]{:S(2)}) collective-permute-start(bf16[256,1536]{1,0:T(8,128)(2,1)} %assemble.2.refs_0_), channel_id=1, source_target_pairs={{0,4},{4,0},{8,12},{12,8},{16,20},{20,16},{24,28},{28,24},{1,5},{5... | collective-permute-start | bytes 2359304 | tf_op jit(solution)/shard_map/ppermute | solution.py:117
  91.2 70.4 %copy-start.28 = (bf16[256,1536]{1,0:T(8,128)(2,1)}, bf16[256,1536]{1,0:T(8,128)(2,1)S(1)}, u32[]{:S(2)}) copy-start(bf16[256,1536]{1,0:T(8,128)(2,1)S(1)} %collective-permute-done.8.refs_2_) | copy-start | bytes 2359300
  91.2 69.1 %collective-permute-start.9 = (bf16[256,1536]{1,0:T(8,128)(2,1)S(1)}, bf16[256,1536]{1,0:T(8,128)(2,1)}, u32[]{:S(2)}, u32[]{:S(2)}) collective-permute-start(bf16[256,1536]{1,0:T(8,128)(2,1)S(1)} %collective-permute-done.8.refs_2_), channel_id=1, source_target_pairs={{0,4},{4,0},{8,12},{12,8},{16,20},{20,16},{24,28},{28,24},{1,5},{5... | collective-permute-start | bytes 2359304 | tf_op jit(solution)/shard_map/ppermute | solution.py:117
  107.4 54.1 %copy-start.29 = (bf16[256,1536]{1,0:T(8,128)(2,1)}, bf16[256,1536]{1,0:T(8,128)(2,1)S(1)}, u32[]{:S(2)}) copy-start(bf16[256,1536]{1,0:T(8,128)(2,1)S(1)} %collective-permute-done.10.refs_4_) | copy-start | bytes 2359300
  107.4 54.1 %collective-permute-start.11 = (bf16[256,1536]{1,0:T(8,128)(2,1)S(1)}, bf16[256,1536]{1,0:T(8,128)(2,1)}, u32[]{:S(2)}, u32[]{:S(2)}) collective-permute-start(bf16[256,1536]{1,0:T(8,128)(2,1)S(1)} %collective-permute-done.10.refs_4_), channel_id=1, source_target_pairs={{0,4},{4,0},{8,12},{12,8},{16,20},{20,16},{24,28},{28,24},{1,5},{5... | collective-permute-start | bytes 2359304 | tf_op jit(solution)/shard_map/ppermute | solution.py:117
  107.4 54.1 %collective-permute-start.13 = (bf16[256,1536]{1,0:T(8,128)(2,1)}, bf16[256,1536]{1,0:T(8,128)(2,1)}, u32[]{:S(2)}, u32[]{:S(2)}) collective-permute-start(bf16[256,1536]{1,0:T(8,128)(2,1)} %collective-permute-done.12.refs_6_), channel_id=1, source_target_pairs={{0,4},{4,0},{8,12},{12,8},{16,20},{20,16},{24,28},{28,24},{1,5},{5... | collective-permute-start | bytes 2359304 | tf_op jit(solution)/shard_map/ppermute | solution.py:117
  107.9 21.8 %collective-permute-start.16 = (bf16[64,1024]{1,0:T(8,128)(2,1)S(1)}, bf16[64,1024]{1,0:T(8,128)(2,1)S(1)}, u32[]{:S(2)}, u32[]{:S(2)}) collective-permute-start(bf16[64,1024]{1,0:T(8,128)(2,1)S(1)} %copy-done.36), channel_id=1, source_target_pairs={{0,1},{1,2},{2,3},{3,0},{4,5},{5,6},{6,7},{7,4},{8,9},{9,10},{10,1... | collective-permute-start | bytes 393224 | tf_op jit(solution)/shard_map/ppermute | solution.py:505
  129.7 25.7 %copy-start.23 = (bf16[64,1024]{1,0:T(8,128)(2,1)}, bf16[64,1024]{1,0:T(8,128)(2,1)S(1)}, u32[]{:S(2)}) copy-start(bf16[64,1024]{1,0:T(8,128)(2,1)S(1)} %collective-permute-done.16.refs_1_) | copy-start | bytes 393220
  129.7 19.4 %collective-permute-start.17 = (bf16[64,1024]{1,0:T(8,128)(2,1)S(1)}, bf16[64,1024]{1,0:T(8,128)(2,1)S(1)}, u32[]{:S(2)}, u32[]{:S(2)}) collective-permute-start(bf16[64,1024]{1,0:T(8,128)(2,1)S(1)} %copy-done.35), channel_id=1, source_target_pairs={{0,2},{1,3},{2,0},{3,1},{4,6},{5,7},{6,4},{7,5},{8,10},{9,11},{10,... | collective-permute-start | bytes 393224 | tf_op jit(solution)/shard_map/ppermute | solution.py:505
  149.1 6.3 %copy-start.24 = (bf16[64,1024]{1,0:T(8,128)(2,1)}, bf16[64,1024]{1,0:T(8,128)(2,1)S(1)}, u32[]{:S(2)}) copy-start(bf16[64,1024]{1,0:T(8,128)(2,1)S(1)} %collective-permute-done.17.refs_2_) | copy-start | bytes 393220
  149.1 6.3 %collective-permute-start.18 = (bf16[64,1024]{1,0:T(8,128)(2,1)S(1)}, bf16[64,1024]{1,0:T(8,128)(2,1)S(1)}, u32[]{:S(2)}, u32[]{:S(2)}) collective-permute-start(bf16[64,1024]{1,0:T(8,128)(2,1)S(1)} %copy-done.34), channel_id=1, source_target_pairs={{0,3},{1,0},{2,1},{3,2},{4,7},{5,4},{6,5},{7,6},{8,11},{9,8},{10,9... | collective-permute-start | bytes 393224 | tf_op jit(solution)/shard_map/ppermute | solution.py:505
  158.0 19.5 %collective-permute-start.20 = (bf16[256,1024]{1,0:T(8,128)(2,1)}, bf16[256,1024]{1,0:T(8,128)(2,1)S(1)}, u32[]{:S(2)}, u32[]{:S(2)}) collective-permute-start(bf16[256,1024]{1,0:T(8,128)(2,1)} %assemble.3.refs_0_), channel_id=1, source_target_pairs={{0,8},{4,12},{8,0},{12,4},{16,24},{20,28},{24,16},{28,20},{1,9},{5... | collective-permute-start | bytes 1572872 | tf_op jit(solution)/shard_map/ppermute | solution.py:117
  159.7 24.4 %collective-permute-start.22 = (bf16[256,1024]{1,0:T(8,128)(2,1)}, bf16[256,1024]{1,0:T(8,128)(2,1)S(1)}, u32[]{:S(2)}, u32[]{:S(2)}) collective-permute-start(bf16[256,1024]{1,0:T(8,128)(2,1)} %assemble.3.refs_0_), channel_id=1, source_target_pairs={{0,16},{4,20},{8,24},{12,28},{16,0},{20,4},{24,8},{28,12},{1,17},{... | collective-permute-start | bytes 1572872 | tf_op jit(solution)/shard_map/ppermute | solution.py:117
  160.3 23.8 %collective-permute-start.24 = (bf16[256,1024]{1,0:T(8,128)(2,1)}, bf16[256,1024]{1,0:T(8,128)(2,1)S(1)}, u32[]{:S(2)}, u32[]{:S(2)}) collective-permute-start(bf16[256,1024]{1,0:T(8,128)(2,1)} %assemble.3.refs_0_), channel_id=1, source_target_pairs={{0,24},{4,28},{8,16},{12,20},{16,8},{20,12},{24,0},{28,4},{1,25},{... | collective-permute-start | bytes 1572872 | tf_op jit(solution)/shard_map/ppermute | solution.py:117
  161.5 13.0 %copy-start.1 = (bf16[256,1024]{1,0:T(8,128)(2,1)S(1)}, bf16[256,1024]{1,0:T(8,128)(2,1)}, u32[]{:S(2)}) copy-start(bf16[256,1024]{1,0:T(8,128)(2,1)} %assemble.3.refs_0_) | copy-start | bytes 1572868
  171.9 38.7 %collective-permute-start.14 = (bf16[2,512,512]{2,1,0:T(8,128)(2,1)}, bf16[2,512,512]{2,1,0:T(8,128)(2,1)S(1)}, u32[]{:S(2)}, u32[]{:S(2)}) collective-permute-start(bf16[2,512,512]{2,1,0:T(8,128)(2,1)} %slice.38), channel_id=1, source_target_pairs={{0,4},{4,8},{8,12},{12,16},{16,20},{20,24},{24,28},{1,5},{5,9},{9,... | collective-permute-start | bytes 3145736 | tf_op jit(solution)/shard_map/ppermute | solution.py:25
  174.5 22.2 %collective-permute-start.19 = (bf16[256,1024]{1,0:T(8,128)(2,1)S(1)}, bf16[256,1024]{1,0:T(8,128)(2,1)}, u32[]{:S(2)}, u32[]{:S(2)}) collective-permute-start(bf16[256,1024]{1,0:T(8,128)(2,1)S(1)} %copy-done.1), channel_id=1, source_target_pairs={{0,4},{4,0},{8,12},{12,8},{16,20},{20,16},{24,28},{28,24},{1,5},{5... | collective-permute-start | bytes 1572872 | tf_op jit(solution)/shard_map/ppermute | solution.py:117
  177.5 15.2 %copy-start.2 = (bf16[256,1024]{1,0:T(8,128)(2,1)}, bf16[256,1024]{1,0:T(8,128)(2,1)S(1)}, u32[]{:S(2)}) copy-start(bf16[256,1024]{1,0:T(8,128)(2,1)S(1)} %collective-permute-done.20.refs_2_) | copy-start | bytes 1572868
  177.5 38.1 %collective-permute-start.21 = (bf16[256,1024]{1,0:T(8,128)(2,1)S(1)}, bf16[256,1024]{1,0:T(8,128)(2,1)}, u32[]{:S(2)}, u32[]{:S(2)}) collective-permute-start(bf16[256,1024]{1,0:T(8,128)(2,1)S(1)} %collective-permute-done.20.refs_2_), channel_id=1, source_target_pairs={{0,4},{4,0},{8,12},{12,8},{16,20},{20,16},{24,28},{28,24},{1,5},{5... | collective-permute-start | bytes 1572872 | tf_op jit(solution)/shard_map/ppermute | solution.py:117
  184.1 8.6 %copy-start.3 = (bf16[256,1024]{1,0:T(8,128)(2,1)}, bf16[256,1024]{1,0:T(8,128)(2,1)S(1)}, u32[]{:S(2)}) copy-start(bf16[256,1024]{1,0:T(8,128)(2,1)S(1)} %collective-permute-done.22.refs_4_) | copy-start | bytes 1572868
  184.1 32.6 %collective-permute-start.23 = (bf16[256,1024]{1,0:T(8,128)(2,1)S(1)}, bf16[256,1024]{1,0:T(8,128)(2,1)}, u32[]{:S(2)}, u32[]{:S(2)}) collective-permute-start(bf16[256,1024]{1,0:T(8,128)(2,1)S(1)} %collective-permute-done.22.refs_4_), channel_id=1, source_target_pairs={{0,4},{4,0},{8,12},{12,8},{16,20},{20,16},{24,28},{28,24},{1,5},{5... | collective-permute-start | bytes 1572872 | tf_op jit(solution)/shard_map/ppermute | solution.py:117
  184.1 8.6 %copy-start.4 = (bf16[256,1024]{1,0:T(8,128)(2,1)}, bf16[256,1024]{1,0:T(8,128)(2,1)S(1)}, u32[]{:S(2)}) copy-start(bf16[256,1024]{1,0:T(8,128)(2,1)S(1)} %collective-permute-done.24.refs_6_) | copy-start | bytes 1572868
  184.1 32.6 %collective-permute-start.25 = (bf16[256,1024]{1,0:T(8,128)(2,1)S(1)}, bf16[256,1024]{1,0:T(8,128)(2,1)}, u32[]{:S(2)}, u32[]{:S(2)}) collective-permute-start(bf16[256,1024]{1,0:T(8,128)(2,1)S(1)} %collective-permute-done.24.refs_6_), channel_id=1, source_target_pairs={{0,4},{4,0},{8,12},{12,8},{16,20},{20,16},{24,28},{28,24},{1,5},{5... | collective-permute-start | bytes 1572872 | tf_op jit(solution)/shard_map/ppermute | solution.py:117
  196.7 20.0 %collective-permute-start.31 = (bf16[256,512]{1,0:T(8,128)(2,1)}, bf16[256,512]{1,0:T(8,128)(2,1)S(1)}, u32[]{:S(2)}, u32[]{:S(2)}) collective-permute-start(bf16[256,512]{1,0:T(8,128)(2,1)} %attend.6.own_ref), channel_id=1, source_target_pairs={{0,1},{1,0},{2,3},{3,2},{4,5},{5,4},{6,7},{7,6},{8,9},{9,8},{10,11... | collective-permute-start | bytes 786440 | tf_op jit(solution)/shard_map/ppermute | solution.py:117
  210.6 20.7 %collective-permute-start.34 = (bf16[256,512]{1,0:T(8,128)(2,1)}, bf16[256,512]{1,0:T(8,128)(2,1)S(1)}, u32[]{:S(2)}, u32[]{:S(2)}) collective-permute-start(bf16[256,512]{1,0:T(8,128)(2,1)} %attend.7.own_ref), channel_id=1, source_target_pairs={{0,1},{1,0},{2,3},{3,2},{4,5},{5,4},{6,7},{7,6},{8,9},{9,8},{10,11... | collective-permute-start | bytes 786440 | tf_op jit(solution)/shard_map/ppermute | solution.py:117
  215.6 23.0 %collective-permute-start.28 = (bf16[256,512]{1,0:T(8,128)(2,1)}, bf16[256,512]{1,0:T(8,128)(2,1)S(1)}, u32[]{:S(2)}, u32[]{:S(2)}) collective-permute-start(bf16[256,512]{1,0:T(8,128)(2,1)} %attend.5.own_ref), channel_id=1, source_target_pairs={{0,1},{1,0},{2,3},{3,2},{4,5},{5,4},{6,7},{7,6},{8,9},{9,8},{10,11... | collective-permute-start | bytes 786440 | tf_op jit(solution)/shard_map/ppermute | solution.py:117
  222.1 22.7 %collective-permute-start.32 = (bf16[256,512]{1,0:T(8,128)(2,1)}, bf16[256,512]{1,0:T(8,128)(2,1)S(1)}, u32[]{:S(2)}, u32[]{:S(2)}) collective-permute-start(bf16[256,512]{1,0:T(8,128)(2,1)} %get-tuple-element.72), channel_id=1, source_target_pairs={{1,2},{2,1},{5,6},{6,5},{9,10},{10,9},{13,14},{14,13},{17,18},{18,... | collective-permute-start | bytes 786440 | tf_op jit(solution)/shard_map/ppermute | solution.py:551
  226.8 11.8 %copy-start.30 = (bf16[256,512]{1,0:T(8,128)(2,1)S(1)}, bf16[256,512]{1,0:T(8,128)(2,1)}, u32[]{:S(2)}) copy-start(bf16[256,512]{1,0:T(8,128)(2,1)} %get-tuple-element.73) | copy-start | bytes 786436
  226.8 18.7 %collective-permute-start.15 = (bf16[256,512]{1,0:T(8,128)(2,1)}, bf16[256,512]{1,0:T(8,128)(2,1)S(1)}, u32[]{:S(2)}, u32[]{:S(2)}) collective-permute-start(bf16[256,512]{1,0:T(8,128)(2,1)} %attend.4.own_ref), channel_id=1, source_target_pairs={{0,1},{1,0},{2,3},{3,2},{4,5},{5,4},{6,7},{7,6},{8,9},{9,8},{10,11... | collective-permute-start | bytes 786440 | tf_op jit(solution)/shard_map/ppermute | solution.py:117
  236.6 14.9 %collective-permute-start.35 = (bf16[256,512]{1,0:T(8,128)(2,1)}, bf16[256,512]{1,0:T(8,128)(2,1)S(1)}, u32[]{:S(2)}, u32[]{:S(2)}) collective-permute-start(bf16[256,512]{1,0:T(8,128)(2,1)} %get-tuple-element.75), channel_id=1, source_target_pairs={{1,2},{2,1},{5,6},{6,5},{9,10},{10,9},{13,14},{14,13},{17,18},{18,... | collective-permute-start | bytes 786440 | tf_op jit(solution)/shard_map/ppermute | solution.py:551
  237.3 15.7 %collective-permute-start.36 = (bf16[256,512]{1,0:T(8,128)(2,1)}, bf16[256,512]{1,0:T(8,128)(2,1)S(1)}, u32[]{:S(2)}, u32[]{:S(2)}) collective-permute-start(bf16[256,512]{1,0:T(8,128)(2,1)} %get-tuple-element.76), channel_id=1, source_target_pairs={{1,3},{2,0},{5,7},{6,4},{9,11},{10,8},{13,15},{14,12},{17,19},{18,... | collective-permute-start | bytes 786440 | tf_op jit(solution)/shard_map/ppermute | solution.py:552
  238.6 1.5 copy-start.11
  238.6 20.0 %collective-permute-start.33 = (bf16[256,512]{1,0:T(8,128)(2,1)S(1)}, bf16[256,512]{1,0:T(8,128)(2,1)S(1)}, u32[]{:S(2)}, u32[]{:S(2)}) collective-permute-start(bf16[256,512]{1,0:T(8,128)(2,1)S(1)} %copy-done.30), channel_id=1, source_target_pairs={{1,3},{2,0},{5,7},{6,4},{9,11},{10,8},{13,15},{14,12},{17,19},{18,... | collective-permute-start | bytes 786440 | tf_op jit(solution)/shard_map/ppermute | solution.py:552
  244.8 13.8 %copy-start.14 = (bf16[256,512]{1,0:T(8,128)(2,1)}, bf16[256,512]{1,0:T(8,128)(2,1)S(1)}, u32[]{:S(2)}) copy-start(bf16[256,512]{1,0:T(8,128)(2,1)S(1)} %collective-permute-done.32.inner_ref) | copy-start | bytes 786436
  244.8 17.9 %collective-permute-start.29 = (bf16[256,512]{1,0:T(8,128)(2,1)}, bf16[256,512]{1,0:T(8,128)(2,1)S(1)}, u32[]{:S(2)}, u32[]{:S(2)}) collective-permute-start(bf16[256,512]{1,0:T(8,128)(2,1)} %get-tuple-element.69), channel_id=1, source_target_pairs={{1,2},{2,1},{5,6},{6,5},{9,10},{10,9},{13,14},{14,13},{17,18},{18,... | collective-permute-start | bytes 786440 | tf_op jit(solution)/shard_map/ppermute | solution.py:551
  245.5 1.3 copy-start.10
  245.5 24.3 %collective-permute-start.30 = (bf16[256,512]{1,0:T(8,128)(2,1)}, bf16[256,512]{1,0:T(8,128)(2,1)S(1)}, u32[]{:S(2)}, u32[]{:S(2)}) collective-permute-start(bf16[256,512]{1,0:T(8,128)(2,1)} %get-tuple-element.70), channel_id=1, source_target_pairs={{1,3},{2,0},{5,7},{6,4},{9,11},{10,8},{13,15},{14,12},{17,19},{18,... | collective-permute-start | bytes 786440 | tf_op jit(solution)/shard_map/ppermute | solution.py:552
  251.5 2.8 copy-start.8
  251.5 22.5 %collective-permute-start.26 = (bf16[256,512]{1,0:T(8,128)(2,1)}, bf16[256,512]{1,0:T(8,128)(2,1)S(1)}, u32[]{:S(2)}, u32[]{:S(2)}) collective-permute-start(bf16[256,512]{1,0:T(8,128)(2,1)} %get-tuple-element.66), channel_id=1, source_target_pairs={{1,2},{2,1},{5,6},{6,5},{9,10},{10,9},{13,14},{14,13},{17,18},{18,... | collective-permute-start | bytes 786440 | tf_op jit(solution)/shard_map/ppermute | solution.py:551
  253.0 26.1 %collective-permute-start.27 = (bf16[256,512]{1,0:T(8,128)(2,1)}, bf16[256,512]{1,0:T(8,128)(2,1)S(1)}, u32[]{:S(2)}, u32[]{:S(2)}) collective-permute-start(bf16[256,512]{1,0:T(8,128)(2,1)} %get-tuple-element.67), channel_id=1, source_target_pairs={{1,3},{2,0},{5,7},{6,4},{9,11},{10,8},{13,15},{14,12},{17,19},{18,... | collective-permute-start | bytes 786440 | tf_op jit(solution)/shard_map/ppermute | solution.py:552
  262.7 7.2 %copy-start.16 = (bf16[256,512]{1,0:T(8,128)(2,1)}, bf16[256,512]{1,0:T(8,128)(2,1)S(1)}, u32[]{:S(2)}) copy-start(bf16[256,512]{1,0:T(8,128)(2,1)S(1)} %collective-permute-done.29.inner_ref) | copy-start | bytes 786436
  273.9 5.2 %copy-start.18 = (bf16[256,512]{1,0:T(8,128)(2,1)}, bf16[256,512]{1,0:T(8,128)(2,1)S(1)}, u32[]{:S(2)}) copy-start(bf16[256,512]{1,0:T(8,128)(2,1)S(1)} %collective-permute-done.26.inner_ref) | copy-start | bytes 786436
  (12 other events, 9.8 us)
Sparse Core Ops, SparseCore 0:
  36.1 59.9 all-gather.4
  97.7 56.7 all-gather.2

commit v5 on v4

--- a/solution.py
+++ b/solution.py
@@ -62,51 +62,56 @@
 
 
 def regroup_kernel(place_ref, master_ref, *parts):
-    servers = len(parts) // 2
+    servers = len(parts)
     width = master_ref.shape[-1] // servers
-    for step in range(servers):
+    for step, part_ref in enumerate(parts):
         server = (place_ref[0] + step) % servers
         own = pl.ds(pl.multiple_of(server * width, width), width)
         pair = pl.ds(pl.multiple_of((server // 2) * 2 * width, 2 * width), 2 * width)
         for slot in range(3):
-            parts[step][:, slot * width : (slot + 1) * width] = master_ref[:, slot, own].astype(BF)
-        parts[servers + step][...] = master_ref[:, 3, pair].astype(BF)
+            part_ref[:, slot * width : (slot + 1) * width] = master_ref[:, slot, own].astype(BF)
+        part_ref[:, 3 * width :] = master_ref[:, 3, pair].astype(BF)
 
 
 def regroup(place, master, servers):
     rows, _, total = master.shape
-    width = total // servers
-    parts = pl.pallas_call(
+    columns = 5 * total // servers
+    return pl.pallas_call(
         regroup_kernel,
         in_specs=[pl.BlockSpec(memory_space=pltpu.SMEM), pl.BlockSpec(memory_space=pltpu.VMEM)],
-        out_specs=[pl.BlockSpec(memory_space=pltpu.VMEM)] * (2 * servers),
-        out_shape=[jax.ShapeDtypeStruct((rows, 3 * width), BF)] * servers
-        + [jax.ShapeDtypeStruct((rows, 2 * width), BF)] * servers,
+        out_specs=[pl.BlockSpec(memory_space=pltpu.VMEM)] * servers,
+        out_shape=[jax.ShapeDtypeStruct((rows, columns), BF)] * servers,
         cost_estimate=cost(0, rows * total * 26),
         compiler_params=params(),
         name="regroup",
     )(place, master)
-    return list(parts[:servers]), list(parts[servers:])
 
 
 def assemble_kernel(place_ref, *refs):
-    out_ref = refs[-1]
-    parts = refs[:-1]
+    qkv_ref, out_ref = refs[-2:]
+    parts = refs[:-2]
     rows = parts[0].shape[0]
+    cut = qkv_ref.shape[1]
     for step, part_ref in enumerate(parts):
         source = (place_ref[0] + len(parts) - step) % len(parts)
-        out_ref[pl.ds(pl.multiple_of(source * rows, rows), rows), :] = part_ref[...]
+        at = pl.ds(pl.multiple_of(source * rows, rows), rows)
+        qkv_ref[at, :] = part_ref[:, :cut]
+        out_ref[at, :] = part_ref[:, cut:]
 
 
 def assemble(place, parts):
     rows, columns = parts[0].shape
+    rows *= len(parts)
     return pl.pallas_call(
         assemble_kernel,
         in_specs=[pl.BlockSpec(memory_space=pltpu.SMEM)]
         + [pl.BlockSpec(memory_space=pltpu.VMEM)] * len(parts),
-        out_specs=pl.BlockSpec(memory_space=pltpu.VMEM),
-        out_shape=jax.ShapeDtypeStruct((rows * len(parts), columns), BF),
-        cost_estimate=cost(0, rows * columns * len(parts) * 4),
+        out_specs=[pl.BlockSpec(memory_space=pltpu.VMEM)] * 2,
+        out_shape=[
+            jax.ShapeDtypeStruct((rows, columns // 5 * 3), BF),
+            jax.ShapeDtypeStruct((rows, columns // 5 * 2), BF),
+        ],
+        cost_estimate=cost(0, rows * columns * 4),
         compiler_params=params(),
         name="assemble",
     )(place, *parts)
@@ -200,7 +205,12 @@
 
 def mix_kernel(offset, static_ref, x_ref, own_ref, a_ref, b_ref, c_ref, sums_ref, normed_ref):
     tokens, _, width = x_ref.shape
-    sums_ref[...] = (own_ref[...] + a_ref[...]) + (b_ref[...] + c_ref[...])
+
+    @pl.when(pl.program_id(0) == 0)
+    def _():
+        sums_ref[...] = (own_ref[...] + a_ref[...]) + (b_ref[...] + c_ref[...])
+
+    base = 4 * (offset + pl.program_id(0) * tokens)
     last = sums_ref.shape[1] - 128
     column = sums_ref[0:1, last : last + 1]
     stream = lax.broadcasted_iota(jnp.int32, (1, 4 * STEP), 1) & 3
@@ -210,7 +220,7 @@
 
     @pl.loop(0, tokens // STEP)
     def _(step):
-        at = pl.multiple_of(4 * offset + step * 4 * STEP, 4 * STEP)
+        at = pl.multiple_of(base + step * 4 * STEP, 4 * STEP)
         first = sums_ref[:, pl.ds(at, 4 * STEP)]
         mean, inverse = centre(first)
         mix = static + jnp.tanh(inverse * (first[0:1] - mean * column))
@@ -238,13 +248,13 @@
     whole = pl.BlockSpec((8, lanes), lambda i: (0, 0))
     return pl.pallas_call(
         functools.partial(mix_kernel, start),
-        grid=(1,),
+        grid=(tokens // CHUNK,),
         in_specs=[
             pl.BlockSpec(memory_space=pltpu.SMEM),
-            pl.BlockSpec((tokens, 4, width), lambda i: (start // tokens, 0, 0)),
+            pl.BlockSpec((CHUNK, 4, width), lambda i: (start // CHUNK + i, 0, 0)),
         ]
         + [whole] * 4,
-        out_specs=[whole, pl.BlockSpec((tokens, width), lambda i: (0, 0))],
+        out_specs=[whole, pl.BlockSpec((CHUNK, width), lambda i: (i, 0))],
         out_shape=[
             jax.ShapeDtypeStruct((8, lanes), F32),
             jax.ShapeDtypeStruct((tokens, width), BF),
@@ -286,9 +296,9 @@
         out_ref[0] = total.astype(BF)
 
 
-def qkv_columns(ring, rows, pieces, cosine, sine, start):
+def qkv_columns(ring, rows, pieces, cosine, sine):
     servers, tokens, width = rows.shape
-    table = pl.BlockSpec((tokens, HEAD_DIM), lambda j: (start // tokens, 0))
+    table = pl.BlockSpec((tokens, HEAD_DIM), lambda j: (0, 0))
     return pl.pallas_call(
         qkv_kernel,
         grid=(3,),
@@ -488,29 +498,26 @@
         [hc_proj.T, jnp.ones((1, width), F32), jnp.zeros((1, width), F32)], axis=0
     )
     own = stats(streams, proj_rows)
-    qkv_parts, out_parts = regroup(place, proj_master, group_size)
-    sums, qkv_parts = lax.optimization_barrier(([own] + from_others(own, "mp"), qkv_parts))
+    parts = list(regroup(place, proj_master, group_size))
+    sums, parts = lax.optimization_barrier(([own] + from_others(own, "mp"), parts))
 
     def gathered(normed):
         rows = lax.all_gather(normed, "mp", axis=0, tiled=True)
         return rows.reshape(group_size, normed.shape[0], width)
 
-    sums_late, normed_late = mix(hc_static, streams, sums, BLOCK, BLOCK)
+    sums_all, normed_late = mix(hc_static, streams, sums, CHUNK, tokens_local - CHUNK)
     rows_late = gathered(normed_late)
-    _, normed_early = mix(hc_static, streams, sums, 0, BLOCK)
-    rows_early = gathered(normed_early)
-
-    def served(parts):
-        for step in range(1, group_size):
-            parts[step] = lax.ppermute(
-                parts[step], "mp", [(at, (at + step) % group_size) for at in range(group_size)]
-            )
-        return assemble(place, parts)
-
-    qkv_part = served(qkv_parts)
-    qkv_part, out_parts, normed_early = lax.optimization_barrier((qkv_part, out_parts, normed_early))
+    _, normed_first = mix(hc_static, streams, sums, 0, CHUNK)
+    rows_first = gathered(normed_first)
+
+    for step in range(1, group_size):
+        parts[step] = lax.ppermute(
+            parts[step], "mp", [(at, (at + step) % group_size) for at in range(group_size)]
+        )
+    qkv_part, out_part = assemble(place, parts)
     qkv_pieces = weight_pieces(qkv_part)
-    out_pieces = weight_pieces(served(out_parts))
+    out_part, qkv_pieces = lax.optimization_barrier((out_part, qkv_pieces))
+    out_pieces = weight_pieces(out_part)
 
     halo = passed_along(segment_ids[-BLOCK:], "blk", 1)
     halo = jnp.where(lax.axis_index("blk") == 0, -1, halo)
@@ -535,23 +542,34 @@
     key_segments = jnp.stack(windows)[:, None, :]
     query_segments = segment_ids[:, None]
 
-    qkv_late = qkv_columns(ring, rows_late, qkv_pieces, cosine, sine, BLOCK)
-    halo_rows = passed_along(qkv_late[1:3], "blk", 1)
-    qkv_early = qkv_columns(ring, rows_early, qkv_pieces, cosine, sine, 0)
-
-    chunks = [(halo_rows, 0, 0), (halo_rows, 0, 1), (qkv_early, 1, 0), (qkv_early, 1, 1)]
-    chunks += [(qkv_late, 1, 0), (qkv_late, 1, 1)]
+    qkv_late = qkv_columns(ring, rows_late, qkv_pieces, cosine[CHUNK:], sine[CHUNK:])
+    halo_rows = passed_along(qkv_late[1:3, -BLOCK:], "blk", 1)
+
+    last = tokens_local // CHUNK - 1
+    late_chunks = [(qkv_late, 1, at) for at in range(last)]
+
+    def attended_chunk(chunk, window):
+        source, _, at = window[-1]
+        return attend((source, at), window, query_segments, key_segments, chunk)
+
+    def projected(own):
+        other = swapped(own, "mp", 1)
+        return project(place, ring, own, other, out_pieces, group_size)
+
+    parts = {last: projected(attended_chunk(last, late_chunks[-3:]))}
+    rows_first, parts[last] = lax.optimization_barrier((rows_first, parts[last]))
+    qkv_first = qkv_columns(ring, rows_first, qkv_pieces, cosine[:CHUNK], sine[:CHUNK])
+    chunks = [(halo_rows, 0, 0), (halo_rows, 0, 1), (qkv_first, 1, 0)] + late_chunks
+    for chunk in reversed(range(last)):
+        parts[chunk] = projected(attended_chunk(chunk, chunks[chunk : chunk + 3]))
+
     result = None
-    for chunk in (2, 3, 0, 1):
-        source, _, at = chunks[chunk + 2]
-        window = chunks[chunk : chunk + 3]
-        attended = attend((source, at), window, query_segments, key_segments, chunk)
-        other = swapped(attended, "mp", 1)
-        kept, inner, outer = project(place, ring, attended, other, out_pieces, group_size)
+    for chunk in reversed(range(last + 1)):
+        kept, inner, outer = parts[chunk]
         inner = lax.ppermute(inner, "mp", [(1, 2), (2, 1)])
         outer = lax.ppermute(outer, "mp", [(1, 3), (2, 0)])
         updates = [kept, inner, outer]
-        result = final(hc_static, streams, sums_late, updates, chunk * CHUNK, result)
+        result = final(hc_static, streams, sums_all, updates, chunk * CHUNK, result)
     return result
 
 

time: 291 us -> 292 us (level)
  starting transfers between devices: 73.7 us -> 64.9 us
  waiting for transfers between devices: 96.1 us -> 104 us
    ppermute x6 -> x3, starting transfers between devices: 27.9 us -> 6.5 us  [body(): lax.ppermute(parts[step], 'mp', [(at, (at + step) % group_size) for at in...]
    ppermute x18, waiting for transfers between devices: 34.8 us -> 51 us  [swapped(): lax.ppermute(value, axis, [(source, source ^ mask) for source in range(co...]
    ppermute x18, starting transfers between devices: 28 us -> 39.4 us  [swapped(): lax.ppermute(value, axis, [(source, source ^ mask) for source in range(co...]
    ppermute x6 -> x3, waiting for transfers between devices: 42.2 us -> 35.2 us  [body(): lax.ppermute(parts[step], 'mp', [(at, (at + step) % group_size) for at in...]
  transfers between devices with their start and end apart: 39 -> 36, of which waited for: 14 -> 12; matrix products, arithmetic and copies ran while one was open for 3% -> 4% of each run, Pallas kernels for 26% -> 25%
where the time goes in v5:
time: 292 us; the launch traced here: 291 us
  waiting for transfers between devices  104 us (36%)
  Pallas kernels  86.5 us (30%)
  starting transfers between devices  64.9 us (22%)
  between operations  15.2 us (5%)
  local copies, waits for them, and re-layouts  11.5 us (4%)
  other arithmetic  8.21 us (3%)
    ppermute x18, waiting for transfers between devices, swapped(): lax.ppermute(value, axis, [(source, source ^ mask) for source in range(co...  51 us
    ppermute x18, starting transfers between devices, swapped(): lax.ppermute(value, axis, [(source, source ^ mask) for source in range(co...  39.4 us
    ppermute x3, waiting for transfers between devices, body(): lax.ppermute(parts[step], 'mp', [(at, (at + step) % group_size) for at in...  35.2 us
    pallas_call x4, Pallas kernels, project(): pl.pallas_call(project_kernel, grid=(1,), in_specs=[pl.BlockSpec(memory_s...  18.5 us
    pallas_call x2, Pallas kernels, qkv_columns(): pl.pallas_call(qkv_kernel, grid=(3,), in_specs=[pl.BlockSpec(memory_space...  16.7 us
    pallas_call x4, Pallas kernels, attend(): pl.pallas_call(attend_kernel, grid=(1,), in_specs=[pl.BlockSpec(block, la...  16.2 us
    pallas_call x4, Pallas kernels, final(): pl.pallas_call(final_kernel, grid=(tokens // STEP,), in_specs=specs, out_...  13.6 us
    ppermute x4, waiting for transfers between devices, body(): outer = lax.ppermute(outer, 'mp', [(1, 3), (2, 0)])  13.3 us
  transfers between devices with their start and end apart: 36, of which 12 were waited for; matrix products, arithmetic and copies ran while one was open for 4% of the time, Pallas kernels for 25%

profile of v5, /device:TPU:0, one launch (start us, length us, event | category | flops | bytes accessed | tf_op | source)
XLA Modules:
  0.0 290.8 jit_solution(15065914000356673719)
XLA Ops:
  6.7 1.4 maximum_maximum_fusion.proj_ref
  8.1 6.4 %stats.1.own_ref = f32[8,5248]{1,0:T(8,128)} custom-call(bf16[1024,4,512]{2,1,0:T(4,128)(2,1)} %x_ref.13, f32[8,512]{1,0:T(8,128)} %maximum_maximum_fusion.proj_ref), custom_call_target="tpu_custom_call" | custom-call | flops 1258291200 | bytes 4194304 | tf_op jit(solution)/shard_map/stats/pallas_call | solution.py:178
  14.5 3.0 %collective-permute-start = (f32[8,5248]{1,0:T(8,128)}, f32[8,5248]{1,0:T(8,128)S(1)}, u32[]{:S(2)}, u32[]{:S(2)}) collective-permute-start(f32[8,5248]{1,0:T(8,128)} %stats.1.own_ref), channel_id=1, source_target_pairs={{0,1},{1,2},{2,3},{3,0},{4,5},{5,6},{6,7},{7,4},{8,9},{9,10},{10,1... | collective-permute-start | bytes 503816 | tf_op jit(solution)/shard_map/ppermute | solution.py:31
  17.5 2.6 collective-permute-start.1
  20.1 1.3 collective-permute-start.2
  21.4 4.9 %regroup.1 = (bf16[64,2560]{1,0:T(8,128)(2,1)}, bf16[64,2560]{1,0:T(8,128)(2,1)}, bf16[64,2560]{1,0:T(8,128)(2,1)}, bf16[64,2560]{1,0:T(8,128)(2,1)}) custom-call(s32[1]{0:T(128)} %bitcast.1.place_ref, f32[64,4,2048]{2,1,0:T(4,128)} %master_ref.1), custom_call_target="tpu_custom_call" | custom-call | bytes 3407872 | tf_op jit(solution)/shard_map/regroup/pallas_call | solution.py:79
  26.4 4.9 %collective-permute-done.1.b_ref = f32[8,5248]{1,0:T(8,128)S(1)} collective-permute-done((f32[8,5248]{1,0:T(8,128)}, f32[8,5248]{1,0:T(8,128)S(1)}, u32[]{:S(2)}, u32[]{:S(2)}) %collective-permute-start.1) | collective-permute-done | bytes 167968 | tf_op jit(solution)/shard_map/ppermute | solution.py:31
  32.0 4.9 %mix.2 = (f32[8,5248]{1,0:T(8,128)}, bf16[768,512]{1,0:T(8,128)(2,1)}) custom-call(f32[4,6]{1,0:T(4,128)} %static_ref.11, bf16[1024,4,512]{2,1,0:T(4,128)(2,1)} %x_ref.13, f32[8,5248]{1,0:T(8,128)} %stats.1.own_ref, f32[8,5248]{1,0:T(8,128)} %copy-done.12, f32[8,5248]{1,0:T(8,128)} %copy-done.13, f32[8,5248]{1,0:T(8,128)} %copy-done.14), custom_call_target="tpu_custom_call" | custom-call | flops 629145600 | bytes 3932160 | tf_op jit(solution)/shard_map/mix/pallas_call | solution.py:249
  37.0 4.1 %collective-permute-start.4 = (bf16[64,2560]{1,0:T(8,128)(2,1)S(1)}, bf16[64,2560]{1,0:T(8,128)(2,1)S(1)}, u32[]{:S(2)}, u32[]{:S(2)}) collective-permute-start(bf16[64,2560]{1,0:T(8,128)(2,1)S(1)} %copy-done.34), channel_id=1, source_target_pairs={{0,1},{1,2},{2,3},{3,0},{4,5},{5,6},{6,7},{7,4},{8,9},{9,10},{10,1... | collective-permute-start | bytes 983048 | tf_op jit(solution)/shard_map/ppermute | solution.py:514
  41.0 1.7 collective-permute-start.5
  42.7 0.7 collective-permute-start.6
  43.5 7.5 %collective-permute-done.4.refs_1_ = bf16[64,2560]{1,0:T(8,128)(2,1)S(1)} collective-permute-done((bf16[64,2560]{1,0:T(8,128)(2,1)S(1)}, bf16[64,2560]{1,0:T(8,128)(2,1)S(1)}, u32[]{:S(2)}, u32[]{:S(2)}) %collective-permute-start.4) | collective-permute-done | bytes 327712 | tf_op jit(solution)/shard_map/ppermute | solution.py:514
  50.9 27.7 %collective-permute-done.5.refs_2_ = bf16[64,2560]{1,0:T(8,128)(2,1)S(1)} collective-permute-done((bf16[64,2560]{1,0:T(8,128)(2,1)S(1)}, bf16[64,2560]{1,0:T(8,128)(2,1)S(1)}, u32[]{:S(2)}, u32[]{:S(2)}) %collective-permute-start.5) | collective-permute-done | bytes 327712 | tf_op jit(solution)/shard_map/ppermute | solution.py:514
  78.6 0.7 copy-done.16
  79.4 0.7 copy-done.17
  80.1 2.4 assemble.1
  82.5 1.5 collective-permute-start.8
  84.0 1.5 collective-permute-start.10
  87.3 1.3 collective-permute-start.3
  88.6 2.3 collective-permute-start.7
  90.9 12.2 %collective-permute-done.8.refs_2_ = bf16[256,1536]{1,0:T(8,128)(2,1)S(1)} collective-permute-done((bf16[256,1536]{1,0:T(8,128)(2,1)}, bf16[256,1536]{1,0:T(8,128)(2,1)S(1)}, u32[]{:S(2)}, u32[]{:S(2)}) %collective-permute-start.8) | collective-permute-done | bytes 786464 | tf_op jit(solution)/shard_map/ppermute | solution.py:122
  103.2 16.9 %collective-permute-done.10.refs_4_ = bf16[256,1536]{1,0:T(8,128)(2,1)S(1)} collective-permute-done((bf16[256,1536]{1,0:T(8,128)(2,1)}, bf16[256,1536]{1,0:T(8,128)(2,1)S(1)}, u32[]{:S(2)}, u32[]{:S(2)}) %collective-permute-start.10) | collective-permute-done | bytes 786464 | tf_op jit(solution)/shard_map/ppermute | solution.py:122
  121.2 1.1 copy.14.qseg_ref
  122.3 1.6 convert_reduce_fusion
  124.0 0.8 collective-permute-start.16
  124.8 1.3 collective-permute-start.18
  126.1 1.4 collective-permute-start.20
  127.5 2.9 %mix.3 = (f32[8,5248]{1,0:T(8,128)}, bf16[256,512]{1,0:T(8,128)(2,1)}) custom-call(f32[4,6]{1,0:T(4,128)} %static_ref.11, bf16[1024,4,512]{2,1,0:T(4,128)(2,1)} %x_ref.13, f32[8,5248]{1,0:T(8,128)} %stats.1.own_ref, f32[8,5248]{1,0:T(8,128)} %copy-done.12, f32[8,5248]{1,0:T(8,128)} %copy-done.13, f32[8,5248]{1,0:T(8,128)} %copy-done.14), custom_call_target="tpu_custom_call" | custom-call | flops 209715200 | bytes 1310720 | tf_op jit(solution)/shard_map/mix/pallas_call | solution.py:249
  130.5 1.9 multiply_sine_fusion
  132.4 1.4 fusion.1
  133.8 5.2 %collective-permute-done.16.refs_2_ = bf16[256,1024]{1,0:T(8,128)(2,1)S(1)} collective-permute-done((bf16[256,1024]{1,0:T(8,128)(2,1)}, bf16[256,1024]{1,0:T(8,128)(2,1)S(1)}, u32[]{:S(2)}, u32[]{:S(2)}) %collective-permute-start.16) | collective-permute-done | bytes 524320 | tf_op jit(solution)/shard_map/ppermute | solution.py:122
  139.0 9.8 %collective-permute-done.18.refs_4_ = bf16[256,1024]{1,0:T(8,128)(2,1)S(1)} collective-permute-done((bf16[256,1024]{1,0:T(8,128)(2,1)}, bf16[256,1024]{1,0:T(8,128)(2,1)S(1)}, u32[]{:S(2)}, u32[]{:S(2)}) %collective-permute-start.18) | collective-permute-done | bytes 524320 | tf_op jit(solution)/shard_map/ppermute | solution.py:122
  148.8 1.5 collective-permute-done.20.refs_6_
  150.5 10.4 %qkv.2.q_ref.k0.k1.k2.v0.v1.v2 = bf16[3,768,512]{2,1,0:T(8,128)(2,1)} custom-call(s32[1]{0:T(128)} %bitcast.2.ring_ref, bf16[4,768,512]{2,1,0:T(8,128)(2,1)} %bitcast.13, f32[768,128]{1,0:T(8,128)} %get-tuple-element.104.cosine_ref, f32[768,128]{1,0:T(8,128)} %get-tuple-element.103.sine_ref, bf16[256,1536]{1,0:T(8,128)(2,1)} %get-tuple-element.64.refs_0_, ...), custom_call_target="tpu_custom_call" | custom-call | flops 4831838208 | bytes 14155776 | tf_op jit(solution)/shard_map/qkv/pallas_call | solution.py:302
  160.9 2.3 slice.58
  163.2 2.6 collective-permute-start.22
  166.4 4.1 %attend.4.own_ref = bf16[256,512]{1,0:T(8,128)(2,1)} custom-call(bf16[3,768,512]{2,1,0:T(8,128)(2,1)} %qkv.2.q_ref.k0.k1.k2.v0.v1.v2, bf16[3,768,512]{2,1,0:T(8,128)(2,1)} %qkv.2.q_ref.k0.k1.k2.v0.v1.v2, bf16[3,768,512]{2,1,0:T(8,128)(2,1)} %qkv.2.q_ref.k0.k1.k2.v0.v1.v2, bf16[3,768,512]{2,1,0:T(8,128)(2,1)} %qkv.2.q_ref.k0.k1.k2.v0.v1.v2, ...), custom_call_target="tpu_custom_call" | custom-call | flops 402653184 | bytes 2097152 | tf_op jit(solution)/shard_map/attend/pallas_call | solution.py:350
  170.5 24.3 %collective-permute-start.14 = (bf16[256,512]{1,0:T(8,128)(2,1)}, bf16[256,512]{1,0:T(8,128)(2,1)S(1)}, u32[]{:S(2)}, u32[]{:S(2)}) collective-permute-start(bf16[256,512]{1,0:T(8,128)(2,1)} %attend.4.own_ref), channel_id=1, source_target_pairs={{0,1},{1,0},{2,3},{3,2},{4,5},{5,4},{6,7},{7,6},{8,9},{9,8},{10,11... | collective-permute-start | bytes 786440 | tf_op jit(solution)/shard_map/ppermute | solution.py:122
  194.8 1.9 pad_maximum_fusion
  196.7 5.3 %collective-permute-done.14.other_ref = bf16[256,512]{1,0:T(8,128)(2,1)S(1)} collective-permute-done((bf16[256,512]{1,0:T(8,128)(2,1)}, bf16[256,512]{1,0:T(8,128)(2,1)S(1)}, u32[]{:S(2)}, u32[]{:S(2)}) %collective-permute-start.14) | collective-permute-done | bytes 262176 | tf_op jit(solution)/shard_map/ppermute | solution.py:122
  202.7 4.6 %project.4 = (f32[256,512]{1,0:T(8,128)}, bf16[256,512]{1,0:T(8,128)(2,1)}, bf16[256,512]{1,0:T(8,128)(2,1)}) custom-call(s32[1]{0:T(128)} %bitcast.1.place_ref, s32[1]{0:T(128)} %bitcast.2.ring_ref, bf16[256,512]{1,0:T(8,128)(2,1)} %attend.4.own_ref, bf16[256,512]{1,0:T(8,128)(2,1)} %copy-done.23, bf16[256,1024]{1,0:T(8,128)(2,1)} %get-tuple-element.72.refs_0_, ...), custom_call_target="tpu_custom_call" | custom-call | flops 1073741824 | bytes 5767168 | tf_op jit(solution)/shard_map/project/pallas_call | solution.py:399
  207.3 6.3 %qkv.3.q_ref.k2.v2.k1.v1.k0.v0 = bf16[3,256,512]{2,1,0:T(8,128)(2,1)} custom-call(s32[1]{0:T(128)} %bitcast.2.ring_ref, bf16[4,256,512]{2,1,0:T(8,128)(2,1)} %bitcast.10, f32[256,128]{1,0:T(8,128)} %get-tuple-element.106.cosine_ref, f32[256,128]{1,0:T(8,128)} %get-tuple-element.105.sine_ref, bf16[256,1536]{1,0:T(8,128)(2,1)} %get-tuple-element.64.refs_0_, ...), custom_call_target="tpu_custom_call" | custom-call | flops 1610612736 | bytes 8912896 | tf_op jit(solution)/shard_map/qkv/pallas_call | solution.py:302
  213.7 4.0 %attend.7.own_ref = bf16[256,512]{1,0:T(8,128)(2,1)} custom-call(bf16[3,768,512]{2,1,0:T(8,128)(2,1)} %qkv.2.q_ref.k0.k1.k2.v0.v1.v2, bf16[3,256,512]{2,1,0:T(8,128)(2,1)} %qkv.3.q_ref.k2.v2.k1.v1.k0.v0, bf16[3,768,512]{2,1,0:T(8,128)(2,1)} %qkv.2.q_ref.k0.k1.k2.v0.v1.v2, bf16[3,768,512]{2,1,0:T(8,128)(2,1)} %qkv.2.q_ref.k0.k1.k2.v0.v1.v2, ...), custom_call_target="tpu_custom_call" | custom-call | flops 402653184 | bytes 2097152 | tf_op jit(solution)/shard_map/attend/pallas_call | solution.py:350
  217.7 2.1 collective-permute-start.29
  219.8 1.0 copy-done
  220.7 4.0 %attend.6.own_ref = bf16[256,512]{1,0:T(8,128)(2,1)} custom-call(bf16[3,768,512]{2,1,0:T(8,128)(2,1)} %qkv.2.q_ref.k0.k1.k2.v0.v1.v2, bf16[2,512,512]{2,1,0:T(8,128)(2,1)} %copy-done, bf16[3,256,512]{2,1,0:T(8,128)(2,1)} %qkv.3.q_ref.k2.v2.k1.v1.k0.v0, bf16[3,768,512]{2,1,0:T(8,128)(2,1)} %qkv.2.q_ref.k0.k1.k2.v0.v1.v2, bf16[2,512,512]{2,1,0:T(8,128)(2,1)} %copy-done, ...), custom_call_target="tpu_custom_call" | custom-call | flops 402653184 | bytes 2097152 | tf_op jit(solution)/shard_map/attend/pallas_call | solution.py:350
  224.8 0.8 collective-permute-start.32
  225.6 4.0 %attend.5.own_ref = bf16[256,512]{1,0:T(8,128)(2,1)} custom-call(bf16[3,256,512]{2,1,0:T(8,128)(2,1)} %qkv.3.q_ref.k2.v2.k1.v1.k0.v0, bf16[2,512,512]{2,1,0:T(8,128)(2,1)} %copy-done, bf16[2,512,512]{2,1,0:T(8,128)(2,1)} %copy-done, bf16[3,256,512]{2,1,0:T(8,128)(2,1)} %qkv.3.q_ref.k2.v2.k1.v1.k0.v0, bf16[2,512,512]{2,1,0:T(8,128)(2,1)} %copy-done, ...), custom_call_target="tpu_custom_call" | custom-call | flops 402653184 | bytes 2097152 | tf_op jit(solution)/shard_map/attend/pallas_call | solution.py:350
  229.6 3.1 %collective-permute-start.23 = (bf16[256,512]{1,0:T(8,128)(2,1)}, bf16[256,512]{1,0:T(8,128)(2,1)S(1)}, u32[]{:S(2)}, u32[]{:S(2)}) collective-permute-start(bf16[256,512]{1,0:T(8,128)(2,1)} %attend.5.own_ref), channel_id=1, source_target_pairs={{0,1},{1,0},{2,3},{3,2},{4,5},{5,4},{6,7},{7,6},{8,9},{9,8},{10,11... | collective-permute-start | bytes 786440 | tf_op jit(solution)/shard_map/ppermute | solution.py:122
  232.8 1.3 collective-permute-start.33
  234.8 4.6 %project.7 = (f32[256,512]{1,0:T(8,128)}, bf16[256,512]{1,0:T(8,128)(2,1)}, bf16[256,512]{1,0:T(8,128)(2,1)}) custom-call(s32[1]{0:T(128)} %bitcast.1.place_ref, s32[1]{0:T(128)} %bitcast.2.ring_ref, bf16[256,512]{1,0:T(8,128)(2,1)} %attend.7.own_ref, bf16[256,512]{1,0:T(8,128)(2,1)} %copy-done.22, bf16[256,1024]{1,0:T(8,128)(2,1)} %get-tuple-element.72.refs_0_, ...), custom_call_target="tpu_custom_call" | custom-call | flops 1073741824 | bytes 5767168 | tf_op jit(solution)/shard_map/project/pallas_call | solution.py:399
  240.1 1.3 collective-permute-start.31
  241.4 4.6 %project.6 = (f32[256,512]{1,0:T(8,128)}, bf16[256,512]{1,0:T(8,128)(2,1)}, bf16[256,512]{1,0:T(8,128)(2,1)}) custom-call(s32[1]{0:T(128)} %bitcast.1.place_ref, s32[1]{0:T(128)} %bitcast.2.ring_ref, bf16[256,512]{1,0:T(8,128)(2,1)} %attend.6.own_ref, bf16[256,512]{1,0:T(8,128)(2,1)} %copy-done.21, bf16[256,1024]{1,0:T(8,128)(2,1)} %get-tuple-element.72.refs_0_, ...), custom_call_target="tpu_custom_call" | custom-call | flops 1073741824 | bytes 5767168 | tf_op jit(solution)/shard_map/project/pallas_call | solution.py:399
  246.0 0.9 collective-permute-start.27
  247.0 1.3 collective-permute-start.28
  248.3 4.6 %project.5 = (f32[256,512]{1,0:T(8,128)}, bf16[256,512]{1,0:T(8,128)(2,1)}, bf16[256,512]{1,0:T(8,128)(2,1)}) custom-call(s32[1]{0:T(128)} %bitcast.1.place_ref, s32[1]{0:T(128)} %bitcast.2.ring_ref, bf16[256,512]{1,0:T(8,128)(2,1)} %attend.5.own_ref, bf16[256,512]{1,0:T(8,128)(2,1)} %copy-done.20, bf16[256,1024]{1,0:T(8,128)(2,1)} %get-tuple-element.72.refs_0_, ...), custom_call_target="tpu_custom_call" | custom-call | flops 1073741824 | bytes 5767168 | tf_op jit(solution)/shard_map/project/pallas_call | solution.py:399
  253.6 1.3 collective-permute-start.25
  254.9 3.4 %final.4.rest_0_ = bf16[1024,4,512]{2,1,0:T(4,128)(2,1)} custom-call(f32[4,6]{1,0:T(4,128)} %static_ref.11, bf16[1024,4,512]{2,1,0:T(4,128)(2,1)} %x_ref.13, f32[8,5248]{1,0:T(8,128)} %get-tuple-element.55.first_ref.folded_ref.column_ref, f32[8,5248]{1,0:T(8,128)} %get-tuple-element.55.first_ref.folded_ref.column_ref, ...), custom_call_target="tpu_custom_call" | custom-call | flops 629145600 | bytes 2883584 | tf_op jit(solution)/shard_map/final/pallas_call | solution.py:478
  258.4 1.5 collective-permute-done.31.outer_ref
  260.6 3.4 %final.5.rest_0_ = bf16[1024,4,512]{2,1,0:T(4,128)(2,1)} custom-call(f32[4,6]{1,0:T(4,128)} %static_ref.11, bf16[1024,4,512]{2,1,0:T(4,128)(2,1)} %x_ref.13, f32[8,5248]{1,0:T(8,128)} %get-tuple-element.55.first_ref.folded_ref.column_ref, f32[8,5248]{1,0:T(8,128)} %get-tuple-element.55.first_ref.folded_ref.column_ref, ...), custom_call_target="tpu_custom_call", output_to_operand_aliasing={{}: (8, {})} | custom-call | flops 629145600 | bytes 2883584 | tf_op jit(solution)/shard_map/final/pallas_call | solution.py:478
  264.0 7.1 %collective-permute-done.28.outer_ref = bf16[256,512]{1,0:T(8,128)(2,1)S(1)} collective-permute-done((bf16[256,512]{1,0:T(8,128)(2,1)}, bf16[256,512]{1,0:T(8,128)(2,1)S(1)}, u32[]{:S(2)}, u32[]{:S(2)}) %collective-permute-start.28) | collective-permute-done | bytes 262176 | tf_op jit(solution)/shard_map/ppermute | solution.py:570
  271.8 3.4 %final.6.rest_0_ = bf16[1024,4,512]{2,1,0:T(4,128)(2,1)} custom-call(f32[4,6]{1,0:T(4,128)} %static_ref.11, bf16[1024,4,512]{2,1,0:T(4,128)(2,1)} %x_ref.13, f32[8,5248]{1,0:T(8,128)} %get-tuple-element.55.first_ref.folded_ref.column_ref, f32[8,5248]{1,0:T(8,128)} %get-tuple-element.55.first_ref.folded_ref.column_ref, ...), custom_call_target="tpu_custom_call", output_to_operand_aliasing={{}: (8, {})} | custom-call | flops 629145600 | bytes 2883584 | tf_op jit(solution)/shard_map/final/pallas_call | solution.py:478
  275.2 4.7 %collective-permute-done.25.outer_ref = bf16[256,512]{1,0:T(8,128)(2,1)S(1)} collective-permute-done((bf16[256,512]{1,0:T(8,128)(2,1)}, bf16[256,512]{1,0:T(8,128)(2,1)S(1)}, u32[]{:S(2)}, u32[]{:S(2)}) %collective-permute-start.25) | collective-permute-done | bytes 262176 | tf_op jit(solution)/shard_map/ppermute | solution.py:570
  280.6 3.4 %final.7 = bf16[1024,4,512]{2,1,0:T(4,128)(2,1)} custom-call(f32[4,6]{1,0:T(4,128)} %static_ref.11, bf16[1024,4,512]{2,1,0:T(4,128)(2,1)} %x_ref.13, f32[8,5248]{1,0:T(8,128)} %get-tuple-element.55.first_ref.folded_ref.column_ref, f32[8,5248]{1,0:T(8,128)} %get-tuple-element.55.first_ref.folded_ref.column_ref, ...), custom_call_target="tpu_custom_call", output_to_operand_aliasing={{}: (8, {})} | custom-call | flops 629145600 | bytes 2883584 | tf_op jit(solution)/shard_map/final/pallas_call | solution.py:478
  (129 shorter events, 8.4 us)
Async XLA Ops:
  6.5 144.0 %all-gather.5.cloned.1.call-start = ((), (), s32[]{:S(2)}) async-start(), calls=%async_computation.1 | async-start | bytes 3932160 | tf_op jit(solution)/shard_map/all_gather | solution.py:505
  14.5 11.9 %collective-permute-start = (f32[8,5248]{1,0:T(8,128)}, f32[8,5248]{1,0:T(8,128)S(1)}, u32[]{:S(2)}, u32[]{:S(2)}) collective-permute-start(f32[8,5248]{1,0:T(8,128)} %stats.1.own_ref), channel_id=1, source_target_pairs={{0,1},{1,2},{2,3},{3,0},{4,5},{5,6},{6,7},{7,4},{8,9},{9,10},{10,1... | collective-permute-start | bytes 503816 | tf_op jit(solution)/shard_map/ppermute | solution.py:31
  17.5 13.8 %collective-permute-start.1 = (f32[8,5248]{1,0:T(8,128)}, f32[8,5248]{1,0:T(8,128)S(1)}, u32[]{:S(2)}, u32[]{:S(2)}) collective-permute-start(f32[8,5248]{1,0:T(8,128)} %stats.1.own_ref), channel_id=1, source_target_pairs={{0,2},{1,3},{2,0},{3,1},{4,6},{5,7},{6,4},{7,5},{8,10},{9,11},{10,... | collective-permute-start | bytes 503816 | tf_op jit(solution)/shard_map/ppermute | solution.py:31
  20.1 11.2 %collective-permute-start.2 = (f32[8,5248]{1,0:T(8,128)}, f32[8,5248]{1,0:T(8,128)S(1)}, u32[]{:S(2)}, u32[]{:S(2)}) collective-permute-start(f32[8,5248]{1,0:T(8,128)} %stats.1.own_ref), channel_id=1, source_target_pairs={{0,3},{1,0},{2,1},{3,2},{4,7},{5,4},{6,5},{7,6},{8,11},{9,8},{10,9... | collective-permute-start | bytes 503816 | tf_op jit(solution)/shard_map/ppermute | solution.py:31
  21.4 64.6 %copy-start.31 = (s32[2]{0:T(128)S(1)}, s32[2]{0:T(128)}, u32[]{:S(2)}) copy-start(s32[2]{0:T(128)} %param.11) | copy-start | bytes 28
  21.4 65.9 %copy-start.30 = (s32[1024]{0:T(1024)S(1)}, s32[1024]{0:T(1024)}, u32[]{:S(2)}) copy-start(s32[1024]{0:T(1024)} %param.10) | copy-start | bytes 12292
  26.3 10.6 %copy-start.34 = (bf16[64,2560]{1,0:T(8,128)(2,1)S(1)}, bf16[64,2560]{1,0:T(8,128)(2,1)}, u32[]{:S(2)}) copy-start(bf16[64,2560]{1,0:T(8,128)(2,1)} %get-tuple-element.59) | copy-start | bytes 983044
  26.4 14.7 %copy-start.33 = (bf16[64,2560]{1,0:T(8,128)(2,1)S(1)}, bf16[64,2560]{1,0:T(8,128)(2,1)}, u32[]{:S(2)}) copy-start(bf16[64,2560]{1,0:T(8,128)(2,1)} %get-tuple-element.60) | copy-start | bytes 983044
  26.4 16.4 %copy-start.32 = (bf16[64,2560]{1,0:T(8,128)(2,1)S(1)}, bf16[64,2560]{1,0:T(8,128)(2,1)}, u32[]{:S(2)}) copy-start(bf16[64,2560]{1,0:T(8,128)(2,1)} %get-tuple-element.61) | copy-start | bytes 983044
  26.4 4.9 %copy-start.12 = (f32[8,5248]{1,0:T(8,128)}, f32[8,5248]{1,0:T(8,128)S(1)}, u32[]{:S(2)}) copy-start(f32[8,5248]{1,0:T(8,128)S(1)} %collective-permute-done.a_ref) | copy-start | bytes 503812
  36.9 170.5 %all-gather.3.cloned.1.call-start = ((), (), s32[]{:S(2)}) async-start(), calls=%async_computation | async-start | bytes 1310720 | tf_op jit(solution)/shard_map/all_gather | solution.py:505
  37.0 14.0 %collective-permute-start.4 = (bf16[64,2560]{1,0:T(8,128)(2,1)S(1)}, bf16[64,2560]{1,0:T(8,128)(2,1)S(1)}, u32[]{:S(2)}, u32[]{:S(2)}) collective-permute-start(bf16[64,2560]{1,0:T(8,128)(2,1)S(1)} %copy-done.34), channel_id=1, source_target_pairs={{0,1},{1,2},{2,3},{3,0},{4,5},{5,6},{6,7},{7,4},{8,9},{9,10},{10,1... | collective-permute-start | bytes 983048 | tf_op jit(solution)/shard_map/ppermute | solution.py:514
  41.0 37.6 %collective-permute-start.5 = (bf16[64,2560]{1,0:T(8,128)(2,1)S(1)}, bf16[64,2560]{1,0:T(8,128)(2,1)S(1)}, u32[]{:S(2)}, u32[]{:S(2)}) collective-permute-start(bf16[64,2560]{1,0:T(8,128)(2,1)S(1)} %copy-done.33), channel_id=1, source_target_pairs={{0,2},{1,3},{2,0},{3,1},{4,6},{5,7},{6,4},{7,5},{8,10},{9,11},{10,... | collective-permute-start | bytes 983048 | tf_op jit(solution)/shard_map/ppermute | solution.py:514
  42.7 35.9 %collective-permute-start.6 = (bf16[64,2560]{1,0:T(8,128)(2,1)S(1)}, bf16[64,2560]{1,0:T(8,128)(2,1)S(1)}, u32[]{:S(2)}, u32[]{:S(2)}) collective-permute-start(bf16[64,2560]{1,0:T(8,128)(2,1)S(1)} %copy-done.32), channel_id=1, source_target_pairs={{0,3},{1,0},{2,1},{3,2},{4,7},{5,4},{6,5},{7,6},{8,11},{9,8},{10,9... | collective-permute-start | bytes 983048 | tf_op jit(solution)/shard_map/ppermute | solution.py:514
  50.9 27.7 %copy-start.15 = (bf16[64,2560]{1,0:T(8,128)(2,1)}, bf16[64,2560]{1,0:T(8,128)(2,1)S(1)}, u32[]{:S(2)}) copy-start(bf16[64,2560]{1,0:T(8,128)(2,1)S(1)} %collective-permute-done.4.refs_1_) | copy-start | bytes 983044
  82.5 20.6 %collective-permute-start.8 = (bf16[256,1536]{1,0:T(8,128)(2,1)}, bf16[256,1536]{1,0:T(8,128)(2,1)S(1)}, u32[]{:S(2)}, u32[]{:S(2)}) collective-permute-start(bf16[256,1536]{1,0:T(8,128)(2,1)} %get-tuple-element.64.refs_0_), channel_id=1, source_target_pairs={{0,8},{4,12},{8,0},{12,4},{16,24},{20,28},{24,16},{28,20},{1,9},{5... | collective-permute-start | bytes 2359304 | tf_op jit(solution)/shard_map/ppermute | solution.py:122
  84.0 36.0 %collective-permute-start.10 = (bf16[256,1536]{1,0:T(8,128)(2,1)}, bf16[256,1536]{1,0:T(8,128)(2,1)S(1)}, u32[]{:S(2)}, u32[]{:S(2)}) collective-permute-start(bf16[256,1536]{1,0:T(8,128)(2,1)} %get-tuple-element.64.refs_0_), channel_id=1, source_target_pairs={{0,16},{4,20},{8,24},{12,28},{16,0},{20,4},{24,8},{28,12},{1,17},{... | collective-permute-start | bytes 2359304 | tf_op jit(solution)/shard_map/ppermute | solution.py:122
  85.5 34.5 %collective-permute-start.12 = (bf16[256,1536]{1,0:T(8,128)(2,1)}, bf16[256,1536]{1,0:T(8,128)(2,1)S(1)}, u32[]{:S(2)}, u32[]{:S(2)}) collective-permute-start(bf16[256,1536]{1,0:T(8,128)(2,1)} %get-tuple-element.64.refs_0_), channel_id=1, source_target_pairs={{0,24},{4,28},{8,16},{12,20},{16,8},{20,12},{24,0},{28,4},{1,25},{... | collective-permute-start | bytes 2359304 | tf_op jit(solution)/shard_map/ppermute | solution.py:122
  87.3 35.0 %collective-permute-start.3 = (s32[512]{0:T(512)S(1)}, s32[512]{0:T(512)S(1)}, u32[]{:S(2)}, u32[]{:S(2)}) collective-permute-start(s32[512]{0:T(512)S(1)} %get-tuple-element.98), channel_id=1, source_target_pairs={{0,4},{4,8},{8,12},{12,16},{16,20},{20,24},{24,28},{1,5},{5,9},{9,... | collective-permute-start | bytes 6152 | tf_op jit(solution)/shard_map/ppermute | solution.py:25
  88.6 35.3 %collective-permute-start.7 = (bf16[256,1536]{1,0:T(8,128)(2,1)}, bf16[256,1536]{1,0:T(8,128)(2,1)}, u32[]{:S(2)}, u32[]{:S(2)}) collective-permute-start(bf16[256,1536]{1,0:T(8,128)(2,1)} %get-tuple-element.64.refs_0_), channel_id=1, source_target_pairs={{0,4},{4,0},{8,12},{12,8},{16,20},{20,16},{24,28},{28,24},{1,5},{5... | collective-permute-start | bytes 2359304 | tf_op jit(solution)/shard_map/ppermute | solution.py:122
  103.2 30.6 %copy-start.9 = (bf16[256,1536]{1,0:T(8,128)(2,1)}, bf16[256,1536]{1,0:T(8,128)(2,1)S(1)}, u32[]{:S(2)}) copy-start(bf16[256,1536]{1,0:T(8,128)(2,1)S(1)} %collective-permute-done.8.refs_2_) | copy-start | bytes 2359300
  103.2 20.8 %collective-permute-start.9 = (bf16[256,1536]{1,0:T(8,128)(2,1)S(1)}, bf16[256,1536]{1,0:T(8,128)(2,1)}, u32[]{:S(2)}, u32[]{:S(2)}) collective-permute-start(bf16[256,1536]{1,0:T(8,128)(2,1)S(1)} %collective-permute-done.8.refs_2_), channel_id=1, source_target_pairs={{0,4},{4,0},{8,12},{12,8},{16,20},{20,16},{24,28},{28,24},{1,5},{5... | collective-permute-start | bytes 2359304 | tf_op jit(solution)/shard_map/ppermute | solution.py:122
  120.0 3.9 %copy-start.10 = (bf16[256,1536]{1,0:T(8,128)(2,1)}, bf16[256,1536]{1,0:T(8,128)(2,1)S(1)}, u32[]{:S(2)}) copy-start(bf16[256,1536]{1,0:T(8,128)(2,1)S(1)} %collective-permute-done.10.refs_4_) | copy-start | bytes 2359300
  120.0 3.9 %collective-permute-start.11 = (bf16[256,1536]{1,0:T(8,128)(2,1)S(1)}, bf16[256,1536]{1,0:T(8,128)(2,1)}, u32[]{:S(2)}, u32[]{:S(2)}) collective-permute-start(bf16[256,1536]{1,0:T(8,128)(2,1)S(1)} %collective-permute-done.10.refs_4_), channel_id=1, source_target_pairs={{0,4},{4,0},{8,12},{12,8},{16,20},{20,16},{24,28},{28,24},{1,5},{5... | collective-permute-start | bytes 2359304 | tf_op jit(solution)/shard_map/ppermute | solution.py:122
  120.1 3.9 %copy-start.11 = (bf16[256,1536]{1,0:T(8,128)(2,1)}, bf16[256,1536]{1,0:T(8,128)(2,1)S(1)}, u32[]{:S(2)}) copy-start(bf16[256,1536]{1,0:T(8,128)(2,1)S(1)} %collective-permute-done.12.refs_6_) | copy-start | bytes 2359300
  120.1 3.9 %collective-permute-start.13 = (bf16[256,1536]{1,0:T(8,128)(2,1)S(1)}, bf16[256,1536]{1,0:T(8,128)(2,1)}, u32[]{:S(2)}, u32[]{:S(2)}) collective-permute-start(bf16[256,1536]{1,0:T(8,128)(2,1)S(1)} %collective-permute-done.12.refs_6_), channel_id=1, source_target_pairs={{0,4},{4,0},{8,12},{12,8},{16,20},{20,16},{24,28},{28,24},{1,5},{5... | collective-permute-start | bytes 2359304 | tf_op jit(solution)/shard_map/ppermute | solution.py:122
  124.0 15.1 %collective-permute-start.16 = (bf16[256,1024]{1,0:T(8,128)(2,1)}, bf16[256,1024]{1,0:T(8,128)(2,1)S(1)}, u32[]{:S(2)}, u32[]{:S(2)}) collective-permute-start(bf16[256,1024]{1,0:T(8,128)(2,1)} %get-tuple-element.72.refs_0_), channel_id=1, source_target_pairs={{0,8},{4,12},{8,0},{12,4},{16,24},{20,28},{24,16},{28,20},{1,9},{5... | collective-permute-start | bytes 1572872 | tf_op jit(solution)/shard_map/ppermute | solution.py:122
  124.8 24.0 %collective-permute-start.18 = (bf16[256,1024]{1,0:T(8,128)(2,1)}, bf16[256,1024]{1,0:T(8,128)(2,1)S(1)}, u32[]{:S(2)}, u32[]{:S(2)}) collective-permute-start(bf16[256,1024]{1,0:T(8,128)(2,1)} %get-tuple-element.72.refs_0_), channel_id=1, source_target_pairs={{0,16},{4,20},{8,24},{12,28},{16,0},{20,4},{24,8},{28,12},{1,17},{... | collective-permute-start | bytes 1572872 | tf_op jit(solution)/shard_map/ppermute | solution.py:122
  126.1 24.3 %collective-permute-start.20 = (bf16[256,1024]{1,0:T(8,128)(2,1)}, bf16[256,1024]{1,0:T(8,128)(2,1)S(1)}, u32[]{:S(2)}, u32[]{:S(2)}) collective-permute-start(bf16[256,1024]{1,0:T(8,128)(2,1)} %get-tuple-element.72.refs_0_), channel_id=1, source_target_pairs={{0,24},{4,28},{8,16},{12,20},{16,8},{20,12},{24,0},{28,4},{1,25},{... | collective-permute-start | bytes 1572872 | tf_op jit(solution)/shard_map/ppermute | solution.py:122
  127.5 6.3 %copy-start.1 = (bf16[256,1024]{1,0:T(8,128)(2,1)S(1)}, bf16[256,1024]{1,0:T(8,128)(2,1)}, u32[]{:S(2)}) copy-start(bf16[256,1024]{1,0:T(8,128)(2,1)} %get-tuple-element.72.refs_0_) | copy-start | bytes 1572868
  132.4 18.0 %copy-start.5 = (f32[1024,64]{1,0:T(8,128)}, f32[1024,64]{1,0:T(8,128)S(1)}, u32[]{:S(2)}) copy-start(f32[1024,64]{1,0:T(8,128)S(1)} %get-tuple-element.91) | copy-start | bytes 786436
  132.4 18.0 %copy-start.7 = (f32[1024,64]{1,0:T(8,128)}, f32[1024,64]{1,0:T(8,128)S(1)}, u32[]{:S(2)}) copy-start(f32[1024,64]{1,0:T(8,128)S(1)} %get-tuple-element.92) | copy-start | bytes 786436
  132.4 18.0 %copy-start.8 = (f32[1024,64]{1,0:T(8,128)}, f32[1024,64]{1,0:T(8,128)S(1)}, u32[]{:S(2)}) copy-start(f32[1024,64]{1,0:T(8,128)S(1)} %get-tuple-element.93) | copy-start | bytes 786436
  133.8 36.7 %collective-permute-start.15 = (bf16[256,1024]{1,0:T(8,128)(2,1)S(1)}, bf16[256,1024]{1,0:T(8,128)(2,1)}, u32[]{:S(2)}, u32[]{:S(2)}) collective-permute-start(bf16[256,1024]{1,0:T(8,128)(2,1)S(1)} %copy-done.1), channel_id=1, source_target_pairs={{0,4},{4,0},{8,12},{12,8},{16,20},{20,16},{24,28},{28,24},{1,5},{5... | collective-permute-start | bytes 1572872 | tf_op jit(solution)/shard_map/ppermute | solution.py:122
  139.0 21.8 %copy-start.2 = (bf16[256,1024]{1,0:T(8,128)(2,1)}, bf16[256,1024]{1,0:T(8,128)(2,1)S(1)}, u32[]{:S(2)}) copy-start(bf16[256,1024]{1,0:T(8,128)(2,1)S(1)} %collective-permute-done.16.refs_2_) | copy-start | bytes 1572868
  139.0 57.6 %collective-permute-start.17 = (bf16[256,1024]{1,0:T(8,128)(2,1)S(1)}, bf16[256,1024]{1,0:T(8,128)(2,1)}, u32[]{:S(2)}, u32[]{:S(2)}) collective-permute-start(bf16[256,1024]{1,0:T(8,128)(2,1)S(1)} %collective-permute-done.16.refs_2_), channel_id=1, source_target_pairs={{0,4},{4,0},{8,12},{12,8},{16,20},{20,16},{24,28},{28,24},{1,5},{5... | collective-permute-start | bytes 1572872 | tf_op jit(solution)/shard_map/ppermute | solution.py:122
  148.8 12.0 %copy-start.3 = (bf16[256,1024]{1,0:T(8,128)(2,1)}, bf16[256,1024]{1,0:T(8,128)(2,1)S(1)}, u32[]{:S(2)}) copy-start(bf16[256,1024]{1,0:T(8,128)(2,1)S(1)} %collective-permute-done.18.refs_4_) | copy-start | bytes 1572868
  148.8 47.8 %collective-permute-start.19 = (bf16[256,1024]{1,0:T(8,128)(2,1)S(1)}, bf16[256,1024]{1,0:T(8,128)(2,1)}, u32[]{:S(2)}, u32[]{:S(2)}) collective-permute-start(bf16[256,1024]{1,0:T(8,128)(2,1)S(1)} %collective-permute-done.18.refs_4_), channel_id=1, source_target_pairs={{0,4},{4,0},{8,12},{12,8},{16,20},{20,16},{24,28},{28,24},{1,5},{5... | collective-permute-start | bytes 1572872 | tf_op jit(solution)/shard_map/ppermute | solution.py:122
  150.4 10.5 %copy-start.4 = (bf16[256,1024]{1,0:T(8,128)(2,1)}, bf16[256,1024]{1,0:T(8,128)(2,1)S(1)}, u32[]{:S(2)}) copy-start(bf16[256,1024]{1,0:T(8,128)(2,1)S(1)} %collective-permute-done.20.refs_6_) | copy-start | bytes 1572868
  150.4 46.3 %collective-permute-start.21 = (bf16[256,1024]{1,0:T(8,128)(2,1)S(1)}, bf16[256,1024]{1,0:T(8,128)(2,1)}, u32[]{:S(2)}, u32[]{:S(2)}) collective-permute-start(bf16[256,1024]{1,0:T(8,128)(2,1)S(1)} %collective-permute-done.20.refs_6_), channel_id=1, source_target_pairs={{0,4},{4,0},{8,12},{12,8},{16,20},{20,16},{24,28},{28,24},{1,5},{5... | collective-permute-start | bytes 1572872 | tf_op jit(solution)/shard_map/ppermute | solution.py:122
  163.2 56.6 %collective-permute-start.22 = (bf16[2,512,512]{2,1,0:T(8,128)(2,1)}, bf16[2,512,512]{2,1,0:T(8,128)(2,1)S(1)}, u32[]{:S(2)}, u32[]{:S(2)}) collective-permute-start(bf16[2,512,512]{2,1,0:T(8,128)(2,1)} %slice.58), channel_id=1, source_target_pairs={{0,4},{4,8},{8,12},{12,16},{16,20},{20,24},{24,28},{1,5},{5,9},{9,... | collective-permute-start | bytes 3145736 | tf_op jit(solution)/shard_map/ppermute | solution.py:25
  166.4 28.4 %copy-start.6 = (f32[1024,64]{1,0:T(8,128)S(1)}, f32[1024,64]{1,0:T(8,128)}, u32[]{:S(2)}) copy-start(f32[1024,64]{1,0:T(8,128)} %copy-done.5) | copy-start | bytes 786436
  170.5 31.5 %collective-permute-start.14 = (bf16[256,512]{1,0:T(8,128)(2,1)}, bf16[256,512]{1,0:T(8,128)(2,1)S(1)}, u32[]{:S(2)}, u32[]{:S(2)}) collective-permute-start(bf16[256,512]{1,0:T(8,128)(2,1)} %attend.4.own_ref), channel_id=1, source_target_pairs={{0,1},{1,0},{2,3},{3,2},{4,5},{5,4},{6,7},{7,6},{8,9},{9,8},{10,11... | collective-permute-start | bytes 786440 | tf_op jit(solution)/shard_map/ppermute | solution.py:122
  217.7 7.1 %copy-start.36 = (bf16[256,512]{1,0:T(8,128)(2,1)S(1)}, bf16[256,512]{1,0:T(8,128)(2,1)}, u32[]{:S(2)}) copy-start(bf16[256,512]{1,0:T(8,128)(2,1)} %get-tuple-element.87) | copy-start | bytes 786436
  217.7 16.3 %collective-permute-start.29 = (bf16[256,512]{1,0:T(8,128)(2,1)}, bf16[256,512]{1,0:T(8,128)(2,1)S(1)}, u32[]{:S(2)}, u32[]{:S(2)}) collective-permute-start(bf16[256,512]{1,0:T(8,128)(2,1)} %attend.7.own_ref), channel_id=1, source_target_pairs={{0,1},{1,0},{2,3},{3,2},{4,5},{5,4},{6,7},{7,6},{8,9},{9,8},{10,11... | collective-permute-start | bytes 786440 | tf_op jit(solution)/shard_map/ppermute | solution.py:122
  219.8 1.0 copy-start
  224.8 8.0 %copy-start.35 = (bf16[256,512]{1,0:T(8,128)(2,1)S(1)}, bf16[256,512]{1,0:T(8,128)(2,1)}, u32[]{:S(2)}) copy-start(bf16[256,512]{1,0:T(8,128)(2,1)} %get-tuple-element.88) | copy-start | bytes 786436
  224.8 15.3 %collective-permute-start.26 = (bf16[256,512]{1,0:T(8,128)(2,1)}, bf16[256,512]{1,0:T(8,128)(2,1)S(1)}, u32[]{:S(2)}, u32[]{:S(2)}) collective-permute-start(bf16[256,512]{1,0:T(8,128)(2,1)} %attend.6.own_ref), channel_id=1, source_target_pairs={{0,1},{1,0},{2,3},{3,2},{4,5},{5,4},{6,7},{7,6},{8,9},{9,8},{10,11... | collective-permute-start | bytes 786440 | tf_op jit(solution)/shard_map/ppermute | solution.py:122
  224.8 21.3 %collective-permute-start.32 = (bf16[256,512]{1,0:T(8,128)(2,1)S(1)}, bf16[256,512]{1,0:T(8,128)(2,1)S(1)}, u32[]{:S(2)}, u32[]{:S(2)}) collective-permute-start(bf16[256,512]{1,0:T(8,128)(2,1)S(1)} %copy-done.36), channel_id=1, source_target_pairs={{1,2},{2,1},{5,6},{6,5},{9,10},{10,9},{13,14},{14,13},{17,18},{18,... | collective-permute-start | bytes 786440 | tf_op jit(solution)/shard_map/ppermute | solution.py:569
  229.6 17.3 %collective-permute-start.23 = (bf16[256,512]{1,0:T(8,128)(2,1)}, bf16[256,512]{1,0:T(8,128)(2,1)S(1)}, u32[]{:S(2)}, u32[]{:S(2)}) collective-permute-start(bf16[256,512]{1,0:T(8,128)(2,1)} %attend.5.own_ref), channel_id=1, source_target_pairs={{0,1},{1,0},{2,3},{3,2},{4,5},{5,4},{6,7},{7,6},{8,9},{9,8},{10,11... | collective-permute-start | bytes 786440 | tf_op jit(solution)/shard_map/ppermute | solution.py:122
  232.8 20.2 %collective-permute-start.33 = (bf16[256,512]{1,0:T(8,128)(2,1)S(1)}, bf16[256,512]{1,0:T(8,128)(2,1)S(1)}, u32[]{:S(2)}, u32[]{:S(2)}) collective-permute-start(bf16[256,512]{1,0:T(8,128)(2,1)S(1)} %copy-done.35), channel_id=1, source_target_pairs={{1,3},{2,0},{5,7},{6,4},{9,11},{10,8},{13,15},{14,12},{17,19},{18,... | collective-permute-start | bytes 786440 | tf_op jit(solution)/shard_map/ppermute | solution.py:570
  239.4 14.2 %collective-permute-start.30 = (bf16[256,512]{1,0:T(8,128)(2,1)}, bf16[256,512]{1,0:T(8,128)(2,1)S(1)}, u32[]{:S(2)}, u32[]{:S(2)}) collective-permute-start(bf16[256,512]{1,0:T(8,128)(2,1)} %get-tuple-element.84), channel_id=1, source_target_pairs={{1,2},{2,1},{5,6},{6,5},{9,10},{10,9},{13,14},{14,13},{17,18},{18,... | collective-permute-start | bytes 786440 | tf_op jit(solution)/shard_map/ppermute | solution.py:569
  240.1 1.3 copy-start.21
  240.1 19.8 %collective-permute-start.31 = (bf16[256,512]{1,0:T(8,128)(2,1)}, bf16[256,512]{1,0:T(8,128)(2,1)S(1)}, u32[]{:S(2)}, u32[]{:S(2)}) collective-permute-start(bf16[256,512]{1,0:T(8,128)(2,1)} %get-tuple-element.85), channel_id=1, source_target_pairs={{1,3},{2,0},{5,7},{6,4},{9,11},{10,8},{13,15},{14,12},{17,19},{18,... | collective-permute-start | bytes 786440 | tf_op jit(solution)/shard_map/ppermute | solution.py:570
  246.0 8.9 %copy-start.18 = (bf16[256,512]{1,0:T(8,128)(2,1)}, bf16[256,512]{1,0:T(8,128)(2,1)S(1)}, u32[]{:S(2)}) copy-start(bf16[256,512]{1,0:T(8,128)(2,1)S(1)} %collective-permute-done.32.inner_ref) | copy-start | bytes 786436
  246.0 18.0 %collective-permute-start.27 = (bf16[256,512]{1,0:T(8,128)(2,1)}, bf16[256,512]{1,0:T(8,128)(2,1)S(1)}, u32[]{:S(2)}, u32[]{:S(2)}) collective-permute-start(bf16[256,512]{1,0:T(8,128)(2,1)} %get-tuple-element.81), channel_id=1, source_target_pairs={{1,2},{2,1},{5,6},{6,5},{9,10},{10,9},{13,14},{14,13},{17,18},{18,... | collective-permute-start | bytes 786440 | tf_op jit(solution)/shard_map/ppermute | solution.py:569
  247.0 1.3 copy-start.20
  247.0 24.2 %collective-permute-start.28 = (bf16[256,512]{1,0:T(8,128)(2,1)}, bf16[256,512]{1,0:T(8,128)(2,1)S(1)}, u32[]{:S(2)}, u32[]{:S(2)}) collective-permute-start(bf16[256,512]{1,0:T(8,128)(2,1)} %get-tuple-element.82), channel_id=1, source_target_pairs={{1,3},{2,0},{5,7},{6,4},{9,11},{10,8},{13,15},{14,12},{17,19},{18,... | collective-permute-start | bytes 786440 | tf_op jit(solution)/shard_map/ppermute | solution.py:570
  252.9 2.0 copy-start.19
  252.9 22.3 %collective-permute-start.24 = (bf16[256,512]{1,0:T(8,128)(2,1)}, bf16[256,512]{1,0:T(8,128)(2,1)S(1)}, u32[]{:S(2)}, u32[]{:S(2)}) collective-permute-start(bf16[256,512]{1,0:T(8,128)(2,1)} %get-tuple-element.78), channel_id=1, source_target_pairs={{1,2},{2,1},{5,6},{6,5},{9,10},{10,9},{13,14},{14,13},{17,18},{18,... | collective-permute-start | bytes 786440 | tf_op jit(solution)/shard_map/ppermute | solution.py:569
  253.6 4.8 %copy-start.24 = (bf16[256,512]{1,0:T(8,128)(2,1)}, bf16[256,512]{1,0:T(8,128)(2,1)S(1)}, u32[]{:S(2)}) copy-start(bf16[256,512]{1,0:T(8,128)(2,1)S(1)} %collective-permute-done.30.inner_ref) | copy-start | bytes 786436
  253.6 26.3 %collective-permute-start.25 = (bf16[256,512]{1,0:T(8,128)(2,1)}, bf16[256,512]{1,0:T(8,128)(2,1)S(1)}, u32[]{:S(2)}, u32[]{:S(2)}) collective-permute-start(bf16[256,512]{1,0:T(8,128)(2,1)} %get-tuple-element.79), channel_id=1, source_target_pairs={{1,3},{2,0},{5,7},{6,4},{9,11},{10,8},{13,15},{14,12},{17,19},{18,... | collective-permute-start | bytes 786440 | tf_op jit(solution)/shard_map/ppermute | solution.py:570
  264.0 7.1 %copy-start.26 = (bf16[256,512]{1,0:T(8,128)(2,1)}, bf16[256,512]{1,0:T(8,128)(2,1)S(1)}, u32[]{:S(2)}) copy-start(bf16[256,512]{1,0:T(8,128)(2,1)S(1)} %collective-permute-done.27.inner_ref) | copy-start | bytes 786436
  275.2 4.7 %copy-start.28 = (bf16[256,512]{1,0:T(8,128)(2,1)}, bf16[256,512]{1,0:T(8,128)(2,1)S(1)}, u32[]{:S(2)}) copy-start(bf16[256,512]{1,0:T(8,128)(2,1)S(1)} %collective-permute-done.24.inner_ref) | copy-start | bytes 786436
  (9 other events, 6.4 us)
Sparse Core Ops, SparseCore 0:
  37.0 83.9 all-gather.4
  130.6 48.9 all-gather.2

commit v6 on v5

--- a/solution.py
+++ b/solution.py
@@ -505,15 +505,18 @@
         rows = lax.all_gather(normed, "mp", axis=0, tiled=True)
         return rows.reshape(group_size, normed.shape[0], width)
 
-    sums_all, normed_late = mix(hc_static, streams, sums, CHUNK, tokens_local - CHUNK)
-    rows_late = gathered(normed_late)
-    _, normed_first = mix(hc_static, streams, sums, 0, CHUNK)
-    rows_first = gathered(normed_first)
-
     for step in range(1, group_size):
         parts[step] = lax.ppermute(
             parts[step], "mp", [(at, (at + step) % group_size) for at in range(group_size)]
         )
+    sums_all, normed_late = mix(hc_static, streams, sums, CHUNK, tokens_local - CHUNK)
+    _, normed_first = mix(hc_static, streams, sums, 0, CHUNK)
+    parts[1], normed_late, normed_first = lax.optimization_barrier(
+        (parts[1], normed_late, normed_first)
+    )
+    rows_late = gathered(normed_late)
+    rows_first = gathered(normed_first)
+
     qkv_part, out_part = assemble(place, parts)
     qkv_pieces = weight_pieces(qkv_part)
     out_part, qkv_pieces = lax.optimization_barrier((out_part, qkv_pieces))

time: 292 us -> 282 us (0.966)
  waiting for transfers between devices: 104 us -> 92.3 us
  starting transfers between devices: 64.9 us -> 68.7 us
    ppermute x3, waiting for transfers between devices: 35.2 us -> 26.5 us  [body(): lax.ppermute(parts[step], 'mp', [(at, (at + step) % group_size) for at in...]
    ppermute x18, waiting for transfers between devices: 51 us -> 47.6 us  [swapped(): lax.ppermute(value, axis, [(source, source ^ mask) for source in range(co...]
    unnamed x74 -> x72, local copies, waits for them, and re-layouts: 6.74 us -> 6.03 us
  transfers between devices with their start and end apart: 36 -> 36, of which waited for: 12 -> 14; matrix products, arithmetic and copies ran while one was open for 4% -> 4% of each run, Pallas kernels for 25% -> 27%
where the time goes in v6:
time: 282 us; the launch traced here: 281 us
  waiting for transfers between devices  92.3 us (33%)
  Pallas kernels  86.3 us (31%)
  starting transfers between devices  68.7 us (24%)
  between operations  15.2 us (5%)
  local copies, waits for them, and re-layouts  10.8 us (4%)
  other arithmetic  8.2 us (3%)
    ppermute x18, waiting for transfers between devices, swapped(): lax.ppermute(value, axis, [(source, source ^ mask) for source in range(co...  47.6 us
    ppermute x18, starting transfers between devices, swapped(): lax.ppermute(value, axis, [(source, source ^ mask) for source in range(co...  41.5 us
    ppermute x3, waiting for transfers between devices, body(): lax.ppermute(parts[step], 'mp', [(at, (at + step) % group_size) for at in...  26.5 us
    pallas_call x4, Pallas kernels, project(): pl.pallas_call(project_kernel, grid=(1,), in_specs=[pl.BlockSpec(memory_s...  18.6 us
    pallas_call x2, Pallas kernels, qkv_columns(): pl.pallas_call(qkv_kernel, grid=(3,), in_specs=[pl.BlockSpec(memory_space...  16.6 us
    pallas_call x4, Pallas kernels, attend(): pl.pallas_call(attend_kernel, grid=(1,), in_specs=[pl.BlockSpec(block, la...  16.1 us
    pallas_call x4, Pallas kernels, final(): pl.pallas_call(final_kernel, grid=(tokens // STEP,), in_specs=specs, out_...  13.6 us
    ppermute x4, waiting for transfers between devices, body(): outer = lax.ppermute(outer, 'mp', [(1, 3), (2, 0)])  13.2 us
  transfers between devices with their start and end apart: 36, of which 14 were waited for; matrix products, arithmetic and copies ran while one was open for 4% of the time, Pallas kernels for 27%

profile of v6, /device:TPU:0, one launch (start us, length us, event | category | flops | bytes accessed | tf_op | source)
XLA Modules:
  0.0 281.4 jit_solution(1470877175128718759)
XLA Ops:
  6.7 1.4 maximum_maximum_fusion.proj_ref
  8.1 6.4 %stats.1.own_ref = f32[8,5248]{1,0:T(8,128)} custom-call(bf16[1024,4,512]{2,1,0:T(4,128)(2,1)} %x_ref.13, f32[8,512]{1,0:T(8,128)} %maximum_maximum_fusion.proj_ref), custom_call_target="tpu_custom_call" | custom-call | flops 1258291200 | bytes 4194304 | tf_op jit(solution)/shard_map/stats/pallas_call | solution.py:178
  14.4 3.0 %collective-permute-start = (f32[8,5248]{1,0:T(8,128)}, f32[8,5248]{1,0:T(8,128)S(1)}, u32[]{:S(2)}, u32[]{:S(2)}) collective-permute-start(f32[8,5248]{1,0:T(8,128)} %stats.1.own_ref), channel_id=1, source_target_pairs={{0,1},{1,2},{2,3},{3,0},{4,5},{5,6},{6,7},{7,4},{8,9},{9,10},{10,1... | collective-permute-start | bytes 503816 | tf_op jit(solution)/shard_map/ppermute | solution.py:31
  17.5 2.6 collective-permute-start.1
  20.1 1.3 collective-permute-start.2
  21.4 4.9 %regroup.1 = (bf16[64,2560]{1,0:T(8,128)(2,1)}, bf16[64,2560]{1,0:T(8,128)(2,1)}, bf16[64,2560]{1,0:T(8,128)(2,1)}, bf16[64,2560]{1,0:T(8,128)(2,1)}) custom-call(s32[1]{0:T(128)} %bitcast.1.place_ref, f32[64,4,2048]{2,1,0:T(4,128)} %master_ref.1), custom_call_target="tpu_custom_call" | custom-call | bytes 3407872 | tf_op jit(solution)/shard_map/regroup/pallas_call | solution.py:79
  26.3 5.0 %collective-permute-done.1.b_ref = f32[8,5248]{1,0:T(8,128)S(1)} collective-permute-done((f32[8,5248]{1,0:T(8,128)}, f32[8,5248]{1,0:T(8,128)S(1)}, u32[]{:S(2)}, u32[]{:S(2)}) %collective-permute-start.1) | collective-permute-done | bytes 167968 | tf_op jit(solution)/shard_map/ppermute | solution.py:31
  31.3 4.1 %collective-permute-start.3 = (bf16[64,2560]{1,0:T(8,128)(2,1)}, bf16[64,2560]{1,0:T(8,128)(2,1)S(1)}, u32[]{:S(2)}, u32[]{:S(2)}) collective-permute-start(bf16[64,2560]{1,0:T(8,128)(2,1)} %get-tuple-element.59), channel_id=1, source_target_pairs={{0,1},{1,2},{2,3},{3,0},{4,5},{5,6},{6,7},{7,4},{8,9},{9,10},{10,1... | collective-permute-start | bytes 983048 | tf_op jit(solution)/shard_map/ppermute | solution.py:509
  35.4 2.9 %mix.3 = (f32[8,5248]{1,0:T(8,128)}, bf16[256,512]{1,0:T(8,128)(2,1)}) custom-call(f32[4,6]{1,0:T(4,128)} %static_ref.11, bf16[1024,4,512]{2,1,0:T(4,128)(2,1)} %x_ref.13, f32[8,5248]{1,0:T(8,128)} %stats.1.own_ref, f32[8,5248]{1,0:T(8,128)} %copy-done.12, f32[8,5248]{1,0:T(8,128)} %copy-done.13, f32[8,5248]{1,0:T(8,128)} %copy-done.14), custom_call_target="tpu_custom_call" | custom-call | flops 209715200 | bytes 1310720 | tf_op jit(solution)/shard_map/mix/pallas_call | solution.py:249
  38.2 4.9 %mix.2 = (f32[8,5248]{1,0:T(8,128)}, bf16[768,512]{1,0:T(8,128)(2,1)}) custom-call(f32[4,6]{1,0:T(4,128)} %static_ref.11, bf16[1024,4,512]{2,1,0:T(4,128)(2,1)} %x_ref.13, f32[8,5248]{1,0:T(8,128)} %stats.1.own_ref, f32[8,5248]{1,0:T(8,128)} %copy-done.12, f32[8,5248]{1,0:T(8,128)} %copy-done.13, f32[8,5248]{1,0:T(8,128)} %copy-done.14), custom_call_target="tpu_custom_call" | custom-call | flops 629145600 | bytes 3932160 | tf_op jit(solution)/shard_map/mix/pallas_call | solution.py:249
  43.6 1.4 collective-permute-start.5
  45.1 2.6 collective-permute-start.6
  47.7 26.0 %collective-permute-done.5.refs_2_ = bf16[64,2560]{1,0:T(8,128)(2,1)S(1)} collective-permute-done((bf16[64,2560]{1,0:T(8,128)(2,1)S(1)}, bf16[64,2560]{1,0:T(8,128)(2,1)S(1)}, u32[]{:S(2)}, u32[]{:S(2)}) %collective-permute-start.5) | collective-permute-done | bytes 327712 | tf_op jit(solution)/shard_map/ppermute | solution.py:509
  73.7 0.7 copy-done.16
  74.5 0.7 copy-done.17
  75.2 2.4 assemble.1
  77.6 1.5 collective-permute-start.8
  79.2 1.5 collective-permute-start.10
  82.4 1.3 collective-permute-start.4
  83.7 2.3 collective-permute-start.7
  86.0 12.3 %collective-permute-done.8.refs_2_ = bf16[256,1536]{1,0:T(8,128)(2,1)S(1)} collective-permute-done((bf16[256,1536]{1,0:T(8,128)(2,1)}, bf16[256,1536]{1,0:T(8,128)(2,1)S(1)}, u32[]{:S(2)}, u32[]{:S(2)}) %collective-permute-start.8) | collective-permute-done | bytes 786464 | tf_op jit(solution)/shard_map/ppermute | solution.py:122
  98.3 10.7 %collective-permute-done.10.refs_4_ = bf16[256,1536]{1,0:T(8,128)(2,1)S(1)} collective-permute-done((bf16[256,1536]{1,0:T(8,128)(2,1)}, bf16[256,1536]{1,0:T(8,128)(2,1)S(1)}, u32[]{:S(2)}, u32[]{:S(2)}) %collective-permute-start.10) | collective-permute-done | bytes 786464 | tf_op jit(solution)/shard_map/ppermute | solution.py:122
  110.2 1.0 copy.14.qseg_ref
  111.4 1.1 collective-permute-done.13.refs_7_
  112.7 1.9 collective-permute-start.18
  114.6 1.4 collective-permute-start.20
  116.0 1.6 convert_reduce_fusion
  117.7 1.9 multiply_sine_fusion
  119.6 1.4 fusion.1
  121.0 6.5 %collective-permute-done.16.refs_2_ = bf16[256,1024]{1,0:T(8,128)(2,1)S(1)} collective-permute-done((bf16[256,1024]{1,0:T(8,128)(2,1)}, bf16[256,1024]{1,0:T(8,128)(2,1)S(1)}, u32[]{:S(2)}, u32[]{:S(2)}) %collective-permute-start.16) | collective-permute-done | bytes 524320 | tf_op jit(solution)/shard_map/ppermute | solution.py:122
  127.5 9.9 %collective-permute-done.18.refs_4_ = bf16[256,1024]{1,0:T(8,128)(2,1)S(1)} collective-permute-done((bf16[256,1024]{1,0:T(8,128)(2,1)}, bf16[256,1024]{1,0:T(8,128)(2,1)S(1)}, u32[]{:S(2)}, u32[]{:S(2)}) %collective-permute-start.18) | collective-permute-done | bytes 524320 | tf_op jit(solution)/shard_map/ppermute | solution.py:122
  137.4 1.6 collective-permute-done.20.refs_6_
  139.1 10.3 %qkv.2.q_ref.k0.k1.k2.v0.v1.v2 = bf16[3,768,512]{2,1,0:T(8,128)(2,1)} custom-call(s32[1]{0:T(128)} %bitcast.2.ring_ref, bf16[4,768,512]{2,1,0:T(8,128)(2,1)} %bitcast.13, f32[768,128]{1,0:T(8,128)} %get-tuple-element.110.cosine_ref, f32[768,128]{1,0:T(8,128)} %get-tuple-element.109.sine_ref, bf16[256,1536]{1,0:T(8,128)(2,1)} %get-tuple-element.70.refs_0_, ...), custom_call_target="tpu_custom_call" | custom-call | flops 4831838208 | bytes 14155776 | tf_op jit(solution)/shard_map/qkv/pallas_call | solution.py:302
  149.5 2.3 slice.58
  151.8 2.6 collective-permute-start.22
  155.0 4.1 %attend.4.own_ref = bf16[256,512]{1,0:T(8,128)(2,1)} custom-call(bf16[3,768,512]{2,1,0:T(8,128)(2,1)} %qkv.2.q_ref.k0.k1.k2.v0.v1.v2, bf16[3,768,512]{2,1,0:T(8,128)(2,1)} %qkv.2.q_ref.k0.k1.k2.v0.v1.v2, bf16[3,768,512]{2,1,0:T(8,128)(2,1)} %qkv.2.q_ref.k0.k1.k2.v0.v1.v2, bf16[3,768,512]{2,1,0:T(8,128)(2,1)} %qkv.2.q_ref.k0.k1.k2.v0.v1.v2, ...), custom_call_target="tpu_custom_call" | custom-call | flops 402653184 | bytes 2097152 | tf_op jit(solution)/shard_map/attend/pallas_call | solution.py:350
  159.1 26.5 %collective-permute-start.14 = (bf16[256,512]{1,0:T(8,128)(2,1)}, bf16[256,512]{1,0:T(8,128)(2,1)S(1)}, u32[]{:S(2)}, u32[]{:S(2)}) collective-permute-start(bf16[256,512]{1,0:T(8,128)(2,1)} %attend.4.own_ref), channel_id=1, source_target_pairs={{0,1},{1,0},{2,3},{3,2},{4,5},{5,4},{6,7},{7,6},{8,9},{9,8},{10,11... | collective-permute-start | bytes 786440 | tf_op jit(solution)/shard_map/ppermute | solution.py:122
  185.6 1.9 pad_maximum_fusion
  187.5 5.4 %collective-permute-done.14.other_ref = bf16[256,512]{1,0:T(8,128)(2,1)S(1)} collective-permute-done((bf16[256,512]{1,0:T(8,128)(2,1)}, bf16[256,512]{1,0:T(8,128)(2,1)S(1)}, u32[]{:S(2)}, u32[]{:S(2)}) %collective-permute-start.14) | collective-permute-done | bytes 262176 | tf_op jit(solution)/shard_map/ppermute | solution.py:122
  193.6 4.6 %project.4 = (f32[256,512]{1,0:T(8,128)}, bf16[256,512]{1,0:T(8,128)(2,1)}, bf16[256,512]{1,0:T(8,128)(2,1)}) custom-call(s32[1]{0:T(128)} %bitcast.1.place_ref, s32[1]{0:T(128)} %bitcast.2.ring_ref, bf16[256,512]{1,0:T(8,128)(2,1)} %attend.4.own_ref, bf16[256,512]{1,0:T(8,128)(2,1)} %copy-done.23, bf16[256,1024]{1,0:T(8,128)(2,1)} %get-tuple-element.78.refs_0_, ...), custom_call_target="tpu_custom_call" | custom-call | flops 1073741824 | bytes 5767168 | tf_op jit(solution)/shard_map/project/pallas_call | solution.py:399
  198.2 6.3 %qkv.3.q_ref.k2.v2.k1.v1.k0.v0 = bf16[3,256,512]{2,1,0:T(8,128)(2,1)} custom-call(s32[1]{0:T(128)} %bitcast.2.ring_ref, bf16[4,256,512]{2,1,0:T(8,128)(2,1)} %bitcast.10, f32[256,128]{1,0:T(8,128)} %get-tuple-element.112.cosine_ref, f32[256,128]{1,0:T(8,128)} %get-tuple-element.111.sine_ref, bf16[256,1536]{1,0:T(8,128)(2,1)} %get-tuple-element.70.refs_0_, ...), custom_call_target="tpu_custom_call" | custom-call | flops 1610612736 | bytes 8912896 | tf_op jit(solution)/shard_map/qkv/pallas_call | solution.py:302
  204.4 4.0 %attend.7.own_ref = bf16[256,512]{1,0:T(8,128)(2,1)} custom-call(bf16[3,768,512]{2,1,0:T(8,128)(2,1)} %qkv.2.q_ref.k0.k1.k2.v0.v1.v2, bf16[3,256,512]{2,1,0:T(8,128)(2,1)} %qkv.3.q_ref.k2.v2.k1.v1.k0.v0, bf16[3,768,512]{2,1,0:T(8,128)(2,1)} %qkv.2.q_ref.k0.k1.k2.v0.v1.v2, bf16[3,768,512]{2,1,0:T(8,128)(2,1)} %qkv.2.q_ref.k0.k1.k2.v0.v1.v2, ...), custom_call_target="tpu_custom_call" | custom-call | flops 402653184 | bytes 2097152 | tf_op jit(solution)/shard_map/attend/pallas_call | solution.py:350
  208.5 2.0 collective-permute-start.29
  210.4 1.0 copy-done
  211.4 4.0 %attend.6.own_ref = bf16[256,512]{1,0:T(8,128)(2,1)} custom-call(bf16[3,768,512]{2,1,0:T(8,128)(2,1)} %qkv.2.q_ref.k0.k1.k2.v0.v1.v2, bf16[2,512,512]{2,1,0:T(8,128)(2,1)} %copy-done, bf16[3,256,512]{2,1,0:T(8,128)(2,1)} %qkv.3.q_ref.k2.v2.k1.v1.k0.v0, bf16[3,768,512]{2,1,0:T(8,128)(2,1)} %qkv.2.q_ref.k0.k1.k2.v0.v1.v2, bf16[2,512,512]{2,1,0:T(8,128)(2,1)} %copy-done, ...), custom_call_target="tpu_custom_call" | custom-call | flops 402653184 | bytes 2097152 | tf_op jit(solution)/shard_map/attend/pallas_call | solution.py:350
  215.5 0.8 collective-permute-start.32
  216.3 4.0 %attend.5.own_ref = bf16[256,512]{1,0:T(8,128)(2,1)} custom-call(bf16[3,256,512]{2,1,0:T(8,128)(2,1)} %qkv.3.q_ref.k2.v2.k1.v1.k0.v0, bf16[2,512,512]{2,1,0:T(8,128)(2,1)} %copy-done, bf16[2,512,512]{2,1,0:T(8,128)(2,1)} %copy-done, bf16[3,256,512]{2,1,0:T(8,128)(2,1)} %qkv.3.q_ref.k2.v2.k1.v1.k0.v0, bf16[2,512,512]{2,1,0:T(8,128)(2,1)} %copy-done, ...), custom_call_target="tpu_custom_call" | custom-call | flops 402653184 | bytes 2097152 | tf_op jit(solution)/shard_map/attend/pallas_call | solution.py:350
  220.3 3.1 %collective-permute-start.23 = (bf16[256,512]{1,0:T(8,128)(2,1)}, bf16[256,512]{1,0:T(8,128)(2,1)S(1)}, u32[]{:S(2)}, u32[]{:S(2)}) collective-permute-start(bf16[256,512]{1,0:T(8,128)(2,1)} %attend.5.own_ref), channel_id=1, source_target_pairs={{0,1},{1,0},{2,3},{3,2},{4,5},{5,4},{6,7},{7,6},{8,9},{9,8},{10,11... | collective-permute-start | bytes 786440 | tf_op jit(solution)/shard_map/ppermute | solution.py:122
  223.4 1.3 collective-permute-start.33
  225.4 4.6 %project.7 = (f32[256,512]{1,0:T(8,128)}, bf16[256,512]{1,0:T(8,128)(2,1)}, bf16[256,512]{1,0:T(8,128)(2,1)}) custom-call(s32[1]{0:T(128)} %bitcast.1.place_ref, s32[1]{0:T(128)} %bitcast.2.ring_ref, bf16[256,512]{1,0:T(8,128)(2,1)} %attend.7.own_ref, bf16[256,512]{1,0:T(8,128)(2,1)} %copy-done.22, bf16[256,1024]{1,0:T(8,128)(2,1)} %get-tuple-element.78.refs_0_, ...), custom_call_target="tpu_custom_call" | custom-call | flops 1073741824 | bytes 5767168 | tf_op jit(solution)/shard_map/project/pallas_call | solution.py:399
  230.8 1.3 collective-permute-start.31
  232.1 4.6 %project.6 = (f32[256,512]{1,0:T(8,128)}, bf16[256,512]{1,0:T(8,128)(2,1)}, bf16[256,512]{1,0:T(8,128)(2,1)}) custom-call(s32[1]{0:T(128)} %bitcast.1.place_ref, s32[1]{0:T(128)} %bitcast.2.ring_ref, bf16[256,512]{1,0:T(8,128)(2,1)} %attend.6.own_ref, bf16[256,512]{1,0:T(8,128)(2,1)} %copy-done.21, bf16[256,1024]{1,0:T(8,128)(2,1)} %get-tuple-element.78.refs_0_, ...), custom_call_target="tpu_custom_call" | custom-call | flops 1073741824 | bytes 5767168 | tf_op jit(solution)/shard_map/project/pallas_call | solution.py:399
  236.7 0.9 collective-permute-start.27
  237.6 1.3 collective-permute-start.28
  238.9 4.7 %project.5 = (f32[256,512]{1,0:T(8,128)}, bf16[256,512]{1,0:T(8,128)(2,1)}, bf16[256,512]{1,0:T(8,128)(2,1)}) custom-call(s32[1]{0:T(128)} %bitcast.1.place_ref, s32[1]{0:T(128)} %bitcast.2.ring_ref, bf16[256,512]{1,0:T(8,128)(2,1)} %attend.5.own_ref, bf16[256,512]{1,0:T(8,128)(2,1)} %copy-done.20, bf16[256,1024]{1,0:T(8,128)(2,1)} %get-tuple-element.78.refs_0_, ...), custom_call_target="tpu_custom_call" | custom-call | flops 1073741824 | bytes 5767168 | tf_op jit(solution)/shard_map/project/pallas_call | solution.py:399
  244.3 1.3 collective-permute-start.25
  245.6 3.4 %final.4.rest_0_ = bf16[1024,4,512]{2,1,0:T(4,128)(2,1)} custom-call(f32[4,6]{1,0:T(4,128)} %static_ref.11, bf16[1024,4,512]{2,1,0:T(4,128)(2,1)} %x_ref.13, f32[8,5248]{1,0:T(8,128)} %get-tuple-element.58.first_ref.folded_ref.column_ref, f32[8,5248]{1,0:T(8,128)} %get-tuple-element.58.first_ref.folded_ref.column_ref, ...), custom_call_target="tpu_custom_call" | custom-call | flops 629145600 | bytes 2883584 | tf_op jit(solution)/shard_map/final/pallas_call | solution.py:478
  249.1 1.5 collective-permute-done.31.outer_ref
  250.6 0.7 copy-done.25
  251.3 3.4 %final.5.rest_0_ = bf16[1024,4,512]{2,1,0:T(4,128)(2,1)} custom-call(f32[4,6]{1,0:T(4,128)} %static_ref.11, bf16[1024,4,512]{2,1,0:T(4,128)(2,1)} %x_ref.13, f32[8,5248]{1,0:T(8,128)} %get-tuple-element.58.first_ref.folded_ref.column_ref, f32[8,5248]{1,0:T(8,128)} %get-tuple-element.58.first_ref.folded_ref.column_ref, ...), custom_call_target="tpu_custom_call", output_to_operand_aliasing={{}: (8, {})} | custom-call | flops 629145600 | bytes 2883584 | tf_op jit(solution)/shard_map/final/pallas_call | solution.py:478
  254.7 7.1 %collective-permute-done.28.outer_ref = bf16[256,512]{1,0:T(8,128)(2,1)S(1)} collective-permute-done((bf16[256,512]{1,0:T(8,128)(2,1)}, bf16[256,512]{1,0:T(8,128)(2,1)S(1)}, u32[]{:S(2)}, u32[]{:S(2)}) %collective-permute-start.28) | collective-permute-done | bytes 262176 | tf_op jit(solution)/shard_map/ppermute | solution.py:573
  262.5 3.4 %final.6.rest_0_ = bf16[1024,4,512]{2,1,0:T(4,128)(2,1)} custom-call(f32[4,6]{1,0:T(4,128)} %static_ref.11, bf16[1024,4,512]{2,1,0:T(4,128)(2,1)} %x_ref.13, f32[8,5248]{1,0:T(8,128)} %get-tuple-element.58.first_ref.folded_ref.column_ref, f32[8,5248]{1,0:T(8,128)} %get-tuple-element.58.first_ref.folded_ref.column_ref, ...), custom_call_target="tpu_custom_call", output_to_operand_aliasing={{}: (8, {})} | custom-call | flops 629145600 | bytes 2883584 | tf_op jit(solution)/shard_map/final/pallas_call | solution.py:478
  265.9 4.6 %collective-permute-done.25.outer_ref = bf16[256,512]{1,0:T(8,128)(2,1)S(1)} collective-permute-done((bf16[256,512]{1,0:T(8,128)(2,1)}, bf16[256,512]{1,0:T(8,128)(2,1)S(1)}, u32[]{:S(2)}, u32[]{:S(2)}) %collective-permute-start.25) | collective-permute-done | bytes 262176 | tf_op jit(solution)/shard_map/ppermute | solution.py:573
  271.2 3.4 %final.7 = bf16[1024,4,512]{2,1,0:T(4,128)(2,1)} custom-call(f32[4,6]{1,0:T(4,128)} %static_ref.11, bf16[1024,4,512]{2,1,0:T(4,128)(2,1)} %x_ref.13, f32[8,5248]{1,0:T(8,128)} %get-tuple-element.58.first_ref.folded_ref.column_ref, f32[8,5248]{1,0:T(8,128)} %get-tuple-element.58.first_ref.folded_ref.column_ref, ...), custom_call_target="tpu_custom_call", output_to_operand_aliasing={{}: (8, {})} | custom-call | flops 629145600 | bytes 2883584 | tf_op jit(solution)/shard_map/final/pallas_call | solution.py:478
  (127 shorter events, 7.7 us)
Async XLA Ops:
  6.5 132.6 %all-gather.5.cloned.1.call-start = ((), (), s32[]{:S(2)}) async-start(), calls=%async_computation.1 | async-start | bytes 3932160 | tf_op jit(solution)/shard_map/all_gather | solution.py:505
  14.4 11.8 %collective-permute-start = (f32[8,5248]{1,0:T(8,128)}, f32[8,5248]{1,0:T(8,128)S(1)}, u32[]{:S(2)}, u32[]{:S(2)}) collective-permute-start(f32[8,5248]{1,0:T(8,128)} %stats.1.own_ref), channel_id=1, source_target_pairs={{0,1},{1,2},{2,3},{3,0},{4,5},{5,6},{6,7},{7,4},{8,9},{9,10},{10,1... | collective-permute-start | bytes 503816 | tf_op jit(solution)/shard_map/ppermute | solution.py:31
  17.5 13.8 %collective-permute-start.1 = (f32[8,5248]{1,0:T(8,128)}, f32[8,5248]{1,0:T(8,128)S(1)}, u32[]{:S(2)}, u32[]{:S(2)}) collective-permute-start(f32[8,5248]{1,0:T(8,128)} %stats.1.own_ref), channel_id=1, source_target_pairs={{0,2},{1,3},{2,0},{3,1},{4,6},{5,7},{6,4},{7,5},{8,10},{9,11},{10,... | collective-permute-start | bytes 503816 | tf_op jit(solution)/shard_map/ppermute | solution.py:31
  20.1 11.2 %collective-permute-start.2 = (f32[8,5248]{1,0:T(8,128)}, f32[8,5248]{1,0:T(8,128)S(1)}, u32[]{:S(2)}, u32[]{:S(2)}) collective-permute-start(f32[8,5248]{1,0:T(8,128)} %stats.1.own_ref), channel_id=1, source_target_pairs={{0,3},{1,0},{2,1},{3,2},{4,7},{5,4},{6,5},{7,6},{8,11},{9,8},{10,9... | collective-permute-start | bytes 503816 | tf_op jit(solution)/shard_map/ppermute | solution.py:31
  26.3 9.1 %copy-start.12 = (f32[8,5248]{1,0:T(8,128)}, f32[8,5248]{1,0:T(8,128)S(1)}, u32[]{:S(2)}) copy-start(f32[8,5248]{1,0:T(8,128)S(1)} %collective-permute-done.a_ref) | copy-start | bytes 503812
  31.3 4.1 %copy-start.13 = (f32[8,5248]{1,0:T(8,128)}, f32[8,5248]{1,0:T(8,128)S(1)}, u32[]{:S(2)}) copy-start(f32[8,5248]{1,0:T(8,128)S(1)} %collective-permute-done.1.b_ref) | copy-start | bytes 503812
  31.3 4.1 %copy-start.14 = (f32[8,5248]{1,0:T(8,128)}, f32[8,5248]{1,0:T(8,128)S(1)}, u32[]{:S(2)}) copy-start(f32[8,5248]{1,0:T(8,128)S(1)} %collective-permute-done.2.c_ref) | copy-start | bytes 503812
  31.3 12.3 %copy-start.33 = (bf16[64,2560]{1,0:T(8,128)(2,1)S(1)}, bf16[64,2560]{1,0:T(8,128)(2,1)}, u32[]{:S(2)}) copy-start(bf16[64,2560]{1,0:T(8,128)(2,1)} %get-tuple-element.66) | copy-start | bytes 983044
  31.3 13.8 %copy-start.32 = (bf16[64,2560]{1,0:T(8,128)(2,1)S(1)}, bf16[64,2560]{1,0:T(8,128)(2,1)}, u32[]{:S(2)}) copy-start(bf16[64,2560]{1,0:T(8,128)(2,1)} %get-tuple-element.67) | copy-start | bytes 983044
  31.3 12.2 %collective-permute-start.3 = (bf16[64,2560]{1,0:T(8,128)(2,1)}, bf16[64,2560]{1,0:T(8,128)(2,1)S(1)}, u32[]{:S(2)}, u32[]{:S(2)}) collective-permute-start(bf16[64,2560]{1,0:T(8,128)(2,1)} %get-tuple-element.59), channel_id=1, source_target_pairs={{0,1},{1,2},{2,3},{3,0},{4,5},{5,6},{6,7},{7,4},{8,9},{9,10},{10,1... | collective-permute-start | bytes 983048 | tf_op jit(solution)/shard_map/ppermute | solution.py:509
  38.2 42.9 %copy-start.31 = (s32[2]{0:T(128)S(1)}, s32[2]{0:T(128)}, u32[]{:S(2)}) copy-start(s32[2]{0:T(128)} %param.11) | copy-start | bytes 28
  38.2 44.1 %copy-start.30 = (s32[1024]{0:T(1024)S(1)}, s32[1024]{0:T(1024)}, u32[]{:S(2)}) copy-start(s32[1024]{0:T(1024)} %param.10) | copy-start | bytes 12292
  43.5 30.2 %copy-start.15 = (bf16[64,2560]{1,0:T(8,128)(2,1)}, bf16[64,2560]{1,0:T(8,128)(2,1)S(1)}, u32[]{:S(2)}) copy-start(bf16[64,2560]{1,0:T(8,128)(2,1)S(1)} %collective-permute-done.3.refs_1_) | copy-start | bytes 983044
  43.6 154.6 %all-gather.3.cloned.1.call-start = ((), (), s32[]{:S(2)}) async-start(), calls=%async_computation | async-start | bytes 1310720 | tf_op jit(solution)/shard_map/all_gather | solution.py:505
  43.6 30.1 %collective-permute-start.5 = (bf16[64,2560]{1,0:T(8,128)(2,1)S(1)}, bf16[64,2560]{1,0:T(8,128)(2,1)S(1)}, u32[]{:S(2)}, u32[]{:S(2)}) collective-permute-start(bf16[64,2560]{1,0:T(8,128)(2,1)S(1)} %copy-done.33), channel_id=1, source_target_pairs={{0,2},{1,3},{2,0},{3,1},{4,6},{5,7},{6,4},{7,5},{8,10},{9,11},{10,... | collective-permute-start | bytes 983048 | tf_op jit(solution)/shard_map/ppermute | solution.py:509
  45.1 28.7 %collective-permute-start.6 = (bf16[64,2560]{1,0:T(8,128)(2,1)S(1)}, bf16[64,2560]{1,0:T(8,128)(2,1)S(1)}, u32[]{:S(2)}, u32[]{:S(2)}) collective-permute-start(bf16[64,2560]{1,0:T(8,128)(2,1)S(1)} %copy-done.32), channel_id=1, source_target_pairs={{0,3},{1,0},{2,1},{3,2},{4,7},{5,4},{6,5},{7,6},{8,11},{9,8},{10,9... | collective-permute-start | bytes 983048 | tf_op jit(solution)/shard_map/ppermute | solution.py:509
  77.6 43.4 %copy-start.1 = (bf16[256,1024]{1,0:T(8,128)(2,1)S(1)}, bf16[256,1024]{1,0:T(8,128)(2,1)}, u32[]{:S(2)}) copy-start(bf16[256,1024]{1,0:T(8,128)(2,1)} %get-tuple-element.78.refs_0_) | copy-start | bytes 1572868
  77.6 20.7 %collective-permute-start.8 = (bf16[256,1536]{1,0:T(8,128)(2,1)}, bf16[256,1536]{1,0:T(8,128)(2,1)S(1)}, u32[]{:S(2)}, u32[]{:S(2)}) collective-permute-start(bf16[256,1536]{1,0:T(8,128)(2,1)} %get-tuple-element.70.refs_0_), channel_id=1, source_target_pairs={{0,8},{4,12},{8,0},{12,4},{16,24},{20,28},{24,16},{28,20},{1,9},{5... | collective-permute-start | bytes 2359304 | tf_op jit(solution)/shard_map/ppermute | solution.py:122
  79.2 29.8 %collective-permute-start.10 = (bf16[256,1536]{1,0:T(8,128)(2,1)}, bf16[256,1536]{1,0:T(8,128)(2,1)S(1)}, u32[]{:S(2)}, u32[]{:S(2)}) collective-permute-start(bf16[256,1536]{1,0:T(8,128)(2,1)} %get-tuple-element.70.refs_0_), channel_id=1, source_target_pairs={{0,16},{4,20},{8,24},{12,28},{16,0},{20,4},{24,8},{28,12},{1,17},{... | collective-permute-start | bytes 2359304 | tf_op jit(solution)/shard_map/ppermute | solution.py:122
  80.7 28.3 %collective-permute-start.12 = (bf16[256,1536]{1,0:T(8,128)(2,1)}, bf16[256,1536]{1,0:T(8,128)(2,1)S(1)}, u32[]{:S(2)}, u32[]{:S(2)}) collective-permute-start(bf16[256,1536]{1,0:T(8,128)(2,1)} %get-tuple-element.70.refs_0_), channel_id=1, source_target_pairs={{0,24},{4,28},{8,16},{12,20},{16,8},{20,12},{24,0},{28,4},{1,25},{... | collective-permute-start | bytes 2359304 | tf_op jit(solution)/shard_map/ppermute | solution.py:122
  82.4 28.8 %collective-permute-start.4 = (s32[512]{0:T(512)S(1)}, s32[512]{0:T(512)S(1)}, u32[]{:S(2)}, u32[]{:S(2)}) collective-permute-start(s32[512]{0:T(512)S(1)} %get-tuple-element.104), channel_id=1, source_target_pairs={{0,4},{4,8},{8,12},{12,16},{16,20},{20,24},{24,28},{1,5},{5,9},{9,... | collective-permute-start | bytes 6152 | tf_op jit(solution)/shard_map/ppermute | solution.py:25
  83.7 27.6 %collective-permute-start.7 = (bf16[256,1536]{1,0:T(8,128)(2,1)}, bf16[256,1536]{1,0:T(8,128)(2,1)}, u32[]{:S(2)}, u32[]{:S(2)}) collective-permute-start(bf16[256,1536]{1,0:T(8,128)(2,1)} %get-tuple-element.70.refs_0_), channel_id=1, source_target_pairs={{0,4},{4,0},{8,12},{12,8},{16,20},{20,16},{24,28},{28,24},{1,5},{5... | collective-permute-start | bytes 2359304 | tf_op jit(solution)/shard_map/ppermute | solution.py:122
  98.3 40.8 %copy-start.9 = (bf16[256,1536]{1,0:T(8,128)(2,1)}, bf16[256,1536]{1,0:T(8,128)(2,1)S(1)}, u32[]{:S(2)}) copy-start(bf16[256,1536]{1,0:T(8,128)(2,1)S(1)} %collective-permute-done.8.refs_2_) | copy-start | bytes 2359300
  98.3 13.0 %collective-permute-start.9 = (bf16[256,1536]{1,0:T(8,128)(2,1)S(1)}, bf16[256,1536]{1,0:T(8,128)(2,1)}, u32[]{:S(2)}, u32[]{:S(2)}) collective-permute-start(bf16[256,1536]{1,0:T(8,128)(2,1)S(1)} %collective-permute-done.8.refs_2_), channel_id=1, source_target_pairs={{0,4},{4,0},{8,12},{12,8},{16,20},{20,16},{24,28},{28,24},{1,5},{5... | collective-permute-start | bytes 2359304 | tf_op jit(solution)/shard_map/ppermute | solution.py:122
  109.0 3.5 %copy-start.10 = (bf16[256,1536]{1,0:T(8,128)(2,1)}, bf16[256,1536]{1,0:T(8,128)(2,1)S(1)}, u32[]{:S(2)}) copy-start(bf16[256,1536]{1,0:T(8,128)(2,1)S(1)} %collective-permute-done.10.refs_4_) | copy-start | bytes 2359300
  109.0 2.4 collective-permute-start.11
  109.0 3.5 %copy-start.11 = (bf16[256,1536]{1,0:T(8,128)(2,1)}, bf16[256,1536]{1,0:T(8,128)(2,1)S(1)}, u32[]{:S(2)}) copy-start(bf16[256,1536]{1,0:T(8,128)(2,1)S(1)} %collective-permute-done.12.refs_6_) | copy-start | bytes 2359300
  109.0 3.5 %collective-permute-start.13 = (bf16[256,1536]{1,0:T(8,128)(2,1)S(1)}, bf16[256,1536]{1,0:T(8,128)(2,1)}, u32[]{:S(2)}, u32[]{:S(2)}) collective-permute-start(bf16[256,1536]{1,0:T(8,128)(2,1)S(1)} %collective-permute-done.12.refs_6_), channel_id=1, source_target_pairs={{0,4},{4,0},{8,12},{12,8},{16,20},{20,16},{24,28},{28,24},{1,5},{5... | collective-permute-start | bytes 2359304 | tf_op jit(solution)/shard_map/ppermute | solution.py:122
  112.5 15.0 %collective-permute-start.16 = (bf16[256,1024]{1,0:T(8,128)(2,1)}, bf16[256,1024]{1,0:T(8,128)(2,1)S(1)}, u32[]{:S(2)}, u32[]{:S(2)}) collective-permute-start(bf16[256,1024]{1,0:T(8,128)(2,1)} %get-tuple-element.78.refs_0_), channel_id=1, source_target_pairs={{0,8},{4,12},{8,0},{12,4},{16,24},{20,28},{24,16},{28,20},{1,9},{5... | collective-permute-start | bytes 1572872 | tf_op jit(solution)/shard_map/ppermute | solution.py:122
  112.7 24.7 %collective-permute-start.18 = (bf16[256,1024]{1,0:T(8,128)(2,1)}, bf16[256,1024]{1,0:T(8,128)(2,1)S(1)}, u32[]{:S(2)}, u32[]{:S(2)}) collective-permute-start(bf16[256,1024]{1,0:T(8,128)(2,1)} %get-tuple-element.78.refs_0_), channel_id=1, source_target_pairs={{0,16},{4,20},{8,24},{12,28},{16,0},{20,4},{24,8},{28,12},{1,17},{... | collective-permute-start | bytes 1572872 | tf_op jit(solution)/shard_map/ppermute | solution.py:122
  114.6 24.3 %collective-permute-start.20 = (bf16[256,1024]{1,0:T(8,128)(2,1)}, bf16[256,1024]{1,0:T(8,128)(2,1)S(1)}, u32[]{:S(2)}, u32[]{:S(2)}) collective-permute-start(bf16[256,1024]{1,0:T(8,128)(2,1)} %get-tuple-element.78.refs_0_), channel_id=1, source_target_pairs={{0,24},{4,28},{8,16},{12,20},{16,8},{20,12},{24,0},{28,4},{1,25},{... | collective-permute-start | bytes 1572872 | tf_op jit(solution)/shard_map/ppermute | solution.py:122
  119.6 19.4 %copy-start.5 = (f32[1024,64]{1,0:T(8,128)}, f32[1024,64]{1,0:T(8,128)S(1)}, u32[]{:S(2)}) copy-start(f32[1024,64]{1,0:T(8,128)S(1)} %get-tuple-element.97) | copy-start | bytes 786436
  119.6 19.4 %copy-start.7 = (f32[1024,64]{1,0:T(8,128)}, f32[1024,64]{1,0:T(8,128)S(1)}, u32[]{:S(2)}) copy-start(f32[1024,64]{1,0:T(8,128)S(1)} %get-tuple-element.98) | copy-start | bytes 786436
  119.6 19.4 %copy-start.8 = (f32[1024,64]{1,0:T(8,128)}, f32[1024,64]{1,0:T(8,128)S(1)}, u32[]{:S(2)}) copy-start(f32[1024,64]{1,0:T(8,128)S(1)} %get-tuple-element.99) | copy-start | bytes 786436
  121.0 38.1 %collective-permute-start.15 = (bf16[256,1024]{1,0:T(8,128)(2,1)S(1)}, bf16[256,1024]{1,0:T(8,128)(2,1)}, u32[]{:S(2)}, u32[]{:S(2)}) collective-permute-start(bf16[256,1024]{1,0:T(8,128)(2,1)S(1)} %copy-done.1), channel_id=1, source_target_pairs={{0,4},{4,0},{8,12},{12,8},{16,20},{20,16},{24,28},{28,24},{1,5},{5... | collective-permute-start | bytes 1572872 | tf_op jit(solution)/shard_map/ppermute | solution.py:122
  127.5 22.0 %copy-start.2 = (bf16[256,1024]{1,0:T(8,128)(2,1)}, bf16[256,1024]{1,0:T(8,128)(2,1)S(1)}, u32[]{:S(2)}) copy-start(bf16[256,1024]{1,0:T(8,128)(2,1)S(1)} %collective-permute-done.16.refs_2_) | copy-start | bytes 1572868
  127.5 60.0 %collective-permute-start.17 = (bf16[256,1024]{1,0:T(8,128)(2,1)S(1)}, bf16[256,1024]{1,0:T(8,128)(2,1)}, u32[]{:S(2)}, u32[]{:S(2)}) collective-permute-start(bf16[256,1024]{1,0:T(8,128)(2,1)S(1)} %collective-permute-done.16.refs_2_), channel_id=1, source_target_pairs={{0,4},{4,0},{8,12},{12,8},{16,20},{20,16},{24,28},{28,24},{1,5},{5... | collective-permute-start | bytes 1572872 | tf_op jit(solution)/shard_map/ppermute | solution.py:122
  137.4 12.1 %copy-start.3 = (bf16[256,1024]{1,0:T(8,128)(2,1)}, bf16[256,1024]{1,0:T(8,128)(2,1)S(1)}, u32[]{:S(2)}) copy-start(bf16[256,1024]{1,0:T(8,128)(2,1)S(1)} %collective-permute-done.18.refs_4_) | copy-start | bytes 1572868
  137.4 50.1 %collective-permute-start.19 = (bf16[256,1024]{1,0:T(8,128)(2,1)S(1)}, bf16[256,1024]{1,0:T(8,128)(2,1)}, u32[]{:S(2)}, u32[]{:S(2)}) collective-permute-start(bf16[256,1024]{1,0:T(8,128)(2,1)S(1)} %collective-permute-done.18.refs_4_), channel_id=1, source_target_pairs={{0,4},{4,0},{8,12},{12,8},{16,20},{20,16},{24,28},{28,24},{1,5},{5... | collective-permute-start | bytes 1572872 | tf_op jit(solution)/shard_map/ppermute | solution.py:122
  139.0 10.5 %copy-start.4 = (bf16[256,1024]{1,0:T(8,128)(2,1)}, bf16[256,1024]{1,0:T(8,128)(2,1)S(1)}, u32[]{:S(2)}) copy-start(bf16[256,1024]{1,0:T(8,128)(2,1)S(1)} %collective-permute-done.20.refs_6_) | copy-start | bytes 1572868
  139.0 48.5 %collective-permute-start.21 = (bf16[256,1024]{1,0:T(8,128)(2,1)S(1)}, bf16[256,1024]{1,0:T(8,128)(2,1)}, u32[]{:S(2)}, u32[]{:S(2)}) collective-permute-start(bf16[256,1024]{1,0:T(8,128)(2,1)S(1)} %collective-permute-done.20.refs_6_), channel_id=1, source_target_pairs={{0,4},{4,0},{8,12},{12,8},{16,20},{20,16},{24,28},{28,24},{1,5},{5... | collective-permute-start | bytes 1572872 | tf_op jit(solution)/shard_map/ppermute | solution.py:122
  151.8 58.7 %collective-permute-start.22 = (bf16[2,512,512]{2,1,0:T(8,128)(2,1)}, bf16[2,512,512]{2,1,0:T(8,128)(2,1)S(1)}, u32[]{:S(2)}, u32[]{:S(2)}) collective-permute-start(bf16[2,512,512]{2,1,0:T(8,128)(2,1)} %slice.58), channel_id=1, source_target_pairs={{0,4},{4,8},{8,12},{12,16},{16,20},{20,24},{24,28},{1,5},{5,9},{9,... | collective-permute-start | bytes 3145736 | tf_op jit(solution)/shard_map/ppermute | solution.py:25
  155.0 30.6 %copy-start.6 = (f32[1024,64]{1,0:T(8,128)S(1)}, f32[1024,64]{1,0:T(8,128)}, u32[]{:S(2)}) copy-start(f32[1024,64]{1,0:T(8,128)} %copy-done.5) | copy-start | bytes 786436
  159.1 33.8 %collective-permute-start.14 = (bf16[256,512]{1,0:T(8,128)(2,1)}, bf16[256,512]{1,0:T(8,128)(2,1)S(1)}, u32[]{:S(2)}, u32[]{:S(2)}) collective-permute-start(bf16[256,512]{1,0:T(8,128)(2,1)} %attend.4.own_ref), channel_id=1, source_target_pairs={{0,1},{1,0},{2,3},{3,2},{4,5},{5,4},{6,7},{7,6},{8,9},{9,8},{10,11... | collective-permute-start | bytes 786440 | tf_op jit(solution)/shard_map/ppermute | solution.py:122
  208.5 7.0 %copy-start.35 = (bf16[256,512]{1,0:T(8,128)(2,1)S(1)}, bf16[256,512]{1,0:T(8,128)(2,1)}, u32[]{:S(2)}) copy-start(bf16[256,512]{1,0:T(8,128)(2,1)} %get-tuple-element.93) | copy-start | bytes 786436
  208.5 16.2 %collective-permute-start.29 = (bf16[256,512]{1,0:T(8,128)(2,1)}, bf16[256,512]{1,0:T(8,128)(2,1)S(1)}, u32[]{:S(2)}, u32[]{:S(2)}) collective-permute-start(bf16[256,512]{1,0:T(8,128)(2,1)} %attend.7.own_ref), channel_id=1, source_target_pairs={{0,1},{1,0},{2,3},{3,2},{4,5},{5,4},{6,7},{7,6},{8,9},{9,8},{10,11... | collective-permute-start | bytes 786440 | tf_op jit(solution)/shard_map/ppermute | solution.py:122
  215.4 8.0 %copy-start.34 = (bf16[256,512]{1,0:T(8,128)(2,1)S(1)}, bf16[256,512]{1,0:T(8,128)(2,1)}, u32[]{:S(2)}) copy-start(bf16[256,512]{1,0:T(8,128)(2,1)} %get-tuple-element.94) | copy-start | bytes 786436
  215.4 15.3 %collective-permute-start.26 = (bf16[256,512]{1,0:T(8,128)(2,1)}, bf16[256,512]{1,0:T(8,128)(2,1)S(1)}, u32[]{:S(2)}, u32[]{:S(2)}) collective-permute-start(bf16[256,512]{1,0:T(8,128)(2,1)} %attend.6.own_ref), channel_id=1, source_target_pairs={{0,1},{1,0},{2,3},{3,2},{4,5},{5,4},{6,7},{7,6},{8,9},{9,8},{10,11... | collective-permute-start | bytes 786440 | tf_op jit(solution)/shard_map/ppermute | solution.py:122
  215.5 21.2 %collective-permute-start.32 = (bf16[256,512]{1,0:T(8,128)(2,1)S(1)}, bf16[256,512]{1,0:T(8,128)(2,1)S(1)}, u32[]{:S(2)}, u32[]{:S(2)}) collective-permute-start(bf16[256,512]{1,0:T(8,128)(2,1)S(1)} %copy-done.35), channel_id=1, source_target_pairs={{1,2},{2,1},{5,6},{6,5},{9,10},{10,9},{13,14},{14,13},{17,18},{18,... | collective-permute-start | bytes 786440 | tf_op jit(solution)/shard_map/ppermute | solution.py:572
  220.3 17.3 %collective-permute-start.23 = (bf16[256,512]{1,0:T(8,128)(2,1)}, bf16[256,512]{1,0:T(8,128)(2,1)S(1)}, u32[]{:S(2)}, u32[]{:S(2)}) collective-permute-start(bf16[256,512]{1,0:T(8,128)(2,1)} %attend.5.own_ref), channel_id=1, source_target_pairs={{0,1},{1,0},{2,3},{3,2},{4,5},{5,4},{6,7},{7,6},{8,9},{9,8},{10,11... | collective-permute-start | bytes 786440 | tf_op jit(solution)/shard_map/ppermute | solution.py:122
  223.4 20.2 %collective-permute-start.33 = (bf16[256,512]{1,0:T(8,128)(2,1)S(1)}, bf16[256,512]{1,0:T(8,128)(2,1)S(1)}, u32[]{:S(2)}, u32[]{:S(2)}) collective-permute-start(bf16[256,512]{1,0:T(8,128)(2,1)S(1)} %copy-done.34), channel_id=1, source_target_pairs={{1,3},{2,0},{5,7},{6,4},{9,11},{10,8},{13,15},{14,12},{17,19},{18,... | collective-permute-start | bytes 786440 | tf_op jit(solution)/shard_map/ppermute | solution.py:573
  230.1 14.2 %collective-permute-start.30 = (bf16[256,512]{1,0:T(8,128)(2,1)}, bf16[256,512]{1,0:T(8,128)(2,1)S(1)}, u32[]{:S(2)}, u32[]{:S(2)}) collective-permute-start(bf16[256,512]{1,0:T(8,128)(2,1)} %get-tuple-element.90), channel_id=1, source_target_pairs={{1,2},{2,1},{5,6},{6,5},{9,10},{10,9},{13,14},{14,13},{17,18},{18,... | collective-permute-start | bytes 786440 | tf_op jit(solution)/shard_map/ppermute | solution.py:572
  230.7 1.3 copy-start.21
  230.8 19.8 %collective-permute-start.31 = (bf16[256,512]{1,0:T(8,128)(2,1)}, bf16[256,512]{1,0:T(8,128)(2,1)S(1)}, u32[]{:S(2)}, u32[]{:S(2)}) collective-permute-start(bf16[256,512]{1,0:T(8,128)(2,1)} %get-tuple-element.91), channel_id=1, source_target_pairs={{1,3},{2,0},{5,7},{6,4},{9,11},{10,8},{13,15},{14,12},{17,19},{18,... | collective-permute-start | bytes 786440 | tf_op jit(solution)/shard_map/ppermute | solution.py:573
  236.7 8.9 %copy-start.18 = (bf16[256,512]{1,0:T(8,128)(2,1)}, bf16[256,512]{1,0:T(8,128)(2,1)S(1)}, u32[]{:S(2)}) copy-start(bf16[256,512]{1,0:T(8,128)(2,1)S(1)} %collective-permute-done.32.inner_ref) | copy-start | bytes 786436
  236.7 18.0 %collective-permute-start.27 = (bf16[256,512]{1,0:T(8,128)(2,1)}, bf16[256,512]{1,0:T(8,128)(2,1)S(1)}, u32[]{:S(2)}, u32[]{:S(2)}) collective-permute-start(bf16[256,512]{1,0:T(8,128)(2,1)} %get-tuple-element.87), channel_id=1, source_target_pairs={{1,2},{2,1},{5,6},{6,5},{9,10},{10,9},{13,14},{14,13},{17,18},{18,... | collective-permute-start | bytes 786440 | tf_op jit(solution)/shard_map/ppermute | solution.py:572
  237.6 1.3 copy-start.20
  237.6 24.2 %collective-permute-start.28 = (bf16[256,512]{1,0:T(8,128)(2,1)}, bf16[256,512]{1,0:T(8,128)(2,1)S(1)}, u32[]{:S(2)}, u32[]{:S(2)}) collective-permute-start(bf16[256,512]{1,0:T(8,128)(2,1)} %get-tuple-element.88), channel_id=1, source_target_pairs={{1,3},{2,0},{5,7},{6,4},{9,11},{10,8},{13,15},{14,12},{17,19},{18,... | collective-permute-start | bytes 786440 | tf_op jit(solution)/shard_map/ppermute | solution.py:573
  243.6 2.0 copy-start.19
  243.6 22.3 %collective-permute-start.24 = (bf16[256,512]{1,0:T(8,128)(2,1)}, bf16[256,512]{1,0:T(8,128)(2,1)S(1)}, u32[]{:S(2)}, u32[]{:S(2)}) collective-permute-start(bf16[256,512]{1,0:T(8,128)(2,1)} %get-tuple-element.84), channel_id=1, source_target_pairs={{1,2},{2,1},{5,6},{6,5},{9,10},{10,9},{13,14},{14,13},{17,18},{18,... | collective-permute-start | bytes 786440 | tf_op jit(solution)/shard_map/ppermute | solution.py:572
  244.3 4.8 %copy-start.24 = (bf16[256,512]{1,0:T(8,128)(2,1)}, bf16[256,512]{1,0:T(8,128)(2,1)S(1)}, u32[]{:S(2)}) copy-start(bf16[256,512]{1,0:T(8,128)(2,1)S(1)} %collective-permute-done.30.inner_ref) | copy-start | bytes 786436
  244.3 26.2 %collective-permute-start.25 = (bf16[256,512]{1,0:T(8,128)(2,1)}, bf16[256,512]{1,0:T(8,128)(2,1)S(1)}, u32[]{:S(2)}, u32[]{:S(2)}) collective-permute-start(bf16[256,512]{1,0:T(8,128)(2,1)} %get-tuple-element.85), channel_id=1, source_target_pairs={{1,3},{2,0},{5,7},{6,4},{9,11},{10,8},{13,15},{14,12},{17,19},{18,... | collective-permute-start | bytes 786440 | tf_op jit(solution)/shard_map/ppermute | solution.py:573
  254.7 7.1 %copy-start.26 = (bf16[256,512]{1,0:T(8,128)(2,1)}, bf16[256,512]{1,0:T(8,128)(2,1)S(1)}, u32[]{:S(2)}) copy-start(bf16[256,512]{1,0:T(8,128)(2,1)S(1)} %collective-permute-done.27.inner_ref) | copy-start | bytes 786436
  265.9 4.6 %copy-start.28 = (bf16[256,512]{1,0:T(8,128)(2,1)}, bf16[256,512]{1,0:T(8,128)(2,1)S(1)}, u32[]{:S(2)}) copy-start(bf16[256,512]{1,0:T(8,128)(2,1)S(1)} %collective-permute-done.24.inner_ref) | copy-start | bytes 786436
  (8 other events, 6.0 us)
Sparse Core Ops, SparseCore 0:
  43.7 74.7 all-gather.4
  120.1 48.9 all-gather.2

commit v7 on v5

--- a/solution.py
+++ b/solution.py
@@ -88,30 +88,23 @@
 
 
 def assemble_kernel(place_ref, *refs):
-    qkv_ref, out_ref = refs[-2:]
-    parts = refs[:-2]
+    out_ref = refs[-1]
+    parts = refs[:-1]
     rows = parts[0].shape[0]
-    cut = qkv_ref.shape[1]
     for step, part_ref in enumerate(parts):
         source = (place_ref[0] + len(parts) - step) % len(parts)
-        at = pl.ds(pl.multiple_of(source * rows, rows), rows)
-        qkv_ref[at, :] = part_ref[:, :cut]
-        out_ref[at, :] = part_ref[:, cut:]
+        out_ref[pl.ds(pl.multiple_of(source * rows, rows), rows), :] = part_ref[...]
 
 
 def assemble(place, parts):
     rows, columns = parts[0].shape
-    rows *= len(parts)
     return pl.pallas_call(
         assemble_kernel,
         in_specs=[pl.BlockSpec(memory_space=pltpu.SMEM)]
         + [pl.BlockSpec(memory_space=pltpu.VMEM)] * len(parts),
-        out_specs=[pl.BlockSpec(memory_space=pltpu.VMEM)] * 2,
-        out_shape=[
-            jax.ShapeDtypeStruct((rows, columns // 5 * 3), BF),
-            jax.ShapeDtypeStruct((rows, columns // 5 * 2), BF),
-        ],
-        cost_estimate=cost(0, rows * columns * 4),
+        out_specs=pl.BlockSpec(memory_space=pltpu.VMEM),
+        out_shape=jax.ShapeDtypeStruct((rows * len(parts), columns), BF),
+        cost_estimate=cost(0, rows * columns * len(parts) * 4),
         compiler_params=params(),
         name="assemble",
     )(place, *parts)
@@ -266,8 +259,8 @@
 
 
 def qkv_kernel(ring_ref, rows_ref, cosine_ref, sine_ref, *refs):
-    out_ref = refs[-1]
-    pieces = refs[:-1]
+    out_ref, halo_ref = refs[-2:]
+    pieces = refs[:-2]
     servers, _, width = rows_ref.shape
     depth = pieces[0].shape[0]
     if len(pieces) == 1:
@@ -295,6 +288,8 @@
     def _():
         out_ref[0] = total.astype(BF)
 
+    halo_ref[0] = out_ref[0, -BLOCK:, :]
+
 
 def qkv_columns(ring, rows, pieces, cosine, sine):
     servers, tokens, width = rows.shape
@@ -309,8 +304,14 @@
             table,
         ]
         + [pl.BlockSpec((pieces[0].shape[0], width), lambda j: (0, j))] * len(pieces),
-        out_specs=pl.BlockSpec((1, tokens, width), lambda j: (j, 0, 0)),
-        out_shape=jax.ShapeDtypeStruct((3, tokens, width), BF),
+        out_specs=[
+            pl.BlockSpec((1, tokens, width), lambda j: (j, 0, 0)),
+            pl.BlockSpec((1, BLOCK, width), lambda j: (jnp.maximum(j - 1, 0), 0, 0)),
+        ],
+        out_shape=[
+            jax.ShapeDtypeStruct((3, tokens, width), BF),
+            jax.ShapeDtypeStruct((2, BLOCK, width), BF),
+        ],
         cost_estimate=cost(2 * tokens * D * 3 * width, D * 6 * width + tokens * D * 5),
         compiler_params=params(),
         name="qkv",
@@ -393,8 +394,9 @@
 
 def project(place, ring, own, other, pieces, servers):
     tokens, width = own.shape
-    rows, pair = pieces[0].shape
-    tail = pl.BlockSpec((rows, pair), lambda i: (0, 0))
+    rows, columns = pieces[0].shape
+    pair = 2 * width
+    tail = pl.BlockSpec((pl.Element(rows), pl.Element(pair)), lambda i: (0, columns - pair))
     full = pl.BlockSpec((tokens, width), lambda i: (0, 0))
     return pl.pallas_call(
         project_kernel,
@@ -505,19 +507,16 @@
         rows = lax.all_gather(normed, "mp", axis=0, tiled=True)
         return rows.reshape(group_size, normed.shape[0], width)
 
-    sums_all, normed_late = mix(hc_static, streams, sums, CHUNK, tokens_local - CHUNK)
-    rows_late = gathered(normed_late)
-    _, normed_first = mix(hc_static, streams, sums, 0, CHUNK)
-    rows_first = gathered(normed_first)
-
     for step in range(1, group_size):
         parts[step] = lax.ppermute(
             parts[step], "mp", [(at, (at + step) % group_size) for at in range(group_size)]
         )
-    qkv_part, out_part = assemble(place, parts)
-    qkv_pieces = weight_pieces(qkv_part)
-    out_part, qkv_pieces = lax.optimization_barrier((out_part, qkv_pieces))
-    out_pieces = weight_pieces(out_part)
+    sums_all, normed = mix(hc_static, streams, sums, 0, tokens_local)
+    parts, normed = lax.optimization_barrier((parts, normed))
+    rows = gathered(normed)
+
+    pieces = weight_pieces(assemble(place, parts))
+    rows, pieces = lax.optimization_barrier((rows, pieces))
 
     halo = passed_along(segment_ids[-BLOCK:], "blk", 1)
     halo = jnp.where(lax.axis_index("blk") == 0, -1, halo)
@@ -542,26 +541,20 @@
     key_segments = jnp.stack(windows)[:, None, :]
     query_segments = segment_ids[:, None]
 
-    qkv_late = qkv_columns(ring, rows_late, qkv_pieces, cosine[CHUNK:], sine[CHUNK:])
-    halo_rows = passed_along(qkv_late[1:3, -BLOCK:], "blk", 1)
-
-    last = tokens_local // CHUNK - 1
-    late_chunks = [(qkv_late, 1, at) for at in range(last)]
-
-    def attended_chunk(chunk, window):
-        source, _, at = window[-1]
-        return attend((source, at), window, query_segments, key_segments, chunk)
+    qkv, halo_rows = qkv_columns(ring, rows, pieces, cosine, sine)
+    halo_rows = passed_along(halo_rows, "blk", 1)
 
     def projected(own):
         other = swapped(own, "mp", 1)
-        return project(place, ring, own, other, out_pieces, group_size)
-
-    parts = {last: projected(attended_chunk(last, late_chunks[-3:]))}
-    rows_first, parts[last] = lax.optimization_barrier((rows_first, parts[last]))
-    qkv_first = qkv_columns(ring, rows_first, qkv_pieces, cosine[:CHUNK], sine[:CHUNK])
-    chunks = [(halo_rows, 0, 0), (halo_rows, 0, 1), (qkv_first, 1, 0)] + late_chunks
-    for chunk in reversed(range(last)):
-        parts[chunk] = projected(attended_chunk(chunk, chunks[chunk : chunk + 3]))
+        return project(place, ring, own, other, pieces, group_size)
+
+    last = tokens_local // CHUNK - 1
+    chunks = [(halo_rows, 0, 0), (halo_rows, 0, 1)] + [(qkv, 1, at) for at in range(last + 1)]
+    parts = {}
+    for chunk in reversed(range(last + 1)):
+        window = chunks[chunk : chunk + 3]
+        own = attend((qkv, chunk), window, query_segments, key_segments, chunk)
+        parts[chunk] = projected(own)
 
     result = None
     for chunk in reversed(range(last + 1)):

time: 292 us -> 252 us (0.86)
  starting transfers between devices: 64.9 us -> 34.8 us
  Pallas kernels: 86.5 us -> 80.8 us
  local copies, waits for them, and re-layouts: 11.5 us -> 7.83 us
    ppermute x18 -> x11, starting transfers between devices: 39.4 us -> 9.38 us  [swapped(): lax.ppermute(value, axis, [(source, source ^ mask) for source in range(co...]
    ppermute x3, waiting for transfers between devices: 35.2 us -> 14.3 us  [body(): lax.ppermute(parts[step], 'mp', [(at, (at + step) % group_size) for at in...]
    all_gather x2 -> x1, waiting for transfers between devices: 0.02 us -> 14.8 us  [gathered(): rows = lax.all_gather(normed, 'mp', axis=0, tiled=True)]
    ppermute x18 -> x11, waiting for transfers between devices: 51 us -> 55.4 us  [swapped(): lax.ppermute(value, axis, [(source, source ^ mask) for source in range(co...]
    pallas_call x2 -> x1, Pallas kernels: 16.7 us -> 13 us  [qkv_columns(): pl.pallas_call(qkv_kernel, grid=(3,), in_specs=[pl.BlockSpec(memory_space...]
    pallas_call x2 -> x1, Pallas kernels: 7.76 us -> 5.64 us  [mix(): pl.pallas_call(functools.partial(mix_kernel, start), grid=(tokens // CHUN...]
    unnamed x74 -> x46, local copies, waits for them, and re-layouts: 6.74 us -> 5.41 us
  transfers between devices with their start and end apart: 36 -> 28, of which waited for: 12 -> 11; matrix products, arithmetic and copies ran while one was open for 4% -> 3% of each run, Pallas kernels for 25% -> 23%
where the time goes in v7:
time: 252 us; the launch traced here: 251 us
  waiting for transfers between devices  106 us (42%)
  Pallas kernels  80.8 us (32%)
  starting transfers between devices  34.8 us (14%)
  between operations  15 us (6%)
  local copies, waits for them, and re-layouts  7.83 us (3%)
  other arithmetic  6.28 us (2%)
    ppermute x11, waiting for transfers between devices, swapped(): lax.ppermute(value, axis, [(source, source ^ mask) for source in range(co...  55.4 us
    pallas_call x4, Pallas kernels, project(): pl.pallas_call(project_kernel, grid=(1,), in_specs=[pl.BlockSpec(memory_s...  18.7 us
    pallas_call x4, Pallas kernels, attend(): pl.pallas_call(attend_kernel, grid=(1,), in_specs=[pl.BlockSpec(block, la...  16.1 us
    ppermute x4, waiting for transfers between devices, body(): outer = lax.ppermute(outer, 'mp', [(1, 3), (2, 0)])  15.5 us
    all_gather x1, waiting for transfers between devices, gathered(): rows = lax.all_gather(normed, 'mp', axis=0, tiled=True)  14.8 us
    ppermute x3, waiting for transfers between devices, body(): lax.ppermute(parts[step], 'mp', [(at, (at + step) % group_size) for at in...  14.3 us
    pallas_call x4, Pallas kernels, final(): pl.pallas_call(final_kernel, grid=(tokens // STEP,), in_specs=specs, out_...  13.6 us
    pallas_call x1, Pallas kernels, qkv_columns(): pl.pallas_call(qkv_kernel, grid=(3,), in_specs=[pl.BlockSpec(memory_space...  13 us
  transfers between devices with their start and end apart: 28, of which 11 were waited for; matrix products, arithmetic and copies ran while one was open for 3% of the time, Pallas kernels for 23%

profile of v7, /device:TPU:0, one launch (start us, length us, event | category | flops | bytes accessed | tf_op | source)
XLA Modules:
  0.0 251.1 jit_solution(17421183010013354086)
XLA Ops:
  6.7 1.4 maximum_maximum_fusion.proj_ref
  8.1 6.4 %stats.1.own_ref = f32[8,5248]{1,0:T(8,128)} custom-call(bf16[1024,4,512]{2,1,0:T(4,128)(2,1)} %x_ref.11, f32[8,512]{1,0:T(8,128)} %maximum_maximum_fusion.proj_ref), custom_call_target="tpu_custom_call" | custom-call | flops 1258291200 | bytes 4194304 | tf_op jit(solution)/shard_map/stats/pallas_call | solution.py:171
  14.5 3.0 %collective-permute-start = (f32[8,5248]{1,0:T(8,128)}, f32[8,5248]{1,0:T(8,128)S(1)}, u32[]{:S(2)}, u32[]{:S(2)}) collective-permute-start(f32[8,5248]{1,0:T(8,128)} %stats.1.own_ref), channel_id=1, source_target_pairs={{0,1},{1,2},{2,3},{3,0},{4,5},{5,6},{6,7},{7,4},{8,9},{9,10},{10,1... | collective-permute-start | bytes 503816 | tf_op jit(solution)/shard_map/ppermute | solution.py:31
  17.5 2.6 %collective-permute-start.1 = (f32[8,5248]{1,0:T(8,128)}, f32[8,5248]{1,0:T(8,128)S(1)}, u32[]{:S(2)}, u32[]{:S(2)}) collective-permute-start(f32[8,5248]{1,0:T(8,128)} %stats.1.own_ref), channel_id=1, source_target_pairs={{0,2},{1,3},{2,0},{3,1},{4,6},{5,7},{6,4},{7,5},{8,10},{9,11},{10,... | collective-permute-start | bytes 503816 | tf_op jit(solution)/shard_map/ppermute | solution.py:31
  20.1 1.3 collective-permute-start.2
  21.4 4.9 %regroup.1 = (bf16[64,2560]{1,0:T(8,128)(2,1)}, bf16[64,2560]{1,0:T(8,128)(2,1)}, bf16[64,2560]{1,0:T(8,128)(2,1)}, bf16[64,2560]{1,0:T(8,128)(2,1)}) custom-call(s32[1]{0:T(128)} %bitcast.1.place_ref, f32[64,4,2048]{2,1,0:T(4,128)} %master_ref.1), custom_call_target="tpu_custom_call" | custom-call | bytes 3407872 | tf_op jit(solution)/shard_map/regroup/pallas_call | solution.py:79
  26.3 5.0 %collective-permute-done.1.b_ref = f32[8,5248]{1,0:T(8,128)S(1)} collective-permute-done((f32[8,5248]{1,0:T(8,128)}, f32[8,5248]{1,0:T(8,128)S(1)}, u32[]{:S(2)}, u32[]{:S(2)}) %collective-permute-start.1) | collective-permute-done | bytes 167968 | tf_op jit(solution)/shard_map/ppermute | solution.py:31
  31.3 4.0 %collective-permute-start.3 = (bf16[64,2560]{1,0:T(8,128)(2,1)}, bf16[64,2560]{1,0:T(8,128)(2,1)S(1)}, u32[]{:S(2)}, u32[]{:S(2)}) collective-permute-start(bf16[64,2560]{1,0:T(8,128)(2,1)} %get-tuple-element.57), channel_id=1, source_target_pairs={{0,1},{1,2},{2,3},{3,0},{4,5},{5,6},{6,7},{7,4},{8,9},{9,10},{10,1... | collective-permute-start | bytes 983048 | tf_op jit(solution)/shard_map/ppermute | solution.py:511
  35.4 1.7 collective-permute-start.4
  37.1 0.7 collective-permute-start.5
  37.8 5.6 %mix.1 = (f32[8,5248]{1,0:T(8,128)}, bf16[1024,512]{1,0:T(8,128)(2,1)}) custom-call(f32[4,6]{1,0:T(4,128)} %static_ref.9, bf16[1024,4,512]{2,1,0:T(4,128)(2,1)} %x_ref.11, f32[8,5248]{1,0:T(8,128)} %stats.1.own_ref, f32[8,5248]{1,0:T(8,128)} %copy-done.17, f32[8,5248]{1,0:T(8,128)} %copy-done.18, f32[8,5248]{1,0:T(8,128)} %copy-done.19), custom_call_target="tpu_custom_call" | custom-call | flops 838860800 | bytes 5242880 | tf_op jit(solution)/shard_map/mix/pallas_call | solution.py:242
  43.5 2.0 collective-permute-done.3.refs_1_
  45.5 12.2 %collective-permute-done.4.refs_2_ = bf16[64,2560]{1,0:T(8,128)(2,1)S(1)} collective-permute-done((bf16[64,2560]{1,0:T(8,128)(2,1)}, bf16[64,2560]{1,0:T(8,128)(2,1)S(1)}, u32[]{:S(2)}, u32[]{:S(2)}) %collective-permute-start.4) | collective-permute-done | bytes 327712 | tf_op jit(solution)/shard_map/ppermute | solution.py:511
  57.8 0.7 copy-done.3
  58.6 2.5 assemble.1.refs_0_
  61.1 1.5 collective-permute-start.7
  62.5 1.5 collective-permute-start.9
  64.1 0.5 collective-permute-start.11
  64.5 0.6 fusion.5
  65.8 27.1 %collective-permute-done.7.refs_2_ = bf16[256,2560]{1,0:T(8,128)(2,1)S(1)} collective-permute-done((bf16[256,2560]{1,0:T(8,128)(2,1)}, bf16[256,2560]{1,0:T(8,128)(2,1)S(1)}, u32[]{:S(2)}, u32[]{:S(2)}) %collective-permute-start.7) | collective-permute-done | bytes 1310752 | tf_op jit(solution)/shard_map/ppermute | solution.py:115
  92.9 28.3 %collective-permute-done.9.refs_4_ = bf16[256,2560]{1,0:T(8,128)(2,1)} collective-permute-done((bf16[256,2560]{1,0:T(8,128)(2,1)}, bf16[256,2560]{1,0:T(8,128)(2,1)}, u32[]{:S(2)}, u32[]{:S(2)}) %collective-permute-start.9) | collective-permute-done | bytes 1310752 | tf_op jit(solution)/shard_map/ppermute | solution.py:115
  121.3 0.5 collective-permute-start.12
  121.8 1.9 collective-permute-start.13
  124.4 1.4 collective-permute-done.13
  125.8 1.6 convert_reduce_fusion
  127.4 1.9 fusion.1
  129.3 1.3 pad_maximum_fusion
  130.7 14.8 %all-gather.2.cloned.1.call-done = bf16[4096,512]{1,0:T(8,128)(2,1)} async-done(((bf16[1024,512]{1,0:T(8,128)(2,1)}), bf16[4096,512]{1,0:T(8,128)(2,1)}) %all-gather.2.cloned.1.call-update) | async-done | bytes 4194320 | tf_op jit(solution)/shard_map/all_gather | solution.py:507
  145.5 13.0 %qkv.1 = (bf16[3,1024,512]{2,1,0:T(8,128)(2,1)}, bf16[2,512,512]{2,1,0:T(8,128)(2,1)}) custom-call(s32[1]{0:T(128)} %bitcast.2.ring_ref, bf16[4,1024,512]{2,1,0:T(8,128)(2,1)} %bitcast.11, f32[1024,128]{1,0:T(8,128)} %get-tuple-element.103.cosine_ref, f32[1024,128]{1,0:T(8,128)} %get-tuple-element.104.sine_ref, bf16[256,2560]{1,0:T(8,128)(2,1)} %assemble.1.refs_0_, ...), custom_call_target="tpu_custom_call" | custom-call | flops 6442450944 | bytes 16777216 | tf_op jit(solution)/shard_map/qkv/pallas_call | solution.py:297
  158.5 2.0 collective-permute-start.14
  160.5 1.0 copy.14.qseg_ref
  161.7 0.6 broadcast_in_dim.29.kseg_ref
  162.3 4.0 %attend.6.own_ref = bf16[256,512]{1,0:T(8,128)(2,1)} custom-call(bf16[3,1024,512]{2,1,0:T(8,128)(2,1)} %get-tuple-element.75.q_ref.k2.v2.k1.v1.k0.v0, bf16[3,1024,512]{2,1,0:T(8,128)(2,1)} %get-tuple-element.75.q_ref.k2.v2.k1.v1.k0.v0, bf16[3,1024,512]{2,1,0:T(8,128)(2,1)} %get-tuple-element.75.q_ref.k2.v2.k1.v1.k0.v0, ...), custom_call_target="tpu_custom_call" | custom-call | flops 402653184 | bytes 2097152 | tf_op jit(solution)/shard_map/attend/pallas_call | solution.py:351
  166.3 4.0 %attend.7.own_ref = bf16[256,512]{1,0:T(8,128)(2,1)} custom-call(bf16[3,1024,512]{2,1,0:T(8,128)(2,1)} %get-tuple-element.75.q_ref.k2.v2.k1.v1.k0.v0, bf16[3,1024,512]{2,1,0:T(8,128)(2,1)} %get-tuple-element.75.q_ref.k2.v2.k1.v1.k0.v0, bf16[3,1024,512]{2,1,0:T(8,128)(2,1)} %get-tuple-element.75.q_ref.k2.v2.k1.v1.k0.v0, ...), custom_call_target="tpu_custom_call" | custom-call | flops 402653184 | bytes 2097152 | tf_op jit(solution)/shard_map/attend/pallas_call | solution.py:351
  170.3 2.0 collective-permute-start.24
  172.4 1.0 copy-done
  173.4 4.0 %attend.5.own_ref = bf16[256,512]{1,0:T(8,128)(2,1)} custom-call(bf16[3,1024,512]{2,1,0:T(8,128)(2,1)} %get-tuple-element.75.q_ref.k2.v2.k1.v1.k0.v0, bf16[2,512,512]{2,1,0:T(8,128)(2,1)} %copy-done, bf16[3,1024,512]{2,1,0:T(8,128)(2,1)} %get-tuple-element.75.q_ref.k2.v2.k1.v1.k0.v0, bf16[3,1024,512]{2,1,0:T(8,128)(2,1)} %get-tuple-element.75.q_ref.k2.v2.k1.v1.k0.v0, ...), custom_call_target="tpu_custom_call" | custom-call | flops 402653184 | bytes 2097152 | tf_op jit(solution)/shard_map/attend/pallas_call | solution.py:351
  177.4 0.7 copy-done.10
  178.1 4.7 %project.6 = (f32[256,512]{1,0:T(8,128)}, bf16[256,512]{1,0:T(8,128)(2,1)}, bf16[256,512]{1,0:T(8,128)(2,1)}) custom-call(s32[1]{0:T(128)} %bitcast.1.place_ref, s32[1]{0:T(128)} %bitcast.2.ring_ref, bf16[256,512]{1,0:T(8,128)(2,1)} %attend.6.own_ref, bf16[256,512]{1,0:T(8,128)(2,1)} %copy-done.10, bf16[256,2560]{1,0:T(8,128)(2,1)} %assemble.1.refs_0_, ...), custom_call_target="tpu_custom_call" | custom-call | flops 1073741824 | bytes 5767168 | tf_op jit(solution)/shard_map/project/pallas_call | solution.py:401
  182.8 0.7 collective-permute-start.22
  183.5 4.0 %attend.4.own_ref = bf16[256,512]{1,0:T(8,128)(2,1)} custom-call(bf16[3,1024,512]{2,1,0:T(8,128)(2,1)} %get-tuple-element.75.q_ref.k2.v2.k1.v1.k0.v0, bf16[2,512,512]{2,1,0:T(8,128)(2,1)} %copy-done, bf16[2,512,512]{2,1,0:T(8,128)(2,1)} %copy-done, bf16[3,1024,512]{2,1,0:T(8,128)(2,1)} %get-tuple-element.75.q_ref.k2.v2.k1.v1.k0.v0, ...), custom_call_target="tpu_custom_call" | custom-call | flops 402653184 | bytes 2097152 | tf_op jit(solution)/shard_map/attend/pallas_call | solution.py:351
  187.5 3.3 %collective-permute-start.15 = (bf16[256,512]{1,0:T(8,128)(2,1)}, bf16[256,512]{1,0:T(8,128)(2,1)S(1)}, u32[]{:S(2)}, u32[]{:S(2)}) collective-permute-start(bf16[256,512]{1,0:T(8,128)(2,1)} %attend.4.own_ref), channel_id=1, source_target_pairs={{0,1},{1,0},{2,3},{3,2},{4,5},{5,4},{6,7},{7,6},{8,9},{9,8},{10,11... | collective-permute-start | bytes 786440 | tf_op jit(solution)/shard_map/ppermute | solution.py:115
  190.8 0.7 copy-done.9
  191.5 4.7 %project.7 = (f32[256,512]{1,0:T(8,128)}, bf16[256,512]{1,0:T(8,128)(2,1)}, bf16[256,512]{1,0:T(8,128)(2,1)}) custom-call(s32[1]{0:T(128)} %bitcast.1.place_ref, s32[1]{0:T(128)} %bitcast.2.ring_ref, bf16[256,512]{1,0:T(8,128)(2,1)} %attend.7.own_ref, bf16[256,512]{1,0:T(8,128)(2,1)} %copy-done.9, bf16[256,2560]{1,0:T(8,128)(2,1)} %assemble.1.refs_0_, ...), custom_call_target="tpu_custom_call" | custom-call | flops 1073741824 | bytes 5767168 | tf_op jit(solution)/shard_map/project/pallas_call | solution.py:401
  196.1 0.7 collective-permute-start.25
  196.8 1.3 collective-permute-start.26
  198.2 1.3 collective-permute-start.23
  199.5 4.7 %project.5 = (f32[256,512]{1,0:T(8,128)}, bf16[256,512]{1,0:T(8,128)(2,1)}, bf16[256,512]{1,0:T(8,128)(2,1)}) custom-call(s32[1]{0:T(128)} %bitcast.1.place_ref, s32[1]{0:T(128)} %bitcast.2.ring_ref, bf16[256,512]{1,0:T(8,128)(2,1)} %attend.5.own_ref, bf16[256,512]{1,0:T(8,128)(2,1)} %copy-done.8, bf16[256,2560]{1,0:T(8,128)(2,1)} %assemble.1.refs_0_, ...), custom_call_target="tpu_custom_call" | custom-call | flops 1073741824 | bytes 5767168 | tf_op jit(solution)/shard_map/project/pallas_call | solution.py:401
  204.1 0.7 collective-permute-start.19
  204.8 1.5 collective-permute-start.20
  206.4 4.7 %project.4 = (f32[256,512]{1,0:T(8,128)}, bf16[256,512]{1,0:T(8,128)(2,1)}, bf16[256,512]{1,0:T(8,128)(2,1)}) custom-call(s32[1]{0:T(128)} %bitcast.1.place_ref, s32[1]{0:T(128)} %bitcast.2.ring_ref, bf16[256,512]{1,0:T(8,128)(2,1)} %attend.4.own_ref, bf16[256,512]{1,0:T(8,128)(2,1)} %copy-done.7, bf16[256,2560]{1,0:T(8,128)(2,1)} %assemble.1.refs_0_, ...), custom_call_target="tpu_custom_call" | custom-call | flops 1073741824 | bytes 5767168 | tf_op jit(solution)/shard_map/project/pallas_call | solution.py:401
  211.1 0.7 collective-permute-start.16
  211.7 0.4 collective-permute-done.26.outer_ref
  212.1 1.3 collective-permute-start.17
  213.4 3.4 %final.4.rest_0_ = bf16[1024,4,512]{2,1,0:T(4,128)(2,1)} custom-call(f32[4,6]{1,0:T(4,128)} %static_ref.9, bf16[1024,4,512]{2,1,0:T(4,128)(2,1)} %x_ref.11, f32[8,5248]{1,0:T(8,128)} %get-tuple-element.55.first_ref.folded_ref.column_ref, f32[8,5248]{1,0:T(8,128)} %get-tuple-element.55.first_ref.folded_ref.column_ref, ...), custom_call_target="tpu_custom_call" | custom-call | flops 629145600 | bytes 2883584 | tf_op jit(solution)/shard_map/final/pallas_call | solution.py:480
  216.8 0.9 collective-permute-done.23.outer_ref
  217.7 0.7 copy-done.12
  218.4 3.4 %final.5.rest_0_ = bf16[1024,4,512]{2,1,0:T(4,128)(2,1)} custom-call(f32[4,6]{1,0:T(4,128)} %static_ref.9, bf16[1024,4,512]{2,1,0:T(4,128)(2,1)} %x_ref.11, f32[8,5248]{1,0:T(8,128)} %get-tuple-element.55.first_ref.folded_ref.column_ref, f32[8,5248]{1,0:T(8,128)} %get-tuple-element.55.first_ref.folded_ref.column_ref, ...), custom_call_target="tpu_custom_call", output_to_operand_aliasing={{}: (8, {})} | custom-call | flops 629145600 | bytes 2883584 | tf_op jit(solution)/shard_map/final/pallas_call | solution.py:480
  221.8 7.1 %collective-permute-done.20.outer_ref = bf16[256,512]{1,0:T(8,128)(2,1)S(1)} collective-permute-done((bf16[256,512]{1,0:T(8,128)(2,1)}, bf16[256,512]{1,0:T(8,128)(2,1)S(1)}, u32[]{:S(2)}, u32[]{:S(2)}) %collective-permute-start.20) | collective-permute-done | bytes 262176 | tf_op jit(solution)/shard_map/ppermute | solution.py:563
  229.0 0.7 copy-done.14
  229.7 3.4 %final.6.rest_0_ = bf16[1024,4,512]{2,1,0:T(4,128)(2,1)} custom-call(f32[4,6]{1,0:T(4,128)} %static_ref.9, bf16[1024,4,512]{2,1,0:T(4,128)(2,1)} %x_ref.11, f32[8,5248]{1,0:T(8,128)} %get-tuple-element.55.first_ref.folded_ref.column_ref, f32[8,5248]{1,0:T(8,128)} %get-tuple-element.55.first_ref.folded_ref.column_ref, ...), custom_call_target="tpu_custom_call", output_to_operand_aliasing={{}: (8, {})} | custom-call | flops 629145600 | bytes 2883584 | tf_op jit(solution)/shard_map/final/pallas_call | solution.py:480
  233.1 7.1 %collective-permute-done.17.outer_ref = bf16[256,512]{1,0:T(8,128)(2,1)S(1)} collective-permute-done((bf16[256,512]{1,0:T(8,128)(2,1)}, bf16[256,512]{1,0:T(8,128)(2,1)S(1)}, u32[]{:S(2)}, u32[]{:S(2)}) %collective-permute-start.17) | collective-permute-done | bytes 262176 | tf_op jit(solution)/shard_map/ppermute | solution.py:563
  240.2 0.7 copy-done.16
  240.9 3.4 %final.7 = bf16[1024,4,512]{2,1,0:T(4,128)(2,1)} custom-call(f32[4,6]{1,0:T(4,128)} %static_ref.9, bf16[1024,4,512]{2,1,0:T(4,128)(2,1)} %x_ref.11, f32[8,5248]{1,0:T(8,128)} %get-tuple-element.55.first_ref.folded_ref.column_ref, f32[8,5248]{1,0:T(8,128)} %get-tuple-element.55.first_ref.folded_ref.column_ref, ...), custom_call_target="tpu_custom_call", output_to_operand_aliasing={{}: (8, {})} | custom-call | flops 629145600 | bytes 2883584 | tf_op jit(solution)/shard_map/final/pallas_call | solution.py:480
  (80 shorter events, 0.6 us)
Async XLA Ops:
  6.5 139.0 %all-gather.2.cloned.1.call-start = ((), (), s32[]{:S(2)}) async-start(), calls=%async_computation | async-start | bytes 5242880 | tf_op jit(solution)/shard_map/all_gather | solution.py:507
  14.5 11.9 %collective-permute-start = (f32[8,5248]{1,0:T(8,128)}, f32[8,5248]{1,0:T(8,128)S(1)}, u32[]{:S(2)}, u32[]{:S(2)}) collective-permute-start(f32[8,5248]{1,0:T(8,128)} %stats.1.own_ref), channel_id=1, source_target_pairs={{0,1},{1,2},{2,3},{3,0},{4,5},{5,6},{6,7},{7,4},{8,9},{9,10},{10,1... | collective-permute-start | bytes 503816 | tf_op jit(solution)/shard_map/ppermute | solution.py:31
  17.5 13.8 %collective-permute-start.1 = (f32[8,5248]{1,0:T(8,128)}, f32[8,5248]{1,0:T(8,128)S(1)}, u32[]{:S(2)}, u32[]{:S(2)}) collective-permute-start(f32[8,5248]{1,0:T(8,128)} %stats.1.own_ref), channel_id=1, source_target_pairs={{0,2},{1,3},{2,0},{3,1},{4,6},{5,7},{6,4},{7,5},{8,10},{9,11},{10,... | collective-permute-start | bytes 503816 | tf_op jit(solution)/shard_map/ppermute | solution.py:31
  20.1 11.2 %collective-permute-start.2 = (f32[8,5248]{1,0:T(8,128)}, f32[8,5248]{1,0:T(8,128)S(1)}, u32[]{:S(2)}, u32[]{:S(2)}) collective-permute-start(f32[8,5248]{1,0:T(8,128)} %stats.1.own_ref), channel_id=1, source_target_pairs={{0,3},{1,0},{2,1},{3,2},{4,7},{5,4},{6,5},{7,6},{8,11},{9,8},{10,9... | collective-permute-start | bytes 503816 | tf_op jit(solution)/shard_map/ppermute | solution.py:31
  26.3 11.5 %copy-start.17 = (f32[8,5248]{1,0:T(8,128)}, f32[8,5248]{1,0:T(8,128)S(1)}, u32[]{:S(2)}) copy-start(f32[8,5248]{1,0:T(8,128)S(1)} %collective-permute-done.a_ref) | copy-start | bytes 503812
  31.3 6.5 %copy-start.18 = (f32[8,5248]{1,0:T(8,128)}, f32[8,5248]{1,0:T(8,128)S(1)}, u32[]{:S(2)}) copy-start(f32[8,5248]{1,0:T(8,128)S(1)} %collective-permute-done.1.b_ref) | copy-start | bytes 503812
  31.3 6.5 %copy-start.19 = (f32[8,5248]{1,0:T(8,128)}, f32[8,5248]{1,0:T(8,128)S(1)}, u32[]{:S(2)}) copy-start(f32[8,5248]{1,0:T(8,128)S(1)} %collective-permute-done.2.c_ref) | copy-start | bytes 503812
  31.3 33.2 %copy-start.21 = (s32[2]{0:T(128)S(1)}, s32[2]{0:T(128)}, u32[]{:S(2)}) copy-start(s32[2]{0:T(128)} %param.11) | copy-start | bytes 28
  31.3 90.5 %copy-start.20 = (s32[1024]{0:T(1024)S(1)}, s32[1024]{0:T(1024)}, u32[]{:S(2)}) copy-start(s32[1024]{0:T(1024)} %param.10) | copy-start | bytes 12292
  31.3 14.2 %collective-permute-start.3 = (bf16[64,2560]{1,0:T(8,128)(2,1)}, bf16[64,2560]{1,0:T(8,128)(2,1)S(1)}, u32[]{:S(2)}, u32[]{:S(2)}) collective-permute-start(bf16[64,2560]{1,0:T(8,128)(2,1)} %get-tuple-element.57), channel_id=1, source_target_pairs={{0,1},{1,2},{2,3},{3,0},{4,5},{5,6},{6,7},{7,4},{8,9},{9,10},{10,1... | collective-permute-start | bytes 983048 | tf_op jit(solution)/shard_map/ppermute | solution.py:511
  35.4 22.4 %collective-permute-start.4 = (bf16[64,2560]{1,0:T(8,128)(2,1)}, bf16[64,2560]{1,0:T(8,128)(2,1)S(1)}, u32[]{:S(2)}, u32[]{:S(2)}) collective-permute-start(bf16[64,2560]{1,0:T(8,128)(2,1)} %get-tuple-element.58), channel_id=1, source_target_pairs={{0,2},{1,3},{2,0},{3,1},{4,6},{5,7},{6,4},{7,5},{8,10},{9,11},{10,... | collective-permute-start | bytes 983048 | tf_op jit(solution)/shard_map/ppermute | solution.py:511
  37.1 20.7 %collective-permute-start.5 = (bf16[64,2560]{1,0:T(8,128)(2,1)}, bf16[64,2560]{1,0:T(8,128)(2,1)S(1)}, u32[]{:S(2)}, u32[]{:S(2)}) collective-permute-start(bf16[64,2560]{1,0:T(8,128)(2,1)} %get-tuple-element.59), channel_id=1, source_target_pairs={{0,3},{1,0},{2,1},{3,2},{4,7},{5,4},{6,5},{7,6},{8,11},{9,8},{10,9... | collective-permute-start | bytes 983048 | tf_op jit(solution)/shard_map/ppermute | solution.py:511
  45.5 12.3 %copy-start.2 = (bf16[64,2560]{1,0:T(8,128)(2,1)}, bf16[64,2560]{1,0:T(8,128)(2,1)S(1)}, u32[]{:S(2)}) copy-start(bf16[64,2560]{1,0:T(8,128)(2,1)S(1)} %collective-permute-done.3.refs_1_) | copy-start | bytes 983044
  57.7 0.7 copy-start.3
  57.7 0.8 copy-start.4
  61.1 31.9 %collective-permute-start.7 = (bf16[256,2560]{1,0:T(8,128)(2,1)}, bf16[256,2560]{1,0:T(8,128)(2,1)S(1)}, u32[]{:S(2)}, u32[]{:S(2)}) collective-permute-start(bf16[256,2560]{1,0:T(8,128)(2,1)} %assemble.1.refs_0_), channel_id=1, source_target_pairs={{0,8},{4,12},{8,0},{12,4},{16,24},{20,28},{24,16},{28,20},{1,9},{5... | collective-permute-start | bytes 3932168 | tf_op jit(solution)/shard_map/ppermute | solution.py:115
  62.5 58.7 %collective-permute-start.9 = (bf16[256,2560]{1,0:T(8,128)(2,1)}, bf16[256,2560]{1,0:T(8,128)(2,1)}, u32[]{:S(2)}, u32[]{:S(2)}) collective-permute-start(bf16[256,2560]{1,0:T(8,128)(2,1)} %assemble.1.refs_0_), channel_id=1, source_target_pairs={{0,16},{4,20},{8,24},{12,28},{16,0},{20,4},{24,8},{28,12},{1,17},{... | collective-permute-start | bytes 3932168 | tf_op jit(solution)/shard_map/ppermute | solution.py:115
  64.1 57.2 %collective-permute-start.11 = (bf16[256,2560]{1,0:T(8,128)(2,1)}, bf16[256,2560]{1,0:T(8,128)(2,1)}, u32[]{:S(2)}, u32[]{:S(2)}) collective-permute-start(bf16[256,2560]{1,0:T(8,128)(2,1)} %assemble.1.refs_0_), channel_id=1, source_target_pairs={{0,24},{4,28},{8,16},{12,20},{16,8},{20,12},{24,0},{28,4},{1,25},{... | collective-permute-start | bytes 3932168 | tf_op jit(solution)/shard_map/ppermute | solution.py:115
  65.8 64.9 %collective-permute-start.6 = (bf16[256,2560]{1,0:T(8,128)(2,1)}, bf16[256,2560]{1,0:T(8,128)(2,1)}, u32[]{:S(2)}, u32[]{:S(2)}) collective-permute-start(bf16[256,2560]{1,0:T(8,128)(2,1)} %assemble.1.refs_0_), channel_id=1, source_target_pairs={{0,4},{4,0},{8,12},{12,8},{16,20},{20,16},{24,28},{28,24},{1,5},{5... | collective-permute-start | bytes 3932168 | tf_op jit(solution)/shard_map/ppermute | solution.py:115
  92.9 52.6 %copy-start.1 = (bf16[256,2560]{1,0:T(8,128)(2,1)}, bf16[256,2560]{1,0:T(8,128)(2,1)S(1)}, u32[]{:S(2)}) copy-start(bf16[256,2560]{1,0:T(8,128)(2,1)S(1)} %collective-permute-done.7.refs_2_) | copy-start | bytes 3932164
  92.9 37.8 %collective-permute-start.8 = (bf16[256,2560]{1,0:T(8,128)(2,1)S(1)}, bf16[256,2560]{1,0:T(8,128)(2,1)}, u32[]{:S(2)}, u32[]{:S(2)}) collective-permute-start(bf16[256,2560]{1,0:T(8,128)(2,1)S(1)} %collective-permute-done.7.refs_2_), channel_id=1, source_target_pairs={{0,4},{4,0},{8,12},{12,8},{16,20},{20,16},{24,28},{28,24},{1,5},{5... | collective-permute-start | bytes 3932168 | tf_op jit(solution)/shard_map/ppermute | solution.py:115
  121.3 9.4 %collective-permute-start.10 = (bf16[256,2560]{1,0:T(8,128)(2,1)}, bf16[256,2560]{1,0:T(8,128)(2,1)}, u32[]{:S(2)}, u32[]{:S(2)}) collective-permute-start(bf16[256,2560]{1,0:T(8,128)(2,1)} %collective-permute-done.9.refs_4_), channel_id=1, source_target_pairs={{0,4},{4,0},{8,12},{12,8},{16,20},{20,16},{24,28},{28,24},{1,5},{5... | collective-permute-start | bytes 3932168 | tf_op jit(solution)/shard_map/ppermute | solution.py:115
  121.3 9.4 %collective-permute-start.12 = (bf16[256,2560]{1,0:T(8,128)(2,1)}, bf16[256,2560]{1,0:T(8,128)(2,1)}, u32[]{:S(2)}, u32[]{:S(2)}) collective-permute-start(bf16[256,2560]{1,0:T(8,128)(2,1)} %collective-permute-done.11.refs_6_), channel_id=1, source_target_pairs={{0,4},{4,0},{8,12},{12,8},{16,20},{20,16},{24,28},{28,24},{1,5},{5... | collective-permute-start | bytes 3932168 | tf_op jit(solution)/shard_map/ppermute | solution.py:115
  121.8 4.0 %collective-permute-start.13 = (s32[512]{0:T(512)S(1)}, s32[512]{0:T(512)S(1)}, u32[]{:S(2)}, u32[]{:S(2)}) collective-permute-start(s32[512]{0:T(512)S(1)} %get-tuple-element.98), channel_id=1, source_target_pairs={{0,4},{4,8},{8,12},{12,16},{16,20},{20,24},{24,28},{1,5},{5,9},{9,... | collective-permute-start | bytes 6152 | tf_op jit(solution)/shard_map/ppermute | solution.py:25
  158.5 13.8 %collective-permute-start.14 = (bf16[2,512,512]{2,1,0:T(8,128)(2,1)}, bf16[2,512,512]{2,1,0:T(8,128)(2,1)S(1)}, u32[]{:S(2)}, u32[]{:S(2)}) collective-permute-start(bf16[2,512,512]{2,1,0:T(8,128)(2,1)} %get-tuple-element.76), channel_id=1, source_target_pairs={{0,4},{4,8},{8,12},{12,16},{16,20},{20,24},{24,28},{1,5},{5,9},{9,... | collective-permute-start | bytes 3145736 | tf_op jit(solution)/shard_map/ppermute | solution.py:25
  166.3 11.1 %collective-permute-start.21 = (bf16[256,512]{1,0:T(8,128)(2,1)}, bf16[256,512]{1,0:T(8,128)(2,1)S(1)}, u32[]{:S(2)}, u32[]{:S(2)}) collective-permute-start(bf16[256,512]{1,0:T(8,128)(2,1)} %attend.6.own_ref), channel_id=1, source_target_pairs={{0,1},{1,0},{2,3},{3,2},{4,5},{5,4},{6,7},{7,6},{8,9},{9,8},{10,11... | collective-permute-start | bytes 786440 | tf_op jit(solution)/shard_map/ppermute | solution.py:115
  170.3 20.4 %collective-permute-start.24 = (bf16[256,512]{1,0:T(8,128)(2,1)}, bf16[256,512]{1,0:T(8,128)(2,1)S(1)}, u32[]{:S(2)}, u32[]{:S(2)}) collective-permute-start(bf16[256,512]{1,0:T(8,128)(2,1)} %attend.7.own_ref), channel_id=1, source_target_pairs={{0,1},{1,0},{2,3},{3,2},{4,5},{5,4},{6,7},{7,6},{8,9},{9,8},{10,11... | collective-permute-start | bytes 786440 | tf_op jit(solution)/shard_map/ppermute | solution.py:115
  172.4 1.0 copy-start
  177.4 20.7 %collective-permute-start.18 = (bf16[256,512]{1,0:T(8,128)(2,1)}, bf16[256,512]{1,0:T(8,128)(2,1)S(1)}, u32[]{:S(2)}, u32[]{:S(2)}) collective-permute-start(bf16[256,512]{1,0:T(8,128)(2,1)} %attend.5.own_ref), channel_id=1, source_target_pairs={{0,1},{1,0},{2,3},{3,2},{4,5},{5,4},{6,7},{7,6},{8,9},{9,8},{10,11... | collective-permute-start | bytes 786440 | tf_op jit(solution)/shard_map/ppermute | solution.py:115
  177.4 0.7 copy-start.10
  182.8 21.3 %collective-permute-start.22 = (bf16[256,512]{1,0:T(8,128)(2,1)}, bf16[256,512]{1,0:T(8,128)(2,1)S(1)}, u32[]{:S(2)}, u32[]{:S(2)}) collective-permute-start(bf16[256,512]{1,0:T(8,128)(2,1)} %get-tuple-element.84), channel_id=1, source_target_pairs={{1,2},{2,1},{5,6},{6,5},{9,10},{10,9},{13,14},{14,13},{17,18},{18,... | collective-permute-start | bytes 786440 | tf_op jit(solution)/shard_map/ppermute | solution.py:562
  187.5 10.6 %copy-start.22 = (bf16[256,512]{1,0:T(8,128)(2,1)S(1)}, bf16[256,512]{1,0:T(8,128)(2,1)}, u32[]{:S(2)}) copy-start(bf16[256,512]{1,0:T(8,128)(2,1)} %get-tuple-element.85) | copy-start | bytes 786436
  187.5 17.3 %collective-permute-start.15 = (bf16[256,512]{1,0:T(8,128)(2,1)}, bf16[256,512]{1,0:T(8,128)(2,1)S(1)}, u32[]{:S(2)}, u32[]{:S(2)}) collective-permute-start(bf16[256,512]{1,0:T(8,128)(2,1)} %attend.4.own_ref), channel_id=1, source_target_pairs={{0,1},{1,0},{2,3},{3,2},{4,5},{5,4},{6,7},{7,6},{8,9},{9,8},{10,11... | collective-permute-start | bytes 786440 | tf_op jit(solution)/shard_map/ppermute | solution.py:115
  190.8 0.7 copy-start.9
  196.1 14.9 %collective-permute-start.25 = (bf16[256,512]{1,0:T(8,128)(2,1)}, bf16[256,512]{1,0:T(8,128)(2,1)S(1)}, u32[]{:S(2)}, u32[]{:S(2)}) collective-permute-start(bf16[256,512]{1,0:T(8,128)(2,1)} %get-tuple-element.87), channel_id=1, source_target_pairs={{1,2},{2,1},{5,6},{6,5},{9,10},{10,9},{13,14},{14,13},{17,18},{18,... | collective-permute-start | bytes 786440 | tf_op jit(solution)/shard_map/ppermute | solution.py:562
  196.8 15.3 %collective-permute-start.26 = (bf16[256,512]{1,0:T(8,128)(2,1)}, bf16[256,512]{1,0:T(8,128)(2,1)S(1)}, u32[]{:S(2)}, u32[]{:S(2)}) collective-permute-start(bf16[256,512]{1,0:T(8,128)(2,1)} %get-tuple-element.88), channel_id=1, source_target_pairs={{1,3},{2,0},{5,7},{6,4},{9,11},{10,8},{13,15},{14,12},{17,19},{18,... | collective-permute-start | bytes 786440 | tf_op jit(solution)/shard_map/ppermute | solution.py:563
  198.1 1.3 copy-start.8
  198.2 19.6 %collective-permute-start.23 = (bf16[256,512]{1,0:T(8,128)(2,1)S(1)}, bf16[256,512]{1,0:T(8,128)(2,1)S(1)}, u32[]{:S(2)}, u32[]{:S(2)}) collective-permute-start(bf16[256,512]{1,0:T(8,128)(2,1)S(1)} %copy-done.22), channel_id=1, source_target_pairs={{1,3},{2,0},{5,7},{6,4},{9,11},{10,8},{13,15},{14,12},{17,19},{18,... | collective-permute-start | bytes 786440 | tf_op jit(solution)/shard_map/ppermute | solution.py:563
  204.1 12.7 %copy-start.11 = (bf16[256,512]{1,0:T(8,128)(2,1)}, bf16[256,512]{1,0:T(8,128)(2,1)S(1)}, u32[]{:S(2)}) copy-start(bf16[256,512]{1,0:T(8,128)(2,1)S(1)} %collective-permute-done.22.inner_ref) | copy-start | bytes 786436
  204.1 17.7 %collective-permute-start.19 = (bf16[256,512]{1,0:T(8,128)(2,1)}, bf16[256,512]{1,0:T(8,128)(2,1)S(1)}, u32[]{:S(2)}, u32[]{:S(2)}) collective-permute-start(bf16[256,512]{1,0:T(8,128)(2,1)} %get-tuple-element.81), channel_id=1, source_target_pairs={{1,2},{2,1},{5,6},{6,5},{9,10},{10,9},{13,14},{14,13},{17,18},{18,... | collective-permute-start | bytes 786440 | tf_op jit(solution)/shard_map/ppermute | solution.py:562
  204.8 1.5 copy-start.7
  204.8 24.1 %collective-permute-start.20 = (bf16[256,512]{1,0:T(8,128)(2,1)}, bf16[256,512]{1,0:T(8,128)(2,1)S(1)}, u32[]{:S(2)}, u32[]{:S(2)}) collective-permute-start(bf16[256,512]{1,0:T(8,128)(2,1)} %get-tuple-element.82), channel_id=1, source_target_pairs={{1,3},{2,0},{5,7},{6,4},{9,11},{10,8},{13,15},{14,12},{17,19},{18,... | collective-permute-start | bytes 786440 | tf_op jit(solution)/shard_map/ppermute | solution.py:563
  211.0 2.3 copy-start.5
  211.1 22.0 %collective-permute-start.16 = (bf16[256,512]{1,0:T(8,128)(2,1)}, bf16[256,512]{1,0:T(8,128)(2,1)S(1)}, u32[]{:S(2)}, u32[]{:S(2)}) collective-permute-start(bf16[256,512]{1,0:T(8,128)(2,1)} %get-tuple-element.78), channel_id=1, source_target_pairs={{1,2},{2,1},{5,6},{6,5},{9,10},{10,9},{13,14},{14,13},{17,18},{18,... | collective-permute-start | bytes 786440 | tf_op jit(solution)/shard_map/ppermute | solution.py:562
  212.1 1.3 copy-start.6
  212.1 28.1 %collective-permute-start.17 = (bf16[256,512]{1,0:T(8,128)(2,1)}, bf16[256,512]{1,0:T(8,128)(2,1)S(1)}, u32[]{:S(2)}, u32[]{:S(2)}) collective-permute-start(bf16[256,512]{1,0:T(8,128)(2,1)} %get-tuple-element.79), channel_id=1, source_target_pairs={{1,3},{2,0},{5,7},{6,4},{9,11},{10,8},{13,15},{14,12},{17,19},{18,... | collective-permute-start | bytes 786440 | tf_op jit(solution)/shard_map/ppermute | solution.py:563
  217.7 0.7 copy-start.12
  221.8 7.1 %copy-start.13 = (bf16[256,512]{1,0:T(8,128)(2,1)}, bf16[256,512]{1,0:T(8,128)(2,1)S(1)}, u32[]{:S(2)}) copy-start(bf16[256,512]{1,0:T(8,128)(2,1)S(1)} %collective-permute-done.19.inner_ref) | copy-start | bytes 786436
  228.9 0.7 copy-start.14
  233.1 7.1 %copy-start.15 = (bf16[256,512]{1,0:T(8,128)(2,1)}, bf16[256,512]{1,0:T(8,128)(2,1)S(1)}, u32[]{:S(2)}) copy-start(bf16[256,512]{1,0:T(8,128)(2,1)S(1)} %collective-permute-done.16.inner_ref) | copy-start | bytes 786436
  240.2 0.7 copy-start.16
Sparse Core Ops, SparseCore 0:
  57.9 87.5 all-gather.1

commit v8 on v7

--- a/solution.py
+++ b/solution.py
@@ -115,25 +115,28 @@
     return lax.ppermute(value, axis, [(source, source ^ mask) for source in range(count)])
 
 
-def weight_pieces(part):
+def weight_pieces(part, beside):
     count = lax.axis_size("blk")
     if count & (count - 1) or part.shape[0] % HEAD_DIM or count > 8:
-        return [lax.all_gather(part, "blk", axis=0, tiled=True)]
-    pieces = {0: part}
-    for mask in range(2, count, 2):
-        pieces[mask] = swapped(part, "blk", mask)
-    for mask in range(0, count, 2):
-        pieces[mask + 1] = swapped(pieces[mask], "blk", 1)
-    return [pieces[mask] for mask in range(count)]
-
-
-def stats_kernel(x_ref, proj_ref, out_ref):
+        return [lax.all_gather(part, "blk", axis=0, tiled=True)], beside
+    even = [part] + [swapped(part, "blk", mask) for mask in range(2, count, 2)]
+    even, beside = lax.optimization_barrier((even, beside))
+    pieces = []
+    for piece in even:
+        pieces += [piece, swapped(piece, "blk", 1)]
+    return pieces, beside
+
+
+def stats_kernel(x_ref, proj_ref, first_ref, second_ref):
     block, _, width = x_ref.shape
     tokens = block * pl.num_programs(0)
     base = pl.program_id(0) * (block // STEP)
     proj = proj_ref[...]
     pieces = jnp.concatenate(split(proj, 3), axis=0)
-    out_ref[:, out_ref.shape[1] - 128 :] = jnp.broadcast_to(jnp.sum(proj, axis=1, keepdims=True), (8, 128))
+    column = jnp.broadcast_to(jnp.sum(proj, axis=1, keepdims=True), (8, 128))
+    first_ref[:, 5 * tokens :] = column[0:4]
+    second_ref[:, 5 * tokens : 5 * tokens + 128] = column[1:5]
+    second_ref[:, 5 * tokens + 128 :] = column[5:6] + jnp.zeros((4, 128), F32)
     row, col = iotas(4 * SUB, 4 * SUB)
     same = (row >> 2) == (col >> 2)
     ring = jnp.where(same, (row - col) & 3, -1)
@@ -148,26 +151,27 @@
             sums = contract(pieces, v, 1, 1)
             sums = sums[0:8] + sums[8:16] + sums[16:24]
             gram = contract(v, v, 1, 1)
-            out_ref[0:1, lanes] = sums[0:1]
-            out_ref[1:2, lanes] = sums[6:7]
-            for shift in range(3):
-                out_ref[2 + shift : 3 + shift, lanes] = jnp.sum(
-                    jnp.where(ring == shift, gram, 0.0), axis=0, keepdims=True
-                )
-            out_ref[5:8, lanes] = sums[1:4]
-            folded.append(sums[4:6])
+            gram = [
+                jnp.sum(jnp.where(ring == shift, gram, 0.0), axis=0, keepdims=True)
+                for shift in range(3)
+            ]
+            first_ref[0:1, lanes] = sums[0:1]
+            first_ref[1:2, lanes] = sums[6:7]
+            first_ref[2:3, lanes] = gram[0]
+            first_ref[3:4, lanes] = gram[1]
+            second_ref[:, lanes] = sums[1:5]
+            folded.append(jnp.concatenate([gram[2], sums[5:6]], axis=0))
         folded = jnp.concatenate(folded, axis=1)
         lanes = pl.ds(pl.multiple_of(4 * tokens + step * STEP, STEP), STEP)
         for part in range(4):
-            for which in range(2):
-                out_ref[4 * which + part : 4 * which + part + 1, lanes] = folded[
-                    which : which + 1, part * STEP : (part + 1) * STEP
-                ]
+            piece = folded[:, part * STEP : (part + 1) * STEP]
+            first_ref[part : part + 1, lanes] = piece[0:1]
+            second_ref[part : part + 1, lanes] = piece[1:2]
 
 
 def stats(x, proj):
     tokens, _, width = x.shape
-    lanes = 5 * tokens + 128
+    lanes = [5 * tokens + 128, 5 * tokens + 256]
     return pl.pallas_call(
         stats_kernel,
         grid=(tokens // (2 * STEP),),
@@ -175,12 +179,16 @@
             pl.BlockSpec((2 * STEP, 4, width), lambda i: (i, 0, 0)),
             pl.BlockSpec((8, width), lambda i: (0, 0)),
         ],
-        out_specs=pl.BlockSpec((8, lanes), lambda i: (0, 0)),
-        out_shape=jax.ShapeDtypeStruct((8, lanes), F32),
+        out_specs=[pl.BlockSpec((4, count), lambda i: (0, 0)) for count in lanes],
+        out_shape=[jax.ShapeDtypeStruct((4, count), F32) for count in lanes],
         cost_estimate=cost(tokens * 4 * width * 600, tokens * 8 * width),
         compiler_params=params(),
         name="stats",
     )(x, proj)
+
+
+def unfolded(block):
+    return jnp.concatenate([block[part : part + 1] for part in range(4)], axis=1)
 
 
 def by_stream(static_ref, column, stream):
@@ -215,12 +223,14 @@
     def _(step):
         at = pl.multiple_of(base + step * 4 * STEP, 4 * STEP)
         first = sums_ref[:, pl.ds(at, 4 * STEP)]
+        folded = pl.multiple_of(4 * (last // 5) + base // 4 + step * STEP, STEP)
+        cross = unfolded(sums_ref[:, pl.ds(folded, STEP)])
         mean, inverse = centre(first)
         mix = static + jnp.tanh(inverse * (first[0:1] - mean * column))
         one = jnp.where(stream < 3, pltpu.roll(mix, 4 * STEP - 1, 1), pltpu.roll(mix, 3, 1))
         two = jnp.where(stream < 2, pltpu.roll(mix, 4 * STEP - 2, 1), pltpu.roll(mix, 2, 1))
         linear = mix * first[1:2]
-        square = mix * (mix * first[2:3] + 2.0 * one * first[3:4] + two * first[4:5])
+        square = mix * (mix * first[2:3] + 2.0 * one * first[3:4] + two * cross)
         for half in range(STEP // SUB):
             lanes = slice(half * 4 * SUB, (half + 1) * 4 * SUB)
             rows = pl.ds(step * STEP + half * SUB, SUB)
@@ -238,7 +248,7 @@
 def mix(static, x, parts, start, tokens):
     width = x.shape[-1]
     lanes = parts[0].shape[1]
-    whole = pl.BlockSpec((8, lanes), lambda i: (0, 0))
+    whole = pl.BlockSpec((4, lanes), lambda i: (0, 0))
     return pl.pallas_call(
         functools.partial(mix_kernel, start),
         grid=(tokens // CHUNK,),
@@ -249,7 +259,7 @@
         + [whole] * 4,
         out_specs=[whole, pl.BlockSpec((CHUNK, width), lambda i: (i, 0))],
         out_shape=[
-            jax.ShapeDtypeStruct((8, lanes), F32),
+            jax.ShapeDtypeStruct((4, lanes), F32),
             jax.ShapeDtypeStruct((tokens, width), BF),
         ],
         cost_estimate=cost(tokens * 4 * width * 400, tokens * 10 * width),
@@ -259,22 +269,27 @@
 
 
 def qkv_kernel(ring_ref, rows_ref, cosine_ref, sine_ref, *refs):
-    out_ref, halo_ref = refs[-2:]
-    pieces = refs[:-2]
+    out_ref, halo_ref, left_ref = refs[-3:]
+    pieces = refs[:-3]
     servers, _, width = rows_ref.shape
     depth = pieces[0].shape[0]
-    if len(pieces) == 1:
-        left = [rows_ref[server] for server in range(servers)]
-    else:
-        left = []
-        for piece in range(len(pieces)):
-            source = ring_ref[0] ^ piece
-            inside = pl.multiple_of((source % (width // depth)) * depth, depth)
-            left.append(rows_ref[source // (width // depth), :, pl.ds(inside, depth)])
-    left = jnp.concatenate(left, axis=1)
+    slot = pl.program_id(0)
+
+    @pl.when(slot == 0)
+    def _():
+        if len(pieces) == 1:
+            for server in range(servers):
+                left_ref[:, server * width : (server + 1) * width] = rows_ref[server]
+        else:
+            for piece in range(len(pieces)):
+                source = ring_ref[0] ^ piece
+                inside = pl.multiple_of((source % (width // depth)) * depth, depth)
+                left_ref[:, piece * depth : (piece + 1) * depth] = rows_ref[
+                    source // (width // depth), :, pl.ds(inside, depth)
+                ]
+
     right = jnp.concatenate([piece[...] for piece in pieces], axis=0)
-    total = contract(left, right, 1, 0)
-    slot = pl.program_id(0)
+    total = contract(left_ref[...], right, 1, 0)
 
     @pl.when(slot < 2)
     def _():
@@ -288,11 +303,12 @@
     def _():
         out_ref[0] = total.astype(BF)
 
-    halo_ref[0] = out_ref[0, -BLOCK:, :]
+    halo_ref[0] = out_ref[0, -halo_ref.shape[1] :, :]
 
 
 def qkv_columns(ring, rows, pieces, cosine, sine):
     servers, tokens, width = rows.shape
+    kept = min(BLOCK, tokens)
     table = pl.BlockSpec((tokens, HEAD_DIM), lambda j: (0, 0))
     return pl.pallas_call(
         qkv_kernel,
@@ -306,12 +322,13 @@
         + [pl.BlockSpec((pieces[0].shape[0], width), lambda j: (0, j))] * len(pieces),
         out_specs=[
             pl.BlockSpec((1, tokens, width), lambda j: (j, 0, 0)),
-            pl.BlockSpec((1, BLOCK, width), lambda j: (jnp.maximum(j - 1, 0), 0, 0)),
+            pl.BlockSpec((1, kept, width), lambda j: (jnp.maximum(j - 1, 0), 0, 0)),
         ],
         out_shape=[
             jax.ShapeDtypeStruct((3, tokens, width), BF),
-            jax.ShapeDtypeStruct((2, BLOCK, width), BF),
+            jax.ShapeDtypeStruct((2, kept, width), BF),
         ],
+        scratch_shapes=[pltpu.VMEM((tokens, D), BF)],
         cost_estimate=cost(2 * tokens * D * 3 * width, D * 6 * width + tokens * D * 5),
         compiler_params=params(),
         name="qkv",
@@ -415,26 +432,23 @@
     )(place, ring, own, other, *pieces)
 
 
-def final_kernel(
-    static_ref, x_ref, first_ref, folded_ref, column_ref, own_ref, inner_ref, outer_ref, *rest
-):
-    new_ref = rest[-1]
+def final_kernel(static_ref, x_ref, first_ref, *refs):
+    second = [refs[3 * at][...] for at in range(4)]
+    folded = [refs[3 * at + 1][...] for at in range(4)]
+    column = [refs[3 * at + 2][...] for at in range(4)]
+    second, folded, column = [(a + b) + (c + d) for a, b, c, d in (second, folded, column)]
+    own_ref, inner_ref, outer_ref = refs[12:15]
+    new_ref = refs[-1]
     tokens, _, width = x_ref.shape
-    first = first_ref[...]
-    mean, inverse = centre(first)
+    mean, inverse = centre(first_ref[...])
     stream = lax.broadcasted_iota(jnp.int32, (1, 4 * tokens), 1) & 3
-
-    def coefficient(column, projected):
-        dynamic = jnp.tanh(inverse * (projected - mean * column_ref[column : column + 1, 0:1]))
-        return by_stream(static_ref, column, stream) + dynamic
-
-    def unfolded(which):
-        return jnp.concatenate(
-            [folded_ref[4 * which + part : 4 * which + part + 1] for part in range(4)], axis=1
-        )
-
-    projected = [first[5:6], first[6:7], first[7:8], unfolded(0), unfolded(1)]
-    columns = [coefficient(1 + j, projected[j]) for j in range(5)]
+    projected = [second[at : at + 1] for at in range(4)] + [unfolded(folded)]
+    totals = [column[at : at + 1, 0:1] for at in range(4)] + [column[0:1, 128:129]]
+    columns = [
+        by_stream(static_ref, 1 + at, stream)
+        + jnp.tanh(inverse * (projected[at] - mean * totals[at]))
+        for at in range(5)
+    ]
     residual = jnp.concatenate(columns[:4] + columns[:4], axis=0)
     row, col = iotas(4 * SUB, 4 * SUB)
     same = (row >> 2) == (col >> 2)
@@ -459,19 +473,23 @@
         new_ref[rows] = new.astype(BF).reshape(SUB, 4, width)
 
 
-def final(static, x, sums, updates, start, previous):
+def final(static, x, sums, second, updates, start, previous):
     tokens, width = updates[0].shape
-    group = (sums.shape[1] - 128) // 5
+    group = x.shape[0]
     stream_block = pl.BlockSpec((STEP, 4, width), lambda i: (start // STEP + i, 0, 0))
     specs = [
         pl.BlockSpec(memory_space=pltpu.SMEM),
         stream_block,
-        pl.BlockSpec((8, 4 * STEP), lambda i: (0, start // STEP + i)),
-        pl.BlockSpec((8, STEP), lambda i: (0, 4 * group // STEP + start // STEP + i)),
-        pl.BlockSpec((8, 128), lambda i: (0, 5 * group // 128)),
+        pl.BlockSpec((4, 4 * STEP), lambda i: (0, start // STEP + i)),
     ]
+    specs += [
+        pl.BlockSpec((4, 4 * STEP), lambda i: (0, start // STEP + i)),
+        pl.BlockSpec((4, STEP), lambda i: (0, 4 * group // STEP + start // STEP + i)),
+        pl.BlockSpec((4, 256), lambda i: (0, 5 * group // 256)),
+    ] * 4
+    seconds = [array for array in second for _ in range(3)]
     specs += [pl.BlockSpec((STEP, width), lambda i: (i, 0))] * 3
-    args = [static, x, sums, sums, sums, *updates]
+    args = [static, x, sums, *seconds, *updates]
     aliases = {}
     if previous is not None:
         specs.append(pl.BlockSpec(memory_space=pl.ANY))
@@ -499,26 +517,28 @@
     proj_rows = jnp.concatenate(
         [hc_proj.T, jnp.ones((1, width), F32), jnp.zeros((1, width), F32)], axis=0
     )
-    own = stats(streams, proj_rows)
+    first, second = stats(streams, proj_rows)
     parts = list(regroup(place, proj_master, group_size))
-    sums, parts = lax.optimization_barrier(([own] + from_others(own, "mp"), parts))
-
-    def gathered(normed):
-        rows = lax.all_gather(normed, "mp", axis=0, tiled=True)
-        return rows.reshape(group_size, normed.shape[0], width)
-
+    halo = passed_along(segment_ids[-BLOCK:], "blk", 1)
+    sums = [first] + from_others(first, "mp")
+    sums, parts, halo = lax.optimization_barrier((sums, parts, halo))
     for step in range(1, group_size):
         parts[step] = lax.ppermute(
             parts[step], "mp", [(at, (at + step) % group_size) for at in range(group_size)]
         )
-    sums_all, normed = mix(hc_static, streams, sums, 0, tokens_local)
-    parts, normed = lax.optimization_barrier((parts, normed))
-    rows = gathered(normed)
-
-    pieces = weight_pieces(assemble(place, parts))
-    rows, pieces = lax.optimization_barrier((rows, pieces))
-
-    halo = passed_along(segment_ids[-BLOCK:], "blk", 1)
+
+    sums_all, normed_late = mix(hc_static, streams, sums, CHUNK, tokens_local - CHUNK)
+    _, normed_first = mix(hc_static, streams, sums, 0, CHUNK)
+    parts, normed_late, normed_first = lax.optimization_barrier((parts, normed_late, normed_first))
+    rows_late = lax.all_gather(normed_late, "mp", axis=0, tiled=True)
+    rows_late = rows_late.reshape(group_size, tokens_local - CHUNK, width)
+    others = from_others(normed_first, "mp")
+    pieces, others = weight_pieces(assemble(place, parts), others)
+    rows_first = assemble(place, [normed_first] + others)
+    rows_first = rows_first.reshape(group_size, CHUNK, width)
+    second, pieces = lax.optimization_barrier((second, pieces))
+    second = [second] + from_others(second, "mp")
+
     halo = jnp.where(lax.axis_index("blk") == 0, -1, halo)
     extended = jnp.concatenate([halo, segment_ids])
     key_at = jnp.arange(tokens_local + BLOCK, dtype=jnp.int32)[None, :]
@@ -541,7 +561,9 @@
     key_segments = jnp.stack(windows)[:, None, :]
     query_segments = segment_ids[:, None]
 
-    qkv, halo_rows = qkv_columns(ring, rows, pieces, cosine, sine)
+    qkv_first, _ = qkv_columns(ring, rows_first, pieces, cosine[:CHUNK], sine[:CHUNK])
+    rows_late, qkv_first, second = lax.optimization_barrier((rows_late, qkv_first, second))
+    qkv_late, halo_rows = qkv_columns(ring, rows_late, pieces, cosine[CHUNK:], sine[CHUNK:])
     halo_rows = passed_along(halo_rows, "blk", 1)
 
     def projected(own):
@@ -549,11 +571,13 @@
         return project(place, ring, own, other, pieces, group_size)
 
     last = tokens_local // CHUNK - 1
-    chunks = [(halo_rows, 0, 0), (halo_rows, 0, 1)] + [(qkv, 1, at) for at in range(last + 1)]
+    chunks = [(halo_rows, 0, 0), (halo_rows, 0, 1), (qkv_first, 1, 0)]
+    chunks += [(qkv_late, 1, at) for at in range(last)]
     parts = {}
     for chunk in reversed(range(last + 1)):
         window = chunks[chunk : chunk + 3]
-        own = attend((qkv, chunk), window, query_segments, key_segments, chunk)
+        source, _, at = window[-1]
+        own = attend((source, at), window, query_segments, key_segments, chunk)
         parts[chunk] = projected(own)
 
     result = None
@@ -562,7 +586,7 @@
         inner = lax.ppermute(inner, "mp", [(1, 2), (2, 1)])
         outer = lax.ppermute(outer, "mp", [(1, 3), (2, 0)])
         updates = [kept, inner, outer]
-        result = final(hc_static, streams, sums_all, updates, chunk * CHUNK, result)
+        result = final(hc_static, streams, sums_all, second, updates, chunk * CHUNK, result)
     return result
 
 

time: 252 us -> 257 us (1.020)
  waiting for transfers between devices: 106 us -> 82.8 us
  starting transfers between devices: 34.8 us -> 53.5 us
  Pallas kernels: 80.8 us -> 89.9 us
    ppermute x11, waiting for transfers between devices: 55.4 us -> 9.86 us  [swapped(): lax.ppermute(value, axis, [(source, source ^ mask) for source in range(co...]
    ppermute x3 -> x9, waiting for transfers between devices: 4.98 us -> 38.4 us  [from_others(): lax.ppermute(value, axis, [(source, (source + step) % count) for source i...]
    ppermute x3 -> x9, starting transfers between devices: 6.96 us -> 26.3 us  [from_others(): lax.ppermute(value, axis, [(source, (source + step) % count) for source i...]
    all_gather x1, waiting for transfers between devices: 14.8 us -> 4.39 us  [body(): rows_late = lax.all_gather(normed_late, 'mp', axis=0, tiled=True)]
    pallas_call x1 -> x2, Pallas kernels: 13 us -> 17.5 us  [qkv_columns(): pl.pallas_call(qkv_kernel, grid=(3,), in_specs=[pl.BlockSpec(memory_space...]
    ppermute x11, starting transfers between devices: 9.38 us -> 12 us  [swapped(): lax.ppermute(value, axis, [(source, source ^ mask) for source in range(co...]
    ppermute x3, starting transfers between devices: 6.48 us -> 3.88 us  [body(): lax.ppermute(parts[step], 'mp', [(at, (at + step) % group_size) for at in...]
    pallas_call x1 -> x2, Pallas kernels: 5.64 us -> 7.46 us  [mix(): pl.pallas_call(functools.partial(mix_kernel, start), grid=(tokens // CHUN...]
  transfers between devices with their start and end apart: 28 -> 34, of which waited for: 11 -> 13; matrix products, arithmetic and copies ran while one was open for 3% -> 3% of each run, Pallas kernels for 23% -> 27%
where the time goes in v8:
time: 257 us; the launch traced here: 256 us
  Pallas kernels  89.9 us (35%)
  waiting for transfers between devices  82.8 us (32%)
  starting transfers between devices  53.5 us (21%)
  between operations  15.2 us (6%)
  local copies, waits for them, and re-layouts  7.81 us (3%)
  other arithmetic  6.96 us (3%)
    ppermute x9, waiting for transfers between devices, from_others(): lax.ppermute(value, axis, [(source, (source + step) % count) for source i...  38.4 us
    ppermute x9, starting transfers between devices, from_others(): lax.ppermute(value, axis, [(source, (source + step) % count) for source i...  26.3 us
    pallas_call x4, Pallas kernels, project(): pl.pallas_call(project_kernel, grid=(1,), in_specs=[pl.BlockSpec(memory_s...  18.7 us
    pallas_call x2, Pallas kernels, qkv_columns(): pl.pallas_call(qkv_kernel, grid=(3,), in_specs=[pl.BlockSpec(memory_space...  17.5 us
    pallas_call x4, Pallas kernels, attend(): pl.pallas_call(attend_kernel, grid=(1,), in_specs=[pl.BlockSpec(block, la...  16.1 us
    ppermute x4, waiting for transfers between devices, body(): outer = lax.ppermute(outer, 'mp', [(1, 3), (2, 0)])  15.2 us
    ppermute x3, waiting for transfers between devices, body(): lax.ppermute(parts[step], 'mp', [(at, (at + step) % group_size) for at in...  14.8 us
    pallas_call x4, Pallas kernels, final(): pl.pallas_call(final_kernel, grid=(tokens // STEP,), in_specs=specs, out_...  14.1 us
  transfers between devices with their start and end apart: 34, of which 13 were waited for; matrix products, arithmetic and copies ran while one was open for 3% of the time, Pallas kernels for 27%

profile of v8, /device:TPU:0, one launch (start us, length us, event | category | flops | bytes accessed | tf_op | source)
XLA Modules:
  0.0 256.1 jit_solution(5701402578330633546)
XLA Ops:
  6.7 1.4 maximum_maximum_fusion.proj_ref
  8.1 6.4 %stats.1 = (f32[4,5248]{1,0:T(4,128)}, f32[4,5376]{1,0:T(4,128)}) custom-call(bf16[1024,4,512]{2,1,0:T(4,128)(2,1)} %x_ref.13, f32[8,512]{1,0:T(8,128)} %maximum_maximum_fusion.proj_ref), custom_call_target="tpu_custom_call" | custom-call | flops 1258291200 | bytes 4194304 | tf_op jit(solution)/shard_map/stats/pallas_call | solution.py:175
  14.5 3.0 %collective-permute-start = (f32[4,5248]{1,0:T(4,128)}, f32[4,5248]{1,0:T(4,128)S(1)}, u32[]{:S(2)}, u32[]{:S(2)}) collective-permute-start(f32[4,5248]{1,0:T(4,128)} %get-tuple-element.71.own_ref), channel_id=1, source_target_pairs={{0,1},{1,2},{2,3},{3,0},{4,5},{5,6},{6,7},{7,4},{8,9},{9,10},{10,1... | collective-permute-start | bytes 251912 | tf_op jit(solution)/shard_map/ppermute | solution.py:31
  17.5 2.6 %collective-permute-start.1 = (f32[4,5248]{1,0:T(4,128)}, f32[4,5248]{1,0:T(4,128)S(1)}, u32[]{:S(2)}, u32[]{:S(2)}) collective-permute-start(f32[4,5248]{1,0:T(4,128)} %get-tuple-element.71.own_ref), channel_id=1, source_target_pairs={{0,2},{1,3},{2,0},{3,1},{4,6},{5,7},{6,4},{7,5},{8,10},{9,11},{10,... | collective-permute-start | bytes 251912 | tf_op jit(solution)/shard_map/ppermute | solution.py:31
  20.1 1.3 collective-permute-start.2
  22.7 1.3 collective-permute-start.3
  24.0 4.9 %regroup.1 = (bf16[64,2560]{1,0:T(8,128)(2,1)}, bf16[64,2560]{1,0:T(8,128)(2,1)}, bf16[64,2560]{1,0:T(8,128)(2,1)}, bf16[64,2560]{1,0:T(8,128)(2,1)}) custom-call(s32[1]{0:T(128)} %bitcast.1.place_ref, f32[64,4,2048]{2,1,0:T(4,128)} %master_ref.1), custom_call_target="tpu_custom_call" | custom-call | bytes 3407872 | tf_op jit(solution)/shard_map/regroup/pallas_call | solution.py:79
  28.9 0.7 collective-permute-start.4
  30.0 2.8 %collective-permute-start.6 = (bf16[64,2560]{1,0:T(8,128)(2,1)}, bf16[64,2560]{1,0:T(8,128)(2,1)S(1)}, u32[]{:S(2)}, u32[]{:S(2)}) collective-permute-start(bf16[64,2560]{1,0:T(8,128)(2,1)} %get-tuple-element.79), channel_id=1, source_target_pairs={{0,3},{1,0},{2,1},{3,2},{4,7},{5,4},{6,5},{7,6},{8,11},{9,8},{10,9... | collective-permute-start | bytes 983048 | tf_op jit(solution)/shard_map/ppermute | solution.py:526
  32.8 2.7 %mix.3 = (f32[4,5248]{1,0:T(4,128)}, bf16[256,512]{1,0:T(8,128)(2,1)}) custom-call(f32[4,6]{1,0:T(4,128)} %static_ref.11, bf16[1024,4,512]{2,1,0:T(4,128)(2,1)} %x_ref.13, f32[4,5248]{1,0:T(4,128)} %get-tuple-element.71.own_ref, f32[4,5248]{1,0:T(4,128)} %copy-done.7, f32[4,5248]{1,0:T(4,128)} %copy-done.8, f32[4,5248]{1,0:T(4,128)} %copy-done.9), custom_call_target="tpu_custom_call" | custom-call | flops 209715200 | bytes 1310720 | tf_op jit(solution)/shard_map/mix/pallas_call | solution.py:252
  35.6 4.7 %mix.2 = (f32[4,5248]{1,0:T(4,128)}, bf16[768,512]{1,0:T(8,128)(2,1)}) custom-call(f32[4,6]{1,0:T(4,128)} %static_ref.11, bf16[1024,4,512]{2,1,0:T(4,128)(2,1)} %x_ref.13, f32[4,5248]{1,0:T(4,128)} %get-tuple-element.71.own_ref, f32[4,5248]{1,0:T(4,128)} %copy-done.7, f32[4,5248]{1,0:T(4,128)} %copy-done.8, f32[4,5248]{1,0:T(4,128)} %copy-done.9), custom_call_target="tpu_custom_call" | custom-call | flops 629145600 | bytes 3932160 | tf_op jit(solution)/shard_map/mix/pallas_call | solution.py:252
  40.5 14.6 %collective-permute-done.5.refs_2_ = bf16[64,2560]{1,0:T(8,128)(2,1)S(1)} collective-permute-done((bf16[64,2560]{1,0:T(8,128)(2,1)}, bf16[64,2560]{1,0:T(8,128)(2,1)S(1)}, u32[]{:S(2)}, u32[]{:S(2)}) %collective-permute-start.5) | collective-permute-done | bytes 327712 | tf_op jit(solution)/shard_map/ppermute | solution.py:526
  56.0 2.5 assemble.2.refs_0_
  58.5 2.1 collective-permute-start.7
  60.6 1.5 collective-permute-start.9
  62.1 7.5 %collective-permute-start.10 = (bf16[256,512]{1,0:T(8,128)(2,1)S(1)}, bf16[256,512]{1,0:T(8,128)(2,1)S(1)}, u32[]{:S(2)}, u32[]{:S(2)}) collective-permute-start(bf16[256,512]{1,0:T(8,128)(2,1)S(1)} %copy-done.19), channel_id=1, source_target_pairs={{0,1},{1,2},{2,3},{3,0},{4,5},{5,6},{6,7},{7,4},{8,9},{9,10},{10,1... | collective-permute-start | bytes 786440 | tf_op jit(solution)/shard_map/ppermute | solution.py:31
  69.5 12.3 %collective-permute-done.10.refs_1_ = bf16[256,512]{1,0:T(8,128)(2,1)S(1)} collective-permute-done((bf16[256,512]{1,0:T(8,128)(2,1)S(1)}, bf16[256,512]{1,0:T(8,128)(2,1)S(1)}, u32[]{:S(2)}, u32[]{:S(2)}) %collective-permute-start.10) | collective-permute-done | bytes 262176 | tf_op jit(solution)/shard_map/ppermute | solution.py:31
  81.8 2.4 collective-permute-start.12
  84.8 15.4 %collective-permute-done.11.refs_2_ = bf16[256,512]{1,0:T(8,128)(2,1)S(1)} collective-permute-done((bf16[256,512]{1,0:T(8,128)(2,1)S(1)}, bf16[256,512]{1,0:T(8,128)(2,1)S(1)}, u32[]{:S(2)}, u32[]{:S(2)}) %collective-permute-start.11) | collective-permute-done | bytes 262176 | tf_op jit(solution)/shard_map/ppermute | solution.py:31
  100.2 10.0 %collective-permute-done.12.refs_3_ = bf16[256,512]{1,0:T(8,128)(2,1)S(1)} collective-permute-done((bf16[256,512]{1,0:T(8,128)(2,1)S(1)}, bf16[256,512]{1,0:T(8,128)(2,1)S(1)}, u32[]{:S(2)}, u32[]{:S(2)}) %collective-permute-start.12) | collective-permute-done | bytes 262176 | tf_op jit(solution)/shard_map/ppermute | solution.py:31
  110.2 9.7 %collective-permute-done.8.refs_4_ = bf16[256,2560]{1,0:T(8,128)(2,1)} collective-permute-done((bf16[256,2560]{1,0:T(8,128)(2,1)}, bf16[256,2560]{1,0:T(8,128)(2,1)}, u32[]{:S(2)}, u32[]{:S(2)}) %collective-permute-start.8) | collective-permute-done | bytes 1310752 | tf_op jit(solution)/shard_map/ppermute | solution.py:115
  120.9 1.6 convert_reduce_fusion
  122.5 1.9 fusion.1
  124.4 0.8 pad_maximum_fusion.2
  125.3 1.2 pad_maximum_fusion
  126.5 2.2 assemble.3
  128.9 7.1 %collective-permute-start.17 = (f32[4,5376]{1,0:T(4,128)S(1)}, f32[4,5376]{1,0:T(4,128)S(1)}, u32[]{:S(2)}, u32[]{:S(2)}) collective-permute-start(f32[4,5376]{1,0:T(4,128)S(1)} %copy-done.3), channel_id=1, source_target_pairs={{0,1},{1,2},{2,3},{3,0},{4,5},{5,6},{6,7},{7,4},{8,9},{9,10},{10,1... | collective-permute-start | bytes 258056 | tf_op jit(solution)/shard_map/ppermute | solution.py:31
  136.0 2.4 collective-permute-start.19
  138.4 6.5 %qkv.2 = (bf16[3,256,512]{2,1,0:T(8,128)(2,1)}, bf16[2,256,512]{2,1,0:T(8,128)(2,1)}) custom-call(s32[1]{0:T(128)} %bitcast.3.ring_ref, bf16[4,256,512]{2,1,0:T(8,128)(2,1)} %bitcast.10, f32[256,128]{1,0:T(8,128)} %get-tuple-element.144.cosine_ref, f32[256,128]{1,0:T(8,128)} %get-tuple-element.143.sine_ref, bf16[256,2560]{1,0:T(8,128)(2,1)} %assemble.2.refs_0_, ...), custom_call_target="tpu_custom_call" | custom-call | flops 1610612736 | bytes 8912896 | tf_op jit(solution)/shard_map/qkv/pallas_call | solution.py:313
  144.9 0.8 collective-permute-done.18.refs_6_.refs_7_.refs_8_
  145.7 4.4 %all-gather.2.cloned.1.call-done = bf16[3072,512]{1,0:T(8,128)(2,1)} async-done(((bf16[768,512]{1,0:T(8,128)(2,1)}), bf16[3072,512]{1,0:T(8,128)(2,1)}) %all-gather.2.cloned.1.call-update) | async-done | bytes 3145744 | tf_op jit(solution)/shard_map/all_gather | solution.py:533
  150.1 11.1 %qkv.3 = (bf16[3,768,512]{2,1,0:T(8,128)(2,1)}, bf16[2,512,512]{2,1,0:T(8,128)(2,1)}) custom-call(s32[1]{0:T(128)} %bitcast.3.ring_ref, bf16[4,768,512]{2,1,0:T(8,128)(2,1)} %bitcast.13, f32[768,128]{1,0:T(8,128)} %get-tuple-element.142.cosine_ref, f32[768,128]{1,0:T(8,128)} %get-tuple-element.141.sine_ref, bf16[256,2560]{1,0:T(8,128)(2,1)} %assemble.2.refs_0_, ...), custom_call_target="tpu_custom_call" | custom-call | flops 4831838208 | bytes 14155776 | tf_op jit(solution)/shard_map/qkv/pallas_call | solution.py:313
  161.2 1.9 collective-permute-start.20
  163.1 1.0 copy.14.qseg_ref
  164.9 4.0 %attend.6.own_ref = bf16[256,512]{1,0:T(8,128)(2,1)} custom-call(bf16[3,768,512]{2,1,0:T(8,128)(2,1)} %get-tuple-element.117.q_ref.k2.v2.k1.v1.k0.v0, bf16[3,256,512]{2,1,0:T(8,128)(2,1)} %get-tuple-element.111.q_ref.k2.v2.k1.v1.k0.v0, bf16[3,768,512]{2,1,0:T(8,128)(2,1)} %get-tuple-element.117.q_ref.k2.v2.k1.v1.k0.v0, ...), custom_call_target="tpu_custom_call" | custom-call | flops 402653184 | bytes 2097152 | tf_op jit(solution)/shard_map/attend/pallas_call | solution.py:368
  168.9 4.0 %attend.7.own_ref = bf16[256,512]{1,0:T(8,128)(2,1)} custom-call(bf16[3,768,512]{2,1,0:T(8,128)(2,1)} %get-tuple-element.117.q_ref.k2.v2.k1.v1.k0.v0, bf16[3,768,512]{2,1,0:T(8,128)(2,1)} %get-tuple-element.117.q_ref.k2.v2.k1.v1.k0.v0, bf16[3,768,512]{2,1,0:T(8,128)(2,1)} %get-tuple-element.117.q_ref.k2.v2.k1.v1.k0.v0, ...), custom_call_target="tpu_custom_call" | custom-call | flops 402653184 | bytes 2097152 | tf_op jit(solution)/shard_map/attend/pallas_call | solution.py:368
  172.9 2.0 collective-permute-start.30
  175.0 1.0 copy-done
  175.9 4.0 %attend.5.own_ref = bf16[256,512]{1,0:T(8,128)(2,1)} custom-call(bf16[3,768,512]{2,1,0:T(8,128)(2,1)} %get-tuple-element.117.q_ref.k2.v2.k1.v1.k0.v0, bf16[2,512,512]{2,1,0:T(8,128)(2,1)} %copy-done, bf16[3,256,512]{2,1,0:T(8,128)(2,1)} %get-tuple-element.111.q_ref.k2.v2.k1.v1.k0.v0, bf16[3,768,512]{2,1,0:T(8,128)(2,1)} %get-tuple-element.117.q_ref.k2.v2.k1.v1.k0.v0, ...), custom_call_target="tpu_custom_call" | custom-call | flops 402653184 | bytes 2097152 | tf_op jit(solution)/shard_map/attend/pallas_call | solution.py:368
  180.0 0.7 copy-done.28
  180.7 4.6 %project.6 = (f32[256,512]{1,0:T(8,128)}, bf16[256,512]{1,0:T(8,128)(2,1)}, bf16[256,512]{1,0:T(8,128)(2,1)}) custom-call(s32[1]{0:T(128)} %bitcast.1.place_ref, s32[1]{0:T(128)} %bitcast.3.ring_ref, bf16[256,512]{1,0:T(8,128)(2,1)} %attend.6.own_ref, bf16[256,512]{1,0:T(8,128)(2,1)} %copy-done.28, bf16[256,2560]{1,0:T(8,128)(2,1)} %assemble.2.refs_0_, ...), custom_call_target="tpu_custom_call" | custom-call | flops 1073741824 | bytes 5767168 | tf_op jit(solution)/shard_map/project/pallas_call | solution.py:418
  185.3 0.9 collective-permute-start.28
  186.2 4.0 %attend.4.own_ref = bf16[256,512]{1,0:T(8,128)(2,1)} custom-call(bf16[3,256,512]{2,1,0:T(8,128)(2,1)} %get-tuple-element.111.q_ref.k2.v2.k1.v1.k0.v0, bf16[2,512,512]{2,1,0:T(8,128)(2,1)} %copy-done, bf16[2,512,512]{2,1,0:T(8,128)(2,1)} %copy-done, bf16[3,256,512]{2,1,0:T(8,128)(2,1)} %get-tuple-element.111.q_ref.k2.v2.k1.v1.k0.v0, ...), custom_call_target="tpu_custom_call" | custom-call | flops 402653184 | bytes 2097152 | tf_op jit(solution)/shard_map/attend/pallas_call | solution.py:368
  190.2 5.4 %collective-permute-start.21 = (bf16[256,512]{1,0:T(8,128)(2,1)}, bf16[256,512]{1,0:T(8,128)(2,1)S(1)}, u32[]{:S(2)}, u32[]{:S(2)}) collective-permute-start(bf16[256,512]{1,0:T(8,128)(2,1)} %attend.4.own_ref), channel_id=1, source_target_pairs={{0,1},{1,0},{2,3},{3,2},{4,5},{5,4},{6,7},{7,6},{8,9},{9,8},{10,11... | collective-permute-start | bytes 786440 | tf_op jit(solution)/shard_map/ppermute | solution.py:115
  195.6 0.7 copy-done.27
  196.3 4.6 %project.7 = (f32[256,512]{1,0:T(8,128)}, bf16[256,512]{1,0:T(8,128)(2,1)}, bf16[256,512]{1,0:T(8,128)(2,1)}) custom-call(s32[1]{0:T(128)} %bitcast.1.place_ref, s32[1]{0:T(128)} %bitcast.3.ring_ref, bf16[256,512]{1,0:T(8,128)(2,1)} %attend.7.own_ref, bf16[256,512]{1,0:T(8,128)(2,1)} %copy-done.27, bf16[256,2560]{1,0:T(8,128)(2,1)} %assemble.2.refs_0_, ...), custom_call_target="tpu_custom_call" | custom-call | flops 1073741824 | bytes 5767168 | tf_op jit(solution)/shard_map/project/pallas_call | solution.py:418
  201.6 1.3 collective-permute-start.32
  202.9 1.3 collective-permute-start.29
  204.3 4.7 %project.5 = (f32[256,512]{1,0:T(8,128)}, bf16[256,512]{1,0:T(8,128)(2,1)}, bf16[256,512]{1,0:T(8,128)(2,1)}) custom-call(s32[1]{0:T(128)} %bitcast.1.place_ref, s32[1]{0:T(128)} %bitcast.3.ring_ref, bf16[256,512]{1,0:T(8,128)(2,1)} %attend.5.own_ref, bf16[256,512]{1,0:T(8,128)(2,1)} %copy-done.26, bf16[256,2560]{1,0:T(8,128)(2,1)} %assemble.2.refs_0_, ...), custom_call_target="tpu_custom_call" | custom-call | flops 1073741824 | bytes 5767168 | tf_op jit(solution)/shard_map/project/pallas_call | solution.py:418
  209.0 0.7 collective-permute-start.25
  209.7 1.3 collective-permute-start.26
  211.0 4.7 %project.4 = (f32[256,512]{1,0:T(8,128)}, bf16[256,512]{1,0:T(8,128)(2,1)}, bf16[256,512]{1,0:T(8,128)(2,1)}) custom-call(s32[1]{0:T(128)} %bitcast.1.place_ref, s32[1]{0:T(128)} %bitcast.3.ring_ref, bf16[256,512]{1,0:T(8,128)(2,1)} %attend.4.own_ref, bf16[256,512]{1,0:T(8,128)(2,1)} %copy-done.25, bf16[256,2560]{1,0:T(8,128)(2,1)} %assemble.2.refs_0_, ...), custom_call_target="tpu_custom_call" | custom-call | flops 1073741824 | bytes 5767168 | tf_op jit(solution)/shard_map/project/pallas_call | solution.py:418
  215.7 0.7 collective-permute-start.22
  216.9 1.3 collective-permute-start.23
  218.2 3.5 %final.4.refs_15_ = bf16[1024,4,512]{2,1,0:T(4,128)(2,1)} custom-call(f32[4,6]{1,0:T(4,128)} %static_ref.11, bf16[1024,4,512]{2,1,0:T(4,128)(2,1)} %x_ref.13, f32[4,5248]{1,0:T(4,128)} %get-tuple-element.75.first_ref, f32[4,5376]{1,0:T(4,128)} %get-tuple-element.107.refs_0_.refs_1_.refs_2_, f32[4,5376]{1,0:T(4,128)} %get-tuple-element.107.refs_0_.refs_1_.refs_2_, ...), custom_call_target="tpu_custom_call" | custom-call | flops 629145600 | bytes 2883584 | tf_op jit(solution)/shard_map/final/pallas_call | solution.py:498
  221.8 0.8 collective-permute-done.29.refs_14_
  222.5 0.7 copy-done.14
  223.2 3.5 %final.5.refs_15_ = bf16[1024,4,512]{2,1,0:T(4,128)(2,1)} custom-call(f32[4,6]{1,0:T(4,128)} %static_ref.11, bf16[1024,4,512]{2,1,0:T(4,128)(2,1)} %x_ref.13, f32[4,5248]{1,0:T(4,128)} %get-tuple-element.75.first_ref, f32[4,5376]{1,0:T(4,128)} %get-tuple-element.107.refs_0_.refs_1_.refs_2_, ...), custom_call_target="tpu_custom_call", output_to_operand_aliasing={{}: (18, {})} | custom-call | flops 629145600 | bytes 2883584 | tf_op jit(solution)/shard_map/final/pallas_call | solution.py:498
  226.8 7.0 %collective-permute-done.26.refs_14_ = bf16[256,512]{1,0:T(8,128)(2,1)S(1)} collective-permute-done((bf16[256,512]{1,0:T(8,128)(2,1)}, bf16[256,512]{1,0:T(8,128)(2,1)S(1)}, u32[]{:S(2)}, u32[]{:S(2)}) %collective-permute-start.26) | collective-permute-done | bytes 262176 | tf_op jit(solution)/shard_map/ppermute | solution.py:587
  233.8 0.7 copy-done.16
  234.4 3.5 %final.6.refs_15_ = bf16[1024,4,512]{2,1,0:T(4,128)(2,1)} custom-call(f32[4,6]{1,0:T(4,128)} %static_ref.11, bf16[1024,4,512]{2,1,0:T(4,128)(2,1)} %x_ref.13, f32[4,5248]{1,0:T(4,128)} %get-tuple-element.75.first_ref, f32[4,5376]{1,0:T(4,128)} %get-tuple-element.107.refs_0_.refs_1_.refs_2_, ...), custom_call_target="tpu_custom_call", output_to_operand_aliasing={{}: (18, {})} | custom-call | flops 629145600 | bytes 2883584 | tf_op jit(solution)/shard_map/final/pallas_call | solution.py:498
  238.0 7.0 %collective-permute-done.23.refs_14_ = bf16[256,512]{1,0:T(8,128)(2,1)S(1)} collective-permute-done((bf16[256,512]{1,0:T(8,128)(2,1)}, bf16[256,512]{1,0:T(8,128)(2,1)S(1)}, u32[]{:S(2)}, u32[]{:S(2)}) %collective-permute-start.23) | collective-permute-done | bytes 262176 | tf_op jit(solution)/shard_map/ppermute | solution.py:587
  245.0 0.7 copy-done.18
  245.7 3.5 %final.7 = bf16[1024,4,512]{2,1,0:T(4,128)(2,1)} custom-call(f32[4,6]{1,0:T(4,128)} %static_ref.11, bf16[1024,4,512]{2,1,0:T(4,128)(2,1)} %x_ref.13, f32[4,5248]{1,0:T(4,128)} %get-tuple-element.75.first_ref, f32[4,5376]{1,0:T(4,128)} %get-tuple-element.107.refs_0_.refs_1_.refs_2_, ...), custom_call_target="tpu_custom_call", output_to_operand_aliasing={{}: (18, {})} | custom-call | flops 629145600 | bytes 2883584 | tf_op jit(solution)/shard_map/final/pallas_call | solution.py:498
  (114 shorter events, 5.4 us)
Async XLA Ops:
  6.5 14.9 %copy-start.30 = (s32[2]{0:T(128)S(1)}, s32[2]{0:T(128)}, u32[]{:S(2)}) copy-start(s32[2]{0:T(128)} %param.11) | copy-start | bytes 28
  6.5 16.1 %copy-start.29 = (s32[1024]{0:T(1024)S(1)}, s32[1024]{0:T(1024)}, u32[]{:S(2)}) copy-start(s32[1024]{0:T(1024)} %param.10) | copy-start | bytes 12292
  6.5 143.5 %all-gather.2.cloned.1.call-start = ((), (), s32[]{:S(2)}) async-start(), calls=%async_computation | async-start | bytes 3932160 | tf_op jit(solution)/shard_map/all_gather | solution.py:533
  14.5 14.4 %collective-permute-start = (f32[4,5248]{1,0:T(4,128)}, f32[4,5248]{1,0:T(4,128)S(1)}, u32[]{:S(2)}, u32[]{:S(2)}) collective-permute-start(f32[4,5248]{1,0:T(4,128)} %get-tuple-element.71.own_ref), channel_id=1, source_target_pairs={{0,1},{1,2},{2,3},{3,0},{4,5},{5,6},{6,7},{7,4},{8,9},{9,10},{10,1... | collective-permute-start | bytes 251912 | tf_op jit(solution)/shard_map/ppermute | solution.py:31
  17.5 11.4 %collective-permute-start.1 = (f32[4,5248]{1,0:T(4,128)}, f32[4,5248]{1,0:T(4,128)S(1)}, u32[]{:S(2)}, u32[]{:S(2)}) collective-permute-start(f32[4,5248]{1,0:T(4,128)} %get-tuple-element.71.own_ref), channel_id=1, source_target_pairs={{0,2},{1,3},{2,0},{3,1},{4,6},{5,7},{6,4},{7,5},{8,10},{9,11},{10,... | collective-permute-start | bytes 251912 | tf_op jit(solution)/shard_map/ppermute | solution.py:31
  20.1 8.8 %collective-permute-start.2 = (f32[4,5248]{1,0:T(4,128)}, f32[4,5248]{1,0:T(4,128)S(1)}, u32[]{:S(2)}, u32[]{:S(2)}) collective-permute-start(f32[4,5248]{1,0:T(4,128)} %get-tuple-element.71.own_ref), channel_id=1, source_target_pairs={{0,3},{1,0},{2,1},{3,2},{4,7},{5,4},{6,5},{7,6},{8,11},{9,8},{10,9... | collective-permute-start | bytes 251912 | tf_op jit(solution)/shard_map/ppermute | solution.py:31
  22.7 6.2 %collective-permute-start.3 = (s32[512]{0:T(512)S(1)}, s32[512]{0:T(512)S(1)}, u32[]{:S(2)}, u32[]{:S(2)}) collective-permute-start(s32[512]{0:T(512)S(1)} %get-tuple-element.136), channel_id=1, source_target_pairs={{0,4},{4,8},{8,12},{12,16},{16,20},{20,24},{24,28},{1,5},{5,9},{9,... | collective-permute-start | bytes 6152 | tf_op jit(solution)/shard_map/ppermute | solution.py:25
  28.9 3.9 %copy-start.7 = (f32[4,5248]{1,0:T(4,128)}, f32[4,5248]{1,0:T(4,128)S(1)}, u32[]{:S(2)}) copy-start(f32[4,5248]{1,0:T(4,128)S(1)} %collective-permute-done.a_ref) | copy-start | bytes 251908
  28.9 3.9 %copy-start.8 = (f32[4,5248]{1,0:T(4,128)}, f32[4,5248]{1,0:T(4,128)S(1)}, u32[]{:S(2)}) copy-start(f32[4,5248]{1,0:T(4,128)S(1)} %collective-permute-done.1.b_ref) | copy-start | bytes 251908
  28.9 3.9 %copy-start.9 = (f32[4,5248]{1,0:T(4,128)}, f32[4,5248]{1,0:T(4,128)S(1)}, u32[]{:S(2)}) copy-start(f32[4,5248]{1,0:T(4,128)S(1)} %collective-permute-done.2.c_ref) | copy-start | bytes 251908
  28.9 11.6 %collective-permute-start.4 = (bf16[64,2560]{1,0:T(8,128)(2,1)}, bf16[64,2560]{1,0:T(8,128)(2,1)S(1)}, u32[]{:S(2)}, u32[]{:S(2)}) collective-permute-start(bf16[64,2560]{1,0:T(8,128)(2,1)} %get-tuple-element.77), channel_id=1, source_target_pairs={{0,1},{1,2},{2,3},{3,0},{4,5},{5,6},{6,7},{7,4},{8,9},{9,10},{10,1... | collective-permute-start | bytes 983048 | tf_op jit(solution)/shard_map/ppermute | solution.py:526
  29.7 25.5 %collective-permute-start.5 = (bf16[64,2560]{1,0:T(8,128)(2,1)}, bf16[64,2560]{1,0:T(8,128)(2,1)S(1)}, u32[]{:S(2)}, u32[]{:S(2)}) collective-permute-start(bf16[64,2560]{1,0:T(8,128)(2,1)} %get-tuple-element.78), channel_id=1, source_target_pairs={{0,2},{1,3},{2,0},{3,1},{4,6},{5,7},{6,4},{7,5},{8,10},{9,11},{10,... | collective-permute-start | bytes 983048 | tf_op jit(solution)/shard_map/ppermute | solution.py:526
  30.0 25.1 %collective-permute-start.6 = (bf16[64,2560]{1,0:T(8,128)(2,1)}, bf16[64,2560]{1,0:T(8,128)(2,1)S(1)}, u32[]{:S(2)}, u32[]{:S(2)}) collective-permute-start(bf16[64,2560]{1,0:T(8,128)(2,1)} %get-tuple-element.79), channel_id=1, source_target_pairs={{0,3},{1,0},{2,1},{3,2},{4,7},{5,4},{6,5},{7,6},{8,11},{9,8},{10,9... | collective-permute-start | bytes 983048 | tf_op jit(solution)/shard_map/ppermute | solution.py:526
  40.3 21.8 %copy-start.19 = (bf16[256,512]{1,0:T(8,128)(2,1)S(1)}, bf16[256,512]{1,0:T(8,128)(2,1)}, u32[]{:S(2)}) copy-start(bf16[256,512]{1,0:T(8,128)(2,1)} %get-tuple-element.83.refs_0_) | copy-start | bytes 786436
  40.5 14.6 %copy-start.10 = (bf16[64,2560]{1,0:T(8,128)(2,1)}, bf16[64,2560]{1,0:T(8,128)(2,1)S(1)}, u32[]{:S(2)}) copy-start(bf16[64,2560]{1,0:T(8,128)(2,1)S(1)} %collective-permute-done.4.refs_1_) | copy-start | bytes 983044
  55.1 0.7 copy-start.11
  55.1 0.8 copy-start.12
  58.5 51.7 %collective-permute-start.7 = (bf16[256,2560]{1,0:T(8,128)(2,1)}, bf16[256,2560]{1,0:T(8,128)(2,1)S(1)}, u32[]{:S(2)}, u32[]{:S(2)}) collective-permute-start(bf16[256,2560]{1,0:T(8,128)(2,1)} %assemble.2.refs_0_), channel_id=1, source_target_pairs={{0,8},{4,12},{8,0},{12,4},{16,24},{20,28},{24,16},{28,20},{1,9},{5... | collective-permute-start | bytes 3932168 | tf_op jit(solution)/shard_map/ppermute | solution.py:115
  60.6 59.3 %collective-permute-start.8 = (bf16[256,2560]{1,0:T(8,128)(2,1)}, bf16[256,2560]{1,0:T(8,128)(2,1)}, u32[]{:S(2)}, u32[]{:S(2)}) collective-permute-start(bf16[256,2560]{1,0:T(8,128)(2,1)} %assemble.2.refs_0_), channel_id=1, source_target_pairs={{0,16},{4,20},{8,24},{12,28},{16,0},{20,4},{24,8},{28,12},{1,17},{... | collective-permute-start | bytes 3932168 | tf_op jit(solution)/shard_map/ppermute | solution.py:115
  60.6 59.2 %collective-permute-start.9 = (bf16[256,2560]{1,0:T(8,128)(2,1)}, bf16[256,2560]{1,0:T(8,128)(2,1)}, u32[]{:S(2)}, u32[]{:S(2)}) collective-permute-start(bf16[256,2560]{1,0:T(8,128)(2,1)} %assemble.2.refs_0_), channel_id=1, source_target_pairs={{0,24},{4,28},{8,16},{12,20},{16,8},{20,12},{24,0},{28,4},{1,25},{... | collective-permute-start | bytes 3932168 | tf_op jit(solution)/shard_map/ppermute | solution.py:115
  62.1 19.7 %collective-permute-start.10 = (bf16[256,512]{1,0:T(8,128)(2,1)S(1)}, bf16[256,512]{1,0:T(8,128)(2,1)S(1)}, u32[]{:S(2)}, u32[]{:S(2)}) collective-permute-start(bf16[256,512]{1,0:T(8,128)(2,1)S(1)} %copy-done.19), channel_id=1, source_target_pairs={{0,1},{1,2},{2,3},{3,0},{4,5},{5,6},{6,7},{7,4},{8,9},{9,10},{10,1... | collective-permute-start | bytes 786440 | tf_op jit(solution)/shard_map/ppermute | solution.py:31
  69.5 30.7 %collective-permute-start.11 = (bf16[256,512]{1,0:T(8,128)(2,1)S(1)}, bf16[256,512]{1,0:T(8,128)(2,1)S(1)}, u32[]{:S(2)}, u32[]{:S(2)}) collective-permute-start(bf16[256,512]{1,0:T(8,128)(2,1)S(1)} %copy-done.19), channel_id=1, source_target_pairs={{0,2},{1,3},{2,0},{3,1},{4,6},{5,7},{6,4},{7,5},{8,10},{9,11},{10,... | collective-permute-start | bytes 786440 | tf_op jit(solution)/shard_map/ppermute | solution.py:31
  81.8 44.6 %copy-start.20 = (bf16[256,512]{1,0:T(8,128)(2,1)}, bf16[256,512]{1,0:T(8,128)(2,1)S(1)}, u32[]{:S(2)}) copy-start(bf16[256,512]{1,0:T(8,128)(2,1)S(1)} %collective-permute-done.10.refs_1_) | copy-start | bytes 786436
  81.8 28.4 %collective-permute-start.12 = (bf16[256,512]{1,0:T(8,128)(2,1)S(1)}, bf16[256,512]{1,0:T(8,128)(2,1)S(1)}, u32[]{:S(2)}, u32[]{:S(2)}) collective-permute-start(bf16[256,512]{1,0:T(8,128)(2,1)S(1)} %copy-done.19), channel_id=1, source_target_pairs={{0,3},{1,0},{2,1},{3,2},{4,7},{5,4},{6,5},{7,6},{8,11},{9,8},{10,9... | collective-permute-start | bytes 786440 | tf_op jit(solution)/shard_map/ppermute | solution.py:31
  100.2 26.3 %copy-start.21 = (bf16[256,512]{1,0:T(8,128)(2,1)}, bf16[256,512]{1,0:T(8,128)(2,1)S(1)}, u32[]{:S(2)}) copy-start(bf16[256,512]{1,0:T(8,128)(2,1)S(1)} %collective-permute-done.11.refs_2_) | copy-start | bytes 786436
  110.2 9.7 %copy-start.22 = (bf16[256,512]{1,0:T(8,128)(2,1)}, bf16[256,512]{1,0:T(8,128)(2,1)S(1)}, u32[]{:S(2)}) copy-start(bf16[256,512]{1,0:T(8,128)(2,1)S(1)} %collective-permute-done.12.refs_3_) | copy-start | bytes 786436
  110.2 16.3 %copy-start.1 = (bf16[256,2560]{1,0:T(8,128)(2,1)}, bf16[256,2560]{1,0:T(8,128)(2,1)S(1)}, u32[]{:S(2)}) copy-start(bf16[256,2560]{1,0:T(8,128)(2,1)S(1)} %collective-permute-done.7.refs_2_) | copy-start | bytes 3932164
  119.9 8.8 %collective-permute-start.13 = (bf16[256,2560]{1,0:T(8,128)(2,1)}, bf16[256,2560]{1,0:T(8,128)(2,1)S(1)}, u32[]{:S(2)}, u32[]{:S(2)}) collective-permute-start(bf16[256,2560]{1,0:T(8,128)(2,1)} %assemble.2.refs_0_), channel_id=1, source_target_pairs={{0,4},{4,0},{8,12},{12,8},{16,20},{20,16},{24,28},{28,24},{1,5},{5... | collective-permute-start | bytes 3932168 | tf_op jit(solution)/shard_map/ppermute | solution.py:115
  119.9 8.8 %collective-permute-start.14 = (bf16[256,2560]{1,0:T(8,128)(2,1)S(1)}, bf16[256,2560]{1,0:T(8,128)(2,1)}, u32[]{:S(2)}, u32[]{:S(2)}) collective-permute-start(bf16[256,2560]{1,0:T(8,128)(2,1)S(1)} %collective-permute-done.7.refs_2_), channel_id=1, source_target_pairs={{0,4},{4,0},{8,12},{12,8},{16,20},{20,16},{24,28},{28,24},{1,5},{5... | collective-permute-start | bytes 3932168 | tf_op jit(solution)/shard_map/ppermute | solution.py:115
  120.4 8.3 %collective-permute-start.15 = (bf16[256,2560]{1,0:T(8,128)(2,1)}, bf16[256,2560]{1,0:T(8,128)(2,1)}, u32[]{:S(2)}, u32[]{:S(2)}) collective-permute-start(bf16[256,2560]{1,0:T(8,128)(2,1)} %collective-permute-done.8.refs_4_), channel_id=1, source_target_pairs={{0,4},{4,0},{8,12},{12,8},{16,20},{20,16},{24,28},{28,24},{1,5},{5... | collective-permute-start | bytes 3932168 | tf_op jit(solution)/shard_map/ppermute | solution.py:115
  120.4 8.4 %collective-permute-start.16 = (bf16[256,2560]{1,0:T(8,128)(2,1)}, bf16[256,2560]{1,0:T(8,128)(2,1)}, u32[]{:S(2)}, u32[]{:S(2)}) collective-permute-start(bf16[256,2560]{1,0:T(8,128)(2,1)} %collective-permute-done.9.refs_6_), channel_id=1, source_target_pairs={{0,4},{4,0},{8,12},{12,8},{16,20},{20,16},{24,28},{28,24},{1,5},{5... | collective-permute-start | bytes 3932168 | tf_op jit(solution)/shard_map/ppermute | solution.py:115
  125.3 3.6 %copy-start.3 = (f32[4,5376]{1,0:T(4,128)S(1)}, f32[4,5376]{1,0:T(4,128)}, u32[]{:S(2)}) copy-start(f32[4,5376]{1,0:T(4,128)} %get-tuple-element.107.refs_0_.refs_1_.refs_2_) | copy-start | bytes 258052
  128.7 9.7 %copy-start.2 = (bf16[256,2560]{1,0:T(8,128)(2,1)}, bf16[256,2560]{1,0:T(8,128)(2,1)S(1)}, u32[]{:S(2)}) copy-start(bf16[256,2560]{1,0:T(8,128)(2,1)S(1)} %collective-permute-done.13.refs_1_) | copy-start | bytes 3932164
  128.9 16.0 %collective-permute-start.17 = (f32[4,5376]{1,0:T(4,128)S(1)}, f32[4,5376]{1,0:T(4,128)S(1)}, u32[]{:S(2)}, u32[]{:S(2)}) collective-permute-start(f32[4,5376]{1,0:T(4,128)S(1)} %copy-done.3), channel_id=1, source_target_pairs={{0,1},{1,2},{2,3},{3,0},{4,5},{5,6},{6,7},{7,4},{8,9},{9,10},{10,1... | collective-permute-start | bytes 258056 | tf_op jit(solution)/shard_map/ppermute | solution.py:31
  136.0 9.7 %collective-permute-start.18 = (f32[4,5376]{1,0:T(4,128)S(1)}, f32[4,5376]{1,0:T(4,128)S(1)}, u32[]{:S(2)}, u32[]{:S(2)}) collective-permute-start(f32[4,5376]{1,0:T(4,128)S(1)} %copy-done.3), channel_id=1, source_target_pairs={{0,2},{1,3},{2,0},{3,1},{4,6},{5,7},{6,4},{7,5},{8,10},{9,11},{10,... | collective-permute-start | bytes 258056 | tf_op jit(solution)/shard_map/ppermute | solution.py:31
  136.0 9.7 %collective-permute-start.19 = (f32[4,5376]{1,0:T(4,128)S(1)}, f32[4,5376]{1,0:T(4,128)S(1)}, u32[]{:S(2)}, u32[]{:S(2)}) collective-permute-start(f32[4,5376]{1,0:T(4,128)S(1)} %copy-done.3), channel_id=1, source_target_pairs={{0,3},{1,0},{2,1},{3,2},{4,7},{5,4},{6,5},{7,6},{8,11},{9,8},{10,9... | collective-permute-start | bytes 258056 | tf_op jit(solution)/shard_map/ppermute | solution.py:31
  144.8 16.3 %copy-start.4 = (f32[4,5376]{1,0:T(4,128)}, f32[4,5376]{1,0:T(4,128)S(1)}, u32[]{:S(2)}) copy-start(f32[4,5376]{1,0:T(4,128)S(1)} %collective-permute-done.17.refs_3_.refs_4_.refs_5_) | copy-start | bytes 258052
  145.7 15.5 %copy-start.5 = (f32[4,5376]{1,0:T(4,128)}, f32[4,5376]{1,0:T(4,128)S(1)}, u32[]{:S(2)}) copy-start(f32[4,5376]{1,0:T(4,128)S(1)} %collective-permute-done.18.refs_6_.refs_7_.refs_8_) | copy-start | bytes 258052
  145.7 15.5 %copy-start.6 = (f32[4,5376]{1,0:T(4,128)}, f32[4,5376]{1,0:T(4,128)S(1)}, u32[]{:S(2)}) copy-start(f32[4,5376]{1,0:T(4,128)S(1)} %collective-permute-done.19.refs_9_.refs_10_.refs_11_) | copy-start | bytes 258052
  161.2 13.8 %collective-permute-start.20 = (bf16[2,512,512]{2,1,0:T(8,128)(2,1)}, bf16[2,512,512]{2,1,0:T(8,128)(2,1)S(1)}, u32[]{:S(2)}, u32[]{:S(2)}) collective-permute-start(bf16[2,512,512]{2,1,0:T(8,128)(2,1)} %get-tuple-element.113), channel_id=1, source_target_pairs={{0,4},{4,8},{8,12},{12,16},{16,20},{20,24},{24,28},{1,5},{5,9},{9,... | collective-permute-start | bytes 3145736 | tf_op jit(solution)/shard_map/ppermute | solution.py:25
  168.9 11.1 %collective-permute-start.27 = (bf16[256,512]{1,0:T(8,128)(2,1)}, bf16[256,512]{1,0:T(8,128)(2,1)S(1)}, u32[]{:S(2)}, u32[]{:S(2)}) collective-permute-start(bf16[256,512]{1,0:T(8,128)(2,1)} %attend.6.own_ref), channel_id=1, source_target_pairs={{0,1},{1,0},{2,3},{3,2},{4,5},{5,4},{6,7},{7,6},{8,9},{9,8},{10,11... | collective-permute-start | bytes 786440 | tf_op jit(solution)/shard_map/ppermute | solution.py:115
  172.9 22.7 %collective-permute-start.30 = (bf16[256,512]{1,0:T(8,128)(2,1)}, bf16[256,512]{1,0:T(8,128)(2,1)S(1)}, u32[]{:S(2)}, u32[]{:S(2)}) collective-permute-start(bf16[256,512]{1,0:T(8,128)(2,1)} %attend.7.own_ref), channel_id=1, source_target_pairs={{0,1},{1,0},{2,3},{3,2},{4,5},{5,4},{6,7},{7,6},{8,9},{9,8},{10,11... | collective-permute-start | bytes 786440 | tf_op jit(solution)/shard_map/ppermute | solution.py:115
  175.0 1.0 copy-start
  179.9 23.0 %collective-permute-start.24 = (bf16[256,512]{1,0:T(8,128)(2,1)}, bf16[256,512]{1,0:T(8,128)(2,1)S(1)}, u32[]{:S(2)}, u32[]{:S(2)}) collective-permute-start(bf16[256,512]{1,0:T(8,128)(2,1)} %attend.5.own_ref), channel_id=1, source_target_pairs={{0,1},{1,0},{2,3},{3,2},{4,5},{5,4},{6,7},{7,6},{8,9},{9,8},{10,11... | collective-permute-start | bytes 786440 | tf_op jit(solution)/shard_map/ppermute | solution.py:115
  180.0 0.7 copy-start.28
  185.3 23.7 %collective-permute-start.28 = (bf16[256,512]{1,0:T(8,128)(2,1)}, bf16[256,512]{1,0:T(8,128)(2,1)S(1)}, u32[]{:S(2)}, u32[]{:S(2)}) collective-permute-start(bf16[256,512]{1,0:T(8,128)(2,1)} %get-tuple-element.122), channel_id=1, source_target_pairs={{1,2},{2,1},{5,6},{6,5},{9,10},{10,9},{13,14},{14,13},{17,18},{18,... | collective-permute-start | bytes 786440 | tf_op jit(solution)/shard_map/ppermute | solution.py:586
  190.2 12.7 %copy-start.31 = (bf16[256,512]{1,0:T(8,128)(2,1)S(1)}, bf16[256,512]{1,0:T(8,128)(2,1)}, u32[]{:S(2)}) copy-start(bf16[256,512]{1,0:T(8,128)(2,1)} %get-tuple-element.123) | copy-start | bytes 786436
  190.2 19.4 %collective-permute-start.21 = (bf16[256,512]{1,0:T(8,128)(2,1)}, bf16[256,512]{1,0:T(8,128)(2,1)S(1)}, u32[]{:S(2)}, u32[]{:S(2)}) collective-permute-start(bf16[256,512]{1,0:T(8,128)(2,1)} %attend.4.own_ref), channel_id=1, source_target_pairs={{0,1},{1,0},{2,3},{3,2},{4,5},{5,4},{6,7},{7,6},{8,9},{9,8},{10,11... | collective-permute-start | bytes 786440 | tf_op jit(solution)/shard_map/ppermute | solution.py:115
  195.6 0.7 copy-start.27
  200.9 14.8 %collective-permute-start.31 = (bf16[256,512]{1,0:T(8,128)(2,1)}, bf16[256,512]{1,0:T(8,128)(2,1)S(1)}, u32[]{:S(2)}, u32[]{:S(2)}) collective-permute-start(bf16[256,512]{1,0:T(8,128)(2,1)} %get-tuple-element.125), channel_id=1, source_target_pairs={{1,2},{2,1},{5,6},{6,5},{9,10},{10,9},{13,14},{14,13},{17,18},{18,... | collective-permute-start | bytes 786440 | tf_op jit(solution)/shard_map/ppermute | solution.py:586
  201.6 15.3 %collective-permute-start.32 = (bf16[256,512]{1,0:T(8,128)(2,1)}, bf16[256,512]{1,0:T(8,128)(2,1)S(1)}, u32[]{:S(2)}, u32[]{:S(2)}) collective-permute-start(bf16[256,512]{1,0:T(8,128)(2,1)} %get-tuple-element.126), channel_id=1, source_target_pairs={{1,3},{2,0},{5,7},{6,4},{9,11},{10,8},{13,15},{14,12},{17,19},{18,... | collective-permute-start | bytes 786440 | tf_op jit(solution)/shard_map/ppermute | solution.py:587
  202.9 1.3 copy-start.26
  202.9 19.6 %collective-permute-start.29 = (bf16[256,512]{1,0:T(8,128)(2,1)S(1)}, bf16[256,512]{1,0:T(8,128)(2,1)S(1)}, u32[]{:S(2)}, u32[]{:S(2)}) collective-permute-start(bf16[256,512]{1,0:T(8,128)(2,1)S(1)} %copy-done.31), channel_id=1, source_target_pairs={{1,3},{2,0},{5,7},{6,4},{9,11},{10,8},{13,15},{14,12},{17,19},{18,... | collective-permute-start | bytes 786440 | tf_op jit(solution)/shard_map/ppermute | solution.py:587
  209.0 6.7 %copy-start.13 = (bf16[256,512]{1,0:T(8,128)(2,1)}, bf16[256,512]{1,0:T(8,128)(2,1)S(1)}, u32[]{:S(2)}) copy-start(bf16[256,512]{1,0:T(8,128)(2,1)S(1)} %collective-permute-done.28.refs_13_) | copy-start | bytes 786436
  209.0 17.8 %collective-permute-start.25 = (bf16[256,512]{1,0:T(8,128)(2,1)}, bf16[256,512]{1,0:T(8,128)(2,1)S(1)}, u32[]{:S(2)}, u32[]{:S(2)}) collective-permute-start(bf16[256,512]{1,0:T(8,128)(2,1)} %get-tuple-element.119), channel_id=1, source_target_pairs={{1,2},{2,1},{5,6},{6,5},{9,10},{10,9},{13,14},{14,13},{17,18},{18,... | collective-permute-start | bytes 786440 | tf_op jit(solution)/shard_map/ppermute | solution.py:586
  209.7 1.3 copy-start.25
  209.7 24.1 %collective-permute-start.26 = (bf16[256,512]{1,0:T(8,128)(2,1)}, bf16[256,512]{1,0:T(8,128)(2,1)S(1)}, u32[]{:S(2)}, u32[]{:S(2)}) collective-permute-start(bf16[256,512]{1,0:T(8,128)(2,1)} %get-tuple-element.120), channel_id=1, source_target_pairs={{1,3},{2,0},{5,7},{6,4},{9,11},{10,8},{13,15},{14,12},{17,19},{18,... | collective-permute-start | bytes 786440 | tf_op jit(solution)/shard_map/ppermute | solution.py:587
  215.7 2.5 copy-start.23
  215.7 22.2 %collective-permute-start.22 = (bf16[256,512]{1,0:T(8,128)(2,1)}, bf16[256,512]{1,0:T(8,128)(2,1)S(1)}, u32[]{:S(2)}, u32[]{:S(2)}) collective-permute-start(bf16[256,512]{1,0:T(8,128)(2,1)} %get-tuple-element.115), channel_id=1, source_target_pairs={{1,2},{2,1},{5,6},{6,5},{9,10},{10,9},{13,14},{14,13},{17,18},{18,... | collective-permute-start | bytes 786440 | tf_op jit(solution)/shard_map/ppermute | solution.py:586
  216.9 1.3 copy-start.24
  216.9 28.1 %collective-permute-start.23 = (bf16[256,512]{1,0:T(8,128)(2,1)}, bf16[256,512]{1,0:T(8,128)(2,1)S(1)}, u32[]{:S(2)}, u32[]{:S(2)}) collective-permute-start(bf16[256,512]{1,0:T(8,128)(2,1)} %get-tuple-element.116), channel_id=1, source_target_pairs={{1,3},{2,0},{5,7},{6,4},{9,11},{10,8},{13,15},{14,12},{17,19},{18,... | collective-permute-start | bytes 786440 | tf_op jit(solution)/shard_map/ppermute | solution.py:587
  226.8 7.0 %copy-start.15 = (bf16[256,512]{1,0:T(8,128)(2,1)}, bf16[256,512]{1,0:T(8,128)(2,1)S(1)}, u32[]{:S(2)}) copy-start(bf16[256,512]{1,0:T(8,128)(2,1)S(1)} %collective-permute-done.25.refs_13_) | copy-start | bytes 786436
  238.0 7.0 %copy-start.17 = (bf16[256,512]{1,0:T(8,128)(2,1)}, bf16[256,512]{1,0:T(8,128)(2,1)S(1)}, u32[]{:S(2)}) copy-start(bf16[256,512]{1,0:T(8,128)(2,1)S(1)} %collective-permute-done.22.refs_13_) | copy-start | bytes 786436
  245.0 0.7 copy-start.18
  (2 other events, 1.4 us)
Sparse Core Ops, SparseCore 0:
  55.3 94.7 all-gather.1

commit v9 on v8

--- a/solution.py
+++ b/solution.py
@@ -115,16 +115,16 @@
     return lax.ppermute(value, axis, [(source, source ^ mask) for source in range(count)])
 
 
-def weight_pieces(part, beside):
+def weight_pieces(part):
     count = lax.axis_size("blk")
     if count & (count - 1) or part.shape[0] % HEAD_DIM or count > 8:
-        return [lax.all_gather(part, "blk", axis=0, tiled=True)], beside
-    even = [part] + [swapped(part, "blk", mask) for mask in range(2, count, 2)]
-    even, beside = lax.optimization_barrier((even, beside))
-    pieces = []
-    for piece in even:
-        pieces += [piece, swapped(piece, "blk", 1)]
-    return pieces, beside
+        return [lax.all_gather(part, "blk", axis=0, tiled=True)]
+    pieces = {0: part}
+    for mask in range(2, count, 2):
+        pieces[mask] = swapped(part, "blk", mask)
+    for mask in range(0, count, 2):
+        pieces[mask + 1] = swapped(pieces[mask], "blk", 1)
+    return [pieces[mask] for mask in range(count)]
 
 
 def stats_kernel(x_ref, proj_ref, first_ref, second_ref):
@@ -269,27 +269,22 @@
 
 
 def qkv_kernel(ring_ref, rows_ref, cosine_ref, sine_ref, *refs):
-    out_ref, halo_ref, left_ref = refs[-3:]
-    pieces = refs[:-3]
+    out_ref, halo_ref = refs[-2:]
+    pieces = refs[:-2]
     servers, _, width = rows_ref.shape
     depth = pieces[0].shape[0]
+    if len(pieces) == 1:
+        left = [rows_ref[server] for server in range(servers)]
+    else:
+        left = []
+        for piece in range(len(pieces)):
+            source = ring_ref[0] ^ piece
+            inside = pl.multiple_of((source % (width // depth)) * depth, depth)
+            left.append(rows_ref[source // (width // depth), :, pl.ds(inside, depth)])
+    left = jnp.concatenate(left, axis=1)
+    right = jnp.concatenate([piece[...] for piece in pieces], axis=0)
+    total = contract(left, right, 1, 0)
     slot = pl.program_id(0)
-
-    @pl.when(slot == 0)
-    def _():
-        if len(pieces) == 1:
-            for server in range(servers):
-                left_ref[:, server * width : (server + 1) * width] = rows_ref[server]
-        else:
-            for piece in range(len(pieces)):
-                source = ring_ref[0] ^ piece
-                inside = pl.multiple_of((source % (width // depth)) * depth, depth)
-                left_ref[:, piece * depth : (piece + 1) * depth] = rows_ref[
-                    source // (width // depth), :, pl.ds(inside, depth)
-                ]
-
-    right = jnp.concatenate([piece[...] for piece in pieces], axis=0)
-    total = contract(left_ref[...], right, 1, 0)
 
     @pl.when(slot < 2)
     def _():
@@ -303,12 +298,11 @@
     def _():
         out_ref[0] = total.astype(BF)
 
-    halo_ref[0] = out_ref[0, -halo_ref.shape[1] :, :]
+    halo_ref[0] = out_ref[0, -BLOCK:, :]
 
 
 def qkv_columns(ring, rows, pieces, cosine, sine):
     servers, tokens, width = rows.shape
-    kept = min(BLOCK, tokens)
     table = pl.BlockSpec((tokens, HEAD_DIM), lambda j: (0, 0))
     return pl.pallas_call(
         qkv_kernel,
@@ -322,13 +316,12 @@
         + [pl.BlockSpec((pieces[0].shape[0], width), lambda j: (0, j))] * len(pieces),
         out_specs=[
             pl.BlockSpec((1, tokens, width), lambda j: (j, 0, 0)),
-            pl.BlockSpec((1, kept, width), lambda j: (jnp.maximum(j - 1, 0), 0, 0)),
+            pl.BlockSpec((1, BLOCK, width), lambda j: (jnp.maximum(j - 1, 0), 0, 0)),
         ],
         out_shape=[
             jax.ShapeDtypeStruct((3, tokens, width), BF),
-            jax.ShapeDtypeStruct((2, kept, width), BF),
+            jax.ShapeDtypeStruct((2, BLOCK, width), BF),
         ],
-        scratch_shapes=[pltpu.VMEM((tokens, D), BF)],
         cost_estimate=cost(2 * tokens * D * 3 * width, D * 6 * width + tokens * D * 5),
         compiler_params=params(),
         name="qkv",
@@ -517,27 +510,25 @@
     proj_rows = jnp.concatenate(
         [hc_proj.T, jnp.ones((1, width), F32), jnp.zeros((1, width), F32)], axis=0
     )
-    first, second = stats(streams, proj_rows)
     parts = list(regroup(place, proj_master, group_size))
-    halo = passed_along(segment_ids[-BLOCK:], "blk", 1)
-    sums = [first] + from_others(first, "mp")
-    sums, parts, halo = lax.optimization_barrier((sums, parts, halo))
+    proj_rows, parts = lax.optimization_barrier((proj_rows, parts))
     for step in range(1, group_size):
         parts[step] = lax.ppermute(
             parts[step], "mp", [(at, (at + step) % group_size) for at in range(group_size)]
         )
-
-    sums_all, normed_late = mix(hc_static, streams, sums, CHUNK, tokens_local - CHUNK)
-    _, normed_first = mix(hc_static, streams, sums, 0, CHUNK)
-    parts, normed_late, normed_first = lax.optimization_barrier((parts, normed_late, normed_first))
-    rows_late = lax.all_gather(normed_late, "mp", axis=0, tiled=True)
-    rows_late = rows_late.reshape(group_size, tokens_local - CHUNK, width)
-    others = from_others(normed_first, "mp")
-    pieces, others = weight_pieces(assemble(place, parts), others)
-    rows_first = assemble(place, [normed_first] + others)
-    rows_first = rows_first.reshape(group_size, CHUNK, width)
+    first, second = stats(streams, proj_rows)
+    halo = passed_along(segment_ids[-BLOCK:], "blk", 1)
+
+    sums = [first] + from_others(first, "mp")
+    sums_all, normed = mix(hc_static, streams, sums, 0, tokens_local)
+    parts, normed, halo = lax.optimization_barrier((parts, normed, halo))
+    rows = lax.all_gather(normed, "mp", axis=0, tiled=True)
+    rows = rows.reshape(group_size, tokens_local, width)
+
+    pieces = weight_pieces(assemble(place, parts))
     second, pieces = lax.optimization_barrier((second, pieces))
     second = [second] + from_others(second, "mp")
+    rows, pieces, second = lax.optimization_barrier((rows, pieces, second))
 
     halo = jnp.where(lax.axis_index("blk") == 0, -1, halo)
     extended = jnp.concatenate([halo, segment_ids])
@@ -561,9 +552,7 @@
     key_segments = jnp.stack(windows)[:, None, :]
     query_segments = segment_ids[:, None]
 
-    qkv_first, _ = qkv_columns(ring, rows_first, pieces, cosine[:CHUNK], sine[:CHUNK])
-    rows_late, qkv_first, second = lax.optimization_barrier((rows_late, qkv_first, second))
-    qkv_late, halo_rows = qkv_columns(ring, rows_late, pieces, cosine[CHUNK:], sine[CHUNK:])
+    qkv, halo_rows = qkv_columns(ring, rows, pieces, cosine, sine)
     halo_rows = passed_along(halo_rows, "blk", 1)
 
     def projected(own):
@@ -571,13 +560,11 @@
         return project(place, ring, own, other, pieces, group_size)
 
     last = tokens_local // CHUNK - 1
-    chunks = [(halo_rows, 0, 0), (halo_rows, 0, 1), (qkv_first, 1, 0)]
-    chunks += [(qkv_late, 1, at) for at in range(last)]
+    chunks = [(halo_rows, 0, 0), (halo_rows, 0, 1)] + [(qkv, 1, at) for at in range(last + 1)]
     parts = {}
     for chunk in reversed(range(last + 1)):
         window = chunks[chunk : chunk + 3]
-        source, _, at = window[-1]
-        own = attend((source, at), window, query_segments, key_segments, chunk)
+        own = attend((qkv, chunk), window, query_segments, key_segments, chunk)
         parts[chunk] = projected(own)
 
     result = None

time: 257 us -> 260 us (1.012)
  waiting for transfers between devices: 82.8 us -> 106 us
  starting transfers between devices: 53.5 us -> 41.9 us
  Pallas kernels: 89.9 us -> 81.1 us
    ppermute x11, waiting for transfers between devices: 9.86 us -> 56.9 us  [swapped(): lax.ppermute(value, axis, [(source, source ^ mask) for source in range(co...]
    ppermute x3, waiting for transfers between devices: 14.8 us -> 0.01 us  [body(): lax.ppermute(parts[step], 'mp', [(at, (at + step) % group_size) for at in...]
    ppermute x9 -> x6, waiting for transfers between devices: 38.4 us -> 28.4 us  [from_others(): lax.ppermute(value, axis, [(source, (source + step) % count) for source i...]
    ppermute x9 -> x6, starting transfers between devices: 26.3 us -> 16.9 us  [from_others(): lax.ppermute(value, axis, [(source, (source + step) % count) for source i...]
    pallas_call x2 -> x1, Pallas kernels: 17.5 us -> 13 us  [qkv_columns(): pl.pallas_call(qkv_kernel, grid=(3,), in_specs=[pl.BlockSpec(memory_space...]
    ppermute x11, starting transfers between devices: 12 us -> 9.29 us  [swapped(): lax.ppermute(value, axis, [(source, source ^ mask) for source in range(co...]
    pallas_call x2 -> x1, Pallas kernels: 7.46 us -> 5.51 us  [mix(): pl.pallas_call(functools.partial(mix_kernel, start), grid=(tokens // CHUN...]
    unnamed x64 -> x60, local copies, waits for them, and re-layouts: 5.42 us -> 6.11 us
  transfers between devices with their start and end apart: 34 -> 31, of which waited for: 13 -> 13; matrix products, arithmetic and copies ran while one was open for 3% -> 3% of each run, Pallas kernels for 27% -> 21%
where the time goes in v9:
time: 260 us; the launch traced here: 259 us
  waiting for transfers between devices  106 us (41%)
  Pallas kernels  81.1 us (31%)
  starting transfers between devices  41.9 us (16%)
  between operations  15.2 us (6%)
  local copies, waits for them, and re-layouts  8.51 us (3%)
  other arithmetic  6.35 us (2%)
    ppermute x11, waiting for transfers between devices, swapped(): lax.ppermute(value, axis, [(source, source ^ mask) for source in range(co...  56.9 us
    ppermute x6, waiting for transfers between devices, from_others(): lax.ppermute(value, axis, [(source, (source + step) % count) for source i...  28.4 us
    pallas_call x4, Pallas kernels, project(): pl.pallas_call(project_kernel, grid=(1,), in_specs=[pl.BlockSpec(memory_s...  18.6 us
    ppermute x6, starting transfers between devices, from_others(): lax.ppermute(value, axis, [(source, (source + step) % count) for source i...  16.9 us
    pallas_call x4, Pallas kernels, attend(): pl.pallas_call(attend_kernel, grid=(1,), in_specs=[pl.BlockSpec(block, la...  16.1 us
    ppermute x4, waiting for transfers between devices, body(): outer = lax.ppermute(outer, 'mp', [(1, 3), (2, 0)])  15.1 us
    pallas_call x4, Pallas kernels, final(): pl.pallas_call(final_kernel, grid=(tokens // STEP,), in_specs=specs, out_...  14.1 us
    pallas_call x1, Pallas kernels, qkv_columns(): pl.pallas_call(qkv_kernel, grid=(3,), in_specs=[pl.BlockSpec(memory_space...  13 us
  transfers between devices with their start and end apart: 31, of which 13 were waited for; matrix products, arithmetic and copies ran while one was open for 3% of the time, Pallas kernels for 21%

profile of v9, /device:TPU:0, one launch (start us, length us, event | category | flops | bytes accessed | tf_op | source)
XLA Modules:
  0.0 259.3 jit_solution(7434441250850914443)
XLA Ops:
  6.7 4.9 %regroup.1 = (bf16[64,2560]{1,0:T(8,128)(2,1)}, bf16[64,2560]{1,0:T(8,128)(2,1)}, bf16[64,2560]{1,0:T(8,128)(2,1)}, bf16[64,2560]{1,0:T(8,128)(2,1)}) custom-call(s32[1]{0:T(128)} %bitcast.1.place_ref, f32[64,4,2048]{2,1,0:T(4,128)} %master_ref.1), custom_call_target="tpu_custom_call" | custom-call | bytes 3407872 | tf_op jit(solution)/shard_map/regroup/pallas_call | solution.py:79
  11.6 1.5 maximum_maximum_fusion.proj_ref
  13.1 6.4 %stats.1 = (f32[4,5248]{1,0:T(4,128)}, f32[4,5376]{1,0:T(4,128)}) custom-call(bf16[1024,4,512]{2,1,0:T(4,128)(2,1)} %x_ref.11, f32[8,512]{1,0:T(8,128)} %maximum_maximum_fusion.proj_ref), custom_call_target="tpu_custom_call" | custom-call | flops 1258291200 | bytes 4194304 | tf_op jit(solution)/shard_map/stats/pallas_call | solution.py:175
  19.5 3.0 %collective-permute-start = (f32[4,5248]{1,0:T(4,128)}, f32[4,5248]{1,0:T(4,128)S(1)}, u32[]{:S(2)}, u32[]{:S(2)}) collective-permute-start(f32[4,5248]{1,0:T(4,128)} %get-tuple-element.65.own_ref), channel_id=1, source_target_pairs={{0,1},{1,2},{2,3},{3,0},{4,5},{5,6},{6,7},{7,4},{8,9},{9,10},{10,1... | collective-permute-start | bytes 251912 | tf_op jit(solution)/shard_map/ppermute | solution.py:31
  22.5 2.6 collective-permute-start.1
  25.1 1.9 collective-permute-start.4
  27.0 2.0 collective-permute-start.5
  29.0 0.6 fusion.5
  30.2 0.6 collective-permute-start.2
  30.9 14.2 %collective-permute-done.1.b_ref = f32[4,5248]{1,0:T(4,128)S(1)} collective-permute-done((f32[4,5248]{1,0:T(4,128)}, f32[4,5248]{1,0:T(4,128)S(1)}, u32[]{:S(2)}, u32[]{:S(2)}) %collective-permute-start.1) | collective-permute-done | bytes 84000 | tf_op jit(solution)/shard_map/ppermute | solution.py:31
  45.1 1.7 collective-permute-start.6
  46.8 6.6 %collective-permute-done.2.c_ref = f32[4,5248]{1,0:T(4,128)S(1)} collective-permute-done((f32[4,5248]{1,0:T(4,128)}, f32[4,5248]{1,0:T(4,128)S(1)}, u32[]{:S(2)}, u32[]{:S(2)}) %collective-permute-start.2) | collective-permute-done | bytes 84000 | tf_op jit(solution)/shard_map/ppermute | solution.py:31
  53.5 0.6 copy-done.23
  54.1 5.5 %mix.1 = (f32[4,5248]{1,0:T(4,128)}, bf16[1024,512]{1,0:T(8,128)(2,1)}) custom-call(f32[4,6]{1,0:T(4,128)} %static_ref.9, bf16[1024,4,512]{2,1,0:T(4,128)(2,1)} %x_ref.11, f32[4,5248]{1,0:T(4,128)} %get-tuple-element.65.own_ref, f32[4,5248]{1,0:T(4,128)} %copy-done.21, f32[4,5248]{1,0:T(4,128)} %copy-done.22, f32[4,5248]{1,0:T(4,128)} %copy-done.23), custom_call_target="tpu_custom_call" | custom-call | flops 838860800 | bytes 5242880 | tf_op jit(solution)/shard_map/mix/pallas_call | solution.py:252
  59.7 0.7 copy-done.6
  60.6 2.5 assemble.1.refs_0_
  63.0 1.4 collective-permute-start.8
  64.4 1.5 collective-permute-start.10
  66.5 28.4 %collective-permute-done.8.refs_2_ = bf16[256,2560]{1,0:T(8,128)(2,1)S(1)} collective-permute-done((bf16[256,2560]{1,0:T(8,128)(2,1)}, bf16[256,2560]{1,0:T(8,128)(2,1)S(1)}, u32[]{:S(2)}, u32[]{:S(2)}) %collective-permute-start.8) | collective-permute-done | bytes 1310752 | tf_op jit(solution)/shard_map/ppermute | solution.py:115
  94.9 27.9 %collective-permute-done.10.refs_4_ = bf16[256,2560]{1,0:T(8,128)(2,1)} collective-permute-done((bf16[256,2560]{1,0:T(8,128)(2,1)}, bf16[256,2560]{1,0:T(8,128)(2,1)}, u32[]{:S(2)}, u32[]{:S(2)}) %collective-permute-start.10) | collective-permute-done | bytes 1310752 | tf_op jit(solution)/shard_map/ppermute | solution.py:115
  124.1 1.6 convert_reduce_fusion
  125.7 1.9 fusion.1
  128.1 8.3 %collective-permute-start.14 = (f32[4,5376]{1,0:T(4,128)S(1)}, f32[4,5376]{1,0:T(4,128)S(1)}, u32[]{:S(2)}, u32[]{:S(2)}) collective-permute-start(f32[4,5376]{1,0:T(4,128)S(1)} %copy-done.2), channel_id=1, source_target_pairs={{0,1},{1,2},{2,3},{3,0},{4,5},{5,6},{6,7},{7,4},{8,9},{9,10},{10,1... | collective-permute-start | bytes 258056 | tf_op jit(solution)/shard_map/ppermute | solution.py:31
  136.4 2.4 collective-permute-start.16
  138.8 1.3 pad_maximum_fusion
  140.1 1.0 collective-permute-done.14.refs_3_.refs_4_.refs_5_
  141.2 5.7 %collective-permute-done.15.refs_6_.refs_7_.refs_8_ = f32[4,5376]{1,0:T(4,128)S(1)} collective-permute-done((f32[4,5376]{1,0:T(4,128)S(1)}, f32[4,5376]{1,0:T(4,128)S(1)}, u32[]{:S(2)}, u32[]{:S(2)}) %collective-permute-start.15) | collective-permute-done | bytes 86048 | tf_op jit(solution)/shard_map/ppermute | solution.py:31
  146.8 0.8 collective-permute-done.16.refs_9_.refs_10_.refs_11_
  147.6 5.9 %all-gather.2.cloned.1.call-done = bf16[4096,512]{1,0:T(8,128)(2,1)} async-done(((bf16[1024,512]{1,0:T(8,128)(2,1)}), bf16[4096,512]{1,0:T(8,128)(2,1)}) %all-gather.2.cloned.1.call-update) | async-done | bytes 4194320 | tf_op jit(solution)/shard_map/all_gather | solution.py:525
  153.5 13.0 %qkv.1 = (bf16[3,1024,512]{2,1,0:T(8,128)(2,1)}, bf16[2,512,512]{2,1,0:T(8,128)(2,1)}) custom-call(s32[1]{0:T(128)} %bitcast.3.ring_ref, bf16[4,1024,512]{2,1,0:T(8,128)(2,1)} %bitcast.11, f32[1024,128]{1,0:T(8,128)} %get-tuple-element.129.cosine_ref, f32[1024,128]{1,0:T(8,128)} %get-tuple-element.130.sine_ref, bf16[256,2560]{1,0:T(8,128)(2,1)} %assemble.1.refs_0_, ...), custom_call_target="tpu_custom_call" | custom-call | flops 6442450944 | bytes 16777216 | tf_op jit(solution)/shard_map/qkv/pallas_call | solution.py:307
  166.5 2.0 collective-permute-start.17
  168.5 1.0 copy.14.qseg_ref
  169.7 0.6 broadcast_in_dim.29.kseg_ref
  170.3 4.0 %attend.6.own_ref = bf16[256,512]{1,0:T(8,128)(2,1)} custom-call(bf16[3,1024,512]{2,1,0:T(8,128)(2,1)} %get-tuple-element.101.q_ref.k2.v2.k1.v1.k0.v0, bf16[3,1024,512]{2,1,0:T(8,128)(2,1)} %get-tuple-element.101.q_ref.k2.v2.k1.v1.k0.v0, bf16[3,1024,512]{2,1,0:T(8,128)(2,1)} %get-tuple-element.101.q_ref.k2.v2.k1.v1.k0.v0, ...), custom_call_target="tpu_custom_call" | custom-call | flops 402653184 | bytes 2097152 | tf_op jit(solution)/shard_map/attend/pallas_call | solution.py:361
  174.3 4.0 %attend.7.own_ref = bf16[256,512]{1,0:T(8,128)(2,1)} custom-call(bf16[3,1024,512]{2,1,0:T(8,128)(2,1)} %get-tuple-element.101.q_ref.k2.v2.k1.v1.k0.v0, bf16[3,1024,512]{2,1,0:T(8,128)(2,1)} %get-tuple-element.101.q_ref.k2.v2.k1.v1.k0.v0, bf16[3,1024,512]{2,1,0:T(8,128)(2,1)} %get-tuple-element.101.q_ref.k2.v2.k1.v1.k0.v0, ...), custom_call_target="tpu_custom_call" | custom-call | flops 402653184 | bytes 2097152 | tf_op jit(solution)/shard_map/attend/pallas_call | solution.py:361
  178.4 2.0 collective-permute-start.27
  180.4 1.0 copy-done
  181.4 4.0 %attend.5.own_ref = bf16[256,512]{1,0:T(8,128)(2,1)} custom-call(bf16[3,1024,512]{2,1,0:T(8,128)(2,1)} %get-tuple-element.101.q_ref.k2.v2.k1.v1.k0.v0, bf16[2,512,512]{2,1,0:T(8,128)(2,1)} %copy-done, bf16[3,1024,512]{2,1,0:T(8,128)(2,1)} %get-tuple-element.101.q_ref.k2.v2.k1.v1.k0.v0, bf16[3,1024,512]{2,1,0:T(8,128)(2,1)} %get-tuple-element.101.q_ref.k2.v2.k1.v1.k0.v0, ...), custom_call_target="tpu_custom_call" | custom-call | flops 402653184 | bytes 2097152 | tf_op jit(solution)/shard_map/attend/pallas_call | solution.py:361
  185.4 0.7 copy-done.20
  186.1 4.6 %project.6 = (f32[256,512]{1,0:T(8,128)}, bf16[256,512]{1,0:T(8,128)(2,1)}, bf16[256,512]{1,0:T(8,128)(2,1)}) custom-call(s32[1]{0:T(128)} %bitcast.1.place_ref, s32[1]{0:T(128)} %bitcast.3.ring_ref, bf16[256,512]{1,0:T(8,128)(2,1)} %attend.6.own_ref, bf16[256,512]{1,0:T(8,128)(2,1)} %copy-done.20, bf16[256,2560]{1,0:T(8,128)(2,1)} %assemble.1.refs_0_, ...), custom_call_target="tpu_custom_call" | custom-call | flops 1073741824 | bytes 5767168 | tf_op jit(solution)/shard_map/project/pallas_call | solution.py:411
  190.8 0.7 collective-permute-start.25
  191.5 4.0 %attend.4.own_ref = bf16[256,512]{1,0:T(8,128)(2,1)} custom-call(bf16[3,1024,512]{2,1,0:T(8,128)(2,1)} %get-tuple-element.101.q_ref.k2.v2.k1.v1.k0.v0, bf16[2,512,512]{2,1,0:T(8,128)(2,1)} %copy-done, bf16[2,512,512]{2,1,0:T(8,128)(2,1)} %copy-done, bf16[3,1024,512]{2,1,0:T(8,128)(2,1)} %get-tuple-element.101.q_ref.k2.v2.k1.v1.k0.v0, ...), custom_call_target="tpu_custom_call" | custom-call | flops 402653184 | bytes 2097152 | tf_op jit(solution)/shard_map/attend/pallas_call | solution.py:361
  195.5 3.3 %collective-permute-start.18 = (bf16[256,512]{1,0:T(8,128)(2,1)}, bf16[256,512]{1,0:T(8,128)(2,1)S(1)}, u32[]{:S(2)}, u32[]{:S(2)}) collective-permute-start(bf16[256,512]{1,0:T(8,128)(2,1)} %attend.4.own_ref), channel_id=1, source_target_pairs={{0,1},{1,0},{2,3},{3,2},{4,5},{5,4},{6,7},{7,6},{8,9},{9,8},{10,11... | collective-permute-start | bytes 786440 | tf_op jit(solution)/shard_map/ppermute | solution.py:115
  198.8 0.7 copy-done.19
  199.5 4.7 %project.7 = (f32[256,512]{1,0:T(8,128)}, bf16[256,512]{1,0:T(8,128)(2,1)}, bf16[256,512]{1,0:T(8,128)(2,1)}) custom-call(s32[1]{0:T(128)} %bitcast.1.place_ref, s32[1]{0:T(128)} %bitcast.3.ring_ref, bf16[256,512]{1,0:T(8,128)(2,1)} %attend.7.own_ref, bf16[256,512]{1,0:T(8,128)(2,1)} %copy-done.19, bf16[256,2560]{1,0:T(8,128)(2,1)} %assemble.1.refs_0_, ...), custom_call_target="tpu_custom_call" | custom-call | flops 1073741824 | bytes 5767168 | tf_op jit(solution)/shard_map/project/pallas_call | solution.py:411
  204.1 0.7 collective-permute-start.28
  204.8 1.3 collective-permute-start.29
  206.1 1.3 collective-permute-start.26
  207.4 4.7 %project.5 = (f32[256,512]{1,0:T(8,128)}, bf16[256,512]{1,0:T(8,128)(2,1)}, bf16[256,512]{1,0:T(8,128)(2,1)}) custom-call(s32[1]{0:T(128)} %bitcast.1.place_ref, s32[1]{0:T(128)} %bitcast.3.ring_ref, bf16[256,512]{1,0:T(8,128)(2,1)} %attend.5.own_ref, bf16[256,512]{1,0:T(8,128)(2,1)} %copy-done.18, bf16[256,2560]{1,0:T(8,128)(2,1)} %assemble.1.refs_0_, ...), custom_call_target="tpu_custom_call" | custom-call | flops 1073741824 | bytes 5767168 | tf_op jit(solution)/shard_map/project/pallas_call | solution.py:411
  212.1 0.7 collective-permute-start.22
  212.8 1.5 collective-permute-start.23
  214.3 4.7 %project.4 = (f32[256,512]{1,0:T(8,128)}, bf16[256,512]{1,0:T(8,128)(2,1)}, bf16[256,512]{1,0:T(8,128)(2,1)}) custom-call(s32[1]{0:T(128)} %bitcast.1.place_ref, s32[1]{0:T(128)} %bitcast.3.ring_ref, bf16[256,512]{1,0:T(8,128)(2,1)} %attend.4.own_ref, bf16[256,512]{1,0:T(8,128)(2,1)} %copy-done.17, bf16[256,2560]{1,0:T(8,128)(2,1)} %assemble.1.refs_0_, ...), custom_call_target="tpu_custom_call" | custom-call | flops 1073741824 | bytes 5767168 | tf_op jit(solution)/shard_map/project/pallas_call | solution.py:411
  219.0 0.7 collective-permute-start.19
  220.1 1.3 collective-permute-start.20
  221.4 3.5 %final.4.refs_15_ = bf16[1024,4,512]{2,1,0:T(4,128)(2,1)} custom-call(f32[4,6]{1,0:T(4,128)} %static_ref.9, bf16[1024,4,512]{2,1,0:T(4,128)(2,1)} %x_ref.11, f32[4,5248]{1,0:T(4,128)} %get-tuple-element.66.first_ref, f32[4,5376]{1,0:T(4,128)} %get-tuple-element.87.refs_0_.refs_1_.refs_2_, f32[4,5376]{1,0:T(4,128)} %get-tuple-element.87.refs_0_.refs_1_.refs_2_, ...), custom_call_target="tpu_custom_call" | custom-call | flops 629145600 | bytes 2883584 | tf_op jit(solution)/shard_map/final/pallas_call | solution.py:491
  225.0 0.8 collective-permute-done.26.refs_14_
  225.8 0.7 copy-done.10
  226.5 3.5 %final.5.refs_15_ = bf16[1024,4,512]{2,1,0:T(4,128)(2,1)} custom-call(f32[4,6]{1,0:T(4,128)} %static_ref.9, bf16[1024,4,512]{2,1,0:T(4,128)(2,1)} %x_ref.11, f32[4,5248]{1,0:T(4,128)} %get-tuple-element.66.first_ref, f32[4,5376]{1,0:T(4,128)} %get-tuple-element.87.refs_0_.refs_1_.refs_2_, ...), custom_call_target="tpu_custom_call", output_to_operand_aliasing={{}: (18, {})} | custom-call | flops 629145600 | bytes 2883584 | tf_op jit(solution)/shard_map/final/pallas_call | solution.py:491
  230.0 7.0 %collective-permute-done.23.refs_14_ = bf16[256,512]{1,0:T(8,128)(2,1)S(1)} collective-permute-done((bf16[256,512]{1,0:T(8,128)(2,1)}, bf16[256,512]{1,0:T(8,128)(2,1)S(1)}, u32[]{:S(2)}, u32[]{:S(2)}) %collective-permute-start.23) | collective-permute-done | bytes 262176 | tf_op jit(solution)/shard_map/ppermute | solution.py:574
  237.0 0.7 copy-done.12
  237.7 3.5 %final.6.refs_15_ = bf16[1024,4,512]{2,1,0:T(4,128)(2,1)} custom-call(f32[4,6]{1,0:T(4,128)} %static_ref.9, bf16[1024,4,512]{2,1,0:T(4,128)(2,1)} %x_ref.11, f32[4,5248]{1,0:T(4,128)} %get-tuple-element.66.first_ref, f32[4,5376]{1,0:T(4,128)} %get-tuple-element.87.refs_0_.refs_1_.refs_2_, ...), custom_call_target="tpu_custom_call", output_to_operand_aliasing={{}: (18, {})} | custom-call | flops 629145600 | bytes 2883584 | tf_op jit(solution)/shard_map/final/pallas_call | solution.py:491
  241.2 7.0 %collective-permute-done.20.refs_14_ = bf16[256,512]{1,0:T(8,128)(2,1)S(1)} collective-permute-done((bf16[256,512]{1,0:T(8,128)(2,1)}, bf16[256,512]{1,0:T(8,128)(2,1)S(1)}, u32[]{:S(2)}, u32[]{:S(2)}) %collective-permute-start.20) | collective-permute-done | bytes 262176 | tf_op jit(solution)/shard_map/ppermute | solution.py:574
  248.2 0.7 copy-done.14
  248.9 3.5 %final.7 = bf16[1024,4,512]{2,1,0:T(4,128)(2,1)} custom-call(f32[4,6]{1,0:T(4,128)} %static_ref.9, bf16[1024,4,512]{2,1,0:T(4,128)(2,1)} %x_ref.11, f32[4,5248]{1,0:T(4,128)} %get-tuple-element.66.first_ref, f32[4,5376]{1,0:T(4,128)} %get-tuple-element.87.refs_0_.refs_1_.refs_2_, ...), custom_call_target="tpu_custom_call", output_to_operand_aliasing={{}: (18, {})} | custom-call | flops 629145600 | bytes 2883584 | tf_op jit(solution)/shard_map/final/pallas_call | solution.py:491
  (100 shorter events, 2.7 us)
Async XLA Ops:
  6.5 147.0 %all-gather.2.cloned.1.call-start = ((), (), s32[]{:S(2)}) async-start(), calls=%async_computation | async-start | bytes 5242880 | tf_op jit(solution)/shard_map/all_gather | solution.py:525
  6.7 22.3 %copy-start.25 = (s32[2]{0:T(128)S(1)}, s32[2]{0:T(128)}, u32[]{:S(2)}) copy-start(s32[2]{0:T(128)} %param.11) | copy-start | bytes 28
  6.7 24.2 %copy-start.24 = (s32[1024]{0:T(1024)S(1)}, s32[1024]{0:T(1024)}, u32[]{:S(2)}) copy-start(s32[1024]{0:T(1024)} %param.10) | copy-start | bytes 12292
  11.6 13.5 %copy-start.28 = (bf16[64,2560]{1,0:T(8,128)(2,1)S(1)}, bf16[64,2560]{1,0:T(8,128)(2,1)}, u32[]{:S(2)}) copy-start(bf16[64,2560]{1,0:T(8,128)(2,1)} %get-tuple-element.68) | copy-start | bytes 983044
  11.6 13.5 %copy-start.27 = (bf16[64,2560]{1,0:T(8,128)(2,1)S(1)}, bf16[64,2560]{1,0:T(8,128)(2,1)}, u32[]{:S(2)}) copy-start(bf16[64,2560]{1,0:T(8,128)(2,1)} %get-tuple-element.69) | copy-start | bytes 983044
  11.6 15.4 %copy-start.26 = (bf16[64,2560]{1,0:T(8,128)(2,1)S(1)}, bf16[64,2560]{1,0:T(8,128)(2,1)}, u32[]{:S(2)}) copy-start(bf16[64,2560]{1,0:T(8,128)(2,1)} %get-tuple-element.70) | copy-start | bytes 983044
  19.5 10.7 %collective-permute-start = (f32[4,5248]{1,0:T(4,128)}, f32[4,5248]{1,0:T(4,128)S(1)}, u32[]{:S(2)}, u32[]{:S(2)}) collective-permute-start(f32[4,5248]{1,0:T(4,128)} %get-tuple-element.65.own_ref), channel_id=1, source_target_pairs={{0,1},{1,2},{2,3},{3,0},{4,5},{5,6},{6,7},{7,4},{8,9},{9,10},{10,1... | collective-permute-start | bytes 251912 | tf_op jit(solution)/shard_map/ppermute | solution.py:31
  22.5 22.6 %collective-permute-start.1 = (f32[4,5248]{1,0:T(4,128)}, f32[4,5248]{1,0:T(4,128)S(1)}, u32[]{:S(2)}, u32[]{:S(2)}) collective-permute-start(f32[4,5248]{1,0:T(4,128)} %get-tuple-element.65.own_ref), channel_id=1, source_target_pairs={{0,2},{1,3},{2,0},{3,1},{4,6},{5,7},{6,4},{7,5},{8,10},{9,11},{10,... | collective-permute-start | bytes 251912 | tf_op jit(solution)/shard_map/ppermute | solution.py:31
  25.1 34.5 %collective-permute-start.3 = (bf16[64,2560]{1,0:T(8,128)(2,1)S(1)}, bf16[64,2560]{1,0:T(8,128)(2,1)S(1)}, u32[]{:S(2)}, u32[]{:S(2)}) collective-permute-start(bf16[64,2560]{1,0:T(8,128)(2,1)S(1)} %copy-done.28), channel_id=1, source_target_pairs={{0,1},{1,2},{2,3},{3,0},{4,5},{5,6},{6,7},{7,4},{8,9},{9,10},{10,1... | collective-permute-start | bytes 983048 | tf_op jit(solution)/shard_map/ppermute | solution.py:516
  25.1 34.5 %collective-permute-start.4 = (bf16[64,2560]{1,0:T(8,128)(2,1)S(1)}, bf16[64,2560]{1,0:T(8,128)(2,1)S(1)}, u32[]{:S(2)}, u32[]{:S(2)}) collective-permute-start(bf16[64,2560]{1,0:T(8,128)(2,1)S(1)} %copy-done.27), channel_id=1, source_target_pairs={{0,2},{1,3},{2,0},{3,1},{4,6},{5,7},{6,4},{7,5},{8,10},{9,11},{10,... | collective-permute-start | bytes 983048 | tf_op jit(solution)/shard_map/ppermute | solution.py:516
  27.0 32.7 %collective-permute-start.5 = (bf16[64,2560]{1,0:T(8,128)(2,1)S(1)}, bf16[64,2560]{1,0:T(8,128)(2,1)S(1)}, u32[]{:S(2)}, u32[]{:S(2)}) collective-permute-start(bf16[64,2560]{1,0:T(8,128)(2,1)S(1)} %copy-done.26), channel_id=1, source_target_pairs={{0,3},{1,0},{2,1},{3,2},{4,7},{5,4},{6,5},{7,6},{8,11},{9,8},{10,9... | collective-permute-start | bytes 983048 | tf_op jit(solution)/shard_map/ppermute | solution.py:516
  30.2 23.2 %copy-start.21 = (f32[4,5248]{1,0:T(4,128)}, f32[4,5248]{1,0:T(4,128)S(1)}, u32[]{:S(2)}) copy-start(f32[4,5248]{1,0:T(4,128)S(1)} %collective-permute-done.a_ref) | copy-start | bytes 251908
  30.2 23.2 %collective-permute-start.2 = (f32[4,5248]{1,0:T(4,128)}, f32[4,5248]{1,0:T(4,128)S(1)}, u32[]{:S(2)}, u32[]{:S(2)}) collective-permute-start(f32[4,5248]{1,0:T(4,128)} %get-tuple-element.65.own_ref), channel_id=1, source_target_pairs={{0,3},{1,0},{2,1},{3,2},{4,7},{5,4},{6,5},{7,6},{8,11},{9,8},{10,9... | collective-permute-start | bytes 251912 | tf_op jit(solution)/shard_map/ppermute | solution.py:31
  45.1 8.4 %copy-start.22 = (f32[4,5248]{1,0:T(4,128)}, f32[4,5248]{1,0:T(4,128)S(1)}, u32[]{:S(2)}) copy-start(f32[4,5248]{1,0:T(4,128)S(1)} %collective-permute-done.1.b_ref) | copy-start | bytes 251908
  45.1 14.5 %collective-permute-start.6 = (s32[512]{0:T(512)S(1)}, s32[512]{0:T(512)S(1)}, u32[]{:S(2)}, u32[]{:S(2)}) collective-permute-start(s32[512]{0:T(512)S(1)} %get-tuple-element.124), channel_id=1, source_target_pairs={{0,4},{4,8},{8,12},{12,16},{16,20},{20,24},{24,28},{1,5},{5,9},{9,... | collective-permute-start | bytes 6152 | tf_op jit(solution)/shard_map/ppermute | solution.py:25
  53.5 0.6 copy-start.23
  59.6 68.5 %copy-start.2 = (f32[4,5376]{1,0:T(4,128)S(1)}, f32[4,5376]{1,0:T(4,128)}, u32[]{:S(2)}) copy-start(f32[4,5376]{1,0:T(4,128)} %get-tuple-element.87.refs_0_.refs_1_.refs_2_) | copy-start | bytes 258052
  59.6 0.8 copy-start.6
  59.6 0.8 copy-start.7
  59.7 0.9 copy-start.8
  63.0 31.9 %collective-permute-start.8 = (bf16[256,2560]{1,0:T(8,128)(2,1)}, bf16[256,2560]{1,0:T(8,128)(2,1)S(1)}, u32[]{:S(2)}, u32[]{:S(2)}) collective-permute-start(bf16[256,2560]{1,0:T(8,128)(2,1)} %assemble.1.refs_0_), channel_id=1, source_target_pairs={{0,8},{4,12},{8,0},{12,4},{16,24},{20,28},{24,16},{28,20},{1,9},{5... | collective-permute-start | bytes 3932168 | tf_op jit(solution)/shard_map/ppermute | solution.py:115
  64.4 58.4 %collective-permute-start.10 = (bf16[256,2560]{1,0:T(8,128)(2,1)}, bf16[256,2560]{1,0:T(8,128)(2,1)}, u32[]{:S(2)}, u32[]{:S(2)}) collective-permute-start(bf16[256,2560]{1,0:T(8,128)(2,1)} %assemble.1.refs_0_), channel_id=1, source_target_pairs={{0,16},{4,20},{8,24},{12,28},{16,0},{20,4},{24,8},{28,12},{1,17},{... | collective-permute-start | bytes 3932168 | tf_op jit(solution)/shard_map/ppermute | solution.py:115
  66.0 56.9 %collective-permute-start.12 = (bf16[256,2560]{1,0:T(8,128)(2,1)}, bf16[256,2560]{1,0:T(8,128)(2,1)}, u32[]{:S(2)}, u32[]{:S(2)}) collective-permute-start(bf16[256,2560]{1,0:T(8,128)(2,1)} %assemble.1.refs_0_), channel_id=1, source_target_pairs={{0,24},{4,28},{8,16},{12,20},{16,8},{20,12},{24,0},{28,4},{1,25},{... | collective-permute-start | bytes 3932168 | tf_op jit(solution)/shard_map/ppermute | solution.py:115
  66.5 61.1 %collective-permute-start.7 = (bf16[256,2560]{1,0:T(8,128)(2,1)}, bf16[256,2560]{1,0:T(8,128)(2,1)}, u32[]{:S(2)}, u32[]{:S(2)}) collective-permute-start(bf16[256,2560]{1,0:T(8,128)(2,1)} %assemble.1.refs_0_), channel_id=1, source_target_pairs={{0,4},{4,0},{8,12},{12,8},{16,20},{20,16},{24,28},{28,24},{1,5},{5... | collective-permute-start | bytes 3932168 | tf_op jit(solution)/shard_map/ppermute | solution.py:115
  94.9 58.6 %copy-start.1 = (bf16[256,2560]{1,0:T(8,128)(2,1)}, bf16[256,2560]{1,0:T(8,128)(2,1)S(1)}, u32[]{:S(2)}) copy-start(bf16[256,2560]{1,0:T(8,128)(2,1)S(1)} %collective-permute-done.8.refs_2_) | copy-start | bytes 3932164
  94.9 32.7 %collective-permute-start.9 = (bf16[256,2560]{1,0:T(8,128)(2,1)S(1)}, bf16[256,2560]{1,0:T(8,128)(2,1)}, u32[]{:S(2)}, u32[]{:S(2)}) collective-permute-start(bf16[256,2560]{1,0:T(8,128)(2,1)S(1)} %collective-permute-done.8.refs_2_), channel_id=1, source_target_pairs={{0,4},{4,0},{8,12},{12,8},{16,20},{20,16},{24,28},{28,24},{1,5},{5... | collective-permute-start | bytes 3932168 | tf_op jit(solution)/shard_map/ppermute | solution.py:115
  122.9 4.7 %collective-permute-start.11 = (bf16[256,2560]{1,0:T(8,128)(2,1)}, bf16[256,2560]{1,0:T(8,128)(2,1)}, u32[]{:S(2)}, u32[]{:S(2)}) collective-permute-start(bf16[256,2560]{1,0:T(8,128)(2,1)} %collective-permute-done.10.refs_4_), channel_id=1, source_target_pairs={{0,4},{4,0},{8,12},{12,8},{16,20},{20,16},{24,28},{28,24},{1,5},{5... | collective-permute-start | bytes 3932168 | tf_op jit(solution)/shard_map/ppermute | solution.py:115
  122.9 5.2 %collective-permute-start.13 = (bf16[256,2560]{1,0:T(8,128)(2,1)}, bf16[256,2560]{1,0:T(8,128)(2,1)}, u32[]{:S(2)}, u32[]{:S(2)}) collective-permute-start(bf16[256,2560]{1,0:T(8,128)(2,1)} %collective-permute-done.12.refs_6_), channel_id=1, source_target_pairs={{0,4},{4,0},{8,12},{12,8},{16,20},{20,16},{24,28},{28,24},{1,5},{5... | collective-permute-start | bytes 3932168 | tf_op jit(solution)/shard_map/ppermute | solution.py:115
  128.1 13.0 %collective-permute-start.14 = (f32[4,5376]{1,0:T(4,128)S(1)}, f32[4,5376]{1,0:T(4,128)S(1)}, u32[]{:S(2)}, u32[]{:S(2)}) collective-permute-start(f32[4,5376]{1,0:T(4,128)S(1)} %copy-done.2), channel_id=1, source_target_pairs={{0,1},{1,2},{2,3},{3,0},{4,5},{5,6},{6,7},{7,4},{8,9},{9,10},{10,1... | collective-permute-start | bytes 258056 | tf_op jit(solution)/shard_map/ppermute | solution.py:31
  136.4 10.4 %collective-permute-start.15 = (f32[4,5376]{1,0:T(4,128)S(1)}, f32[4,5376]{1,0:T(4,128)S(1)}, u32[]{:S(2)}, u32[]{:S(2)}) collective-permute-start(f32[4,5376]{1,0:T(4,128)S(1)} %copy-done.2), channel_id=1, source_target_pairs={{0,2},{1,3},{2,0},{3,1},{4,6},{5,7},{6,4},{7,5},{8,10},{9,11},{10,... | collective-permute-start | bytes 258056 | tf_op jit(solution)/shard_map/ppermute | solution.py:31
  136.4 11.2 %collective-permute-start.16 = (f32[4,5376]{1,0:T(4,128)S(1)}, f32[4,5376]{1,0:T(4,128)S(1)}, u32[]{:S(2)}, u32[]{:S(2)}) collective-permute-start(f32[4,5376]{1,0:T(4,128)S(1)} %copy-done.2), channel_id=1, source_target_pairs={{0,3},{1,0},{2,1},{3,2},{4,7},{5,4},{6,5},{7,6},{8,11},{9,8},{10,9... | collective-permute-start | bytes 258056 | tf_op jit(solution)/shard_map/ppermute | solution.py:31
  141.2 25.4 %copy-start.3 = (f32[4,5376]{1,0:T(4,128)}, f32[4,5376]{1,0:T(4,128)S(1)}, u32[]{:S(2)}) copy-start(f32[4,5376]{1,0:T(4,128)S(1)} %collective-permute-done.14.refs_3_.refs_4_.refs_5_) | copy-start | bytes 258052
  146.8 19.7 %copy-start.4 = (f32[4,5376]{1,0:T(4,128)}, f32[4,5376]{1,0:T(4,128)S(1)}, u32[]{:S(2)}) copy-start(f32[4,5376]{1,0:T(4,128)S(1)} %collective-permute-done.15.refs_6_.refs_7_.refs_8_) | copy-start | bytes 258052
  147.6 18.9 %copy-start.5 = (f32[4,5376]{1,0:T(4,128)}, f32[4,5376]{1,0:T(4,128)S(1)}, u32[]{:S(2)}) copy-start(f32[4,5376]{1,0:T(4,128)S(1)} %collective-permute-done.16.refs_9_.refs_10_.refs_11_) | copy-start | bytes 258052
  166.5 13.9 %collective-permute-start.17 = (bf16[2,512,512]{2,1,0:T(8,128)(2,1)}, bf16[2,512,512]{2,1,0:T(8,128)(2,1)S(1)}, u32[]{:S(2)}, u32[]{:S(2)}) collective-permute-start(bf16[2,512,512]{2,1,0:T(8,128)(2,1)} %get-tuple-element.102), channel_id=1, source_target_pairs={{0,4},{4,8},{8,12},{12,16},{16,20},{20,24},{24,28},{1,5},{5,9},{9,... | collective-permute-start | bytes 3145736 | tf_op jit(solution)/shard_map/ppermute | solution.py:25
  174.3 11.1 %collective-permute-start.24 = (bf16[256,512]{1,0:T(8,128)(2,1)}, bf16[256,512]{1,0:T(8,128)(2,1)S(1)}, u32[]{:S(2)}, u32[]{:S(2)}) collective-permute-start(bf16[256,512]{1,0:T(8,128)(2,1)} %attend.6.own_ref), channel_id=1, source_target_pairs={{0,1},{1,0},{2,3},{3,2},{4,5},{5,4},{6,7},{7,6},{8,9},{9,8},{10,11... | collective-permute-start | bytes 786440 | tf_op jit(solution)/shard_map/ppermute | solution.py:115
  178.4 20.4 %collective-permute-start.27 = (bf16[256,512]{1,0:T(8,128)(2,1)}, bf16[256,512]{1,0:T(8,128)(2,1)S(1)}, u32[]{:S(2)}, u32[]{:S(2)}) collective-permute-start(bf16[256,512]{1,0:T(8,128)(2,1)} %attend.7.own_ref), channel_id=1, source_target_pairs={{0,1},{1,0},{2,3},{3,2},{4,5},{5,4},{6,7},{7,6},{8,9},{9,8},{10,11... | collective-permute-start | bytes 786440 | tf_op jit(solution)/shard_map/ppermute | solution.py:115
  180.4 1.0 copy-start
  185.4 20.7 %collective-permute-start.21 = (bf16[256,512]{1,0:T(8,128)(2,1)}, bf16[256,512]{1,0:T(8,128)(2,1)S(1)}, u32[]{:S(2)}, u32[]{:S(2)}) collective-permute-start(bf16[256,512]{1,0:T(8,128)(2,1)} %attend.5.own_ref), channel_id=1, source_target_pairs={{0,1},{1,0},{2,3},{3,2},{4,5},{5,4},{6,7},{7,6},{8,9},{9,8},{10,11... | collective-permute-start | bytes 786440 | tf_op jit(solution)/shard_map/ppermute | solution.py:115
  185.4 0.7 copy-start.20
  190.8 21.3 %collective-permute-start.25 = (bf16[256,512]{1,0:T(8,128)(2,1)}, bf16[256,512]{1,0:T(8,128)(2,1)S(1)}, u32[]{:S(2)}, u32[]{:S(2)}) collective-permute-start(bf16[256,512]{1,0:T(8,128)(2,1)} %get-tuple-element.110), channel_id=1, source_target_pairs={{1,2},{2,1},{5,6},{6,5},{9,10},{10,9},{13,14},{14,13},{17,18},{18,... | collective-permute-start | bytes 786440 | tf_op jit(solution)/shard_map/ppermute | solution.py:573
  195.5 10.6 %copy-start.29 = (bf16[256,512]{1,0:T(8,128)(2,1)S(1)}, bf16[256,512]{1,0:T(8,128)(2,1)}, u32[]{:S(2)}) copy-start(bf16[256,512]{1,0:T(8,128)(2,1)} %get-tuple-element.111) | copy-start | bytes 786436
  195.5 17.3 %collective-permute-start.18 = (bf16[256,512]{1,0:T(8,128)(2,1)}, bf16[256,512]{1,0:T(8,128)(2,1)S(1)}, u32[]{:S(2)}, u32[]{:S(2)}) collective-permute-start(bf16[256,512]{1,0:T(8,128)(2,1)} %attend.4.own_ref), channel_id=1, source_target_pairs={{0,1},{1,0},{2,3},{3,2},{4,5},{5,4},{6,7},{7,6},{8,9},{9,8},{10,11... | collective-permute-start | bytes 786440 | tf_op jit(solution)/shard_map/ppermute | solution.py:115
  198.8 0.7 copy-start.19
  204.1 14.9 %collective-permute-start.28 = (bf16[256,512]{1,0:T(8,128)(2,1)}, bf16[256,512]{1,0:T(8,128)(2,1)S(1)}, u32[]{:S(2)}, u32[]{:S(2)}) collective-permute-start(bf16[256,512]{1,0:T(8,128)(2,1)} %get-tuple-element.113), channel_id=1, source_target_pairs={{1,2},{2,1},{5,6},{6,5},{9,10},{10,9},{13,14},{14,13},{17,18},{18,... | collective-permute-start | bytes 786440 | tf_op jit(solution)/shard_map/ppermute | solution.py:573
  204.8 15.3 %collective-permute-start.29 = (bf16[256,512]{1,0:T(8,128)(2,1)}, bf16[256,512]{1,0:T(8,128)(2,1)S(1)}, u32[]{:S(2)}, u32[]{:S(2)}) collective-permute-start(bf16[256,512]{1,0:T(8,128)(2,1)} %get-tuple-element.114), channel_id=1, source_target_pairs={{1,3},{2,0},{5,7},{6,4},{9,11},{10,8},{13,15},{14,12},{17,19},{18,... | collective-permute-start | bytes 786440 | tf_op jit(solution)/shard_map/ppermute | solution.py:574
  206.1 1.3 copy-start.18
  206.1 19.6 %collective-permute-start.26 = (bf16[256,512]{1,0:T(8,128)(2,1)S(1)}, bf16[256,512]{1,0:T(8,128)(2,1)S(1)}, u32[]{:S(2)}, u32[]{:S(2)}) collective-permute-start(bf16[256,512]{1,0:T(8,128)(2,1)S(1)} %copy-done.29), channel_id=1, source_target_pairs={{1,3},{2,0},{5,7},{6,4},{9,11},{10,8},{13,15},{14,12},{17,19},{18,... | collective-permute-start | bytes 786440 | tf_op jit(solution)/shard_map/ppermute | solution.py:574
  212.1 6.9 %copy-start.9 = (bf16[256,512]{1,0:T(8,128)(2,1)}, bf16[256,512]{1,0:T(8,128)(2,1)S(1)}, u32[]{:S(2)}) copy-start(bf16[256,512]{1,0:T(8,128)(2,1)S(1)} %collective-permute-done.25.refs_13_) | copy-start | bytes 786436
  212.1 17.9 %collective-permute-start.22 = (bf16[256,512]{1,0:T(8,128)(2,1)}, bf16[256,512]{1,0:T(8,128)(2,1)S(1)}, u32[]{:S(2)}, u32[]{:S(2)}) collective-permute-start(bf16[256,512]{1,0:T(8,128)(2,1)} %get-tuple-element.107), channel_id=1, source_target_pairs={{1,2},{2,1},{5,6},{6,5},{9,10},{10,9},{13,14},{14,13},{17,18},{18,... | collective-permute-start | bytes 786440 | tf_op jit(solution)/shard_map/ppermute | solution.py:573
  212.8 1.5 copy-start.17
  212.8 24.2 %collective-permute-start.23 = (bf16[256,512]{1,0:T(8,128)(2,1)}, bf16[256,512]{1,0:T(8,128)(2,1)S(1)}, u32[]{:S(2)}, u32[]{:S(2)}) collective-permute-start(bf16[256,512]{1,0:T(8,128)(2,1)} %get-tuple-element.108), channel_id=1, source_target_pairs={{1,3},{2,0},{5,7},{6,4},{9,11},{10,8},{13,15},{14,12},{17,19},{18,... | collective-permute-start | bytes 786440 | tf_op jit(solution)/shard_map/ppermute | solution.py:574
  219.0 2.4 copy-start.15
  219.0 22.2 %collective-permute-start.19 = (bf16[256,512]{1,0:T(8,128)(2,1)}, bf16[256,512]{1,0:T(8,128)(2,1)S(1)}, u32[]{:S(2)}, u32[]{:S(2)}) collective-permute-start(bf16[256,512]{1,0:T(8,128)(2,1)} %get-tuple-element.104), channel_id=1, source_target_pairs={{1,2},{2,1},{5,6},{6,5},{9,10},{10,9},{13,14},{14,13},{17,18},{18,... | collective-permute-start | bytes 786440 | tf_op jit(solution)/shard_map/ppermute | solution.py:573
  220.1 1.3 copy-start.16
  220.1 28.1 %collective-permute-start.20 = (bf16[256,512]{1,0:T(8,128)(2,1)}, bf16[256,512]{1,0:T(8,128)(2,1)S(1)}, u32[]{:S(2)}, u32[]{:S(2)}) collective-permute-start(bf16[256,512]{1,0:T(8,128)(2,1)} %get-tuple-element.105), channel_id=1, source_target_pairs={{1,3},{2,0},{5,7},{6,4},{9,11},{10,8},{13,15},{14,12},{17,19},{18,... | collective-permute-start | bytes 786440 | tf_op jit(solution)/shard_map/ppermute | solution.py:574
  225.7 0.7 copy-start.10
  230.0 7.0 %copy-start.11 = (bf16[256,512]{1,0:T(8,128)(2,1)}, bf16[256,512]{1,0:T(8,128)(2,1)S(1)}, u32[]{:S(2)}) copy-start(bf16[256,512]{1,0:T(8,128)(2,1)S(1)} %collective-permute-done.22.refs_13_) | copy-start | bytes 786436
  237.0 0.7 copy-start.12
  241.2 7.0 %copy-start.13 = (bf16[256,512]{1,0:T(8,128)(2,1)}, bf16[256,512]{1,0:T(8,128)(2,1)S(1)}, u32[]{:S(2)}) copy-start(bf16[256,512]{1,0:T(8,128)(2,1)S(1)} %collective-permute-done.19.refs_13_) | copy-start | bytes 786436
  248.2 0.7 copy-start.14
Sparse Core Ops, SparseCore 0:
  59.8 93.6 all-gather.1

commit v10 on v7

--- a/solution.py
+++ b/solution.py
@@ -288,11 +288,12 @@
     def _():
         out_ref[0] = total.astype(BF)
 
-    halo_ref[0] = out_ref[0, -BLOCK:, :]
+    halo_ref[0] = out_ref[0, -halo_ref.shape[1] :, :]
 
 
 def qkv_columns(ring, rows, pieces, cosine, sine):
     servers, tokens, width = rows.shape
+    kept = min(BLOCK, tokens)
     table = pl.BlockSpec((tokens, HEAD_DIM), lambda j: (0, 0))
     return pl.pallas_call(
         qkv_kernel,
@@ -306,11 +307,11 @@
         + [pl.BlockSpec((pieces[0].shape[0], width), lambda j: (0, j))] * len(pieces),
         out_specs=[
             pl.BlockSpec((1, tokens, width), lambda j: (j, 0, 0)),
-            pl.BlockSpec((1, BLOCK, width), lambda j: (jnp.maximum(j - 1, 0), 0, 0)),
+            pl.BlockSpec((1, kept, width), lambda j: (jnp.maximum(j - 1, 0), 0, 0)),
         ],
         out_shape=[
             jax.ShapeDtypeStruct((3, tokens, width), BF),
-            jax.ShapeDtypeStruct((2, BLOCK, width), BF),
+            jax.ShapeDtypeStruct((2, kept, width), BF),
         ],
         cost_estimate=cost(2 * tokens * D * 3 * width, D * 6 * width + tokens * D * 5),
         compiler_params=params(),
@@ -511,12 +512,14 @@
         parts[step] = lax.ppermute(
             parts[step], "mp", [(at, (at + step) % group_size) for at in range(group_size)]
         )
-    sums_all, normed = mix(hc_static, streams, sums, 0, tokens_local)
-    parts, normed = lax.optimization_barrier((parts, normed))
-    rows = gathered(normed)
+    sums_all, normed_late = mix(hc_static, streams, sums, CHUNK, tokens_local - CHUNK)
+    _, normed_first = mix(hc_static, streams, sums, 0, CHUNK)
+    parts, normed_late, normed_first = lax.optimization_barrier((parts, normed_late, normed_first))
+    rows_late = gathered(normed_late)
+    rows_first = gathered(normed_first)
 
     pieces = weight_pieces(assemble(place, parts))
-    rows, pieces = lax.optimization_barrier((rows, pieces))
+    rows_late, pieces = lax.optimization_barrier((rows_late, pieces))
 
     halo = passed_along(segment_ids[-BLOCK:], "blk", 1)
     halo = jnp.where(lax.axis_index("blk") == 0, -1, halo)
@@ -541,20 +544,28 @@
     key_segments = jnp.stack(windows)[:, None, :]
     query_segments = segment_ids[:, None]
 
-    qkv, halo_rows = qkv_columns(ring, rows, pieces, cosine, sine)
+    qkv_late, halo_rows = qkv_columns(ring, rows_late, pieces, cosine[CHUNK:], sine[CHUNK:])
     halo_rows = passed_along(halo_rows, "blk", 1)
 
-    def projected(own):
-        other = swapped(own, "mp", 1)
+    def projected(own, other):
         return project(place, ring, own, other, pieces, group_size)
 
     last = tokens_local // CHUNK - 1
-    chunks = [(halo_rows, 0, 0), (halo_rows, 0, 1)] + [(qkv, 1, at) for at in range(last + 1)]
-    parts = {}
-    for chunk in reversed(range(last + 1)):
-        window = chunks[chunk : chunk + 3]
-        own = attend((qkv, chunk), window, query_segments, key_segments, chunk)
-        parts[chunk] = projected(own)
+    late_chunks = [(qkv_late, 1, at) for at in range(last)]
+
+    def attended(chunk, window):
+        source, _, at = window[-1]
+        return attend((source, at), window, query_segments, key_segments, chunk)
+
+    own = attended(last, late_chunks[-3:])
+    both = (own, swapped(own, "mp", 1))
+    rows_first, both = lax.optimization_barrier((rows_first, both))
+    parts = {last: projected(*both)}
+    qkv_first, _ = qkv_columns(ring, rows_first, pieces, cosine[:CHUNK], sine[:CHUNK])
+    chunks = [(halo_rows, 0, 0), (halo_rows, 0, 1), (qkv_first, 1, 0)] + late_chunks
+    for chunk in reversed(range(last)):
+        own = attended(chunk, chunks[chunk : chunk + 3])
+        parts[chunk] = projected(own, swapped(own, "mp", 1))
 
     result = None
     for chunk in reversed(range(last + 1)):

time: 252 us -> 251 us (level)
  waiting for transfers between devices: 106 us -> 91.6 us
  starting transfers between devices: 34.8 us -> 41.7 us
  Pallas kernels: 80.8 us -> 87 us
    all_gather x1 -> x2, waiting for transfers between devices: 14.8 us -> 4.54 us  [gathered(): rows = lax.all_gather(normed, 'mp', axis=0, tiled=True)]
    ppermute x11, starting transfers between devices: 9.38 us -> 18.4 us  [swapped(): lax.ppermute(value, axis, [(source, source ^ mask) for source in range(co...]
    pallas_call x1 -> x2, Pallas kernels: 13 us -> 17.1 us  [qkv_columns(): pl.pallas_call(qkv_kernel, grid=(3,), in_specs=[pl.BlockSpec(memory_space...]
    ppermute x4, waiting for transfers between devices: 15.5 us -> 11.6 us  [body(): outer = lax.ppermute(outer, 'mp', [(1, 3), (2, 0)])]
    ppermute x3, waiting for transfers between devices: 4.98 us -> 8.51 us  [from_others(): lax.ppermute(value, axis, [(source, (source + step) % count) for source i...]
    pallas_call x1 -> x2, Pallas kernels: 5.64 us -> 7.71 us  [mix(): pl.pallas_call(functools.partial(mix_kernel, start), grid=(tokens // CHUN...]
    unnamed x46 -> x50, local copies, waits for them, and re-layouts: 5.41 us -> 4.66 us
  transfers between devices with their start and end apart: 28 -> 29, of which waited for: 11 -> 10; matrix products, arithmetic and copies ran while one was open for 3% -> 3% of each run, Pallas kernels for 23% -> 31%
where the time goes in v10:
time: 251 us; the launch traced here: 250 us
  waiting for transfers between devices  91.6 us (36%)
  Pallas kernels  87 us (35%)
  starting transfers between devices  41.7 us (17%)
  between operations  15.2 us (6%)
  local copies, waits for them, and re-layouts  7.13 us (3%)
  other arithmetic  6.97 us (3%)
    ppermute x11, waiting for transfers between devices, swapped(): lax.ppermute(value, axis, [(source, source ^ mask) for source in range(co...  54.8 us
    pallas_call x4, Pallas kernels, project(): pl.pallas_call(project_kernel, grid=(1,), in_specs=[pl.BlockSpec(memory_s...  18.7 us
    ppermute x11, starting transfers between devices, swapped(): lax.ppermute(value, axis, [(source, source ^ mask) for source in range(co...  18.4 us
    pallas_call x2, Pallas kernels, qkv_columns(): pl.pallas_call(qkv_kernel, grid=(3,), in_specs=[pl.BlockSpec(memory_space...  17.1 us
    pallas_call x4, Pallas kernels, attend(): pl.pallas_call(attend_kernel, grid=(1,), in_specs=[pl.BlockSpec(block, la...  16.2 us
    pallas_call x4, Pallas kernels, final(): pl.pallas_call(final_kernel, grid=(tokens // STEP,), in_specs=specs, out_...  13.6 us
    ppermute x3, waiting for transfers between devices, body(): lax.ppermute(parts[step], 'mp', [(at, (at + step) % group_size) for at in...  12.1 us
    ppermute x4, waiting for transfers between devices, body(): outer = lax.ppermute(outer, 'mp', [(1, 3), (2, 0)])  11.6 us
  transfers between devices with their start and end apart: 29, of which 10 were waited for; matrix products, arithmetic and copies ran while one was open for 3% of the time, Pallas kernels for 31%

profile of v10, /device:TPU:0, one launch (start us, length us, event | category | flops | bytes accessed | tf_op | source)
XLA Modules:
  0.0 249.6 jit_solution(639162843910543566)
XLA Ops:
  6.7 1.4 maximum_maximum_fusion.proj_ref
  8.1 6.4 %stats.1.own_ref = f32[8,5248]{1,0:T(8,128)} custom-call(bf16[1024,4,512]{2,1,0:T(4,128)(2,1)} %x_ref.13, f32[8,512]{1,0:T(8,128)} %maximum_maximum_fusion.proj_ref), custom_call_target="tpu_custom_call" | custom-call | flops 1258291200 | bytes 4194304 | tf_op jit(solution)/shard_map/stats/pallas_call | solution.py:171
  14.4 5.0 %collective-permute-start.2 = (f32[8,5248]{1,0:T(8,128)}, f32[8,5248]{1,0:T(8,128)S(1)}, u32[]{:S(2)}, u32[]{:S(2)}) collective-permute-start(f32[8,5248]{1,0:T(8,128)} %stats.1.own_ref), channel_id=1, source_target_pairs={{0,3},{1,0},{2,1},{3,2},{4,7},{5,4},{6,5},{7,6},{8,11},{9,8},{10,9... | collective-permute-start | bytes 503816 | tf_op jit(solution)/shard_map/ppermute | solution.py:31
  19.5 1.0 collective-permute-start
  20.5 4.9 %regroup.1 = (bf16[64,2560]{1,0:T(8,128)(2,1)}, bf16[64,2560]{1,0:T(8,128)(2,1)}, bf16[64,2560]{1,0:T(8,128)(2,1)}, bf16[64,2560]{1,0:T(8,128)(2,1)}) custom-call(s32[1]{0:T(128)} %bitcast.1.place_ref, f32[64,4,2048]{2,1,0:T(4,128)} %master_ref.1), custom_call_target="tpu_custom_call" | custom-call | bytes 3407872 | tf_op jit(solution)/shard_map/regroup/pallas_call | solution.py:79
  25.4 8.5 %collective-permute-done.1.b_ref = f32[8,5248]{1,0:T(8,128)S(1)} collective-permute-done((f32[8,5248]{1,0:T(8,128)}, f32[8,5248]{1,0:T(8,128)S(1)}, u32[]{:S(2)}, u32[]{:S(2)}) %collective-permute-start.1) | collective-permute-done | bytes 167968 | tf_op jit(solution)/shard_map/ppermute | solution.py:31
  33.9 1.0 collective-permute-start.3
  34.9 1.8 collective-permute-start.4
  36.8 2.9 %collective-permute-start.5 = (bf16[64,2560]{1,0:T(8,128)(2,1)}, bf16[64,2560]{1,0:T(8,128)(2,1)S(1)}, u32[]{:S(2)}, u32[]{:S(2)}) collective-permute-start(bf16[64,2560]{1,0:T(8,128)(2,1)} %get-tuple-element.65), channel_id=1, source_target_pairs={{0,3},{1,0},{2,1},{3,2},{4,7},{5,4},{6,5},{7,6},{8,11},{9,8},{10,9... | collective-permute-start | bytes 983048 | tf_op jit(solution)/shard_map/ppermute | solution.py:512
  39.7 2.9 %mix.3 = (f32[8,5248]{1,0:T(8,128)}, bf16[256,512]{1,0:T(8,128)(2,1)}) custom-call(f32[4,6]{1,0:T(4,128)} %static_ref.11, bf16[1024,4,512]{2,1,0:T(4,128)(2,1)} %x_ref.13, f32[8,5248]{1,0:T(8,128)} %stats.1.own_ref, f32[8,5248]{1,0:T(8,128)} %copy-done.6, f32[8,5248]{1,0:T(8,128)} %copy-done.5, f32[8,5248]{1,0:T(8,128)} %copy-done.4), custom_call_target="tpu_custom_call" | custom-call | flops 209715200 | bytes 1310720 | tf_op jit(solution)/shard_map/mix/pallas_call | solution.py:242
  42.5 4.9 %mix.2 = (f32[8,5248]{1,0:T(8,128)}, bf16[768,512]{1,0:T(8,128)(2,1)}) custom-call(f32[4,6]{1,0:T(4,128)} %static_ref.11, bf16[1024,4,512]{2,1,0:T(4,128)(2,1)} %x_ref.13, f32[8,5248]{1,0:T(8,128)} %stats.1.own_ref, f32[8,5248]{1,0:T(8,128)} %copy-done.6, f32[8,5248]{1,0:T(8,128)} %copy-done.5, f32[8,5248]{1,0:T(8,128)} %copy-done.4), custom_call_target="tpu_custom_call" | custom-call | flops 629145600 | bytes 3932160 | tf_op jit(solution)/shard_map/mix/pallas_call | solution.py:242
  47.4 12.1 %collective-permute-done.4.refs_2_ = bf16[64,2560]{1,0:T(8,128)(2,1)S(1)} collective-permute-done((bf16[64,2560]{1,0:T(8,128)(2,1)}, bf16[64,2560]{1,0:T(8,128)(2,1)S(1)}, u32[]{:S(2)}, u32[]{:S(2)}) %collective-permute-start.4) | collective-permute-done | bytes 327712 | tf_op jit(solution)/shard_map/ppermute | solution.py:512
  59.6 0.6 copy-done.8
  60.3 2.4 assemble.1.refs_0_
  62.8 2.4 collective-permute-start.11
  65.7 0.5 collective-permute-start.7
  66.3 0.7 fusion.7
  67.7 1.3 collective-permute-start.13
  69.0 2.3 collective-permute-start.6
  71.2 24.4 %collective-permute-done.11.refs_6_ = bf16[256,2560]{1,0:T(8,128)(2,1)S(1)} collective-permute-done((bf16[256,2560]{1,0:T(8,128)(2,1)}, bf16[256,2560]{1,0:T(8,128)(2,1)S(1)}, u32[]{:S(2)}, u32[]{:S(2)}) %collective-permute-start.11) | collective-permute-done | bytes 1310752 | tf_op jit(solution)/shard_map/ppermute | solution.py:115
  95.7 25.6 %collective-permute-done.9.refs_4_ = bf16[256,2560]{1,0:T(8,128)(2,1)} collective-permute-done((bf16[256,2560]{1,0:T(8,128)(2,1)}, bf16[256,2560]{1,0:T(8,128)(2,1)}, u32[]{:S(2)}, u32[]{:S(2)}) %collective-permute-start.9) | collective-permute-done | bytes 1310752 | tf_op jit(solution)/shard_map/ppermute | solution.py:115
  122.6 1.6 convert_reduce_fusion
  124.2 1.9 multiply_sine_fusion
  126.1 1.2 fusion.1
  127.3 1.8 all-gather.5.cloned.1.call-done
  129.1 10.6 %qkv.2 = (bf16[3,768,512]{2,1,0:T(8,128)(2,1)}, bf16[2,512,512]{2,1,0:T(8,128)(2,1)}) custom-call(s32[1]{0:T(128)} %bitcast.2.ring_ref, bf16[4,768,512]{2,1,0:T(8,128)(2,1)} %bitcast.13, f32[768,128]{1,0:T(8,128)} %get-tuple-element.116.cosine_ref, f32[768,128]{1,0:T(8,128)} %get-tuple-element.115.sine_ref, bf16[256,2560]{1,0:T(8,128)(2,1)} %assemble.1.refs_0_, ...), custom_call_target="tpu_custom_call" | custom-call | flops 4831838208 | bytes 14155776 | tf_op jit(solution)/shard_map/qkv/pallas_call | solution.py:298
  139.7 2.0 collective-permute-start.15
  141.7 1.0 copy.14.qseg_ref
  142.8 0.6 broadcast_in_dim.29.kseg_ref
  143.4 4.1 %attend.4.own_ref = bf16[256,512]{1,0:T(8,128)(2,1)} custom-call(bf16[3,768,512]{2,1,0:T(8,128)(2,1)} %get-tuple-element.83.q_ref.k0.k1.k2.v0.v1.v2, bf16[3,768,512]{2,1,0:T(8,128)(2,1)} %get-tuple-element.83.q_ref.k0.k1.k2.v0.v1.v2, bf16[3,768,512]{2,1,0:T(8,128)(2,1)} %get-tuple-element.83.q_ref.k0.k1.k2.v0.v1.v2, ...), custom_call_target="tpu_custom_call" | custom-call | flops 402653184 | bytes 2097152 | tf_op jit(solution)/shard_map/attend/pallas_call | solution.py:352
  147.5 6.1 %collective-permute-start.14 = (bf16[256,512]{1,0:T(8,128)(2,1)}, bf16[256,512]{1,0:T(8,128)(2,1)S(1)}, u32[]{:S(2)}, u32[]{:S(2)}) collective-permute-start(bf16[256,512]{1,0:T(8,128)(2,1)} %attend.4.own_ref), channel_id=1, source_target_pairs={{0,1},{1,0},{2,3},{3,2},{4,5},{5,4},{6,7},{7,6},{8,9},{9,8},{10,11... | collective-permute-start | bytes 786440 | tf_op jit(solution)/shard_map/ppermute | solution.py:115
  153.6 0.9 pad_maximum_fusion
  154.4 2.7 %all-gather.3.cloned.1.call-done = bf16[1024,512]{1,0:T(8,128)(2,1)} async-done(((bf16[256,512]{1,0:T(8,128)(2,1)}), bf16[1024,512]{1,0:T(8,128)(2,1)}) %all-gather.3.cloned.1.call-update) | async-done | bytes 1048592 | tf_op jit(solution)/shard_map/all_gather | solution.py:508
  157.2 4.7 %collective-permute-done.14.other_ref = bf16[256,512]{1,0:T(8,128)(2,1)S(1)} collective-permute-done((bf16[256,512]{1,0:T(8,128)(2,1)}, bf16[256,512]{1,0:T(8,128)(2,1)S(1)}, u32[]{:S(2)}, u32[]{:S(2)}) %collective-permute-start.14) | collective-permute-done | bytes 262176 | tf_op jit(solution)/shard_map/ppermute | solution.py:115
  161.8 6.5 %qkv.3 = (bf16[3,256,512]{2,1,0:T(8,128)(2,1)}, bf16[2,256,512]{2,1,0:T(8,128)(2,1)}) custom-call(s32[1]{0:T(128)} %bitcast.2.ring_ref, bf16[4,256,512]{2,1,0:T(8,128)(2,1)} %bitcast.10, f32[256,128]{1,0:T(8,128)} %get-tuple-element.118.cosine_ref, f32[256,128]{1,0:T(8,128)} %get-tuple-element.117.sine_ref, bf16[256,2560]{1,0:T(8,128)(2,1)} %assemble.1.refs_0_, ...), custom_call_target="tpu_custom_call" | custom-call | flops 1610612736 | bytes 8912896 | tf_op jit(solution)/shard_map/qkv/pallas_call | solution.py:298
  168.3 4.0 %attend.7.own_ref = bf16[256,512]{1,0:T(8,128)(2,1)} custom-call(bf16[3,768,512]{2,1,0:T(8,128)(2,1)} %get-tuple-element.83.q_ref.k0.k1.k2.v0.v1.v2, bf16[3,256,512]{2,1,0:T(8,128)(2,1)} %get-tuple-element.85.q_ref.k2.v2.k1.v1.k0.v0, bf16[3,768,512]{2,1,0:T(8,128)(2,1)} %get-tuple-element.83.q_ref.k0.k1.k2.v0.v1.v2, ...), custom_call_target="tpu_custom_call" | custom-call | flops 402653184 | bytes 2097152 | tf_op jit(solution)/shard_map/attend/pallas_call | solution.py:352
  172.4 0.8 collective-permute-start.22
  173.1 1.0 copy-done
  174.1 4.0 %attend.6.own_ref = bf16[256,512]{1,0:T(8,128)(2,1)} custom-call(bf16[3,768,512]{2,1,0:T(8,128)(2,1)} %get-tuple-element.83.q_ref.k0.k1.k2.v0.v1.v2, bf16[2,512,512]{2,1,0:T(8,128)(2,1)} %copy-done, bf16[3,256,512]{2,1,0:T(8,128)(2,1)} %get-tuple-element.85.q_ref.k2.v2.k1.v1.k0.v0, bf16[3,768,512]{2,1,0:T(8,128)(2,1)} %get-tuple-element.83.q_ref.k0.k1.k2.v0.v1.v2, ...), custom_call_target="tpu_custom_call" | custom-call | flops 402653184 | bytes 2097152 | tf_op jit(solution)/shard_map/attend/pallas_call | solution.py:352
  178.2 1.3 collective-permute-start.19
  179.4 4.6 %project.7 = (f32[256,512]{1,0:T(8,128)}, bf16[256,512]{1,0:T(8,128)(2,1)}, bf16[256,512]{1,0:T(8,128)(2,1)}) custom-call(s32[1]{0:T(128)} %bitcast.1.place_ref, s32[1]{0:T(128)} %bitcast.2.ring_ref, bf16[256,512]{1,0:T(8,128)(2,1)} %attend.4.own_ref, bf16[256,512]{1,0:T(8,128)(2,1)} %copy-done.14, bf16[256,2560]{1,0:T(8,128)(2,1)} %assemble.1.refs_0_, ...), custom_call_target="tpu_custom_call" | custom-call | flops 1073741824 | bytes 5767168 | tf_op jit(solution)/shard_map/project/pallas_call | solution.py:402
  184.1 0.8 collective-permute-start.25
  184.9 4.0 %attend.5.own_ref = bf16[256,512]{1,0:T(8,128)(2,1)} custom-call(bf16[3,256,512]{2,1,0:T(8,128)(2,1)} %get-tuple-element.85.q_ref.k2.v2.k1.v1.k0.v0, bf16[2,512,512]{2,1,0:T(8,128)(2,1)} %copy-done, bf16[2,512,512]{2,1,0:T(8,128)(2,1)} %copy-done, bf16[3,256,512]{2,1,0:T(8,128)(2,1)} %get-tuple-element.85.q_ref.k2.v2.k1.v1.k0.v0, ...), custom_call_target="tpu_custom_call" | custom-call | flops 402653184 | bytes 2097152 | tf_op jit(solution)/shard_map/attend/pallas_call | solution.py:352
  188.9 4.2 %collective-permute-start.16 = (bf16[256,512]{1,0:T(8,128)(2,1)}, bf16[256,512]{1,0:T(8,128)(2,1)S(1)}, u32[]{:S(2)}, u32[]{:S(2)}) collective-permute-start(bf16[256,512]{1,0:T(8,128)(2,1)} %attend.5.own_ref), channel_id=1, source_target_pairs={{0,1},{1,0},{2,3},{3,2},{4,5},{5,4},{6,7},{7,6},{8,9},{9,8},{10,11... | collective-permute-start | bytes 786440 | tf_op jit(solution)/shard_map/ppermute | solution.py:115
  193.1 1.3 collective-permute-start.26
  194.4 0.7 copy-done.15
  195.1 4.7 %project.6 = (f32[256,512]{1,0:T(8,128)}, bf16[256,512]{1,0:T(8,128)(2,1)}, bf16[256,512]{1,0:T(8,128)(2,1)}) custom-call(s32[1]{0:T(128)} %bitcast.1.place_ref, s32[1]{0:T(128)} %bitcast.2.ring_ref, bf16[256,512]{1,0:T(8,128)(2,1)} %attend.7.own_ref, bf16[256,512]{1,0:T(8,128)(2,1)} %copy-done.15, bf16[256,2560]{1,0:T(8,128)(2,1)} %assemble.1.refs_0_, ...), custom_call_target="tpu_custom_call" | custom-call | flops 1073741824 | bytes 5767168 | tf_op jit(solution)/shard_map/project/pallas_call | solution.py:402
  199.8 0.7 collective-permute-start.23
  200.5 1.5 collective-permute-start.24
  202.0 4.7 %project.5 = (f32[256,512]{1,0:T(8,128)}, bf16[256,512]{1,0:T(8,128)(2,1)}, bf16[256,512]{1,0:T(8,128)(2,1)}) custom-call(s32[1]{0:T(128)} %bitcast.1.place_ref, s32[1]{0:T(128)} %bitcast.2.ring_ref, bf16[256,512]{1,0:T(8,128)(2,1)} %attend.6.own_ref, bf16[256,512]{1,0:T(8,128)(2,1)} %copy-done.13, bf16[256,2560]{1,0:T(8,128)(2,1)} %assemble.1.refs_0_, ...), custom_call_target="tpu_custom_call" | custom-call | flops 1073741824 | bytes 5767168 | tf_op jit(solution)/shard_map/project/pallas_call | solution.py:402
  206.7 0.7 collective-permute-start.20
  207.4 1.3 collective-permute-start.21
  208.7 4.7 %project.4 = (f32[256,512]{1,0:T(8,128)}, bf16[256,512]{1,0:T(8,128)(2,1)}, bf16[256,512]{1,0:T(8,128)(2,1)}) custom-call(s32[1]{0:T(128)} %bitcast.1.place_ref, s32[1]{0:T(128)} %bitcast.2.ring_ref, bf16[256,512]{1,0:T(8,128)(2,1)} %attend.5.own_ref, bf16[256,512]{1,0:T(8,128)(2,1)} %copy-done.12, bf16[256,2560]{1,0:T(8,128)(2,1)} %assemble.1.refs_0_, ...), custom_call_target="tpu_custom_call" | custom-call | flops 1073741824 | bytes 5767168 | tf_op jit(solution)/shard_map/project/pallas_call | solution.py:402
  213.5 0.7 collective-permute-start.17
  214.2 1.3 collective-permute-start.18
  215.5 3.4 %final.4.rest_0_ = bf16[1024,4,512]{2,1,0:T(4,128)(2,1)} custom-call(f32[4,6]{1,0:T(4,128)} %static_ref.11, bf16[1024,4,512]{2,1,0:T(4,128)(2,1)} %x_ref.13, f32[8,5248]{1,0:T(8,128)} %get-tuple-element.61.first_ref.folded_ref.column_ref, f32[8,5248]{1,0:T(8,128)} %get-tuple-element.61.first_ref.folded_ref.column_ref, ...), custom_call_target="tpu_custom_call" | custom-call | flops 629145600 | bytes 2883584 | tf_op jit(solution)/shard_map/final/pallas_call | solution.py:481
  218.9 0.7 copy-done.17
  219.6 3.4 %final.5.rest_0_ = bf16[1024,4,512]{2,1,0:T(4,128)(2,1)} custom-call(f32[4,6]{1,0:T(4,128)} %static_ref.11, bf16[1024,4,512]{2,1,0:T(4,128)(2,1)} %x_ref.13, f32[8,5248]{1,0:T(8,128)} %get-tuple-element.61.first_ref.folded_ref.column_ref, f32[8,5248]{1,0:T(8,128)} %get-tuple-element.61.first_ref.folded_ref.column_ref, ...), custom_call_target="tpu_custom_call", output_to_operand_aliasing={{}: (8, {})} | custom-call | flops 629145600 | bytes 2883584 | tf_op jit(solution)/shard_map/final/pallas_call | solution.py:481
  223.0 6.0 %collective-permute-done.21.outer_ref = bf16[256,512]{1,0:T(8,128)(2,1)S(1)} collective-permute-done((bf16[256,512]{1,0:T(8,128)(2,1)}, bf16[256,512]{1,0:T(8,128)(2,1)S(1)}, u32[]{:S(2)}, u32[]{:S(2)}) %collective-permute-start.21) | collective-permute-done | bytes 262176 | tf_op jit(solution)/shard_map/ppermute | solution.py:574
  229.0 0.7 copy-done.19
  229.7 3.4 %final.6.rest_0_ = bf16[1024,4,512]{2,1,0:T(4,128)(2,1)} custom-call(f32[4,6]{1,0:T(4,128)} %static_ref.11, bf16[1024,4,512]{2,1,0:T(4,128)(2,1)} %x_ref.13, f32[8,5248]{1,0:T(8,128)} %get-tuple-element.61.first_ref.folded_ref.column_ref, f32[8,5248]{1,0:T(8,128)} %get-tuple-element.61.first_ref.folded_ref.column_ref, ...), custom_call_target="tpu_custom_call", output_to_operand_aliasing={{}: (8, {})} | custom-call | flops 629145600 | bytes 2883584 | tf_op jit(solution)/shard_map/final/pallas_call | solution.py:481
  233.1 5.6 %collective-permute-done.18.outer_ref = bf16[256,512]{1,0:T(8,128)(2,1)S(1)} collective-permute-done((bf16[256,512]{1,0:T(8,128)(2,1)}, bf16[256,512]{1,0:T(8,128)(2,1)S(1)}, u32[]{:S(2)}, u32[]{:S(2)}) %collective-permute-start.18) | collective-permute-done | bytes 262176 | tf_op jit(solution)/shard_map/ppermute | solution.py:574
  238.7 0.7 copy-done.21
  239.4 3.4 %final.7 = bf16[1024,4,512]{2,1,0:T(4,128)(2,1)} custom-call(f32[4,6]{1,0:T(4,128)} %static_ref.11, bf16[1024,4,512]{2,1,0:T(4,128)(2,1)} %x_ref.13, f32[8,5248]{1,0:T(8,128)} %get-tuple-element.61.first_ref.folded_ref.column_ref, f32[8,5248]{1,0:T(8,128)} %get-tuple-element.61.first_ref.folded_ref.column_ref, ...), custom_call_target="tpu_custom_call", output_to_operand_aliasing={{}: (8, {})} | custom-call | flops 629145600 | bytes 2883584 | tf_op jit(solution)/shard_map/final/pallas_call | solution.py:481
  (90 shorter events, 1.6 us)
Async XLA Ops:
  6.5 122.6 %all-gather.5.cloned.1.call-start = ((), (), s32[]{:S(2)}) async-start(), calls=%async_computation.1 | async-start | bytes 3932160 | tf_op jit(solution)/shard_map/all_gather | solution.py:508
  14.4 11.0 %collective-permute-start.2 = (f32[8,5248]{1,0:T(8,128)}, f32[8,5248]{1,0:T(8,128)S(1)}, u32[]{:S(2)}, u32[]{:S(2)}) collective-permute-start(f32[8,5248]{1,0:T(8,128)} %stats.1.own_ref), channel_id=1, source_target_pairs={{0,3},{1,0},{2,1},{3,2},{4,7},{5,4},{6,5},{7,6},{8,11},{9,8},{10,9... | collective-permute-start | bytes 503816 | tf_op jit(solution)/shard_map/ppermute | solution.py:31
  19.5 14.4 %collective-permute-start.1 = (f32[8,5248]{1,0:T(8,128)}, f32[8,5248]{1,0:T(8,128)S(1)}, u32[]{:S(2)}, u32[]{:S(2)}) collective-permute-start(f32[8,5248]{1,0:T(8,128)} %stats.1.own_ref), channel_id=1, source_target_pairs={{0,2},{1,3},{2,0},{3,1},{4,6},{5,7},{6,4},{7,5},{8,10},{9,11},{10,... | collective-permute-start | bytes 503816 | tf_op jit(solution)/shard_map/ppermute | solution.py:31
  19.5 14.4 %collective-permute-start = (f32[8,5248]{1,0:T(8,128)}, f32[8,5248]{1,0:T(8,128)S(1)}, u32[]{:S(2)}, u32[]{:S(2)}) collective-permute-start(f32[8,5248]{1,0:T(8,128)} %stats.1.own_ref), channel_id=1, source_target_pairs={{0,1},{1,2},{2,3},{3,0},{4,5},{5,6},{6,7},{7,4},{8,9},{9,10},{10,1... | collective-permute-start | bytes 503816 | tf_op jit(solution)/shard_map/ppermute | solution.py:31
  25.4 14.2 %copy-start.4 = (f32[8,5248]{1,0:T(8,128)}, f32[8,5248]{1,0:T(8,128)S(1)}, u32[]{:S(2)}) copy-start(f32[8,5248]{1,0:T(8,128)S(1)} %collective-permute-done.2.c_ref) | copy-start | bytes 503812
  33.9 5.7 %copy-start.5 = (f32[8,5248]{1,0:T(8,128)}, f32[8,5248]{1,0:T(8,128)S(1)}, u32[]{:S(2)}) copy-start(f32[8,5248]{1,0:T(8,128)S(1)} %collective-permute-done.1.b_ref) | copy-start | bytes 503812
  33.9 5.7 %copy-start.6 = (f32[8,5248]{1,0:T(8,128)}, f32[8,5248]{1,0:T(8,128)S(1)}, u32[]{:S(2)}) copy-start(f32[8,5248]{1,0:T(8,128)S(1)} %collective-permute-done.a_ref) | copy-start | bytes 503812
  33.9 13.5 %collective-permute-start.3 = (bf16[64,2560]{1,0:T(8,128)(2,1)}, bf16[64,2560]{1,0:T(8,128)(2,1)S(1)}, u32[]{:S(2)}, u32[]{:S(2)}) collective-permute-start(bf16[64,2560]{1,0:T(8,128)(2,1)} %get-tuple-element.63), channel_id=1, source_target_pairs={{0,1},{1,2},{2,3},{3,0},{4,5},{5,6},{6,7},{7,4},{8,9},{9,10},{10,1... | collective-permute-start | bytes 983048 | tf_op jit(solution)/shard_map/ppermute | solution.py:512
  34.9 24.5 %collective-permute-start.4 = (bf16[64,2560]{1,0:T(8,128)(2,1)}, bf16[64,2560]{1,0:T(8,128)(2,1)S(1)}, u32[]{:S(2)}, u32[]{:S(2)}) collective-permute-start(bf16[64,2560]{1,0:T(8,128)(2,1)} %get-tuple-element.64), channel_id=1, source_target_pairs={{0,2},{1,3},{2,0},{3,1},{4,6},{5,7},{6,4},{7,5},{8,10},{9,11},{10,... | collective-permute-start | bytes 983048 | tf_op jit(solution)/shard_map/ppermute | solution.py:512
  36.8 22.7 %collective-permute-start.5 = (bf16[64,2560]{1,0:T(8,128)(2,1)}, bf16[64,2560]{1,0:T(8,128)(2,1)S(1)}, u32[]{:S(2)}, u32[]{:S(2)}) collective-permute-start(bf16[64,2560]{1,0:T(8,128)(2,1)} %get-tuple-element.65), channel_id=1, source_target_pairs={{0,3},{1,0},{2,1},{3,2},{4,7},{5,4},{6,5},{7,6},{8,11},{9,8},{10,9... | collective-permute-start | bytes 983048 | tf_op jit(solution)/shard_map/ppermute | solution.py:512
  47.4 18.9 %copy-start.23 = (s32[2]{0:T(128)S(1)}, s32[2]{0:T(128)}, u32[]{:S(2)}) copy-start(s32[2]{0:T(128)} %param.11) | copy-start | bytes 28
  47.4 20.2 %copy-start.22 = (s32[1024]{0:T(1024)S(1)}, s32[1024]{0:T(1024)}, u32[]{:S(2)}) copy-start(s32[1024]{0:T(1024)} %param.10) | copy-start | bytes 12292
  47.4 12.2 %copy-start.7 = (bf16[64,2560]{1,0:T(8,128)(2,1)}, bf16[64,2560]{1,0:T(8,128)(2,1)S(1)}, u32[]{:S(2)}) copy-start(bf16[64,2560]{1,0:T(8,128)(2,1)S(1)} %collective-permute-done.3.refs_1_) | copy-start | bytes 983044
  59.5 0.7 copy-start.8
  59.5 0.8 copy-start.9
  59.5 97.7 %all-gather.3.cloned.1.call-start = ((), (), s32[]{:S(2)}) async-start(), calls=%async_computation | async-start | bytes 1310720 | tf_op jit(solution)/shard_map/all_gather | solution.py:508
  62.8 32.9 %collective-permute-start.11 = (bf16[256,2560]{1,0:T(8,128)(2,1)}, bf16[256,2560]{1,0:T(8,128)(2,1)S(1)}, u32[]{:S(2)}, u32[]{:S(2)}) collective-permute-start(bf16[256,2560]{1,0:T(8,128)(2,1)} %assemble.1.refs_0_), channel_id=1, source_target_pairs={{0,24},{4,28},{8,16},{12,20},{16,8},{20,12},{24,0},{28,4},{1,25},{... | collective-permute-start | bytes 3932168 | tf_op jit(solution)/shard_map/ppermute | solution.py:115
  65.2 56.1 %collective-permute-start.9 = (bf16[256,2560]{1,0:T(8,128)(2,1)}, bf16[256,2560]{1,0:T(8,128)(2,1)}, u32[]{:S(2)}, u32[]{:S(2)}) collective-permute-start(bf16[256,2560]{1,0:T(8,128)(2,1)} %assemble.1.refs_0_), channel_id=1, source_target_pairs={{0,16},{4,20},{8,24},{12,28},{16,0},{20,4},{24,8},{28,12},{1,17},{... | collective-permute-start | bytes 3932168 | tf_op jit(solution)/shard_map/ppermute | solution.py:115
  65.7 55.7 %collective-permute-start.7 = (bf16[256,2560]{1,0:T(8,128)(2,1)}, bf16[256,2560]{1,0:T(8,128)(2,1)}, u32[]{:S(2)}, u32[]{:S(2)}) collective-permute-start(bf16[256,2560]{1,0:T(8,128)(2,1)} %assemble.1.refs_0_), channel_id=1, source_target_pairs={{0,8},{4,12},{8,0},{12,4},{16,24},{20,28},{24,16},{28,20},{1,9},{5... | collective-permute-start | bytes 3932168 | tf_op jit(solution)/shard_map/ppermute | solution.py:115
  67.7 54.9 %collective-permute-start.13 = (s32[512]{0:T(512)S(1)}, s32[512]{0:T(512)S(1)}, u32[]{:S(2)}, u32[]{:S(2)}) collective-permute-start(s32[512]{0:T(512)S(1)} %get-tuple-element.110), channel_id=1, source_target_pairs={{0,4},{4,8},{8,12},{12,16},{16,20},{20,24},{24,28},{1,5},{5,9},{9,... | collective-permute-start | bytes 6152 | tf_op jit(solution)/shard_map/ppermute | solution.py:25
  69.0 58.3 %collective-permute-start.6 = (bf16[256,2560]{1,0:T(8,128)(2,1)}, bf16[256,2560]{1,0:T(8,128)(2,1)}, u32[]{:S(2)}, u32[]{:S(2)}) collective-permute-start(bf16[256,2560]{1,0:T(8,128)(2,1)} %assemble.1.refs_0_), channel_id=1, source_target_pairs={{0,4},{4,0},{8,12},{12,8},{16,20},{20,16},{24,28},{28,24},{1,5},{5... | collective-permute-start | bytes 3932168 | tf_op jit(solution)/shard_map/ppermute | solution.py:115
  95.7 33.5 %copy-start.1 = (bf16[256,2560]{1,0:T(8,128)(2,1)}, bf16[256,2560]{1,0:T(8,128)(2,1)S(1)}, u32[]{:S(2)}) copy-start(bf16[256,2560]{1,0:T(8,128)(2,1)S(1)} %collective-permute-done.11.refs_6_) | copy-start | bytes 3932164
  95.7 31.6 %collective-permute-start.12 = (bf16[256,2560]{1,0:T(8,128)(2,1)S(1)}, bf16[256,2560]{1,0:T(8,128)(2,1)}, u32[]{:S(2)}, u32[]{:S(2)}) collective-permute-start(bf16[256,2560]{1,0:T(8,128)(2,1)S(1)} %collective-permute-done.11.refs_6_), channel_id=1, source_target_pairs={{0,4},{4,0},{8,12},{12,8},{16,20},{20,16},{24,28},{28,24},{1,5},{5... | collective-permute-start | bytes 3932168 | tf_op jit(solution)/shard_map/ppermute | solution.py:115
  121.3 6.0 %collective-permute-start.10 = (bf16[256,2560]{1,0:T(8,128)(2,1)}, bf16[256,2560]{1,0:T(8,128)(2,1)}, u32[]{:S(2)}, u32[]{:S(2)}) collective-permute-start(bf16[256,2560]{1,0:T(8,128)(2,1)} %collective-permute-done.9.refs_4_), channel_id=1, source_target_pairs={{0,4},{4,0},{8,12},{12,8},{16,20},{20,16},{24,28},{28,24},{1,5},{5... | collective-permute-start | bytes 3932168 | tf_op jit(solution)/shard_map/ppermute | solution.py:115
  121.4 5.9 %collective-permute-start.8 = (bf16[256,2560]{1,0:T(8,128)(2,1)}, bf16[256,2560]{1,0:T(8,128)(2,1)}, u32[]{:S(2)}, u32[]{:S(2)}) collective-permute-start(bf16[256,2560]{1,0:T(8,128)(2,1)} %collective-permute-done.7.refs_2_), channel_id=1, source_target_pairs={{0,4},{4,0},{8,12},{12,8},{16,20},{20,16},{24,28},{28,24},{1,5},{5... | collective-permute-start | bytes 3932168 | tf_op jit(solution)/shard_map/ppermute | solution.py:115
  126.1 1.2 copy-start.2
  139.7 33.4 %collective-permute-start.15 = (bf16[2,512,512]{2,1,0:T(8,128)(2,1)}, bf16[2,512,512]{2,1,0:T(8,128)(2,1)S(1)}, u32[]{:S(2)}, u32[]{:S(2)}) collective-permute-start(bf16[2,512,512]{2,1,0:T(8,128)(2,1)} %get-tuple-element.86), channel_id=1, source_target_pairs={{0,4},{4,8},{8,12},{12,16},{16,20},{20,24},{24,28},{1,5},{5,9},{9,... | collective-permute-start | bytes 3145736 | tf_op jit(solution)/shard_map/ppermute | solution.py:25
  143.4 10.2 %copy-start.3 = (f32[1024,64]{1,0:T(8,128)S(1)}, f32[1024,64]{1,0:T(8,128)}, u32[]{:S(2)}) copy-start(f32[1024,64]{1,0:T(8,128)} %copy-done.2) | copy-start | bytes 786436
  147.5 14.3 %collective-permute-start.14 = (bf16[256,512]{1,0:T(8,128)(2,1)}, bf16[256,512]{1,0:T(8,128)(2,1)S(1)}, u32[]{:S(2)}, u32[]{:S(2)}) collective-permute-start(bf16[256,512]{1,0:T(8,128)(2,1)} %attend.4.own_ref), channel_id=1, source_target_pairs={{0,1},{1,0},{2,3},{3,2},{4,5},{5,4},{6,7},{7,6},{8,9},{9,8},{10,11... | collective-permute-start | bytes 786440 | tf_op jit(solution)/shard_map/ppermute | solution.py:115
  161.8 6.5 %copy-start.14 = (bf16[256,512]{1,0:T(8,128)(2,1)}, bf16[256,512]{1,0:T(8,128)(2,1)S(1)}, u32[]{:S(2)}) copy-start(bf16[256,512]{1,0:T(8,128)(2,1)S(1)} %collective-permute-done.14.other_ref) | copy-start | bytes 786436
  172.4 22.0 %collective-permute-start.22 = (bf16[256,512]{1,0:T(8,128)(2,1)}, bf16[256,512]{1,0:T(8,128)(2,1)S(1)}, u32[]{:S(2)}, u32[]{:S(2)}) collective-permute-start(bf16[256,512]{1,0:T(8,128)(2,1)} %attend.7.own_ref), channel_id=1, source_target_pairs={{0,1},{1,0},{2,3},{3,2},{4,5},{5,4},{6,7},{7,6},{8,9},{9,8},{10,11... | collective-permute-start | bytes 786440 | tf_op jit(solution)/shard_map/ppermute | solution.py:115
  173.1 1.0 copy-start
  178.2 22.3 %collective-permute-start.19 = (bf16[256,512]{1,0:T(8,128)(2,1)}, bf16[256,512]{1,0:T(8,128)(2,1)S(1)}, u32[]{:S(2)}, u32[]{:S(2)}) collective-permute-start(bf16[256,512]{1,0:T(8,128)(2,1)} %attend.6.own_ref), channel_id=1, source_target_pairs={{0,1},{1,0},{2,3},{3,2},{4,5},{5,4},{6,7},{7,6},{8,9},{9,8},{10,11... | collective-permute-start | bytes 786440 | tf_op jit(solution)/shard_map/ppermute | solution.py:115
  184.1 9.0 %copy-start.24 = (bf16[256,512]{1,0:T(8,128)(2,1)S(1)}, bf16[256,512]{1,0:T(8,128)(2,1)}, u32[]{:S(2)}) copy-start(bf16[256,512]{1,0:T(8,128)(2,1)} %get-tuple-element.100) | copy-start | bytes 786436
  184.1 22.6 %collective-permute-start.25 = (bf16[256,512]{1,0:T(8,128)(2,1)}, bf16[256,512]{1,0:T(8,128)(2,1)S(1)}, u32[]{:S(2)}, u32[]{:S(2)}) collective-permute-start(bf16[256,512]{1,0:T(8,128)(2,1)} %get-tuple-element.99), channel_id=1, source_target_pairs={{1,2},{2,1},{5,6},{6,5},{9,10},{10,9},{13,14},{14,13},{17,18},{18,... | collective-permute-start | bytes 786440 | tf_op jit(solution)/shard_map/ppermute | solution.py:573
  188.9 18.5 %collective-permute-start.16 = (bf16[256,512]{1,0:T(8,128)(2,1)}, bf16[256,512]{1,0:T(8,128)(2,1)S(1)}, u32[]{:S(2)}, u32[]{:S(2)}) collective-permute-start(bf16[256,512]{1,0:T(8,128)(2,1)} %attend.5.own_ref), channel_id=1, source_target_pairs={{0,1},{1,0},{2,3},{3,2},{4,5},{5,4},{6,7},{7,6},{8,9},{9,8},{10,11... | collective-permute-start | bytes 786440 | tf_op jit(solution)/shard_map/ppermute | solution.py:115
  193.1 20.3 %collective-permute-start.26 = (bf16[256,512]{1,0:T(8,128)(2,1)S(1)}, bf16[256,512]{1,0:T(8,128)(2,1)S(1)}, u32[]{:S(2)}, u32[]{:S(2)}) collective-permute-start(bf16[256,512]{1,0:T(8,128)(2,1)S(1)} %copy-done.24), channel_id=1, source_target_pairs={{1,3},{2,0},{5,7},{6,4},{9,11},{10,8},{13,15},{14,12},{17,19},{18,... | collective-permute-start | bytes 786440 | tf_op jit(solution)/shard_map/ppermute | solution.py:574
  194.4 0.7 copy-start.15
  199.8 14.3 %collective-permute-start.23 = (bf16[256,512]{1,0:T(8,128)(2,1)}, bf16[256,512]{1,0:T(8,128)(2,1)S(1)}, u32[]{:S(2)}, u32[]{:S(2)}) collective-permute-start(bf16[256,512]{1,0:T(8,128)(2,1)} %get-tuple-element.94), channel_id=1, source_target_pairs={{1,2},{2,1},{5,6},{6,5},{9,10},{10,9},{13,14},{14,13},{17,18},{18,... | collective-permute-start | bytes 786440 | tf_op jit(solution)/shard_map/ppermute | solution.py:573
  200.5 1.5 copy-start.13
  200.5 18.4 %collective-permute-start.24 = (bf16[256,512]{1,0:T(8,128)(2,1)}, bf16[256,512]{1,0:T(8,128)(2,1)S(1)}, u32[]{:S(2)}, u32[]{:S(2)}) collective-permute-start(bf16[256,512]{1,0:T(8,128)(2,1)} %get-tuple-element.95), channel_id=1, source_target_pairs={{1,3},{2,0},{5,7},{6,4},{9,11},{10,8},{13,15},{14,12},{17,19},{18,... | collective-permute-start | bytes 786440 | tf_op jit(solution)/shard_map/ppermute | solution.py:574
  206.7 6.7 %copy-start.10 = (bf16[256,512]{1,0:T(8,128)(2,1)}, bf16[256,512]{1,0:T(8,128)(2,1)S(1)}, u32[]{:S(2)}) copy-start(bf16[256,512]{1,0:T(8,128)(2,1)S(1)} %collective-permute-done.25.inner_ref) | copy-start | bytes 786436
  206.7 16.3 %collective-permute-start.20 = (bf16[256,512]{1,0:T(8,128)(2,1)}, bf16[256,512]{1,0:T(8,128)(2,1)S(1)}, u32[]{:S(2)}, u32[]{:S(2)}) collective-permute-start(bf16[256,512]{1,0:T(8,128)(2,1)} %get-tuple-element.91), channel_id=1, source_target_pairs={{1,2},{2,1},{5,6},{6,5},{9,10},{10,9},{13,14},{14,13},{17,18},{18,... | collective-permute-start | bytes 786440 | tf_op jit(solution)/shard_map/ppermute | solution.py:573
  207.4 1.3 copy-start.12
  207.4 21.6 %collective-permute-start.21 = (bf16[256,512]{1,0:T(8,128)(2,1)}, bf16[256,512]{1,0:T(8,128)(2,1)S(1)}, u32[]{:S(2)}, u32[]{:S(2)}) collective-permute-start(bf16[256,512]{1,0:T(8,128)(2,1)} %get-tuple-element.92), channel_id=1, source_target_pairs={{1,3},{2,0},{5,7},{6,4},{9,11},{10,8},{13,15},{14,12},{17,19},{18,... | collective-permute-start | bytes 786440 | tf_op jit(solution)/shard_map/ppermute | solution.py:574
  213.4 2.0 copy-start.11
  213.5 19.7 %collective-permute-start.17 = (bf16[256,512]{1,0:T(8,128)(2,1)}, bf16[256,512]{1,0:T(8,128)(2,1)S(1)}, u32[]{:S(2)}, u32[]{:S(2)}) collective-permute-start(bf16[256,512]{1,0:T(8,128)(2,1)} %get-tuple-element.88), channel_id=1, source_target_pairs={{1,2},{2,1},{5,6},{6,5},{9,10},{10,9},{13,14},{14,13},{17,18},{18,... | collective-permute-start | bytes 786440 | tf_op jit(solution)/shard_map/ppermute | solution.py:573
  214.1 4.7 %copy-start.16 = (bf16[256,512]{1,0:T(8,128)(2,1)}, bf16[256,512]{1,0:T(8,128)(2,1)S(1)}, u32[]{:S(2)}) copy-start(bf16[256,512]{1,0:T(8,128)(2,1)S(1)} %collective-permute-done.23.inner_ref) | copy-start | bytes 786436
  214.2 24.5 %collective-permute-start.18 = (bf16[256,512]{1,0:T(8,128)(2,1)}, bf16[256,512]{1,0:T(8,128)(2,1)S(1)}, u32[]{:S(2)}, u32[]{:S(2)}) collective-permute-start(bf16[256,512]{1,0:T(8,128)(2,1)} %get-tuple-element.89), channel_id=1, source_target_pairs={{1,3},{2,0},{5,7},{6,4},{9,11},{10,8},{13,15},{14,12},{17,19},{18,... | collective-permute-start | bytes 786440 | tf_op jit(solution)/shard_map/ppermute | solution.py:574
  218.9 0.7 copy-start.17
  223.0 6.0 %copy-start.18 = (bf16[256,512]{1,0:T(8,128)(2,1)}, bf16[256,512]{1,0:T(8,128)(2,1)S(1)}, u32[]{:S(2)}) copy-start(bf16[256,512]{1,0:T(8,128)(2,1)S(1)} %collective-permute-done.20.inner_ref) | copy-start | bytes 786436
  229.0 0.7 copy-start.19
  233.1 5.6 %copy-start.20 = (bf16[256,512]{1,0:T(8,128)(2,1)}, bf16[256,512]{1,0:T(8,128)(2,1)S(1)}, u32[]{:S(2)}) copy-start(bf16[256,512]{1,0:T(8,128)(2,1)S(1)} %collective-permute-done.17.inner_ref) | copy-start | bytes 786436
  238.7 0.7 copy-start.21
Sparse Core Ops, SparseCore 0:
  59.6 69.4 all-gather.4
  130.7 26.4 all-gather.2

commit v11 on v10

--- a/solution.py
+++ b/solution.py
@@ -319,7 +319,7 @@
     )(ring, rows, cosine, sine, *pieces)
 
 
-def attend_kernel(q_ref, k0, k1, k2, v0, v1, v2, qseg_ref, kseg_ref, attended_ref):
+def attend_step(q_ref, k0, k1, k2, v0, v1, v2, qseg_ref, kseg_ref, attended_ref):
     tokens, width = q_ref.shape[1:]
     window = kseg_ref.shape[-1]
     row, col = iotas(tokens, window)
@@ -339,81 +339,98 @@
         attended_ref[:, lanes] = (contract(weights.astype(BF), values, 1, 0) / total).astype(BF)
 
 
-def attend(query, window, qseg, kseg, chunk):
-    source, at = query
-    width = source.shape[-1]
-    block = (1, CHUNK, width)
-    keys = [pl.BlockSpec(block, lambda i, s=slot, r=where: (s, r, 0)) for _, slot, where in window]
-    values = [
-        pl.BlockSpec(block, lambda i, s=slot + 1, r=where: (s, r, 0)) for _, slot, where in window
-    ]
-    arrays = [array for array, _, _ in window]
-    reach = kseg.shape[-1]
-    return pl.pallas_call(
-        attend_kernel,
-        grid=(1,),
-        in_specs=[pl.BlockSpec(block, lambda i: (0, at, 0))]
-        + keys
-        + values
-        + [
+def project_step(place_ref, ring_ref, own_ref, other_ref, pieces, kept_ref, inner_ref, outer_ref, sums):
+    servers, _, width = sums.shape
+    half = pl.program_id(0)
+    place = place_ref[0]
+    left = jnp.where(place % 2 == half, own_ref[...], other_ref[...])
+    depth = pieces[0].shape[0]
+
+    def add(server, lanes, rows):
+        so_far = jnp.where(half == 0, 0.0, sums[server, :, lanes])
+        sums[server, :, lanes] = so_far + contract(left, rows, 1, 1)
+
+    if len(pieces) == 1:
+        for server in range(servers):
+            add(server, slice(None), pieces[0][server * width : (server + 1) * width, :])
+    else:
+        for at, piece in enumerate(pieces):
+            target = ring_ref[0] ^ at
+            inside = pl.multiple_of((target % (width // depth)) * depth, depth)
+            add(target // (width // depth), pl.ds(inside, depth), piece[...])
+
+    @pl.when(half == 1)
+    def _():
+        kept_ref[...] = sums[place]
+        low = place < 2
+        inner_ref[...] = sums[jnp.where(low, 2, 1)].astype(BF)
+        outer_ref[...] = sums[jnp.where(low, 3, 0)].astype(BF)
+
+
+def output_kernel(attends, projects, *refs):
+    refs = list(refs)
+    left = [refs.pop(0) for _ in range(9 if attends else 0)]
+    right = [refs.pop(0) for _ in range(4 if projects else 0)]
+    sums = refs.pop() if projects else None
+    updates = [refs.pop() for _ in range(3 if projects else 0)][::-1]
+    if attends:
+        attended_ref = refs.pop()
+
+        @pl.when(pl.program_id(0) == 0)
+        def _():
+            attend_step(*left, attended_ref)
+
+    if projects:
+        project_step(*right, refs, *updates, sums)
+
+
+def output_step(attends, projects):
+    specs, args, outs, shapes, scratch = [], [], [], [], []
+    work = 0
+    smem = pl.BlockSpec(memory_space=pltpu.SMEM)
+    if attends:
+        chunk, window, qseg, kseg = attends
+        source, _, at = window[-1]
+        width = source.shape[-1]
+        block = (1, CHUNK, width)
+        reach = kseg.shape[-1]
+        specs.append(pl.BlockSpec(block, lambda i: (0, at, 0)))
+        for which in range(2):
+            specs += [
+                pl.BlockSpec(block, lambda i, s=slot + which, r=where: (s, r, 0))
+                for _, slot, where in window
+            ]
+        specs += [
             pl.BlockSpec((CHUNK, 1), lambda i: (chunk, 0)),
             pl.BlockSpec((1, 1, reach), lambda i: (chunk, 0, 0)),
-        ],
-        out_specs=pl.BlockSpec((CHUNK, width), lambda i: (0, 0)),
-        out_shape=jax.ShapeDtypeStruct((CHUNK, width), BF),
-        cost_estimate=cost(4 * CHUNK * reach * width, CHUNK * width * 16, CHUNK * reach * 4),
+        ]
+        args += [source] + [array for array, _, _ in window] * 2 + [qseg, kseg]
+        outs.append(pl.BlockSpec((CHUNK, width), lambda i: (0, 0)))
+        shapes.append(jax.ShapeDtypeStruct((CHUNK, width), BF))
+        work += 4 * CHUNK * reach * width
+    if projects:
+        place, ring, own, other, pieces, servers = projects
+        tokens, width = own.shape
+        rows, columns = pieces[0].shape
+        full = pl.BlockSpec((tokens, width), lambda i: (0, 0))
+        tail = pl.BlockSpec((rows, width), lambda i: (0, columns // width - 2 + i))
+        specs += [smem] * 2 + [full] * 2 + [tail] * len(pieces)
+        args += [place, ring, own, other, *pieces]
+        outs += [full] * 3
+        shapes += [jax.ShapeDtypeStruct((tokens, width), kind) for kind in (F32, BF, BF)]
+        scratch.append(pltpu.VMEM((servers, tokens, width), F32))
+        work += 4 * tokens * D * width
+    return pl.pallas_call(
+        functools.partial(output_kernel, bool(attends), bool(projects)),
+        grid=(2 if projects else 1,),
+        in_specs=specs,
+        out_specs=outs,
+        out_shape=shapes,
+        scratch_shapes=scratch,
+        cost_estimate=cost(work, work // 512),
         compiler_params=params(),
-        name="attend",
-    )(source, *arrays, *arrays, qseg, kseg)
-
-
-def project_kernel(place_ref, ring_ref, own_ref, other_ref, *refs):
-    pieces = refs[:-4]
-    kept_ref, inner_ref, outer_ref, sums = refs[-4:]
-    servers, _, width = sums.shape
-    place = place_ref[0]
-    even = place % 2 == 0
-    own, other = own_ref[...], other_ref[...]
-    both = jnp.concatenate([jnp.where(even, own, other), jnp.where(even, other, own)], axis=1)
-    depth = pieces[0].shape[0]
-    if len(pieces) == 1:
-        for server in range(servers):
-            rows = pieces[0][server * width : (server + 1) * width, :]
-            sums[server] = contract(both, rows, 1, 1)
-    else:
-        for piece in range(len(pieces)):
-            target = ring_ref[0] ^ piece
-            inside = pl.multiple_of((target % (width // depth)) * depth, depth)
-            sums[target // (width // depth), :, pl.ds(inside, depth)] = contract(
-                both, pieces[piece][...], 1, 1
-            )
-    kept_ref[...] = sums[place]
-    low = place < 2
-    inner_ref[...] = sums[jnp.where(low, 2, 1)].astype(BF)
-    outer_ref[...] = sums[jnp.where(low, 3, 0)].astype(BF)
-
-
-def project(place, ring, own, other, pieces, servers):
-    tokens, width = own.shape
-    rows, columns = pieces[0].shape
-    pair = 2 * width
-    tail = pl.BlockSpec((pl.Element(rows), pl.Element(pair)), lambda i: (0, columns - pair))
-    full = pl.BlockSpec((tokens, width), lambda i: (0, 0))
-    return pl.pallas_call(
-        project_kernel,
-        grid=(1,),
-        in_specs=[pl.BlockSpec(memory_space=pltpu.SMEM)] * 2 + [full] * 2 + [tail] * len(pieces),
-        out_specs=[full] * 3,
-        out_shape=[
-            jax.ShapeDtypeStruct((tokens, width), F32),
-            jax.ShapeDtypeStruct((tokens, width), BF),
-            jax.ShapeDtypeStruct((tokens, width), BF),
-        ],
-        scratch_shapes=[pltpu.VMEM((servers, tokens, width), F32)],
-        cost_estimate=cost(2 * tokens * D * pair, D * pair * 2 + tokens * width * 12),
-        compiler_params=params(),
-        name="project",
-    )(place, ring, own, other, *pieces)
+        name="output" if attends and projects else "attend" if attends else "project",
+    )(*args)
 
 
 def final_kernel(
@@ -547,25 +564,31 @@
     qkv_late, halo_rows = qkv_columns(ring, rows_late, pieces, cosine[CHUNK:], sine[CHUNK:])
     halo_rows = passed_along(halo_rows, "blk", 1)
 
-    def projected(own, other):
-        return project(place, ring, own, other, pieces, group_size)
-
     last = tokens_local // CHUNK - 1
     late_chunks = [(qkv_late, 1, at) for at in range(last)]
 
-    def attended(chunk, window):
-        source, _, at = window[-1]
-        return attend((source, at), window, query_segments, key_segments, chunk)
-
-    own = attended(last, late_chunks[-3:])
-    both = (own, swapped(own, "mp", 1))
-    rows_first, both = lax.optimization_barrier((rows_first, both))
-    parts = {last: projected(*both)}
+    def attends(chunk, window):
+        return (chunk, window, query_segments, key_segments)
+
+    def projects(own):
+        return (place, ring, own, swapped(own, "mp", 1), pieces, group_size)
+
+    waiting = []
+    (own,) = output_step(attends(last, late_chunks[-3:]), None)
+    both = projects(own)
+    rows_first, both = lax.optimization_barrier((rows_first, both[:4]))
+    waiting.append((last, (*both, pieces, group_size)))
     qkv_first, _ = qkv_columns(ring, rows_first, pieces, cosine[:CHUNK], sine[:CHUNK])
     chunks = [(halo_rows, 0, 0), (halo_rows, 0, 1), (qkv_first, 1, 0)] + late_chunks
+    parts = {}
     for chunk in reversed(range(last)):
-        own = attended(chunk, chunks[chunk : chunk + 3])
-        parts[chunk] = projected(own, swapped(own, "mp", 1))
+        due = waiting.pop(0) if (last - chunk) % 2 else None
+        step = output_step(attends(chunk, chunks[chunk : chunk + 3]), due and due[1])
+        waiting.append((chunk, projects(step[0])))
+        if due:
+            parts[due[0]] = step[1:]
+    for chunk, due in waiting:
+        parts[chunk] = output_step(None, due)
 
     result = None
     for chunk in reversed(range(last + 1)):

time: 251 us -> 251 us (level)
  waiting for transfers between devices: 91.6 us -> 95.2 us
  Pallas kernels: 87 us -> 84.4 us
    ppermute x11, waiting for transfers between devices: 54.8 us -> 58.8 us  [swapped(): lax.ppermute(value, axis, [(source, source ^ mask) for source in range(co...]
    pallas_call x8 -> x6, Pallas kernels: 34.9 us -> 32.3 us  [output_step(): pl.pallas_call(functools.partial(output_kernel, bool(attends), bool(proje...]
  transfers between devices with their start and end apart: 29 -> 29, of which waited for: 10 -> 11; matrix products, arithmetic and copies ran while one was open for 3% -> 3% of each run, Pallas kernels for 31% -> 30%
where the time goes in v11:
time: 251 us; the launch traced here: 250 us
  waiting for transfers between devices  95.2 us (38%)
  Pallas kernels  84.4 us (34%)
  starting transfers between devices  41.5 us (17%)
  between operations  15.2 us (6%)
  local copies, waits for them, and re-layouts  7.15 us (3%)
  other arithmetic  7 us (3%)
    ppermute x11, waiting for transfers between devices, swapped(): lax.ppermute(value, axis, [(source, source ^ mask) for source in range(co...  58.8 us
    pallas_call x6, Pallas kernels, output_step(): pl.pallas_call(functools.partial(output_kernel, bool(attends), bool(proje...  32.3 us
    ppermute x11, starting transfers between devices, swapped(): lax.ppermute(value, axis, [(source, source ^ mask) for source in range(co...  18.4 us
    pallas_call x2, Pallas kernels, qkv_columns(): pl.pallas_call(qkv_kernel, grid=(3,), in_specs=[pl.BlockSpec(memory_space...  17.1 us
    pallas_call x4, Pallas kernels, final(): pl.pallas_call(final_kernel, grid=(tokens // STEP,), in_specs=specs, out_...  13.6 us
    ppermute x3, waiting for transfers between devices, body(): lax.ppermute(parts[step], 'mp', [(at, (at + step) % group_size) for at in...  12.1 us
    ppermute x4, waiting for transfers between devices, body(): outer = lax.ppermute(outer, 'mp', [(1, 3), (2, 0)])  10.8 us
    ppermute x3, waiting for transfers between devices, from_others(): lax.ppermute(value, axis, [(source, (source + step) % count) for source i...  8.51 us
  transfers between devices with their start and end apart: 29, of which 11 were waited for; matrix products, arithmetic and copies ran while one was open for 3% of the time, Pallas kernels for 30%

profile of v11, /device:TPU:0, one launch (start us, length us, event | category | flops | bytes accessed | tf_op | source)
XLA Modules:
  0.0 250.5 jit_solution(3275584071534277887)
XLA Ops:
  6.7 1.4 maximum_maximum_fusion.proj_ref
  8.1 6.4 %stats.1.own_ref = f32[8,5248]{1,0:T(8,128)} custom-call(bf16[1024,4,512]{2,1,0:T(4,128)(2,1)} %x_ref.13, f32[8,512]{1,0:T(8,128)} %maximum_maximum_fusion.proj_ref), custom_call_target="tpu_custom_call" | custom-call | flops 1258291200 | bytes 4194304 | tf_op jit(solution)/shard_map/stats/pallas_call | solution.py:171
  14.4 5.0 %collective-permute-start.2 = (f32[8,5248]{1,0:T(8,128)}, f32[8,5248]{1,0:T(8,128)S(1)}, u32[]{:S(2)}, u32[]{:S(2)}) collective-permute-start(f32[8,5248]{1,0:T(8,128)} %stats.1.own_ref), channel_id=1, source_target_pairs={{0,3},{1,0},{2,1},{3,2},{4,7},{5,4},{6,5},{7,6},{8,11},{9,8},{10,9... | collective-permute-start | bytes 503816 | tf_op jit(solution)/shard_map/ppermute | solution.py:31
  19.5 1.0 collective-permute-start
  20.5 4.9 %regroup.1 = (bf16[64,2560]{1,0:T(8,128)(2,1)}, bf16[64,2560]{1,0:T(8,128)(2,1)}, bf16[64,2560]{1,0:T(8,128)(2,1)}, bf16[64,2560]{1,0:T(8,128)(2,1)}) custom-call(s32[1]{0:T(128)} %bitcast.1.place_ref.refs_9_.refs_0_, f32[64,4,2048]{2,1,0:T(4,128)} %master_ref.1), custom_call_target="tpu_custom_call" | custom-call | bytes 3407872 | tf_op jit(solution)/shard_map/regroup/pallas_call | solution.py:79
  25.4 8.5 %collective-permute-done.1.b_ref = f32[8,5248]{1,0:T(8,128)S(1)} collective-permute-done((f32[8,5248]{1,0:T(8,128)}, f32[8,5248]{1,0:T(8,128)S(1)}, u32[]{:S(2)}, u32[]{:S(2)}) %collective-permute-start.1) | collective-permute-done | bytes 167968 | tf_op jit(solution)/shard_map/ppermute | solution.py:31
  33.9 1.0 collective-permute-start.3
  34.9 1.8 collective-permute-start.4
  36.8 2.9 %collective-permute-start.5 = (bf16[64,2560]{1,0:T(8,128)(2,1)}, bf16[64,2560]{1,0:T(8,128)(2,1)S(1)}, u32[]{:S(2)}, u32[]{:S(2)}) collective-permute-start(bf16[64,2560]{1,0:T(8,128)(2,1)} %get-tuple-element.69), channel_id=1, source_target_pairs={{0,3},{1,0},{2,1},{3,2},{4,7},{5,4},{6,5},{7,6},{8,11},{9,8},{10,9... | collective-permute-start | bytes 983048 | tf_op jit(solution)/shard_map/ppermute | solution.py:529
  39.7 2.9 %mix.3 = (f32[8,5248]{1,0:T(8,128)}, bf16[256,512]{1,0:T(8,128)(2,1)}) custom-call(f32[4,6]{1,0:T(4,128)} %static_ref.11, bf16[1024,4,512]{2,1,0:T(4,128)(2,1)} %x_ref.13, f32[8,5248]{1,0:T(8,128)} %stats.1.own_ref, f32[8,5248]{1,0:T(8,128)} %copy-done.6, f32[8,5248]{1,0:T(8,128)} %copy-done.5, f32[8,5248]{1,0:T(8,128)} %copy-done.4), custom_call_target="tpu_custom_call" | custom-call | flops 209715200 | bytes 1310720 | tf_op jit(solution)/shard_map/mix/pallas_call | solution.py:242
  42.5 4.8 %mix.2 = (f32[8,5248]{1,0:T(8,128)}, bf16[768,512]{1,0:T(8,128)(2,1)}) custom-call(f32[4,6]{1,0:T(4,128)} %static_ref.11, bf16[1024,4,512]{2,1,0:T(4,128)(2,1)} %x_ref.13, f32[8,5248]{1,0:T(8,128)} %stats.1.own_ref, f32[8,5248]{1,0:T(8,128)} %copy-done.6, f32[8,5248]{1,0:T(8,128)} %copy-done.5, f32[8,5248]{1,0:T(8,128)} %copy-done.4), custom_call_target="tpu_custom_call" | custom-call | flops 629145600 | bytes 3932160 | tf_op jit(solution)/shard_map/mix/pallas_call | solution.py:242
  47.4 12.1 %collective-permute-done.4.refs_2_ = bf16[64,2560]{1,0:T(8,128)(2,1)S(1)} collective-permute-done((bf16[64,2560]{1,0:T(8,128)(2,1)}, bf16[64,2560]{1,0:T(8,128)(2,1)S(1)}, u32[]{:S(2)}, u32[]{:S(2)}) %collective-permute-start.4) | collective-permute-done | bytes 327712 | tf_op jit(solution)/shard_map/ppermute | solution.py:529
  59.6 0.6 copy-done.8
  60.3 2.4 assemble.1.refs_0_.refs_13_.refs_4_
  62.8 2.4 collective-permute-start.11
  65.2 0.5 collective-permute-start.9
  65.7 0.5 collective-permute-start.7
  66.3 0.7 fusion.7
  67.7 1.3 collective-permute-start.13
  69.0 2.3 collective-permute-start.6
  71.3 24.4 %collective-permute-done.11.refs_6_.refs_19_.refs_10_ = bf16[256,2560]{1,0:T(8,128)(2,1)S(1)} collective-permute-done((bf16[256,2560]{1,0:T(8,128)(2,1)}, bf16[256,2560]{1,0:T(8,128)(2,1)S(1)}, u32[]{:S(2)}, u32[]{:S(2)}) %collective-permute-start.11) | collective-permute-done | bytes 1310752 | tf_op jit(solution)/shard_map/ppermute | solution.py:115
  95.7 25.6 %collective-permute-done.9.refs_4_.refs_17_.refs_8_ = bf16[256,2560]{1,0:T(8,128)(2,1)} collective-permute-done((bf16[256,2560]{1,0:T(8,128)(2,1)}, bf16[256,2560]{1,0:T(8,128)(2,1)}, u32[]{:S(2)}, u32[]{:S(2)}) %collective-permute-start.9) | collective-permute-done | bytes 1310752 | tf_op jit(solution)/shard_map/ppermute | solution.py:115
  121.4 0.4 collective-permute-start.8
  122.6 1.0 copy.14.refs_7_
  123.6 1.6 convert_reduce_fusion
  125.3 1.9 multiply_sine_fusion
  127.2 1.2 fusion.1
  128.4 0.7 all-gather.5.cloned.1.call-done
  129.1 10.6 %qkv.2 = (bf16[3,768,512]{2,1,0:T(8,128)(2,1)}, bf16[2,512,512]{2,1,0:T(8,128)(2,1)}) custom-call(s32[1]{0:T(128)} %bitcast.2.ring_ref.refs_10_.refs_1_, bf16[4,768,512]{2,1,0:T(8,128)(2,1)} %bitcast.13, f32[768,128]{1,0:T(8,128)} %get-tuple-element.124.cosine_ref, f32[768,128]{1,0:T(8,128)} %get-tuple-element.123.sine_ref, ...), custom_call_target="tpu_custom_call" | custom-call | flops 4831838208 | bytes 14155776 | tf_op jit(solution)/shard_map/qkv/pallas_call | solution.py:298
  139.7 1.9 collective-permute-start.15
  141.7 0.6 broadcast_in_dim.29.refs_8_
  142.4 4.1 %attend.2.refs_11_ = bf16[256,512]{1,0:T(8,128)(2,1)} custom-call(bf16[3,768,512]{2,1,0:T(8,128)(2,1)} %get-tuple-element.87.refs_0_.refs_1_.refs_2_.refs_3_.refs_4_.refs_5_.refs_6_, bf16[3,768,512]{2,1,0:T(8,128)(2,1)} %get-tuple-element.87.refs_0_.refs_1_.refs_2_.refs_3_.refs_4_.refs_5_.refs_6_, ...), custom_call_target="tpu_custom_call" | custom-call | flops 402653184 | bytes 786432 | tf_op jit(solution)/shard_map/attend/pallas_call | solution.py:423
  146.4 7.2 %collective-permute-start.14 = (bf16[256,512]{1,0:T(8,128)(2,1)}, bf16[256,512]{1,0:T(8,128)(2,1)S(1)}, u32[]{:S(2)}, u32[]{:S(2)}) collective-permute-start(bf16[256,512]{1,0:T(8,128)(2,1)} %attend.2.refs_11_), channel_id=1, source_target_pairs={{0,1},{1,0},{2,3},{3,2},{4,5},{5,4},{6,7},{7,6},{8,9},{9,8},{10,11... | collective-permute-start | bytes 786440 | tf_op jit(solution)/shard_map/ppermute | solution.py:115
  153.6 0.9 pad_maximum_fusion
  154.5 4.3 %all-gather.3.cloned.1.call-done = bf16[1024,512]{1,0:T(8,128)(2,1)} async-done(((bf16[256,512]{1,0:T(8,128)(2,1)}), bf16[1024,512]{1,0:T(8,128)(2,1)}) %all-gather.3.cloned.1.call-update) | async-done | bytes 1048592 | tf_op jit(solution)/shard_map/all_gather | solution.py:525
  158.7 4.2 %collective-permute-done.14.refs_12_ = bf16[256,512]{1,0:T(8,128)(2,1)S(1)} collective-permute-done((bf16[256,512]{1,0:T(8,128)(2,1)}, bf16[256,512]{1,0:T(8,128)(2,1)S(1)}, u32[]{:S(2)}, u32[]{:S(2)}) %collective-permute-start.14) | collective-permute-done | bytes 262176 | tf_op jit(solution)/shard_map/ppermute | solution.py:115
  162.9 6.5 %qkv.3 = (bf16[3,256,512]{2,1,0:T(8,128)(2,1)}, bf16[2,256,512]{2,1,0:T(8,128)(2,1)}) custom-call(s32[1]{0:T(128)} %bitcast.2.ring_ref.refs_10_.refs_1_, bf16[4,256,512]{2,1,0:T(8,128)(2,1)} %bitcast.10, f32[256,128]{1,0:T(8,128)} %get-tuple-element.126.cosine_ref, f32[256,128]{1,0:T(8,128)} %get-tuple-element.125.sine_ref, ...), custom_call_target="tpu_custom_call" | custom-call | flops 1610612736 | bytes 8912896 | tf_op jit(solution)/shard_map/qkv/pallas_call | solution.py:298
  169.4 7.4 %output.2 = (bf16[256,512]{1,0:T(8,128)(2,1)}, f32[256,512]{1,0:T(8,128)}, bf16[256,512]{1,0:T(8,128)(2,1)}, bf16[256,512]{1,0:T(8,128)(2,1)}) custom-call(bf16[3,768,512]{2,1,0:T(8,128)(2,1)} %get-tuple-element.87.refs_0_.refs_1_.refs_2_.refs_3_.refs_4_.refs_5_.refs_6_, ...), custom_call_target="tpu_custom_call" | custom-call | flops 1476395008 | bytes 2883584 | tf_op jit(solution)/shard_map/output/pallas_call | solution.py:423
  176.8 0.3 collective-permute-start.16
  177.1 0.7 collective-permute-start.25
  177.8 1.0 copy-done
  178.8 4.0 %attend.3.refs_2_ = bf16[256,512]{1,0:T(8,128)(2,1)} custom-call(bf16[3,768,512]{2,1,0:T(8,128)(2,1)} %get-tuple-element.87.refs_0_.refs_1_.refs_2_.refs_3_.refs_4_.refs_5_.refs_6_, bf16[2,512,512]{2,1,0:T(8,128)(2,1)} %copy-done, bf16[3,256,512]{2,1,0:T(8,128)(2,1)} %get-tuple-element.89.refs_1_.refs_4_.refs_0_.refs_3_.refs_6_.refs_2_.refs_5_, ...), custom_call_target="tpu_custom_call" | custom-call | flops 402653184 | bytes 786432 | tf_op jit(solution)/shard_map/attend/pallas_call | solution.py:423
  182.9 4.6 %collective-permute-start.20 = (bf16[256,512]{1,0:T(8,128)(2,1)}, bf16[256,512]{1,0:T(8,128)(2,1)S(1)}, u32[]{:S(2)}, u32[]{:S(2)}) collective-permute-start(bf16[256,512]{1,0:T(8,128)(2,1)} %attend.3.refs_2_), channel_id=1, source_target_pairs={{0,1},{1,0},{2,3},{3,2},{4,5},{5,4},{6,7},{7,6},{8,9},{9,8},{10,11... | collective-permute-start | bytes 786440 | tf_op jit(solution)/shard_map/ppermute | solution.py:115
  187.5 0.7 copy-done.11
  188.2 7.3 %output.3 = (bf16[256,512]{1,0:T(8,128)(2,1)}, f32[256,512]{1,0:T(8,128)}, bf16[256,512]{1,0:T(8,128)(2,1)}, bf16[256,512]{1,0:T(8,128)(2,1)}) custom-call(bf16[3,256,512]{2,1,0:T(8,128)(2,1)} %get-tuple-element.89.refs_1_.refs_4_.refs_0_.refs_3_.refs_6_.refs_2_.refs_5_, bf16[2,512,512]{2,1,0:T(8,128)(2,1)} %copy-done, bf16[2,512,512]{2,1,0:T(8,128)(2,1)} %copy-done, ...), custom_call_target="tpu_custom_call" | custom-call | flops 1476395008 | bytes 2883584 | tf_op jit(solution)/shard_map/output/pallas_call | solution.py:423
  195.6 1.3 collective-permute-start.26
  196.9 0.7 collective-permute-start.23
  197.6 1.3 collective-permute-start.24
  198.9 4.8 %project.3 = (f32[256,512]{1,0:T(8,128)}, bf16[256,512]{1,0:T(8,128)(2,1)}, bf16[256,512]{1,0:T(8,128)(2,1)}) custom-call(s32[1]{0:T(128)} %bitcast.1.place_ref.refs_9_.refs_0_, s32[1]{0:T(128)} %bitcast.2.ring_ref.refs_10_.refs_1_, bf16[256,512]{1,0:T(8,128)(2,1)} %attend.3.refs_2_, bf16[256,512]{1,0:T(8,128)(2,1)} %copy-done.15, ...), custom_call_target="tpu_custom_call" | custom-call | flops 1073741824 | bytes 2097152 | tf_op jit(solution)/shard_map/project/pallas_call | solution.py:423
  203.7 0.7 collective-permute-start.21
  204.3 4.5 %collective-permute-done.17.refs_3_ = bf16[256,512]{1,0:T(8,128)(2,1)S(1)} collective-permute-done((bf16[256,512]{1,0:T(8,128)(2,1)}, bf16[256,512]{1,0:T(8,128)(2,1)S(1)}, u32[]{:S(2)}, u32[]{:S(2)}) %collective-permute-start.17) | collective-permute-done | bytes 262176 | tf_op jit(solution)/shard_map/ppermute | solution.py:115
  208.8 1.3 collective-permute-start.22
  210.1 4.7 %project.2 = (f32[256,512]{1,0:T(8,128)}, bf16[256,512]{1,0:T(8,128)(2,1)}, bf16[256,512]{1,0:T(8,128)(2,1)}) custom-call(s32[1]{0:T(128)} %bitcast.1.place_ref.refs_9_.refs_0_, s32[1]{0:T(128)} %bitcast.2.ring_ref.refs_10_.refs_1_, bf16[256,512]{1,0:T(8,128)(2,1)} %get-tuple-element.96.refs_2_, bf16[256,512]{1,0:T(8,128)(2,1)} %copy-done.14, ...), custom_call_target="tpu_custom_call" | custom-call | flops 1073741824 | bytes 2097152 | tf_op jit(solution)/shard_map/project/pallas_call | solution.py:423
  214.9 0.9 collective-permute-start.18
  215.8 1.3 collective-permute-start.19
  217.1 3.4 %final.4.rest_0_ = bf16[1024,4,512]{2,1,0:T(4,128)(2,1)} custom-call(f32[4,6]{1,0:T(4,128)} %static_ref.11, bf16[1024,4,512]{2,1,0:T(4,128)(2,1)} %x_ref.13, f32[8,5248]{1,0:T(8,128)} %get-tuple-element.65.first_ref.folded_ref.column_ref, f32[8,5248]{1,0:T(8,128)} %get-tuple-element.65.first_ref.folded_ref.column_ref, ...), custom_call_target="tpu_custom_call" | custom-call | flops 629145600 | bytes 2883584 | tf_op jit(solution)/shard_map/final/pallas_call | solution.py:498
  220.6 0.7 copy-done.17
  221.3 3.4 %final.5.rest_0_ = bf16[1024,4,512]{2,1,0:T(4,128)(2,1)} custom-call(f32[4,6]{1,0:T(4,128)} %static_ref.11, bf16[1024,4,512]{2,1,0:T(4,128)(2,1)} %x_ref.13, f32[8,5248]{1,0:T(8,128)} %get-tuple-element.65.first_ref.folded_ref.column_ref, f32[8,5248]{1,0:T(8,128)} %get-tuple-element.65.first_ref.folded_ref.column_ref, ...), custom_call_target="tpu_custom_call", output_to_operand_aliasing={{}: (8, {})} | custom-call | flops 629145600 | bytes 2883584 | tf_op jit(solution)/shard_map/final/pallas_call | solution.py:498
  224.7 5.4 %collective-permute-done.22.outer_ref = bf16[256,512]{1,0:T(8,128)(2,1)S(1)} collective-permute-done((bf16[256,512]{1,0:T(8,128)(2,1)}, bf16[256,512]{1,0:T(8,128)(2,1)S(1)}, u32[]{:S(2)}, u32[]{:S(2)}) %collective-permute-start.22) | collective-permute-done | bytes 262176 | tf_op jit(solution)/shard_map/ppermute | solution.py:597
  230.1 0.7 copy-done.19
  230.8 3.4 %final.6.rest_0_ = bf16[1024,4,512]{2,1,0:T(4,128)(2,1)} custom-call(f32[4,6]{1,0:T(4,128)} %static_ref.11, bf16[1024,4,512]{2,1,0:T(4,128)(2,1)} %x_ref.13, f32[8,5248]{1,0:T(8,128)} %get-tuple-element.65.first_ref.folded_ref.column_ref, f32[8,5248]{1,0:T(8,128)} %get-tuple-element.65.first_ref.folded_ref.column_ref, ...), custom_call_target="tpu_custom_call", output_to_operand_aliasing={{}: (8, {})} | custom-call | flops 629145600 | bytes 2883584 | tf_op jit(solution)/shard_map/final/pallas_call | solution.py:498
  234.2 5.4 %collective-permute-done.19.outer_ref = bf16[256,512]{1,0:T(8,128)(2,1)S(1)} collective-permute-done((bf16[256,512]{1,0:T(8,128)(2,1)}, bf16[256,512]{1,0:T(8,128)(2,1)S(1)}, u32[]{:S(2)}, u32[]{:S(2)}) %collective-permute-start.19) | collective-permute-done | bytes 262176 | tf_op jit(solution)/shard_map/ppermute | solution.py:597
  239.6 0.7 copy-done.21
  240.3 3.4 %final.7 = bf16[1024,4,512]{2,1,0:T(4,128)(2,1)} custom-call(f32[4,6]{1,0:T(4,128)} %static_ref.11, bf16[1024,4,512]{2,1,0:T(4,128)(2,1)} %x_ref.13, f32[8,5248]{1,0:T(8,128)} %get-tuple-element.65.first_ref.folded_ref.column_ref, f32[8,5248]{1,0:T(8,128)} %get-tuple-element.65.first_ref.folded_ref.column_ref, ...), custom_call_target="tpu_custom_call", output_to_operand_aliasing={{}: (8, {})} | custom-call | flops 629145600 | bytes 2883584 | tf_op jit(solution)/shard_map/final/pallas_call | solution.py:498
  (88 shorter events, 0.8 us)
Async XLA Ops:
  6.5 122.6 %all-gather.5.cloned.1.call-start = ((), (), s32[]{:S(2)}) async-start(), calls=%async_computation.1 | async-start | bytes 3932160 | tf_op jit(solution)/shard_map/all_gather | solution.py:525
  14.4 11.0 %collective-permute-start.2 = (f32[8,5248]{1,0:T(8,128)}, f32[8,5248]{1,0:T(8,128)S(1)}, u32[]{:S(2)}, u32[]{:S(2)}) collective-permute-start(f32[8,5248]{1,0:T(8,128)} %stats.1.own_ref), channel_id=1, source_target_pairs={{0,3},{1,0},{2,1},{3,2},{4,7},{5,4},{6,5},{7,6},{8,11},{9,8},{10,9... | collective-permute-start | bytes 503816 | tf_op jit(solution)/shard_map/ppermute | solution.py:31
  19.5 14.4 %collective-permute-start.1 = (f32[8,5248]{1,0:T(8,128)}, f32[8,5248]{1,0:T(8,128)S(1)}, u32[]{:S(2)}, u32[]{:S(2)}) collective-permute-start(f32[8,5248]{1,0:T(8,128)} %stats.1.own_ref), channel_id=1, source_target_pairs={{0,2},{1,3},{2,0},{3,1},{4,6},{5,7},{6,4},{7,5},{8,10},{9,11},{10,... | collective-permute-start | bytes 503816 | tf_op jit(solution)/shard_map/ppermute | solution.py:31
  19.5 14.4 %collective-permute-start = (f32[8,5248]{1,0:T(8,128)}, f32[8,5248]{1,0:T(8,128)S(1)}, u32[]{:S(2)}, u32[]{:S(2)}) collective-permute-start(f32[8,5248]{1,0:T(8,128)} %stats.1.own_ref), channel_id=1, source_target_pairs={{0,1},{1,2},{2,3},{3,0},{4,5},{5,6},{6,7},{7,4},{8,9},{9,10},{10,1... | collective-permute-start | bytes 503816 | tf_op jit(solution)/shard_map/ppermute | solution.py:31
  25.4 14.2 %copy-start.4 = (f32[8,5248]{1,0:T(8,128)}, f32[8,5248]{1,0:T(8,128)S(1)}, u32[]{:S(2)}) copy-start(f32[8,5248]{1,0:T(8,128)S(1)} %collective-permute-done.2.c_ref) | copy-start | bytes 503812
  33.9 5.7 %copy-start.5 = (f32[8,5248]{1,0:T(8,128)}, f32[8,5248]{1,0:T(8,128)S(1)}, u32[]{:S(2)}) copy-start(f32[8,5248]{1,0:T(8,128)S(1)} %collective-permute-done.1.b_ref) | copy-start | bytes 503812
  33.9 5.7 %copy-start.6 = (f32[8,5248]{1,0:T(8,128)}, f32[8,5248]{1,0:T(8,128)S(1)}, u32[]{:S(2)}) copy-start(f32[8,5248]{1,0:T(8,128)S(1)} %collective-permute-done.a_ref) | copy-start | bytes 503812
  33.9 13.5 %collective-permute-start.3 = (bf16[64,2560]{1,0:T(8,128)(2,1)}, bf16[64,2560]{1,0:T(8,128)(2,1)S(1)}, u32[]{:S(2)}, u32[]{:S(2)}) collective-permute-start(bf16[64,2560]{1,0:T(8,128)(2,1)} %get-tuple-element.67), channel_id=1, source_target_pairs={{0,1},{1,2},{2,3},{3,0},{4,5},{5,6},{6,7},{7,4},{8,9},{9,10},{10,1... | collective-permute-start | bytes 983048 | tf_op jit(solution)/shard_map/ppermute | solution.py:529
  34.9 24.5 %collective-permute-start.4 = (bf16[64,2560]{1,0:T(8,128)(2,1)}, bf16[64,2560]{1,0:T(8,128)(2,1)S(1)}, u32[]{:S(2)}, u32[]{:S(2)}) collective-permute-start(bf16[64,2560]{1,0:T(8,128)(2,1)} %get-tuple-element.68), channel_id=1, source_target_pairs={{0,2},{1,3},{2,0},{3,1},{4,6},{5,7},{6,4},{7,5},{8,10},{9,11},{10,... | collective-permute-start | bytes 983048 | tf_op jit(solution)/shard_map/ppermute | solution.py:529
  36.8 22.7 %collective-permute-start.5 = (bf16[64,2560]{1,0:T(8,128)(2,1)}, bf16[64,2560]{1,0:T(8,128)(2,1)S(1)}, u32[]{:S(2)}, u32[]{:S(2)}) collective-permute-start(bf16[64,2560]{1,0:T(8,128)(2,1)} %get-tuple-element.69), channel_id=1, source_target_pairs={{0,3},{1,0},{2,1},{3,2},{4,7},{5,4},{6,5},{7,6},{8,11},{9,8},{10,9... | collective-permute-start | bytes 983048 | tf_op jit(solution)/shard_map/ppermute | solution.py:529
  47.4 18.9 %copy-start.23 = (s32[2]{0:T(128)S(1)}, s32[2]{0:T(128)}, u32[]{:S(2)}) copy-start(s32[2]{0:T(128)} %param.11) | copy-start | bytes 28
  47.4 20.2 %copy-start.22 = (s32[1024]{0:T(1024)S(1)}, s32[1024]{0:T(1024)}, u32[]{:S(2)}) copy-start(s32[1024]{0:T(1024)} %param.10) | copy-start | bytes 12292
  47.4 12.2 %copy-start.7 = (bf16[64,2560]{1,0:T(8,128)(2,1)}, bf16[64,2560]{1,0:T(8,128)(2,1)S(1)}, u32[]{:S(2)}) copy-start(bf16[64,2560]{1,0:T(8,128)(2,1)S(1)} %collective-permute-done.3.refs_1_) | copy-start | bytes 983044
  59.5 0.7 copy-start.8
  59.5 0.8 copy-start.9
  59.5 99.2 %all-gather.3.cloned.1.call-start = ((), (), s32[]{:S(2)}) async-start(), calls=%async_computation | async-start | bytes 1310720 | tf_op jit(solution)/shard_map/all_gather | solution.py:525
  62.8 32.9 %collective-permute-start.11 = (bf16[256,2560]{1,0:T(8,128)(2,1)}, bf16[256,2560]{1,0:T(8,128)(2,1)S(1)}, u32[]{:S(2)}, u32[]{:S(2)}) collective-permute-start(bf16[256,2560]{1,0:T(8,128)(2,1)} %assemble.1.refs_0_.refs_13_.refs_4_), channel_id=1, source_target_pairs={{0,24},{4,28},{8,16},{12,20},{16,8},{20,12},{24,0},{28,4},{1,25},{... | collective-permute-start | bytes 3932168 | tf_op jit(solution)/shard_map/ppermute | solution.py:115
  65.2 56.1 %collective-permute-start.9 = (bf16[256,2560]{1,0:T(8,128)(2,1)}, bf16[256,2560]{1,0:T(8,128)(2,1)}, u32[]{:S(2)}, u32[]{:S(2)}) collective-permute-start(bf16[256,2560]{1,0:T(8,128)(2,1)} %assemble.1.refs_0_.refs_13_.refs_4_), channel_id=1, source_target_pairs={{0,16},{4,20},{8,24},{12,28},{16,0},{20,4},{24,8},{28,12},{1,17},{... | collective-permute-start | bytes 3932168 | tf_op jit(solution)/shard_map/ppermute | solution.py:115
  65.7 55.7 %collective-permute-start.7 = (bf16[256,2560]{1,0:T(8,128)(2,1)}, bf16[256,2560]{1,0:T(8,128)(2,1)}, u32[]{:S(2)}, u32[]{:S(2)}) collective-permute-start(bf16[256,2560]{1,0:T(8,128)(2,1)} %assemble.1.refs_0_.refs_13_.refs_4_), channel_id=1, source_target_pairs={{0,8},{4,12},{8,0},{12,4},{16,24},{20,28},{24,16},{28,20},{1,9},{5... | collective-permute-start | bytes 3932168 | tf_op jit(solution)/shard_map/ppermute | solution.py:115
  67.7 55.9 %collective-permute-start.13 = (s32[512]{0:T(512)S(1)}, s32[512]{0:T(512)S(1)}, u32[]{:S(2)}, u32[]{:S(2)}) collective-permute-start(s32[512]{0:T(512)S(1)} %get-tuple-element.118), channel_id=1, source_target_pairs={{0,4},{4,8},{8,12},{12,16},{16,20},{20,24},{24,28},{1,5},{5,9},{9,... | collective-permute-start | bytes 6152 | tf_op jit(solution)/shard_map/ppermute | solution.py:25
  69.0 59.4 %collective-permute-start.6 = (bf16[256,2560]{1,0:T(8,128)(2,1)}, bf16[256,2560]{1,0:T(8,128)(2,1)}, u32[]{:S(2)}, u32[]{:S(2)}) collective-permute-start(bf16[256,2560]{1,0:T(8,128)(2,1)} %assemble.1.refs_0_.refs_13_.refs_4_), channel_id=1, source_target_pairs={{0,4},{4,0},{8,12},{12,8},{16,20},{20,16},{24,28},{28,24},{1,5},{5... | collective-permute-start | bytes 3932168 | tf_op jit(solution)/shard_map/ppermute | solution.py:115
  95.7 32.7 %copy-start.1 = (bf16[256,2560]{1,0:T(8,128)(2,1)}, bf16[256,2560]{1,0:T(8,128)(2,1)S(1)}, u32[]{:S(2)}) copy-start(bf16[256,2560]{1,0:T(8,128)(2,1)S(1)} %collective-permute-done.11.refs_6_.refs_19_.refs_10_) | copy-start | bytes 3932164
  95.7 32.7 %collective-permute-start.12 = (bf16[256,2560]{1,0:T(8,128)(2,1)S(1)}, bf16[256,2560]{1,0:T(8,128)(2,1)}, u32[]{:S(2)}, u32[]{:S(2)}) collective-permute-start(bf16[256,2560]{1,0:T(8,128)(2,1)S(1)} %collective-permute-done.11.refs_6_.refs_19_.refs_10_), channel_id=1, source_target_pairs={{0,4},{4,0},{8,12},{12,8},{16,20},{20,16},{24,28},{28,24},{1,5},{5... | collective-permute-start | bytes 3932168 | tf_op jit(solution)/shard_map/ppermute | solution.py:115
  121.3 7.1 %collective-permute-start.10 = (bf16[256,2560]{1,0:T(8,128)(2,1)}, bf16[256,2560]{1,0:T(8,128)(2,1)}, u32[]{:S(2)}, u32[]{:S(2)}) collective-permute-start(bf16[256,2560]{1,0:T(8,128)(2,1)} %collective-permute-done.9.refs_4_.refs_17_.refs_8_), channel_id=1, source_target_pairs={{0,4},{4,0},{8,12},{12,8},{16,20},{20,16},{24,28},{28,24},{1,5},{5... | collective-permute-start | bytes 3932168 | tf_op jit(solution)/shard_map/ppermute | solution.py:115
  121.4 7.0 %collective-permute-start.8 = (bf16[256,2560]{1,0:T(8,128)(2,1)}, bf16[256,2560]{1,0:T(8,128)(2,1)}, u32[]{:S(2)}, u32[]{:S(2)}) collective-permute-start(bf16[256,2560]{1,0:T(8,128)(2,1)} %collective-permute-done.7.refs_2_.refs_15_.refs_6_), channel_id=1, source_target_pairs={{0,4},{4,0},{8,12},{12,8},{16,20},{20,16},{24,28},{28,24},{1,5},{5... | collective-permute-start | bytes 3932168 | tf_op jit(solution)/shard_map/ppermute | solution.py:115
  127.2 1.2 copy-start.2
  139.7 38.1 %collective-permute-start.15 = (bf16[2,512,512]{2,1,0:T(8,128)(2,1)}, bf16[2,512,512]{2,1,0:T(8,128)(2,1)S(1)}, u32[]{:S(2)}, u32[]{:S(2)}) collective-permute-start(bf16[2,512,512]{2,1,0:T(8,128)(2,1)} %get-tuple-element.90), channel_id=1, source_target_pairs={{0,4},{4,8},{8,12},{12,16},{16,20},{20,24},{24,28},{1,5},{5,9},{9,... | collective-permute-start | bytes 3145736 | tf_op jit(solution)/shard_map/ppermute | solution.py:25
  142.4 11.3 %copy-start.3 = (f32[1024,64]{1,0:T(8,128)S(1)}, f32[1024,64]{1,0:T(8,128)}, u32[]{:S(2)}) copy-start(f32[1024,64]{1,0:T(8,128)} %copy-done.2) | copy-start | bytes 786436
  146.4 16.5 %collective-permute-start.14 = (bf16[256,512]{1,0:T(8,128)(2,1)}, bf16[256,512]{1,0:T(8,128)(2,1)S(1)}, u32[]{:S(2)}, u32[]{:S(2)}) collective-permute-start(bf16[256,512]{1,0:T(8,128)(2,1)} %attend.2.refs_11_), channel_id=1, source_target_pairs={{0,1},{1,0},{2,3},{3,2},{4,5},{5,4},{6,7},{7,6},{8,9},{9,8},{10,11... | collective-permute-start | bytes 786440 | tf_op jit(solution)/shard_map/ppermute | solution.py:115
  162.9 6.5 %copy-start.10 = (bf16[256,512]{1,0:T(8,128)(2,1)}, bf16[256,512]{1,0:T(8,128)(2,1)S(1)}, u32[]{:S(2)}) copy-start(bf16[256,512]{1,0:T(8,128)(2,1)S(1)} %collective-permute-done.14.refs_12_) | copy-start | bytes 786436
  176.8 10.7 %collective-permute-start.16 = (bf16[256,512]{1,0:T(8,128)(2,1)}, bf16[256,512]{1,0:T(8,128)(2,1)S(1)}, u32[]{:S(2)}, u32[]{:S(2)}) collective-permute-start(bf16[256,512]{1,0:T(8,128)(2,1)} %get-tuple-element.95.refs_11_), channel_id=1, source_target_pairs={{0,1},{1,0},{2,3},{3,2},{4,5},{5,4},{6,7},{7,6},{8,9},{9,8},{10,11... | collective-permute-start | bytes 786440 | tf_op jit(solution)/shard_map/ppermute | solution.py:115
  177.1 26.5 %collective-permute-start.25 = (bf16[256,512]{1,0:T(8,128)(2,1)}, bf16[256,512]{1,0:T(8,128)(2,1)S(1)}, u32[]{:S(2)}, u32[]{:S(2)}) collective-permute-start(bf16[256,512]{1,0:T(8,128)(2,1)} %get-tuple-element.107), channel_id=1, source_target_pairs={{1,2},{2,1},{5,6},{6,5},{9,10},{10,9},{13,14},{14,13},{17,18},{18,... | collective-permute-start | bytes 786440 | tf_op jit(solution)/shard_map/ppermute | solution.py:596
  177.8 1.0 copy-start
  182.9 12.7 %copy-start.24 = (bf16[256,512]{1,0:T(8,128)(2,1)S(1)}, bf16[256,512]{1,0:T(8,128)(2,1)}, u32[]{:S(2)}) copy-start(bf16[256,512]{1,0:T(8,128)(2,1)} %get-tuple-element.108) | copy-start | bytes 786436
  182.9 14.7 %collective-permute-start.20 = (bf16[256,512]{1,0:T(8,128)(2,1)}, bf16[256,512]{1,0:T(8,128)(2,1)S(1)}, u32[]{:S(2)}, u32[]{:S(2)}) collective-permute-start(bf16[256,512]{1,0:T(8,128)(2,1)} %attend.3.refs_2_), channel_id=1, source_target_pairs={{0,1},{1,0},{2,3},{3,2},{4,5},{5,4},{6,7},{7,6},{8,9},{9,8},{10,11... | collective-permute-start | bytes 786440 | tf_op jit(solution)/shard_map/ppermute | solution.py:115
  187.5 0.7 copy-start.11
  195.5 13.3 %collective-permute-start.17 = (bf16[256,512]{1,0:T(8,128)(2,1)}, bf16[256,512]{1,0:T(8,128)(2,1)S(1)}, u32[]{:S(2)}, u32[]{:S(2)}) collective-permute-start(bf16[256,512]{1,0:T(8,128)(2,1)} %get-tuple-element.96.refs_2_), channel_id=1, source_target_pairs={{0,1},{1,0},{2,3},{3,2},{4,5},{5,4},{6,7},{7,6},{8,9},{9,8},{10,11... | collective-permute-start | bytes 786440 | tf_op jit(solution)/shard_map/ppermute | solution.py:115
  195.6 19.3 %collective-permute-start.26 = (bf16[256,512]{1,0:T(8,128)(2,1)S(1)}, bf16[256,512]{1,0:T(8,128)(2,1)S(1)}, u32[]{:S(2)}, u32[]{:S(2)}) collective-permute-start(bf16[256,512]{1,0:T(8,128)(2,1)S(1)} %copy-done.24), channel_id=1, source_target_pairs={{1,3},{2,0},{5,7},{6,4},{9,11},{10,8},{13,15},{14,12},{17,19},{18,... | collective-permute-start | bytes 786440 | tf_op jit(solution)/shard_map/ppermute | solution.py:597
  196.9 18.9 %collective-permute-start.23 = (bf16[256,512]{1,0:T(8,128)(2,1)}, bf16[256,512]{1,0:T(8,128)(2,1)S(1)}, u32[]{:S(2)}, u32[]{:S(2)}) collective-permute-start(bf16[256,512]{1,0:T(8,128)(2,1)} %get-tuple-element.104), channel_id=1, source_target_pairs={{1,2},{2,1},{5,6},{6,5},{9,10},{10,9},{13,14},{14,13},{17,18},{18,... | collective-permute-start | bytes 786440 | tf_op jit(solution)/shard_map/ppermute | solution.py:596
  197.6 1.3 copy-start.15
  197.6 23.0 %collective-permute-start.24 = (bf16[256,512]{1,0:T(8,128)(2,1)}, bf16[256,512]{1,0:T(8,128)(2,1)S(1)}, u32[]{:S(2)}, u32[]{:S(2)}) collective-permute-start(bf16[256,512]{1,0:T(8,128)(2,1)} %get-tuple-element.105), channel_id=1, source_target_pairs={{1,3},{2,0},{5,7},{6,4},{9,11},{10,8},{13,15},{14,12},{17,19},{18,... | collective-permute-start | bytes 786440 | tf_op jit(solution)/shard_map/ppermute | solution.py:597
  203.7 11.2 %copy-start.12 = (bf16[256,512]{1,0:T(8,128)(2,1)}, bf16[256,512]{1,0:T(8,128)(2,1)S(1)}, u32[]{:S(2)}) copy-start(bf16[256,512]{1,0:T(8,128)(2,1)S(1)} %collective-permute-done.25.inner_ref) | copy-start | bytes 786436
  203.7 21.0 %collective-permute-start.21 = (bf16[256,512]{1,0:T(8,128)(2,1)}, bf16[256,512]{1,0:T(8,128)(2,1)S(1)}, u32[]{:S(2)}, u32[]{:S(2)}) collective-permute-start(bf16[256,512]{1,0:T(8,128)(2,1)} %get-tuple-element.101), channel_id=1, source_target_pairs={{1,2},{2,1},{5,6},{6,5},{9,10},{10,9},{13,14},{14,13},{17,18},{18,... | collective-permute-start | bytes 786440 | tf_op jit(solution)/shard_map/ppermute | solution.py:596
  208.8 1.3 copy-start.14
  208.8 21.3 %collective-permute-start.22 = (bf16[256,512]{1,0:T(8,128)(2,1)}, bf16[256,512]{1,0:T(8,128)(2,1)S(1)}, u32[]{:S(2)}, u32[]{:S(2)}) collective-permute-start(bf16[256,512]{1,0:T(8,128)(2,1)} %get-tuple-element.102), channel_id=1, source_target_pairs={{1,3},{2,0},{5,7},{6,4},{9,11},{10,8},{13,15},{14,12},{17,19},{18,... | collective-permute-start | bytes 786440 | tf_op jit(solution)/shard_map/ppermute | solution.py:597
  214.9 2.2 copy-start.13
  214.9 19.3 %collective-permute-start.18 = (bf16[256,512]{1,0:T(8,128)(2,1)}, bf16[256,512]{1,0:T(8,128)(2,1)S(1)}, u32[]{:S(2)}, u32[]{:S(2)}) collective-permute-start(bf16[256,512]{1,0:T(8,128)(2,1)} %get-tuple-element.98), channel_id=1, source_target_pairs={{1,2},{2,1},{5,6},{6,5},{9,10},{10,9},{13,14},{14,13},{17,18},{18,... | collective-permute-start | bytes 786440 | tf_op jit(solution)/shard_map/ppermute | solution.py:596
  215.8 4.8 %copy-start.16 = (bf16[256,512]{1,0:T(8,128)(2,1)}, bf16[256,512]{1,0:T(8,128)(2,1)S(1)}, u32[]{:S(2)}) copy-start(bf16[256,512]{1,0:T(8,128)(2,1)S(1)} %collective-permute-done.23.inner_ref) | copy-start | bytes 786436
  215.8 23.8 %collective-permute-start.19 = (bf16[256,512]{1,0:T(8,128)(2,1)}, bf16[256,512]{1,0:T(8,128)(2,1)S(1)}, u32[]{:S(2)}, u32[]{:S(2)}) collective-permute-start(bf16[256,512]{1,0:T(8,128)(2,1)} %get-tuple-element.99), channel_id=1, source_target_pairs={{1,3},{2,0},{5,7},{6,4},{9,11},{10,8},{13,15},{14,12},{17,19},{18,... | collective-permute-start | bytes 786440 | tf_op jit(solution)/shard_map/ppermute | solution.py:597
  220.6 0.7 copy-start.17
  224.7 5.4 %copy-start.18 = (bf16[256,512]{1,0:T(8,128)(2,1)}, bf16[256,512]{1,0:T(8,128)(2,1)S(1)}, u32[]{:S(2)}) copy-start(bf16[256,512]{1,0:T(8,128)(2,1)S(1)} %collective-permute-done.21.inner_ref) | copy-start | bytes 786436
  230.1 0.7 copy-start.19
  234.2 5.4 %copy-start.20 = (bf16[256,512]{1,0:T(8,128)(2,1)}, bf16[256,512]{1,0:T(8,128)(2,1)S(1)}, u32[]{:S(2)}) copy-start(bf16[256,512]{1,0:T(8,128)(2,1)S(1)} %collective-permute-done.18.inner_ref) | copy-start | bytes 786436
  239.6 0.7 copy-start.21
Sparse Core Ops, SparseCore 0:
  59.6 69.4 all-gather.4
  130.7 28.0 all-gather.2

commit v12 on v10

--- a/solution.py
+++ b/solution.py
@@ -121,7 +121,14 @@
         return [lax.all_gather(part, "blk", axis=0, tiled=True)]
     pieces = {0: part}
     for mask in range(2, count, 2):
-        pieces[mask] = swapped(part, "blk", mask)
+        if mask & (mask - 1):
+            low = mask & -mask
+            cut = part.shape[0] // 2
+            halves = [swapped(pieces[mask ^ low][:cut], "blk", low)]
+            halves.append(swapped(pieces[low][cut:], "blk", mask ^ low))
+            pieces[mask] = jnp.concatenate(halves, axis=0)
+        else:
+            pieces[mask] = swapped(part, "blk", mask)
     for mask in range(0, count, 2):
         pieces[mask + 1] = swapped(pieces[mask], "blk", 1)
     return [pieces[mask] for mask in range(count)]
@@ -570,9 +577,9 @@
     result = None
     for chunk in reversed(range(last + 1)):
         kept, inner, outer = parts[chunk]
+        outer = lax.ppermute(outer, "mp", [(1, 3), (2, 0)])
         inner = lax.ppermute(inner, "mp", [(1, 2), (2, 1)])
-        outer = lax.ppermute(outer, "mp", [(1, 3), (2, 0)])
-        updates = [kept, inner, outer]
+        updates = [kept, outer, inner]
         result = final(hc_static, streams, sums_all, updates, chunk * CHUNK, result)
     return result
 

time: 251 us -> 247 us (0.984)
  starting transfers between devices: 41.7 us -> 36.1 us
  local copies, waits for them, and re-layouts: 7.13 us -> 10.3 us
    all_gather x2, waiting for transfers between devices: 4.54 us -> 24.6 us  [gathered(): rows = lax.all_gather(normed, 'mp', axis=0, tiled=True)]
    ppermute x11 -> x12, waiting for transfers between devices: 54.8 us -> 36.9 us  [swapped(): lax.ppermute(value, axis, [(source, source ^ mask) for source in range(co...]
    ppermute x11 -> x12, starting transfers between devices: 18.4 us -> 12.9 us  [swapped(): lax.ppermute(value, axis, [(source, source ^ mask) for source in range(co...]
    ppermute x4, waiting for transfers between devices: 11.6 us -> 7.31 us  [body(): outer = lax.ppermute(outer, 'mp', [(1, 3), (2, 0)])]
    unnamed x50 -> x57, local copies, waits for them, and re-layouts: 4.66 us -> 5.74 us
  transfers between devices with their start and end apart: 29 -> 30, of which waited for: 10 -> 11; matrix products, arithmetic and copies ran while one was open for 3% -> 4% of each run, Pallas kernels for 31% -> 32%
where the time goes in v12:
time: 247 us; the launch traced here: 245 us
  waiting for transfers between devices  89.5 us (36%)
  Pallas kernels  87 us (35%)
  starting transfers between devices  36.1 us (15%)
  between operations  15.2 us (6%)
  local copies, waits for them, and re-layouts  10.3 us (4%)
  other arithmetic  7.04 us (3%)
    ppermute x12, waiting for transfers between devices, swapped(): lax.ppermute(value, axis, [(source, source ^ mask) for source in range(co...  36.9 us
    all_gather x2, waiting for transfers between devices, gathered(): rows = lax.all_gather(normed, 'mp', axis=0, tiled=True)  24.6 us
    pallas_call x4, Pallas kernels, project(): pl.pallas_call(project_kernel, grid=(1,), in_specs=[pl.BlockSpec(memory_s...  18.7 us
    pallas_call x2, Pallas kernels, qkv_columns(): pl.pallas_call(qkv_kernel, grid=(3,), in_specs=[pl.BlockSpec(memory_space...  17.1 us
    pallas_call x4, Pallas kernels, attend(): pl.pallas_call(attend_kernel, grid=(1,), in_specs=[pl.BlockSpec(block, la...  16.2 us
    pallas_call x4, Pallas kernels, final(): pl.pallas_call(final_kernel, grid=(tokens // STEP,), in_specs=specs, out_...  13.6 us
    ppermute x12, starting transfers between devices, swapped(): lax.ppermute(value, axis, [(source, source ^ mask) for source in range(co...  12.9 us
    ppermute x3, waiting for transfers between devices, body(): lax.ppermute(parts[step], 'mp', [(at, (at + step) % group_size) for at in...  12.1 us
  transfers between devices with their start and end apart: 30, of which 11 were waited for; matrix products, arithmetic and copies ran while one was open for 4% of the time, Pallas kernels for 32%

profile of v12, /device:TPU:0, one launch (start us, length us, event | category | flops | bytes accessed | tf_op | source)
XLA Modules:
  0.0 245.1 jit_solution(17222720656940987055)
XLA Ops:
  6.7 1.4 maximum_maximum_fusion.proj_ref
  8.1 6.4 %stats.1.own_ref = f32[8,5248]{1,0:T(8,128)} custom-call(bf16[1024,4,512]{2,1,0:T(4,128)(2,1)} %x_ref.13, f32[8,512]{1,0:T(8,128)} %maximum_maximum_fusion.proj_ref), custom_call_target="tpu_custom_call" | custom-call | flops 1258291200 | bytes 4194304 | tf_op jit(solution)/shard_map/stats/pallas_call | solution.py:178
  14.4 5.0 %collective-permute-start.2 = (f32[8,5248]{1,0:T(8,128)}, f32[8,5248]{1,0:T(8,128)S(1)}, u32[]{:S(2)}, u32[]{:S(2)}) collective-permute-start(f32[8,5248]{1,0:T(8,128)} %stats.1.own_ref), channel_id=1, source_target_pairs={{0,3},{1,0},{2,1},{3,2},{4,7},{5,4},{6,5},{7,6},{8,11},{9,8},{10,9... | collective-permute-start | bytes 503816 | tf_op jit(solution)/shard_map/ppermute | solution.py:31
  19.5 1.0 collective-permute-start
  20.5 4.9 %regroup.1 = (bf16[64,2560]{1,0:T(8,128)(2,1)}, bf16[64,2560]{1,0:T(8,128)(2,1)}, bf16[64,2560]{1,0:T(8,128)(2,1)}, bf16[64,2560]{1,0:T(8,128)(2,1)}) custom-call(s32[1]{0:T(128)} %bitcast.1.place_ref, f32[64,4,2048]{2,1,0:T(4,128)} %master_ref.1), custom_call_target="tpu_custom_call" | custom-call | bytes 3407872 | tf_op jit(solution)/shard_map/regroup/pallas_call | solution.py:79
  25.4 8.5 %collective-permute-done.1.b_ref = f32[8,5248]{1,0:T(8,128)S(1)} collective-permute-done((f32[8,5248]{1,0:T(8,128)}, f32[8,5248]{1,0:T(8,128)S(1)}, u32[]{:S(2)}, u32[]{:S(2)}) %collective-permute-start.1) | collective-permute-done | bytes 167968 | tf_op jit(solution)/shard_map/ppermute | solution.py:31
  33.9 1.0 collective-permute-start.3
  34.9 1.8 collective-permute-start.4
  36.7 2.9 %collective-permute-start.5 = (bf16[64,2560]{1,0:T(8,128)(2,1)}, bf16[64,2560]{1,0:T(8,128)(2,1)S(1)}, u32[]{:S(2)}, u32[]{:S(2)}) collective-permute-start(bf16[64,2560]{1,0:T(8,128)(2,1)} %get-tuple-element.65), channel_id=1, source_target_pairs={{0,3},{1,0},{2,1},{3,2},{4,7},{5,4},{6,5},{7,6},{8,11},{9,8},{10,9... | collective-permute-start | bytes 983048 | tf_op jit(solution)/shard_map/ppermute | solution.py:519
  39.7 2.9 %mix.3 = (f32[8,5248]{1,0:T(8,128)}, bf16[256,512]{1,0:T(8,128)(2,1)}) custom-call(f32[4,6]{1,0:T(4,128)} %static_ref.11, bf16[1024,4,512]{2,1,0:T(4,128)(2,1)} %x_ref.13, f32[8,5248]{1,0:T(8,128)} %stats.1.own_ref, f32[8,5248]{1,0:T(8,128)} %copy-done.9, f32[8,5248]{1,0:T(8,128)} %copy-done.8, f32[8,5248]{1,0:T(8,128)} %copy-done.7), custom_call_target="tpu_custom_call" | custom-call | flops 209715200 | bytes 1310720 | tf_op jit(solution)/shard_map/mix/pallas_call | solution.py:249
  42.6 4.9 %mix.2 = (f32[8,5248]{1,0:T(8,128)}, bf16[768,512]{1,0:T(8,128)(2,1)}) custom-call(f32[4,6]{1,0:T(4,128)} %static_ref.11, bf16[1024,4,512]{2,1,0:T(4,128)(2,1)} %x_ref.13, f32[8,5248]{1,0:T(8,128)} %stats.1.own_ref, f32[8,5248]{1,0:T(8,128)} %copy-done.9, f32[8,5248]{1,0:T(8,128)} %copy-done.8, f32[8,5248]{1,0:T(8,128)} %copy-done.7), custom_call_target="tpu_custom_call" | custom-call | flops 629145600 | bytes 3932160 | tf_op jit(solution)/shard_map/mix/pallas_call | solution.py:249
  47.4 12.1 %collective-permute-done.4.refs_2_ = bf16[64,2560]{1,0:T(8,128)(2,1)S(1)} collective-permute-done((bf16[64,2560]{1,0:T(8,128)(2,1)}, bf16[64,2560]{1,0:T(8,128)(2,1)S(1)}, u32[]{:S(2)}, u32[]{:S(2)}) %collective-permute-start.4) | collective-permute-done | bytes 327712 | tf_op jit(solution)/shard_map/ppermute | solution.py:519
  60.3 2.5 %assemble.1.refs_0_ = bf16[256,2560]{1,0:T(8,128)(2,1)} custom-call(s32[1]{0:T(128)} %bitcast.1.place_ref, bf16[64,2560]{1,0:T(8,128)(2,1)} %get-tuple-element.70.refs_0_, bf16[64,2560]{1,0:T(8,128)(2,1)} %copy-done.10, bf16[64,2560]{1,0:T(8,128)(2,1)} %copy-done.11, bf16[64,2560]{1,0:T(8,128)(2,1)} %copy-done.12), custom_call_target="tpu_custom_call" | custom-call | bytes 2621440 | tf_op jit(solution)/shard_map/assemble/pallas_call | solution.py:101
  62.8 1.6 collective-permute-start.9
  64.4 1.5 collective-permute-start.7
  65.9 26.4 %collective-permute-done.9.refs_4_ = bf16[256,2560]{1,0:T(8,128)(2,1)S(1)} collective-permute-done((bf16[256,2560]{1,0:T(8,128)(2,1)}, bf16[256,2560]{1,0:T(8,128)(2,1)S(1)}, u32[]{:S(2)}, u32[]{:S(2)}) %collective-permute-start.9) | collective-permute-done | bytes 1310752 | tf_op jit(solution)/shard_map/ppermute | solution.py:115
  92.3 1.5 collective-permute-start.11
  94.4 1.1 slice.59
  95.5 1.1 collective-permute-start.12
  97.9 1.3 collective-permute-start.14
  99.2 1.3 collective-permute-start.6
  100.6 6.9 %collective-permute-done.11 = bf16[128,2560]{1,0:T(8,128)(2,1)S(1)} collective-permute-done((bf16[128,2560]{1,0:T(8,128)(2,1)S(1)}, bf16[128,2560]{1,0:T(8,128)(2,1)S(1)}, u32[]{:S(2)}, u32[]{:S(2)}) %collective-permute-start.11) | collective-permute-done | bytes 655392 | tf_op jit(solution)/shard_map/ppermute | solution.py:115
  107.6 0.9 constant_dynamic-update-slice_fusion.1
  108.4 0.7 collective-permute-done.12
  109.1 0.9 constant_dynamic-update-slice_fusion.refs_6_
  110.8 1.6 convert_reduce_fusion
  112.4 1.9 multiply_sine_fusion
  114.3 1.2 fusion.1
  115.6 13.5 %all-gather.5.cloned.1.call-done = bf16[3072,512]{1,0:T(8,128)(2,1)} async-done(((bf16[768,512]{1,0:T(8,128)(2,1)}), bf16[3072,512]{1,0:T(8,128)(2,1)}) %all-gather.5.cloned.1.call-update) | async-done | bytes 3145744 | tf_op jit(solution)/shard_map/all_gather | solution.py:515
  129.1 10.6 %qkv.2 = (bf16[3,768,512]{2,1,0:T(8,128)(2,1)}, bf16[2,512,512]{2,1,0:T(8,128)(2,1)}) custom-call(s32[1]{0:T(128)} %bitcast.2.ring_ref, bf16[4,768,512]{2,1,0:T(8,128)(2,1)} %bitcast.13, f32[768,128]{1,0:T(8,128)} %get-tuple-element.116.cosine_ref, f32[768,128]{1,0:T(8,128)} %get-tuple-element.115.sine_ref, bf16[256,2560]{1,0:T(8,128)(2,1)} %assemble.1.refs_0_, ...), custom_call_target="tpu_custom_call" | custom-call | flops 4831838208 | bytes 14155776 | tf_op jit(solution)/shard_map/qkv/pallas_call | solution.py:305
  139.7 1.9 collective-permute-start.16
  141.7 1.0 copy.14.qseg_ref
  143.4 4.1 %attend.4.own_ref = bf16[256,512]{1,0:T(8,128)(2,1)} custom-call(bf16[3,768,512]{2,1,0:T(8,128)(2,1)} %get-tuple-element.83.q_ref.k0.k1.k2.v0.v1.v2, bf16[3,768,512]{2,1,0:T(8,128)(2,1)} %get-tuple-element.83.q_ref.k0.k1.k2.v0.v1.v2, bf16[3,768,512]{2,1,0:T(8,128)(2,1)} %get-tuple-element.83.q_ref.k0.k1.k2.v0.v1.v2, ...), custom_call_target="tpu_custom_call" | custom-call | flops 402653184 | bytes 2097152 | tf_op jit(solution)/shard_map/attend/pallas_call | solution.py:359
  147.6 0.9 pad_maximum_fusion
  148.4 11.1 %all-gather.3.cloned.1.call-done = bf16[1024,512]{1,0:T(8,128)(2,1)} async-done(((bf16[256,512]{1,0:T(8,128)(2,1)}), bf16[1024,512]{1,0:T(8,128)(2,1)}) %all-gather.3.cloned.1.call-update) | async-done | bytes 1048592 | tf_op jit(solution)/shard_map/all_gather | solution.py:515
  159.5 2.4 collective-permute-done.15.other_ref
  161.9 6.5 %qkv.3 = (bf16[3,256,512]{2,1,0:T(8,128)(2,1)}, bf16[2,256,512]{2,1,0:T(8,128)(2,1)}) custom-call(s32[1]{0:T(128)} %bitcast.2.ring_ref, bf16[4,256,512]{2,1,0:T(8,128)(2,1)} %bitcast.10, f32[256,128]{1,0:T(8,128)} %get-tuple-element.118.cosine_ref, f32[256,128]{1,0:T(8,128)} %get-tuple-element.117.sine_ref, bf16[256,2560]{1,0:T(8,128)(2,1)} %assemble.1.refs_0_, ...), custom_call_target="tpu_custom_call" | custom-call | flops 1610612736 | bytes 8912896 | tf_op jit(solution)/shard_map/qkv/pallas_call | solution.py:305
  168.4 4.0 %attend.7.own_ref = bf16[256,512]{1,0:T(8,128)(2,1)} custom-call(bf16[3,768,512]{2,1,0:T(8,128)(2,1)} %get-tuple-element.83.q_ref.k0.k1.k2.v0.v1.v2, bf16[3,256,512]{2,1,0:T(8,128)(2,1)} %get-tuple-element.85.q_ref.k2.v2.k1.v1.k0.v0, bf16[3,768,512]{2,1,0:T(8,128)(2,1)} %get-tuple-element.83.q_ref.k0.k1.k2.v0.v1.v2, ...), custom_call_target="tpu_custom_call" | custom-call | flops 402653184 | bytes 2097152 | tf_op jit(solution)/shard_map/attend/pallas_call | solution.py:359
  172.4 2.4 collective-permute-start.23
  174.8 1.0 copy-done.2
  175.8 4.0 %attend.6.own_ref = bf16[256,512]{1,0:T(8,128)(2,1)} custom-call(bf16[3,768,512]{2,1,0:T(8,128)(2,1)} %get-tuple-element.83.q_ref.k0.k1.k2.v0.v1.v2, bf16[2,512,512]{2,1,0:T(8,128)(2,1)} %copy-done.2, bf16[3,256,512]{2,1,0:T(8,128)(2,1)} %get-tuple-element.85.q_ref.k2.v2.k1.v1.k0.v0, bf16[3,768,512]{2,1,0:T(8,128)(2,1)} %get-tuple-element.83.q_ref.k0.k1.k2.v0.v1.v2, ...), custom_call_target="tpu_custom_call" | custom-call | flops 402653184 | bytes 2097152 | tf_op jit(solution)/shard_map/attend/pallas_call | solution.py:359
  179.8 4.6 %project.7 = (f32[256,512]{1,0:T(8,128)}, bf16[256,512]{1,0:T(8,128)(2,1)}, bf16[256,512]{1,0:T(8,128)(2,1)}) custom-call(s32[1]{0:T(128)} %bitcast.1.place_ref, s32[1]{0:T(128)} %bitcast.2.ring_ref, bf16[256,512]{1,0:T(8,128)(2,1)} %attend.4.own_ref, bf16[256,512]{1,0:T(8,128)(2,1)} %copy-done.17, bf16[256,2560]{1,0:T(8,128)(2,1)} %assemble.1.refs_0_, ...), custom_call_target="tpu_custom_call" | custom-call | flops 1073741824 | bytes 5767168 | tf_op jit(solution)/shard_map/project/pallas_call | solution.py:409
  184.5 1.4 collective-permute-start.26
  185.9 4.0 %attend.5.own_ref = bf16[256,512]{1,0:T(8,128)(2,1)} custom-call(bf16[3,256,512]{2,1,0:T(8,128)(2,1)} %get-tuple-element.85.q_ref.k2.v2.k1.v1.k0.v0, bf16[2,512,512]{2,1,0:T(8,128)(2,1)} %copy-done.2, bf16[2,512,512]{2,1,0:T(8,128)(2,1)} %copy-done.2, bf16[3,256,512]{2,1,0:T(8,128)(2,1)} %get-tuple-element.85.q_ref.k2.v2.k1.v1.k0.v0, ...), custom_call_target="tpu_custom_call" | custom-call | flops 402653184 | bytes 2097152 | tf_op jit(solution)/shard_map/attend/pallas_call | solution.py:359
  189.9 3.4 %collective-permute-start.17 = (bf16[256,512]{1,0:T(8,128)(2,1)}, bf16[256,512]{1,0:T(8,128)(2,1)S(1)}, u32[]{:S(2)}, u32[]{:S(2)}) collective-permute-start(bf16[256,512]{1,0:T(8,128)(2,1)} %attend.5.own_ref), channel_id=1, source_target_pairs={{0,1},{1,0},{2,3},{3,2},{4,5},{5,4},{6,7},{7,6},{8,9},{9,8},{10,11... | collective-permute-start | bytes 786440 | tf_op jit(solution)/shard_map/ppermute | solution.py:115
  193.3 0.7 collective-permute-start.27
  194.0 0.7 copy-done.18
  194.7 4.7 %project.6 = (f32[256,512]{1,0:T(8,128)}, bf16[256,512]{1,0:T(8,128)(2,1)}, bf16[256,512]{1,0:T(8,128)(2,1)}) custom-call(s32[1]{0:T(128)} %bitcast.1.place_ref, s32[1]{0:T(128)} %bitcast.2.ring_ref, bf16[256,512]{1,0:T(8,128)(2,1)} %attend.7.own_ref, bf16[256,512]{1,0:T(8,128)(2,1)} %copy-done.18, bf16[256,2560]{1,0:T(8,128)(2,1)} %assemble.1.refs_0_, ...), custom_call_target="tpu_custom_call" | custom-call | flops 1073741824 | bytes 5767168 | tf_op jit(solution)/shard_map/project/pallas_call | solution.py:409
  199.3 1.3 collective-permute-start.24
  200.7 0.9 collective-permute-start.25
  201.6 4.7 %project.5 = (f32[256,512]{1,0:T(8,128)}, bf16[256,512]{1,0:T(8,128)(2,1)}, bf16[256,512]{1,0:T(8,128)(2,1)}) custom-call(s32[1]{0:T(128)} %bitcast.1.place_ref, s32[1]{0:T(128)} %bitcast.2.ring_ref, bf16[256,512]{1,0:T(8,128)(2,1)} %attend.6.own_ref, bf16[256,512]{1,0:T(8,128)(2,1)} %copy-done.16, bf16[256,2560]{1,0:T(8,128)(2,1)} %assemble.1.refs_0_, ...), custom_call_target="tpu_custom_call" | custom-call | flops 1073741824 | bytes 5767168 | tf_op jit(solution)/shard_map/project/pallas_call | solution.py:409
  206.3 1.3 collective-permute-start.21
  207.6 0.7 collective-permute-start.22
  208.3 4.7 %project.4 = (f32[256,512]{1,0:T(8,128)}, bf16[256,512]{1,0:T(8,128)(2,1)}, bf16[256,512]{1,0:T(8,128)(2,1)}) custom-call(s32[1]{0:T(128)} %bitcast.1.place_ref, s32[1]{0:T(128)} %bitcast.2.ring_ref, bf16[256,512]{1,0:T(8,128)(2,1)} %attend.5.own_ref, bf16[256,512]{1,0:T(8,128)(2,1)} %copy-done.15, bf16[256,2560]{1,0:T(8,128)(2,1)} %assemble.1.refs_0_, ...), custom_call_target="tpu_custom_call" | custom-call | flops 1073741824 | bytes 5767168 | tf_op jit(solution)/shard_map/project/pallas_call | solution.py:409
  213.0 1.3 collective-permute-start.18
  214.3 0.7 collective-permute-start.19
  215.0 3.4 %final.4.rest_0_ = bf16[1024,4,512]{2,1,0:T(4,128)(2,1)} custom-call(f32[4,6]{1,0:T(4,128)} %static_ref.11, bf16[1024,4,512]{2,1,0:T(4,128)(2,1)} %x_ref.13, f32[8,5248]{1,0:T(8,128)} %get-tuple-element.61.first_ref.folded_ref.column_ref, f32[8,5248]{1,0:T(8,128)} %get-tuple-element.61.first_ref.folded_ref.column_ref, ...), custom_call_target="tpu_custom_call" | custom-call | flops 629145600 | bytes 2883584 | tf_op jit(solution)/shard_map/final/pallas_call | solution.py:488
  218.5 0.7 copy-done.20
  219.2 3.4 %final.5.rest_0_ = bf16[1024,4,512]{2,1,0:T(4,128)(2,1)} custom-call(f32[4,6]{1,0:T(4,128)} %static_ref.11, bf16[1024,4,512]{2,1,0:T(4,128)(2,1)} %x_ref.13, f32[8,5248]{1,0:T(8,128)} %get-tuple-element.61.first_ref.folded_ref.column_ref, f32[8,5248]{1,0:T(8,128)} %get-tuple-element.61.first_ref.folded_ref.column_ref, ...), custom_call_target="tpu_custom_call", output_to_operand_aliasing={{}: (8, {})} | custom-call | flops 629145600 | bytes 2883584 | tf_op jit(solution)/shard_map/final/pallas_call | solution.py:488
  222.8 0.7 copy-done.21
  223.6 3.4 %final.6.rest_0_ = bf16[1024,4,512]{2,1,0:T(4,128)(2,1)} custom-call(f32[4,6]{1,0:T(4,128)} %static_ref.11, bf16[1024,4,512]{2,1,0:T(4,128)(2,1)} %x_ref.13, f32[8,5248]{1,0:T(8,128)} %get-tuple-element.61.first_ref.folded_ref.column_ref, f32[8,5248]{1,0:T(8,128)} %get-tuple-element.61.first_ref.folded_ref.column_ref, ...), custom_call_target="tpu_custom_call", output_to_operand_aliasing={{}: (8, {})} | custom-call | flops 629145600 | bytes 2883584 | tf_op jit(solution)/shard_map/final/pallas_call | solution.py:488
  227.0 7.0 %collective-permute-done.18.inner_ref = bf16[256,512]{1,0:T(8,128)(2,1)S(1)} collective-permute-done((bf16[256,512]{1,0:T(8,128)(2,1)}, bf16[256,512]{1,0:T(8,128)(2,1)S(1)}, u32[]{:S(2)}, u32[]{:S(2)}) %collective-permute-start.18) | collective-permute-done | bytes 262176 | tf_op jit(solution)/shard_map/ppermute | solution.py:580
  234.1 0.7 copy-done.23
  234.9 3.4 %final.7 = bf16[1024,4,512]{2,1,0:T(4,128)(2,1)} custom-call(f32[4,6]{1,0:T(4,128)} %static_ref.11, bf16[1024,4,512]{2,1,0:T(4,128)(2,1)} %x_ref.13, f32[8,5248]{1,0:T(8,128)} %get-tuple-element.61.first_ref.folded_ref.column_ref, f32[8,5248]{1,0:T(8,128)} %get-tuple-element.61.first_ref.folded_ref.column_ref, ...), custom_call_target="tpu_custom_call", output_to_operand_aliasing={{}: (8, {})} | custom-call | flops 629145600 | bytes 2883584 | tf_op jit(solution)/shard_map/final/pallas_call | solution.py:488
  (102 shorter events, 3.6 us)
Async XLA Ops:
  6.5 122.6 %all-gather.5.cloned.1.call-start = ((), (), s32[]{:S(2)}) async-start(), calls=%async_computation.1 | async-start | bytes 3932160 | tf_op jit(solution)/shard_map/all_gather | solution.py:515
  14.4 11.0 %collective-permute-start.2 = (f32[8,5248]{1,0:T(8,128)}, f32[8,5248]{1,0:T(8,128)S(1)}, u32[]{:S(2)}, u32[]{:S(2)}) collective-permute-start(f32[8,5248]{1,0:T(8,128)} %stats.1.own_ref), channel_id=1, source_target_pairs={{0,3},{1,0},{2,1},{3,2},{4,7},{5,4},{6,5},{7,6},{8,11},{9,8},{10,9... | collective-permute-start | bytes 503816 | tf_op jit(solution)/shard_map/ppermute | solution.py:31
  19.5 14.4 %collective-permute-start.1 = (f32[8,5248]{1,0:T(8,128)}, f32[8,5248]{1,0:T(8,128)S(1)}, u32[]{:S(2)}, u32[]{:S(2)}) collective-permute-start(f32[8,5248]{1,0:T(8,128)} %stats.1.own_ref), channel_id=1, source_target_pairs={{0,2},{1,3},{2,0},{3,1},{4,6},{5,7},{6,4},{7,5},{8,10},{9,11},{10,... | collective-permute-start | bytes 503816 | tf_op jit(solution)/shard_map/ppermute | solution.py:31
  19.5 14.4 %collective-permute-start = (f32[8,5248]{1,0:T(8,128)}, f32[8,5248]{1,0:T(8,128)S(1)}, u32[]{:S(2)}, u32[]{:S(2)}) collective-permute-start(f32[8,5248]{1,0:T(8,128)} %stats.1.own_ref), channel_id=1, source_target_pairs={{0,1},{1,2},{2,3},{3,0},{4,5},{5,6},{6,7},{7,4},{8,9},{9,10},{10,1... | collective-permute-start | bytes 503816 | tf_op jit(solution)/shard_map/ppermute | solution.py:31
  25.4 14.2 %copy-start.7 = (f32[8,5248]{1,0:T(8,128)}, f32[8,5248]{1,0:T(8,128)S(1)}, u32[]{:S(2)}) copy-start(f32[8,5248]{1,0:T(8,128)S(1)} %collective-permute-done.2.c_ref) | copy-start | bytes 503812
  33.9 5.7 %copy-start.8 = (f32[8,5248]{1,0:T(8,128)}, f32[8,5248]{1,0:T(8,128)S(1)}, u32[]{:S(2)}) copy-start(f32[8,5248]{1,0:T(8,128)S(1)} %collective-permute-done.1.b_ref) | copy-start | bytes 503812
  33.9 5.7 %copy-start.9 = (f32[8,5248]{1,0:T(8,128)}, f32[8,5248]{1,0:T(8,128)S(1)}, u32[]{:S(2)}) copy-start(f32[8,5248]{1,0:T(8,128)S(1)} %collective-permute-done.a_ref) | copy-start | bytes 503812
  33.9 13.5 %collective-permute-start.3 = (bf16[64,2560]{1,0:T(8,128)(2,1)}, bf16[64,2560]{1,0:T(8,128)(2,1)S(1)}, u32[]{:S(2)}, u32[]{:S(2)}) collective-permute-start(bf16[64,2560]{1,0:T(8,128)(2,1)} %get-tuple-element.63), channel_id=1, source_target_pairs={{0,1},{1,2},{2,3},{3,0},{4,5},{5,6},{6,7},{7,4},{8,9},{9,10},{10,1... | collective-permute-start | bytes 983048 | tf_op jit(solution)/shard_map/ppermute | solution.py:519
  34.9 24.5 %collective-permute-start.4 = (bf16[64,2560]{1,0:T(8,128)(2,1)}, bf16[64,2560]{1,0:T(8,128)(2,1)S(1)}, u32[]{:S(2)}, u32[]{:S(2)}) collective-permute-start(bf16[64,2560]{1,0:T(8,128)(2,1)} %get-tuple-element.64), channel_id=1, source_target_pairs={{0,2},{1,3},{2,0},{3,1},{4,6},{5,7},{6,4},{7,5},{8,10},{9,11},{10,... | collective-permute-start | bytes 983048 | tf_op jit(solution)/shard_map/ppermute | solution.py:519
  36.7 22.7 %collective-permute-start.5 = (bf16[64,2560]{1,0:T(8,128)(2,1)}, bf16[64,2560]{1,0:T(8,128)(2,1)S(1)}, u32[]{:S(2)}, u32[]{:S(2)}) collective-permute-start(bf16[64,2560]{1,0:T(8,128)(2,1)} %get-tuple-element.65), channel_id=1, source_target_pairs={{0,3},{1,0},{2,1},{3,2},{4,7},{5,4},{6,5},{7,6},{8,11},{9,8},{10,9... | collective-permute-start | bytes 983048 | tf_op jit(solution)/shard_map/ppermute | solution.py:519
  47.4 12.2 %copy-start.10 = (bf16[64,2560]{1,0:T(8,128)(2,1)}, bf16[64,2560]{1,0:T(8,128)(2,1)S(1)}, u32[]{:S(2)}) copy-start(bf16[64,2560]{1,0:T(8,128)(2,1)S(1)} %collective-permute-done.3.refs_1_) | copy-start | bytes 983044
  59.5 0.7 copy-start.11
  59.5 0.8 copy-start.12
  59.5 100.0 %all-gather.3.cloned.1.call-start = ((), (), s32[]{:S(2)}) async-start(), calls=%async_computation | async-start | bytes 1310720 | tf_op jit(solution)/shard_map/all_gather | solution.py:515
  62.8 33.8 %copy-start.26 = (s32[2]{0:T(128)S(1)}, s32[2]{0:T(128)}, u32[]{:S(2)}) copy-start(s32[2]{0:T(128)} %param.11) | copy-start | bytes 28
  62.8 35.1 %copy-start.25 = (s32[1024]{0:T(1024)S(1)}, s32[1024]{0:T(1024)}, u32[]{:S(2)}) copy-start(s32[1024]{0:T(1024)} %param.10) | copy-start | bytes 12292
  62.8 36.4 %copy-start = (bf16[256,2560]{1,0:T(8,128)(2,1)S(1)}, bf16[256,2560]{1,0:T(8,128)(2,1)}, u32[]{:S(2)}) copy-start(bf16[256,2560]{1,0:T(8,128)(2,1)} %assemble.1.refs_0_) | copy-start | bytes 3932164
  62.8 29.5 %collective-permute-start.9 = (bf16[256,2560]{1,0:T(8,128)(2,1)}, bf16[256,2560]{1,0:T(8,128)(2,1)S(1)}, u32[]{:S(2)}, u32[]{:S(2)}) collective-permute-start(bf16[256,2560]{1,0:T(8,128)(2,1)} %assemble.1.refs_0_), channel_id=1, source_target_pairs={{0,16},{4,20},{8,24},{12,28},{16,0},{20,4},{24,8},{28,12},{1,17},{... | collective-permute-start | bytes 3932168 | tf_op jit(solution)/shard_map/ppermute | solution.py:115
  64.4 30.0 %collective-permute-start.7 = (bf16[256,2560]{1,0:T(8,128)(2,1)}, bf16[256,2560]{1,0:T(8,128)(2,1)}, u32[]{:S(2)}, u32[]{:S(2)}) collective-permute-start(bf16[256,2560]{1,0:T(8,128)(2,1)} %assemble.1.refs_0_), channel_id=1, source_target_pairs={{0,8},{4,12},{8,0},{12,4},{16,24},{20,28},{24,16},{28,20},{1,9},{5... | collective-permute-start | bytes 3932168 | tf_op jit(solution)/shard_map/ppermute | solution.py:115
  92.3 16.2 %copy-start.1 = (bf16[256,2560]{1,0:T(8,128)(2,1)}, bf16[256,2560]{1,0:T(8,128)(2,1)S(1)}, u32[]{:S(2)}) copy-start(bf16[256,2560]{1,0:T(8,128)(2,1)S(1)} %collective-permute-done.9.refs_4_) | copy-start | bytes 3932164
  92.3 15.3 %collective-permute-start.11 = (bf16[128,2560]{1,0:T(8,128)(2,1)S(1)}, bf16[128,2560]{1,0:T(8,128)(2,1)S(1)}, u32[]{:S(2)}, u32[]{:S(2)}) collective-permute-start(bf16[128,2560]{1,0:T(8,128)(2,1)S(1)} %slice.58), channel_id=1, source_target_pairs={{0,8},{4,12},{8,0},{12,4},{16,24},{20,28},{24,16},{28,20},{1,9},{5... | collective-permute-start | bytes 1966088 | tf_op jit(solution)/shard_map/ppermute | solution.py:115
  95.5 13.6 %collective-permute-start.12 = (bf16[128,2560]{1,0:T(8,128)(2,1)S(1)}, bf16[128,2560]{1,0:T(8,128)(2,1)S(1)}, u32[]{:S(2)}, u32[]{:S(2)}) collective-permute-start(bf16[128,2560]{1,0:T(8,128)(2,1)S(1)} %slice.59), channel_id=1, source_target_pairs={{0,16},{4,20},{8,24},{12,28},{16,0},{20,4},{24,8},{28,12},{1,17},{... | collective-permute-start | bytes 1966088 | tf_op jit(solution)/shard_map/ppermute | solution.py:115
  97.9 12.8 %collective-permute-start.14 = (s32[512]{0:T(512)S(1)}, s32[512]{0:T(512)S(1)}, u32[]{:S(2)}, u32[]{:S(2)}) collective-permute-start(s32[512]{0:T(512)S(1)} %get-tuple-element.110), channel_id=1, source_target_pairs={{0,4},{4,8},{8,12},{12,16},{16,20},{20,24},{24,28},{1,5},{5,9},{9,... | collective-permute-start | bytes 6152 | tf_op jit(solution)/shard_map/ppermute | solution.py:25
  99.2 16.3 %collective-permute-start.6 = (bf16[256,2560]{1,0:T(8,128)(2,1)S(1)}, bf16[256,2560]{1,0:T(8,128)(2,1)}, u32[]{:S(2)}, u32[]{:S(2)}) collective-permute-start(bf16[256,2560]{1,0:T(8,128)(2,1)S(1)} %copy-done), channel_id=1, source_target_pairs={{0,4},{4,0},{8,12},{12,8},{16,20},{20,16},{24,28},{28,24},{1,5},{5... | collective-permute-start | bytes 3932168 | tf_op jit(solution)/shard_map/ppermute | solution.py:115
  100.5 15.0 %collective-permute-start.10 = (bf16[256,2560]{1,0:T(8,128)(2,1)S(1)}, bf16[256,2560]{1,0:T(8,128)(2,1)}, u32[]{:S(2)}, u32[]{:S(2)}) collective-permute-start(bf16[256,2560]{1,0:T(8,128)(2,1)S(1)} %collective-permute-done.9.refs_4_), channel_id=1, source_target_pairs={{0,4},{4,0},{8,12},{12,8},{16,20},{20,16},{24,28},{28,24},{1,5},{5... | collective-permute-start | bytes 3932168 | tf_op jit(solution)/shard_map/ppermute | solution.py:115
  107.6 8.0 %collective-permute-start.8 = (bf16[256,2560]{1,0:T(8,128)(2,1)}, bf16[256,2560]{1,0:T(8,128)(2,1)}, u32[]{:S(2)}, u32[]{:S(2)}) collective-permute-start(bf16[256,2560]{1,0:T(8,128)(2,1)} %collective-permute-done.7.refs_2_), channel_id=1, source_target_pairs={{0,4},{4,0},{8,12},{12,8},{16,20},{20,16},{24,28},{28,24},{1,5},{5... | collective-permute-start | bytes 3932168 | tf_op jit(solution)/shard_map/ppermute | solution.py:115
  110.0 5.6 %collective-permute-start.13 = (bf16[256,2560]{1,0:T(8,128)(2,1)}, bf16[256,2560]{1,0:T(8,128)(2,1)}, u32[]{:S(2)}, u32[]{:S(2)}) collective-permute-start(bf16[256,2560]{1,0:T(8,128)(2,1)} %constant_dynamic-update-slice_fusion.refs_6_), channel_id=1, source_target_pairs={{0,4},{4,0},{8,12},{12,8},{16,20},{20,16},{24,28},{28,24},{1,5},{5... | collective-permute-start | bytes 3932168 | tf_op jit(solution)/shard_map/ppermute | solution.py:115
  114.3 1.3 copy-start.3
  114.3 1.3 copy-start.5
  139.7 35.0 %collective-permute-start.16 = (bf16[2,512,512]{2,1,0:T(8,128)(2,1)}, bf16[2,512,512]{2,1,0:T(8,128)(2,1)S(1)}, u32[]{:S(2)}, u32[]{:S(2)}) collective-permute-start(bf16[2,512,512]{2,1,0:T(8,128)(2,1)} %get-tuple-element.86), channel_id=1, source_target_pairs={{0,4},{4,8},{8,12},{12,16},{16,20},{20,24},{24,28},{1,5},{5,9},{9,... | collective-permute-start | bytes 3145736 | tf_op jit(solution)/shard_map/ppermute | solution.py:25
  143.4 4.1 %copy-start.4 = (f32[1024,64]{1,0:T(8,128)S(1)}, f32[1024,64]{1,0:T(8,128)}, u32[]{:S(2)}) copy-start(f32[1024,64]{1,0:T(8,128)} %copy-done.3) | copy-start | bytes 786436
  143.4 4.1 %copy-start.6 = (f32[1024,64]{1,0:T(8,128)S(1)}, f32[1024,64]{1,0:T(8,128)}, u32[]{:S(2)}) copy-start(f32[1024,64]{1,0:T(8,128)} %copy-done.5) | copy-start | bytes 786436
  147.6 14.3 %collective-permute-start.15 = (bf16[256,512]{1,0:T(8,128)(2,1)}, bf16[256,512]{1,0:T(8,128)(2,1)S(1)}, u32[]{:S(2)}, u32[]{:S(2)}) collective-permute-start(bf16[256,512]{1,0:T(8,128)(2,1)} %attend.4.own_ref), channel_id=1, source_target_pairs={{0,1},{1,0},{2,3},{3,2},{4,5},{5,4},{6,7},{7,6},{8,9},{9,8},{10,11... | collective-permute-start | bytes 786440 | tf_op jit(solution)/shard_map/ppermute | solution.py:115
  161.9 6.5 %copy-start.17 = (bf16[256,512]{1,0:T(8,128)(2,1)}, bf16[256,512]{1,0:T(8,128)(2,1)S(1)}, u32[]{:S(2)}) copy-start(bf16[256,512]{1,0:T(8,128)(2,1)S(1)} %collective-permute-done.15.other_ref) | copy-start | bytes 786436
  172.4 21.5 %collective-permute-start.23 = (bf16[256,512]{1,0:T(8,128)(2,1)}, bf16[256,512]{1,0:T(8,128)(2,1)S(1)}, u32[]{:S(2)}, u32[]{:S(2)}) collective-permute-start(bf16[256,512]{1,0:T(8,128)(2,1)} %attend.7.own_ref), channel_id=1, source_target_pairs={{0,1},{1,0},{2,3},{3,2},{4,5},{5,4},{6,7},{7,6},{8,9},{9,8},{10,11... | collective-permute-start | bytes 786440 | tf_op jit(solution)/shard_map/ppermute | solution.py:115
  174.8 1.0 copy-start.2
  179.8 20.8 %collective-permute-start.20 = (bf16[256,512]{1,0:T(8,128)(2,1)}, bf16[256,512]{1,0:T(8,128)(2,1)S(1)}, u32[]{:S(2)}, u32[]{:S(2)}) collective-permute-start(bf16[256,512]{1,0:T(8,128)(2,1)} %attend.6.own_ref), channel_id=1, source_target_pairs={{0,1},{1,0},{2,3},{3,2},{4,5},{5,4},{6,7},{7,6},{8,9},{9,8},{10,11... | collective-permute-start | bytes 786440 | tf_op jit(solution)/shard_map/ppermute | solution.py:115
  184.5 8.8 %copy-start.27 = (bf16[256,512]{1,0:T(8,128)(2,1)S(1)}, bf16[256,512]{1,0:T(8,128)(2,1)}, u32[]{:S(2)}) copy-start(bf16[256,512]{1,0:T(8,128)(2,1)} %get-tuple-element.100) | copy-start | bytes 786436
  184.5 21.8 %collective-permute-start.26 = (bf16[256,512]{1,0:T(8,128)(2,1)}, bf16[256,512]{1,0:T(8,128)(2,1)S(1)}, u32[]{:S(2)}, u32[]{:S(2)}) collective-permute-start(bf16[256,512]{1,0:T(8,128)(2,1)} %get-tuple-element.99), channel_id=1, source_target_pairs={{1,3},{2,0},{5,7},{6,4},{9,11},{10,8},{13,15},{14,12},{17,19},{18,... | collective-permute-start | bytes 786440 | tf_op jit(solution)/shard_map/ppermute | solution.py:580
  189.9 17.6 %collective-permute-start.17 = (bf16[256,512]{1,0:T(8,128)(2,1)}, bf16[256,512]{1,0:T(8,128)(2,1)S(1)}, u32[]{:S(2)}, u32[]{:S(2)}) collective-permute-start(bf16[256,512]{1,0:T(8,128)(2,1)} %attend.5.own_ref), channel_id=1, source_target_pairs={{0,1},{1,0},{2,3},{3,2},{4,5},{5,4},{6,7},{7,6},{8,9},{9,8},{10,11... | collective-permute-start | bytes 786440 | tf_op jit(solution)/shard_map/ppermute | solution.py:115
  193.3 19.7 %collective-permute-start.27 = (bf16[256,512]{1,0:T(8,128)(2,1)S(1)}, bf16[256,512]{1,0:T(8,128)(2,1)S(1)}, u32[]{:S(2)}, u32[]{:S(2)}) collective-permute-start(bf16[256,512]{1,0:T(8,128)(2,1)S(1)} %copy-done.27), channel_id=1, source_target_pairs={{1,2},{2,1},{5,6},{6,5},{9,10},{10,9},{13,14},{14,13},{17,18},{18,... | collective-permute-start | bytes 786440 | tf_op jit(solution)/shard_map/ppermute | solution.py:581
  194.0 0.7 copy-start.18
  199.3 14.9 %collective-permute-start.24 = (bf16[256,512]{1,0:T(8,128)(2,1)}, bf16[256,512]{1,0:T(8,128)(2,1)S(1)}, u32[]{:S(2)}, u32[]{:S(2)}) collective-permute-start(bf16[256,512]{1,0:T(8,128)(2,1)} %get-tuple-element.94), channel_id=1, source_target_pairs={{1,3},{2,0},{5,7},{6,4},{9,11},{10,8},{13,15},{14,12},{17,19},{18,... | collective-permute-start | bytes 786440 | tf_op jit(solution)/shard_map/ppermute | solution.py:580
  200.6 0.9 copy-start.16
  200.7 17.8 %collective-permute-start.25 = (bf16[256,512]{1,0:T(8,128)(2,1)}, bf16[256,512]{1,0:T(8,128)(2,1)S(1)}, u32[]{:S(2)}, u32[]{:S(2)}) collective-permute-start(bf16[256,512]{1,0:T(8,128)(2,1)} %get-tuple-element.95), channel_id=1, source_target_pairs={{1,2},{2,1},{5,6},{6,5},{9,10},{10,9},{13,14},{14,13},{17,18},{18,... | collective-permute-start | bytes 786440 | tf_op jit(solution)/shard_map/ppermute | solution.py:581
  206.3 6.7 %copy-start.13 = (bf16[256,512]{1,0:T(8,128)(2,1)}, bf16[256,512]{1,0:T(8,128)(2,1)S(1)}, u32[]{:S(2)}) copy-start(bf16[256,512]{1,0:T(8,128)(2,1)S(1)} %collective-permute-done.26.inner_ref) | copy-start | bytes 786436
  206.3 16.6 %collective-permute-start.21 = (bf16[256,512]{1,0:T(8,128)(2,1)}, bf16[256,512]{1,0:T(8,128)(2,1)S(1)}, u32[]{:S(2)}, u32[]{:S(2)}) collective-permute-start(bf16[256,512]{1,0:T(8,128)(2,1)} %get-tuple-element.91), channel_id=1, source_target_pairs={{1,3},{2,0},{5,7},{6,4},{9,11},{10,8},{13,15},{14,12},{17,19},{18,... | collective-permute-start | bytes 786440 | tf_op jit(solution)/shard_map/ppermute | solution.py:580
  207.6 0.7 copy-start.15
  207.6 15.2 %collective-permute-start.22 = (bf16[256,512]{1,0:T(8,128)(2,1)}, bf16[256,512]{1,0:T(8,128)(2,1)S(1)}, u32[]{:S(2)}, u32[]{:S(2)}) collective-permute-start(bf16[256,512]{1,0:T(8,128)(2,1)} %get-tuple-element.92), channel_id=1, source_target_pairs={{1,2},{2,1},{5,6},{6,5},{9,10},{10,9},{13,14},{14,13},{17,18},{18,... | collective-permute-start | bytes 786440 | tf_op jit(solution)/shard_map/ppermute | solution.py:581
  213.0 2.0 copy-start.14
  213.0 21.1 %collective-permute-start.18 = (bf16[256,512]{1,0:T(8,128)(2,1)}, bf16[256,512]{1,0:T(8,128)(2,1)S(1)}, u32[]{:S(2)}, u32[]{:S(2)}) collective-permute-start(bf16[256,512]{1,0:T(8,128)(2,1)} %get-tuple-element.88), channel_id=1, source_target_pairs={{1,3},{2,0},{5,7},{6,4},{9,11},{10,8},{13,15},{14,12},{17,19},{18,... | collective-permute-start | bytes 786440 | tf_op jit(solution)/shard_map/ppermute | solution.py:580
  214.3 4.1 %copy-start.19 = (bf16[256,512]{1,0:T(8,128)(2,1)}, bf16[256,512]{1,0:T(8,128)(2,1)S(1)}, u32[]{:S(2)}) copy-start(bf16[256,512]{1,0:T(8,128)(2,1)S(1)} %collective-permute-done.24.inner_ref) | copy-start | bytes 786436
  214.3 19.8 %collective-permute-start.19 = (bf16[256,512]{1,0:T(8,128)(2,1)}, bf16[256,512]{1,0:T(8,128)(2,1)S(1)}, u32[]{:S(2)}, u32[]{:S(2)}) collective-permute-start(bf16[256,512]{1,0:T(8,128)(2,1)} %get-tuple-element.89), channel_id=1, source_target_pairs={{1,2},{2,1},{5,6},{6,5},{9,10},{10,9},{13,14},{14,13},{17,18},{18,... | collective-permute-start | bytes 786440 | tf_op jit(solution)/shard_map/ppermute | solution.py:581
  218.4 0.7 copy-start.20
  222.8 0.7 copy-start.21
  222.8 0.8 copy-start.22
  234.1 0.7 copy-start.23
  234.1 0.8 copy-start.24
Sparse Core Ops, SparseCore 0:
  59.6 69.4 all-gather.4
  130.7 28.7 all-gather.2

commit v13 on v12

--- a/solution.py
+++ b/solution.py
@@ -570,17 +570,23 @@
     parts = {last: projected(*both)}
     qkv_first, _ = qkv_columns(ring, rows_first, pieces, cosine[:CHUNK], sine[:CHUNK])
     chunks = [(halo_rows, 0, 0), (halo_rows, 0, 1), (qkv_first, 1, 0)] + late_chunks
+    def crossed(parts):
+        kept, inner, outer = parts
+        outer = lax.ppermute(outer, "mp", [(1, 3), (2, 0)])
+        inner = lax.ppermute(inner, "mp", [(1, 2), (2, 1)])
+        return [kept, outer, inner]
+
+    updates = {last: crossed(parts[last])}
     for chunk in reversed(range(last)):
         own = attended(chunk, chunks[chunk : chunk + 3])
-        parts[chunk] = projected(own, swapped(own, "mp", 1))
+        both = (own, swapped(own, "mp", 1))
+        if chunk == last - 2:
+            both, updates[last] = lax.optimization_barrier((both, updates[last]))
+        updates[chunk] = crossed(projected(*both))
 
     result = None
     for chunk in reversed(range(last + 1)):
-        kept, inner, outer = parts[chunk]
-        outer = lax.ppermute(outer, "mp", [(1, 3), (2, 0)])
-        inner = lax.ppermute(inner, "mp", [(1, 2), (2, 1)])
-        updates = [kept, outer, inner]
-        result = final(hc_static, streams, sums_all, updates, chunk * CHUNK, result)
+        result = final(hc_static, streams, sums_all, updates[chunk], chunk * CHUNK, result)
     return result
 
 

time: 247 us -> 249 us (level)
  waiting for transfers between devices: 89.5 us -> 86.4 us
    ppermute x8, waiting for transfers between devices: 7.32 us -> 4.65 us  [the longest x4 4.64 us: crossed(): outer = lax.ppermute(outer, 'mp', [(1, 3), (2, 0)])]
    unnamed x57 -> x55, local copies, waits for them, and re-layouts: 5.74 us -> 7.1 us
  transfers between devices with their start and end apart: 30 -> 30, of which waited for: 11 -> 9; matrix products, arithmetic and copies ran while one was open for 4% -> 4% of each run, Pallas kernels for 32% -> 31%
where the time goes in v13:
time: 249 us; the launch traced here: 246 us
  Pallas kernels  86.9 us (35%)
  waiting for transfers between devices  86.4 us (35%)
  starting transfers between devices  38.4 us (15%)
  between operations  15.2 us (6%)
  local copies, waits for them, and re-layouts  11.6 us (5%)
  other arithmetic  7.04 us (3%)
    ppermute x12, waiting for transfers between devices, swapped(): lax.ppermute(value, axis, [(source, source ^ mask) for source in range(co...  37.3 us
    all_gather x2, waiting for transfers between devices, gathered(): rows = lax.all_gather(normed, 'mp', axis=0, tiled=True)  23.8 us
    pallas_call x4, Pallas kernels, project(): pl.pallas_call(project_kernel, grid=(1,), in_specs=[pl.BlockSpec(memory_s...  18.6 us
    pallas_call x2, Pallas kernels, qkv_columns(): pl.pallas_call(qkv_kernel, grid=(3,), in_specs=[pl.BlockSpec(memory_space...  17.1 us
    pallas_call x4, Pallas kernels, attend(): pl.pallas_call(attend_kernel, grid=(1,), in_specs=[pl.BlockSpec(block, la...  16.2 us
    ppermute x12, starting transfers between devices, swapped(): lax.ppermute(value, axis, [(source, source ^ mask) for source in range(co...  15.3 us
    pallas_call x4, Pallas kernels, final(): pl.pallas_call(final_kernel, grid=(tokens // STEP,), in_specs=specs, out_...  13.6 us
    ppermute x3, waiting for transfers between devices, body(): lax.ppermute(parts[step], 'mp', [(at, (at + step) % group_size) for at in...  12.1 us
  transfers between devices with their start and end apart: 30, of which 9 were waited for; matrix products, arithmetic and copies ran while one was open for 4% of the time, Pallas kernels for 31%

profile of v13, /device:TPU:0, one launch (start us, length us, event | category | flops | bytes accessed | tf_op | source)
XLA Modules:
  0.0 245.6 jit_solution(17118136022224308966)
XLA Ops:
  6.7 1.4 maximum_maximum_fusion.proj_ref
  8.1 6.4 %stats.1.own_ref = f32[8,5248]{1,0:T(8,128)} custom-call(bf16[1024,4,512]{2,1,0:T(4,128)(2,1)} %x_ref.13, f32[8,512]{1,0:T(8,128)} %maximum_maximum_fusion.proj_ref), custom_call_target="tpu_custom_call" | custom-call | flops 1258291200 | bytes 4194304 | tf_op jit(solution)/shard_map/stats/pallas_call | solution.py:178
  14.4 5.0 %collective-permute-start.2 = (f32[8,5248]{1,0:T(8,128)}, f32[8,5248]{1,0:T(8,128)S(1)}, u32[]{:S(2)}, u32[]{:S(2)}) collective-permute-start(f32[8,5248]{1,0:T(8,128)} %stats.1.own_ref), channel_id=1, source_target_pairs={{0,3},{1,0},{2,1},{3,2},{4,7},{5,4},{6,5},{7,6},{8,11},{9,8},{10,9... | collective-permute-start | bytes 503816 | tf_op jit(solution)/shard_map/ppermute | solution.py:31
  19.5 1.0 collective-permute-start
  20.5 4.9 %regroup.1 = (bf16[64,2560]{1,0:T(8,128)(2,1)}, bf16[64,2560]{1,0:T(8,128)(2,1)}, bf16[64,2560]{1,0:T(8,128)(2,1)}, bf16[64,2560]{1,0:T(8,128)(2,1)}) custom-call(s32[1]{0:T(128)} %bitcast.1.place_ref, f32[64,4,2048]{2,1,0:T(4,128)} %master_ref.1), custom_call_target="tpu_custom_call" | custom-call | bytes 3407872 | tf_op jit(solution)/shard_map/regroup/pallas_call | solution.py:79
  25.4 8.5 %collective-permute-done.1.b_ref = f32[8,5248]{1,0:T(8,128)S(1)} collective-permute-done((f32[8,5248]{1,0:T(8,128)}, f32[8,5248]{1,0:T(8,128)S(1)}, u32[]{:S(2)}, u32[]{:S(2)}) %collective-permute-start.1) | collective-permute-done | bytes 167968 | tf_op jit(solution)/shard_map/ppermute | solution.py:31
  33.9 1.0 collective-permute-start.3
  34.9 1.8 collective-permute-start.4
  36.7 2.9 %collective-permute-start.5 = (bf16[64,2560]{1,0:T(8,128)(2,1)}, bf16[64,2560]{1,0:T(8,128)(2,1)S(1)}, u32[]{:S(2)}, u32[]{:S(2)}) collective-permute-start(bf16[64,2560]{1,0:T(8,128)(2,1)} %get-tuple-element.70), channel_id=1, source_target_pairs={{0,3},{1,0},{2,1},{3,2},{4,7},{5,4},{6,5},{7,6},{8,11},{9,8},{10,9... | collective-permute-start | bytes 983048 | tf_op jit(solution)/shard_map/ppermute | solution.py:519
  39.7 2.9 %mix.3 = (f32[8,5248]{1,0:T(8,128)}, bf16[256,512]{1,0:T(8,128)(2,1)}) custom-call(f32[4,6]{1,0:T(4,128)} %static_ref.11, bf16[1024,4,512]{2,1,0:T(4,128)(2,1)} %x_ref.13, f32[8,5248]{1,0:T(8,128)} %stats.1.own_ref, f32[8,5248]{1,0:T(8,128)} %copy-done.9, f32[8,5248]{1,0:T(8,128)} %copy-done.8, f32[8,5248]{1,0:T(8,128)} %copy-done.7), custom_call_target="tpu_custom_call" | custom-call | flops 209715200 | bytes 1310720 | tf_op jit(solution)/shard_map/mix/pallas_call | solution.py:249
  42.5 4.9 %mix.2 = (f32[8,5248]{1,0:T(8,128)}, bf16[768,512]{1,0:T(8,128)(2,1)}) custom-call(f32[4,6]{1,0:T(4,128)} %static_ref.11, bf16[1024,4,512]{2,1,0:T(4,128)(2,1)} %x_ref.13, f32[8,5248]{1,0:T(8,128)} %stats.1.own_ref, f32[8,5248]{1,0:T(8,128)} %copy-done.9, f32[8,5248]{1,0:T(8,128)} %copy-done.8, f32[8,5248]{1,0:T(8,128)} %copy-done.7), custom_call_target="tpu_custom_call" | custom-call | flops 629145600 | bytes 3932160 | tf_op jit(solution)/shard_map/mix/pallas_call | solution.py:249
  47.4 12.1 %collective-permute-done.4.refs_2_ = bf16[64,2560]{1,0:T(8,128)(2,1)S(1)} collective-permute-done((bf16[64,2560]{1,0:T(8,128)(2,1)}, bf16[64,2560]{1,0:T(8,128)(2,1)S(1)}, u32[]{:S(2)}, u32[]{:S(2)}) %collective-permute-start.4) | collective-permute-done | bytes 327712 | tf_op jit(solution)/shard_map/ppermute | solution.py:519
  60.3 2.4 assemble.1.refs_0_
  62.8 1.5 collective-permute-start.9
  64.3 1.5 collective-permute-start.7
  65.8 26.4 %collective-permute-done.9.refs_4_ = bf16[256,2560]{1,0:T(8,128)(2,1)S(1)} collective-permute-done((bf16[256,2560]{1,0:T(8,128)(2,1)}, bf16[256,2560]{1,0:T(8,128)(2,1)S(1)}, u32[]{:S(2)}, u32[]{:S(2)}) %collective-permute-start.9) | collective-permute-done | bytes 1310752 | tf_op jit(solution)/shard_map/ppermute | solution.py:115
  92.3 1.5 collective-permute-start.11
  95.2 1.1 slice.59
  96.3 1.6 collective-permute-start.12
  97.9 1.3 collective-permute-start.14
  99.2 1.3 collective-permute-start.6
  100.6 6.9 %collective-permute-done.11 = bf16[128,2560]{1,0:T(8,128)(2,1)S(1)} collective-permute-done((bf16[128,2560]{1,0:T(8,128)(2,1)S(1)}, bf16[128,2560]{1,0:T(8,128)(2,1)S(1)}, u32[]{:S(2)}, u32[]{:S(2)}) %collective-permute-start.11) | collective-permute-done | bytes 655392 | tf_op jit(solution)/shard_map/ppermute | solution.py:115
  107.5 0.9 constant_dynamic-update-slice_fusion.1
  108.4 2.1 collective-permute-done.12
  110.4 0.9 constant_dynamic-update-slice_fusion.refs_6_
  112.0 1.0 copy.14.qseg_ref
  113.0 1.6 convert_reduce_fusion
  114.7 1.9 multiply_sine_fusion
  116.6 1.2 fusion.1
  117.9 11.2 %all-gather.5.cloned.1.call-done = bf16[3072,512]{1,0:T(8,128)(2,1)} async-done(((bf16[768,512]{1,0:T(8,128)(2,1)}), bf16[3072,512]{1,0:T(8,128)(2,1)}) %all-gather.5.cloned.1.call-update) | async-done | bytes 3145744 | tf_op jit(solution)/shard_map/all_gather | solution.py:515
  129.1 10.7 %qkv.2 = (bf16[3,768,512]{2,1,0:T(8,128)(2,1)}, bf16[2,512,512]{2,1,0:T(8,128)(2,1)}) custom-call(s32[1]{0:T(128)} %bitcast.2.ring_ref, bf16[4,768,512]{2,1,0:T(8,128)(2,1)} %bitcast.13, f32[768,128]{1,0:T(8,128)} %get-tuple-element.126.cosine_ref, f32[768,128]{1,0:T(8,128)} %get-tuple-element.125.sine_ref, bf16[256,2560]{1,0:T(8,128)(2,1)} %assemble.1.refs_0_, ...), custom_call_target="tpu_custom_call" | custom-call | flops 4831838208 | bytes 14155776 | tf_op jit(solution)/shard_map/qkv/pallas_call | solution.py:305
  139.8 1.9 collective-permute-start.16
  142.4 4.1 %attend.4.own_ref = bf16[256,512]{1,0:T(8,128)(2,1)} custom-call(bf16[3,768,512]{2,1,0:T(8,128)(2,1)} %get-tuple-element.88.q_ref.k0.k1.k2.v0.v1.v2, bf16[3,768,512]{2,1,0:T(8,128)(2,1)} %get-tuple-element.88.q_ref.k0.k1.k2.v0.v1.v2, bf16[3,768,512]{2,1,0:T(8,128)(2,1)} %get-tuple-element.88.q_ref.k0.k1.k2.v0.v1.v2, ...), custom_call_target="tpu_custom_call" | custom-call | flops 402653184 | bytes 2097152 | tf_op jit(solution)/shard_map/attend/pallas_call | solution.py:359
  146.6 0.9 pad_maximum_fusion
  147.4 12.6 %all-gather.3.cloned.1.call-done = bf16[1024,512]{1,0:T(8,128)(2,1)} async-done(((bf16[256,512]{1,0:T(8,128)(2,1)}), bf16[1024,512]{1,0:T(8,128)(2,1)}) %all-gather.3.cloned.1.call-update) | async-done | bytes 1048592 | tf_op jit(solution)/shard_map/all_gather | solution.py:515
  160.0 2.0 collective-permute-done.15.other_ref
  162.0 6.5 %qkv.3 = (bf16[3,256,512]{2,1,0:T(8,128)(2,1)}, bf16[2,256,512]{2,1,0:T(8,128)(2,1)}) custom-call(s32[1]{0:T(128)} %bitcast.2.ring_ref, bf16[4,256,512]{2,1,0:T(8,128)(2,1)} %bitcast.10, f32[256,128]{1,0:T(8,128)} %get-tuple-element.128.cosine_ref, f32[256,128]{1,0:T(8,128)} %get-tuple-element.127.sine_ref, bf16[256,2560]{1,0:T(8,128)(2,1)} %assemble.1.refs_0_, ...), custom_call_target="tpu_custom_call" | custom-call | flops 1610612736 | bytes 8912896 | tf_op jit(solution)/shard_map/qkv/pallas_call | solution.py:305
  168.4 4.0 %attend.7.own_ref = bf16[256,512]{1,0:T(8,128)(2,1)} custom-call(bf16[3,768,512]{2,1,0:T(8,128)(2,1)} %get-tuple-element.88.q_ref.k0.k1.k2.v0.v1.v2, bf16[3,256,512]{2,1,0:T(8,128)(2,1)} %get-tuple-element.90.q_ref.k2.v2.k1.v1.k0.v0, bf16[3,768,512]{2,1,0:T(8,128)(2,1)} %get-tuple-element.88.q_ref.k0.k1.k2.v0.v1.v2, ...), custom_call_target="tpu_custom_call" | custom-call | flops 402653184 | bytes 2097152 | tf_op jit(solution)/shard_map/attend/pallas_call | solution.py:359
  172.4 2.4 collective-permute-start.25
  174.8 4.7 %project.5 = (f32[256,512]{1,0:T(8,128)}, bf16[256,512]{1,0:T(8,128)(2,1)}, bf16[256,512]{1,0:T(8,128)(2,1)}) custom-call(s32[1]{0:T(128)} %bitcast.1.place_ref, s32[1]{0:T(128)} %bitcast.2.ring_ref, bf16[256,512]{1,0:T(8,128)(2,1)} %attend.4.own_ref, bf16[256,512]{1,0:T(8,128)(2,1)} %copy-done.18, bf16[256,2560]{1,0:T(8,128)(2,1)} %assemble.1.refs_0_, ...), custom_call_target="tpu_custom_call" | custom-call | flops 1073741824 | bytes 5767168 | tf_op jit(solution)/shard_map/project/pallas_call | solution.py:409
  179.5 1.3 collective-permute-start.21
  180.8 0.7 collective-permute-start.22
  181.5 1.0 copy-done.2
  182.5 4.0 %attend.6.own_ref = bf16[256,512]{1,0:T(8,128)(2,1)} custom-call(bf16[3,768,512]{2,1,0:T(8,128)(2,1)} %get-tuple-element.88.q_ref.k0.k1.k2.v0.v1.v2, bf16[2,512,512]{2,1,0:T(8,128)(2,1)} %copy-done.2, bf16[3,256,512]{2,1,0:T(8,128)(2,1)} %get-tuple-element.90.q_ref.k2.v2.k1.v1.k0.v0, bf16[3,768,512]{2,1,0:T(8,128)(2,1)} %get-tuple-element.88.q_ref.k0.k1.k2.v0.v1.v2, ...), custom_call_target="tpu_custom_call" | custom-call | flops 402653184 | bytes 2097152 | tf_op jit(solution)/shard_map/attend/pallas_call | solution.py:359
  186.5 5.3 %collective-permute-start.20 = (bf16[256,512]{1,0:T(8,128)(2,1)}, bf16[256,512]{1,0:T(8,128)(2,1)S(1)}, u32[]{:S(2)}, u32[]{:S(2)}) collective-permute-start(bf16[256,512]{1,0:T(8,128)(2,1)} %attend.6.own_ref), channel_id=1, source_target_pairs={{0,1},{1,0},{2,3},{3,2},{4,5},{5,4},{6,7},{7,6},{8,9},{9,8},{10,11... | collective-permute-start | bytes 786440 | tf_op jit(solution)/shard_map/ppermute | solution.py:115
  191.8 4.0 %attend.5.own_ref = bf16[256,512]{1,0:T(8,128)(2,1)} custom-call(bf16[3,256,512]{2,1,0:T(8,128)(2,1)} %get-tuple-element.90.q_ref.k2.v2.k1.v1.k0.v0, bf16[2,512,512]{2,1,0:T(8,128)(2,1)} %copy-done.2, bf16[2,512,512]{2,1,0:T(8,128)(2,1)} %copy-done.2, bf16[3,256,512]{2,1,0:T(8,128)(2,1)} %get-tuple-element.90.q_ref.k2.v2.k1.v1.k0.v0, ...), custom_call_target="tpu_custom_call" | custom-call | flops 402653184 | bytes 2097152 | tf_op jit(solution)/shard_map/attend/pallas_call | solution.py:359
  195.9 0.7 copy-done.17
  196.6 4.6 %project.7 = (f32[256,512]{1,0:T(8,128)}, bf16[256,512]{1,0:T(8,128)(2,1)}, bf16[256,512]{1,0:T(8,128)(2,1)}) custom-call(s32[1]{0:T(128)} %bitcast.1.place_ref, s32[1]{0:T(128)} %bitcast.2.ring_ref, bf16[256,512]{1,0:T(8,128)(2,1)} %attend.7.own_ref, bf16[256,512]{1,0:T(8,128)(2,1)} %copy-done.17, bf16[256,2560]{1,0:T(8,128)(2,1)} %assemble.1.refs_0_, ...), custom_call_target="tpu_custom_call" | custom-call | flops 1073741824 | bytes 5767168 | tf_op jit(solution)/shard_map/project/pallas_call | solution.py:409
  201.2 1.3 collective-permute-start.26
  202.5 0.9 collective-permute-start.27
  203.5 0.7 copy-done.16
  204.2 4.7 %project.6 = (f32[256,512]{1,0:T(8,128)}, bf16[256,512]{1,0:T(8,128)(2,1)}, bf16[256,512]{1,0:T(8,128)(2,1)}) custom-call(s32[1]{0:T(128)} %bitcast.1.place_ref, s32[1]{0:T(128)} %bitcast.2.ring_ref, bf16[256,512]{1,0:T(8,128)(2,1)} %attend.6.own_ref, bf16[256,512]{1,0:T(8,128)(2,1)} %copy-done.16, bf16[256,2560]{1,0:T(8,128)(2,1)} %assemble.1.refs_0_, ...), custom_call_target="tpu_custom_call" | custom-call | flops 1073741824 | bytes 5767168 | tf_op jit(solution)/shard_map/project/pallas_call | solution.py:409
  208.9 1.3 collective-permute-start.23
  210.9 0.7 copy-done.15
  211.6 4.7 %project.4 = (f32[256,512]{1,0:T(8,128)}, bf16[256,512]{1,0:T(8,128)(2,1)}, bf16[256,512]{1,0:T(8,128)(2,1)}) custom-call(s32[1]{0:T(128)} %bitcast.1.place_ref, s32[1]{0:T(128)} %bitcast.2.ring_ref, bf16[256,512]{1,0:T(8,128)(2,1)} %attend.5.own_ref, bf16[256,512]{1,0:T(8,128)(2,1)} %copy-done.15, bf16[256,2560]{1,0:T(8,128)(2,1)} %assemble.1.refs_0_, ...), custom_call_target="tpu_custom_call" | custom-call | flops 1073741824 | bytes 5767168 | tf_op jit(solution)/shard_map/project/pallas_call | solution.py:409
  216.2 1.3 collective-permute-start.18
  218.2 3.4 %final.4.rest_0_ = bf16[1024,4,512]{2,1,0:T(4,128)(2,1)} custom-call(f32[4,6]{1,0:T(4,128)} %static_ref.11, bf16[1024,4,512]{2,1,0:T(4,128)(2,1)} %x_ref.13, f32[8,5248]{1,0:T(8,128)} %get-tuple-element.66.first_ref.folded_ref.column_ref, f32[8,5248]{1,0:T(8,128)} %get-tuple-element.66.first_ref.folded_ref.column_ref, ...), custom_call_target="tpu_custom_call" | custom-call | flops 629145600 | bytes 2883584 | tf_op jit(solution)/shard_map/final/pallas_call | solution.py:488
  221.7 0.7 copy-done.20
  222.4 3.4 %final.5.rest_0_ = bf16[1024,4,512]{2,1,0:T(4,128)(2,1)} custom-call(f32[4,6]{1,0:T(4,128)} %static_ref.11, bf16[1024,4,512]{2,1,0:T(4,128)(2,1)} %x_ref.13, f32[8,5248]{1,0:T(8,128)} %get-tuple-element.66.first_ref.folded_ref.column_ref, f32[8,5248]{1,0:T(8,128)} %get-tuple-element.66.first_ref.folded_ref.column_ref, ...), custom_call_target="tpu_custom_call", output_to_operand_aliasing={{}: (8, {})} | custom-call | flops 629145600 | bytes 2883584 | tf_op jit(solution)/shard_map/final/pallas_call | solution.py:488
  225.8 0.7 copy-done.21
  226.6 3.4 %final.6.rest_0_ = bf16[1024,4,512]{2,1,0:T(4,128)(2,1)} custom-call(f32[4,6]{1,0:T(4,128)} %static_ref.11, bf16[1024,4,512]{2,1,0:T(4,128)(2,1)} %x_ref.13, f32[8,5248]{1,0:T(8,128)} %get-tuple-element.66.first_ref.folded_ref.column_ref, f32[8,5248]{1,0:T(8,128)} %get-tuple-element.66.first_ref.folded_ref.column_ref, ...), custom_call_target="tpu_custom_call", output_to_operand_aliasing={{}: (8, {})} | custom-call | flops 629145600 | bytes 2883584 | tf_op jit(solution)/shard_map/final/pallas_call | solution.py:488
  230.0 4.6 %collective-permute-done.18.inner_ref = bf16[256,512]{1,0:T(8,128)(2,1)S(1)} collective-permute-done((bf16[256,512]{1,0:T(8,128)(2,1)}, bf16[256,512]{1,0:T(8,128)(2,1)S(1)}, u32[]{:S(2)}, u32[]{:S(2)}) %collective-permute-start.18) | collective-permute-done | bytes 262176 | tf_op jit(solution)/shard_map/ppermute | solution.py:575
  234.6 0.7 copy-done.23
  235.4 3.4 %final.7 = bf16[1024,4,512]{2,1,0:T(4,128)(2,1)} custom-call(f32[4,6]{1,0:T(4,128)} %static_ref.11, bf16[1024,4,512]{2,1,0:T(4,128)(2,1)} %x_ref.13, f32[8,5248]{1,0:T(8,128)} %get-tuple-element.66.first_ref.folded_ref.column_ref, f32[8,5248]{1,0:T(8,128)} %get-tuple-element.66.first_ref.folded_ref.column_ref, ...), custom_call_target="tpu_custom_call", output_to_operand_aliasing={{}: (8, {})} | custom-call | flops 629145600 | bytes 2883584 | tf_op jit(solution)/shard_map/final/pallas_call | solution.py:488
  (100 shorter events, 4.2 us)
Async XLA Ops:
  6.5 122.6 %all-gather.5.cloned.1.call-start = ((), (), s32[]{:S(2)}) async-start(), calls=%async_computation.1 | async-start | bytes 3932160 | tf_op jit(solution)/shard_map/all_gather | solution.py:515
  14.4 11.0 %collective-permute-start.2 = (f32[8,5248]{1,0:T(8,128)}, f32[8,5248]{1,0:T(8,128)S(1)}, u32[]{:S(2)}, u32[]{:S(2)}) collective-permute-start(f32[8,5248]{1,0:T(8,128)} %stats.1.own_ref), channel_id=1, source_target_pairs={{0,3},{1,0},{2,1},{3,2},{4,7},{5,4},{6,5},{7,6},{8,11},{9,8},{10,9... | collective-permute-start | bytes 503816 | tf_op jit(solution)/shard_map/ppermute | solution.py:31
  19.5 14.4 %collective-permute-start.1 = (f32[8,5248]{1,0:T(8,128)}, f32[8,5248]{1,0:T(8,128)S(1)}, u32[]{:S(2)}, u32[]{:S(2)}) collective-permute-start(f32[8,5248]{1,0:T(8,128)} %stats.1.own_ref), channel_id=1, source_target_pairs={{0,2},{1,3},{2,0},{3,1},{4,6},{5,7},{6,4},{7,5},{8,10},{9,11},{10,... | collective-permute-start | bytes 503816 | tf_op jit(solution)/shard_map/ppermute | solution.py:31
  19.5 14.4 %collective-permute-start = (f32[8,5248]{1,0:T(8,128)}, f32[8,5248]{1,0:T(8,128)S(1)}, u32[]{:S(2)}, u32[]{:S(2)}) collective-permute-start(f32[8,5248]{1,0:T(8,128)} %stats.1.own_ref), channel_id=1, source_target_pairs={{0,1},{1,2},{2,3},{3,0},{4,5},{5,6},{6,7},{7,4},{8,9},{9,10},{10,1... | collective-permute-start | bytes 503816 | tf_op jit(solution)/shard_map/ppermute | solution.py:31
  25.4 14.3 %copy-start.7 = (f32[8,5248]{1,0:T(8,128)}, f32[8,5248]{1,0:T(8,128)S(1)}, u32[]{:S(2)}) copy-start(f32[8,5248]{1,0:T(8,128)S(1)} %collective-permute-done.2.c_ref) | copy-start | bytes 503812
  33.9 5.7 %copy-start.8 = (f32[8,5248]{1,0:T(8,128)}, f32[8,5248]{1,0:T(8,128)S(1)}, u32[]{:S(2)}) copy-start(f32[8,5248]{1,0:T(8,128)S(1)} %collective-permute-done.1.b_ref) | copy-start | bytes 503812
  33.9 5.7 %copy-start.9 = (f32[8,5248]{1,0:T(8,128)}, f32[8,5248]{1,0:T(8,128)S(1)}, u32[]{:S(2)}) copy-start(f32[8,5248]{1,0:T(8,128)S(1)} %collective-permute-done.a_ref) | copy-start | bytes 503812
  33.9 13.4 %collective-permute-start.3 = (bf16[64,2560]{1,0:T(8,128)(2,1)}, bf16[64,2560]{1,0:T(8,128)(2,1)S(1)}, u32[]{:S(2)}, u32[]{:S(2)}) collective-permute-start(bf16[64,2560]{1,0:T(8,128)(2,1)} %get-tuple-element.68), channel_id=1, source_target_pairs={{0,1},{1,2},{2,3},{3,0},{4,5},{5,6},{6,7},{7,4},{8,9},{9,10},{10,1... | collective-permute-start | bytes 983048 | tf_op jit(solution)/shard_map/ppermute | solution.py:519
  34.9 24.5 %collective-permute-start.4 = (bf16[64,2560]{1,0:T(8,128)(2,1)}, bf16[64,2560]{1,0:T(8,128)(2,1)S(1)}, u32[]{:S(2)}, u32[]{:S(2)}) collective-permute-start(bf16[64,2560]{1,0:T(8,128)(2,1)} %get-tuple-element.69), channel_id=1, source_target_pairs={{0,2},{1,3},{2,0},{3,1},{4,6},{5,7},{6,4},{7,5},{8,10},{9,11},{10,... | collective-permute-start | bytes 983048 | tf_op jit(solution)/shard_map/ppermute | solution.py:519
  36.7 22.7 %collective-permute-start.5 = (bf16[64,2560]{1,0:T(8,128)(2,1)}, bf16[64,2560]{1,0:T(8,128)(2,1)S(1)}, u32[]{:S(2)}, u32[]{:S(2)}) collective-permute-start(bf16[64,2560]{1,0:T(8,128)(2,1)} %get-tuple-element.70), channel_id=1, source_target_pairs={{0,3},{1,0},{2,1},{3,2},{4,7},{5,4},{6,5},{7,6},{8,11},{9,8},{10,9... | collective-permute-start | bytes 983048 | tf_op jit(solution)/shard_map/ppermute | solution.py:519
  47.4 12.2 %copy-start.10 = (bf16[64,2560]{1,0:T(8,128)(2,1)}, bf16[64,2560]{1,0:T(8,128)(2,1)S(1)}, u32[]{:S(2)}) copy-start(bf16[64,2560]{1,0:T(8,128)(2,1)S(1)} %collective-permute-done.3.refs_1_) | copy-start | bytes 983044
  59.5 0.7 copy-start.11
  59.5 0.8 copy-start.12
  59.5 34.3 %copy-start.26 = (s32[2]{0:T(128)S(1)}, s32[2]{0:T(128)}, u32[]{:S(2)}) copy-start(s32[2]{0:T(128)} %param.11) | copy-start | bytes 28
  59.5 100.5 %all-gather.3.cloned.1.call-start = ((), (), s32[]{:S(2)}) async-start(), calls=%async_computation | async-start | bytes 1310720 | tf_op jit(solution)/shard_map/all_gather | solution.py:515
  62.8 35.1 %copy-start.25 = (s32[1024]{0:T(1024)S(1)}, s32[1024]{0:T(1024)}, u32[]{:S(2)}) copy-start(s32[1024]{0:T(1024)} %param.10) | copy-start | bytes 12292
  62.8 36.5 %copy-start = (bf16[256,2560]{1,0:T(8,128)(2,1)S(1)}, bf16[256,2560]{1,0:T(8,128)(2,1)}, u32[]{:S(2)}) copy-start(bf16[256,2560]{1,0:T(8,128)(2,1)} %assemble.1.refs_0_) | copy-start | bytes 3932164
  62.8 29.4 %collective-permute-start.9 = (bf16[256,2560]{1,0:T(8,128)(2,1)}, bf16[256,2560]{1,0:T(8,128)(2,1)S(1)}, u32[]{:S(2)}, u32[]{:S(2)}) collective-permute-start(bf16[256,2560]{1,0:T(8,128)(2,1)} %assemble.1.refs_0_), channel_id=1, source_target_pairs={{0,16},{4,20},{8,24},{12,28},{16,0},{20,4},{24,8},{28,12},{1,17},{... | collective-permute-start | bytes 3932168 | tf_op jit(solution)/shard_map/ppermute | solution.py:115
  64.3 30.9 %collective-permute-start.7 = (bf16[256,2560]{1,0:T(8,128)(2,1)}, bf16[256,2560]{1,0:T(8,128)(2,1)}, u32[]{:S(2)}, u32[]{:S(2)}) collective-permute-start(bf16[256,2560]{1,0:T(8,128)(2,1)} %assemble.1.refs_0_), channel_id=1, source_target_pairs={{0,8},{4,12},{8,0},{12,4},{16,24},{20,28},{24,16},{28,20},{1,9},{5... | collective-permute-start | bytes 3932168 | tf_op jit(solution)/shard_map/ppermute | solution.py:115
  92.2 16.2 %copy-start.1 = (bf16[256,2560]{1,0:T(8,128)(2,1)}, bf16[256,2560]{1,0:T(8,128)(2,1)S(1)}, u32[]{:S(2)}) copy-start(bf16[256,2560]{1,0:T(8,128)(2,1)S(1)} %collective-permute-done.9.refs_4_) | copy-start | bytes 3932164
  92.3 15.3 %collective-permute-start.11 = (bf16[128,2560]{1,0:T(8,128)(2,1)S(1)}, bf16[128,2560]{1,0:T(8,128)(2,1)S(1)}, u32[]{:S(2)}, u32[]{:S(2)}) collective-permute-start(bf16[128,2560]{1,0:T(8,128)(2,1)S(1)} %slice.58), channel_id=1, source_target_pairs={{0,8},{4,12},{8,0},{12,4},{16,24},{20,28},{24,16},{28,20},{1,9},{5... | collective-permute-start | bytes 1966088 | tf_op jit(solution)/shard_map/ppermute | solution.py:115
  96.3 14.1 %collective-permute-start.12 = (bf16[128,2560]{1,0:T(8,128)(2,1)S(1)}, bf16[128,2560]{1,0:T(8,128)(2,1)S(1)}, u32[]{:S(2)}, u32[]{:S(2)}) collective-permute-start(bf16[128,2560]{1,0:T(8,128)(2,1)S(1)} %slice.59), channel_id=1, source_target_pairs={{0,16},{4,20},{8,24},{12,28},{16,0},{20,4},{24,8},{28,12},{1,17},{... | collective-permute-start | bytes 1966088 | tf_op jit(solution)/shard_map/ppermute | solution.py:115
  97.9 15.1 %collective-permute-start.14 = (s32[512]{0:T(512)S(1)}, s32[512]{0:T(512)S(1)}, u32[]{:S(2)}, u32[]{:S(2)}) collective-permute-start(s32[512]{0:T(512)S(1)} %get-tuple-element.120), channel_id=1, source_target_pairs={{0,4},{4,8},{8,12},{12,16},{16,20},{20,24},{24,28},{1,5},{5,9},{9,... | collective-permute-start | bytes 6152 | tf_op jit(solution)/shard_map/ppermute | solution.py:25
  99.2 18.6 %collective-permute-start.6 = (bf16[256,2560]{1,0:T(8,128)(2,1)S(1)}, bf16[256,2560]{1,0:T(8,128)(2,1)}, u32[]{:S(2)}, u32[]{:S(2)}) collective-permute-start(bf16[256,2560]{1,0:T(8,128)(2,1)S(1)} %copy-done), channel_id=1, source_target_pairs={{0,4},{4,0},{8,12},{12,8},{16,20},{20,16},{24,28},{28,24},{1,5},{5... | collective-permute-start | bytes 3932168 | tf_op jit(solution)/shard_map/ppermute | solution.py:115
  100.6 17.3 %collective-permute-start.10 = (bf16[256,2560]{1,0:T(8,128)(2,1)S(1)}, bf16[256,2560]{1,0:T(8,128)(2,1)}, u32[]{:S(2)}, u32[]{:S(2)}) collective-permute-start(bf16[256,2560]{1,0:T(8,128)(2,1)S(1)} %collective-permute-done.9.refs_4_), channel_id=1, source_target_pairs={{0,4},{4,0},{8,12},{12,8},{16,20},{20,16},{24,28},{28,24},{1,5},{5... | collective-permute-start | bytes 3932168 | tf_op jit(solution)/shard_map/ppermute | solution.py:115
  107.5 10.3 %collective-permute-start.8 = (bf16[256,2560]{1,0:T(8,128)(2,1)}, bf16[256,2560]{1,0:T(8,128)(2,1)}, u32[]{:S(2)}, u32[]{:S(2)}) collective-permute-start(bf16[256,2560]{1,0:T(8,128)(2,1)} %collective-permute-done.7.refs_2_), channel_id=1, source_target_pairs={{0,4},{4,0},{8,12},{12,8},{16,20},{20,16},{24,28},{28,24},{1,5},{5... | collective-permute-start | bytes 3932168 | tf_op jit(solution)/shard_map/ppermute | solution.py:115
  111.3 6.6 %collective-permute-start.13 = (bf16[256,2560]{1,0:T(8,128)(2,1)}, bf16[256,2560]{1,0:T(8,128)(2,1)}, u32[]{:S(2)}, u32[]{:S(2)}) collective-permute-start(bf16[256,2560]{1,0:T(8,128)(2,1)} %constant_dynamic-update-slice_fusion.refs_6_), channel_id=1, source_target_pairs={{0,4},{4,0},{8,12},{12,8},{16,20},{20,16},{24,28},{28,24},{1,5},{5... | collective-permute-start | bytes 3932168 | tf_op jit(solution)/shard_map/ppermute | solution.py:115
  116.6 1.3 copy-start.3
  116.6 1.3 copy-start.5
  139.8 41.7 %collective-permute-start.16 = (bf16[2,512,512]{2,1,0:T(8,128)(2,1)}, bf16[2,512,512]{2,1,0:T(8,128)(2,1)S(1)}, u32[]{:S(2)}, u32[]{:S(2)}) collective-permute-start(bf16[2,512,512]{2,1,0:T(8,128)(2,1)} %get-tuple-element.91), channel_id=1, source_target_pairs={{0,4},{4,8},{8,12},{12,16},{16,20},{20,24},{24,28},{1,5},{5,9},{9,... | collective-permute-start | bytes 3145736 | tf_op jit(solution)/shard_map/ppermute | solution.py:25
  142.4 4.1 %copy-start.4 = (f32[1024,64]{1,0:T(8,128)S(1)}, f32[1024,64]{1,0:T(8,128)}, u32[]{:S(2)}) copy-start(f32[1024,64]{1,0:T(8,128)} %copy-done.3) | copy-start | bytes 786436
  142.4 4.1 %copy-start.6 = (f32[1024,64]{1,0:T(8,128)S(1)}, f32[1024,64]{1,0:T(8,128)}, u32[]{:S(2)}) copy-start(f32[1024,64]{1,0:T(8,128)} %copy-done.5) | copy-start | bytes 786436
  146.5 15.4 %collective-permute-start.15 = (bf16[256,512]{1,0:T(8,128)(2,1)}, bf16[256,512]{1,0:T(8,128)(2,1)S(1)}, u32[]{:S(2)}, u32[]{:S(2)}) collective-permute-start(bf16[256,512]{1,0:T(8,128)(2,1)} %attend.4.own_ref), channel_id=1, source_target_pairs={{0,1},{1,0},{2,3},{3,2},{4,5},{5,4},{6,7},{7,6},{8,9},{9,8},{10,11... | collective-permute-start | bytes 786440 | tf_op jit(solution)/shard_map/ppermute | solution.py:115
  162.0 6.5 %copy-start.18 = (bf16[256,512]{1,0:T(8,128)(2,1)}, bf16[256,512]{1,0:T(8,128)(2,1)S(1)}, u32[]{:S(2)}) copy-start(bf16[256,512]{1,0:T(8,128)(2,1)S(1)} %collective-permute-done.15.other_ref) | copy-start | bytes 786436
  172.4 23.4 %collective-permute-start.25 = (bf16[256,512]{1,0:T(8,128)(2,1)}, bf16[256,512]{1,0:T(8,128)(2,1)S(1)}, u32[]{:S(2)}, u32[]{:S(2)}) collective-permute-start(bf16[256,512]{1,0:T(8,128)(2,1)} %attend.7.own_ref), channel_id=1, source_target_pairs={{0,1},{1,0},{2,3},{3,2},{4,5},{5,4},{6,7},{7,6},{8,9},{9,8},{10,11... | collective-permute-start | bytes 786440 | tf_op jit(solution)/shard_map/ppermute | solution.py:115
  179.5 23.0 %collective-permute-start.21 = (bf16[256,512]{1,0:T(8,128)(2,1)}, bf16[256,512]{1,0:T(8,128)(2,1)S(1)}, u32[]{:S(2)}, u32[]{:S(2)}) collective-permute-start(bf16[256,512]{1,0:T(8,128)(2,1)} %get-tuple-element.98), channel_id=1, source_target_pairs={{1,3},{2,0},{5,7},{6,4},{9,11},{10,8},{13,15},{14,12},{17,19},{18,... | collective-permute-start | bytes 786440 | tf_op jit(solution)/shard_map/ppermute | solution.py:575
  180.8 22.7 %collective-permute-start.22 = (bf16[256,512]{1,0:T(8,128)(2,1)}, bf16[256,512]{1,0:T(8,128)(2,1)S(1)}, u32[]{:S(2)}, u32[]{:S(2)}) collective-permute-start(bf16[256,512]{1,0:T(8,128)(2,1)} %get-tuple-element.99), channel_id=1, source_target_pairs={{1,2},{2,1},{5,6},{6,5},{9,10},{10,9},{13,14},{14,13},{17,18},{18,... | collective-permute-start | bytes 786440 | tf_op jit(solution)/shard_map/ppermute | solution.py:576
  181.5 1.0 copy-start.2
  186.5 17.0 %collective-permute-start.20 = (bf16[256,512]{1,0:T(8,128)(2,1)}, bf16[256,512]{1,0:T(8,128)(2,1)S(1)}, u32[]{:S(2)}, u32[]{:S(2)}) collective-permute-start(bf16[256,512]{1,0:T(8,128)(2,1)} %attend.6.own_ref), channel_id=1, source_target_pairs={{0,1},{1,0},{2,3},{3,2},{4,5},{5,4},{6,7},{7,6},{8,9},{9,8},{10,11... | collective-permute-start | bytes 786440 | tf_op jit(solution)/shard_map/ppermute | solution.py:115
  195.9 15.0 %collective-permute-start.17 = (bf16[256,512]{1,0:T(8,128)(2,1)}, bf16[256,512]{1,0:T(8,128)(2,1)S(1)}, u32[]{:S(2)}, u32[]{:S(2)}) collective-permute-start(bf16[256,512]{1,0:T(8,128)(2,1)} %attend.5.own_ref), channel_id=1, source_target_pairs={{0,1},{1,0},{2,3},{3,2},{4,5},{5,4},{6,7},{7,6},{8,9},{9,8},{10,11... | collective-permute-start | bytes 786440 | tf_op jit(solution)/shard_map/ppermute | solution.py:115
  195.9 0.7 copy-start.17
  201.2 16.3 %collective-permute-start.26 = (bf16[256,512]{1,0:T(8,128)(2,1)}, bf16[256,512]{1,0:T(8,128)(2,1)S(1)}, u32[]{:S(2)}, u32[]{:S(2)}) collective-permute-start(bf16[256,512]{1,0:T(8,128)(2,1)} %get-tuple-element.106), channel_id=1, source_target_pairs={{1,3},{2,0},{5,7},{6,4},{9,11},{10,8},{13,15},{14,12},{17,19},{18,... | collective-permute-start | bytes 786440 | tf_op jit(solution)/shard_map/ppermute | solution.py:575
  202.5 6.3 %copy-start.13 = (bf16[256,512]{1,0:T(8,128)(2,1)}, bf16[256,512]{1,0:T(8,128)(2,1)S(1)}, u32[]{:S(2)}) copy-start(bf16[256,512]{1,0:T(8,128)(2,1)S(1)} %collective-permute-done.21.inner_ref) | copy-start | bytes 786436
  202.5 19.2 %collective-permute-start.27 = (bf16[256,512]{1,0:T(8,128)(2,1)}, bf16[256,512]{1,0:T(8,128)(2,1)S(1)}, u32[]{:S(2)}, u32[]{:S(2)}) collective-permute-start(bf16[256,512]{1,0:T(8,128)(2,1)} %get-tuple-element.107), channel_id=1, source_target_pairs={{1,2},{2,1},{5,6},{6,5},{9,10},{10,9},{13,14},{14,13},{17,18},{18,... | collective-permute-start | bytes 786440 | tf_op jit(solution)/shard_map/ppermute | solution.py:576
  203.4 5.4 %copy-start.14 = (bf16[256,512]{1,0:T(8,128)(2,1)}, bf16[256,512]{1,0:T(8,128)(2,1)S(1)}, u32[]{:S(2)}) copy-start(bf16[256,512]{1,0:T(8,128)(2,1)S(1)} %collective-permute-done.22.outer_ref) | copy-start | bytes 786436
  203.5 0.7 copy-start.16
  208.9 16.9 %collective-permute-start.23 = (bf16[256,512]{1,0:T(8,128)(2,1)}, bf16[256,512]{1,0:T(8,128)(2,1)S(1)}, u32[]{:S(2)}, u32[]{:S(2)}) collective-permute-start(bf16[256,512]{1,0:T(8,128)(2,1)} %get-tuple-element.103), channel_id=1, source_target_pairs={{1,3},{2,0},{5,7},{6,4},{9,11},{10,8},{13,15},{14,12},{17,19},{18,... | collective-permute-start | bytes 786440 | tf_op jit(solution)/shard_map/ppermute | solution.py:575
  210.2 15.6 %collective-permute-start.24 = (bf16[256,512]{1,0:T(8,128)(2,1)}, bf16[256,512]{1,0:T(8,128)(2,1)S(1)}, u32[]{:S(2)}, u32[]{:S(2)}) collective-permute-start(bf16[256,512]{1,0:T(8,128)(2,1)} %get-tuple-element.104), channel_id=1, source_target_pairs={{1,2},{2,1},{5,6},{6,5},{9,10},{10,9},{13,14},{14,13},{17,18},{18,... | collective-permute-start | bytes 786440 | tf_op jit(solution)/shard_map/ppermute | solution.py:576
  210.9 0.7 copy-start.15
  216.2 18.4 %collective-permute-start.18 = (bf16[256,512]{1,0:T(8,128)(2,1)}, bf16[256,512]{1,0:T(8,128)(2,1)S(1)}, u32[]{:S(2)}, u32[]{:S(2)}) collective-permute-start(bf16[256,512]{1,0:T(8,128)(2,1)} %get-tuple-element.93), channel_id=1, source_target_pairs={{1,3},{2,0},{5,7},{6,4},{9,11},{10,8},{13,15},{14,12},{17,19},{18,... | collective-permute-start | bytes 786440 | tf_op jit(solution)/shard_map/ppermute | solution.py:575
  217.5 4.1 %copy-start.19 = (bf16[256,512]{1,0:T(8,128)(2,1)}, bf16[256,512]{1,0:T(8,128)(2,1)S(1)}, u32[]{:S(2)}) copy-start(bf16[256,512]{1,0:T(8,128)(2,1)S(1)} %collective-permute-done.26.inner_ref) | copy-start | bytes 786436
  217.5 17.1 %collective-permute-start.19 = (bf16[256,512]{1,0:T(8,128)(2,1)}, bf16[256,512]{1,0:T(8,128)(2,1)S(1)}, u32[]{:S(2)}, u32[]{:S(2)}) collective-permute-start(bf16[256,512]{1,0:T(8,128)(2,1)} %get-tuple-element.94), channel_id=1, source_target_pairs={{1,2},{2,1},{5,6},{6,5},{9,10},{10,9},{13,14},{14,13},{17,18},{18,... | collective-permute-start | bytes 786440 | tf_op jit(solution)/shard_map/ppermute | solution.py:576
  221.7 0.7 copy-start.20
  225.8 0.7 copy-start.21
  225.8 0.8 copy-start.22
  234.6 0.7 copy-start.23
  234.6 0.8 copy-start.24
Sparse Core Ops, SparseCore 0:
  59.6 69.4 all-gather.4
  130.7 29.2 all-gather.2

commit v14 on v11

--- a/solution.py
+++ b/solution.py
@@ -121,7 +121,14 @@
         return [lax.all_gather(part, "blk", axis=0, tiled=True)]
     pieces = {0: part}
     for mask in range(2, count, 2):
-        pieces[mask] = swapped(part, "blk", mask)
+        if mask & (mask - 1):
+            low = mask & -mask
+            cut = part.shape[0] // 2
+            halves = [swapped(pieces[mask ^ low][:cut], "blk", low)]
+            halves.append(swapped(pieces[low][cut:], "blk", mask ^ low))
+            pieces[mask] = jnp.concatenate(halves, axis=0)
+        else:
+            pieces[mask] = swapped(part, "blk", mask)
     for mask in range(0, count, 2):
         pieces[mask + 1] = swapped(pieces[mask], "blk", 1)
     return [pieces[mask] for mask in range(count)]
@@ -593,9 +600,9 @@
     result = None
     for chunk in reversed(range(last + 1)):
         kept, inner, outer = parts[chunk]
+        outer = lax.ppermute(outer, "mp", [(1, 3), (2, 0)])
         inner = lax.ppermute(inner, "mp", [(1, 2), (2, 1)])
-        outer = lax.ppermute(outer, "mp", [(1, 3), (2, 0)])
-        updates = [kept, inner, outer]
+        updates = [kept, outer, inner]
         result = final(hc_static, streams, sums_all, updates, chunk * CHUNK, result)
     return result
 

time: 251 us -> 252 us (level)
  local copies, waits for them, and re-layouts: 7.15 us -> 10.3 us
  starting transfers between devices: 41.5 us -> 38.4 us
    ppermute x11 -> x12, waiting for transfers between devices: 58.8 us -> 46.2 us  [swapped(): lax.ppermute(value, axis, [(source, source ^ mask) for source in range(co...]
    all_gather x2, waiting for transfers between devices: 4.98 us -> 16.4 us  [gathered(): rows = lax.all_gather(normed, 'mp', axis=0, tiled=True)]
    ppermute x11 -> x12, starting transfers between devices: 18.4 us -> 15.2 us  [swapped(): lax.ppermute(value, axis, [(source, source ^ mask) for source in range(co...]
    unnamed x50 -> x57, local copies, waits for them, and re-layouts: 4.67 us -> 5.72 us
  transfers between devices with their start and end apart: 29 -> 30, of which waited for: 11 -> 12; matrix products, arithmetic and copies ran while one was open for 3% -> 4% of each run, Pallas kernels for 30% -> 30%
where the time goes in v14:
time: 252 us; the launch traced here: 251 us
  waiting for transfers between devices  95 us (38%)
  Pallas kernels  84.6 us (34%)
  starting transfers between devices  38.4 us (15%)
  between operations  15.2 us (6%)
  local copies, waits for them, and re-layouts  10.3 us (4%)
  other arithmetic  7.07 us (3%)
    ppermute x12, waiting for transfers between devices, swapped(): lax.ppermute(value, axis, [(source, source ^ mask) for source in range(co...  46.2 us
    pallas_call x6, Pallas kernels, output_step(): pl.pallas_call(functools.partial(output_kernel, bool(attends), bool(proje...  32.5 us
    pallas_call x2, Pallas kernels, qkv_columns(): pl.pallas_call(qkv_kernel, grid=(3,), in_specs=[pl.BlockSpec(memory_space...  17.1 us
    all_gather x2, waiting for transfers between devices, gathered(): rows = lax.all_gather(normed, 'mp', axis=0, tiled=True)  16.4 us
    ppermute x12, starting transfers between devices, swapped(): lax.ppermute(value, axis, [(source, source ^ mask) for source in range(co...  15.2 us
    pallas_call x4, Pallas kernels, final(): pl.pallas_call(final_kernel, grid=(tokens // STEP,), in_specs=specs, out_...  13.6 us
    ppermute x3, waiting for transfers between devices, body(): lax.ppermute(parts[step], 'mp', [(at, (at + step) % group_size) for at in...  12.1 us
    ppermute x4, waiting for transfers between devices, body(): outer = lax.ppermute(outer, 'mp', [(1, 3), (2, 0)])  11.7 us
  transfers between devices with their start and end apart: 30, of which 12 were waited for; matrix products, arithmetic and copies ran while one was open for 4% of the time, Pallas kernels for 30%

profile of v14, /device:TPU:0, one launch (start us, length us, event | category | flops | bytes accessed | tf_op | source)
XLA Modules:
  0.0 250.5 jit_solution(15482330009070862971)
XLA Ops:
  6.7 1.4 maximum_maximum_fusion.proj_ref
  8.1 6.4 %stats.1.own_ref = f32[8,5248]{1,0:T(8,128)} custom-call(bf16[1024,4,512]{2,1,0:T(4,128)(2,1)} %x_ref.13, f32[8,512]{1,0:T(8,128)} %maximum_maximum_fusion.proj_ref), custom_call_target="tpu_custom_call" | custom-call | flops 1258291200 | bytes 4194304 | tf_op jit(solution)/shard_map/stats/pallas_call | solution.py:178
  14.4 5.0 %collective-permute-start.2 = (f32[8,5248]{1,0:T(8,128)}, f32[8,5248]{1,0:T(8,128)S(1)}, u32[]{:S(2)}, u32[]{:S(2)}) collective-permute-start(f32[8,5248]{1,0:T(8,128)} %stats.1.own_ref), channel_id=1, source_target_pairs={{0,3},{1,0},{2,1},{3,2},{4,7},{5,4},{6,5},{7,6},{8,11},{9,8},{10,9... | collective-permute-start | bytes 503816 | tf_op jit(solution)/shard_map/ppermute | solution.py:31
  19.5 1.0 collective-permute-start
  20.5 4.9 %regroup.1 = (bf16[64,2560]{1,0:T(8,128)(2,1)}, bf16[64,2560]{1,0:T(8,128)(2,1)}, bf16[64,2560]{1,0:T(8,128)(2,1)}, bf16[64,2560]{1,0:T(8,128)(2,1)}) custom-call(s32[1]{0:T(128)} %bitcast.1.place_ref.refs_9_.refs_0_, f32[64,4,2048]{2,1,0:T(4,128)} %master_ref.1), custom_call_target="tpu_custom_call" | custom-call | bytes 3407872 | tf_op jit(solution)/shard_map/regroup/pallas_call | solution.py:79
  25.4 8.5 %collective-permute-done.1.b_ref = f32[8,5248]{1,0:T(8,128)S(1)} collective-permute-done((f32[8,5248]{1,0:T(8,128)}, f32[8,5248]{1,0:T(8,128)S(1)}, u32[]{:S(2)}, u32[]{:S(2)}) %collective-permute-start.1) | collective-permute-done | bytes 167968 | tf_op jit(solution)/shard_map/ppermute | solution.py:31
  33.9 1.0 collective-permute-start.3
  34.9 1.8 collective-permute-start.4
  36.7 2.9 %collective-permute-start.5 = (bf16[64,2560]{1,0:T(8,128)(2,1)}, bf16[64,2560]{1,0:T(8,128)(2,1)S(1)}, u32[]{:S(2)}, u32[]{:S(2)}) collective-permute-start(bf16[64,2560]{1,0:T(8,128)(2,1)} %get-tuple-element.69), channel_id=1, source_target_pairs={{0,3},{1,0},{2,1},{3,2},{4,7},{5,4},{6,5},{7,6},{8,11},{9,8},{10,9... | collective-permute-start | bytes 983048 | tf_op jit(solution)/shard_map/ppermute | solution.py:536
  39.7 2.9 %mix.3 = (f32[8,5248]{1,0:T(8,128)}, bf16[256,512]{1,0:T(8,128)(2,1)}) custom-call(f32[4,6]{1,0:T(4,128)} %static_ref.11, bf16[1024,4,512]{2,1,0:T(4,128)(2,1)} %x_ref.13, f32[8,5248]{1,0:T(8,128)} %stats.1.own_ref, f32[8,5248]{1,0:T(8,128)} %copy-done.9, f32[8,5248]{1,0:T(8,128)} %copy-done.8, f32[8,5248]{1,0:T(8,128)} %copy-done.7), custom_call_target="tpu_custom_call" | custom-call | flops 209715200 | bytes 1310720 | tf_op jit(solution)/shard_map/mix/pallas_call | solution.py:249
  42.5 4.9 %mix.2 = (f32[8,5248]{1,0:T(8,128)}, bf16[768,512]{1,0:T(8,128)(2,1)}) custom-call(f32[4,6]{1,0:T(4,128)} %static_ref.11, bf16[1024,4,512]{2,1,0:T(4,128)(2,1)} %x_ref.13, f32[8,5248]{1,0:T(8,128)} %stats.1.own_ref, f32[8,5248]{1,0:T(8,128)} %copy-done.9, f32[8,5248]{1,0:T(8,128)} %copy-done.8, f32[8,5248]{1,0:T(8,128)} %copy-done.7), custom_call_target="tpu_custom_call" | custom-call | flops 629145600 | bytes 3932160 | tf_op jit(solution)/shard_map/mix/pallas_call | solution.py:249
  47.4 12.1 %collective-permute-done.4.refs_2_ = bf16[64,2560]{1,0:T(8,128)(2,1)S(1)} collective-permute-done((bf16[64,2560]{1,0:T(8,128)(2,1)}, bf16[64,2560]{1,0:T(8,128)(2,1)S(1)}, u32[]{:S(2)}, u32[]{:S(2)}) %collective-permute-start.4) | collective-permute-done | bytes 327712 | tf_op jit(solution)/shard_map/ppermute | solution.py:536
  60.3 2.5 assemble.1.refs_0_.refs_13_.refs_4_
  62.8 1.5 collective-permute-start.9
  64.3 1.5 collective-permute-start.7
  65.8 26.4 %collective-permute-done.9.refs_4_.refs_17_.refs_8_ = bf16[256,2560]{1,0:T(8,128)(2,1)S(1)} collective-permute-done((bf16[256,2560]{1,0:T(8,128)(2,1)}, bf16[256,2560]{1,0:T(8,128)(2,1)S(1)}, u32[]{:S(2)}, u32[]{:S(2)}) %collective-permute-start.9) | collective-permute-done | bytes 1310752 | tf_op jit(solution)/shard_map/ppermute | solution.py:115
  92.3 1.5 collective-permute-start.11
  95.1 1.3 collective-permute-start.14
  96.4 1.1 slice.59
  97.6 2.2 collective-permute-start.12
  100.4 7.1 %collective-permute-done.11 = bf16[128,2560]{1,0:T(8,128)(2,1)S(1)} collective-permute-done((bf16[128,2560]{1,0:T(8,128)(2,1)S(1)}, bf16[128,2560]{1,0:T(8,128)(2,1)S(1)}, u32[]{:S(2)}, u32[]{:S(2)}) %collective-permute-start.11) | collective-permute-done | bytes 655392 | tf_op jit(solution)/shard_map/ppermute | solution.py:115
  107.5 0.9 constant_dynamic-update-slice_fusion.1
  108.4 6.8 %collective-permute-done.12 = bf16[128,2560]{1,0:T(8,128)(2,1)S(1)} collective-permute-done((bf16[128,2560]{1,0:T(8,128)(2,1)S(1)}, bf16[128,2560]{1,0:T(8,128)(2,1)S(1)}, u32[]{:S(2)}, u32[]{:S(2)}) %collective-permute-start.12) | collective-permute-done | bytes 655392 | tf_op jit(solution)/shard_map/ppermute | solution.py:115
  115.2 0.9 constant_dynamic-update-slice_fusion.refs_6_.refs_19_.refs_10_
  117.2 1.0 copy.14.refs_7_
  118.3 1.6 convert_reduce_fusion
  119.9 1.9 multiply_sine_fusion
  121.8 1.2 fusion.1
  123.1 6.0 %all-gather.5.cloned.1.call-done = bf16[3072,512]{1,0:T(8,128)(2,1)} async-done(((bf16[768,512]{1,0:T(8,128)(2,1)}), bf16[3072,512]{1,0:T(8,128)(2,1)}) %all-gather.5.cloned.1.call-update) | async-done | bytes 3145744 | tf_op jit(solution)/shard_map/all_gather | solution.py:532
  129.1 10.6 %qkv.2 = (bf16[3,768,512]{2,1,0:T(8,128)(2,1)}, bf16[2,512,512]{2,1,0:T(8,128)(2,1)}) custom-call(s32[1]{0:T(128)} %bitcast.2.ring_ref.refs_10_.refs_1_, bf16[4,768,512]{2,1,0:T(8,128)(2,1)} %bitcast.13, f32[768,128]{1,0:T(8,128)} %get-tuple-element.124.cosine_ref, f32[768,128]{1,0:T(8,128)} %get-tuple-element.123.sine_ref, ...), custom_call_target="tpu_custom_call" | custom-call | flops 4831838208 | bytes 14155776 | tf_op jit(solution)/shard_map/qkv/pallas_call | solution.py:305
  139.7 1.9 collective-permute-start.16
  142.4 4.1 %attend.2.refs_11_ = bf16[256,512]{1,0:T(8,128)(2,1)} custom-call(bf16[3,768,512]{2,1,0:T(8,128)(2,1)} %get-tuple-element.87.refs_0_.refs_1_.refs_2_.refs_3_.refs_4_.refs_5_.refs_6_, bf16[3,768,512]{2,1,0:T(8,128)(2,1)} %get-tuple-element.87.refs_0_.refs_1_.refs_2_.refs_3_.refs_4_.refs_5_.refs_6_, ...), custom_call_target="tpu_custom_call" | custom-call | flops 402653184 | bytes 786432 | tf_op jit(solution)/shard_map/attend/pallas_call | solution.py:430
  146.5 1.8 collective-permute-start.15
  148.4 0.9 pad_maximum_fusion
  149.2 10.4 %all-gather.3.cloned.1.call-done = bf16[1024,512]{1,0:T(8,128)(2,1)} async-done(((bf16[256,512]{1,0:T(8,128)(2,1)}), bf16[1024,512]{1,0:T(8,128)(2,1)}) %all-gather.3.cloned.1.call-update) | async-done | bytes 1048592 | tf_op jit(solution)/shard_map/all_gather | solution.py:532
  159.7 2.3 collective-permute-done.15.refs_12_
  161.9 6.5 %qkv.3 = (bf16[3,256,512]{2,1,0:T(8,128)(2,1)}, bf16[2,256,512]{2,1,0:T(8,128)(2,1)}) custom-call(s32[1]{0:T(128)} %bitcast.2.ring_ref.refs_10_.refs_1_, bf16[4,256,512]{2,1,0:T(8,128)(2,1)} %bitcast.10, f32[256,128]{1,0:T(8,128)} %get-tuple-element.126.cosine_ref, f32[256,128]{1,0:T(8,128)} %get-tuple-element.125.sine_ref, ...), custom_call_target="tpu_custom_call" | custom-call | flops 1610612736 | bytes 8912896 | tf_op jit(solution)/shard_map/qkv/pallas_call | solution.py:305
  168.4 7.5 %output.2 = (bf16[256,512]{1,0:T(8,128)(2,1)}, f32[256,512]{1,0:T(8,128)}, bf16[256,512]{1,0:T(8,128)(2,1)}, bf16[256,512]{1,0:T(8,128)(2,1)}) custom-call(bf16[3,768,512]{2,1,0:T(8,128)(2,1)} %get-tuple-element.87.refs_0_.refs_1_.refs_2_.refs_3_.refs_4_.refs_5_.refs_6_, ...), custom_call_target="tpu_custom_call" | custom-call | flops 1476395008 | bytes 2883584 | tf_op jit(solution)/shard_map/output/pallas_call | solution.py:430
  175.9 2.5 collective-permute-start.17
  178.4 1.3 collective-permute-start.26
  179.7 1.0 copy-done.2
  180.7 4.0 %attend.3.refs_2_ = bf16[256,512]{1,0:T(8,128)(2,1)} custom-call(bf16[3,768,512]{2,1,0:T(8,128)(2,1)} %get-tuple-element.87.refs_0_.refs_1_.refs_2_.refs_3_.refs_4_.refs_5_.refs_6_, bf16[2,512,512]{2,1,0:T(8,128)(2,1)} %copy-done.2, bf16[3,256,512]{2,1,0:T(8,128)(2,1)} %get-tuple-element.89.refs_1_.refs_4_.refs_0_.refs_3_.refs_6_.refs_2_.refs_5_, ...), custom_call_target="tpu_custom_call" | custom-call | flops 402653184 | bytes 786432 | tf_op jit(solution)/shard_map/attend/pallas_call | solution.py:430
  184.7 3.1 %collective-permute-start.21 = (bf16[256,512]{1,0:T(8,128)(2,1)}, bf16[256,512]{1,0:T(8,128)(2,1)S(1)}, u32[]{:S(2)}, u32[]{:S(2)}) collective-permute-start(bf16[256,512]{1,0:T(8,128)(2,1)} %attend.3.refs_2_), channel_id=1, source_target_pairs={{0,1},{1,0},{2,3},{3,2},{4,5},{5,4},{6,7},{7,6},{8,9},{9,8},{10,11... | collective-permute-start | bytes 786440 | tf_op jit(solution)/shard_map/ppermute | solution.py:115
  187.8 3.5 %collective-permute-done.17.refs_12_ = bf16[256,512]{1,0:T(8,128)(2,1)S(1)} collective-permute-done((bf16[256,512]{1,0:T(8,128)(2,1)}, bf16[256,512]{1,0:T(8,128)(2,1)S(1)}, u32[]{:S(2)}, u32[]{:S(2)}) %collective-permute-start.17) | collective-permute-done | bytes 262176 | tf_op jit(solution)/shard_map/ppermute | solution.py:115
  191.4 0.7 copy-done.14
  192.1 7.3 %output.3 = (bf16[256,512]{1,0:T(8,128)(2,1)}, f32[256,512]{1,0:T(8,128)}, bf16[256,512]{1,0:T(8,128)(2,1)}, bf16[256,512]{1,0:T(8,128)(2,1)}) custom-call(bf16[3,256,512]{2,1,0:T(8,128)(2,1)} %get-tuple-element.89.refs_1_.refs_4_.refs_0_.refs_3_.refs_6_.refs_2_.refs_5_, bf16[2,512,512]{2,1,0:T(8,128)(2,1)} %copy-done.2, bf16[2,512,512]{2,1,0:T(8,128)(2,1)} %copy-done.2, ...), custom_call_target="tpu_custom_call" | custom-call | flops 1476395008 | bytes 2883584 | tf_op jit(solution)/shard_map/output/pallas_call | solution.py:430
  199.5 0.7 collective-permute-start.27
  200.2 1.3 collective-permute-start.24
  201.5 0.7 collective-permute-start.25
  202.2 4.8 %project.3 = (f32[256,512]{1,0:T(8,128)}, bf16[256,512]{1,0:T(8,128)(2,1)}, bf16[256,512]{1,0:T(8,128)(2,1)}) custom-call(s32[1]{0:T(128)} %bitcast.1.place_ref.refs_9_.refs_0_, s32[1]{0:T(128)} %bitcast.2.ring_ref.refs_10_.refs_1_, bf16[256,512]{1,0:T(8,128)(2,1)} %attend.3.refs_2_, bf16[256,512]{1,0:T(8,128)(2,1)} %copy-done.18, ...), custom_call_target="tpu_custom_call" | custom-call | flops 1073741824 | bytes 2097152 | tf_op jit(solution)/shard_map/project/pallas_call | solution.py:430
  207.0 1.3 collective-permute-start.22
  208.3 0.7 collective-permute-start.23
  209.0 4.8 %project.2 = (f32[256,512]{1,0:T(8,128)}, bf16[256,512]{1,0:T(8,128)(2,1)}, bf16[256,512]{1,0:T(8,128)(2,1)}) custom-call(s32[1]{0:T(128)} %bitcast.1.place_ref.refs_9_.refs_0_, s32[1]{0:T(128)} %bitcast.2.ring_ref.refs_10_.refs_1_, bf16[256,512]{1,0:T(8,128)(2,1)} %get-tuple-element.96.refs_2_, bf16[256,512]{1,0:T(8,128)(2,1)} %copy-done.17, ...), custom_call_target="tpu_custom_call" | custom-call | flops 1073741824 | bytes 2097152 | tf_op jit(solution)/shard_map/project/pallas_call | solution.py:430
  213.8 1.5 collective-permute-start.19
  215.3 2.4 collective-permute-done.24.inner_ref
  218.4 3.4 %final.4.rest_0_ = bf16[1024,4,512]{2,1,0:T(4,128)(2,1)} custom-call(f32[4,6]{1,0:T(4,128)} %static_ref.11, bf16[1024,4,512]{2,1,0:T(4,128)(2,1)} %x_ref.13, f32[8,5248]{1,0:T(8,128)} %get-tuple-element.65.first_ref.folded_ref.column_ref, f32[8,5248]{1,0:T(8,128)} %get-tuple-element.65.first_ref.folded_ref.column_ref, ...), custom_call_target="tpu_custom_call" | custom-call | flops 629145600 | bytes 2883584 | tf_op jit(solution)/shard_map/final/pallas_call | solution.py:505
  221.8 0.7 copy-done.20
  222.6 3.4 %final.5.rest_0_ = bf16[1024,4,512]{2,1,0:T(4,128)(2,1)} custom-call(f32[4,6]{1,0:T(4,128)} %static_ref.11, bf16[1024,4,512]{2,1,0:T(4,128)(2,1)} %x_ref.13, f32[8,5248]{1,0:T(8,128)} %get-tuple-element.65.first_ref.folded_ref.column_ref, f32[8,5248]{1,0:T(8,128)} %get-tuple-element.65.first_ref.folded_ref.column_ref, ...), custom_call_target="tpu_custom_call", output_to_operand_aliasing={{}: (8, {})} | custom-call | flops 629145600 | bytes 2883584 | tf_op jit(solution)/shard_map/final/pallas_call | solution.py:505
  225.9 3.0 %collective-permute-done.22.inner_ref = bf16[256,512]{1,0:T(8,128)(2,1)S(1)} collective-permute-done((bf16[256,512]{1,0:T(8,128)(2,1)}, bf16[256,512]{1,0:T(8,128)(2,1)S(1)}, u32[]{:S(2)}, u32[]{:S(2)}) %collective-permute-start.22) | collective-permute-done | bytes 262176 | tf_op jit(solution)/shard_map/ppermute | solution.py:603
  228.9 0.7 copy-done.21
  229.7 3.4 %final.6.rest_0_ = bf16[1024,4,512]{2,1,0:T(4,128)(2,1)} custom-call(f32[4,6]{1,0:T(4,128)} %static_ref.11, bf16[1024,4,512]{2,1,0:T(4,128)(2,1)} %x_ref.13, f32[8,5248]{1,0:T(8,128)} %get-tuple-element.65.first_ref.folded_ref.column_ref, f32[8,5248]{1,0:T(8,128)} %get-tuple-element.65.first_ref.folded_ref.column_ref, ...), custom_call_target="tpu_custom_call", output_to_operand_aliasing={{}: (8, {})} | custom-call | flops 629145600 | bytes 2883584 | tf_op jit(solution)/shard_map/final/pallas_call | solution.py:505
  233.1 6.4 %collective-permute-done.19.inner_ref = bf16[256,512]{1,0:T(8,128)(2,1)S(1)} collective-permute-done((bf16[256,512]{1,0:T(8,128)(2,1)}, bf16[256,512]{1,0:T(8,128)(2,1)S(1)}, u32[]{:S(2)}, u32[]{:S(2)}) %collective-permute-start.19) | collective-permute-done | bytes 262176 | tf_op jit(solution)/shard_map/ppermute | solution.py:603
  239.5 0.7 copy-done.23
  240.3 3.4 %final.7 = bf16[1024,4,512]{2,1,0:T(4,128)(2,1)} custom-call(f32[4,6]{1,0:T(4,128)} %static_ref.11, bf16[1024,4,512]{2,1,0:T(4,128)(2,1)} %x_ref.13, f32[8,5248]{1,0:T(8,128)} %get-tuple-element.65.first_ref.folded_ref.column_ref, f32[8,5248]{1,0:T(8,128)} %get-tuple-element.65.first_ref.folded_ref.column_ref, ...), custom_call_target="tpu_custom_call", output_to_operand_aliasing={{}: (8, {})} | custom-call | flops 629145600 | bytes 2883584 | tf_op jit(solution)/shard_map/final/pallas_call | solution.py:505
  (100 shorter events, 4.4 us)
Async XLA Ops:
  6.5 122.6 %all-gather.5.cloned.1.call-start = ((), (), s32[]{:S(2)}) async-start(), calls=%async_computation.1 | async-start | bytes 3932160 | tf_op jit(solution)/shard_map/all_gather | solution.py:532
  14.4 11.0 %collective-permute-start.2 = (f32[8,5248]{1,0:T(8,128)}, f32[8,5248]{1,0:T(8,128)S(1)}, u32[]{:S(2)}, u32[]{:S(2)}) collective-permute-start(f32[8,5248]{1,0:T(8,128)} %stats.1.own_ref), channel_id=1, source_target_pairs={{0,3},{1,0},{2,1},{3,2},{4,7},{5,4},{6,5},{7,6},{8,11},{9,8},{10,9... | collective-permute-start | bytes 503816 | tf_op jit(solution)/shard_map/ppermute | solution.py:31
  19.5 14.4 %collective-permute-start.1 = (f32[8,5248]{1,0:T(8,128)}, f32[8,5248]{1,0:T(8,128)S(1)}, u32[]{:S(2)}, u32[]{:S(2)}) collective-permute-start(f32[8,5248]{1,0:T(8,128)} %stats.1.own_ref), channel_id=1, source_target_pairs={{0,2},{1,3},{2,0},{3,1},{4,6},{5,7},{6,4},{7,5},{8,10},{9,11},{10,... | collective-permute-start | bytes 503816 | tf_op jit(solution)/shard_map/ppermute | solution.py:31
  19.5 14.4 %collective-permute-start = (f32[8,5248]{1,0:T(8,128)}, f32[8,5248]{1,0:T(8,128)S(1)}, u32[]{:S(2)}, u32[]{:S(2)}) collective-permute-start(f32[8,5248]{1,0:T(8,128)} %stats.1.own_ref), channel_id=1, source_target_pairs={{0,1},{1,2},{2,3},{3,0},{4,5},{5,6},{6,7},{7,4},{8,9},{9,10},{10,1... | collective-permute-start | bytes 503816 | tf_op jit(solution)/shard_map/ppermute | solution.py:31
  25.4 14.2 %copy-start.7 = (f32[8,5248]{1,0:T(8,128)}, f32[8,5248]{1,0:T(8,128)S(1)}, u32[]{:S(2)}) copy-start(f32[8,5248]{1,0:T(8,128)S(1)} %collective-permute-done.2.c_ref) | copy-start | bytes 503812
  33.9 5.7 %copy-start.8 = (f32[8,5248]{1,0:T(8,128)}, f32[8,5248]{1,0:T(8,128)S(1)}, u32[]{:S(2)}) copy-start(f32[8,5248]{1,0:T(8,128)S(1)} %collective-permute-done.1.b_ref) | copy-start | bytes 503812
  33.9 5.7 %copy-start.9 = (f32[8,5248]{1,0:T(8,128)}, f32[8,5248]{1,0:T(8,128)S(1)}, u32[]{:S(2)}) copy-start(f32[8,5248]{1,0:T(8,128)S(1)} %collective-permute-done.a_ref) | copy-start | bytes 503812
  33.9 13.5 %collective-permute-start.3 = (bf16[64,2560]{1,0:T(8,128)(2,1)}, bf16[64,2560]{1,0:T(8,128)(2,1)S(1)}, u32[]{:S(2)}, u32[]{:S(2)}) collective-permute-start(bf16[64,2560]{1,0:T(8,128)(2,1)} %get-tuple-element.67), channel_id=1, source_target_pairs={{0,1},{1,2},{2,3},{3,0},{4,5},{5,6},{6,7},{7,4},{8,9},{9,10},{10,1... | collective-permute-start | bytes 983048 | tf_op jit(solution)/shard_map/ppermute | solution.py:536
  34.9 24.5 %collective-permute-start.4 = (bf16[64,2560]{1,0:T(8,128)(2,1)}, bf16[64,2560]{1,0:T(8,128)(2,1)S(1)}, u32[]{:S(2)}, u32[]{:S(2)}) collective-permute-start(bf16[64,2560]{1,0:T(8,128)(2,1)} %get-tuple-element.68), channel_id=1, source_target_pairs={{0,2},{1,3},{2,0},{3,1},{4,6},{5,7},{6,4},{7,5},{8,10},{9,11},{10,... | collective-permute-start | bytes 983048 | tf_op jit(solution)/shard_map/ppermute | solution.py:536
  36.7 22.7 %collective-permute-start.5 = (bf16[64,2560]{1,0:T(8,128)(2,1)}, bf16[64,2560]{1,0:T(8,128)(2,1)S(1)}, u32[]{:S(2)}, u32[]{:S(2)}) collective-permute-start(bf16[64,2560]{1,0:T(8,128)(2,1)} %get-tuple-element.69), channel_id=1, source_target_pairs={{0,3},{1,0},{2,1},{3,2},{4,7},{5,4},{6,5},{7,6},{8,11},{9,8},{10,9... | collective-permute-start | bytes 983048 | tf_op jit(solution)/shard_map/ppermute | solution.py:536
  47.4 12.2 %copy-start.10 = (bf16[64,2560]{1,0:T(8,128)(2,1)}, bf16[64,2560]{1,0:T(8,128)(2,1)S(1)}, u32[]{:S(2)}) copy-start(bf16[64,2560]{1,0:T(8,128)(2,1)S(1)} %collective-permute-done.3.refs_1_) | copy-start | bytes 983044
  59.5 0.7 copy-start.11
  59.5 0.8 copy-start.12
  59.5 34.3 %copy-start.26 = (s32[2]{0:T(128)S(1)}, s32[2]{0:T(128)}, u32[]{:S(2)}) copy-start(s32[2]{0:T(128)} %param.11) | copy-start | bytes 28
  59.5 35.6 %copy-start.25 = (s32[1024]{0:T(1024)S(1)}, s32[1024]{0:T(1024)}, u32[]{:S(2)}) copy-start(s32[1024]{0:T(1024)} %param.10) | copy-start | bytes 12292
  59.5 100.1 %all-gather.3.cloned.1.call-start = ((), (), s32[]{:S(2)}) async-start(), calls=%async_computation | async-start | bytes 1310720 | tf_op jit(solution)/shard_map/all_gather | solution.py:532
  62.8 37.0 %copy-start = (bf16[256,2560]{1,0:T(8,128)(2,1)S(1)}, bf16[256,2560]{1,0:T(8,128)(2,1)}, u32[]{:S(2)}) copy-start(bf16[256,2560]{1,0:T(8,128)(2,1)} %assemble.1.refs_0_.refs_13_.refs_4_) | copy-start | bytes 3932164
  62.8 29.4 %collective-permute-start.9 = (bf16[256,2560]{1,0:T(8,128)(2,1)}, bf16[256,2560]{1,0:T(8,128)(2,1)S(1)}, u32[]{:S(2)}, u32[]{:S(2)}) collective-permute-start(bf16[256,2560]{1,0:T(8,128)(2,1)} %assemble.1.refs_0_.refs_13_.refs_4_), channel_id=1, source_target_pairs={{0,16},{4,20},{8,24},{12,28},{16,0},{20,4},{24,8},{28,12},{1,17},{... | collective-permute-start | bytes 3932168 | tf_op jit(solution)/shard_map/ppermute | solution.py:115
  64.3 32.1 %collective-permute-start.7 = (bf16[256,2560]{1,0:T(8,128)(2,1)}, bf16[256,2560]{1,0:T(8,128)(2,1)}, u32[]{:S(2)}, u32[]{:S(2)}) collective-permute-start(bf16[256,2560]{1,0:T(8,128)(2,1)} %assemble.1.refs_0_.refs_13_.refs_4_), channel_id=1, source_target_pairs={{0,8},{4,12},{8,0},{12,4},{16,24},{20,28},{24,16},{28,20},{1,9},{5... | collective-permute-start | bytes 3932168 | tf_op jit(solution)/shard_map/ppermute | solution.py:115
  92.2 16.2 %copy-start.1 = (bf16[256,2560]{1,0:T(8,128)(2,1)}, bf16[256,2560]{1,0:T(8,128)(2,1)S(1)}, u32[]{:S(2)}) copy-start(bf16[256,2560]{1,0:T(8,128)(2,1)S(1)} %collective-permute-done.9.refs_4_.refs_17_.refs_8_) | copy-start | bytes 3932164
  92.3 15.3 %collective-permute-start.11 = (bf16[128,2560]{1,0:T(8,128)(2,1)S(1)}, bf16[128,2560]{1,0:T(8,128)(2,1)S(1)}, u32[]{:S(2)}, u32[]{:S(2)}) collective-permute-start(bf16[128,2560]{1,0:T(8,128)(2,1)S(1)} %slice.58), channel_id=1, source_target_pairs={{0,8},{4,12},{8,0},{12,4},{16,24},{20,28},{24,16},{28,20},{1,9},{5... | collective-permute-start | bytes 1966088 | tf_op jit(solution)/shard_map/ppermute | solution.py:115
  95.1 23.2 %collective-permute-start.14 = (s32[512]{0:T(512)S(1)}, s32[512]{0:T(512)S(1)}, u32[]{:S(2)}, u32[]{:S(2)}) collective-permute-start(s32[512]{0:T(512)S(1)} %get-tuple-element.118), channel_id=1, source_target_pairs={{0,4},{4,8},{8,12},{12,16},{16,20},{20,24},{24,28},{1,5},{5,9},{9,... | collective-permute-start | bytes 6152 | tf_op jit(solution)/shard_map/ppermute | solution.py:25
  97.6 17.7 %collective-permute-start.12 = (bf16[128,2560]{1,0:T(8,128)(2,1)S(1)}, bf16[128,2560]{1,0:T(8,128)(2,1)S(1)}, u32[]{:S(2)}, u32[]{:S(2)}) collective-permute-start(bf16[128,2560]{1,0:T(8,128)(2,1)S(1)} %slice.59), channel_id=1, source_target_pairs={{0,16},{4,20},{8,24},{12,28},{16,0},{20,4},{24,8},{28,12},{1,17},{... | collective-permute-start | bytes 1966088 | tf_op jit(solution)/shard_map/ppermute | solution.py:115
  99.8 23.3 %collective-permute-start.6 = (bf16[256,2560]{1,0:T(8,128)(2,1)S(1)}, bf16[256,2560]{1,0:T(8,128)(2,1)}, u32[]{:S(2)}, u32[]{:S(2)}) collective-permute-start(bf16[256,2560]{1,0:T(8,128)(2,1)S(1)} %copy-done), channel_id=1, source_target_pairs={{0,4},{4,0},{8,12},{12,8},{16,20},{20,16},{24,28},{28,24},{1,5},{5... | collective-permute-start | bytes 3932168 | tf_op jit(solution)/shard_map/ppermute | solution.py:115
  100.2 22.9 %collective-permute-start.10 = (bf16[256,2560]{1,0:T(8,128)(2,1)S(1)}, bf16[256,2560]{1,0:T(8,128)(2,1)}, u32[]{:S(2)}, u32[]{:S(2)}) collective-permute-start(bf16[256,2560]{1,0:T(8,128)(2,1)S(1)} %collective-permute-done.9.refs_4_.refs_17_.refs_8_), channel_id=1, source_target_pairs={{0,4},{4,0},{8,12},{12,8},{16,20},{20,16},{24,28},{28,24},{1,5},{5... | collective-permute-start | bytes 3932168 | tf_op jit(solution)/shard_map/ppermute | solution.py:115
  107.5 15.6 %collective-permute-start.8 = (bf16[256,2560]{1,0:T(8,128)(2,1)}, bf16[256,2560]{1,0:T(8,128)(2,1)}, u32[]{:S(2)}, u32[]{:S(2)}) collective-permute-start(bf16[256,2560]{1,0:T(8,128)(2,1)} %collective-permute-done.7.refs_2_.refs_15_.refs_6_), channel_id=1, source_target_pairs={{0,4},{4,0},{8,12},{12,8},{16,20},{20,16},{24,28},{28,24},{1,5},{5... | collective-permute-start | bytes 3932168 | tf_op jit(solution)/shard_map/ppermute | solution.py:115
  116.1 7.0 %collective-permute-start.13 = (bf16[256,2560]{1,0:T(8,128)(2,1)}, bf16[256,2560]{1,0:T(8,128)(2,1)}, u32[]{:S(2)}, u32[]{:S(2)}) collective-permute-start(bf16[256,2560]{1,0:T(8,128)(2,1)} %constant_dynamic-update-slice_fusion.refs_6_.refs_19_.refs_10_), channel_id=1, source_target_pairs={{0,4},{4,0},{8,12},{12,8},{16,20},{20,16},{24,28},{28,24},{1,5},{5... | collective-permute-start | bytes 3932168 | tf_op jit(solution)/shard_map/ppermute | solution.py:115
  121.8 1.3 copy-start.3
  121.8 1.3 copy-start.5
  139.7 39.9 %collective-permute-start.16 = (bf16[2,512,512]{2,1,0:T(8,128)(2,1)}, bf16[2,512,512]{2,1,0:T(8,128)(2,1)S(1)}, u32[]{:S(2)}, u32[]{:S(2)}) collective-permute-start(bf16[2,512,512]{2,1,0:T(8,128)(2,1)} %get-tuple-element.90), channel_id=1, source_target_pairs={{0,4},{4,8},{8,12},{12,16},{16,20},{20,24},{24,28},{1,5},{5,9},{9,... | collective-permute-start | bytes 3145736 | tf_op jit(solution)/shard_map/ppermute | solution.py:25
  142.4 6.0 %copy-start.4 = (f32[1024,64]{1,0:T(8,128)S(1)}, f32[1024,64]{1,0:T(8,128)}, u32[]{:S(2)}) copy-start(f32[1024,64]{1,0:T(8,128)} %copy-done.3) | copy-start | bytes 786436
  142.4 6.0 %copy-start.6 = (f32[1024,64]{1,0:T(8,128)S(1)}, f32[1024,64]{1,0:T(8,128)}, u32[]{:S(2)}) copy-start(f32[1024,64]{1,0:T(8,128)} %copy-done.5) | copy-start | bytes 786436
  146.5 15.4 %collective-permute-start.15 = (bf16[256,512]{1,0:T(8,128)(2,1)}, bf16[256,512]{1,0:T(8,128)(2,1)S(1)}, u32[]{:S(2)}, u32[]{:S(2)}) collective-permute-start(bf16[256,512]{1,0:T(8,128)(2,1)} %attend.2.refs_11_), channel_id=1, source_target_pairs={{0,1},{1,0},{2,3},{3,2},{4,5},{5,4},{6,7},{7,6},{8,9},{9,8},{10,11... | collective-permute-start | bytes 786440 | tf_op jit(solution)/shard_map/ppermute | solution.py:115
  161.9 6.5 %copy-start.13 = (bf16[256,512]{1,0:T(8,128)(2,1)}, bf16[256,512]{1,0:T(8,128)(2,1)S(1)}, u32[]{:S(2)}) copy-start(bf16[256,512]{1,0:T(8,128)(2,1)S(1)} %collective-permute-done.15.refs_12_) | copy-start | bytes 786436
  175.9 15.5 %collective-permute-start.17 = (bf16[256,512]{1,0:T(8,128)(2,1)}, bf16[256,512]{1,0:T(8,128)(2,1)S(1)}, u32[]{:S(2)}, u32[]{:S(2)}) collective-permute-start(bf16[256,512]{1,0:T(8,128)(2,1)} %get-tuple-element.95.refs_11_), channel_id=1, source_target_pairs={{0,1},{1,0},{2,3},{3,2},{4,5},{5,4},{6,7},{7,6},{8,9},{9,8},{10,11... | collective-permute-start | bytes 786440 | tf_op jit(solution)/shard_map/ppermute | solution.py:115
  178.4 28.6 %collective-permute-start.26 = (bf16[256,512]{1,0:T(8,128)(2,1)}, bf16[256,512]{1,0:T(8,128)(2,1)S(1)}, u32[]{:S(2)}, u32[]{:S(2)}) collective-permute-start(bf16[256,512]{1,0:T(8,128)(2,1)} %get-tuple-element.107), channel_id=1, source_target_pairs={{1,3},{2,0},{5,7},{6,4},{9,11},{10,8},{13,15},{14,12},{17,19},{18,... | collective-permute-start | bytes 786440 | tf_op jit(solution)/shard_map/ppermute | solution.py:603
  179.7 1.0 copy-start.2
  184.7 14.8 %copy-start.27 = (bf16[256,512]{1,0:T(8,128)(2,1)S(1)}, bf16[256,512]{1,0:T(8,128)(2,1)}, u32[]{:S(2)}) copy-start(bf16[256,512]{1,0:T(8,128)(2,1)} %get-tuple-element.108) | copy-start | bytes 786436
  184.7 16.8 %collective-permute-start.21 = (bf16[256,512]{1,0:T(8,128)(2,1)}, bf16[256,512]{1,0:T(8,128)(2,1)S(1)}, u32[]{:S(2)}, u32[]{:S(2)}) collective-permute-start(bf16[256,512]{1,0:T(8,128)(2,1)} %attend.3.refs_2_), channel_id=1, source_target_pairs={{0,1},{1,0},{2,3},{3,2},{4,5},{5,4},{6,7},{7,6},{8,9},{9,8},{10,11... | collective-permute-start | bytes 786440 | tf_op jit(solution)/shard_map/ppermute | solution.py:115
  191.4 0.7 copy-start.14
  199.4 8.9 %collective-permute-start.18 = (bf16[256,512]{1,0:T(8,128)(2,1)}, bf16[256,512]{1,0:T(8,128)(2,1)S(1)}, u32[]{:S(2)}, u32[]{:S(2)}) collective-permute-start(bf16[256,512]{1,0:T(8,128)(2,1)} %get-tuple-element.96.refs_2_), channel_id=1, source_target_pairs={{0,1},{1,0},{2,3},{3,2},{4,5},{5,4},{6,7},{7,6},{8,9},{9,8},{10,11... | collective-permute-start | bytes 786440 | tf_op jit(solution)/shard_map/ppermute | solution.py:115
  199.5 14.3 %collective-permute-start.27 = (bf16[256,512]{1,0:T(8,128)(2,1)S(1)}, bf16[256,512]{1,0:T(8,128)(2,1)S(1)}, u32[]{:S(2)}, u32[]{:S(2)}) collective-permute-start(bf16[256,512]{1,0:T(8,128)(2,1)S(1)} %copy-done.27), channel_id=1, source_target_pairs={{1,2},{2,1},{5,6},{6,5},{9,10},{10,9},{13,14},{14,13},{17,18},{18,... | collective-permute-start | bytes 786440 | tf_op jit(solution)/shard_map/ppermute | solution.py:604
  200.2 17.5 %collective-permute-start.24 = (bf16[256,512]{1,0:T(8,128)(2,1)}, bf16[256,512]{1,0:T(8,128)(2,1)S(1)}, u32[]{:S(2)}, u32[]{:S(2)}) collective-permute-start(bf16[256,512]{1,0:T(8,128)(2,1)} %get-tuple-element.104), channel_id=1, source_target_pairs={{1,3},{2,0},{5,7},{6,4},{9,11},{10,8},{13,15},{14,12},{17,19},{18,... | collective-permute-start | bytes 786440 | tf_op jit(solution)/shard_map/ppermute | solution.py:603
  201.5 0.7 copy-start.18
  201.5 20.3 %collective-permute-start.25 = (bf16[256,512]{1,0:T(8,128)(2,1)}, bf16[256,512]{1,0:T(8,128)(2,1)S(1)}, u32[]{:S(2)}, u32[]{:S(2)}) collective-permute-start(bf16[256,512]{1,0:T(8,128)(2,1)} %get-tuple-element.105), channel_id=1, source_target_pairs={{1,2},{2,1},{5,6},{6,5},{9,10},{10,9},{13,14},{14,13},{17,18},{18,... | collective-permute-start | bytes 786440 | tf_op jit(solution)/shard_map/ppermute | solution.py:604
  207.0 6.8 %copy-start.15 = (bf16[256,512]{1,0:T(8,128)(2,1)}, bf16[256,512]{1,0:T(8,128)(2,1)S(1)}, u32[]{:S(2)}) copy-start(bf16[256,512]{1,0:T(8,128)(2,1)S(1)} %collective-permute-done.26.inner_ref) | copy-start | bytes 786436
  207.0 21.9 %collective-permute-start.22 = (bf16[256,512]{1,0:T(8,128)(2,1)}, bf16[256,512]{1,0:T(8,128)(2,1)S(1)}, u32[]{:S(2)}, u32[]{:S(2)}) collective-permute-start(bf16[256,512]{1,0:T(8,128)(2,1)} %get-tuple-element.101), channel_id=1, source_target_pairs={{1,3},{2,0},{5,7},{6,4},{9,11},{10,8},{13,15},{14,12},{17,19},{18,... | collective-permute-start | bytes 786440 | tf_op jit(solution)/shard_map/ppermute | solution.py:603
  208.3 0.7 copy-start.17
  208.3 20.6 %collective-permute-start.23 = (bf16[256,512]{1,0:T(8,128)(2,1)}, bf16[256,512]{1,0:T(8,128)(2,1)S(1)}, u32[]{:S(2)}, u32[]{:S(2)}) collective-permute-start(bf16[256,512]{1,0:T(8,128)(2,1)} %get-tuple-element.102), channel_id=1, source_target_pairs={{1,2},{2,1},{5,6},{6,5},{9,10},{10,9},{13,14},{14,13},{17,18},{18,... | collective-permute-start | bytes 786440 | tf_op jit(solution)/shard_map/ppermute | solution.py:604
  213.8 4.6 %copy-start.16 = (bf16[256,512]{1,0:T(8,128)(2,1)}, bf16[256,512]{1,0:T(8,128)(2,1)S(1)}, u32[]{:S(2)}) copy-start(bf16[256,512]{1,0:T(8,128)(2,1)S(1)} %collective-permute-done.27.outer_ref) | copy-start | bytes 786436
  213.8 25.7 %collective-permute-start.19 = (bf16[256,512]{1,0:T(8,128)(2,1)}, bf16[256,512]{1,0:T(8,128)(2,1)S(1)}, u32[]{:S(2)}, u32[]{:S(2)}) collective-permute-start(bf16[256,512]{1,0:T(8,128)(2,1)} %get-tuple-element.98), channel_id=1, source_target_pairs={{1,3},{2,0},{5,7},{6,4},{9,11},{10,8},{13,15},{14,12},{17,19},{18,... | collective-permute-start | bytes 786440 | tf_op jit(solution)/shard_map/ppermute | solution.py:603
  217.7 4.1 %copy-start.19 = (bf16[256,512]{1,0:T(8,128)(2,1)}, bf16[256,512]{1,0:T(8,128)(2,1)S(1)}, u32[]{:S(2)}) copy-start(bf16[256,512]{1,0:T(8,128)(2,1)S(1)} %collective-permute-done.24.inner_ref) | copy-start | bytes 786436
  217.7 21.8 %collective-permute-start.20 = (bf16[256,512]{1,0:T(8,128)(2,1)}, bf16[256,512]{1,0:T(8,128)(2,1)S(1)}, u32[]{:S(2)}, u32[]{:S(2)}) collective-permute-start(bf16[256,512]{1,0:T(8,128)(2,1)} %get-tuple-element.99), channel_id=1, source_target_pairs={{1,2},{2,1},{5,6},{6,5},{9,10},{10,9},{13,14},{14,13},{17,18},{18,... | collective-permute-start | bytes 786440 | tf_op jit(solution)/shard_map/ppermute | solution.py:604
  221.8 0.7 copy-start.20
  228.9 0.7 copy-start.21
  228.9 0.8 copy-start.22
  239.5 0.7 copy-start.23
  239.5 0.8 copy-start.24
Sparse Core Ops, SparseCore 0:
  59.6 69.4 all-gather.4
  130.7 28.9 all-gather.2

commit v15 on v12

--- a/solution.py
+++ b/solution.py
@@ -388,12 +388,16 @@
             rows = pieces[0][server * width : (server + 1) * width, :]
             sums[server] = contract(both, rows, 1, 1)
     else:
+        within = (place == 1) | (place == 2)
         for piece in range(len(pieces)):
             target = ring_ref[0] ^ piece
+            server = target // (width // depth)
             inside = pl.multiple_of((target % (width // depth)) * depth, depth)
-            sums[target // (width // depth), :, pl.ds(inside, depth)] = contract(
-                both, pieces[piece][...], 1, 1
-            )
+
+            @pl.when(jnp.where(within, server != place ^ 1, server == place))
+            def _():
+                sums[server, :, pl.ds(inside, depth)] = contract(both, pieces[piece][...], 1, 1)
+
     kept_ref[...] = sums[place]
     low = place < 2
     inner_ref[...] = sums[jnp.where(low, 2, 1)].astype(BF)

time: 247 us -> 247 us (level)
  transfers between devices with their start and end apart: 30 -> 30, of which waited for: 11 -> 11; matrix products, arithmetic and copies ran while one was open for 4% -> 4% of each run, Pallas kernels for 32% -> 31%
where the time goes in v15:
time: 247 us; the launch traced here: 244 us
  waiting for transfers between devices  90.2 us (37%)
  Pallas kernels  85.7 us (35%)
  starting transfers between devices  35.9 us (15%)
  between operations  15.2 us (6%)
  local copies, waits for them, and re-layouts  10.3 us (4%)
  other arithmetic  7.04 us (3%)
    ppermute x12, waiting for transfers between devices, swapped(): lax.ppermute(value, axis, [(source, source ^ mask) for source in range(co...  36.9 us
    all_gather x2, waiting for transfers between devices, gathered(): rows = lax.all_gather(normed, 'mp', axis=0, tiled=True)  24.6 us
    pallas_call x4, Pallas kernels, project(): pl.pallas_call(project_kernel, grid=(1,), in_specs=[pl.BlockSpec(memory_s...  17.3 us
    pallas_call x2, Pallas kernels, qkv_columns(): pl.pallas_call(qkv_kernel, grid=(3,), in_specs=[pl.BlockSpec(memory_space...  17.1 us
    pallas_call x4, Pallas kernels, attend(): pl.pallas_call(attend_kernel, grid=(1,), in_specs=[pl.BlockSpec(block, la...  16.2 us
    pallas_call x4, Pallas kernels, final(): pl.pallas_call(final_kernel, grid=(tokens // STEP,), in_specs=specs, out_...  13.6 us
    ppermute x12, starting transfers between devices, swapped(): lax.ppermute(value, axis, [(source, source ^ mask) for source in range(co...  12.9 us
    ppermute x3, waiting for transfers between devices, body(): lax.ppermute(parts[step], 'mp', [(at, (at + step) % group_size) for at in...  12.1 us
  transfers between devices with their start and end apart: 30, of which 11 were waited for; matrix products, arithmetic and copies ran while one was open for 4% of the time, Pallas kernels for 31%

profile of v15, /device:TPU:0, one launch (start us, length us, event | category | flops | bytes accessed | tf_op | source)
XLA Modules:
  0.0 244.2 jit_solution(6158693667705965908)
XLA Ops:
  6.7 1.4 maximum_maximum_fusion.proj_ref
  8.1 6.4 %stats.1.own_ref = f32[8,5248]{1,0:T(8,128)} custom-call(bf16[1024,4,512]{2,1,0:T(4,128)(2,1)} %x_ref.13, f32[8,512]{1,0:T(8,128)} %maximum_maximum_fusion.proj_ref), custom_call_target="tpu_custom_call" | custom-call | flops 1258291200 | bytes 4194304 | tf_op jit(solution)/shard_map/stats/pallas_call | solution.py:178
  14.4 5.0 %collective-permute-start.2 = (f32[8,5248]{1,0:T(8,128)}, f32[8,5248]{1,0:T(8,128)S(1)}, u32[]{:S(2)}, u32[]{:S(2)}) collective-permute-start(f32[8,5248]{1,0:T(8,128)} %stats.1.own_ref), channel_id=1, source_target_pairs={{0,3},{1,0},{2,1},{3,2},{4,7},{5,4},{6,5},{7,6},{8,11},{9,8},{10,9... | collective-permute-start | bytes 503816 | tf_op jit(solution)/shard_map/ppermute | solution.py:31
  19.5 1.0 collective-permute-start
  20.5 4.9 %regroup.1 = (bf16[64,2560]{1,0:T(8,128)(2,1)}, bf16[64,2560]{1,0:T(8,128)(2,1)}, bf16[64,2560]{1,0:T(8,128)(2,1)}, bf16[64,2560]{1,0:T(8,128)(2,1)}) custom-call(s32[1]{0:T(128)} %bitcast.1.place_ref, f32[64,4,2048]{2,1,0:T(4,128)} %master_ref.1), custom_call_target="tpu_custom_call" | custom-call | bytes 3407872 | tf_op jit(solution)/shard_map/regroup/pallas_call | solution.py:79
  25.4 8.5 %collective-permute-done.1.b_ref = f32[8,5248]{1,0:T(8,128)S(1)} collective-permute-done((f32[8,5248]{1,0:T(8,128)}, f32[8,5248]{1,0:T(8,128)S(1)}, u32[]{:S(2)}, u32[]{:S(2)}) %collective-permute-start.1) | collective-permute-done | bytes 167968 | tf_op jit(solution)/shard_map/ppermute | solution.py:31
  33.9 1.0 collective-permute-start.3
  34.9 1.8 collective-permute-start.4
  36.7 2.9 %collective-permute-start.5 = (bf16[64,2560]{1,0:T(8,128)(2,1)}, bf16[64,2560]{1,0:T(8,128)(2,1)S(1)}, u32[]{:S(2)}, u32[]{:S(2)}) collective-permute-start(bf16[64,2560]{1,0:T(8,128)(2,1)} %get-tuple-element.65), channel_id=1, source_target_pairs={{0,3},{1,0},{2,1},{3,2},{4,7},{5,4},{6,5},{7,6},{8,11},{9,8},{10,9... | collective-permute-start | bytes 983048 | tf_op jit(solution)/shard_map/ppermute | solution.py:523
  39.7 2.9 %mix.3 = (f32[8,5248]{1,0:T(8,128)}, bf16[256,512]{1,0:T(8,128)(2,1)}) custom-call(f32[4,6]{1,0:T(4,128)} %static_ref.11, bf16[1024,4,512]{2,1,0:T(4,128)(2,1)} %x_ref.13, f32[8,5248]{1,0:T(8,128)} %stats.1.own_ref, f32[8,5248]{1,0:T(8,128)} %copy-done.9, f32[8,5248]{1,0:T(8,128)} %copy-done.8, f32[8,5248]{1,0:T(8,128)} %copy-done.7), custom_call_target="tpu_custom_call" | custom-call | flops 209715200 | bytes 1310720 | tf_op jit(solution)/shard_map/mix/pallas_call | solution.py:249
  42.6 4.9 %mix.2 = (f32[8,5248]{1,0:T(8,128)}, bf16[768,512]{1,0:T(8,128)(2,1)}) custom-call(f32[4,6]{1,0:T(4,128)} %static_ref.11, bf16[1024,4,512]{2,1,0:T(4,128)(2,1)} %x_ref.13, f32[8,5248]{1,0:T(8,128)} %stats.1.own_ref, f32[8,5248]{1,0:T(8,128)} %copy-done.9, f32[8,5248]{1,0:T(8,128)} %copy-done.8, f32[8,5248]{1,0:T(8,128)} %copy-done.7), custom_call_target="tpu_custom_call" | custom-call | flops 629145600 | bytes 3932160 | tf_op jit(solution)/shard_map/mix/pallas_call | solution.py:249
  47.4 12.1 %collective-permute-done.4.refs_2_ = bf16[64,2560]{1,0:T(8,128)(2,1)S(1)} collective-permute-done((bf16[64,2560]{1,0:T(8,128)(2,1)}, bf16[64,2560]{1,0:T(8,128)(2,1)S(1)}, u32[]{:S(2)}, u32[]{:S(2)}) %collective-permute-start.4) | collective-permute-done | bytes 327712 | tf_op jit(solution)/shard_map/ppermute | solution.py:523
  60.3 2.5 %assemble.1.refs_0_ = bf16[256,2560]{1,0:T(8,128)(2,1)} custom-call(s32[1]{0:T(128)} %bitcast.1.place_ref, bf16[64,2560]{1,0:T(8,128)(2,1)} %get-tuple-element.70.refs_0_, bf16[64,2560]{1,0:T(8,128)(2,1)} %copy-done.10, bf16[64,2560]{1,0:T(8,128)(2,1)} %copy-done.11, bf16[64,2560]{1,0:T(8,128)(2,1)} %copy-done.12), custom_call_target="tpu_custom_call" | custom-call | bytes 2621440 | tf_op jit(solution)/shard_map/assemble/pallas_call | solution.py:101
  62.8 1.6 collective-permute-start.9
  64.4 1.5 collective-permute-start.7
  65.9 26.4 %collective-permute-done.9.refs_4_ = bf16[256,2560]{1,0:T(8,128)(2,1)S(1)} collective-permute-done((bf16[256,2560]{1,0:T(8,128)(2,1)}, bf16[256,2560]{1,0:T(8,128)(2,1)S(1)}, u32[]{:S(2)}, u32[]{:S(2)}) %collective-permute-start.9) | collective-permute-done | bytes 1310752 | tf_op jit(solution)/shard_map/ppermute | solution.py:115
  92.3 1.5 collective-permute-start.11
  94.4 1.1 slice.59
  95.5 1.1 collective-permute-start.12
  97.9 1.3 collective-permute-start.14
  99.2 1.3 collective-permute-start.6
  100.6 6.9 %collective-permute-done.11 = bf16[128,2560]{1,0:T(8,128)(2,1)S(1)} collective-permute-done((bf16[128,2560]{1,0:T(8,128)(2,1)S(1)}, bf16[128,2560]{1,0:T(8,128)(2,1)S(1)}, u32[]{:S(2)}, u32[]{:S(2)}) %collective-permute-start.11) | collective-permute-done | bytes 655392 | tf_op jit(solution)/shard_map/ppermute | solution.py:115
  107.6 0.9 constant_dynamic-update-slice_fusion.1
  108.4 0.7 collective-permute-done.12
  109.1 0.9 constant_dynamic-update-slice_fusion.refs_6_
  110.8 1.6 convert_reduce_fusion
  112.4 1.9 multiply_sine_fusion
  114.3 1.2 fusion.1
  115.6 13.5 %all-gather.5.cloned.1.call-done = bf16[3072,512]{1,0:T(8,128)(2,1)} async-done(((bf16[768,512]{1,0:T(8,128)(2,1)}), bf16[3072,512]{1,0:T(8,128)(2,1)}) %all-gather.5.cloned.1.call-update) | async-done | bytes 3145744 | tf_op jit(solution)/shard_map/all_gather | solution.py:519
  129.1 10.6 %qkv.2 = (bf16[3,768,512]{2,1,0:T(8,128)(2,1)}, bf16[2,512,512]{2,1,0:T(8,128)(2,1)}) custom-call(s32[1]{0:T(128)} %bitcast.2.ring_ref, bf16[4,768,512]{2,1,0:T(8,128)(2,1)} %bitcast.13, f32[768,128]{1,0:T(8,128)} %get-tuple-element.116.cosine_ref, f32[768,128]{1,0:T(8,128)} %get-tuple-element.115.sine_ref, bf16[256,2560]{1,0:T(8,128)(2,1)} %assemble.1.refs_0_, ...), custom_call_target="tpu_custom_call" | custom-call | flops 4831838208 | bytes 14155776 | tf_op jit(solution)/shard_map/qkv/pallas_call | solution.py:305
  139.7 1.9 collective-permute-start.16
  141.7 1.0 copy.14.qseg_ref
  143.4 4.1 %attend.4.own_ref = bf16[256,512]{1,0:T(8,128)(2,1)} custom-call(bf16[3,768,512]{2,1,0:T(8,128)(2,1)} %get-tuple-element.83.q_ref.k0.k1.k2.v0.v1.v2, bf16[3,768,512]{2,1,0:T(8,128)(2,1)} %get-tuple-element.83.q_ref.k0.k1.k2.v0.v1.v2, bf16[3,768,512]{2,1,0:T(8,128)(2,1)} %get-tuple-element.83.q_ref.k0.k1.k2.v0.v1.v2, ...), custom_call_target="tpu_custom_call" | custom-call | flops 402653184 | bytes 2097152 | tf_op jit(solution)/shard_map/attend/pallas_call | solution.py:359
  147.6 0.9 pad_maximum_fusion
  148.4 11.1 %all-gather.3.cloned.1.call-done = bf16[1024,512]{1,0:T(8,128)(2,1)} async-done(((bf16[256,512]{1,0:T(8,128)(2,1)}), bf16[1024,512]{1,0:T(8,128)(2,1)}) %all-gather.3.cloned.1.call-update) | async-done | bytes 1048592 | tf_op jit(solution)/shard_map/all_gather | solution.py:519
  159.5 2.4 collective-permute-done.15.other_ref
  161.9 6.5 %qkv.3 = (bf16[3,256,512]{2,1,0:T(8,128)(2,1)}, bf16[2,256,512]{2,1,0:T(8,128)(2,1)}) custom-call(s32[1]{0:T(128)} %bitcast.2.ring_ref, bf16[4,256,512]{2,1,0:T(8,128)(2,1)} %bitcast.10, f32[256,128]{1,0:T(8,128)} %get-tuple-element.118.cosine_ref, f32[256,128]{1,0:T(8,128)} %get-tuple-element.117.sine_ref, bf16[256,2560]{1,0:T(8,128)(2,1)} %assemble.1.refs_0_, ...), custom_call_target="tpu_custom_call" | custom-call | flops 1610612736 | bytes 8912896 | tf_op jit(solution)/shard_map/qkv/pallas_call | solution.py:305
  168.4 4.0 %attend.7.own_ref = bf16[256,512]{1,0:T(8,128)(2,1)} custom-call(bf16[3,768,512]{2,1,0:T(8,128)(2,1)} %get-tuple-element.83.q_ref.k0.k1.k2.v0.v1.v2, bf16[3,256,512]{2,1,0:T(8,128)(2,1)} %get-tuple-element.85.q_ref.k2.v2.k1.v1.k0.v0, bf16[3,768,512]{2,1,0:T(8,128)(2,1)} %get-tuple-element.83.q_ref.k0.k1.k2.v0.v1.v2, ...), custom_call_target="tpu_custom_call" | custom-call | flops 402653184 | bytes 2097152 | tf_op jit(solution)/shard_map/attend/pallas_call | solution.py:359
  172.4 2.4 collective-permute-start.23
  174.8 1.0 copy-done.2
  175.8 4.0 %attend.6.own_ref = bf16[256,512]{1,0:T(8,128)(2,1)} custom-call(bf16[3,768,512]{2,1,0:T(8,128)(2,1)} %get-tuple-element.83.q_ref.k0.k1.k2.v0.v1.v2, bf16[2,512,512]{2,1,0:T(8,128)(2,1)} %copy-done.2, bf16[3,256,512]{2,1,0:T(8,128)(2,1)} %get-tuple-element.85.q_ref.k2.v2.k1.v1.k0.v0, bf16[3,768,512]{2,1,0:T(8,128)(2,1)} %get-tuple-element.83.q_ref.k0.k1.k2.v0.v1.v2, ...), custom_call_target="tpu_custom_call" | custom-call | flops 402653184 | bytes 2097152 | tf_op jit(solution)/shard_map/attend/pallas_call | solution.py:359
  179.8 4.2 %project.7 = (f32[256,512]{1,0:T(8,128)}, bf16[256,512]{1,0:T(8,128)(2,1)}, bf16[256,512]{1,0:T(8,128)(2,1)}) custom-call(s32[1]{0:T(128)} %bitcast.1.place_ref, s32[1]{0:T(128)} %bitcast.2.ring_ref, bf16[256,512]{1,0:T(8,128)(2,1)} %attend.4.own_ref, bf16[256,512]{1,0:T(8,128)(2,1)} %copy-done.17, bf16[256,2560]{1,0:T(8,128)(2,1)} %assemble.1.refs_0_, ...), custom_call_target="tpu_custom_call" | custom-call | flops 1073741824 | bytes 5767168 | tf_op jit(solution)/shard_map/project/pallas_call | solution.py:413
  184.1 1.4 collective-permute-start.26
  185.5 4.0 %attend.5.own_ref = bf16[256,512]{1,0:T(8,128)(2,1)} custom-call(bf16[3,256,512]{2,1,0:T(8,128)(2,1)} %get-tuple-element.85.q_ref.k2.v2.k1.v1.k0.v0, bf16[2,512,512]{2,1,0:T(8,128)(2,1)} %copy-done.2, bf16[2,512,512]{2,1,0:T(8,128)(2,1)} %copy-done.2, bf16[3,256,512]{2,1,0:T(8,128)(2,1)} %get-tuple-element.85.q_ref.k2.v2.k1.v1.k0.v0, ...), custom_call_target="tpu_custom_call" | custom-call | flops 402653184 | bytes 2097152 | tf_op jit(solution)/shard_map/attend/pallas_call | solution.py:359
  189.5 3.4 %collective-permute-start.17 = (bf16[256,512]{1,0:T(8,128)(2,1)}, bf16[256,512]{1,0:T(8,128)(2,1)S(1)}, u32[]{:S(2)}, u32[]{:S(2)}) collective-permute-start(bf16[256,512]{1,0:T(8,128)(2,1)} %attend.5.own_ref), channel_id=1, source_target_pairs={{0,1},{1,0},{2,3},{3,2},{4,5},{5,4},{6,7},{7,6},{8,9},{9,8},{10,11... | collective-permute-start | bytes 786440 | tf_op jit(solution)/shard_map/ppermute | solution.py:115
  193.6 0.7 copy-done.18
  194.3 4.3 %project.6 = (f32[256,512]{1,0:T(8,128)}, bf16[256,512]{1,0:T(8,128)(2,1)}, bf16[256,512]{1,0:T(8,128)(2,1)}) custom-call(s32[1]{0:T(128)} %bitcast.1.place_ref, s32[1]{0:T(128)} %bitcast.2.ring_ref, bf16[256,512]{1,0:T(8,128)(2,1)} %attend.7.own_ref, bf16[256,512]{1,0:T(8,128)(2,1)} %copy-done.18, bf16[256,2560]{1,0:T(8,128)(2,1)} %assemble.1.refs_0_, ...), custom_call_target="tpu_custom_call" | custom-call | flops 1073741824 | bytes 5767168 | tf_op jit(solution)/shard_map/project/pallas_call | solution.py:413
  198.5 1.3 collective-permute-start.24
  199.9 0.7 collective-permute-start.25
  200.5 4.5 %project.5 = (f32[256,512]{1,0:T(8,128)}, bf16[256,512]{1,0:T(8,128)(2,1)}, bf16[256,512]{1,0:T(8,128)(2,1)}) custom-call(s32[1]{0:T(128)} %bitcast.1.place_ref, s32[1]{0:T(128)} %bitcast.2.ring_ref, bf16[256,512]{1,0:T(8,128)(2,1)} %attend.6.own_ref, bf16[256,512]{1,0:T(8,128)(2,1)} %copy-done.16, bf16[256,2560]{1,0:T(8,128)(2,1)} %assemble.1.refs_0_, ...), custom_call_target="tpu_custom_call" | custom-call | flops 1073741824 | bytes 5767168 | tf_op jit(solution)/shard_map/project/pallas_call | solution.py:413
  205.1 1.3 collective-permute-start.21
  206.4 0.7 collective-permute-start.22
  207.1 4.3 %project.4 = (f32[256,512]{1,0:T(8,128)}, bf16[256,512]{1,0:T(8,128)(2,1)}, bf16[256,512]{1,0:T(8,128)(2,1)}) custom-call(s32[1]{0:T(128)} %bitcast.1.place_ref, s32[1]{0:T(128)} %bitcast.2.ring_ref, bf16[256,512]{1,0:T(8,128)(2,1)} %attend.5.own_ref, bf16[256,512]{1,0:T(8,128)(2,1)} %copy-done.15, bf16[256,2560]{1,0:T(8,128)(2,1)} %assemble.1.refs_0_, ...), custom_call_target="tpu_custom_call" | custom-call | flops 1073741824 | bytes 5767168 | tf_op jit(solution)/shard_map/project/pallas_call | solution.py:413
  211.4 1.3 collective-permute-start.18
  212.7 0.7 collective-permute-start.19
  213.4 3.4 %final.4.rest_0_ = bf16[1024,4,512]{2,1,0:T(4,128)(2,1)} custom-call(f32[4,6]{1,0:T(4,128)} %static_ref.11, bf16[1024,4,512]{2,1,0:T(4,128)(2,1)} %x_ref.13, f32[8,5248]{1,0:T(8,128)} %get-tuple-element.61.first_ref.folded_ref.column_ref, f32[8,5248]{1,0:T(8,128)} %get-tuple-element.61.first_ref.folded_ref.column_ref, ...), custom_call_target="tpu_custom_call" | custom-call | flops 629145600 | bytes 2883584 | tf_op jit(solution)/shard_map/final/pallas_call | solution.py:492
  216.8 0.7 copy-done.20
  217.5 3.4 %final.5.rest_0_ = bf16[1024,4,512]{2,1,0:T(4,128)(2,1)} custom-call(f32[4,6]{1,0:T(4,128)} %static_ref.11, bf16[1024,4,512]{2,1,0:T(4,128)(2,1)} %x_ref.13, f32[8,5248]{1,0:T(8,128)} %get-tuple-element.61.first_ref.folded_ref.column_ref, f32[8,5248]{1,0:T(8,128)} %get-tuple-element.61.first_ref.folded_ref.column_ref, ...), custom_call_target="tpu_custom_call", output_to_operand_aliasing={{}: (8, {})} | custom-call | flops 629145600 | bytes 2883584 | tf_op jit(solution)/shard_map/final/pallas_call | solution.py:492
  220.9 1.0 collective-permute-done.21.inner_ref
  222.0 0.7 copy-done.21
  222.8 3.4 %final.6.rest_0_ = bf16[1024,4,512]{2,1,0:T(4,128)(2,1)} custom-call(f32[4,6]{1,0:T(4,128)} %static_ref.11, bf16[1024,4,512]{2,1,0:T(4,128)(2,1)} %x_ref.13, f32[8,5248]{1,0:T(8,128)} %get-tuple-element.61.first_ref.folded_ref.column_ref, f32[8,5248]{1,0:T(8,128)} %get-tuple-element.61.first_ref.folded_ref.column_ref, ...), custom_call_target="tpu_custom_call", output_to_operand_aliasing={{}: (8, {})} | custom-call | flops 629145600 | bytes 2883584 | tf_op jit(solution)/shard_map/final/pallas_call | solution.py:492
  226.2 7.0 %collective-permute-done.18.inner_ref = bf16[256,512]{1,0:T(8,128)(2,1)S(1)} collective-permute-done((bf16[256,512]{1,0:T(8,128)(2,1)}, bf16[256,512]{1,0:T(8,128)(2,1)S(1)}, u32[]{:S(2)}, u32[]{:S(2)}) %collective-permute-start.18) | collective-permute-done | bytes 262176 | tf_op jit(solution)/shard_map/ppermute | solution.py:584
  233.2 0.7 copy-done.23
  234.0 3.4 %final.7 = bf16[1024,4,512]{2,1,0:T(4,128)(2,1)} custom-call(f32[4,6]{1,0:T(4,128)} %static_ref.11, bf16[1024,4,512]{2,1,0:T(4,128)(2,1)} %x_ref.13, f32[8,5248]{1,0:T(8,128)} %get-tuple-element.61.first_ref.folded_ref.column_ref, f32[8,5248]{1,0:T(8,128)} %get-tuple-element.61.first_ref.folded_ref.column_ref, ...), custom_call_target="tpu_custom_call", output_to_operand_aliasing={{}: (8, {})} | custom-call | flops 629145600 | bytes 2883584 | tf_op jit(solution)/shard_map/final/pallas_call | solution.py:492
  (102 shorter events, 4.0 us)
Async XLA Ops:
  6.5 122.6 %all-gather.5.cloned.1.call-start = ((), (), s32[]{:S(2)}) async-start(), calls=%async_computation.1 | async-start | bytes 3932160 | tf_op jit(solution)/shard_map/all_gather | solution.py:519
  14.4 11.0 %collective-permute-start.2 = (f32[8,5248]{1,0:T(8,128)}, f32[8,5248]{1,0:T(8,128)S(1)}, u32[]{:S(2)}, u32[]{:S(2)}) collective-permute-start(f32[8,5248]{1,0:T(8,128)} %stats.1.own_ref), channel_id=1, source_target_pairs={{0,3},{1,0},{2,1},{3,2},{4,7},{5,4},{6,5},{7,6},{8,11},{9,8},{10,9... | collective-permute-start | bytes 503816 | tf_op jit(solution)/shard_map/ppermute | solution.py:31
  19.5 14.4 %collective-permute-start.1 = (f32[8,5248]{1,0:T(8,128)}, f32[8,5248]{1,0:T(8,128)S(1)}, u32[]{:S(2)}, u32[]{:S(2)}) collective-permute-start(f32[8,5248]{1,0:T(8,128)} %stats.1.own_ref), channel_id=1, source_target_pairs={{0,2},{1,3},{2,0},{3,1},{4,6},{5,7},{6,4},{7,5},{8,10},{9,11},{10,... | collective-permute-start | bytes 503816 | tf_op jit(solution)/shard_map/ppermute | solution.py:31
  19.5 14.4 %collective-permute-start = (f32[8,5248]{1,0:T(8,128)}, f32[8,5248]{1,0:T(8,128)S(1)}, u32[]{:S(2)}, u32[]{:S(2)}) collective-permute-start(f32[8,5248]{1,0:T(8,128)} %stats.1.own_ref), channel_id=1, source_target_pairs={{0,1},{1,2},{2,3},{3,0},{4,5},{5,6},{6,7},{7,4},{8,9},{9,10},{10,1... | collective-permute-start | bytes 503816 | tf_op jit(solution)/shard_map/ppermute | solution.py:31
  25.4 14.2 %copy-start.7 = (f32[8,5248]{1,0:T(8,128)}, f32[8,5248]{1,0:T(8,128)S(1)}, u32[]{:S(2)}) copy-start(f32[8,5248]{1,0:T(8,128)S(1)} %collective-permute-done.2.c_ref) | copy-start | bytes 503812
  33.9 5.7 %copy-start.8 = (f32[8,5248]{1,0:T(8,128)}, f32[8,5248]{1,0:T(8,128)S(1)}, u32[]{:S(2)}) copy-start(f32[8,5248]{1,0:T(8,128)S(1)} %collective-permute-done.1.b_ref) | copy-start | bytes 503812
  33.9 5.7 %copy-start.9 = (f32[8,5248]{1,0:T(8,128)}, f32[8,5248]{1,0:T(8,128)S(1)}, u32[]{:S(2)}) copy-start(f32[8,5248]{1,0:T(8,128)S(1)} %collective-permute-done.a_ref) | copy-start | bytes 503812
  33.9 13.5 %collective-permute-start.3 = (bf16[64,2560]{1,0:T(8,128)(2,1)}, bf16[64,2560]{1,0:T(8,128)(2,1)S(1)}, u32[]{:S(2)}, u32[]{:S(2)}) collective-permute-start(bf16[64,2560]{1,0:T(8,128)(2,1)} %get-tuple-element.63), channel_id=1, source_target_pairs={{0,1},{1,2},{2,3},{3,0},{4,5},{5,6},{6,7},{7,4},{8,9},{9,10},{10,1... | collective-permute-start | bytes 983048 | tf_op jit(solution)/shard_map/ppermute | solution.py:523
  34.9 24.5 %collective-permute-start.4 = (bf16[64,2560]{1,0:T(8,128)(2,1)}, bf16[64,2560]{1,0:T(8,128)(2,1)S(1)}, u32[]{:S(2)}, u32[]{:S(2)}) collective-permute-start(bf16[64,2560]{1,0:T(8,128)(2,1)} %get-tuple-element.64), channel_id=1, source_target_pairs={{0,2},{1,3},{2,0},{3,1},{4,6},{5,7},{6,4},{7,5},{8,10},{9,11},{10,... | collective-permute-start | bytes 983048 | tf_op jit(solution)/shard_map/ppermute | solution.py:523
  36.7 22.7 %collective-permute-start.5 = (bf16[64,2560]{1,0:T(8,128)(2,1)}, bf16[64,2560]{1,0:T(8,128)(2,1)S(1)}, u32[]{:S(2)}, u32[]{:S(2)}) collective-permute-start(bf16[64,2560]{1,0:T(8,128)(2,1)} %get-tuple-element.65), channel_id=1, source_target_pairs={{0,3},{1,0},{2,1},{3,2},{4,7},{5,4},{6,5},{7,6},{8,11},{9,8},{10,9... | collective-permute-start | bytes 983048 | tf_op jit(solution)/shard_map/ppermute | solution.py:523
  47.4 12.2 %copy-start.10 = (bf16[64,2560]{1,0:T(8,128)(2,1)}, bf16[64,2560]{1,0:T(8,128)(2,1)S(1)}, u32[]{:S(2)}) copy-start(bf16[64,2560]{1,0:T(8,128)(2,1)S(1)} %collective-permute-done.3.refs_1_) | copy-start | bytes 983044
  59.5 0.7 copy-start.11
  59.5 0.8 copy-start.12
  59.5 100.0 %all-gather.3.cloned.1.call-start = ((), (), s32[]{:S(2)}) async-start(), calls=%async_computation | async-start | bytes 1310720 | tf_op jit(solution)/shard_map/all_gather | solution.py:519
  62.8 33.8 %copy-start.26 = (s32[2]{0:T(128)S(1)}, s32[2]{0:T(128)}, u32[]{:S(2)}) copy-start(s32[2]{0:T(128)} %param.11) | copy-start | bytes 28
  62.8 35.1 %copy-start.25 = (s32[1024]{0:T(1024)S(1)}, s32[1024]{0:T(1024)}, u32[]{:S(2)}) copy-start(s32[1024]{0:T(1024)} %param.10) | copy-start | bytes 12292
  62.8 36.4 %copy-start = (bf16[256,2560]{1,0:T(8,128)(2,1)S(1)}, bf16[256,2560]{1,0:T(8,128)(2,1)}, u32[]{:S(2)}) copy-start(bf16[256,2560]{1,0:T(8,128)(2,1)} %assemble.1.refs_0_) | copy-start | bytes 3932164
  62.8 29.5 %collective-permute-start.9 = (bf16[256,2560]{1,0:T(8,128)(2,1)}, bf16[256,2560]{1,0:T(8,128)(2,1)S(1)}, u32[]{:S(2)}, u32[]{:S(2)}) collective-permute-start(bf16[256,2560]{1,0:T(8,128)(2,1)} %assemble.1.refs_0_), channel_id=1, source_target_pairs={{0,16},{4,20},{8,24},{12,28},{16,0},{20,4},{24,8},{28,12},{1,17},{... | collective-permute-start | bytes 3932168 | tf_op jit(solution)/shard_map/ppermute | solution.py:115
  64.4 30.0 %collective-permute-start.7 = (bf16[256,2560]{1,0:T(8,128)(2,1)}, bf16[256,2560]{1,0:T(8,128)(2,1)}, u32[]{:S(2)}, u32[]{:S(2)}) collective-permute-start(bf16[256,2560]{1,0:T(8,128)(2,1)} %assemble.1.refs_0_), channel_id=1, source_target_pairs={{0,8},{4,12},{8,0},{12,4},{16,24},{20,28},{24,16},{28,20},{1,9},{5... | collective-permute-start | bytes 3932168 | tf_op jit(solution)/shard_map/ppermute | solution.py:115
  92.3 16.2 %copy-start.1 = (bf16[256,2560]{1,0:T(8,128)(2,1)}, bf16[256,2560]{1,0:T(8,128)(2,1)S(1)}, u32[]{:S(2)}) copy-start(bf16[256,2560]{1,0:T(8,128)(2,1)S(1)} %collective-permute-done.9.refs_4_) | copy-start | bytes 3932164
  92.3 15.3 %collective-permute-start.11 = (bf16[128,2560]{1,0:T(8,128)(2,1)S(1)}, bf16[128,2560]{1,0:T(8,128)(2,1)S(1)}, u32[]{:S(2)}, u32[]{:S(2)}) collective-permute-start(bf16[128,2560]{1,0:T(8,128)(2,1)S(1)} %slice.58), channel_id=1, source_target_pairs={{0,8},{4,12},{8,0},{12,4},{16,24},{20,28},{24,16},{28,20},{1,9},{5... | collective-permute-start | bytes 1966088 | tf_op jit(solution)/shard_map/ppermute | solution.py:115
  95.5 13.6 %collective-permute-start.12 = (bf16[128,2560]{1,0:T(8,128)(2,1)S(1)}, bf16[128,2560]{1,0:T(8,128)(2,1)S(1)}, u32[]{:S(2)}, u32[]{:S(2)}) collective-permute-start(bf16[128,2560]{1,0:T(8,128)(2,1)S(1)} %slice.59), channel_id=1, source_target_pairs={{0,16},{4,20},{8,24},{12,28},{16,0},{20,4},{24,8},{28,12},{1,17},{... | collective-permute-start | bytes 1966088 | tf_op jit(solution)/shard_map/ppermute | solution.py:115
  97.9 12.8 %collective-permute-start.14 = (s32[512]{0:T(512)S(1)}, s32[512]{0:T(512)S(1)}, u32[]{:S(2)}, u32[]{:S(2)}) collective-permute-start(s32[512]{0:T(512)S(1)} %get-tuple-element.110), channel_id=1, source_target_pairs={{0,4},{4,8},{8,12},{12,16},{16,20},{20,24},{24,28},{1,5},{5,9},{9,... | collective-permute-start | bytes 6152 | tf_op jit(solution)/shard_map/ppermute | solution.py:25
  99.2 16.3 %collective-permute-start.6 = (bf16[256,2560]{1,0:T(8,128)(2,1)S(1)}, bf16[256,2560]{1,0:T(8,128)(2,1)}, u32[]{:S(2)}, u32[]{:S(2)}) collective-permute-start(bf16[256,2560]{1,0:T(8,128)(2,1)S(1)} %copy-done), channel_id=1, source_target_pairs={{0,4},{4,0},{8,12},{12,8},{16,20},{20,16},{24,28},{28,24},{1,5},{5... | collective-permute-start | bytes 3932168 | tf_op jit(solution)/shard_map/ppermute | solution.py:115
  100.5 15.0 %collective-permute-start.10 = (bf16[256,2560]{1,0:T(8,128)(2,1)S(1)}, bf16[256,2560]{1,0:T(8,128)(2,1)}, u32[]{:S(2)}, u32[]{:S(2)}) collective-permute-start(bf16[256,2560]{1,0:T(8,128)(2,1)S(1)} %collective-permute-done.9.refs_4_), channel_id=1, source_target_pairs={{0,4},{4,0},{8,12},{12,8},{16,20},{20,16},{24,28},{28,24},{1,5},{5... | collective-permute-start | bytes 3932168 | tf_op jit(solution)/shard_map/ppermute | solution.py:115
  107.6 8.0 %collective-permute-start.8 = (bf16[256,2560]{1,0:T(8,128)(2,1)}, bf16[256,2560]{1,0:T(8,128)(2,1)}, u32[]{:S(2)}, u32[]{:S(2)}) collective-permute-start(bf16[256,2560]{1,0:T(8,128)(2,1)} %collective-permute-done.7.refs_2_), channel_id=1, source_target_pairs={{0,4},{4,0},{8,12},{12,8},{16,20},{20,16},{24,28},{28,24},{1,5},{5... | collective-permute-start | bytes 3932168 | tf_op jit(solution)/shard_map/ppermute | solution.py:115
  110.0 5.6 %collective-permute-start.13 = (bf16[256,2560]{1,0:T(8,128)(2,1)}, bf16[256,2560]{1,0:T(8,128)(2,1)}, u32[]{:S(2)}, u32[]{:S(2)}) collective-permute-start(bf16[256,2560]{1,0:T(8,128)(2,1)} %constant_dynamic-update-slice_fusion.refs_6_), channel_id=1, source_target_pairs={{0,4},{4,0},{8,12},{12,8},{16,20},{20,16},{24,28},{28,24},{1,5},{5... | collective-permute-start | bytes 3932168 | tf_op jit(solution)/shard_map/ppermute | solution.py:115
  114.3 1.3 copy-start.3
  114.3 1.3 copy-start.5
  139.7 35.0 %collective-permute-start.16 = (bf16[2,512,512]{2,1,0:T(8,128)(2,1)}, bf16[2,512,512]{2,1,0:T(8,128)(2,1)S(1)}, u32[]{:S(2)}, u32[]{:S(2)}) collective-permute-start(bf16[2,512,512]{2,1,0:T(8,128)(2,1)} %get-tuple-element.86), channel_id=1, source_target_pairs={{0,4},{4,8},{8,12},{12,16},{16,20},{20,24},{24,28},{1,5},{5,9},{9,... | collective-permute-start | bytes 3145736 | tf_op jit(solution)/shard_map/ppermute | solution.py:25
  143.4 4.1 %copy-start.4 = (f32[1024,64]{1,0:T(8,128)S(1)}, f32[1024,64]{1,0:T(8,128)}, u32[]{:S(2)}) copy-start(f32[1024,64]{1,0:T(8,128)} %copy-done.3) | copy-start | bytes 786436
  143.4 4.1 %copy-start.6 = (f32[1024,64]{1,0:T(8,128)S(1)}, f32[1024,64]{1,0:T(8,128)}, u32[]{:S(2)}) copy-start(f32[1024,64]{1,0:T(8,128)} %copy-done.5) | copy-start | bytes 786436
  147.6 14.3 %collective-permute-start.15 = (bf16[256,512]{1,0:T(8,128)(2,1)}, bf16[256,512]{1,0:T(8,128)(2,1)S(1)}, u32[]{:S(2)}, u32[]{:S(2)}) collective-permute-start(bf16[256,512]{1,0:T(8,128)(2,1)} %attend.4.own_ref), channel_id=1, source_target_pairs={{0,1},{1,0},{2,3},{3,2},{4,5},{5,4},{6,7},{7,6},{8,9},{9,8},{10,11... | collective-permute-start | bytes 786440 | tf_op jit(solution)/shard_map/ppermute | solution.py:115
  161.9 6.5 %copy-start.17 = (bf16[256,512]{1,0:T(8,128)(2,1)}, bf16[256,512]{1,0:T(8,128)(2,1)S(1)}, u32[]{:S(2)}) copy-start(bf16[256,512]{1,0:T(8,128)(2,1)S(1)} %collective-permute-done.15.other_ref) | copy-start | bytes 786436
  172.4 21.1 %collective-permute-start.23 = (bf16[256,512]{1,0:T(8,128)(2,1)}, bf16[256,512]{1,0:T(8,128)(2,1)S(1)}, u32[]{:S(2)}, u32[]{:S(2)}) collective-permute-start(bf16[256,512]{1,0:T(8,128)(2,1)} %attend.7.own_ref), channel_id=1, source_target_pairs={{0,1},{1,0},{2,3},{3,2},{4,5},{5,4},{6,7},{7,6},{8,9},{9,8},{10,11... | collective-permute-start | bytes 786440 | tf_op jit(solution)/shard_map/ppermute | solution.py:115
  174.8 1.0 copy-start.2
  179.8 20.0 %collective-permute-start.20 = (bf16[256,512]{1,0:T(8,128)(2,1)}, bf16[256,512]{1,0:T(8,128)(2,1)S(1)}, u32[]{:S(2)}, u32[]{:S(2)}) collective-permute-start(bf16[256,512]{1,0:T(8,128)(2,1)} %attend.6.own_ref), channel_id=1, source_target_pairs={{0,1},{1,0},{2,3},{3,2},{4,5},{5,4},{6,7},{7,6},{8,9},{9,8},{10,11... | collective-permute-start | bytes 786440 | tf_op jit(solution)/shard_map/ppermute | solution.py:115
  184.1 8.8 %copy-start.27 = (bf16[256,512]{1,0:T(8,128)(2,1)S(1)}, bf16[256,512]{1,0:T(8,128)(2,1)}, u32[]{:S(2)}) copy-start(bf16[256,512]{1,0:T(8,128)(2,1)} %get-tuple-element.100) | copy-start | bytes 786436
  184.1 21.0 %collective-permute-start.26 = (bf16[256,512]{1,0:T(8,128)(2,1)}, bf16[256,512]{1,0:T(8,128)(2,1)S(1)}, u32[]{:S(2)}, u32[]{:S(2)}) collective-permute-start(bf16[256,512]{1,0:T(8,128)(2,1)} %get-tuple-element.99), channel_id=1, source_target_pairs={{1,3},{2,0},{5,7},{6,4},{9,11},{10,8},{13,15},{14,12},{17,19},{18,... | collective-permute-start | bytes 786440 | tf_op jit(solution)/shard_map/ppermute | solution.py:584
  189.5 16.8 %collective-permute-start.17 = (bf16[256,512]{1,0:T(8,128)(2,1)}, bf16[256,512]{1,0:T(8,128)(2,1)S(1)}, u32[]{:S(2)}, u32[]{:S(2)}) collective-permute-start(bf16[256,512]{1,0:T(8,128)(2,1)} %attend.5.own_ref), channel_id=1, source_target_pairs={{0,1},{1,0},{2,3},{3,2},{4,5},{5,4},{6,7},{7,6},{8,9},{9,8},{10,11... | collective-permute-start | bytes 786440 | tf_op jit(solution)/shard_map/ppermute | solution.py:115
  192.9 18.5 %collective-permute-start.27 = (bf16[256,512]{1,0:T(8,128)(2,1)S(1)}, bf16[256,512]{1,0:T(8,128)(2,1)S(1)}, u32[]{:S(2)}, u32[]{:S(2)}) collective-permute-start(bf16[256,512]{1,0:T(8,128)(2,1)S(1)} %copy-done.27), channel_id=1, source_target_pairs={{1,2},{2,1},{5,6},{6,5},{9,10},{10,9},{13,14},{14,13},{17,18},{18,... | collective-permute-start | bytes 786440 | tf_op jit(solution)/shard_map/ppermute | solution.py:585
  193.6 0.7 copy-start.18
  198.5 14.1 %collective-permute-start.24 = (bf16[256,512]{1,0:T(8,128)(2,1)}, bf16[256,512]{1,0:T(8,128)(2,1)S(1)}, u32[]{:S(2)}, u32[]{:S(2)}) collective-permute-start(bf16[256,512]{1,0:T(8,128)(2,1)} %get-tuple-element.94), channel_id=1, source_target_pairs={{1,3},{2,0},{5,7},{6,4},{9,11},{10,8},{13,15},{14,12},{17,19},{18,... | collective-permute-start | bytes 786440 | tf_op jit(solution)/shard_map/ppermute | solution.py:584
  199.8 0.7 copy-start.16
  199.9 17.0 %collective-permute-start.25 = (bf16[256,512]{1,0:T(8,128)(2,1)}, bf16[256,512]{1,0:T(8,128)(2,1)S(1)}, u32[]{:S(2)}, u32[]{:S(2)}) collective-permute-start(bf16[256,512]{1,0:T(8,128)(2,1)} %get-tuple-element.95), channel_id=1, source_target_pairs={{1,2},{2,1},{5,6},{6,5},{9,10},{10,9},{13,14},{14,13},{17,18},{18,... | collective-permute-start | bytes 786440 | tf_op jit(solution)/shard_map/ppermute | solution.py:585
  205.0 6.3 %copy-start.13 = (bf16[256,512]{1,0:T(8,128)(2,1)}, bf16[256,512]{1,0:T(8,128)(2,1)S(1)}, u32[]{:S(2)}) copy-start(bf16[256,512]{1,0:T(8,128)(2,1)S(1)} %collective-permute-done.26.inner_ref) | copy-start | bytes 786436
  205.1 16.9 %collective-permute-start.21 = (bf16[256,512]{1,0:T(8,128)(2,1)}, bf16[256,512]{1,0:T(8,128)(2,1)S(1)}, u32[]{:S(2)}, u32[]{:S(2)}) collective-permute-start(bf16[256,512]{1,0:T(8,128)(2,1)} %get-tuple-element.91), channel_id=1, source_target_pairs={{1,3},{2,0},{5,7},{6,4},{9,11},{10,8},{13,15},{14,12},{17,19},{18,... | collective-permute-start | bytes 786440 | tf_op jit(solution)/shard_map/ppermute | solution.py:584
  206.4 0.7 copy-start.15
  206.4 15.6 %collective-permute-start.22 = (bf16[256,512]{1,0:T(8,128)(2,1)}, bf16[256,512]{1,0:T(8,128)(2,1)S(1)}, u32[]{:S(2)}, u32[]{:S(2)}) collective-permute-start(bf16[256,512]{1,0:T(8,128)(2,1)} %get-tuple-element.92), channel_id=1, source_target_pairs={{1,2},{2,1},{5,6},{6,5},{9,10},{10,9},{13,14},{14,13},{17,18},{18,... | collective-permute-start | bytes 786440 | tf_op jit(solution)/shard_map/ppermute | solution.py:585
  211.4 2.0 copy-start.14
  211.4 21.8 %collective-permute-start.18 = (bf16[256,512]{1,0:T(8,128)(2,1)}, bf16[256,512]{1,0:T(8,128)(2,1)S(1)}, u32[]{:S(2)}, u32[]{:S(2)}) collective-permute-start(bf16[256,512]{1,0:T(8,128)(2,1)} %get-tuple-element.88), channel_id=1, source_target_pairs={{1,3},{2,0},{5,7},{6,4},{9,11},{10,8},{13,15},{14,12},{17,19},{18,... | collective-permute-start | bytes 786440 | tf_op jit(solution)/shard_map/ppermute | solution.py:584
  212.7 4.1 %copy-start.19 = (bf16[256,512]{1,0:T(8,128)(2,1)}, bf16[256,512]{1,0:T(8,128)(2,1)S(1)}, u32[]{:S(2)}) copy-start(bf16[256,512]{1,0:T(8,128)(2,1)S(1)} %collective-permute-done.24.inner_ref) | copy-start | bytes 786436
  212.7 20.5 %collective-permute-start.19 = (bf16[256,512]{1,0:T(8,128)(2,1)}, bf16[256,512]{1,0:T(8,128)(2,1)S(1)}, u32[]{:S(2)}, u32[]{:S(2)}) collective-permute-start(bf16[256,512]{1,0:T(8,128)(2,1)} %get-tuple-element.89), channel_id=1, source_target_pairs={{1,2},{2,1},{5,6},{6,5},{9,10},{10,9},{13,14},{14,13},{17,18},{18,... | collective-permute-start | bytes 786440 | tf_op jit(solution)/shard_map/ppermute | solution.py:585
  216.8 0.7 copy-start.20
  222.0 0.7 copy-start.21
  222.0 0.8 copy-start.22
  233.2 0.7 copy-start.23
  233.2 0.8 copy-start.24
Sparse Core Ops, SparseCore 0:
  59.6 69.4 all-gather.4
  130.7 28.7 all-gather.2

commit v16 on v12

--- a/solution.py
+++ b/solution.py
@@ -37,7 +37,7 @@
     return pl.CostEstimate(flops=flops, bytes_accessed=nbytes, transcendentals=transcendentals)
 
 
-def params(limit=60):
+def params(limit=28):
     return pltpu.CompilerParams(vmem_limit_bytes=limit << 20)
 
 

time: 247 us -> 238 us (0.964)
  Pallas kernels: 87 us -> 58.6 us
  local copies, waits for them, and re-layouts: 10.3 us -> 21.1 us
  waiting for transfers between devices: 89.5 us -> 99 us
    unnamed x57, local copies, waits for them, and re-layouts: 5.74 us -> 17.1 us
    pallas_call x4, Pallas kernels: 16.2 us -> 8.2 us  [attend(): pl.pallas_call(attend_kernel, grid=(1,), in_specs=[pl.BlockSpec(block, la...]
    ppermute x12, waiting for transfers between devices: 36.9 us -> 43.5 us  [swapped(): lax.ppermute(value, axis, [(source, source ^ mask) for source in range(co...]
    pallas_call x4, Pallas kernels: 18.7 us -> 13.3 us  [project(): pl.pallas_call(project_kernel, grid=(1,), in_specs=[pl.BlockSpec(memory_s...]
    pallas_call x2, Pallas kernels: 17.1 us -> 14 us  [qkv_columns(): pl.pallas_call(qkv_kernel, grid=(3,), in_specs=[pl.BlockSpec(memory_space...]
    pallas_call x4, Pallas kernels: 13.6 us -> 10.9 us  [final(): pl.pallas_call(final_kernel, grid=(tokens // STEP,), in_specs=specs, out_...]
  transfers between devices with their start and end apart: 30 -> 30, of which waited for: 11 -> 13; matrix products, arithmetic and copies ran while one was open for 4% -> 4% of each run, Pallas kernels for 32% -> 22%
where the time goes in v16:
time: 238 us; the launch traced here: 236 us
  waiting for transfers between devices  99 us (42%)
  Pallas kernels  58.6 us (25%)
  starting transfers between devices  36.3 us (15%)
  local copies, waits for them, and re-layouts  21.1 us (9%)
  between operations  15.1 us (6%)
  other arithmetic  5.39 us (2%)
    ppermute x12, waiting for transfers between devices, swapped(): lax.ppermute(value, axis, [(source, source ^ mask) for source in range(co...  43.5 us
    all_gather x2, waiting for transfers between devices, gathered(): rows = lax.all_gather(normed, 'mp', axis=0, tiled=True)  25.7 us
    unnamed x57, local copies, waits for them, and re-layouts  17.1 us
    pallas_call x2, Pallas kernels, qkv_columns(): pl.pallas_call(qkv_kernel, grid=(3,), in_specs=[pl.BlockSpec(memory_space...  14 us
    pallas_call x4, Pallas kernels, project(): pl.pallas_call(project_kernel, grid=(1,), in_specs=[pl.BlockSpec(memory_s...  13.3 us
    ppermute x12, starting transfers between devices, swapped(): lax.ppermute(value, axis, [(source, source ^ mask) for source in range(co...  13 us
    ppermute x3, waiting for transfers between devices, body(): lax.ppermute(parts[step], 'mp', [(at, (at + step) % group_size) for at in...  11.4 us
    pallas_call x4, Pallas kernels, final(): pl.pallas_call(final_kernel, grid=(tokens // STEP,), in_specs=specs, out_...  10.9 us
  transfers between devices with their start and end apart: 30, of which 13 were waited for; matrix products, arithmetic and copies ran while one was open for 4% of the time, Pallas kernels for 22%

profile of v16, /device:TPU:0, one launch (start us, length us, event | category | flops | bytes accessed | tf_op | source)
XLA Modules:
  0.0 235.5 jit_solution(15423708413472306953)
XLA Ops:
  7.5 2.2 copy-done
  9.7 4.3 %stats.1.own_ref = f32[8,5248]{1,0:T(8,128)S(1)} custom-call(bf16[1024,4,512]{2,1,0:T(4,128)(2,1)S(1)} %copy-done, f32[8,512]{1,0:T(8,128)S(1)} %maximum_maximum_fusion.proj_ref), custom_call_target="tpu_custom_call" | custom-call | flops 1258291200 | bytes 4194304 | tf_op jit(solution)/shard_map/stats/pallas_call | solution.py:178
  14.0 5.1 %collective-permute-start.2 = (f32[8,5248]{1,0:T(8,128)S(1)}, f32[8,5248]{1,0:T(8,128)S(1)}, u32[]{:S(2)}, u32[]{:S(2)}) collective-permute-start(f32[8,5248]{1,0:T(8,128)S(1)} %stats.1.own_ref), channel_id=1, source_target_pairs={{0,3},{1,0},{2,1},{3,2},{4,7},{5,4},{6,5},{7,6},{8,11},{9,8},{10,9... | collective-permute-start | bytes 503816 | tf_op jit(solution)/shard_map/ppermute | solution.py:31
  19.1 1.0 collective-permute-start
  20.1 2.6 %regroup.1 = (bf16[64,2560]{1,0:T(8,128)(2,1)S(1)}, bf16[64,2560]{1,0:T(8,128)(2,1)S(1)}, bf16[64,2560]{1,0:T(8,128)(2,1)S(1)}, bf16[64,2560]{1,0:T(8,128)(2,1)S(1)}) custom-call(s32[1]{0:T(128)} %bitcast.1.place_ref, f32[64,4,2048]{2,1,0:T(4,128)S(1)} %copy-done.15), custom_call_target="tpu_custom_call" | custom-call | bytes 3407872 | tf_op jit(solution)/shard_map/regroup/pallas_call | solution.py:79
  22.7 1.1 collective-permute-done.2.c_ref
  23.8 9.5 %collective-permute-done.1.b_ref = f32[8,5248]{1,0:T(8,128)S(1)} collective-permute-done((f32[8,5248]{1,0:T(8,128)S(1)}, f32[8,5248]{1,0:T(8,128)S(1)}, u32[]{:S(2)}, u32[]{:S(2)}) %collective-permute-start.1) | collective-permute-done | bytes 167968 | tf_op jit(solution)/shard_map/ppermute | solution.py:31
  33.3 0.9 collective-permute-start.3
  34.2 1.9 collective-permute-start.4
  36.1 2.9 %collective-permute-start.5 = (bf16[64,2560]{1,0:T(8,128)(2,1)S(1)}, bf16[64,2560]{1,0:T(8,128)(2,1)S(1)}, u32[]{:S(2)}, u32[]{:S(2)}) collective-permute-start(bf16[64,2560]{1,0:T(8,128)(2,1)S(1)} %get-tuple-element.65), channel_id=1, source_target_pairs={{0,3},{1,0},{2,1},{3,2},{4,7},{5,4},{6,5},{7,6},{8,11},{9,8},{10,9... | collective-permute-start | bytes 983048 | tf_op jit(solution)/shard_map/ppermute | solution.py:519
  39.0 2.2 copy-done.1
  41.2 2.0 mix.3
  43.2 3.3 %mix.2 = (f32[8,5248]{1,0:T(8,128)S(1)}, bf16[768,512]{1,0:T(8,128)(2,1)}) custom-call(f32[4,6]{1,0:T(4,128)S(1)} %copy-done.18, bf16[1024,4,512]{2,1,0:T(4,128)(2,1)S(1)} %copy-done.1, f32[8,5248]{1,0:T(8,128)S(1)} %stats.1.own_ref, f32[8,5248]{1,0:T(8,128)S(1)} %collective-permute-done.a_ref, f32[8,5248]{1,0:T(8,128)S(1)} %collective-permute-done.1.b_ref, ...), custom_call_target="tpu_custom_call" | custom-call | flops 629145600 | bytes 3932160 | tf_op jit(solution)/shard_map/mix/pallas_call | solution.py:249
  47.2 11.4 %collective-permute-done.4.refs_2_ = bf16[64,2560]{1,0:T(8,128)(2,1)S(1)} collective-permute-done((bf16[64,2560]{1,0:T(8,128)(2,1)S(1)}, bf16[64,2560]{1,0:T(8,128)(2,1)S(1)}, u32[]{:S(2)}, u32[]{:S(2)}) %collective-permute-start.4) | collective-permute-done | bytes 327712 | tf_op jit(solution)/shard_map/ppermute | solution.py:519
  58.8 1.6 collective-permute-start.9
  60.4 1.5 collective-permute-start.7
  61.9 26.1 %collective-permute-done.9.refs_4_ = bf16[256,2560]{1,0:T(8,128)(2,1)S(1)} collective-permute-done((bf16[256,2560]{1,0:T(8,128)(2,1)S(1)}, bf16[256,2560]{1,0:T(8,128)(2,1)S(1)}, u32[]{:S(2)}, u32[]{:S(2)}) %collective-permute-start.9) | collective-permute-done | bytes 1310752 | tf_op jit(solution)/shard_map/ppermute | solution.py:115
  88.0 1.6 collective-permute-start.11
  90.2 1.1 slice.59
  91.3 1.0 collective-permute-start.12
  93.5 1.3 collective-permute-start.14
  94.8 1.4 collective-permute-start.6
  96.3 7.0 %collective-permute-done.11 = bf16[128,2560]{1,0:T(8,128)(2,1)S(1)} collective-permute-done((bf16[128,2560]{1,0:T(8,128)(2,1)S(1)}, bf16[128,2560]{1,0:T(8,128)(2,1)S(1)}, u32[]{:S(2)}, u32[]{:S(2)}) %collective-permute-start.11) | collective-permute-done | bytes 655392 | tf_op jit(solution)/shard_map/ppermute | solution.py:115
  103.3 0.9 constant_dynamic-update-slice_fusion.1
  104.8 1.0 constant_dynamic-update-slice_fusion.refs_6_
  106.4 1.6 convert_reduce_fusion
  108.1 1.9 multiply_sine_fusion
  111.1 17.1 %all-gather.5.cloned.1.call-done = bf16[3072,512]{1,0:T(8,128)(2,1)} async-done(((bf16[768,512]{1,0:T(8,128)(2,1)}), bf16[3072,512]{1,0:T(8,128)(2,1)}) %all-gather.5.cloned.1.call-update) | async-done | bytes 3145744 | tf_op jit(solution)/shard_map/all_gather | solution.py:515
  128.3 1.3 copy-done.4
  129.6 1.3 copy-done.8
  130.9 1.9 copy-done.19
  132.8 8.7 %qkv.2 = (bf16[3,768,512]{2,1,0:T(8,128)(2,1)S(1)}, bf16[2,512,512]{2,1,0:T(8,128)(2,1)}) custom-call(s32[1]{0:T(128)} %bitcast.2.ring_ref, bf16[4,768,512]{2,1,0:T(8,128)(2,1)S(1)} %bitcast.11, f32[768,128]{1,0:T(8,128)S(1)} %get-tuple-element.116.cosine_ref, f32[768,128]{1,0:T(8,128)S(1)} %get-tuple-element.115.sine_ref, bf16[256,2560]{1,0:T(8,128)(2,1)S(1)} %copy-done.4, ...), custom_call_target="tpu_custom_call" | custom-call | flops 4831838208 | bytes 14155776 | tf_op jit(solution)/shard_map/qkv/pallas_call | solution.py:305
  141.5 1.9 collective-permute-start.16
  143.4 1.0 copy.14.qseg_ref
  144.6 1.0 copy-done.13
  145.6 2.6 %attend.4.own_ref = bf16[256,512]{1,0:T(8,128)(2,1)} custom-call(bf16[3,768,512]{2,1,0:T(8,128)(2,1)S(1)} %get-tuple-element.83.q_ref.k0.k1.k2.v0.v1.v2, bf16[3,768,512]{2,1,0:T(8,128)(2,1)S(1)} %get-tuple-element.83.q_ref.k0.k1.k2.v0.v1.v2, bf16[3,768,512]{2,1,0:T(8,128)(2,1)S(1)} %get-tuple-element.83.q_ref.k0.k1.k2.v0.v1.v2, ...), custom_call_target="tpu_custom_call" | custom-call | flops 402653184 | bytes 2097152 | tf_op jit(solution)/shard_map/attend/pallas_call | solution.py:359
  149.0 8.6 %all-gather.3.cloned.1.call-done = bf16[1024,512]{1,0:T(8,128)(2,1)} async-done(((bf16[256,512]{1,0:T(8,128)(2,1)}), bf16[1024,512]{1,0:T(8,128)(2,1)}) %all-gather.3.cloned.1.call-update) | async-done | bytes 1048592 | tf_op jit(solution)/shard_map/all_gather | solution.py:515
  157.6 3.5 %collective-permute-done.15.other_ref = bf16[256,512]{1,0:T(8,128)(2,1)} collective-permute-done((bf16[256,512]{1,0:T(8,128)(2,1)}, bf16[256,512]{1,0:T(8,128)(2,1)}, u32[]{:S(2)}, u32[]{:S(2)}) %collective-permute-start.15) | collective-permute-done | bytes 262176 | tf_op jit(solution)/shard_map/ppermute | solution.py:115
  161.1 1.3 copy-done.5
  162.4 1.3 copy-done.9
  163.8 1.2 copy-done.16
  165.0 0.9 copy-done.17
  165.9 5.3 %qkv.3 = (bf16[3,256,512]{2,1,0:T(8,128)(2,1)S(1)}, bf16[2,256,512]{2,1,0:T(8,128)(2,1)}) custom-call(s32[1]{0:T(128)} %bitcast.2.ring_ref, bf16[4,256,512]{2,1,0:T(8,128)(2,1)S(1)} %bitcast.10, f32[256,128]{1,0:T(8,128)S(1)} %copy-done.17, f32[256,128]{1,0:T(8,128)S(1)} %get-tuple-element.117.sine_ref, bf16[256,2560]{1,0:T(8,128)(2,1)S(1)} %copy-done.5, ...), custom_call_target="tpu_custom_call" | custom-call | flops 1610612736 | bytes 8912896 | tf_op jit(solution)/shard_map/qkv/pallas_call | solution.py:305
  171.2 1.9 attend.7.own_ref
  173.1 1.0 collective-permute-start.23
  174.1 1.9 attend.6.own_ref
  176.0 1.1 collective-permute-start.20
  177.1 3.4 %project.7 = (f32[256,512]{1,0:T(8,128)S(1)}, bf16[256,512]{1,0:T(8,128)(2,1)S(1)}, bf16[256,512]{1,0:T(8,128)(2,1)S(1)}) custom-call(s32[1]{0:T(128)} %bitcast.1.place_ref, s32[1]{0:T(128)} %bitcast.2.ring_ref, bf16[256,512]{1,0:T(8,128)(2,1)} %attend.4.own_ref, bf16[256,512]{1,0:T(8,128)(2,1)} %collective-permute-done.15.other_ref, ...), custom_call_target="tpu_custom_call" | custom-call | flops 1073741824 | bytes 5767168 | tf_op jit(solution)/shard_map/project/pallas_call | solution.py:409
  180.5 1.3 collective-permute-start.26
  181.8 1.9 attend.5.own_ref
  183.7 3.8 %collective-permute-start.17 = (bf16[256,512]{1,0:T(8,128)(2,1)S(1)}, bf16[256,512]{1,0:T(8,128)(2,1)S(1)}, u32[]{:S(2)}, u32[]{:S(2)}) collective-permute-start(bf16[256,512]{1,0:T(8,128)(2,1)S(1)} %attend.5.own_ref), channel_id=1, source_target_pairs={{0,1},{1,0},{2,3},{3,2},{4,5},{5,4},{6,7},{7,6},{8,9},{9,8},{10,11... | collective-permute-start | bytes 786440 | tf_op jit(solution)/shard_map/ppermute | solution.py:115
  188.2 3.3 %project.6 = (f32[256,512]{1,0:T(8,128)S(1)}, bf16[256,512]{1,0:T(8,128)(2,1)S(1)}, bf16[256,512]{1,0:T(8,128)(2,1)S(1)}) custom-call(s32[1]{0:T(128)} %bitcast.1.place_ref, s32[1]{0:T(128)} %bitcast.2.ring_ref, bf16[256,512]{1,0:T(8,128)(2,1)S(1)} %attend.7.own_ref, bf16[256,512]{1,0:T(8,128)(2,1)S(1)} %collective-permute-done.23.other_ref, ...), custom_call_target="tpu_custom_call" | custom-call | flops 1073741824 | bytes 5767168 | tf_op jit(solution)/shard_map/project/pallas_call | solution.py:409
  191.4 1.3 collective-permute-start.24
  193.5 0.9 collective-permute-start.25
  194.4 3.3 %project.5 = (f32[256,512]{1,0:T(8,128)S(1)}, bf16[256,512]{1,0:T(8,128)(2,1)S(1)}, bf16[256,512]{1,0:T(8,128)(2,1)S(1)}) custom-call(s32[1]{0:T(128)} %bitcast.1.place_ref, s32[1]{0:T(128)} %bitcast.2.ring_ref, bf16[256,512]{1,0:T(8,128)(2,1)S(1)} %attend.6.own_ref, bf16[256,512]{1,0:T(8,128)(2,1)S(1)} %collective-permute-done.20.other_ref, ...), custom_call_target="tpu_custom_call" | custom-call | flops 1073741824 | bytes 5767168 | tf_op jit(solution)/shard_map/project/pallas_call | solution.py:409
  197.7 1.3 collective-permute-start.21
  199.0 4.9 %collective-permute-done.17.other_ref = bf16[256,512]{1,0:T(8,128)(2,1)S(1)} collective-permute-done((bf16[256,512]{1,0:T(8,128)(2,1)S(1)}, bf16[256,512]{1,0:T(8,128)(2,1)S(1)}, u32[]{:S(2)}, u32[]{:S(2)}) %collective-permute-start.17) | collective-permute-done | bytes 262176 | tf_op jit(solution)/shard_map/ppermute | solution.py:115
  204.7 3.4 %project.4 = (f32[256,512]{1,0:T(8,128)S(1)}, bf16[256,512]{1,0:T(8,128)(2,1)S(1)}, bf16[256,512]{1,0:T(8,128)(2,1)S(1)}) custom-call(s32[1]{0:T(128)} %bitcast.1.place_ref, s32[1]{0:T(128)} %bitcast.2.ring_ref, bf16[256,512]{1,0:T(8,128)(2,1)S(1)} %attend.5.own_ref, bf16[256,512]{1,0:T(8,128)(2,1)S(1)} %collective-permute-done.17.other_ref, ...), custom_call_target="tpu_custom_call" | custom-call | flops 1073741824 | bytes 5767168 | tf_op jit(solution)/shard_map/project/pallas_call | solution.py:409
  208.2 1.3 collective-permute-start.18
  210.2 2.7 %final.4.rest_0_ = bf16[1024,4,512]{2,1,0:T(4,128)(2,1)} custom-call(f32[4,6]{1,0:T(4,128)S(1)} %copy-done.18, bf16[1024,4,512]{2,1,0:T(4,128)(2,1)S(1)} %copy-done.2, f32[8,5248]{1,0:T(8,128)S(1)} %copy-done.12, f32[8,5248]{1,0:T(8,128)S(1)} %copy-done.12, f32[8,5248]{1,0:T(8,128)S(1)} %copy-done.12, f32[256,512]{1,0:T(8,128)S(1)} %get-tuple-element.98.own_ref, ...), custom_call_target="tpu_custom_call" | custom-call | flops 629145600 | bytes 2883584 | tf_op jit(solution)/shard_map/final/pallas_call | solution.py:488
  212.9 2.7 %final.5.rest_0_ = bf16[1024,4,512]{2,1,0:T(4,128)(2,1)} custom-call(f32[4,6]{1,0:T(4,128)S(1)} %copy-done.18, bf16[1024,4,512]{2,1,0:T(4,128)(2,1)S(1)} %copy-done.2, f32[8,5248]{1,0:T(8,128)S(1)} %copy-done.12, f32[8,5248]{1,0:T(8,128)S(1)} %copy-done.12, f32[8,5248]{1,0:T(8,128)S(1)} %copy-done.12, ...), custom_call_target="tpu_custom_call", output_to_operand_aliasing={{}: (8, {})} | custom-call | flops 629145600 | bytes 2883584 | tf_op jit(solution)/shard_map/final/pallas_call | solution.py:488
  215.6 2.7 %final.6.rest_0_ = bf16[1024,4,512]{2,1,0:T(4,128)(2,1)} custom-call(f32[4,6]{1,0:T(4,128)S(1)} %copy-done.18, bf16[1024,4,512]{2,1,0:T(4,128)(2,1)S(1)} %copy-done.2, f32[8,5248]{1,0:T(8,128)S(1)} %copy-done.12, f32[8,5248]{1,0:T(8,128)S(1)} %copy-done.12, f32[8,5248]{1,0:T(8,128)S(1)} %copy-done.12, ...), custom_call_target="tpu_custom_call", output_to_operand_aliasing={{}: (8, {})} | custom-call | flops 629145600 | bytes 2883584 | tf_op jit(solution)/shard_map/final/pallas_call | solution.py:488
  218.3 7.6 %collective-permute-done.18.inner_ref = bf16[256,512]{1,0:T(8,128)(2,1)S(1)} collective-permute-done((bf16[256,512]{1,0:T(8,128)(2,1)S(1)}, bf16[256,512]{1,0:T(8,128)(2,1)S(1)}, u32[]{:S(2)}, u32[]{:S(2)}) %collective-permute-start.18) | collective-permute-done | bytes 262176 | tf_op jit(solution)/shard_map/ppermute | solution.py:580
  226.0 2.7 %final.7 = bf16[1024,4,512]{2,1,0:T(4,128)(2,1)} custom-call(f32[4,6]{1,0:T(4,128)S(1)} %copy-done.18, bf16[1024,4,512]{2,1,0:T(4,128)(2,1)S(1)} %copy-done.2, f32[8,5248]{1,0:T(8,128)S(1)} %copy-done.12, f32[8,5248]{1,0:T(8,128)S(1)} %copy-done.12, f32[8,5248]{1,0:T(8,128)S(1)} %copy-done.12, ...), custom_call_target="tpu_custom_call", output_to_operand_aliasing={{}: (8, {})} | custom-call | flops 629145600 | bytes 2883584 | tf_op jit(solution)/shard_map/final/pallas_call | solution.py:488
  (102 shorter events, 8.7 us)
Async XLA Ops:
  6.5 121.7 %all-gather.5.cloned.1.call-start = ((), (), s32[]{:S(2)}) async-start(), calls=%async_computation.1 | async-start | bytes 3932160 | tf_op jit(solution)/shard_map/all_gather | solution.py:515
  7.5 2.2 copy-start
  9.7 10.4 %copy-start.15 = (f32[64,4,2048]{2,1,0:T(4,128)S(1)}, f32[64,4,2048]{2,1,0:T(4,128)}, u32[]{:S(2)}) copy-start(f32[64,4,2048]{2,1,0:T(4,128)} %master_ref.1) | copy-start | bytes 6291460
  14.0 25.1 %copy-start.18 = (f32[4,6]{1,0:T(4,128)S(1)}, f32[4,6]{1,0:T(4,128)}, u32[]{:S(2)}) copy-start(f32[4,6]{1,0:T(4,128)} %static_ref.11) | copy-start | bytes 292
  14.0 9.8 %collective-permute-start.2 = (f32[8,5248]{1,0:T(8,128)S(1)}, f32[8,5248]{1,0:T(8,128)S(1)}, u32[]{:S(2)}, u32[]{:S(2)}) collective-permute-start(f32[8,5248]{1,0:T(8,128)S(1)} %stats.1.own_ref), channel_id=1, source_target_pairs={{0,3},{1,0},{2,1},{3,2},{4,7},{5,4},{6,5},{7,6},{8,11},{9,8},{10,9... | collective-permute-start | bytes 503816 | tf_op jit(solution)/shard_map/ppermute | solution.py:31
  19.1 14.2 %collective-permute-start.1 = (f32[8,5248]{1,0:T(8,128)S(1)}, f32[8,5248]{1,0:T(8,128)S(1)}, u32[]{:S(2)}, u32[]{:S(2)}) collective-permute-start(f32[8,5248]{1,0:T(8,128)S(1)} %stats.1.own_ref), channel_id=1, source_target_pairs={{0,2},{1,3},{2,0},{3,1},{4,6},{5,7},{6,4},{7,5},{8,10},{9,11},{10,... | collective-permute-start | bytes 503816 | tf_op jit(solution)/shard_map/ppermute | solution.py:31
  19.1 14.2 %collective-permute-start = (f32[8,5248]{1,0:T(8,128)S(1)}, f32[8,5248]{1,0:T(8,128)S(1)}, u32[]{:S(2)}, u32[]{:S(2)}) collective-permute-start(f32[8,5248]{1,0:T(8,128)S(1)} %stats.1.own_ref), channel_id=1, source_target_pairs={{0,1},{1,2},{2,3},{3,0},{4,5},{5,6},{6,7},{7,4},{8,9},{9,10},{10,1... | collective-permute-start | bytes 503816 | tf_op jit(solution)/shard_map/ppermute | solution.py:31
  33.3 13.9 %collective-permute-start.3 = (bf16[64,2560]{1,0:T(8,128)(2,1)S(1)}, bf16[64,2560]{1,0:T(8,128)(2,1)S(1)}, u32[]{:S(2)}, u32[]{:S(2)}) collective-permute-start(bf16[64,2560]{1,0:T(8,128)(2,1)S(1)} %get-tuple-element.63), channel_id=1, source_target_pairs={{0,1},{1,2},{2,3},{3,0},{4,5},{5,6},{6,7},{7,4},{8,9},{9,10},{10,1... | collective-permute-start | bytes 983048 | tf_op jit(solution)/shard_map/ppermute | solution.py:519
  34.2 24.4 %collective-permute-start.4 = (bf16[64,2560]{1,0:T(8,128)(2,1)S(1)}, bf16[64,2560]{1,0:T(8,128)(2,1)S(1)}, u32[]{:S(2)}, u32[]{:S(2)}) collective-permute-start(bf16[64,2560]{1,0:T(8,128)(2,1)S(1)} %get-tuple-element.64), channel_id=1, source_target_pairs={{0,2},{1,3},{2,0},{3,1},{4,6},{5,7},{6,4},{7,5},{8,10},{9,11},{10,... | collective-permute-start | bytes 983048 | tf_op jit(solution)/shard_map/ppermute | solution.py:519
  36.1 22.5 %collective-permute-start.5 = (bf16[64,2560]{1,0:T(8,128)(2,1)S(1)}, bf16[64,2560]{1,0:T(8,128)(2,1)S(1)}, u32[]{:S(2)}, u32[]{:S(2)}) collective-permute-start(bf16[64,2560]{1,0:T(8,128)(2,1)S(1)} %get-tuple-element.65), channel_id=1, source_target_pairs={{0,3},{1,0},{2,1},{3,2},{4,7},{5,4},{6,5},{7,6},{8,11},{9,8},{10,9... | collective-permute-start | bytes 983048 | tf_op jit(solution)/shard_map/ppermute | solution.py:519
  39.0 2.2 copy-start.1
  46.5 0.7 copy-start.11
  58.6 99.0 %all-gather.3.cloned.1.call-start = ((), (), s32[]{:S(2)}) async-start(), calls=%async_computation | async-start | bytes 1310720 | tf_op jit(solution)/shard_map/all_gather | solution.py:515
  58.8 45.4 %copy-start.3 = (bf16[256,2560]{1,0:T(8,128)(2,1)}, bf16[256,2560]{1,0:T(8,128)(2,1)S(1)}, u32[]{:S(2)}) copy-start(bf16[256,2560]{1,0:T(8,128)(2,1)S(1)} %assemble.1.refs_0_) | copy-start | bytes 3932164
  58.8 33.5 %copy-start.27 = (s32[2]{0:T(128)S(1)}, s32[2]{0:T(128)}, u32[]{:S(2)}) copy-start(s32[2]{0:T(128)} %param.11) | copy-start | bytes 28
  58.8 34.7 %copy-start.26 = (s32[1024]{0:T(1024)S(1)}, s32[1024]{0:T(1024)}, u32[]{:S(2)}) copy-start(s32[1024]{0:T(1024)} %param.10) | copy-start | bytes 12292
  58.8 29.2 %collective-permute-start.9 = (bf16[256,2560]{1,0:T(8,128)(2,1)S(1)}, bf16[256,2560]{1,0:T(8,128)(2,1)S(1)}, u32[]{:S(2)}, u32[]{:S(2)}) collective-permute-start(bf16[256,2560]{1,0:T(8,128)(2,1)S(1)} %assemble.1.refs_0_), channel_id=1, source_target_pairs={{0,16},{4,20},{8,24},{12,28},{16,0},{20,4},{24,8},{28,12},{1,17},{... | collective-permute-start | bytes 3932168 | tf_op jit(solution)/shard_map/ppermute | solution.py:115
  60.4 29.8 %collective-permute-start.7 = (bf16[256,2560]{1,0:T(8,128)(2,1)S(1)}, bf16[256,2560]{1,0:T(8,128)(2,1)}, u32[]{:S(2)}, u32[]{:S(2)}) collective-permute-start(bf16[256,2560]{1,0:T(8,128)(2,1)S(1)} %assemble.1.refs_0_), channel_id=1, source_target_pairs={{0,8},{4,12},{8,0},{12,4},{16,24},{20,28},{24,16},{28,20},{1,9},{5... | collective-permute-start | bytes 3932168 | tf_op jit(solution)/shard_map/ppermute | solution.py:115
  88.0 16.2 %copy-start.7 = (bf16[256,2560]{1,0:T(8,128)(2,1)}, bf16[256,2560]{1,0:T(8,128)(2,1)S(1)}, u32[]{:S(2)}) copy-start(bf16[256,2560]{1,0:T(8,128)(2,1)S(1)} %collective-permute-done.9.refs_4_) | copy-start | bytes 3932164
  88.0 15.3 %collective-permute-start.11 = (bf16[128,2560]{1,0:T(8,128)(2,1)S(1)}, bf16[128,2560]{1,0:T(8,128)(2,1)S(1)}, u32[]{:S(2)}, u32[]{:S(2)}) collective-permute-start(bf16[128,2560]{1,0:T(8,128)(2,1)S(1)} %slice.58), channel_id=1, source_target_pairs={{0,8},{4,12},{8,0},{12,4},{16,24},{20,28},{24,16},{28,20},{1,9},{5... | collective-permute-start | bytes 1966088 | tf_op jit(solution)/shard_map/ppermute | solution.py:115
  91.3 13.5 %collective-permute-start.12 = (bf16[128,2560]{1,0:T(8,128)(2,1)S(1)}, bf16[128,2560]{1,0:T(8,128)(2,1)S(1)}, u32[]{:S(2)}, u32[]{:S(2)}) collective-permute-start(bf16[128,2560]{1,0:T(8,128)(2,1)S(1)} %slice.59), channel_id=1, source_target_pairs={{0,16},{4,20},{8,24},{12,28},{16,0},{20,4},{24,8},{28,12},{1,17},{... | collective-permute-start | bytes 1966088 | tf_op jit(solution)/shard_map/ppermute | solution.py:115
  93.5 12.9 %collective-permute-start.14 = (s32[512]{0:T(512)S(1)}, s32[512]{0:T(512)S(1)}, u32[]{:S(2)}, u32[]{:S(2)}) collective-permute-start(s32[512]{0:T(512)S(1)} %get-tuple-element.110), channel_id=1, source_target_pairs={{0,4},{4,8},{8,12},{12,16},{16,20},{20,24},{24,28},{1,5},{5,9},{9,... | collective-permute-start | bytes 6152 | tf_op jit(solution)/shard_map/ppermute | solution.py:25
  94.8 15.4 %collective-permute-start.6 = (bf16[256,2560]{1,0:T(8,128)(2,1)S(1)}, bf16[256,2560]{1,0:T(8,128)(2,1)}, u32[]{:S(2)}, u32[]{:S(2)}) collective-permute-start(bf16[256,2560]{1,0:T(8,128)(2,1)S(1)} %assemble.1.refs_0_), channel_id=1, source_target_pairs={{0,4},{4,0},{8,12},{12,8},{16,20},{20,16},{24,28},{28,24},{1,5},{5... | collective-permute-start | bytes 3932168 | tf_op jit(solution)/shard_map/ppermute | solution.py:115
  96.2 14.1 %collective-permute-start.10 = (bf16[256,2560]{1,0:T(8,128)(2,1)S(1)}, bf16[256,2560]{1,0:T(8,128)(2,1)}, u32[]{:S(2)}, u32[]{:S(2)}) collective-permute-start(bf16[256,2560]{1,0:T(8,128)(2,1)S(1)} %collective-permute-done.9.refs_4_), channel_id=1, source_target_pairs={{0,4},{4,0},{8,12},{12,8},{16,20},{20,16},{24,28},{28,24},{1,5},{5... | collective-permute-start | bytes 3932168 | tf_op jit(solution)/shard_map/ppermute | solution.py:115
  103.3 7.5 %collective-permute-start.8 = (bf16[256,2560]{1,0:T(8,128)(2,1)}, bf16[256,2560]{1,0:T(8,128)(2,1)}, u32[]{:S(2)}, u32[]{:S(2)}) collective-permute-start(bf16[256,2560]{1,0:T(8,128)(2,1)} %collective-permute-done.7.refs_2_), channel_id=1, source_target_pairs={{0,4},{4,0},{8,12},{12,8},{16,20},{20,16},{24,28},{28,24},{1,5},{5... | collective-permute-start | bytes 3932168 | tf_op jit(solution)/shard_map/ppermute | solution.py:115
  105.7 5.4 %collective-permute-start.13 = (bf16[256,2560]{1,0:T(8,128)(2,1)}, bf16[256,2560]{1,0:T(8,128)(2,1)}, u32[]{:S(2)}, u32[]{:S(2)}) collective-permute-start(bf16[256,2560]{1,0:T(8,128)(2,1)} %constant_dynamic-update-slice_fusion.refs_6_), channel_id=1, source_target_pairs={{0,4},{4,0},{8,12},{12,8},{16,20},{20,16},{24,28},{28,24},{1,5},{5... | collective-permute-start | bytes 3932168 | tf_op jit(solution)/shard_map/ppermute | solution.py:115
  110.0 0.8 copy-start.20
  110.0 1.0 copy-start.22
  110.0 1.1 copy-start.24
  128.2 1.3 copy-start.4
  129.6 1.3 copy-start.8
  130.9 1.9 copy-start.19
  141.5 32.6 %collective-permute-start.16 = (bf16[2,512,512]{2,1,0:T(8,128)(2,1)}, bf16[2,512,512]{2,1,0:T(8,128)(2,1)S(1)}, u32[]{:S(2)}, u32[]{:S(2)}) collective-permute-start(bf16[2,512,512]{2,1,0:T(8,128)(2,1)} %get-tuple-element.86), channel_id=1, source_target_pairs={{0,4},{4,8},{8,12},{12,16},{16,20},{20,24},{24,28},{1,5},{5,9},{9,... | collective-permute-start | bytes 3145736 | tf_op jit(solution)/shard_map/ppermute | solution.py:25
  144.6 1.1 copy-start.13
  145.6 2.6 %copy-start.21 = (f32[1024,64]{1,0:T(8,128)S(1)}, f32[1024,64]{1,0:T(8,128)}, u32[]{:S(2)}) copy-start(f32[1024,64]{1,0:T(8,128)} %copy-done.20) | copy-start | bytes 786436
  145.6 2.6 %copy-start.23 = (f32[1024,64]{1,0:T(8,128)S(1)}, f32[1024,64]{1,0:T(8,128)}, u32[]{:S(2)}) copy-start(f32[1024,64]{1,0:T(8,128)} %copy-done.22) | copy-start | bytes 786436
  145.6 2.6 %copy-start.25 = (f32[1024,64]{1,0:T(8,128)S(1)}, f32[1024,64]{1,0:T(8,128)}, u32[]{:S(2)}) copy-start(f32[1024,64]{1,0:T(8,128)} %copy-done.24) | copy-start | bytes 786436
  148.2 12.9 %collective-permute-start.15 = (bf16[256,512]{1,0:T(8,128)(2,1)}, bf16[256,512]{1,0:T(8,128)(2,1)}, u32[]{:S(2)}, u32[]{:S(2)}) collective-permute-start(bf16[256,512]{1,0:T(8,128)(2,1)} %attend.4.own_ref), channel_id=1, source_target_pairs={{0,1},{1,0},{2,3},{3,2},{4,5},{5,4},{6,7},{7,6},{8,9},{9,8},{10,11... | collective-permute-start | bytes 786440 | tf_op jit(solution)/shard_map/ppermute | solution.py:115
  161.1 1.3 copy-start.5
  162.4 1.3 copy-start.9
  163.8 1.2 copy-start.16
  165.0 0.9 copy-start.17
  165.9 5.3 %copy-start.14 = (s32[1024,1]{1,0:T(8,128)S(1)}, s32[1024,1]{1,0:T(8,128)}, u32[]{:S(2)}) copy-start(s32[1024,1]{1,0:T(8,128)} %copy.14.qseg_ref) | copy-start | bytes 12292
  173.0 4.1 %copy-start.6 = (bf16[256,2560]{1,0:T(8,128)(2,1)S(1)}, bf16[256,2560]{1,0:T(8,128)(2,1)}, u32[]{:S(2)}) copy-start(bf16[256,2560]{1,0:T(8,128)(2,1)} %copy-done.3) | copy-start | bytes 3932164
  173.1 4.1 %copy-start.10 = (bf16[256,2560]{1,0:T(8,128)(2,1)S(1)}, bf16[256,2560]{1,0:T(8,128)(2,1)}, u32[]{:S(2)}) copy-start(bf16[256,2560]{1,0:T(8,128)(2,1)} %copy-done.7) | copy-start | bytes 3932164
  173.1 15.1 %collective-permute-start.23 = (bf16[256,512]{1,0:T(8,128)(2,1)S(1)}, bf16[256,512]{1,0:T(8,128)(2,1)S(1)}, u32[]{:S(2)}, u32[]{:S(2)}) collective-permute-start(bf16[256,512]{1,0:T(8,128)(2,1)S(1)} %attend.7.own_ref), channel_id=1, source_target_pairs={{0,1},{1,0},{2,3},{3,2},{4,5},{5,4},{6,7},{7,6},{8,9},{9,8},{10,11... | collective-permute-start | bytes 786440 | tf_op jit(solution)/shard_map/ppermute | solution.py:115
  176.0 17.5 %collective-permute-start.20 = (bf16[256,512]{1,0:T(8,128)(2,1)S(1)}, bf16[256,512]{1,0:T(8,128)(2,1)S(1)}, u32[]{:S(2)}, u32[]{:S(2)}) collective-permute-start(bf16[256,512]{1,0:T(8,128)(2,1)S(1)} %attend.6.own_ref), channel_id=1, source_target_pairs={{0,1},{1,0},{2,3},{3,2},{4,5},{5,4},{6,7},{7,6},{8,9},{9,8},{10,11... | collective-permute-start | bytes 786440 | tf_op jit(solution)/shard_map/ppermute | solution.py:115
  180.5 17.1 %collective-permute-start.26 = (bf16[256,512]{1,0:T(8,128)(2,1)S(1)}, bf16[256,512]{1,0:T(8,128)(2,1)S(1)}, u32[]{:S(2)}, u32[]{:S(2)}) collective-permute-start(bf16[256,512]{1,0:T(8,128)(2,1)S(1)} %get-tuple-element.99), channel_id=1, source_target_pairs={{1,3},{2,0},{5,7},{6,4},{9,11},{10,8},{13,15},{14,12},{17,19},{18,... | collective-permute-start | bytes 786440 | tf_op jit(solution)/shard_map/ppermute | solution.py:580
  183.7 20.2 %collective-permute-start.17 = (bf16[256,512]{1,0:T(8,128)(2,1)S(1)}, bf16[256,512]{1,0:T(8,128)(2,1)S(1)}, u32[]{:S(2)}, u32[]{:S(2)}) collective-permute-start(bf16[256,512]{1,0:T(8,128)(2,1)S(1)} %attend.5.own_ref), channel_id=1, source_target_pairs={{0,1},{1,0},{2,3},{3,2},{4,5},{5,4},{6,7},{7,6},{8,9},{9,8},{10,11... | collective-permute-start | bytes 786440 | tf_op jit(solution)/shard_map/ppermute | solution.py:115
  187.5 20.7 %collective-permute-start.27 = (bf16[256,512]{1,0:T(8,128)(2,1)S(1)}, bf16[256,512]{1,0:T(8,128)(2,1)S(1)}, u32[]{:S(2)}, u32[]{:S(2)}) collective-permute-start(bf16[256,512]{1,0:T(8,128)(2,1)S(1)} %get-tuple-element.100), channel_id=1, source_target_pairs={{1,2},{2,1},{5,6},{6,5},{9,10},{10,9},{13,14},{14,13},{17,18},{18,... | collective-permute-start | bytes 786440 | tf_op jit(solution)/shard_map/ppermute | solution.py:581
  191.4 18.0 %collective-permute-start.24 = (bf16[256,512]{1,0:T(8,128)(2,1)S(1)}, bf16[256,512]{1,0:T(8,128)(2,1)S(1)}, u32[]{:S(2)}, u32[]{:S(2)}) collective-permute-start(bf16[256,512]{1,0:T(8,128)(2,1)S(1)} %get-tuple-element.94), channel_id=1, source_target_pairs={{1,3},{2,0},{5,7},{6,4},{9,11},{10,8},{13,15},{14,12},{17,19},{18,... | collective-permute-start | bytes 786440 | tf_op jit(solution)/shard_map/ppermute | solution.py:580
  193.5 19.4 %collective-permute-start.25 = (bf16[256,512]{1,0:T(8,128)(2,1)S(1)}, bf16[256,512]{1,0:T(8,128)(2,1)S(1)}, u32[]{:S(2)}, u32[]{:S(2)}) collective-permute-start(bf16[256,512]{1,0:T(8,128)(2,1)S(1)} %get-tuple-element.95), channel_id=1, source_target_pairs={{1,2},{2,1},{5,6},{6,5},{9,10},{10,9},{13,14},{14,13},{17,18},{18,... | collective-permute-start | bytes 786440 | tf_op jit(solution)/shard_map/ppermute | solution.py:581
  197.7 17.9 %collective-permute-start.21 = (bf16[256,512]{1,0:T(8,128)(2,1)S(1)}, bf16[256,512]{1,0:T(8,128)(2,1)S(1)}, u32[]{:S(2)}, u32[]{:S(2)}) collective-permute-start(bf16[256,512]{1,0:T(8,128)(2,1)S(1)} %get-tuple-element.91), channel_id=1, source_target_pairs={{1,3},{2,0},{5,7},{6,4},{9,11},{10,8},{13,15},{14,12},{17,19},{18,... | collective-permute-start | bytes 786440 | tf_op jit(solution)/shard_map/ppermute | solution.py:580
  203.9 6.2 %copy-start.12 = (f32[8,5248]{1,0:T(8,128)S(1)}, f32[8,5248]{1,0:T(8,128)}, u32[]{:S(2)}) copy-start(f32[8,5248]{1,0:T(8,128)} %copy-done.11) | copy-start | bytes 503812
  203.9 11.7 %collective-permute-start.22 = (bf16[256,512]{1,0:T(8,128)(2,1)S(1)}, bf16[256,512]{1,0:T(8,128)(2,1)S(1)}, u32[]{:S(2)}, u32[]{:S(2)}) collective-permute-start(bf16[256,512]{1,0:T(8,128)(2,1)S(1)} %get-tuple-element.92), channel_id=1, source_target_pairs={{1,2},{2,1},{5,6},{6,5},{9,10},{10,9},{13,14},{14,13},{17,18},{18,... | collective-permute-start | bytes 786440 | tf_op jit(solution)/shard_map/ppermute | solution.py:581
  204.7 5.4 %copy-start.2 = (bf16[1024,4,512]{2,1,0:T(4,128)(2,1)S(1)}, bf16[1024,4,512]{2,1,0:T(4,128)(2,1)}, u32[]{:S(2)}) copy-start(bf16[1024,4,512]{2,1,0:T(4,128)(2,1)} %x_ref.13) | copy-start | bytes 12582916
  208.2 17.8 %collective-permute-start.18 = (bf16[256,512]{1,0:T(8,128)(2,1)S(1)}, bf16[256,512]{1,0:T(8,128)(2,1)S(1)}, u32[]{:S(2)}, u32[]{:S(2)}) collective-permute-start(bf16[256,512]{1,0:T(8,128)(2,1)S(1)} %get-tuple-element.88), channel_id=1, source_target_pairs={{1,3},{2,0},{5,7},{6,4},{9,11},{10,8},{13,15},{14,12},{17,19},{18,... | collective-permute-start | bytes 786440 | tf_op jit(solution)/shard_map/ppermute | solution.py:580
  209.5 16.5 %collective-permute-start.19 = (bf16[256,512]{1,0:T(8,128)(2,1)S(1)}, bf16[256,512]{1,0:T(8,128)(2,1)S(1)}, u32[]{:S(2)}, u32[]{:S(2)}) collective-permute-start(bf16[256,512]{1,0:T(8,128)(2,1)S(1)} %get-tuple-element.89), channel_id=1, source_target_pairs={{1,2},{2,1},{5,6},{6,5},{9,10},{10,9},{13,14},{14,13},{17,18},{18,... | collective-permute-start | bytes 786440 | tf_op jit(solution)/shard_map/ppermute | solution.py:581
Sparse Core Ops, SparseCore 0:
  58.7 69.4 all-gather.4
  129.8 27.7 all-gather.2
